TPU v7x, 32 devices: a whole 2x2x4 slice. The times are simulated.
32 devices in a mesh: dp: 16 (over z, y, core), seq: 2 (over x).
Axes of the slice: x: 2, y: 2, z: 4, core: 2. Of those that a mesh axis runs over, the one named last changes fastest.
Arguments:
- tokens: bfloat16 [4096, 2048], P(('dp', 'seq')), may hold values from -6 to 6
- cotangent: bfloat16 [4096, 2048], P(('dp', 'seq')), may hold values from -6 to 6
- w_qkv: bfloat16 [2048, 5120], P(('dp', 'seq')), may hold values from -0.125 to 0.125
- w_out: bfloat16 [4096, 2048], P(('dp', 'seq')), may hold values from -0.75 to 0.75
- w_router: bfloat16 [2048, 32], P(('dp', 'seq')), may hold values from -0.0625 to 0.0625
- norm_gains: bfloat16 [4352], P(('dp', 'seq')), may hold values from 0.5 to 1.5
- w_expert: bfloat16 [32, 2048, 2304], P(('dp', 'seq')), may hold values from -0.21875 to 0.21875
- lengths: int32 [16, 4], P('dp'), may hold values from 1 to 192, 256 in all within a row
- deal: int32 [16, 256], P('dp'), may hold values from 0 to 255, each once within a row
- routes: int32 [16, 256, 8], P('dp'), may hold values from 0 to 31, all different within a row
Outputs:
- layer_out: bfloat16 [4096, 2048], P(('dp', 'seq'))
- grad_tokens: bfloat16 [4096, 2048], P(('dp', 'seq'))
- grad_qkv: float32 [2048, 5120], P(('dp', 'seq'))
- grad_out: float32 [4096, 2048], P(('dp', 'seq'))
- grad_router: float32 [2048, 32], P(('dp', 'seq'))
- grad_gains: float32 [4352], P(('dp', 'seq'))
- grad_expert: float32 [32, 2048, 2304], P(('dp', 'seq'))
Inputs may be any that keep to these rules, and one draw needn't show every extreme that they name: `lengths`: each group's entries sum to 256; the last counts padding positions. `deal`: each group's row holds every position once. `routes`: each token names 8 different experts.
All inputs are finite; a program needn't handle non-finite values.
Results may differ from a plain program's by a relative error of at most 0.015.
Values may be sent and summed in bfloat16 or wider, within the bound.
No kernel may reach another device: no remote copies, remote signals or barrier semaphores. Data moves between devices by JAX's collectives and lax.ppermute only.
A program may use at most 256 MiB of HBM per device.

v0:
```python
import jax
import jax.numpy as jnp
from jax import lax
from jax.sharding import PartitionSpec as P

D = 2048
HEADS = 32
KV_HEADS = 4
HEAD_DIM = 128
FF = 768
TOPK = 8
NSEG = 4
TOK_DEV = 128
QDIM = 4096
KVDIM = 512


EPS = 1e-06
THETA = 1000000.0


def rms_norm(values, scales):
    return values * lax.rsqrt(jnp.mean(values * values, axis=-1, keepdims=True) + EPS) * scales


def rotary(values, cosine, sine_part):
    half_width = values.shape[-1] // 2
    front_part = values[..., :half_width]
    back_part = values[..., half_width:]
    cos_wide = cosine[..., None, :]
    sin_wide = sine_part[..., None, :]
    return jnp.concatenate(
        [
            front_part * cos_wide - back_part * sin_wide,
            back_part * cos_wide + front_part * sin_wide,
        ],
        axis=-1,
    )


def tables(positions, head_width):
    half_width = head_width // 2
    inverse = THETA ** (-(jnp.arange(half_width, dtype=jnp.float32) * 2.0 / head_width))
    angles = positions.astype(jnp.float32)[..., None] * inverse
    return (jnp.cos(angles), jnp.sin(angles))


def positions_of(lengths_row, row_count):
    end_points = jnp.cumsum(lengths_row)
    starts = end_points - lengths_row
    indices = jnp.arange(row_count, dtype=jnp.int32)
    segment = jnp.sum((indices[:, None] >= end_points[None, :]).astype(jnp.int32), axis=1)
    picked = segment[:, None] == jnp.arange(lengths_row.shape[0], dtype=jnp.int32)[None, :]
    offset = jnp.sum(jnp.where(picked, starts[None, :], 0), axis=1)
    return (segment, indices - offset)


def shards(tokens, cotangent, w_qkv, w_out, w_router, norm_gains, w_expert, lengths, deal, routes):
    seq_count = lax.axis_size("seq")
    seq_index = lax.axis_index("seq")
    row_count = TOK_DEV * seq_count
    experts_all = w_router.shape[1]
    capacity = TOK_DEV * TOPK // experts_all
    kv_local = KV_HEADS // seq_count
    heads_local = HEADS // seq_count
    per_group = HEADS // KV_HEADS
    score_scale = HEAD_DIM ** (-0.5)
    dealt_order = deal[0]
    dealt_mine = lax.dynamic_slice_in_dim(dealt_order, seq_index * TOK_DEV, TOK_DEV)
    inverse = (
        jnp.zeros((row_count,), jnp.int32)
        .at[dealt_order]
        .set(jnp.arange(row_count, dtype=jnp.int32))
    )
    given_mine = lax.dynamic_slice_in_dim(inverse, seq_index * TOK_DEV, TOK_DEV)
    segment, position = positions_of(lengths[0], row_count)
    seg_dealt = jnp.take(segment, dealt_order)
    pos_dealt = jnp.take(position, dealt_order)
    seg_mine = jnp.take(segment, dealt_mine)
    pos_mine = jnp.take(position, dealt_mine)
    full_tokens, full_cot = (
        lax.all_gather(tokens, "seq", axis=0, tiled=True),
        lax.all_gather(cotangent, "seq", axis=0, tiled=True),
    )
    x_rows = jnp.take(full_tokens, dealt_mine, axis=0).astype(jnp.float32)
    cot_rows = jnp.take(full_cot, dealt_mine, axis=0).astype(jnp.float32)
    qkv_full, out_full, router_full, gains_full = (
        lax.all_gather(w_qkv, ("dp", "seq"), axis=0, tiled=True),
        lax.all_gather(w_out, ("dp", "seq"), axis=0, tiled=True),
        lax.all_gather(w_router, ("dp", "seq"), axis=0, tiled=True),
        lax.all_gather(norm_gains, ("dp", "seq"), axis=0, tiled=True),
    )
    gains_float = gains_full.astype(jnp.float32)
    gain_attn = gains_float[:D]
    gain_ffn = gains_float[D : 2 * D]
    gain_query = gains_float[2 * D : 2 * D + HEAD_DIM]
    gain_key = gains_float[2 * D + HEAD_DIM :]
    normed, attn_back = jax.vjp(rms_norm, x_rows, gain_attn)
    normed_low = normed.astype(jnp.bfloat16)
    projected = jnp.dot(normed_low, qkv_full, preferred_element_type=jnp.float32)
    cosine, sine_part = tables(pos_mine, HEAD_DIM)

    def head_piece(proj_qk, scale_query, scale_key):
        query_raw = proj_qk[:, :QDIM].reshape(TOK_DEV, HEADS, HEAD_DIM)
        key_raw = proj_qk[:, QDIM:].reshape(TOK_DEV, KV_HEADS, HEAD_DIM)
        return (
            rotary(rms_norm(query_raw, scale_query), cosine, sine_part),
            rotary(rms_norm(key_raw, scale_key), cosine, sine_part),
        )

    (queries, key_rot), head_back = jax.vjp(
        head_piece, projected[:, : QDIM + KVDIM], gain_query, gain_key
    )
    value_raw = projected[:, QDIM + KVDIM :].reshape(TOK_DEV, KV_HEADS, HEAD_DIM)
    query_heads, key_heads, value_heads = (
        lax.all_to_all(
            queries.astype(jnp.bfloat16), "seq", split_axis=1, concat_axis=0, tiled=True
        ),
        lax.all_to_all(
            key_rot.astype(jnp.bfloat16), "seq", split_axis=1, concat_axis=0, tiled=True
        ),
        lax.all_to_all(
            value_raw.astype(jnp.bfloat16), "seq", split_axis=1, concat_axis=0, tiled=True
        ),
    )
    allowed = (seg_dealt[:, None] == seg_dealt[None, :]) & (
        pos_dealt[None, :] <= pos_dealt[:, None]
    )
    grouped = query_heads.reshape(row_count, kv_local, per_group, HEAD_DIM)
    scores = (
        jnp.einsum("qkgd,skd->kgqs", grouped, key_heads, preferred_element_type=jnp.float32)
        * score_scale
    )
    scores = jnp.where(allowed, scores, -1e30)
    largest = jnp.max(scores, axis=-1, keepdims=True)
    expd_scores = jnp.exp(scores - largest)
    row_total = jnp.sum(expd_scores, axis=-1, keepdims=True)
    log_total = largest + jnp.log(row_total)
    prob_low = (expd_scores / row_total).astype(jnp.bfloat16)
    mixed_heads = jnp.einsum(
        "kgqs,skd->qkgd", prob_low, value_heads, preferred_element_type=jnp.float32
    )
    mixed_low = mixed_heads.reshape(row_count, heads_local, HEAD_DIM).astype(jnp.bfloat16)
    mixed_tok = lax.all_to_all(mixed_low, "seq", split_axis=0, concat_axis=1, tiled=True).reshape(
        TOK_DEV, QDIM
    )
    residual = x_rows + jnp.dot(mixed_tok, out_full, preferred_element_type=jnp.float32)
    normed_two, ffn_back = jax.vjp(rms_norm, residual, gain_ffn)
    ffn_in = normed_two.astype(jnp.bfloat16)
    logits = jnp.dot(ffn_in, router_full, preferred_element_type=jnp.float32)
    route_mine = jnp.take(routes[0], dealt_mine, axis=0)
    gate_probs = jax.nn.softmax(jnp.take_along_axis(logits, route_mine, axis=1), axis=-1)
    pair_count = TOK_DEV * TOPK
    slot_count = experts_all * capacity
    pair_expert = route_mine.reshape(pair_count)
    usable = jnp.repeat(seg_mine != NSEG - 1, TOPK)
    expert_ids = jnp.arange(experts_all, dtype=jnp.int32)
    onehot = ((pair_expert[:, None] == expert_ids[None, :]) & usable[:, None]).astype(jnp.int32)
    before = jnp.cumsum(onehot, axis=0) - onehot
    place_rank = jnp.sum(before * onehot, axis=1)
    kept_pair = usable & (place_rank < capacity)
    pair_slot = jnp.where(kept_pair, pair_expert * capacity + place_rank, slot_count)
    slot_pair = (
        jnp.full((slot_count + 1,), pair_count, jnp.int32)
        .at[pair_slot]
        .set(jnp.arange(pair_count, dtype=jnp.int32))[:slot_count]
    )
    slot_token = slot_pair // TOPK
    padded_in = jnp.concatenate([ffn_in, jnp.zeros((1, D), jnp.bfloat16)], axis=0)
    send_rows = jnp.take(padded_in, slot_token, axis=0).reshape(experts_all, capacity, D)
    expert_weight = w_expert[0]
    received_rows = lax.all_to_all(
        send_rows, ("dp", "seq"), split_axis=0, concat_axis=0, tiled=True
    )
    sources = received_rows.shape[0]
    slot_width = received_rows.shape[1]
    flat_rows = received_rows.reshape(sources * slot_width, D)
    gate_up = jnp.dot(flat_rows, expert_weight[:, : 2 * FF], preferred_element_type=jnp.float32)
    active = (jax.nn.silu(gate_up[:, :FF]) * gate_up[:, FF:]).astype(jnp.bfloat16)
    result = jnp.einsum(
        "rf,df->rd", active, expert_weight[:, 2 * FF :], preferred_element_type=jnp.float32
    ).astype(jnp.bfloat16)
    expert_out = result.reshape(sources, slot_width, D)
    kept_gu = gate_up.reshape(sources, slot_width, 2 * FF)
    returned = lax.all_to_all(
        expert_out, ("dp", "seq"), split_axis=0, concat_axis=0, tiled=True
    ).reshape(slot_count, D)
    padded_out = jnp.concatenate([returned, jnp.zeros((1, D), jnp.bfloat16)], axis=0)
    pair_out = jnp.take(padded_out, pair_slot, axis=0).reshape(TOK_DEV, TOPK, D).astype(jnp.float32)
    final_rows = (residual + jnp.sum(gate_probs[:, :, None] * pair_out, axis=1)).astype(
        jnp.bfloat16
    )
    gate_grad = jnp.sum(cot_rows[:, None, :] * pair_out, axis=2)
    gate_flat = jnp.concatenate([gate_probs.reshape(pair_count), jnp.zeros((1,), jnp.float32)])
    slot_gate = jnp.take(gate_flat, slot_pair)
    padded_cot = jnp.concatenate([cot_rows, jnp.zeros((1, D), jnp.float32)], axis=0)
    slot_grad = (
        (slot_gate[:, None] * jnp.take(padded_cot, slot_token, axis=0))
        .astype(jnp.bfloat16)
        .reshape(experts_all, capacity, D)
    )
    grad_back = lax.all_to_all(slot_grad, ("dp", "seq"), split_axis=0, concat_axis=0, tiled=True)
    source_count = grad_back.shape[0]
    rows_total = source_count * capacity
    grad_flat = grad_back.reshape(rows_total, D)
    gu_flat = kept_gu.reshape(rows_total, 2 * FF)
    in_flat = received_rows.reshape(rows_total, D)
    gate_pre = gu_flat[:, :FF]
    up_pre = gu_flat[:, FF:]
    sig_gate = jax.nn.sigmoid(gate_pre)
    silu_val = jax.nn.silu(gate_pre)
    active = (silu_val * up_pre).astype(jnp.bfloat16)
    act_grad = jnp.dot(grad_flat, expert_weight[:, 2 * FF :], preferred_element_type=jnp.float32)
    down_grad = jnp.einsum("rd,rf->df", grad_flat, active, preferred_element_type=jnp.float32)
    silu_slope = sig_gate * (1.0 + gate_pre * (1.0 - sig_gate))
    gu_grad = jnp.concatenate([act_grad * up_pre * silu_slope, act_grad * silu_val], axis=1).astype(
        jnp.bfloat16
    )
    gu_weight_grad = jnp.einsum("rd,rj->dj", in_flat, gu_grad, preferred_element_type=jnp.float32)
    in_grad = jnp.einsum(
        "rj,dj->rd", gu_grad, expert_weight[:, : 2 * FF], preferred_element_type=jnp.float32
    ).astype(jnp.bfloat16)
    grad_expert = jnp.concatenate([gu_weight_grad, down_grad], axis=1)[None]
    pair_grads = lax.all_to_all(
        in_grad.reshape(source_count, capacity, D),
        ("dp", "seq"),
        split_axis=0,
        concat_axis=0,
        tiled=True,
    ).reshape(slot_count, D)
    padded_grads = jnp.concatenate([pair_grads, jnp.zeros((1, D), jnp.bfloat16)], axis=0)
    from_experts = jnp.sum(
        jnp.take(padded_grads, pair_slot, axis=0).reshape(TOK_DEV, TOPK, D).astype(jnp.float32),
        axis=1,
    )
    mean_term = jnp.sum(gate_probs * gate_grad, axis=1, keepdims=True)
    chosen_grad = gate_probs * (gate_grad - mean_term)
    logit_grad = jnp.sum(
        jnp.where(
            route_mine[:, :, None] == expert_ids[None, None, :], chosen_grad[:, :, None], 0.0
        ),
        axis=1,
    ).astype(jnp.bfloat16)
    router_grad = jnp.einsum("td,te->de", ffn_in, logit_grad, preferred_element_type=jnp.float32)
    ffn_in_grad = from_experts + jnp.einsum(
        "te,de->td", logit_grad, router_full, preferred_element_type=jnp.float32
    )
    resid_part, gain_ffn_grad = ffn_back(ffn_in_grad)
    residual_grad = cot_rows + resid_part
    resid_low = residual_grad.astype(jnp.bfloat16)
    out_weight_grad = jnp.einsum(
        "tq,td->qd", mixed_tok, resid_low, preferred_element_type=jnp.float32
    )
    mixed_grad = (
        jnp.einsum("td,qd->tq", resid_low, out_full, preferred_element_type=jnp.float32)
        .astype(jnp.bfloat16)
        .reshape(TOK_DEV, HEADS, HEAD_DIM)
    )
    grad_heads = lax.all_to_all(mixed_grad, "seq", split_axis=1, concat_axis=0, tiled=True)
    grad_grouped = grad_heads.reshape(row_count, kv_local, per_group, HEAD_DIM)
    scores_again = (
        jnp.einsum("qkgd,skd->kgqs", grouped, key_heads, preferred_element_type=jnp.float32)
        * score_scale
    )
    scores_again = jnp.where(allowed, scores_again, -1e30)
    prob_full = jnp.exp(scores_again - log_total)
    prob_again = prob_full.astype(jnp.bfloat16)
    value_grad = jnp.einsum(
        "kgqs,qkgd->skd", prob_again, grad_grouped, preferred_element_type=jnp.float32
    )
    prob_grad = jnp.einsum(
        "qkgd,skd->kgqs", grad_grouped, value_heads, preferred_element_type=jnp.float32
    )
    score_grad = (
        prob_full * (prob_grad - jnp.sum(prob_full * prob_grad, axis=-1, keepdims=True))
    ).astype(jnp.bfloat16)
    query_grad = (
        jnp.einsum("kgqs,skd->qkgd", score_grad, key_heads, preferred_element_type=jnp.float32)
        * score_scale
    ).reshape(row_count, heads_local, HEAD_DIM)
    key_grad = (
        jnp.einsum("kgqs,qkgd->skd", score_grad, grouped, preferred_element_type=jnp.float32)
        * score_scale
    )
    query_tok, key_tok, value_tok = (
        lax.all_to_all(
            query_grad.astype(jnp.bfloat16), "seq", split_axis=0, concat_axis=1, tiled=True
        ),
        lax.all_to_all(
            key_grad.astype(jnp.bfloat16), "seq", split_axis=0, concat_axis=1, tiled=True
        ),
        lax.all_to_all(
            value_grad.astype(jnp.bfloat16), "seq", split_axis=0, concat_axis=1, tiled=True
        ),
    )
    qk_grad, query_gain_grad, key_gain_grad = head_back(
        (query_tok.astype(jnp.float32), key_tok.astype(jnp.float32))
    )
    proj_grad = jnp.concatenate(
        [qk_grad, value_tok.reshape(TOK_DEV, KVDIM).astype(jnp.float32)], axis=1
    ).astype(jnp.bfloat16)
    qkv_grad = jnp.einsum("td,te->de", normed_low, proj_grad, preferred_element_type=jnp.float32)
    normed_grad = jnp.einsum("te,de->td", proj_grad, qkv_full, preferred_element_type=jnp.float32)
    input_part, gain_attn_grad = attn_back(normed_grad)
    input_grad = (residual_grad + input_part).astype(jnp.bfloat16)
    gains_grad = jnp.concatenate([gain_attn_grad, gain_ffn_grad, query_gain_grad, key_gain_grad])
    qkv_share, out_share, router_share, gains_share = (
        lax.psum_scatter(qkv_grad, ("dp", "seq"), scatter_dimension=0, tiled=True),
        lax.psum_scatter(out_weight_grad, ("dp", "seq"), scatter_dimension=0, tiled=True),
        lax.psum_scatter(router_grad, ("dp", "seq"), scatter_dimension=0, tiled=True),
        lax.psum_scatter(gains_grad, ("dp", "seq"), scatter_dimension=0, tiled=True),
    )
    out_group, input_group = (
        lax.all_gather(final_rows, "seq", axis=0, tiled=True),
        lax.all_gather(input_grad, "seq", axis=0, tiled=True),
    )
    return (
        jnp.take(out_group, given_mine, axis=0),
        jnp.take(input_group, given_mine, axis=0),
        qkv_share,
        out_share,
        router_share,
        gains_share,
        grad_expert,
    )


def solution(mesh):
    in_specs = (
        P(("dp", "seq"), None),
        P(("dp", "seq"), None),
        P(("dp", "seq"), None),
        P(("dp", "seq"), None),
        P(("dp", "seq"), None),
        P(("dp", "seq")),
        P(("dp", "seq"), None, None),
        P("dp", None),
        P("dp", None),
        P("dp", None, None),
    )
    out_specs = (
        P(("dp", "seq"), None),
        P(("dp", "seq"), None),
        P(("dp", "seq"), None),
        P(("dp", "seq"), None),
        P(("dp", "seq"), None),
        P(("dp", "seq")),
        P(("dp", "seq"), None, None),
    )
    return jax.shard_map(shards, mesh=mesh, in_specs=in_specs, out_specs=out_specs, check_vma=False)
```

profile of v0, /device:TPU:0, one launch (start us, length us, event | category | flops | bytes accessed | tf_op | source)
XLA Modules:
  0.0 2521.2 jit_solution(11691838374983396379)
XLA Ops:
  11.7 2.5 gather_fusion.6
  14.9 2.5 gather_fusion.7
  20.9 42.7 %all-reduce.10 = bf16[4352]{0:T(1024)(128)(2,1)S(1)} all-reduce(bf16[4352]{0:T(1024)(128)(2,1)S(1)} %dynamic-update-slice), channel_id=1, replica_groups=mesh['dp'=16,'seq'=2] {'dp','seq'}, use_global_device_ids=true, to_apply=%add.10 | all-reduce | flops 4352 | bytes 17408
  64.5 2.8 gather_fusion.5
  67.6 104.2 %all-gather.10.cloned.1.call-done = bf16[2048,5120]{1,0:T(8,128)(2,1)} async-done(((bf16[64,5120]{1,0:T(8,128)(2,1)}), bf16[2048,5120]{1,0:T(8,128)(2,1)}) %all-gather.10.cloned.1.call-update) | async-done | bytes 20971536 | tf_op jit(solution)/shard_map/all_gather | solution.py:88
  171.8 8.6 fusion.53
  182.6 4.0 all-to-all-start
  192.2 3.0 multiply_reduce_fusion.2
  198.6 3.4 all-to-all-start.1
  204.5 3.5 all-to-all-done.1
  208.0 3.8 all-to-all-start.2
  215.1 16.8 all-to-all-done.2
  237.6 3.6 all-to-all-start.3
  241.9 9.0 reduce-window.11
  251.3 74.4 %all-gather = bf16[32,64,32]{1,2,0:T(8,128)(2,1)S(1)} all-gather(bf16[1,64,32]{1,2,0:T(8,128)(2,1)S(1)} %bitcast.239), channel_id=1, replica_groups=mesh['dp'=16,'seq'=2] {'dp','seq'}, dimensions={0}, use_global_device_ids=true | all-gather | bytes 135168 | tf_op jit(solution)/shard_map/all_gather | solution.py:90
  327.9 8.6 multiply_reduce_fusion.5
  336.9 7.0 gather_fusion.4
  345.1 4.3 scatter_custom_fusion
  350.2 6.0 gather_fusion.1
  356.1 4.7 broadcast_select_fusion.1
  360.8 3.6 all-to-all-start.4
  365.0 48.7 %all-gather.16.cloned.1.call-done = bf16[256,2048]{1,0:T(8,128)(2,1)} async-done(((bf16[128,2048]{1,0:T(8,128)(2,1)}), bf16[256,2048]{1,0:T(8,128)(2,1)}) %all-gather.16.cloned.1.call-update) | async-done | bytes 1048592 | tf_op jit(solution)/shard_map/all_gather | solution.py:83
  413.7 2.9 gather_fusion.12
  420.5 6.3 gather_fusion.2
  426.9 6.7 gather_fusion.3
  433.6 5.2 multiply_convert_fusion
  438.8 19.6 all-to-all-done.4
  458.4 4.5 all-to-all-start.6
  462.9 11.7 fusion.5
  474.6 82.0 %all-to-all-done.6 = bf16[32,32,2048]{2,1,0:T(8,128)(2,1)} async-done(((bf16[32,32,2048]{2,1,0:T(8,128)(2,1)}), bf16[32,32,2048]{2,1,0:T(8,128)(2,1)}, u32[]{:S(2)}, u32[]{:S(2)}) %all-to-all-start.6) | async-done | bytes 4194336 | tf_op jit(solution)/shard_map/all_to_all | solution.py:202
  556.6 11.0 multiply_convert_fusion.2
  567.6 7.4 convolution_convert_fusion.1
  575.0 5.3 all-to-all-start.5
  580.3 11.1 fusion.10
  591.4 82.6 %all-to-all-done.5 = bf16[32,32,2048]{2,1,0:T(8,128)(2,1)} async-done(((bf16[32,32,2048]{2,1,0:T(8,128)(2,1)}), bf16[32,32,2048]{2,1,0:T(8,128)(2,1)}, u32[]{:S(2)}, u32[]{:S(2)}) %all-to-all-start.5) | async-done | bytes 4194336 | tf_op jit(solution)/shard_map/all_to_all | solution.py:185
  674.0 4.9 all-to-all-start.7
  679.1 4.8 concatenate.40
  683.9 11.5 gather_fusion.10
  695.4 3.4 fusion.2
  700.7 74.4 %all-to-all-done.7 = bf16[32,32,2048]{2,1,0:T(8,128)(2,1)} async-done(((bf16[32,32,2048]{2,1,0:T(8,128)(2,1)}), bf16[32,32,2048]{2,1,0:T(8,128)(2,1)}, u32[]{:S(2)}, u32[]{:S(2)}) %all-to-all-start.7) | async-done | bytes 4194336 | tf_op jit(solution)/shard_map/all_to_all | solution.py:224
  775.1 4.8 concatenate.44
  779.9 11.6 gather_fusion.13
  791.5 10.0 convert_reduce_fusion
  803.8 11.8 fusion.25
  817.0 3.6 all-to-all-start.8
  821.1 15.0 all-to-all-done.8
  836.3 3.9 fusion.36
  844.0 4.0 all-to-all-start.9
  853.1 3.4 all-to-all-start.11
  858.4 4.0 all-to-all-done.11
  862.3 3.6 all-to-all-start.10
  871.6 5.2 all-to-all-done.10
  883.1 11.8 fusion.41
  896.2 13.6 fusion.49
  911.1 17.4 fusion.47
  930.7 5.6 fusion.99
  936.3 8.8 fusion.23
  945.2 6.9 maximum_bitcast_fusion
  952.1 18.8 copy.331
  972.3 42.5 %all-reduce.11 = f32[4352]{0:T(1024)S(1)} all-reduce(f32[4352]{0:T(1024)S(1)} %pad_maximum_fusion.8), channel_id=5, replica_groups=mesh['dp'=16,'seq'=2] {'dp','seq'}, use_global_device_ids=true, to_apply=%region_33.38.clone | all-reduce | flops 4352 | bytes 34816
  1015.5 2.8 gather_fusion.11
  1018.4 2.8 gather_fusion.14
  1022.3 605.8 %reduce-scatter.8.cloned.1.call-done = f32[128,2048]{1,0:T(8,128)} async-done(((f32[4096,2048]{1,0:T(8,128)}), f32[128,2048]{1,0:T(8,128)}) %reduce-scatter.8.cloned.1.call-update) | async-done | bytes 1048592 | tf_op jit(solution)/shard_map/reduce_scatter | solution.py:309
  1628.1 886.1 %reduce-scatter.6.cloned.1.call-done = f32[64,5120]{1,0:T(8,128)} async-done(((f32[2048,5120]{1,0:T(8,128)}), f32[64,5120]{1,0:T(8,128)}) %reduce-scatter.6.cloned.1.call-update) | async-done | bytes 1310736 | tf_op jit(solution)/shard_map/reduce_scatter | solution.py:308
  (359 shorter events, 78.5 us)
Async XLA Ops:
  7.2 12.7 copy-start.60
  7.2 12.5 copy-start.68
  7.2 13.5 copy-start.85
  7.2 57.3 %all-gather.8.cloned.1.call-start = ((), (), s32[]{:S(2)}) async-start(), calls=%async_computation.15 | async-start | bytes 1572864 | tf_op jit(solution)/shard_map/all_gather | solution.py:82
  7.9 163.9 %all-gather.10.cloned.1.call-start = ((), (), s32[]{:S(2)}) async-start(), calls=%async_computation.16 | async-start | bytes 21626880 | tf_op jit(solution)/shard_map/all_gather | solution.py:88
  8.7 319.2 %all-gather.12.cloned.1.call-start = ((), (), s32[]{:S(2)}) async-start(), calls=%async_computation.17 | async-start | bytes 17301504 | tf_op jit(solution)/shard_map/all_gather | solution.py:89
  18.2 162.2 %copy-start.78 = (s32[128]{0:T(128)}, s32[128]{0:T(128)S(1)}, u32[]{:S(2)}) copy-start(s32[128]{0:T(128)S(1)} %get-tuple-element.91) | copy-start | bytes 1540
  18.2 309.7 %copy-start.39 = (pred[128]{0:T(512)(128)(4,1)}, pred[128]{0:T(512)(128)(4,1)S(1)}, u32[]{:S(2)}) copy-start(pred[128]{0:T(512)(128)(4,1)S(1)} %get-tuple-element.90) | copy-start | bytes 388
  18.2 153.6 %copy-start.63 = (s32[1024]{0:T(1024)}, s32[1024]{0:T(1024)S(1)}, u32[]{:S(2)}) copy-start(s32[1024]{0:T(1024)S(1)} %pad_clamp_fusion.3) | copy-start | bytes 12292
  63.6 132.1 %copy-start.70 = (f32[128]{0:T(128)}, f32[128]{0:T(128)S(1)}, u32[]{:S(2)}) copy-start(f32[128]{0:T(128)S(1)} %get-tuple-element.108) | copy-start | bytes 1540
  63.6 132.3 %copy-start.66 = (f32[128]{0:T(128)}, f32[128]{0:T(128)S(1)}, u32[]{:S(2)}) copy-start(f32[128]{0:T(128)S(1)} %get-tuple-element.107) | copy-start | bytes 1540
  64.2 107.6 %copy-start.27 = (f32[2048]{0:T(1024)}, f32[2048]{0:T(1024)S(1)}, u32[]{:S(2)}) copy-start(f32[2048]{0:T(1024)S(1)} %get-tuple-element.106) | copy-start | bytes 24580
  64.4 132.3 %copy-start.24 = (f32[128,64]{0,1:T(8,128)}, f32[128,64]{0,1:T(8,128)S(1)}, u32[]{:S(2)}) copy-start(f32[128,64]{0,1:T(8,128)S(1)} %get-tuple-element.114) | copy-start | bytes 98308
  64.4 132.3 %copy-start.25 = (f32[128,64]{0,1:T(8,128)}, f32[128,64]{0,1:T(8,128)S(1)}, u32[]{:S(2)}) copy-start(f32[128,64]{0,1:T(8,128)S(1)} %get-tuple-element.115) | copy-start | bytes 98308
  67.3 260.6 %copy-start.4 = (bf16[128,2048]{1,0:T(8,128)(2,1)}, bf16[128,2048]{1,0:T(8,128)(2,1)S(1)}, u32[]{:S(2)}) copy-start(bf16[128,2048]{1,0:T(8,128)(2,1)S(1)} %gather_fusion.5) | copy-start | bytes 1572868
  67.6 112.9 %copy-start.83 = (f32[128]{0:T(128)}, f32[128]{0:T(128)S(1)}, u32[]{:S(2)}) copy-start(f32[128]{0:T(128)S(1)} %fusion.45) | copy-start | bytes 1540
  67.6 104.2 %copy-start.54 = (f32[128]{0:T(128)}, f32[128]{0:T(128)S(1)}, u32[]{:S(2)}) copy-start(f32[128]{0:T(128)S(1)} %fusion.85) | copy-start | bytes 1540
  182.6 16.0 all-to-all-start
  197.8 13.9 copy-start.61
  197.8 13.9 copy-start.76
  197.8 13.9 copy-start.77
  198.6 9.4 all-to-all-start.1
  208.0 24.0 all-to-all-start.2
  215.1 19.2 copy-start.18
  235.8 15.5 copy-start.69
  237.6 88.6 %all-to-all-start.3 = ((bf16[256,16,128]{2,1,0:T(8,128)(2,1)}), bf16[256,16,128]{2,1,0:T(8,128)(2,1)S(1)}, u32[]{:S(2)}, u32[]{:S(2)}) async-start(bf16[256,16,128]{2,1,0:T(8,128)(2,1)} %copy.301), calls=%async_computation.3 | async-start | bytes 2097152 | tf_op jit(solution)/shard_map/all_to_all | solution.py:144
  241.5 103.6 %copy-start.57 = (pred[1024]{0:T(1024)(128)(4,1)}, pred[1024]{0:T(1024)(128)(4,1)S(1)}, u32[]{:S(2)}) copy-start(pred[1024]{0:T(1024)(128)(4,1)S(1)} %and.101) | copy-start | bytes 3076
  336.4 7.5 copy-start.8
  336.4 7.5 copy-start.81
  336.5 7.5 copy-start.72
  344.8 74.9 %copy-start.37 = (s32[1024]{0:T(1024)}, s32[1024]{0:T(1024)S(1)}, u32[]{:S(2)}) copy-start(s32[1024]{0:T(1024)S(1)} %select_n.226) | copy-start | bytes 12292
  345.1 11.0 copy-start.45
  360.8 97.6 %all-to-all-start.4 = ((bf16[32,32,2048]{2,1,0:T(8,128)(2,1)}), bf16[32,32,2048]{2,1,0:T(8,128)(2,1)}, u32[]{:S(2)}, u32[]{:S(2)}) async-start(bf16[32,32,2048]{2,1,0:T(8,128)(2,1)} %broadcast_select_fusion.1), calls=%async_computation.4 | async-start | bytes 8388608 | tf_op jit(solution)/shard_map/all_to_all | solution.py:172
  364.4 49.3 %all-gather.16.cloned.1.call-start = ((), (), s32[]{:S(2)}) async-start(), calls=%async_computation.19 | async-start | bytes 1572864 | tf_op jit(solution)/shard_map/all_gather | solution.py:83
  365.0 51.9 %copy-start.64 = (f32[128]{0:T(128)S(1)}, f32[128]{0:T(128)}, u32[]{:S(2)}) copy-start(f32[128]{0:T(128)} %get-tuple-element.88) | copy-start | bytes 1540
  458.4 98.2 %all-to-all-start.6 = ((bf16[32,32,2048]{2,1,0:T(8,128)(2,1)}), bf16[32,32,2048]{2,1,0:T(8,128)(2,1)}, u32[]{:S(2)}, u32[]{:S(2)}) async-start(bf16[32,32,2048]{2,1,0:T(8,128)(2,1)} %multiply_convert_fusion), calls=%async_computation.6 | async-start | bytes 8388608 | tf_op jit(solution)/shard_map/all_to_all | solution.py:202
  575.0 99.0 %all-to-all-start.5 = ((bf16[32,32,2048]{2,1,0:T(8,128)(2,1)}), bf16[32,32,2048]{2,1,0:T(8,128)(2,1)}, u32[]{:S(2)}, u32[]{:S(2)}) async-start(bf16[32,32,2048]{2,1,0:T(8,128)(2,1)} %bitcast.217), calls=%async_computation.5 | async-start | bytes 8388608 | tf_op jit(solution)/shard_map/all_to_all | solution.py:185
  674.0 101.1 %all-to-all-start.7 = ((bf16[32,32,2048]{2,1,0:T(8,128)(2,1)}), bf16[32,32,2048]{2,1,0:T(8,128)(2,1)}, u32[]{:S(2)}, u32[]{:S(2)}) async-start(bf16[32,32,2048]{2,1,0:T(8,128)(2,1)} %bitcast.216), calls=%async_computation.7 | async-start | bytes 8388608 | tf_op jit(solution)/shard_map/all_to_all | solution.py:224
  678.9 292.0 %reduce-scatter.10.cloned.1.call-start = ((), (), s32[]{:S(2)}) async-start(), calls=%async_computation.23 | async-start | bytes 1081344
  791.5 10.0 copy-start.9
  791.5 10.0 copy-start.73
  791.5 11.1 copy-start.82
  791.5 11.1 copy-start.41
  803.8 11.9 copy-start.6
  817.0 19.2 all-to-all-start.8
  820.6 194.9 %all-gather.14.cloned.1.call-start = ((), (), s32[]{:S(2)}) async-start(), calls=%async_computation.18 | async-start | bytes 1572864 | tf_op jit(solution)/shard_map/all_gather | solution.py:314
  844.0 9.1 all-to-all-start.9
  848.0 18.0 copy-start.17
  848.0 18.0 copy-start.52
  848.0 18.0 copy-start.71
  853.1 9.2 all-to-all-start.11
  858.4 9.1 copy-start.22
  862.3 14.5 all-to-all-start.10
  865.9 152.4 %all-gather.18.cloned.1.call-start = ((), (), s32[]{:S(2)}) async-start(), calls=%async_computation.20 | async-start | bytes 1572864 | tf_op jit(solution)/shard_map/all_gather | solution.py:315
  867.4 13.4 copy-start.3
  867.4 13.5 copy-start.30
  871.6 9.3 copy-start.67
  882.9 11.9 copy-start.14
  883.0 11.9 copy-start.84
  883.0 11.9 copy-start.7
  896.2 732.0 %reduce-scatter.8.cloned.1.call-start = ((), (), s32[]{:S(2)}) async-start(), calls=%async_computation.22 | async-start | bytes 34603008 | tf_op jit(solution)/shard_map/reduce_scatter | solution.py:309
  909.9 1604.3 %reduce-scatter.6.cloned.1.call-start = ((), (), s32[]{:S(2)}) async-start(), calls=%async_computation.21 | async-start | bytes 43253760 | tf_op jit(solution)/shard_map/reduce_scatter | solution.py:308
  952.1 20.2 copy-start.53
  952.1 20.2 copy-start.80
  (47 other events, 158.3 us)
Sparse Core Ops, SparseCore 0:
  9.6 24.5 all-gather.7
  37.0 134.7 all-gather.9
  174.8 134.3 all-gather.11
  366.5 47.1 all-gather.15
  700.8 140.3 reduce-scatter.9
  843.3 21.9 all-gather.13
  896.3 21.4 all-gather.17
  920.8 707.3 reduce-scatter.7
  1631.1 883.0 reduce-scatter.5
where the time goes:
time: 2530 us; the launch traced here: 2520 us
  waiting for transfers between devices  1950 us (77%)
  blocking collectives  160 us (6%)
  local copies, waits for them, and re-layouts  142 us (6%)
  matrix products  138 us (5%)
  other arithmetic  65.6 us (3%)
  starting transfers between devices  48 us (2%)
    reduce_scatter x1, waiting for transfers between devices, shards(): lax.psum_scatter(qkv_grad, ('dp', 'seq'), scatter_dimension=0, tiled=True)  886 us
    reduce_scatter x1, waiting for transfers between devices, shards(): lax.psum_scatter(out_weight_grad, ('dp', 'seq'), scatter_dimension=0, til...  606 us
    all_gather x1, waiting for transfers between devices, shards(): lax.all_gather(w_qkv, ('dp', 'seq'), axis=0, tiled=True)  104 us
    unnamed x2, blocking collectives  85.2 us
    all_to_all x1, waiting for transfers between devices, shards(): lax.all_to_all(expert_out, ('dp', 'seq'), split_axis=0, concat_axis=0, ti...  82.6 us
    all_to_all x1, waiting for transfers between devices, shards(): lax.all_to_all(slot_grad, ('dp', 'seq'), split_axis=0, concat_axis=0, til...  82 us
    all_gather x1, blocking collectives, shards(): lax.all_gather(w_router, ('dp', 'seq'), axis=0, tiled=True)  74.4 us
    all_to_all x1, waiting for transfers between devices, shards(): lax.all_to_all(in_grad.reshape(source_count, capacity, D), ('dp', 'seq'),...  74.4 us
  transfers between devices with their start and end apart: 21, of which 14 were waited for; matrix products, arithmetic and copies ran while one was open for 11% of the time, Pallas kernels for 0%

commit v1 on v0

v1 whole, which is shorter than its diff:
```python
import jax
import jax.numpy as jnp
from jax import lax
from jax.sharding import Mesh
from jax.sharding import PartitionSpec as P

D = 2048
HEADS = 32
KV_HEADS = 4
HEAD_DIM = 128
FF = 768
TOPK = 8
NSEG = 4
TOK_DEV = 128
ROW = 256
QDIM = 4096
KVDIM = 512
NEAR = 2
CORES = 2
LANES = 128

EPS = 1e-06
THETA = 1000000.0
BF = jnp.bfloat16
F32 = jnp.float32

FAR_AXIS = "far"
NEAR_AXIS = "near"
CORE_AXIS = "core"
SEQ_AXIS = "seq"
HEAD_AXES = (NEAR_AXIS, SEQ_AXIS)
ALL_AXES = (FAR_AXIS, NEAR_AXIS, CORE_AXIS, SEQ_AXIS)
DP_AXES = (FAR_AXIS, NEAR_AXIS, CORE_AXIS)


def rms_norm(values, scales):
    return values * lax.rsqrt(jnp.mean(values * values, axis=-1, keepdims=True) + EPS) * scales


def rotary(values, cosine, sine_part):
    half_width = values.shape[-1] // 2
    front_part = values[..., :half_width]
    back_part = values[..., half_width:]
    cos_wide = cosine[..., None, :]
    sin_wide = sine_part[..., None, :]
    return jnp.concatenate(
        [
            front_part * cos_wide - back_part * sin_wide,
            back_part * cos_wide + front_part * sin_wide,
        ],
        axis=-1,
    )


def tables(positions, head_width):
    half_width = head_width // 2
    inverse = THETA ** (-(jnp.arange(half_width, dtype=F32) * 2.0 / head_width))
    angles = positions.astype(F32)[..., None] * inverse
    return (jnp.cos(angles), jnp.sin(angles))


def dot(left, right, dims):
    return lax.dot_general(left, right, (dims, ((), ())), preferred_element_type=F32)


def mm(left, right):
    return dot(left, right, ((1,), (0,)))


def mm_nt(left, right):
    return dot(left, right, ((1,), (1,)))


def mm_tn(left, right):
    return dot(left, right, ((0,), (0,)))


def swap(value, axis):
    return lax.ppermute(value, axis, [(0, 1), (1, 0)])


def pair_order(own, other, axis):
    first = lax.axis_index(axis) == 0
    return (jnp.where(first, own, other), jnp.where(first, other, own))


def exchange(value, axes):
    return lax.all_to_all(value, axes, split_axis=0, concat_axis=0, tiled=True)


def ring_gather(chunk, axis, count):
    here = lax.axis_index(axis)
    zeros = (0,) * chunk.ndim
    full = jnp.zeros((count,) + chunk.shape, chunk.dtype)
    full = lax.dynamic_update_slice(full, chunk[None], (here,) + zeros)
    for step in range(1, count):
        chunk = lax.ppermute(chunk, axis, [(i, (i + 1) % count) for i in range(count)])
        full = lax.dynamic_update_slice(full, chunk[None], (lax.rem(here + count - step, count),) + zeros)
    return full


def shards(tokens, cotangent, w_qkv, w_out, w_router, norm_gains, w_expert, lengths, deal, routes):
    far_count = lax.axis_size(FAR_AXIS)
    device_count = far_count * NEAR * CORES * 2
    experts_all = w_router.shape[1]
    capacity = TOK_DEV * TOPK // experts_all
    slot_count = experts_all * capacity
    seq_index = lax.axis_index(SEQ_AXIS)
    near_index = lax.axis_index(NEAR_AXIS)
    core_index = lax.axis_index(CORE_AXIS)
    per_group = HEADS // KV_HEADS
    qcols = per_group * HEAD_DIM
    width = qcols + 2 * HEAD_DIM
    qkv_rows = w_qkv.shape[0]
    out_rows = w_out.shape[0]
    gain_rows = norm_gains.shape[0]
    score_scale = HEAD_DIM ** (-0.5)

    router_size = qkv_rows * experts_all
    small_size = router_size + gain_rows
    small_rows = -(-small_size // (8 * LANES)) * 8
    small = jnp.concatenate([w_router.reshape(router_size), norm_gains])
    small = jnp.pad(small, (0, small_rows * LANES - small_size)).reshape(1, small_rows, LANES)
    small_all = exchange(
        jnp.broadcast_to(small, (device_count, small_rows, LANES)), ALL_AXES
    ).reshape(device_count, small_rows * LANES)
    router_full = small_all[:, :router_size].reshape(D, experts_all)
    gains_float = small_all[:, router_size:small_size].reshape(-1).astype(F32)
    gain_attn = gains_float[:D]
    gain_ffn = gains_float[D : 2 * D]
    gain_query = gains_float[2 * D : 2 * D + HEAD_DIM]
    gain_key = gains_float[2 * D + HEAD_DIM :]

    tokens_pair = jnp.concatenate(pair_order(tokens, swap(tokens, SEQ_AXIS), SEQ_AXIS), axis=0)
    tokens_both = jnp.stack(pair_order(tokens_pair, swap(tokens_pair, NEAR_AXIS), NEAR_AXIS))
    table = jnp.concatenate([deal, jnp.pad(lengths, ((0, 0), (0, LANES - NSEG)))], axis=1)
    table_both = jnp.concatenate(pair_order(table, swap(table, NEAR_AXIS), NEAR_AXIS), axis=0)
    deal_both = table_both[:, :ROW]
    ends = jnp.cumsum(table_both[:, ROW : ROW + NSEG], axis=1)
    starts = ends - table_both[:, ROW : ROW + NSEG]
    seg_both = jnp.sum((deal_both[:, :, None] >= ends[:, None, :]).astype(jnp.int32), axis=2)
    picked = seg_both[:, :, None] == jnp.arange(NSEG, dtype=jnp.int32)[None, None, :]
    pos_both = deal_both - jnp.sum(jnp.where(picked, starts[:, None, :], 0), axis=2)
    dealt_hot = (deal_both[:, :, None] == jnp.arange(ROW, dtype=jnp.int32)[None, None, :]).astype(BF)
    hot_mine = lax.dynamic_index_in_dim(dealt_hot, near_index, 0, keepdims=False)
    hot_half = lax.dynamic_slice_in_dim(hot_mine, seq_index * TOK_DEV, TOK_DEV, axis=0)
    back_half = lax.dynamic_slice_in_dim(hot_mine, seq_index * TOK_DEV, TOK_DEV, axis=1)
    seg_mine = lax.dynamic_slice_in_dim(
        lax.dynamic_index_in_dim(seg_both, near_index, 0, keepdims=False), seq_index * TOK_DEV, TOK_DEV
    )

    expert_ids = jnp.arange(experts_all, dtype=jnp.int32)
    chosen_rows = jnp.sum(
        (routes[0][:, :, None] == expert_ids[None, None, :]).astype(jnp.int32), axis=1
    ).astype(BF)
    chosen = mm(hot_half, chosen_rows)
    live = jnp.where((seg_mine != NSEG - 1)[:, None], chosen, 0.0)
    steps = jnp.arange(TOK_DEV, dtype=jnp.int32)
    earlier = (steps[None, :] < steps[:, None]).astype(BF)
    place = mm(earlier, live.astype(BF))
    place = jnp.where(live > 0.5, place, -1.0).astype(jnp.int32)
    slot_hot = place.T[:, None, :] == jnp.arange(capacity, dtype=jnp.int32)[None, :, None]
    slot_low = slot_hot.astype(BF).reshape(slot_count, TOK_DEV)

    cot_pair = jnp.concatenate(pair_order(cotangent, swap(cotangent, SEQ_AXIS), SEQ_AXIS), axis=0)
    cot_low = mm(hot_half, cot_pair).astype(BF)
    cot_rows = cot_low.astype(F32)
    cot_sent = mm(slot_low, cot_low).astype(BF).reshape(experts_all, capacity, D)
    cot_back = exchange(cot_sent, ALL_AXES).reshape(slot_count, D)

    wide = jnp.concatenate(
        [
            w_qkv[:, :QDIM].reshape(qkv_rows, KV_HEADS, qcols),
            w_qkv[:, QDIM : QDIM + KVDIM].reshape(qkv_rows, KV_HEADS, HEAD_DIM),
            w_qkv[:, QDIM + KVDIM :].reshape(qkv_rows, KV_HEADS, HEAD_DIM),
        ],
        axis=2,
    ).transpose(1, 0, 2)
    core_rows = KV_HEADS * qkv_rows
    qkv_own = ring_gather(exchange(wide, HEAD_AXES).reshape(core_rows, width), FAR_AXIS, far_count)
    qkv_own = qkv_own.reshape(far_count * core_rows, width)
    qkv_other = swap(qkv_own, CORE_AXIS)

    def split_core(values):
        parts = values.reshape(values.shape[0], far_count * NEAR, CORES, 2 * qkv_rows)
        own = jnp.where(core_index == 0, parts[:, :, 0], parts[:, :, 1])
        other = jnp.where(core_index == 0, parts[:, :, 1], parts[:, :, 0])
        return (own.reshape(values.shape[0], D // 2), other.reshape(values.shape[0], D // 2))

    def join_core(own, other):
        shape = (own.shape[0], far_count * NEAR, 2 * qkv_rows)
        return jnp.stack(
            pair_order(own.reshape(shape), other.reshape(shape), CORE_AXIS), axis=2
        ).reshape(own.shape[0], D)

    out_slabs = ring_gather(w_out, FAR_AXIS, far_count).reshape(
        KV_HEADS, far_count // KV_HEADS * out_rows, D
    )
    out_mates = exchange(out_slabs, HEAD_AXES).reshape(NEAR, 2, far_count // KV_HEADS, out_rows, D)
    out_own = out_mates.transpose(2, 0, 1, 3, 4).reshape(qcols // 2, D)
    out_other = swap(out_own, CORE_AXIS)
    far_part = far_count // KV_HEADS

    def split_heads(values):
        parts = values.reshape(values.shape[0], far_part * NEAR, CORES, 2 * out_rows)
        own = jnp.where(core_index == 0, parts[:, :, 0], parts[:, :, 1])
        other = jnp.where(core_index == 0, parts[:, :, 1], parts[:, :, 0])
        return (own.reshape(values.shape[0], qcols // 2), other.reshape(values.shape[0], qcols // 2))

    def join_heads(own, other):
        shape = (own.shape[0], far_part * NEAR, 2 * out_rows)
        return jnp.stack(
            pair_order(own.reshape(shape), other.reshape(shape), CORE_AXIS), axis=2
        ).reshape(own.shape[0], qcols)

    x_both = lax.dot_general(
        dealt_hot, tokens_both, (((2,), (1,)), ((0,), (0,))), preferred_element_type=F32
    )
    x_rows = lax.dynamic_slice(
        x_both, (near_index, seq_index * TOK_DEV, 0), (1, TOK_DEV, D)
    )[0]
    normed_low = rms_norm(x_both.reshape(2 * ROW, D), gain_attn).astype(BF)
    normed_own, normed_other = split_core(normed_low)
    projected = mm(normed_own, qkv_own) + mm(normed_other, qkv_other)
    cosine, sine_part = tables(pos_both.reshape(2 * ROW), HEAD_DIM)

    def head_piece(proj_qk, scale_query, scale_key):
        query_raw = proj_qk[:, :qcols].reshape(2 * ROW, per_group, HEAD_DIM)
        key_raw = proj_qk[:, qcols:].reshape(2 * ROW, 1, HEAD_DIM)
        return (
            rotary(rms_norm(query_raw, scale_query), cosine, sine_part),
            rotary(rms_norm(key_raw, scale_key), cosine, sine_part),
        )

    (queries, key_rot), head_back = jax.vjp(
        head_piece, projected[:, : qcols + HEAD_DIM], gain_query, gain_key
    )
    query_heads = queries.astype(BF).reshape(2, ROW, per_group, HEAD_DIM)
    key_heads = key_rot.astype(BF).reshape(2, ROW, HEAD_DIM)
    value_heads = projected[:, qcols + HEAD_DIM :].astype(BF).reshape(2, ROW, HEAD_DIM)
    allowed = (seg_both[:, :, None] == seg_both[:, None, :]) & (
        pos_both[:, None, :] <= pos_both[:, :, None]
    )
    scores = (
        jnp.einsum("bqgd,bsd->bgqs", query_heads, key_heads, preferred_element_type=F32) * score_scale
    )
    scores = jnp.where(allowed[:, None], scores, -1e30)
    prob_full = jax.nn.softmax(scores, axis=-1)
    prob_low = prob_full.astype(BF)
    mixed_heads = jnp.einsum("bgqs,bsd->bqgd", prob_low, value_heads, preferred_element_type=F32)
    mixed_low = mixed_heads.astype(BF).reshape(2 * ROW, qcols)
    mixed_own, mixed_other = split_heads(mixed_low)
    out_partial = mm(mixed_own, out_own) + mm(mixed_other, out_other)
    out_parts = exchange(out_partial.astype(BF).reshape(4, TOK_DEV, D), HEAD_AXES)
    residual = x_rows + jnp.sum(out_parts.astype(F32), axis=0)

    normed_two, ffn_back = jax.vjp(rms_norm, residual, gain_ffn)
    ffn_in = normed_two.astype(BF)
    send_rows = mm(slot_low, ffn_in).astype(BF).reshape(experts_all, capacity, D)
    in_flat = exchange(send_rows, ALL_AXES).reshape(slot_count, D)
    logits = mm(ffn_in, router_full)
    logits = jnp.where(chosen > 0.5, logits, -1e30)
    gate_probs = jax.nn.softmax(logits, axis=-1)
    gate_probs = jnp.where(chosen > 0.5, gate_probs, 0.0)
    slot_gate = jnp.sum(jnp.where(slot_hot, gate_probs.T[:, None, :], 0.0), axis=2)
    gate_back = exchange(slot_gate[:, None, :], ALL_AXES).reshape(slot_count, 1)

    expert_weight = w_expert[0]
    gate_up = mm(in_flat, expert_weight[:, : 2 * FF])
    gate_pre = gate_up[:, :FF]
    up_pre = gate_up[:, FF:]
    sig_gate = jax.nn.sigmoid(gate_pre)
    silu_val = gate_pre * sig_gate
    active = (silu_val * up_pre).astype(BF)
    expert_out = mm_nt(active, expert_weight[:, 2 * FF :]).astype(BF)
    cot_float = cot_back.astype(F32)
    slot_dot = jnp.sum(cot_float * expert_out.astype(F32), axis=1)
    dot_back = exchange(slot_dot.reshape(device_count, 1, capacity), ALL_AXES).reshape(
        experts_all, capacity
    )
    grad_flat = (gate_back * cot_float).astype(BF)
    act_grad = mm(grad_flat, expert_weight[:, 2 * FF :])
    silu_slope = sig_gate * (1.0 + gate_pre * (1.0 - sig_gate))
    gu_grad = jnp.concatenate([act_grad * up_pre * silu_slope, act_grad * silu_val], axis=1).astype(BF)
    in_grad = mm_nt(gu_grad, expert_weight[:, : 2 * FF]).astype(BF)
    pair_grads = exchange(in_grad.reshape(device_count, capacity, D), ALL_AXES).reshape(slot_count, D)
    returned = exchange(expert_out.reshape(device_count, capacity, D), ALL_AXES).reshape(slot_count, D)
    grad_expert = jnp.concatenate([mm_tn(in_flat, gu_grad), mm_tn(grad_flat, active)], axis=1)[None]

    gate_grad = jnp.sum(jnp.where(slot_hot, dot_back[:, :, None], 0.0), axis=1).T
    mean_term = jnp.sum(gate_probs * gate_grad, axis=1, keepdims=True)
    logit_grad = (gate_probs * (gate_grad - mean_term)).astype(BF)
    router_grad = mm_tn(ffn_in, logit_grad)
    ffn_in_grad = mm_tn(slot_low, pair_grads) + mm_nt(logit_grad, router_full)
    resid_part, gain_ffn_grad = ffn_back(ffn_in_grad)
    resid_low = (cot_rows + resid_part).astype(BF)
    resid_pair = jnp.concatenate(pair_order(resid_low, swap(resid_low, SEQ_AXIS), SEQ_AXIS), axis=0)
    resid_both = jnp.concatenate(
        pair_order(resid_pair, swap(resid_pair, NEAR_AXIS), NEAR_AXIS), axis=0
    )

    gate_slots = jnp.where(slot_hot, gate_probs.T[:, None, :], 0.0).reshape(slot_count, TOK_DEV)
    gate_high = gate_slots.astype(BF)
    gate_rest = (gate_slots - gate_high.astype(F32)).astype(BF)
    final_rows = (residual + mm_tn(gate_high, returned) + mm_tn(gate_rest, returned)).astype(BF)
    final_pair = jnp.concatenate(
        pair_order(final_rows, swap(final_rows, SEQ_AXIS), SEQ_AXIS), axis=0
    )
    layer_out = mm_tn(back_half, final_pair).astype(BF)

    mixed_grad = join_heads(mm_nt(resid_both, out_own), mm_nt(resid_both, out_other)).astype(BF)
    grad_heads = mixed_grad.reshape(2, ROW, per_group, HEAD_DIM)
    out_grad = mm_tn(mixed_own, resid_both) + swap(
        mm_tn(mixed_other, resid_both).astype(BF), CORE_AXIS
    ).astype(F32)
    out_grad = (
        out_grad.astype(BF)
        .reshape(far_part, NEAR * 2, out_rows, D)
        .transpose(1, 0, 2, 3)
        .reshape(NEAR * 2, far_part * out_rows, D)
    )
    out_grad = exchange(out_grad, HEAD_AXES).reshape(far_count, out_rows, D)
    out_share = jnp.sum(exchange(out_grad, FAR_AXIS).astype(F32), axis=0)

    value_grad = jnp.einsum("bgqs,bqgd->bsd", prob_low, grad_heads, preferred_element_type=F32)
    prob_grad = jnp.einsum("bqgd,bsd->bgqs", grad_heads, value_heads, preferred_element_type=F32)
    score_grad = (
        prob_full * (prob_grad - jnp.sum(prob_full * prob_grad, axis=-1, keepdims=True))
    ).astype(BF)
    query_grad = (
        jnp.einsum("bgqs,bsd->bqgd", score_grad, key_heads, preferred_element_type=F32) * score_scale
    )
    key_grad = (
        jnp.einsum("bgqs,bqgd->bsd", score_grad, query_heads, preferred_element_type=F32) * score_scale
    )
    qk_grad, query_gain_grad, key_gain_grad = head_back(
        (
            query_grad.reshape(2 * ROW, per_group, HEAD_DIM),
            key_grad.reshape(2 * ROW, 1, HEAD_DIM),
        )
    )
    proj_grad = jnp.concatenate([qk_grad, value_grad.reshape(2 * ROW, HEAD_DIM)], axis=1).astype(BF)
    back_grad = lax.dot_general(
        dealt_hot,
        proj_grad.reshape(2, ROW, width),
        (((1,), (1,)), ((0,), (0,))),
        preferred_element_type=F32,
    ).astype(BF).reshape(2 * ROW, width)
    normed_partial = jnp.concatenate(
        [mm_nt(back_grad, qkv_own), mm_nt(back_grad, qkv_other)], axis=1
    ).astype(BF)
    normed_parts = exchange(normed_partial.reshape(4, TOK_DEV, D), HEAD_AXES)
    normed_grad = jnp.sum(normed_parts.astype(F32), axis=0)
    normed_grad = join_core(normed_grad[:, : D // 2], normed_grad[:, D // 2 :])
    _, attn_back = jax.vjp(rms_norm, tokens.astype(F32), gain_attn)
    input_part, gain_attn_grad = attn_back(normed_grad)
    resid_group = lax.dynamic_slice_in_dim(resid_both, near_index * ROW, ROW, axis=0)
    grad_tokens = (mm_tn(back_half, resid_group) + input_part).astype(BF)

    qkv_grad = mm_tn(normed_own, proj_grad) + swap(
        mm_tn(normed_other, proj_grad).astype(BF), CORE_AXIS
    ).astype(F32)
    qkv_grad = exchange(qkv_grad.astype(BF).reshape(far_count, core_rows, width), FAR_AXIS)
    qkv_grad = jnp.sum(qkv_grad.astype(F32), axis=0).astype(BF).reshape(KV_HEADS, qkv_rows, width)
    qkv_grad = exchange(qkv_grad, HEAD_AXES).transpose(1, 0, 2).astype(F32)
    qkv_share = jnp.concatenate(
        [
            qkv_grad[:, :, :qcols].reshape(qkv_rows, QDIM),
            qkv_grad[:, :, qcols : qcols + HEAD_DIM].reshape(qkv_rows, KVDIM),
            qkv_grad[:, :, qcols + HEAD_DIM :].reshape(qkv_rows, KVDIM),
        ],
        axis=1,
    )

    gains_grad = jnp.concatenate([gain_attn_grad, gain_ffn_grad, query_gain_grad, key_gain_grad])
    small_grad = jnp.concatenate(
        [router_grad.reshape(device_count, router_size), gains_grad.reshape(device_count, gain_rows)],
        axis=1,
    )
    small_grad = jnp.pad(small_grad, ((0, 0), (0, small_rows * LANES - small_size)))
    small_share = jnp.sum(
        exchange(small_grad.reshape(device_count, small_rows, LANES), ALL_AXES), axis=0
    ).reshape(small_rows * LANES)
    router_share = small_share[:router_size].reshape(qkv_rows, experts_all)
    gains_share = small_share[router_size:small_size]
    return (layer_out, grad_tokens, qkv_share, out_share, router_share, gains_share, grad_expert)


def solution(mesh):
    shape = dict(mesh.shape)
    inner = Mesh(
        mesh.devices.reshape(shape["dp"] // (NEAR * CORES), NEAR, CORES, shape["seq"]), ALL_AXES
    )
    rows = P(ALL_AXES, None)
    in_specs = (
        rows,
        rows,
        rows,
        rows,
        rows,
        P(ALL_AXES),
        P(ALL_AXES, None, None),
        P(DP_AXES, None),
        P(DP_AXES, None),
        P(DP_AXES, None, None),
    )
    out_specs = (rows, rows, rows, rows, rows, P(ALL_AXES), P(ALL_AXES, None, None))
    return jax.shard_map(shards, mesh=inner, in_specs=in_specs, out_specs=out_specs, check_vma=False)
```

time: 2530 us -> 983 us (0.39)
  waiting for transfers between devices: 1950 us -> 551 us
  blocking collectives: 160 us -> 35.6 us
  local copies, waits for them, and re-layouts: 142 us -> 91.6 us
  starting transfers between devices: 48 us -> 78.3 us
    reduce_scatter x2 -> x0, waiting for transfers between devices: 1490 us -> none  [the longest x1 886 us: shards(): lax.psum_scatter(qkv_grad, ('dp', 'seq'), scatter_dimension=0, tiled=True)]
    all_to_all x12 -> x14, waiting for transfers between devices: 304 us -> 460 us  [exchange(): return lax.all_to_all(value, axes, split_axis=0, concat_axis=0, tiled=True)]
    all_gather x6 -> x0, waiting for transfers between devices: 153 us -> none  [the longest x1 104 us: shards(): lax.all_gather(w_qkv, ('dp', 'seq'), axis=0, tiled=True)]
    ppermute x0 -> x17, waiting for transfers between devices: none -> 91 us  [the longest x6 56.4 us: ring_gather(): lax.ppermute(chunk, axis, [(i, (i + 1) % count) for i in range(count)])]
    unnamed x2 -> x0, blocking collectives: 85.2 us -> none
    all_gather x1 -> x0, blocking collectives: 74.4 us -> none  [shards(): lax.all_gather(w_router, ('dp', 'seq'), axis=0, tiled=True)]
    gather x19 -> x0, local copies, waits for them, and re-layouts: 69.1 us -> none  [the longest x1 11.6 us: shards(): jnp.take(padded_grads, pair_slot, axis=0).reshape(TOK_DEV, TOPK, D)]
    all_to_all x0 -> x2, blocking collectives: none -> 35.6 us  [exchange(): return lax.all_to_all(value, axes, split_axis=0, concat_axis=0, tiled=True)]
  transfers between devices with their start and end apart: 21 -> 31, of which waited for: 14 -> 20; matrix products, arithmetic and copies ran while one was open for 11% -> 20% of each run, Pallas kernels for 0% -> 0%
where the time goes in v1:
time: 983 us; the launch traced here: 976 us
  waiting for transfers between devices  551 us (56%)
  matrix products  145 us (15%)
  local copies, waits for them, and re-layouts  91.6 us (9%)
  starting transfers between devices  78.3 us (8%)
  other arithmetic  71.9 us (7%)
  blocking collectives  35.6 us (4%)
    all_to_all x14, waiting for transfers between devices, exchange(): return lax.all_to_all(value, axes, split_axis=0, concat_axis=0, tiled=True)  460 us
    dot_general x31, matrix products, dot(): lax.dot_general(left, right, (dims, ((), ())), preferred_element_type=F32)  125 us
    all_to_all x14, starting transfers between devices, exchange(): return lax.all_to_all(value, axes, split_axis=0, concat_axis=0, tiled=True)  62 us
    ppermute x6, waiting for transfers between devices, ring_gather(): lax.ppermute(chunk, axis, [(i, (i + 1) % count) for i in range(count)])  56.4 us
    all_to_all x2, blocking collectives, exchange(): return lax.all_to_all(value, axes, split_axis=0, concat_axis=0, tiled=True)  35.6 us
    ppermute x11, waiting for transfers between devices, swap(): return lax.ppermute(value, axis, [(0, 1), (1, 0)])  34.7 us
    unnamed x210, local copies, waits for them, and re-layouts  33.3 us
  transfers between devices with their start and end apart: 31, of which 20 were waited for; matrix products, arithmetic and copies ran while one was open for 20% of the time, Pallas kernels for 0%

profile of v1, /device:TPU:0, one launch (start us, length us, event | category | flops | bytes accessed | tf_op | source)
XLA Modules:
  0.0 976.4 jit_solution(2496294479850973927)
XLA Ops:
  6.6 4.9 all-to-all-start
  23.6 7.1 all-to-all-done
  30.7 4.2 all-to-all-start.1
  35.9 10.2 %all-to-all-done.1 = bf16[4,64,1280]{2,1,0:T(8,128)(2,1)} async-done(((bf16[4,64,1280]{2,1,0:T(8,128)(2,1)}), bf16[4,64,1280]{2,1,0:T(8,128)(2,1)}, u32[]{:S(2)}, u32[]{:S(2)}) %all-to-all-start.1) | async-done | bytes 655392 | tf_op jit(solution)/shard_map/all_to_all | solution.py:88
  53.9 11.9 %collective-permute-done.3 = bf16[256,1280]{1,0:T(8,128)(2,1)S(1)} collective-permute-done((bf16[256,1280]{1,0:T(8,128)(2,1)}, bf16[256,1280]{1,0:T(8,128)(2,1)S(1)}, u32[]{:S(2)}, u32[]{:S(2)}) %collective-permute-start.3) | collective-permute-done | bytes 655392 | tf_op jit(solution)/shard_map/ppermute | solution.py:97
  70.4 6.6 collective-permute-done.8
  77.0 14.0 %collective-permute-done.4 = bf16[256,1280]{1,0:T(8,128)(2,1)S(1)} collective-permute-done((bf16[256,1280]{1,0:T(8,128)(2,1)S(1)}, bf16[256,1280]{1,0:T(8,128)(2,1)S(1)}, u32[]{:S(2)}, u32[]{:S(2)}) %collective-permute-start.4) | collective-permute-done | bytes 655392 | tf_op jit(solution)/shard_map/ppermute | solution.py:97
  91.2 23.8 %collective-permute-done.5 = bf16[256,1280]{1,0:T(8,128)(2,1)S(1)} collective-permute-done((bf16[256,1280]{1,0:T(8,128)(2,1)S(1)}, bf16[256,1280]{1,0:T(8,128)(2,1)S(1)}, u32[]{:S(2)}, u32[]{:S(2)}) %collective-permute-start.5) | collective-permute-done | bytes 655392 | tf_op jit(solution)/shard_map/ppermute | solution.py:97
  117.0 4.9 all-to-all-start.2
  126.6 6.6 reshape.586
  133.2 7.2 copy.213
  144.5 3.5 all-to-all-done.2
  148.0 3.7 fusion.159
  164.3 5.8 fusion.156
  176.2 3.4 broadcast_select_fusion.1
  187.7 4.4 add_convert_fusion.2
  192.1 4.6 all-to-all-start.3
  198.6 23.9 %all-to-all-done.3 = bf16[4,128,2048]{2,1,0:T(8,128)(2,1)} async-done(((bf16[4,128,2048]{2,1,0:T(8,128)(2,1)}), bf16[4,128,2048]{2,1,0:T(8,128)(2,1)}, u32[]{:S(2)}, u32[]{:S(2)}) %all-to-all-start.3) | async-done | bytes 2097184 | tf_op jit(solution)/shard_map/all_to_all | solution.py:88
  227.7 3.2 convolution_convert_fusion.3
  231.0 3.6 all-to-all-start.4
  238.6 3.3 convolution_convert_fusion.1
  241.9 86.4 %all-to-all-done.4 = bf16[32,32,2048]{2,1,0:T(8,128)(2,1)} async-done(((bf16[32,32,2048]{2,1,0:T(8,128)(2,1)}), bf16[32,32,2048]{2,1,0:T(8,128)(2,1)}, u32[]{:S(2)}, u32[]{:S(2)}) %all-to-all-start.4) | async-done | bytes 4194336 | tf_op jit(solution)/shard_map/all_to_all | solution.py:88
  328.3 4.9 all-to-all-start.7
  336.9 10.1 %fusion.5 = f32[1024,1536]{1,0:T(8,128)S(1)} fusion(bf16[1024,2048]{1,0:T(8,128)(2,1)} %bitcast.43, bf16[2048,2304]{1,0:T(8,128)(2,1)} %bitcast.346), kind=kOutput, calls=%fused_computation.8 | convolution fusion | flops 6442450944 | bytes 16777216 | tf_op jit(solution)/shard_map/dot_general | solution.py:63
  351.8 75.2 %all-to-all-done.7 = bf16[32,32,2048]{2,1,0:T(8,128)(2,1)} async-done(((bf16[32,32,2048]{2,1,0:T(8,128)(2,1)}), bf16[32,32,2048]{2,1,0:T(8,128)(2,1)}, u32[]{:S(2)}, u32[]{:S(2)}) %all-to-all-start.7) | async-done | bytes 4194336 | tf_op jit(solution)/shard_map/all_to_all | solution.py:88
  427.0 9.2 fusion.2
  436.9 4.8 all-to-all-start.9
  441.7 7.2 all-to-all-done.9
  449.2 8.9 all_to_all.80
  459.5 3.1 fusion.1
  463.6 7.9 multiply_convert_fusion.2
  471.6 8.2 fusion.10
  479.9 4.0 all-to-all-start.8
  483.9 93.7 %all-to-all-done.8 = bf16[32,32,2048]{2,1,0:T(8,128)(2,1)} async-done(((bf16[32,32,2048]{2,1,0:T(8,128)(2,1)}), bf16[32,32,2048]{2,1,0:T(8,128)(2,1)}, u32[]{:S(2)}, u32[]{:S(2)}) %all-to-all-start.8) | async-done | bytes 4194336 | tf_op jit(solution)/shard_map/all_to_all | solution.py:88
  583.6 12.2 %collective-permute-done.13 = bf16[128,2048]{1,0:T(8,128)(2,1)S(1)} collective-permute-done((bf16[128,2048]{1,0:T(8,128)(2,1)S(1)}, bf16[128,2048]{1,0:T(8,128)(2,1)S(1)}, u32[]{:S(2)}, u32[]{:S(2)}) %collective-permute-start.13) | collective-permute-done | bytes 524320 | tf_op jit(solution)/shard_map/ppermute | solution.py:79
  597.3 22.5 %collective-permute-done.14 = bf16[256,2048]{1,0:T(8,128)(2,1)S(1)} collective-permute-done((bf16[256,2048]{1,0:T(8,128)(2,1)S(1)}, bf16[256,2048]{1,0:T(8,128)(2,1)S(1)}, u32[]{:S(2)}, u32[]{:S(2)}) %collective-permute-start.14) | collective-permute-done | bytes 1048608 | tf_op jit(solution)/shard_map/ppermute | solution.py:79
  620.4 4.4 fusion.152
  626.9 3.6 fusion.68
  635.2 4.0 fusion.42
  660.2 4.2 add_add_fusion
  669.2 3.3 fusion.34
  672.7 26.7 %all_to_all.81 = bf16[4,128,2048]{2,1,0:T(8,128)(2,1)S(1)} all-to-all(bf16[4,128,2048]{2,1,0:T(8,128)(2,1)S(1)} %pad_maximum_fusion.2), channel_id=1, replica_groups=mesh['far'=4,'near'=2,'core'=2,'seq'=2] {'near','seq'}, dimensions={0} | all-to-all | bytes 4194304 | tf_op jit(solution)/shard_map/all_to_all | solution.py:88
  699.4 5.0 all-to-all-start.5
  705.6 4.3 convolution_convert_fusion.4
  713.5 4.7 convolution_convert_fusion
  726.0 72.1 %all-to-all-done.5 = bf16[32,32,2048]{2,1,0:T(8,128)(2,1)} async-done(((bf16[32,32,2048]{2,1,0:T(8,128)(2,1)}), bf16[32,32,2048]{2,1,0:T(8,128)(2,1)}, u32[]{:S(2)}, u32[]{:S(2)}) %all-to-all-start.5) | async-done | bytes 4194336 | tf_op jit(solution)/shard_map/all_to_all | solution.py:88
  798.1 4.8 all-to-all-start.15
  802.9 4.9 add_convert_fusion.1
  807.8 7.8 all-to-all-done.15
  815.6 4.5 all-to-all-start.13
  820.1 5.1 add_convert_fusion
  825.2 20.9 %all-to-all-done.13 = bf16[4,128,2048]{2,1,0:T(8,128)(2,1)} async-done(((bf16[4,128,2048]{2,1,0:T(8,128)(2,1)}), bf16[4,128,2048]{2,1,0:T(8,128)(2,1)}, u32[]{:S(2)}, u32[]{:S(2)}) %all-to-all-start.13) | async-done | bytes 2097184 | tf_op jit(solution)/shard_map/all_to_all | solution.py:88
  846.1 4.9 all-to-all-start.11
  851.1 11.9 %fusion.33 = f32[2048,1536]{0,1:T(8,128)} fusion(bf16[1024,2048]{1,0:T(8,128)(2,1)} %bitcast.43, bf16[1024,768]{1,0:T(8,128)(2,1)} %copy-done.92, bf16[1024,768]{1,0:T(8,128)(2,1)S(1)} %copy-done.91), kind=kOutput, calls=%fused_computation.85 | convolution fusion | flops 6448742400 | bytes 19922944 | tf_op jit(solution)/shard_map/dot_general | solution.py:63
  863.0 47.8 %all-to-all-done.11 = bf16[4,256,1280]{2,1,0:T(8,128)(2,1)} async-done(((bf16[4,256,1280]{2,1,0:T(8,128)(2,1)}), bf16[4,256,1280]{2,1,0:T(8,128)(2,1)}, u32[]{:S(2)}, u32[]{:S(2)}) %all-to-all-start.11) | async-done | bytes 2621472 | tf_op jit(solution)/shard_map/all_to_all | solution.py:88
  910.9 3.6 all-to-all-start.14
  914.5 6.0 fusion.161
  920.5 3.1 convolution_bitcast_fusion.1
  923.6 3.7 fusion.22
  928.8 6.9 maximum_bitcast_fusion
  935.7 18.7 %copy.245 = f32[1,2048,2304]{2,1,0:T(8,128)} copy(f32[1,2048,2304]{1,2,0:T(8,128)} %maximum_bitcast_fusion) | data formatting | bytes 37748736
  956.7 3.2 reduce_sum.311
  962.2 3.5 all-to-all-start.12
  965.7 3.1 fusion.23
  (391 shorter events, 157.7 us)
Async XLA Ops:
  0.6 15.8 %slice-start.3 = ((bf16[64,5120]{1,0:T(8,128)(2,1)}), bf16[64,4096]{1,0:T(8,128)(2,1)S(1)}, s32[]{:S(2)}) async-start(bf16[64,5120]{1,0:T(8,128)(2,1)} %param.12), calls=%async_computation.19 | async-start | bytes 1048576 | tf_op jit(solution)/shard_map/slice | solution.py:173
  1.4 19.1 %collective-permute-start = (s32[1,384]{1,0:T(1,128)S(1)}, s32[1,384]{1,0:T(1,128)S(1)}, u32[]{:S(2)}, u32[]{:S(2)}) collective-permute-start(s32[1,384]{1,0:T(1,128)S(1)} %pad_add_fusion.2), channel_id=1, source_target_pairs={{0,4},{4,0},{1,5},{5,1},{2,6},{6,2},{3,7},{7,3},{8,12},{12,8},{9,1... | collective-permute-start | bytes 4616 | tf_op jit(solution)/shard_map/ppermute | solution.py:79
  6.6 24.1 %all-to-all-start = ((bf16[32,24,128]{2,1,0:T(8,128)(2,1)}), bf16[32,24,128]{2,1,0:T(8,128)(2,1)S(1)}, u32[]{:S(2)}, u32[]{:S(2)}) async-start(bf16[32,24,128]{2,1,0:T(8,128)(2,1)} %broadcast_in_dim.172), calls=%async_computation | async-start | bytes 393216 | tf_op jit(solution)/shard_map/all_to_all | solution.py:88
  11.5 39.0 %collective-permute-start.12 = (bf16[128,2048]{1,0:T(8,128)(2,1)}, bf16[128,2048]{1,0:T(8,128)(2,1)S(1)}, u32[]{:S(2)}, u32[]{:S(2)}) collective-permute-start(bf16[128,2048]{1,0:T(8,128)(2,1)} %param.11), channel_id=1, source_target_pairs={{0,1},{1,0},{2,3},{3,2},{4,5},{5,4},{6,7},{7,6},{8,9},{9,8},{10,11... | collective-permute-start | bytes 1572872 | tf_op jit(solution)/shard_map/ppermute | solution.py:79
  13.4 35.6 %collective-permute-start.7 = (bf16[128,2048]{1,0:T(8,128)(2,1)}, bf16[128,2048]{1,0:T(8,128)(2,1)}, u32[]{:S(2)}, u32[]{:S(2)}) collective-permute-start(bf16[128,2048]{1,0:T(8,128)(2,1)} %param.13), channel_id=1, source_target_pairs={{0,8},{8,16},{16,24},{24,0},{1,9},{9,17},{17,25},{25,1},{2,10},{10... | collective-permute-start | bytes 1572872 | tf_op jit(solution)/shard_map/ppermute | solution.py:97
  14.8 36.5 %collective-permute-start.1 = (bf16[128,2048]{1,0:T(8,128)(2,1)}, bf16[128,2048]{1,0:T(8,128)(2,1)}, u32[]{:S(2)}, u32[]{:S(2)}) collective-permute-start(bf16[128,2048]{1,0:T(8,128)(2,1)} %param.10), channel_id=1, source_target_pairs={{0,1},{1,0},{2,3},{3,2},{4,5},{5,4},{6,7},{7,6},{8,9},{9,8},{10,11... | collective-permute-start | bytes 1572872 | tf_op jit(solution)/shard_map/ppermute | solution.py:79
  15.4 147.0 %copy-start.77 = (f32[64]{0:T(128)}, f32[64]{0:T(128)S(1)}, u32[]{:S(2)}) copy-start(f32[64]{0:T(128)S(1)} %negate_power_fusion) | copy-start | bytes 772
  20.5 176.3 %copy-start.57 = (s32[2,256]{1,0:T(2,128)}, s32[2,256]{1,0:T(2,128)S(1)}, u32[]{:S(2)}) copy-start(s32[2,256]{1,0:T(2,128)S(1)} %fusion.134) | copy-start | bytes 6148
  20.9 141.5 %copy-start.59 = (f32[1,2,2,128]{3,1,2,0:T(2,128)}, f32[1,2,2,128]{3,1,2,0:T(2,128)S(1)}, u32[]{:S(2)}) copy-start(f32[1,2,2,128]{3,1,2,0:T(2,128)S(1)} %copy.271) | copy-start | bytes 6148
  30.7 15.4 %all-to-all-start.1 = ((bf16[4,64,1280]{2,1,0:T(8,128)(2,1)}), bf16[4,64,1280]{2,1,0:T(8,128)(2,1)}, u32[]{:S(2)}, u32[]{:S(2)}) async-start(bf16[4,64,1280]{2,1,0:T(8,128)(2,1)} %copy.216), calls=%async_computation.1 | async-start | bytes 1310720 | tf_op jit(solution)/shard_map/all_to_all | solution.py:88
  35.7 11.9 %copy-start.54 = (f32[4352]{0:T(1024)}, f32[4352]{0:T(1024)S(1)}, u32[]{:S(2)}) copy-start(f32[4352]{0:T(1024)S(1)} %reshape.622) | copy-start | bytes 52228
  35.8 120.7 %copy-start.69 = (f32[128]{0:T(128)}, f32[128]{0:T(128)S(1)}, u32[]{:S(2)}) copy-start(f32[128]{0:T(128)S(1)} %get-tuple-element.117) | copy-start | bytes 1540
  35.8 125.6 %copy-start.71 = (f32[128]{0:T(128)}, f32[128]{0:T(128)S(1)}, u32[]{:S(2)}) copy-start(f32[128]{0:T(128)S(1)} %get-tuple-element.118) | copy-start | bytes 1540
  46.1 19.7 %collective-permute-start.3 = (bf16[256,1280]{1,0:T(8,128)(2,1)}, bf16[256,1280]{1,0:T(8,128)(2,1)S(1)}, u32[]{:S(2)}, u32[]{:S(2)}) collective-permute-start(bf16[256,1280]{1,0:T(8,128)(2,1)} %bitcast.8), channel_id=1, source_target_pairs={{0,8},{8,16},{16,24},{24,0},{1,9},{9,17},{17,25},{25,1},{2,10},{10... | collective-permute-start | bytes 1966088 | tf_op jit(solution)/shard_map/ppermute | solution.py:97
  49.0 28.0 %collective-permute-start.8 = (bf16[128,2048]{1,0:T(8,128)(2,1)}, bf16[128,2048]{1,0:T(8,128)(2,1)S(1)}, u32[]{:S(2)}, u32[]{:S(2)}) collective-permute-start(bf16[128,2048]{1,0:T(8,128)(2,1)} %collective-permute-done.7), channel_id=1, source_target_pairs={{0,8},{8,16},{16,24},{24,0},{1,9},{9,17},{17,25},{25,1},{2,10},{10... | collective-permute-start | bytes 1572872 | tf_op jit(solution)/shard_map/ppermute | solution.py:97
  53.9 37.3 %copy-start.8 = (bf16[128,2048]{1,0:T(8,128)(2,1)}, bf16[128,2048]{1,0:T(8,128)(2,1)S(1)}, u32[]{:S(2)}) copy-start(bf16[128,2048]{1,0:T(8,128)(2,1)S(1)} %get-tuple-element.134) | copy-start | bytes 1572868
  65.8 25.3 %collective-permute-start.4 = (bf16[256,1280]{1,0:T(8,128)(2,1)S(1)}, bf16[256,1280]{1,0:T(8,128)(2,1)S(1)}, u32[]{:S(2)}, u32[]{:S(2)}) collective-permute-start(bf16[256,1280]{1,0:T(8,128)(2,1)S(1)} %collective-permute-done.3), channel_id=1, source_target_pairs={{0,8},{8,16},{16,24},{24,0},{1,9},{9,17},{17,25},{25,1},{2,10},{10... | collective-permute-start | bytes 1966088 | tf_op jit(solution)/shard_map/ppermute | solution.py:97
  66.8 55.1 %collective-permute-start.2 = (bf16[256,2048]{1,0:T(8,128)(2,1)}, bf16[256,2048]{1,0:T(8,128)(2,1)}, u32[]{:S(2)}, u32[]{:S(2)}) collective-permute-start(bf16[256,2048]{1,0:T(8,128)(2,1)} %pad_maximum_fusion.7), channel_id=1, source_target_pairs={{0,4},{4,0},{1,5},{5,1},{2,6},{6,2},{3,7},{7,3},{8,12},{12,8},{9,1... | collective-permute-start | bytes 3145736 | tf_op jit(solution)/shard_map/ppermute | solution.py:79
  77.0 39.1 %collective-permute-start.9 = (bf16[128,2048]{1,0:T(8,128)(2,1)S(1)}, bf16[128,2048]{1,0:T(8,128)(2,1)S(1)}, u32[]{:S(2)}, u32[]{:S(2)}) collective-permute-start(bf16[128,2048]{1,0:T(8,128)(2,1)S(1)} %collective-permute-done.8), channel_id=1, source_target_pairs={{0,8},{8,16},{16,24},{24,0},{1,9},{9,17},{17,25},{25,1},{2,10},{10... | collective-permute-start | bytes 1572872 | tf_op jit(solution)/shard_map/ppermute | solution.py:97
  91.1 23.9 %collective-permute-start.5 = (bf16[256,1280]{1,0:T(8,128)(2,1)S(1)}, bf16[256,1280]{1,0:T(8,128)(2,1)S(1)}, u32[]{:S(2)}, u32[]{:S(2)}) collective-permute-start(bf16[256,1280]{1,0:T(8,128)(2,1)S(1)} %collective-permute-done.4), channel_id=1, source_target_pairs={{0,8},{8,16},{16,24},{24,0},{1,9},{9,17},{17,25},{25,1},{2,10},{10... | collective-permute-start | bytes 1966088 | tf_op jit(solution)/shard_map/ppermute | solution.py:97
  115.0 36.7 %copy-start.4 = (bf16[4,256,1280]{2,1,0:T(8,128)(2,1)}, bf16[4,256,1280]{2,1,0:T(8,128)(2,1)S(1)}, u32[]{:S(2)}) copy-start(bf16[4,256,1280]{2,1,0:T(8,128)(2,1)S(1)} %bitcast_dynamic-update-slice_fusion) | copy-start | bytes 7864324
  115.0 33.0 %collective-permute-start.6 = (bf16[1024,1280]{1,0:T(8,128)(2,1)S(1)}, bf16[1024,1280]{1,0:T(8,128)(2,1)}, u32[]{:S(2)}, u32[]{:S(2)}) collective-permute-start(bf16[1024,1280]{1,0:T(8,128)(2,1)S(1)} %bitcast.303), channel_id=1, source_target_pairs={{0,2},{2,0},{1,3},{3,1},{4,6},{6,4},{5,7},{7,5},{8,10},{10,8},{9,1... | collective-permute-start | bytes 7864328 | tf_op jit(solution)/shard_map/ppermute | solution.py:79
  117.0 31.0 %all-to-all-start.2 = ((bf16[4,128,2048]{2,1,0:T(8,128)(2,1)}), bf16[4,128,2048]{2,1,0:T(8,128)(2,1)}, u32[]{:S(2)}, u32[]{:S(2)}) async-start(bf16[4,128,2048]{2,1,0:T(8,128)(2,1)} %bitcast_dynamic-update-slice_fusion.4), calls=%async_computation.2 | async-start | bytes 4194304 | tf_op jit(solution)/shard_map/all_to_all | solution.py:88
  148.0 36.6 %collective-permute-start.10 = (bf16[512,2048]{1,0:T(8,128)(2,1)}, bf16[512,2048]{1,0:T(8,128)(2,1)}, u32[]{:S(2)}, u32[]{:S(2)}) collective-permute-start(bf16[512,2048]{1,0:T(8,128)(2,1)} %bitcast.30), channel_id=1, source_target_pairs={{0,2},{2,0},{1,3},{3,1},{4,6},{6,4},{5,7},{7,5},{8,10},{10,8},{9,1... | collective-permute-start | bytes 6291464 | tf_op jit(solution)/shard_map/ppermute | solution.py:79
  160.0 10.1 %copy-start.15 = (bf16[2,256,8,64]{3,1,2,0:T(8,128)(2,1)}, bf16[2,256,8,64]{3,1,2,0:T(8,128)(2,1)S(1)}, u32[]{:S(2)}) copy-start(bf16[2,256,8,64]{3,1,2,0:T(8,128)(2,1)S(1)} %copy.221) | copy-start | bytes 1572868
  192.1 30.5 %all-to-all-start.3 = ((bf16[4,128,2048]{2,1,0:T(8,128)(2,1)}), bf16[4,128,2048]{2,1,0:T(8,128)(2,1)}, u32[]{:S(2)}, u32[]{:S(2)}) async-start(bf16[4,128,2048]{2,1,0:T(8,128)(2,1)} %bitcast.300), calls=%async_computation.3 | async-start | bytes 4194304 | tf_op jit(solution)/shard_map/all_to_all | solution.py:88
  196.9 25.6 %copy-start.47 = (pred[2,256,256]{1,2,0:T(8,128)(4,1)}, pred[2,256,256]{1,2,0:T(8,128)(4,1)S(1)}, u32[]{:S(2)}) copy-start(pred[2,256,256]{1,2,0:T(8,128)(4,1)S(1)} %iota_compare_fusion.2) | copy-start | bytes 393220
  231.0 97.4 %all-to-all-start.4 = ((bf16[32,32,2048]{2,1,0:T(8,128)(2,1)}), bf16[32,32,2048]{2,1,0:T(8,128)(2,1)}, u32[]{:S(2)}, u32[]{:S(2)}) async-start(bf16[32,32,2048]{2,1,0:T(8,128)(2,1)} %bitcast.298), calls=%async_computation.4 | async-start | bytes 8388608 | tf_op jit(solution)/shard_map/all_to_all | solution.py:88
  328.3 98.7 %all-to-all-start.7 = ((bf16[32,32,2048]{2,1,0:T(8,128)(2,1)}), bf16[32,32,2048]{2,1,0:T(8,128)(2,1)}, u32[]{:S(2)}, u32[]{:S(2)}) async-start(bf16[32,32,2048]{2,1,0:T(8,128)(2,1)} %bitcast.297), calls=%async_computation.7 | async-start | bytes 8388608 | tf_op jit(solution)/shard_map/all_to_all | solution.py:88
  436.9 12.0 %all-to-all-start.9 = ((f32[32,1,32]{2,1,0:T(1,128)}), f32[32,1,32]{2,1,0:T(1,128)S(1)}, u32[]{:S(2)}, u32[]{:S(2)}) async-start(f32[32,1,32]{2,1,0:T(1,128)} %reshape.603), calls=%async_computation.9 | async-start | bytes 32768 | tf_op jit(solution)/shard_map/all_to_all | solution.py:88
  441.7 21.0 %copy-start.42 = (f32[32,128]{1,0:T(8,128)}, f32[32,128]{1,0:T(8,128)S(1)}, u32[]{:S(2)}) copy-start(f32[32,128]{1,0:T(8,128)S(1)} %fusion.119) | copy-start | bytes 49156
  459.5 12.0 %slice-start.4 = ((s8[9437184]{0:T(1024)(128)(4,1)}), s8[4194304]{0:T(1024)(128)(4,1)S(1)}, s32[]{:S(2)}) async-start(s8[9437184]{0:T(1024)(128)(4,1)} %bitcast.349), calls=%async_computation.20 | async-start | bytes 8388608
  463.6 8.0 slice-start.5
  463.6 8.0 slice-start.6
  471.6 8.3 copy-start.90
  471.6 8.3 copy-start.92
  479.9 97.8 %all-to-all-start.8 = ((bf16[32,32,2048]{2,1,0:T(8,128)(2,1)}), bf16[32,32,2048]{2,1,0:T(8,128)(2,1)}, u32[]{:S(2)}, u32[]{:S(2)}) async-start(bf16[32,32,2048]{2,1,0:T(8,128)(2,1)} %bitcast.311), calls=%async_computation.8 | async-start | bytes 8388608 | tf_op jit(solution)/shard_map/all_to_all | solution.py:88
  483.9 96.8 %copy-start.52 = (bf16[128,32]{0,1:T(8,128)(2,1)}, bf16[128,32]{0,1:T(8,128)(2,1)S(1)}, u32[]{:S(2)}) copy-start(bf16[128,32]{0,1:T(8,128)(2,1)S(1)} %fusion.115) | copy-start | bytes 24580
  483.9 96.8 %copy-start.45 = (f32[2048]{0:T(1024)S(1)}, f32[2048]{0:T(1024)}, u32[]{:S(2)}) copy-start(f32[2048]{0:T(1024)} %get-tuple-element.116) | copy-start | bytes 24580
  483.9 96.8 %copy-start.75 = (f32[128]{0:T(128)S(1)}, f32[128]{0:T(128)}, u32[]{:S(2)}) copy-start(f32[128]{0:T(128)} %copy-done.74) | copy-start | bytes 1540
  582.2 13.5 %collective-permute-start.13 = (bf16[128,2048]{1,0:T(8,128)(2,1)S(1)}, bf16[128,2048]{1,0:T(8,128)(2,1)S(1)}, u32[]{:S(2)}, u32[]{:S(2)}) collective-permute-start(bf16[128,2048]{1,0:T(8,128)(2,1)S(1)} %fusion.45), channel_id=1, source_target_pairs={{0,1},{1,0},{2,3},{3,2},{4,5},{5,4},{6,7},{7,6},{8,9},{9,8},{10,11... | collective-permute-start | bytes 1572872 | tf_op jit(solution)/shard_map/ppermute | solution.py:79
  596.0 23.9 %collective-permute-start.14 = (bf16[256,2048]{1,0:T(8,128)(2,1)S(1)}, bf16[256,2048]{1,0:T(8,128)(2,1)S(1)}, u32[]{:S(2)}, u32[]{:S(2)}) collective-permute-start(bf16[256,2048]{1,0:T(8,128)(2,1)S(1)} %pad_maximum_fusion.9), channel_id=1, source_target_pairs={{0,4},{4,0},{1,5},{5,1},{2,6},{6,2},{3,7},{7,3},{8,12},{12,8},{9,1... | collective-permute-start | bytes 3145736 | tf_op jit(solution)/shard_map/ppermute | solution.py:79
  699.4 98.7 %all-to-all-start.5 = ((bf16[32,32,2048]{2,1,0:T(8,128)(2,1)}), bf16[32,32,2048]{2,1,0:T(8,128)(2,1)}, u32[]{:S(2)}, u32[]{:S(2)}) async-start(bf16[32,32,2048]{2,1,0:T(8,128)(2,1)} %bitcast.310), calls=%async_computation.5 | async-start | bytes 8388608 | tf_op jit(solution)/shard_map/all_to_all | solution.py:88
  710.0 92.9 %collective-permute-start.16 = (bf16[512,2048]{1,0:T(8,128)(2,1)}, bf16[512,2048]{1,0:T(8,128)(2,1)}, u32[]{:S(2)}, u32[]{:S(2)}) collective-permute-start(bf16[512,2048]{1,0:T(8,128)(2,1)} %convolution_convert_fusion.4), channel_id=1, source_target_pairs={{0,2},{2,0},{1,3},{3,1},{4,6},{6,4},{5,7},{7,5},{8,10},{10,8},{9,1... | collective-permute-start | bytes 6291464 | tf_op jit(solution)/shard_map/ppermute | solution.py:79
  710.4 13.7 %copy-start.81 = (f32[128]{0:T(128)}, f32[128]{0:T(128)S(1)}, u32[]{:S(2)}) copy-start(f32[128]{0:T(128)S(1)} %fusion.137) | copy-start | bytes 1540
  718.1 101.9 %collective-permute-start.15 = (bf16[1024,1280]{1,0:T(8,128)(2,1)}, bf16[1024,1280]{1,0:T(8,128)(2,1)}, u32[]{:S(2)}, u32[]{:S(2)}) collective-permute-start(bf16[1024,1280]{1,0:T(8,128)(2,1)} %convolution_convert_fusion), channel_id=1, source_target_pairs={{0,2},{2,0},{1,3},{3,1},{4,6},{6,4},{5,7},{7,5},{8,10},{10,8},{9,1... | collective-permute-start | bytes 7864328 | tf_op jit(solution)/shard_map/ppermute | solution.py:79
  724.0 78.8 %copy-start.19 = (f32[128,2048]{1,0:T(8,128)}, f32[128,2048]{1,0:T(8,128)S(1)}, u32[]{:S(2)}) copy-start(f32[128,2048]{1,0:T(8,128)S(1)} %reshape.610) | copy-start | bytes 3145732
  724.0 78.8 %copy-start.22 = (bf16[512,2,1,256]{0,3,1,2:T(8,128)(2,1)S(1)}, bf16[512,2,1,256]{0,3,1,2:T(8,128)(2,1)}, u32[]{:S(2)}) copy-start(bf16[512,2,1,256]{0,3,1,2:T(8,128)(2,1)} %copy-done.21) | copy-start | bytes 1572868
  798.1 17.5 %all-to-all-start.15 = ((f32[32,24,128]{2,1,0:T(8,128)}), f32[32,24,128]{2,1,0:T(8,128)S(1)}, u32[]{:S(2)}, u32[]{:S(2)}) async-start(f32[32,24,128]{2,1,0:T(8,128)} %bitcast.114), calls=%async_computation.15 | async-start | bytes 786432 | tf_op jit(solution)/shard_map/all_to_all | solution.py:88
  807.8 12.3 %copy-start.14 = (bf16[512,8,1,128]{0,3,1,2:T(8,128)(2,1)S(1)}, bf16[512,8,1,128]{0,3,1,2:T(8,128)(2,1)}, u32[]{:S(2)}) copy-start(bf16[512,8,1,128]{0,3,1,2:T(8,128)(2,1)} %get-tuple-element.87) | copy-start | bytes 3145732
  807.8 12.3 %copy-start.89 = (bf16[2,256,128]{2,1,0:T(8,128)(2,1)S(1)}, bf16[2,256,128]{2,1,0:T(8,128)(2,1)}, u32[]{:S(2)}) copy-start(bf16[2,256,128]{2,1,0:T(8,128)(2,1)} %fusion.42) | copy-start | bytes 393220
  815.6 9.6 copy-start.30
  815.6 30.5 %all-to-all-start.13 = ((bf16[4,128,2048]{2,1,0:T(8,128)(2,1)}), bf16[4,128,2048]{2,1,0:T(8,128)(2,1)}, u32[]{:S(2)}, u32[]{:S(2)}) async-start(bf16[4,128,2048]{2,1,0:T(8,128)(2,1)} %bitcast.321), calls=%async_computation.13 | async-start | bytes 4194304 | tf_op jit(solution)/shard_map/all_to_all | solution.py:88
  846.1 64.7 %all-to-all-start.11 = ((bf16[4,256,1280]{2,1,0:T(8,128)(2,1)}), bf16[4,256,1280]{2,1,0:T(8,128)(2,1)}, u32[]{:S(2)}, u32[]{:S(2)}) async-start(bf16[4,256,1280]{2,1,0:T(8,128)(2,1)} %bitcast.319), calls=%async_computation.11 | async-start | bytes 5242880 | tf_op jit(solution)/shard_map/all_to_all | solution.py:88
  910.9 51.3 %all-to-all-start.14 = ((bf16[4,128,2048]{2,1,0:T(8,128)(2,1)}), bf16[4,128,2048]{2,1,0:T(8,128)(2,1)S(1)}, u32[]{:S(2)}, u32[]{:S(2)}) async-start(bf16[4,128,2048]{2,1,0:T(8,128)(2,1)} %all-to-all-done.13), calls=%async_computation.14 | async-start | bytes 4194304 | tf_op jit(solution)/shard_map/all_to_all | solution.py:88
  914.5 14.3 %slice-start = ((s8[12582912]{0:T(1024)(128)(4,1)}), s8[4194304]{0:T(1024)(128)(4,1)S(1)}, s32[]{:S(2)}) async-start(s8[12582912]{0:T(1024)(128)(4,1)} %bitcast.301), calls=%async_computation.16 | async-start | bytes 8388608
  914.5 14.3 %slice-start.1 = ((s8[12582912]{0:T(1024)(128)(4,1)}), s8[4194304]{0:T(1024)(128)(4,1)S(1)}, s32[]{:S(2)}) async-start(s8[12582912]{0:T(1024)(128)(4,1)} %bitcast.301), calls=%async_computation.17 | async-start | bytes 8388608
  920.5 8.3 slice-start.2
  927.3 27.0 %collective-permute-start.11 = (bf16[128,2048]{1,0:T(8,128)(2,1)}, bf16[128,2048]{1,0:T(8,128)(2,1)S(1)}, u32[]{:S(2)}, u32[]{:S(2)}) collective-permute-start(bf16[128,2048]{1,0:T(8,128)(2,1)} %fusion.22), channel_id=1, source_target_pairs={{0,1},{1,0},{2,3},{3,2},{4,5},{5,4},{6,7},{7,6},{8,9},{9,8},{10,11... | collective-permute-start | bytes 1572872 | tf_op jit(solution)/shard_map/ppermute | solution.py:79
  935.7 19.8 %copy-start.48 = (pred[2,256,256]{1,2,0:T(8,128)(4,1)S(1)}, pred[2,256,256]{1,2,0:T(8,128)(4,1)}, u32[]{:S(2)}) copy-start(pred[2,256,256]{1,2,0:T(8,128)(4,1)} %copy-done.47) | copy-start | bytes 393220
  956.6 9.0 copy-start.10
  956.6 9.0 copy-start.65
  956.6 9.1 copy-start.82
  962.2 12.4 %all-to-all-start.12 = ((bf16[4,64,1280]{2,1,0:T(8,128)(2,1)}), bf16[4,64,1280]{2,1,0:T(8,128)(2,1)S(1)}, u32[]{:S(2)}, u32[]{:S(2)}) async-start(bf16[4,64,1280]{2,1,0:T(8,128)(2,1)} %bitcast.82), calls=%async_computation.12 | async-start | bytes 1310720 | tf_op jit(solution)/shard_map/all_to_all | solution.py:88
  (67 other events, 215.3 us)

commit v2 on v1

--- a/solution.py
+++ b/solution.py
@@ -1,6 +1,8 @@
 import jax
 import jax.numpy as jnp
 from jax import lax
+from jax.experimental import pallas as pl
+from jax.experimental.pallas import tpu as pltpu
 from jax.sharding import Mesh
 from jax.sharding import PartitionSpec as P
 
@@ -88,6 +90,51 @@
     return lax.all_to_all(value, axes, split_axis=0, concat_axis=0, tiled=True)
 
 
+def quad_index():
+    return lax.axis_index(NEAR_AXIS) * 2 + lax.axis_index(SEQ_AXIS)
+
+
+def quad_send(parts, step):
+    block = lax.dynamic_index_in_dim(parts, lax.bitwise_xor(quad_index(), step), 0, keepdims=False)
+    return lax.ppermute(block, HEAD_AXES, [(i, i ^ step) for i in range(4)])
+
+
+def quad_order(found):
+    low = pair_order(found[0], found[1], SEQ_AXIS)
+    high = pair_order(found[2], found[3], SEQ_AXIS)
+    rows = [pair_order(low[k], high[k], NEAR_AXIS) for k in range(2)]
+    return jnp.stack([rows[0][0], rows[1][0], rows[0][1], rows[1][1]])
+
+
+def quad_gather(value):
+    found = [value] + [
+        lax.ppermute(value, HEAD_AXES, [(i, i ^ step) for i in range(4)]) for step in range(1, 4)
+    ]
+    return quad_order(found)
+
+
+def quad_swap(parts):
+    own = lax.dynamic_index_in_dim(parts, quad_index(), 0, keepdims=False)
+    return quad_order([own] + [quad_send(parts, step) for step in range(1, 4)])
+
+
+def quad_sum(parts):
+    total = lax.dynamic_index_in_dim(parts, quad_index(), 0, keepdims=False).astype(F32)
+    for step in range(1, 4):
+        total = total + quad_send(parts, step).astype(F32)
+    return total
+
+
+def far_sum(parts, count):
+    here = lax.axis_index(FAR_AXIS)
+    total = lax.dynamic_index_in_dim(parts, here, 0, keepdims=False).astype(F32)
+    for step in range(1, count):
+        block = lax.dynamic_index_in_dim(parts, lax.rem(here + step, count), 0, keepdims=False)
+        block = lax.ppermute(block, FAR_AXIS, [(i, (i + step) % count) for i in range(count)])
+        total = total + block.astype(F32)
+    return total
+
+
 def ring_gather(chunk, axis, count):
     here = lax.axis_index(axis)
     zeros = (0,) * chunk.ndim
@@ -97,6 +144,40 @@
         chunk = lax.ppermute(chunk, axis, [(i, (i + 1) % count) for i in range(count)])
         full = lax.dynamic_update_slice(full, chunk[None], (lax.rem(here + count - step, count),) + zeros)
     return full
+
+
+def expert_grad_kernel(in_ref, gu_ref, grad_ref, active_ref, out_ref):
+    column = pl.program_id(1)
+
+    @pl.when(column < 2)
+    def _():
+        out_ref[...] = mm_tn(in_ref[...], gu_ref[...])
+
+    @pl.when(column == 2)
+    def _():
+        out_ref[...] = mm_tn(grad_ref[...], active_ref[...])
+
+
+def expert_grads(in_flat, gu_grad, grad_flat, active):
+    rows = in_flat.shape[0]
+    tile = 512
+    return pl.pallas_call(
+        expert_grad_kernel,
+        grid=(D // tile, 3),
+        in_specs=[
+            pl.BlockSpec((rows, tile), lambda i, j: (0, i)),
+            pl.BlockSpec((rows, FF), lambda i, j: (0, jnp.minimum(j, 1))),
+            pl.BlockSpec((rows, tile), lambda i, j: (0, i)),
+            pl.BlockSpec((rows, FF), lambda i, j: (0, 0)),
+        ],
+        out_specs=pl.BlockSpec((tile, FF), lambda i, j: (i, j)),
+        out_shape=jax.ShapeDtypeStruct((D, 3 * FF), F32),
+        compiler_params=pltpu.CompilerParams(vmem_limit_bytes=48 << 20),
+        cost_estimate=pl.CostEstimate(
+            flops=2 * rows * D * 3 * FF, bytes_accessed=rows * D * 4 + D * 3 * FF * 4, transcendentals=0
+        ),
+        name="expert_grads",
+    )(in_flat, gu_grad, grad_flat, active)
 
 
 def shards(tokens, cotangent, w_qkv, w_out, w_router, norm_gains, w_expert, lengths, deal, routes):
@@ -116,23 +197,7 @@
     gain_rows = norm_gains.shape[0]
     score_scale = HEAD_DIM ** (-0.5)
 
-    router_size = qkv_rows * experts_all
-    small_size = router_size + gain_rows
-    small_rows = -(-small_size // (8 * LANES)) * 8
-    small = jnp.concatenate([w_router.reshape(router_size), norm_gains])
-    small = jnp.pad(small, (0, small_rows * LANES - small_size)).reshape(1, small_rows, LANES)
-    small_all = exchange(
-        jnp.broadcast_to(small, (device_count, small_rows, LANES)), ALL_AXES
-    ).reshape(device_count, small_rows * LANES)
-    router_full = small_all[:, :router_size].reshape(D, experts_all)
-    gains_float = small_all[:, router_size:small_size].reshape(-1).astype(F32)
-    gain_attn = gains_float[:D]
-    gain_ffn = gains_float[D : 2 * D]
-    gain_query = gains_float[2 * D : 2 * D + HEAD_DIM]
-    gain_key = gains_float[2 * D + HEAD_DIM :]
-
-    tokens_pair = jnp.concatenate(pair_order(tokens, swap(tokens, SEQ_AXIS), SEQ_AXIS), axis=0)
-    tokens_both = jnp.stack(pair_order(tokens_pair, swap(tokens_pair, NEAR_AXIS), NEAR_AXIS))
+    tokens_both = quad_gather(tokens).reshape(2, ROW, D)
     table = jnp.concatenate([deal, jnp.pad(lengths, ((0, 0), (0, LANES - NSEG)))], axis=1)
     table_both = jnp.concatenate(pair_order(table, swap(table, NEAR_AXIS), NEAR_AXIS), axis=0)
     deal_both = table_both[:, :ROW]
@@ -162,6 +227,28 @@
     slot_hot = place.T[:, None, :] == jnp.arange(capacity, dtype=jnp.int32)[None, :, None]
     slot_low = slot_hot.astype(BF).reshape(slot_count, TOK_DEV)
 
+    router_size = qkv_rows * experts_all
+    small_size = router_size + gain_rows
+    mask_size = capacity * experts_all
+    small_rows = -(-(small_size + mask_size) // (8 * LANES)) * 8
+    small = jnp.broadcast_to(
+        jnp.concatenate([w_router.reshape(router_size), norm_gains]), (device_count, small_size)
+    )
+    slot_mask = mm(slot_low, chosen.astype(BF)).astype(BF).reshape(device_count, mask_size)
+    small = jnp.concatenate([slot_mask, small], axis=1)
+    small = jnp.pad(small, ((0, 0), (0, small_rows * LANES - small_size - mask_size)))
+    small_all = exchange(small.reshape(device_count, small_rows, LANES), ALL_AXES).reshape(
+        device_count, small_rows * LANES
+    )
+    mask_back = small_all[:, :mask_size].reshape(slot_count, experts_all)
+    small_all = small_all[:, mask_size : mask_size + small_size]
+    router_full = small_all[:, :router_size].reshape(D, experts_all)
+    gains_float = small_all[:, router_size:].reshape(-1).astype(F32)
+    gain_attn = gains_float[:D]
+    gain_ffn = gains_float[D : 2 * D]
+    gain_query = gains_float[2 * D : 2 * D + HEAD_DIM]
+    gain_key = gains_float[2 * D + HEAD_DIM :]
+
     cot_pair = jnp.concatenate(pair_order(cotangent, swap(cotangent, SEQ_AXIS), SEQ_AXIS), axis=0)
     cot_low = mm(hot_half, cot_pair).astype(BF)
     cot_rows = cot_low.astype(F32)
@@ -177,41 +264,22 @@
         axis=2,
     ).transpose(1, 0, 2)
     core_rows = KV_HEADS * qkv_rows
-    qkv_own = ring_gather(exchange(wide, HEAD_AXES).reshape(core_rows, width), FAR_AXIS, far_count)
-    qkv_own = qkv_own.reshape(far_count * core_rows, width)
-    qkv_other = swap(qkv_own, CORE_AXIS)
-
-    def split_core(values):
-        parts = values.reshape(values.shape[0], far_count * NEAR, CORES, 2 * qkv_rows)
-        own = jnp.where(core_index == 0, parts[:, :, 0], parts[:, :, 1])
-        other = jnp.where(core_index == 0, parts[:, :, 1], parts[:, :, 0])
-        return (own.reshape(values.shape[0], D // 2), other.reshape(values.shape[0], D // 2))
-
-    def join_core(own, other):
-        shape = (own.shape[0], far_count * NEAR, 2 * qkv_rows)
-        return jnp.stack(
-            pair_order(own.reshape(shape), other.reshape(shape), CORE_AXIS), axis=2
-        ).reshape(own.shape[0], D)
+    half_rows = 2 * qkv_rows
+    qkv_own = ring_gather(quad_swap(wide).reshape(core_rows, width), FAR_AXIS, far_count)
+    qkv_own = qkv_own.reshape(far_count * NEAR, half_rows, width)
+    qkv_mine = jnp.stack(pair_order(qkv_own, swap(qkv_own, CORE_AXIS), CORE_AXIS), axis=1).reshape(
+        D, width
+    )
 
     out_slabs = ring_gather(w_out, FAR_AXIS, far_count).reshape(
         KV_HEADS, far_count // KV_HEADS * out_rows, D
     )
-    out_mates = exchange(out_slabs, HEAD_AXES).reshape(NEAR, 2, far_count // KV_HEADS, out_rows, D)
-    out_own = out_mates.transpose(2, 0, 1, 3, 4).reshape(qcols // 2, D)
-    out_other = swap(out_own, CORE_AXIS)
     far_part = far_count // KV_HEADS
-
-    def split_heads(values):
-        parts = values.reshape(values.shape[0], far_part * NEAR, CORES, 2 * out_rows)
-        own = jnp.where(core_index == 0, parts[:, :, 0], parts[:, :, 1])
-        other = jnp.where(core_index == 0, parts[:, :, 1], parts[:, :, 0])
-        return (own.reshape(values.shape[0], qcols // 2), other.reshape(values.shape[0], qcols // 2))
-
-    def join_heads(own, other):
-        shape = (own.shape[0], far_part * NEAR, 2 * out_rows)
-        return jnp.stack(
-            pair_order(own.reshape(shape), other.reshape(shape), CORE_AXIS), axis=2
-        ).reshape(own.shape[0], qcols)
+    out_own = quad_swap(out_slabs).reshape(NEAR * 2, far_part, out_rows, D)
+    out_own = out_own.transpose(1, 0, 2, 3).reshape(far_part * NEAR, 2 * out_rows, D)
+    out_mine = jnp.stack(pair_order(out_own, swap(out_own, CORE_AXIS), CORE_AXIS), axis=1).reshape(
+        qcols, D
+    )
 
     x_both = lax.dot_general(
         dealt_hot, tokens_both, (((2,), (1,)), ((0,), (0,))), preferred_element_type=F32
@@ -220,8 +288,7 @@
         x_both, (near_index, seq_index * TOK_DEV, 0), (1, TOK_DEV, D)
     )[0]
     normed_low = rms_norm(x_both.reshape(2 * ROW, D), gain_attn).astype(BF)
-    normed_own, normed_other = split_core(normed_low)
-    projected = mm(normed_own, qkv_own) + mm(normed_other, qkv_other)
+    projected = mm(normed_low, qkv_mine)
     cosine, sine_part = tables(pos_both.reshape(2 * ROW), HEAD_DIM)
 
     def head_piece(proj_qk, scale_query, scale_key):
@@ -249,10 +316,9 @@
     prob_low = prob_full.astype(BF)
     mixed_heads = jnp.einsum("bgqs,bsd->bqgd", prob_low, value_heads, preferred_element_type=F32)
     mixed_low = mixed_heads.astype(BF).reshape(2 * ROW, qcols)
-    mixed_own, mixed_other = split_heads(mixed_low)
-    out_partial = mm(mixed_own, out_own) + mm(mixed_other, out_other)
-    out_parts = exchange(out_partial.astype(BF).reshape(4, TOK_DEV, D), HEAD_AXES)
-    residual = x_rows + jnp.sum(out_parts.astype(F32), axis=0)
+    out_partial = mm(mixed_low, out_mine).astype(BF)
+    residual = x_rows + quad_sum(out_partial.reshape(4, TOK_DEV, D))
+    residual, cot_back = lax.optimization_barrier((residual, cot_back))
 
     normed_two, ffn_back = jax.vjp(rms_norm, residual, gain_ffn)
     ffn_in = normed_two.astype(BF)
@@ -262,10 +328,13 @@
     logits = jnp.where(chosen > 0.5, logits, -1e30)
     gate_probs = jax.nn.softmax(logits, axis=-1)
     gate_probs = jnp.where(chosen > 0.5, gate_probs, 0.0)
-    slot_gate = jnp.sum(jnp.where(slot_hot, gate_probs.T[:, None, :], 0.0), axis=2)
-    gate_back = exchange(slot_gate[:, None, :], ALL_AXES).reshape(slot_count, 1)
-
     expert_weight = w_expert[0]
+    expert_here = (
+        (lax.axis_index(FAR_AXIS) * NEAR + near_index) * CORES + core_index
+    ) * 2 + seq_index
+    slot_logits = jnp.where(mask_back > 0.5, mm(in_flat, router_full), -1e30)
+    slot_probs = jnp.where(mask_back > 0.5, jax.nn.softmax(slot_logits, axis=-1), 0.0)
+    gate_back = jnp.sum(jnp.where(expert_ids == expert_here, slot_probs, 0.0), axis=1, keepdims=True)
     gate_up = mm(in_flat, expert_weight[:, : 2 * FF])
     gate_pre = gate_up[:, :FF]
     up_pre = gate_up[:, FF:]
@@ -285,7 +354,7 @@
     in_grad = mm_nt(gu_grad, expert_weight[:, : 2 * FF]).astype(BF)
     pair_grads = exchange(in_grad.reshape(device_count, capacity, D), ALL_AXES).reshape(slot_count, D)
     returned = exchange(expert_out.reshape(device_count, capacity, D), ALL_AXES).reshape(slot_count, D)
-    grad_expert = jnp.concatenate([mm_tn(in_flat, gu_grad), mm_tn(grad_flat, active)], axis=1)[None]
+    grad_expert = expert_grads(in_flat, gu_grad, grad_flat, active)[None]
 
     gate_grad = jnp.sum(jnp.where(slot_hot, dot_back[:, :, None], 0.0), axis=1).T
     mean_term = jnp.sum(gate_probs * gate_grad, axis=1, keepdims=True)
@@ -294,10 +363,7 @@
     ffn_in_grad = mm_tn(slot_low, pair_grads) + mm_nt(logit_grad, router_full)
     resid_part, gain_ffn_grad = ffn_back(ffn_in_grad)
     resid_low = (cot_rows + resid_part).astype(BF)
-    resid_pair = jnp.concatenate(pair_order(resid_low, swap(resid_low, SEQ_AXIS), SEQ_AXIS), axis=0)
-    resid_both = jnp.concatenate(
-        pair_order(resid_pair, swap(resid_pair, NEAR_AXIS), NEAR_AXIS), axis=0
-    )
+    resid_both = quad_gather(resid_low).reshape(2 * ROW, D)
 
     gate_slots = jnp.where(slot_hot, gate_probs.T[:, None, :], 0.0).reshape(slot_count, TOK_DEV)
     gate_high = gate_slots.astype(BF)
@@ -308,19 +374,22 @@
     )
     layer_out = mm_tn(back_half, final_pair).astype(BF)
 
-    mixed_grad = join_heads(mm_nt(resid_both, out_own), mm_nt(resid_both, out_other)).astype(BF)
+    def core_sum(values):
+        own, other = pair_order(values[:, 0], values[:, 1], CORE_AXIS)
+        return own.astype(F32) + swap(other, CORE_AXIS).astype(F32)
+
+    mixed_grad = mm_nt(resid_both, out_mine).astype(BF)
     grad_heads = mixed_grad.reshape(2, ROW, per_group, HEAD_DIM)
-    out_grad = mm_tn(mixed_own, resid_both) + swap(
-        mm_tn(mixed_other, resid_both).astype(BF), CORE_AXIS
-    ).astype(F32)
+    out_grad = mm_tn(mixed_low, resid_both).astype(BF)
+    out_grad = core_sum(out_grad.reshape(far_part * NEAR, CORES, 2 * out_rows, D))
     out_grad = (
         out_grad.astype(BF)
         .reshape(far_part, NEAR * 2, out_rows, D)
         .transpose(1, 0, 2, 3)
         .reshape(NEAR * 2, far_part * out_rows, D)
     )
-    out_grad = exchange(out_grad, HEAD_AXES).reshape(far_count, out_rows, D)
-    out_share = jnp.sum(exchange(out_grad, FAR_AXIS).astype(F32), axis=0)
+    out_grad = quad_swap(out_grad).reshape(far_count, out_rows, D)
+    out_share = far_sum(out_grad, far_count)
 
     value_grad = jnp.einsum("bgqs,bqgd->bsd", prob_low, grad_heads, preferred_element_type=F32)
     prob_grad = jnp.einsum("bqgd,bsd->bgqs", grad_heads, value_heads, preferred_element_type=F32)
@@ -346,23 +415,18 @@
         (((1,), (1,)), ((0,), (0,))),
         preferred_element_type=F32,
     ).astype(BF).reshape(2 * ROW, width)
-    normed_partial = jnp.concatenate(
-        [mm_nt(back_grad, qkv_own), mm_nt(back_grad, qkv_other)], axis=1
-    ).astype(BF)
-    normed_parts = exchange(normed_partial.reshape(4, TOK_DEV, D), HEAD_AXES)
-    normed_grad = jnp.sum(normed_parts.astype(F32), axis=0)
-    normed_grad = join_core(normed_grad[:, : D // 2], normed_grad[:, D // 2 :])
+    normed_partial = mm_nt(back_grad, qkv_mine).astype(BF)
+    normed_grad = quad_sum(normed_partial.reshape(4, TOK_DEV, D))
     _, attn_back = jax.vjp(rms_norm, tokens.astype(F32), gain_attn)
     input_part, gain_attn_grad = attn_back(normed_grad)
     resid_group = lax.dynamic_slice_in_dim(resid_both, near_index * ROW, ROW, axis=0)
     grad_tokens = (mm_tn(back_half, resid_group) + input_part).astype(BF)
 
-    qkv_grad = mm_tn(normed_own, proj_grad) + swap(
-        mm_tn(normed_other, proj_grad).astype(BF), CORE_AXIS
-    ).astype(F32)
-    qkv_grad = exchange(qkv_grad.astype(BF).reshape(far_count, core_rows, width), FAR_AXIS)
-    qkv_grad = jnp.sum(qkv_grad.astype(F32), axis=0).astype(BF).reshape(KV_HEADS, qkv_rows, width)
-    qkv_grad = exchange(qkv_grad, HEAD_AXES).transpose(1, 0, 2).astype(F32)
+    qkv_grad = mm_tn(normed_low, proj_grad).astype(BF)
+    qkv_grad = core_sum(qkv_grad.reshape(far_count * NEAR, CORES, half_rows, width))
+    qkv_grad = far_sum(qkv_grad.astype(BF).reshape(far_count, core_rows, width), far_count)
+    qkv_grad = quad_swap(qkv_grad.astype(BF).reshape(KV_HEADS, qkv_rows, width))
+    qkv_grad = qkv_grad.transpose(1, 0, 2).astype(F32)
     qkv_share = jnp.concatenate(
         [
             qkv_grad[:, :, :qcols].reshape(qkv_rows, QDIM),
@@ -373,14 +437,15 @@
     )
 
     gains_grad = jnp.concatenate([gain_attn_grad, gain_ffn_grad, query_gain_grad, key_gain_grad])
+    share_rows = -(-small_size // (8 * LANES)) * 8
     small_grad = jnp.concatenate(
         [router_grad.reshape(device_count, router_size), gains_grad.reshape(device_count, gain_rows)],
         axis=1,
     )
-    small_grad = jnp.pad(small_grad, ((0, 0), (0, small_rows * LANES - small_size)))
+    small_grad = jnp.pad(small_grad, ((0, 0), (0, share_rows * LANES - small_size)))
     small_share = jnp.sum(
-        exchange(small_grad.reshape(device_count, small_rows, LANES), ALL_AXES), axis=0
-    ).reshape(small_rows * LANES)
+        exchange(small_grad.reshape(device_count, share_rows, LANES), ALL_AXES), axis=0
+    ).reshape(share_rows * LANES)
     router_share = small_share[:router_size].reshape(qkv_rows, experts_all)
     gains_share = small_share[router_size:small_size]
     return (layer_out, grad_tokens, qkv_share, out_share, router_share, gains_share, grad_expert)

time: 983 us -> 798 us (0.81)
  waiting for transfers between devices: 551 us -> 334 us
  blocking collectives: 35.6 us -> 99.6 us
  matrix products: 145 us -> 95.8 us
  local copies, waits for them, and re-layouts: 91.6 us -> 54.7 us
  starting transfers between devices: 78.3 us -> 111 us
  Pallas kernels: 0 us -> 18.8 us
    all_to_all x14 -> x6, waiting for transfers between devices: 460 us -> 170 us  [exchange(): return lax.all_to_all(value, axes, split_axis=0, concat_axis=0, tiled=True)]
    ppermute x0 -> x30, waiting for transfers between devices: none -> 130 us  [the longest x18 77.8 us: quad_send(): return lax.ppermute(block, HEAD_AXES, [(i, i ^ step) for i in range(4)])]
    ppermute x0 -> x30, starting transfers between devices: none -> 72.6 us  [the longest x18 33.2 us: quad_send(): return lax.ppermute(block, HEAD_AXES, [(i, i ^ step) for i in range(4)])]
    all_to_all x2 -> x1, blocking collectives: 35.6 us -> 99.6 us  [exchange(): return lax.all_to_all(value, axes, split_axis=0, concat_axis=0, tiled=True)]
    dot_general x31 -> x25, matrix products: 125 us -> 82.1 us  [dot(): lax.dot_general(left, right, (dims, ((), ())), preferred_element_type=F32)]
    all_to_all x14 -> x6, starting transfers between devices: 62 us -> 28.2 us  [exchange(): return lax.all_to_all(value, axes, split_axis=0, concat_axis=0, tiled=True)]
    ppermute x6, waiting for transfers between devices: 56.4 us -> 25.1 us  [ring_gather(): lax.ppermute(chunk, axis, [(i, (i + 1) % count) for i in range(count)])]
    ppermute x11 -> x7, waiting for transfers between devices: 34.7 us -> 8.98 us  [swap(): return lax.ppermute(value, axis, [(0, 1), (1, 0)])]
  transfers between devices with their start and end apart: 31 -> 49, of which waited for: 20 -> 20; matrix products, arithmetic and copies ran while one was open for 20% -> 17% of each run, Pallas kernels for 0% -> 2%
where the time goes in v2:
time: 798 us; the launch traced here: 789 us
  waiting for transfers between devices  334 us (42%)
  starting transfers between devices  111 us (14%)
  blocking collectives  99.6 us (12%)
  matrix products  95.8 us (12%)
  other arithmetic  71.7 us (9%)
  local copies, waits for them, and re-layouts  54.7 us (7%)
  Pallas kernels  18.8 us (2%)
    all_to_all x6, waiting for transfers between devices, exchange(): return lax.all_to_all(value, axes, split_axis=0, concat_axis=0, tiled=True)  170 us
    all_to_all x1, blocking collectives, exchange(): return lax.all_to_all(value, axes, split_axis=0, concat_axis=0, tiled=True)  99.6 us
    dot_general x25, matrix products, dot(): lax.dot_general(left, right, (dims, ((), ())), preferred_element_type=F32)  82.1 us
    ppermute x18, waiting for transfers between devices, quad_send(): return lax.ppermute(block, HEAD_AXES, [(i, i ^ step) for i in range(4)])  77.8 us
    ppermute x6, waiting for transfers between devices, far_sum(): lax.ppermute(block, FAR_AXIS, [(i, (i + step) % count) for i in range(cou...  52.5 us
    ppermute x18, starting transfers between devices, quad_send(): return lax.ppermute(block, HEAD_AXES, [(i, i ^ step) for i in range(4)])  33.2 us
    ppermute x6, starting transfers between devices, far_sum(): lax.ppermute(block, FAR_AXIS, [(i, (i + step) % count) for i in range(cou...  31.4 us
    all_to_all x6, starting transfers between devices, exchange(): return lax.all_to_all(value, axes, split_axis=0, concat_axis=0, tiled=True)  28.2 us
  transfers between devices with their start and end apart: 49, of which 20 were waited for; matrix products, arithmetic and copies ran while one was open for 17% of the time, Pallas kernels for 2%

profile of v2, /device:TPU:0, one launch (start us, length us, event | category | flops | bytes accessed | tf_op | source)
XLA Modules:
  0.0 788.8 jit_solution(8012472636238360055)
XLA Ops:
  1.3 3.0 collective-permute-start
  20.7 3.9 all-to-all-start
  39.9 3.8 collective-permute-done.21
  46.3 14.7 %collective-permute-done.12 = bf16[128,2048]{1,0:T(8,128)(2,1)S(1)} collective-permute-done((bf16[128,2048]{1,0:T(8,128)(2,1)}, bf16[128,2048]{1,0:T(8,128)(2,1)S(1)}, u32[]{:S(2)}, u32[]{:S(2)}) %collective-permute-start.12) | collective-permute-done | bytes 524320 | tf_op jit(solution)/shard_map/ppermute | solution.py:144
  63.5 10.4 %collective-permute-done.13 = bf16[128,2048]{1,0:T(8,128)(2,1)S(1)} collective-permute-done((bf16[128,2048]{1,0:T(8,128)(2,1)S(1)}, bf16[128,2048]{1,0:T(8,128)(2,1)S(1)}, u32[]{:S(2)}, u32[]{:S(2)}) %collective-permute-start.13) | collective-permute-done | bytes 524320 | tf_op jit(solution)/shard_map/ppermute | solution.py:144
  76.3 4.3 collective-permute-start.14
  80.6 8.6 %collective-permute-start.16 = (bf16[128,2048]{1,0:T(8,128)(2,1)S(1)}, bf16[128,2048]{1,0:T(8,128)(2,1)S(1)}, u32[]{:S(2)}, u32[]{:S(2)}) collective-permute-start(bf16[128,2048]{1,0:T(8,128)(2,1)S(1)} %get-tuple-element.113), channel_id=1, source_target_pairs={{0,5},{1,4},{4,1},{5,0},{2,7},{3,6},{6,3},{7,2},{8,13},{9,12},{12,... | collective-permute-start | bytes 1572872 | tf_op jit(solution)/shard_map/ppermute | solution.py:99
  89.2 2.1 collective-permute-start.15
  92.6 16.8 %collective-permute-done.16 = bf16[128,2048]{1,0:T(8,128)(2,1)S(1)} collective-permute-done((bf16[128,2048]{1,0:T(8,128)(2,1)S(1)}, bf16[128,2048]{1,0:T(8,128)(2,1)S(1)}, u32[]{:S(2)}, u32[]{:S(2)}) %collective-permute-start.16) | collective-permute-done | bytes 524320 | tf_op jit(solution)/shard_map/ppermute | solution.py:99
  109.4 4.9 collective-permute-done.15
  114.3 3.3 select_bitcast_fusion.15
  120.2 3.3 convolution_convert_fusion.4
  123.5 6.4 all-to-all-start.1
  134.6 2.5 select_bitcast_fusion.3
  137.1 2.4 pad_maximum_fusion.1
  139.6 2.1 select_bitcast_fusion.1
  142.1 2.9 fusion.156
  155.5 5.0 fusion.154
  160.5 2.7 fusion.34
  163.2 11.4 %copy.222 = bf16[2,256,8,128]{3,2,1,0:T(8,128)(2,1)S(1)} copy(bf16[2,256,8,128]{1,3,2,0:T(8,128)(2,1)S(1)} %fusion.34) | data formatting | bytes 2097152 | tf_op jit(solution)/shard_map/convert_element_type | solution.py:318
  174.6 4.9 convolution_convert_fusion.5
  179.7 2.3 collective-permute-start.18
  183.5 13.9 %collective-permute-done.18 = bf16[128,2048]{1,0:T(8,128)(2,1)S(1)} collective-permute-done((bf16[128,2048]{1,0:T(8,128)(2,1)S(1)}, bf16[128,2048]{1,0:T(8,128)(2,1)S(1)}, u32[]{:S(2)}, u32[]{:S(2)}) %collective-permute-start.18) | collective-permute-done | bytes 524320 | tf_op jit(solution)/shard_map/ppermute | solution.py:99
  197.4 17.0 %collective-permute-done.20 = bf16[128,2048]{1,0:T(8,128)(2,1)S(1)} collective-permute-done((bf16[128,2048]{1,0:T(8,128)(2,1)S(1)}, bf16[128,2048]{1,0:T(8,128)(2,1)S(1)}, u32[]{:S(2)}, u32[]{:S(2)}) %collective-permute-start.20) | collective-permute-done | bytes 524320 | tf_op jit(solution)/shard_map/ppermute | solution.py:99
  216.0 8.2 %all-to-all-done.1 = bf16[32,32,2048]{2,1,0:T(8,128)(2,1)} async-done(((bf16[32,32,2048]{2,1,0:T(8,128)(2,1)}), bf16[32,32,2048]{2,1,0:T(8,128)(2,1)}, u32[]{:S(2)}, u32[]{:S(2)}) %all-to-all-start.1) | async-done | bytes 4194336 | tf_op jit(solution)/shard_map/all_to_all | solution.py:90
  225.8 3.3 convolution_convert_fusion.3
  229.1 4.4 all-to-all-start.2
  234.4 92.8 %all-to-all-done.2 = bf16[32,32,2048]{2,1,0:T(8,128)(2,1)} async-done(((bf16[32,32,2048]{2,1,0:T(8,128)(2,1)}), bf16[32,32,2048]{2,1,0:T(8,128)(2,1)}, u32[]{:S(2)}, u32[]{:S(2)}) %all-to-all-start.2) | async-done | bytes 4194336 | tf_op jit(solution)/shard_map/all_to_all | solution.py:90
  327.2 10.0 %fusion.5 = f32[1024,1536]{1,0:T(8,128)S(1)} fusion(bf16[1024,2048]{1,0:T(8,128)(2,1)} %bitcast.65.in_ref, bf16[2048,2304]{1,0:T(8,128)(2,1)} %bitcast.542), kind=kOutput, calls=%fused_computation.8 | convolution fusion | flops 6442450944 | bytes 16777216 | tf_op jit(solution)/shard_map/dot_general | solution.py:65
  337.2 3.5 fusion.155
  340.9 2.9 fusion.1.grad_ref
  343.8 9.1 %multiply_convert_fusion.2 = (bf16[1024,768]{1,0:T(8,128)(2,1)}, bf16[1024,768]{1,0:T(8,128)(2,1)}, bf16[1024,768]{1,0:T(8,128)(2,1)S(1)}) fusion(f32[1024,1536]{1,0:T(8,128)S(1)} %fusion.5, bf16[1024,2048]{1,0:T(8,128)(2,1)S(1)} %fusion.1.grad_ref, bf16[2048,2304]{1,0:T(8,128)(2,1)} %bitcast.543), kind=kOutput, calls=%fused_computation.39 | convolution fusion | flops 3233021952 | bytes 18350080 | tf_op jit(solution)/shard_map/dot_general | solution.py:65
  352.9 7.6 fusion.2
  361.2 4.7 all-to-all-start.5
  366.0 11.1 %fusion.14 = bf16[1024,2048]{1,0:T(8,128)(2,1)} fusion(bf16[2048,2304]{1,0:T(8,128)(2,1)} %bitcast.545, bf16[1024,768]{1,0:T(8,128)(2,1)} %get-tuple-element.71, bf16[1024,768]{1,0:T(8,128)(2,1)} %get-tuple-element.70), kind=kOutput, calls=%fused_computation.30 | convolution fusion | flops 6450839552 | bytes 13631488 | tf_op jit(solution)/shard_map/dot_general | solution.py:65
  377.1 99.6 %all_to_all.35 = bf16[32,32,2048]{2,1,0:T(8,128)(2,1)} all-to-all(bf16[32,32,2048]{2,1,0:T(8,128)(2,1)} %bitcast.503), channel_id=1, replica_groups=mesh['far'=4,'near'=2,'core'=2,'seq'=2] {'far','near','core','seq'}, dimensions={0} | all-to-all | bytes 8388608 | tf_op jit(solution)/shard_map/all_to_all | solution.py:90
  476.7 4.2 all-to-all-start.3
  481.2 4.1 fusion.10
  486.0 18.8 %expert_grads.1 = f32[2048,2304]{1,0:T(8,128)} custom-call(bf16[1024,2048]{1,0:T(8,128)(2,1)} %bitcast.65.in_ref, bf16[1024,1536]{1,0:T(8,128)(2,1)S(1)} %pad_maximum_fusion.2.gu_ref, bf16[1024,2048]{1,0:T(8,128)(2,1)} %copy-done.25, bf16[1024,768]{1,0:T(8,128)(2,1)S(1)} %get-tuple-element.72.active_ref), custom_call_target="tpu_custom_call" | custom-call | flops 9663676416 | bytes 27262976 | tf_op jit(solution)/shard_map/expert_grads/pallas_call | solution.py:164
  508.1 2.8 collective-permute-start.25
  513.1 62.9 %all-to-all-done.3 = bf16[32,32,2048]{2,1,0:T(8,128)(2,1)} async-done(((bf16[32,32,2048]{2,1,0:T(8,128)(2,1)}), bf16[32,32,2048]{2,1,0:T(8,128)(2,1)}, u32[]{:S(2)}, u32[]{:S(2)}) %all-to-all-start.3) | async-done | bytes 4194336 | tf_op jit(solution)/shard_map/all_to_all | solution.py:90
  576.0 3.9 convolution_bitcast_fusion.1
  583.5 2.7 copy-done.22
  586.1 2.4 fusion.33
  596.2 4.5 convolution_convert_fusion.1
  602.5 2.3 fusion.94
  609.7 3.0 multiply_reduce_fusion.1
  614.6 4.3 add_add_fusion
  620.9 3.4 convolution_convert_fusion.6
  630.4 3.2 convolution_convert_fusion
  636.7 3.0 fusion.26
  640.7 9.5 %collective-permute-done.28 = bf16[128,2048]{1,0:T(8,128)(2,1)S(1)} collective-permute-done((bf16[128,2048]{1,0:T(8,128)(2,1)S(1)}, bf16[128,2048]{1,0:T(8,128)(2,1)S(1)}, u32[]{:S(2)}, u32[]{:S(2)}) %collective-permute-start.28) | collective-permute-done | bytes 524320 | tf_op jit(solution)/shard_map/ppermute | solution.py:99
  652.1 4.6 all-to-all-start.6
  656.7 5.1 collective-permute-done.22
  664.2 5.2 all-to-all-done.6
  670.8 4.3 fusion.8
  678.9 2.7 fusion.7
  682.1 3.5 collective-permute-start.32
  685.6 4.5 collective-permute-done.37
  691.9 9.6 %collective-permute-done.39 = bf16[128,2048]{1,0:T(8,128)(2,1)S(1)} collective-permute-done((bf16[128,2048]{1,0:T(8,128)(2,1)S(1)}, bf16[128,2048]{1,0:T(8,128)(2,1)S(1)}, u32[]{:S(2)}, u32[]{:S(2)}) %collective-permute-start.39) | collective-permute-done | bytes 524320 | tf_op jit(solution)/shard_map/ppermute | solution.py:99
  703.8 3.5 collective-permute-start.42
  707.3 21.9 %collective-permute-start.41 = (bf16[128,2048]{1,0:T(8,128)(2,1)S(1)}, bf16[128,2048]{1,0:T(8,128)(2,1)S(1)}, u32[]{:S(2)}, u32[]{:S(2)}) collective-permute-start(bf16[128,2048]{1,0:T(8,128)(2,1)S(1)} %get-tuple-element.94), channel_id=1, source_target_pairs={{0,16},{8,24},{16,0},{24,8},{1,17},{9,25},{17,1},{25,9},{2,18},{10... | collective-permute-start | bytes 1572872 | tf_op jit(solution)/shard_map/ppermute | solution.py:133
  729.2 35.6 %collective-permute-done.31 = bf16[256,1280]{1,0:T(8,128)(2,1)S(1)} collective-permute-done((bf16[256,1280]{1,0:T(8,128)(2,1)S(1)}, bf16[256,1280]{1,0:T(8,128)(2,1)S(1)}, u32[]{:S(2)}, u32[]{:S(2)}) %collective-permute-start.31) | collective-permute-done | bytes 655392 | tf_op jit(solution)/shard_map/ppermute | solution.py:133
  768.8 16.9 %collective-permute-done.41 = bf16[128,2048]{1,0:T(8,128)(2,1)S(1)} collective-permute-done((bf16[128,2048]{1,0:T(8,128)(2,1)S(1)}, bf16[128,2048]{1,0:T(8,128)(2,1)S(1)}, u32[]{:S(2)}, u32[]{:S(2)}) %collective-permute-start.41) | collective-permute-done | bytes 524320 | tf_op jit(solution)/shard_map/ppermute | solution.py:133
  (419 shorter events, 124.1 us)
Async XLA Ops:
  1.3 15.2 %collective-permute-start = (s32[1,384]{1,0:T(1,128)S(1)}, s32[1,384]{1,0:T(1,128)S(1)}, u32[]{:S(2)}, u32[]{:S(2)}) collective-permute-start(s32[1,384]{1,0:T(1,128)S(1)} %pad_add_fusion.2), channel_id=1, source_target_pairs={{0,4},{4,0},{1,5},{5,1},{2,6},{6,2},{3,7},{7,3},{8,12},{12,8},{9,1... | collective-permute-start | bytes 4616 | tf_op jit(solution)/shard_map/ppermute | solution.py:81
  4.3 33.1 %collective-permute-start.11 = (bf16[128,2048]{1,0:T(8,128)(2,1)}, bf16[128,2048]{1,0:T(8,128)(2,1)}, u32[]{:S(2)}, u32[]{:S(2)}) collective-permute-start(bf16[128,2048]{1,0:T(8,128)(2,1)} %param.13), channel_id=1, source_target_pairs={{0,8},{8,16},{16,24},{24,0},{1,9},{9,17},{17,25},{25,1},{2,10},{10... | collective-permute-start | bytes 1572872 | tf_op jit(solution)/shard_map/ppermute | solution.py:144
  5.9 74.7 %collective-permute-start.3 = (bf16[128,2048]{1,0:T(8,128)(2,1)}, bf16[128,2048]{1,0:T(8,128)(2,1)}, u32[]{:S(2)}, u32[]{:S(2)}) collective-permute-start(bf16[128,2048]{1,0:T(8,128)(2,1)} %param.10), channel_id=1, source_target_pairs={{0,5},{1,4},{4,1},{5,0},{2,7},{3,6},{6,3},{7,2},{8,13},{9,12},{12,... | collective-permute-start | bytes 1572872 | tf_op jit(solution)/shard_map/ppermute | solution.py:111
  11.5 15.8 %collective-permute-start.4 = (bf16[64,1280]{1,0:T(8,128)(2,1)S(1)}, bf16[64,1280]{1,0:T(8,128)(2,1)S(1)}, u32[]{:S(2)}, u32[]{:S(2)}) collective-permute-start(bf16[64,1280]{1,0:T(8,128)(2,1)S(1)} %bitcast.531), channel_id=1, source_target_pairs={{0,1},{1,0},{4,5},{5,4},{2,3},{3,2},{6,7},{7,6},{8,9},{9,8},{12,13... | collective-permute-start | bytes 491528 | tf_op jit(solution)/shard_map/ppermute | solution.py:99
  12.1 17.0 %collective-permute-start.5 = (bf16[64,1280]{1,0:T(8,128)(2,1)S(1)}, bf16[64,1280]{1,0:T(8,128)(2,1)S(1)}, u32[]{:S(2)}, u32[]{:S(2)}) collective-permute-start(bf16[64,1280]{1,0:T(8,128)(2,1)S(1)} %bitcast.530), channel_id=1, source_target_pairs={{0,4},{1,5},{4,0},{5,1},{2,6},{3,7},{6,2},{7,3},{8,12},{9,13},{12,... | collective-permute-start | bytes 491528 | tf_op jit(solution)/shard_map/ppermute | solution.py:99
  13.7 10.9 %copy-start.80 = (f32[64]{0:T(128)}, f32[64]{0:T(128)S(1)}, u32[]{:S(2)}) copy-start(f32[64]{0:T(128)S(1)} %negate_power_fusion) | copy-start | bytes 772
  16.5 10.8 %copy-start.9 = (bf16[128,2048]{1,0:T(8,128)(2,1)S(1)}, bf16[128,2048]{1,0:T(8,128)(2,1)}, u32[]{:S(2)}) copy-start(bf16[128,2048]{1,0:T(8,128)(2,1)} %param.10) | copy-start | bytes 1572868
  16.5 14.0 %collective-permute-start.6 = (bf16[64,1280]{1,0:T(8,128)(2,1)S(1)}, bf16[64,1280]{1,0:T(8,128)(2,1)S(1)}, u32[]{:S(2)}, u32[]{:S(2)}) collective-permute-start(bf16[64,1280]{1,0:T(8,128)(2,1)S(1)} %bitcast.532), channel_id=1, source_target_pairs={{0,5},{1,4},{4,1},{5,0},{2,7},{3,6},{6,3},{7,2},{8,13},{9,12},{12,... | collective-permute-start | bytes 491528 | tf_op jit(solution)/shard_map/ppermute | solution.py:99
  18.0 12.6 %copy-start.60 = (s32[2,256]{1,0:T(2,128)}, s32[2,256]{1,0:T(2,128)S(1)}, u32[]{:S(2)}) copy-start(s32[2,256]{1,0:T(2,128)S(1)} %fusion.136) | copy-start | bytes 6148
  18.4 12.1 %copy-start.49 = (pred[2,256,256]{1,2,0:T(8,128)(4,1)}, pred[2,256,256]{1,2,0:T(8,128)(4,1)S(1)}, u32[]{:S(2)}) copy-start(pred[2,256,256]{1,2,0:T(8,128)(4,1)S(1)} %iota_compare_fusion.2) | copy-start | bytes 393220
  18.5 12.0 %copy-start.63 = (f32[1,2,2,128]{3,1,2,0:T(2,128)}, f32[1,2,2,128]{3,1,2,0:T(2,128)S(1)}, u32[]{:S(2)}) copy-start(f32[1,2,2,128]{3,1,2,0:T(2,128)S(1)} %copy.278) | copy-start | bytes 6148
  18.8 11.7 %copy-start.53 = (f32[128,32]{0,1:T(8,128)}, f32[128,32]{0,1:T(8,128)S(1)}, u32[]{:S(2)}) copy-start(f32[128,32]{0,1:T(8,128)S(1)} %fusion.109) | copy-start | bytes 49156
  20.7 14.6 %all-to-all-start = ((bf16[32,32,128]{2,1,0:T(8,128)(2,1)}), bf16[32,32,128]{2,1,0:T(8,128)(2,1)S(1)}, u32[]{:S(2)}, u32[]{:S(2)}) async-start(bf16[32,32,128]{2,1,0:T(8,128)(2,1)} %bitcast.175), calls=%async_computation | async-start | bytes 524288 | tf_op jit(solution)/shard_map/all_to_all | solution.py:90
  27.3 65.2 %collective-permute-start.2 = (bf16[128,2048]{1,0:T(8,128)(2,1)S(1)}, bf16[128,2048]{1,0:T(8,128)(2,1)}, u32[]{:S(2)}, u32[]{:S(2)}) collective-permute-start(bf16[128,2048]{1,0:T(8,128)(2,1)S(1)} %copy-done.9), channel_id=1, source_target_pairs={{0,4},{1,5},{4,0},{5,1},{2,6},{3,7},{6,2},{7,3},{8,12},{9,13},{12,... | collective-permute-start | bytes 1572872 | tf_op jit(solution)/shard_map/ppermute | solution.py:111
  29.1 14.7 %collective-permute-start.21 = (bf16[128,2048]{1,0:T(8,128)(2,1)}, bf16[128,2048]{1,0:T(8,128)(2,1)}, u32[]{:S(2)}, u32[]{:S(2)}) collective-permute-start(bf16[128,2048]{1,0:T(8,128)(2,1)} %param.11), channel_id=1, source_target_pairs={{0,1},{1,0},{2,3},{3,2},{4,5},{5,4},{6,7},{7,6},{8,9},{9,8},{10,11... | collective-permute-start | bytes 1572872 | tf_op jit(solution)/shard_map/ppermute | solution.py:81
  31.6 30.8 %collective-permute-start.7 = (bf16[256,1280]{1,0:T(8,128)(2,1)}, bf16[256,1280]{1,0:T(8,128)(2,1)}, u32[]{:S(2)}, u32[]{:S(2)}) collective-permute-start(bf16[256,1280]{1,0:T(8,128)(2,1)} %bitcast.18), channel_id=1, source_target_pairs={{0,8},{8,16},{16,24},{24,0},{1,9},{9,17},{17,25},{25,1},{2,10},{10... | collective-permute-start | bytes 1966088 | tf_op jit(solution)/shard_map/ppermute | solution.py:144
  36.8 96.4 %copy-start.51 = (f32[2048]{0:T(1024)}, f32[2048]{0:T(1024)S(1)}, u32[]{:S(2)}) copy-start(f32[2048]{0:T(1024)S(1)} %get-tuple-element.143) | copy-start | bytes 24580
  37.4 23.6 %collective-permute-start.12 = (bf16[128,2048]{1,0:T(8,128)(2,1)}, bf16[128,2048]{1,0:T(8,128)(2,1)S(1)}, u32[]{:S(2)}, u32[]{:S(2)}) collective-permute-start(bf16[128,2048]{1,0:T(8,128)(2,1)} %collective-permute-done.11), channel_id=1, source_target_pairs={{0,8},{8,16},{16,24},{24,0},{1,9},{9,17},{17,25},{25,1},{2,10},{10... | collective-permute-start | bytes 1572872 | tf_op jit(solution)/shard_map/ppermute | solution.py:144
  43.8 48.8 %collective-permute-start.1 = (bf16[128,2048]{1,0:T(8,128)(2,1)S(1)}, bf16[128,2048]{1,0:T(8,128)(2,1)S(1)}, u32[]{:S(2)}, u32[]{:S(2)}) collective-permute-start(bf16[128,2048]{1,0:T(8,128)(2,1)S(1)} %copy-done.9), channel_id=1, source_target_pairs={{0,1},{1,0},{4,5},{5,4},{2,3},{3,2},{6,7},{7,6},{8,9},{9,8},{12,13... | collective-permute-start | bytes 1572872 | tf_op jit(solution)/shard_map/ppermute | solution.py:111
  61.1 12.8 %collective-permute-start.13 = (bf16[128,2048]{1,0:T(8,128)(2,1)S(1)}, bf16[128,2048]{1,0:T(8,128)(2,1)S(1)}, u32[]{:S(2)}, u32[]{:S(2)}) collective-permute-start(bf16[128,2048]{1,0:T(8,128)(2,1)S(1)} %collective-permute-done.12), channel_id=1, source_target_pairs={{0,8},{8,16},{16,24},{24,0},{1,9},{9,17},{17,25},{25,1},{2,10},{10... | collective-permute-start | bytes 1572872 | tf_op jit(solution)/shard_map/ppermute | solution.py:144
  62.3 57.9 %copy-start.32 = (bf16[128,2048]{1,0:T(8,128)(2,1)}, bf16[128,2048]{1,0:T(8,128)(2,1)S(1)}, u32[]{:S(2)}) copy-start(bf16[128,2048]{1,0:T(8,128)(2,1)S(1)} %convolution_convert_fusion.9) | copy-start | bytes 1572868
  62.3 26.9 %collective-permute-start.8 = (bf16[256,1280]{1,0:T(8,128)(2,1)}, bf16[256,1280]{1,0:T(8,128)(2,1)S(1)}, u32[]{:S(2)}, u32[]{:S(2)}) collective-permute-start(bf16[256,1280]{1,0:T(8,128)(2,1)} %collective-permute-done.7), channel_id=1, source_target_pairs={{0,8},{8,16},{16,24},{24,0},{1,9},{9,17},{17,25},{25,1},{2,10},{10... | collective-permute-start | bytes 1966088 | tf_op jit(solution)/shard_map/ppermute | solution.py:144
  76.3 16.3 %collective-permute-start.14 = (bf16[128,2048]{1,0:T(8,128)(2,1)S(1)}, bf16[128,2048]{1,0:T(8,128)(2,1)S(1)}, u32[]{:S(2)}, u32[]{:S(2)}) collective-permute-start(bf16[128,2048]{1,0:T(8,128)(2,1)S(1)} %get-tuple-element.112), channel_id=1, source_target_pairs={{0,1},{1,0},{4,5},{5,4},{2,3},{3,2},{6,7},{7,6},{8,9},{9,8},{12,13... | collective-permute-start | bytes 1572872 | tf_op jit(solution)/shard_map/ppermute | solution.py:99
  80.6 28.8 %collective-permute-start.16 = (bf16[128,2048]{1,0:T(8,128)(2,1)S(1)}, bf16[128,2048]{1,0:T(8,128)(2,1)S(1)}, u32[]{:S(2)}, u32[]{:S(2)}) collective-permute-start(bf16[128,2048]{1,0:T(8,128)(2,1)S(1)} %get-tuple-element.113), channel_id=1, source_target_pairs={{0,5},{1,4},{4,1},{5,0},{2,7},{3,6},{6,3},{7,2},{8,13},{9,12},{12,... | collective-permute-start | bytes 1572872 | tf_op jit(solution)/shard_map/ppermute | solution.py:99
  89.2 25.1 %collective-permute-start.15 = (bf16[128,2048]{1,0:T(8,128)(2,1)S(1)}, bf16[128,2048]{1,0:T(8,128)(2,1)S(1)}, u32[]{:S(2)}, u32[]{:S(2)}) collective-permute-start(bf16[128,2048]{1,0:T(8,128)(2,1)S(1)} %get-tuple-element.114), channel_id=1, source_target_pairs={{0,4},{1,5},{4,0},{5,1},{2,6},{3,7},{6,2},{7,3},{8,12},{9,13},{12,... | collective-permute-start | bytes 1572872 | tf_op jit(solution)/shard_map/ppermute | solution.py:99
  92.5 27.5 %collective-permute-start.9 = (bf16[256,1280]{1,0:T(8,128)(2,1)S(1)}, bf16[256,1280]{1,0:T(8,128)(2,1)S(1)}, u32[]{:S(2)}, u32[]{:S(2)}) collective-permute-start(bf16[256,1280]{1,0:T(8,128)(2,1)S(1)} %collective-permute-done.8), channel_id=1, source_target_pairs={{0,8},{8,16},{16,24},{24,0},{1,9},{9,17},{17,25},{25,1},{2,10},{10... | collective-permute-start | bytes 1966088 | tf_op jit(solution)/shard_map/ppermute | solution.py:144
  119.2 15.4 %collective-permute-start.17 = (bf16[2,256,2048]{2,1,0:T(8,128)(2,1)}, bf16[2,256,2048]{2,1,0:T(8,128)(2,1)}, u32[]{:S(2)}, u32[]{:S(2)}) collective-permute-start(bf16[2,256,2048]{2,1,0:T(8,128)(2,1)} %bitcast.50), channel_id=1, source_target_pairs={{0,2},{2,0},{1,3},{3,1},{4,6},{6,4},{5,7},{7,5},{8,10},{10,8},{9,1... | collective-permute-start | bytes 6291464 | tf_op jit(solution)/shard_map/ppermute | solution.py:81
  120.1 19.4 %collective-permute-start.10 = (bf16[8,128,1280]{2,1,0:T(8,128)(2,1)S(1)}, bf16[8,128,1280]{2,1,0:T(8,128)(2,1)}, u32[]{:S(2)}, u32[]{:S(2)}) collective-permute-start(bf16[8,128,1280]{2,1,0:T(8,128)(2,1)S(1)} %bitcast.486), channel_id=1, source_target_pairs={{0,2},{2,0},{1,3},{3,1},{4,6},{6,4},{5,7},{7,5},{8,10},{10,8},{9,1... | collective-permute-start | bytes 7864328 | tf_op jit(solution)/shard_map/ppermute | solution.py:81
  123.5 100.8 %all-to-all-start.1 = ((bf16[32,32,2048]{2,1,0:T(8,128)(2,1)}), bf16[32,32,2048]{2,1,0:T(8,128)(2,1)}, u32[]{:S(2)}, u32[]{:S(2)}) async-start(bf16[32,32,2048]{2,1,0:T(8,128)(2,1)} %bitcast.475), calls=%async_computation.1 | async-start | bytes 8388608 | tf_op jit(solution)/shard_map/all_to_all | solution.py:90
  151.0 9.5 %copy-start.18 = (bf16[2,256,8,64]{3,1,2,0:T(8,128)(2,1)}, bf16[2,256,8,64]{3,1,2,0:T(8,128)(2,1)S(1)}, u32[]{:S(2)}) copy-start(bf16[2,256,8,64]{3,1,2,0:T(8,128)(2,1)S(1)} %copy.218) | copy-start | bytes 1572868
  179.7 17.7 %collective-permute-start.18 = (bf16[128,2048]{1,0:T(8,128)(2,1)S(1)}, bf16[128,2048]{1,0:T(8,128)(2,1)S(1)}, u32[]{:S(2)}, u32[]{:S(2)}) collective-permute-start(bf16[128,2048]{1,0:T(8,128)(2,1)S(1)} %get-tuple-element.105), channel_id=1, source_target_pairs={{0,1},{1,0},{4,5},{5,4},{2,3},{3,2},{6,7},{7,6},{8,9},{9,8},{12,13... | collective-permute-start | bytes 1572872 | tf_op jit(solution)/shard_map/ppermute | solution.py:99
  182.0 32.4 %collective-permute-start.20 = (bf16[128,2048]{1,0:T(8,128)(2,1)S(1)}, bf16[128,2048]{1,0:T(8,128)(2,1)S(1)}, u32[]{:S(2)}, u32[]{:S(2)}) collective-permute-start(bf16[128,2048]{1,0:T(8,128)(2,1)S(1)} %get-tuple-element.106), channel_id=1, source_target_pairs={{0,5},{1,4},{4,1},{5,0},{2,7},{3,6},{6,3},{7,2},{8,13},{9,12},{12,... | collective-permute-start | bytes 1572872 | tf_op jit(solution)/shard_map/ppermute | solution.py:99
  183.1 31.3 %collective-permute-start.19 = (bf16[128,2048]{1,0:T(8,128)(2,1)S(1)}, bf16[128,2048]{1,0:T(8,128)(2,1)S(1)}, u32[]{:S(2)}, u32[]{:S(2)}) collective-permute-start(bf16[128,2048]{1,0:T(8,128)(2,1)S(1)} %get-tuple-element.107), channel_id=1, source_target_pairs={{0,4},{1,5},{4,0},{5,1},{2,6},{3,7},{6,2},{7,3},{8,12},{9,13},{12,... | collective-permute-start | bytes 1572872 | tf_op jit(solution)/shard_map/ppermute | solution.py:99
  229.1 98.1 %all-to-all-start.2 = ((bf16[32,32,2048]{2,1,0:T(8,128)(2,1)}), bf16[32,32,2048]{2,1,0:T(8,128)(2,1)}, u32[]{:S(2)}, u32[]{:S(2)}) async-start(bf16[32,32,2048]{2,1,0:T(8,128)(2,1)} %bitcast.476), calls=%async_computation.2 | async-start | bytes 8388608 | tf_op jit(solution)/shard_map/all_to_all | solution.py:90
  234.4 102.8 %copy-start.11 = (bf16[2048,32]{1,0:T(8,128)(2,1)}, bf16[2048,32]{1,0:T(8,128)(2,1)S(1)}, u32[]{:S(2)}) copy-start(bf16[2048,32]{1,0:T(8,128)(2,1)S(1)} %reshape.523) | copy-start | bytes 393220
  361.2 15.8 %all-to-all-start.5 = ((f32[32,1,32]{2,1,0:T(1,128)}), f32[32,1,32]{2,1,0:T(1,128)S(1)}, u32[]{:S(2)}, u32[]{:S(2)}) async-start(f32[32,1,32]{2,1,0:T(1,128)} %reshape.528), calls=%async_computation.5 | async-start | bytes 32768 | tf_op jit(solution)/shard_map/all_to_all | solution.py:90
  476.7 99.3 %all-to-all-start.3 = ((bf16[32,32,2048]{2,1,0:T(8,128)(2,1)}), bf16[32,32,2048]{2,1,0:T(8,128)(2,1)}, u32[]{:S(2)}, u32[]{:S(2)}) async-start(bf16[32,32,2048]{2,1,0:T(8,128)(2,1)} %bitcast.502), calls=%async_computation.3 | async-start | bytes 8388608 | tf_op jit(solution)/shard_map/all_to_all | solution.py:90
  485.9 19.1 %copy-start.7 = (bf16[32,32,2048]{2,1,0:T(8,128)(2,1)S(1)}, bf16[32,32,2048]{2,1,0:T(8,128)(2,1)}, u32[]{:S(2)}) copy-start(bf16[32,32,2048]{2,1,0:T(8,128)(2,1)} %all_to_all.35) | copy-start | bytes 12582916
  508.1 71.8 %collective-permute-start.25 = (bf16[128,2048]{1,0:T(8,128)(2,1)}, bf16[128,2048]{1,0:T(8,128)(2,1)S(1)}, u32[]{:S(2)}, u32[]{:S(2)}) collective-permute-start(bf16[128,2048]{1,0:T(8,128)(2,1)} %fusion.48), channel_id=1, source_target_pairs={{0,5},{1,4},{4,1},{5,0},{2,7},{3,6},{6,3},{7,2},{8,13},{9,12},{12,... | collective-permute-start | bytes 1572872 | tf_op jit(solution)/shard_map/ppermute | solution.py:111
  510.9 69.0 %collective-permute-start.24 = (bf16[128,2048]{1,0:T(8,128)(2,1)}, bf16[128,2048]{1,0:T(8,128)(2,1)S(1)}, u32[]{:S(2)}, u32[]{:S(2)}) collective-permute-start(bf16[128,2048]{1,0:T(8,128)(2,1)} %fusion.48), channel_id=1, source_target_pairs={{0,4},{1,5},{4,0},{5,1},{2,6},{3,7},{6,2},{7,3},{8,12},{9,13},{12,... | collective-permute-start | bytes 1572872 | tf_op jit(solution)/shard_map/ppermute | solution.py:111
  511.5 70.0 %collective-permute-start.23 = (bf16[128,2048]{1,0:T(8,128)(2,1)}, bf16[128,2048]{1,0:T(8,128)(2,1)}, u32[]{:S(2)}, u32[]{:S(2)}) collective-permute-start(bf16[128,2048]{1,0:T(8,128)(2,1)} %fusion.48), channel_id=1, source_target_pairs={{0,1},{1,0},{4,5},{5,4},{2,3},{3,2},{6,7},{7,6},{8,9},{9,8},{12,13... | collective-permute-start | bytes 1572872 | tf_op jit(solution)/shard_map/ppermute | solution.py:111
  583.4 12.1 %copy-start.16 = (bf16[4,128,2048]{2,1,0:T(8,128)(2,1)}, bf16[4,128,2048]{2,1,0:T(8,128)(2,1)S(1)}, u32[]{:S(2)}) copy-start(bf16[4,128,2048]{2,1,0:T(8,128)(2,1)S(1)} %pad_maximum_fusion.5) | copy-start | bytes 6291460
  624.5 15.3 %collective-permute-start.26 = (bf16[128,2048]{1,0:T(8,128)(2,1)S(1)}, bf16[128,2048]{1,0:T(8,128)(2,1)S(1)}, u32[]{:S(2)}, u32[]{:S(2)}) collective-permute-start(bf16[128,2048]{1,0:T(8,128)(2,1)S(1)} %get-tuple-element.98), channel_id=1, source_target_pairs={{0,1},{1,0},{4,5},{5,4},{2,3},{3,2},{6,7},{7,6},{8,9},{9,8},{12,13... | collective-permute-start | bytes 1572872 | tf_op jit(solution)/shard_map/ppermute | solution.py:99
  625.4 24.8 %collective-permute-start.28 = (bf16[128,2048]{1,0:T(8,128)(2,1)S(1)}, bf16[128,2048]{1,0:T(8,128)(2,1)S(1)}, u32[]{:S(2)}, u32[]{:S(2)}) collective-permute-start(bf16[128,2048]{1,0:T(8,128)(2,1)S(1)} %get-tuple-element.99), channel_id=1, source_target_pairs={{0,5},{1,4},{4,1},{5,0},{2,7},{3,6},{6,3},{7,2},{8,13},{9,12},{12,... | collective-permute-start | bytes 1572872 | tf_op jit(solution)/shard_map/ppermute | solution.py:99
  626.1 24.3 %collective-permute-start.27 = (bf16[128,2048]{1,0:T(8,128)(2,1)S(1)}, bf16[128,2048]{1,0:T(8,128)(2,1)S(1)}, u32[]{:S(2)}, u32[]{:S(2)}) collective-permute-start(bf16[128,2048]{1,0:T(8,128)(2,1)S(1)} %get-tuple-element.100), channel_id=1, source_target_pairs={{0,4},{1,5},{4,0},{5,1},{2,6},{3,7},{6,2},{7,3},{8,12},{9,13},{12,... | collective-permute-start | bytes 1572872 | tf_op jit(solution)/shard_map/ppermute | solution.py:99
  629.6 41.1 %collective-permute-start.36 = (bf16[2,256,2048]{2,1,0:T(8,128)(2,1)}, bf16[2,256,2048]{2,1,0:T(8,128)(2,1)}, u32[]{:S(2)}, u32[]{:S(2)}) collective-permute-start(bf16[2,256,2048]{2,1,0:T(8,128)(2,1)} %fusion.28), channel_id=1, source_target_pairs={{0,2},{2,0},{1,3},{3,1},{4,6},{6,4},{5,7},{7,5},{8,10},{10,8},{9,1... | collective-permute-start | bytes 6291464 | tf_op jit(solution)/shard_map/ppermute | solution.py:81
  636.7 13.7 %copy-start.10 = (bf16[128,2048]{1,0:T(8,128)(2,1)S(1)}, bf16[128,2048]{1,0:T(8,128)(2,1)}, u32[]{:S(2)}) copy-start(bf16[128,2048]{1,0:T(8,128)(2,1)} %param.10) | copy-start | bytes 1572868
  636.7 42.1 %collective-permute-start.29 = (bf16[8,128,1280]{2,1,0:T(8,128)(2,1)}, bf16[8,128,1280]{2,1,0:T(8,128)(2,1)}, u32[]{:S(2)}, u32[]{:S(2)}) collective-permute-start(bf16[8,128,1280]{2,1,0:T(8,128)(2,1)} %fusion.22), channel_id=1, source_target_pairs={{0,2},{2,0},{1,3},{3,1},{4,6},{6,4},{5,7},{7,5},{8,10},{10,8},{9,1... | collective-permute-start | bytes 7864328 | tf_op jit(solution)/shard_map/ppermute | solution.py:81
  639.8 11.4 %copy-start.36 = (f32[32,2048]{1,0:T(8,128)S(1)}, f32[32,2048]{1,0:T(8,128)}, u32[]{:S(2)}) copy-start(f32[32,2048]{1,0:T(8,128)} %reshape.547) | copy-start | bytes 786436
  639.8 22.0 %collective-permute-start.22 = (bf16[128,2048]{1,0:T(8,128)(2,1)S(1)}, bf16[128,2048]{1,0:T(8,128)(2,1)S(1)}, u32[]{:S(2)}, u32[]{:S(2)}) collective-permute-start(bf16[128,2048]{1,0:T(8,128)(2,1)S(1)} %fusion.26), channel_id=1, source_target_pairs={{0,1},{1,0},{2,3},{3,2},{4,5},{5,4},{6,7},{7,6},{8,9},{9,8},{10,11... | collective-permute-start | bytes 1572872 | tf_op jit(solution)/shard_map/ppermute | solution.py:81
  651.2 10.7 %copy-start.50 = (pred[2,256,256]{1,2,0:T(8,128)(4,1)S(1)}, pred[2,256,256]{1,2,0:T(8,128)(4,1)}, u32[]{:S(2)}) copy-start(pred[2,256,256]{1,2,0:T(8,128)(4,1)} %copy-done.49) | copy-start | bytes 393220
  652.1 17.3 %all-to-all-start.6 = ((f32[32,24,128]{2,1,0:T(8,128)}), f32[32,24,128]{2,1,0:T(8,128)S(1)}, u32[]{:S(2)}, u32[]{:S(2)}) async-start(f32[32,24,128]{2,1,0:T(8,128)} %bitcast.193), calls=%async_computation.6 | async-start | bytes 786432 | tf_op jit(solution)/shard_map/all_to_all | solution.py:90
  675.3 14.9 %collective-permute-start.37 = (bf16[128,2048]{1,0:T(8,128)(2,1)S(1)}, bf16[128,2048]{1,0:T(8,128)(2,1)S(1)}, u32[]{:S(2)}, u32[]{:S(2)}) collective-permute-start(bf16[128,2048]{1,0:T(8,128)(2,1)S(1)} %get-tuple-element.95), channel_id=1, source_target_pairs={{0,1},{1,0},{4,5},{5,4},{2,3},{3,2},{6,7},{7,6},{8,9},{9,8},{12,13... | collective-permute-start | bytes 1572872 | tf_op jit(solution)/shard_map/ppermute | solution.py:99
  676.8 24.7 %collective-permute-start.39 = (bf16[128,2048]{1,0:T(8,128)(2,1)S(1)}, bf16[128,2048]{1,0:T(8,128)(2,1)S(1)}, u32[]{:S(2)}, u32[]{:S(2)}) collective-permute-start(bf16[128,2048]{1,0:T(8,128)(2,1)S(1)} %get-tuple-element.96), channel_id=1, source_target_pairs={{0,5},{1,4},{4,1},{5,0},{2,7},{3,6},{6,3},{7,2},{8,13},{9,12},{12,... | collective-permute-start | bytes 1572872 | tf_op jit(solution)/shard_map/ppermute | solution.py:99
  677.7 25.1 %collective-permute-start.38 = (bf16[128,2048]{1,0:T(8,128)(2,1)S(1)}, bf16[128,2048]{1,0:T(8,128)(2,1)S(1)}, u32[]{:S(2)}, u32[]{:S(2)}) collective-permute-start(bf16[128,2048]{1,0:T(8,128)(2,1)S(1)} %get-tuple-element.97), channel_id=1, source_target_pairs={{0,4},{1,5},{4,0},{5,1},{2,6},{3,7},{6,2},{7,3},{8,12},{9,13},{12,... | collective-permute-start | bytes 1572872 | tf_op jit(solution)/shard_map/ppermute | solution.py:99
  681.7 25.6 %collective-permute-start.30 = (bf16[256,1280]{1,0:T(8,128)(2,1)S(1)}, bf16[256,1280]{1,0:T(8,128)(2,1)S(1)}, u32[]{:S(2)}, u32[]{:S(2)}) collective-permute-start(bf16[256,1280]{1,0:T(8,128)(2,1)S(1)} %get-tuple-element.85), channel_id=1, source_target_pairs={{0,8},{8,16},{16,24},{24,0},{1,9},{9,17},{17,25},{25,1},{2,10},{10... | collective-permute-start | bytes 1966088 | tf_op jit(solution)/shard_map/ppermute | solution.py:133
  682.1 47.1 %collective-permute-start.32 = (bf16[256,1280]{1,0:T(8,128)(2,1)S(1)}, bf16[256,1280]{1,0:T(8,128)(2,1)S(1)}, u32[]{:S(2)}, u32[]{:S(2)}) collective-permute-start(bf16[256,1280]{1,0:T(8,128)(2,1)S(1)} %get-tuple-element.86), channel_id=1, source_target_pairs={{0,24},{8,0},{16,8},{24,16},{1,25},{9,1},{17,9},{25,17},{2,26},{10... | collective-permute-start | bytes 1966088 | tf_op jit(solution)/shard_map/ppermute | solution.py:133
  690.1 74.7 %collective-permute-start.31 = (bf16[256,1280]{1,0:T(8,128)(2,1)S(1)}, bf16[256,1280]{1,0:T(8,128)(2,1)S(1)}, u32[]{:S(2)}, u32[]{:S(2)}) collective-permute-start(bf16[256,1280]{1,0:T(8,128)(2,1)S(1)} %get-tuple-element.87), channel_id=1, source_target_pairs={{0,16},{8,24},{16,0},{24,8},{1,17},{9,25},{17,1},{25,9},{2,18},{10... | collective-permute-start | bytes 1966088 | tf_op jit(solution)/shard_map/ppermute | solution.py:133
  703.4 64.1 %collective-permute-start.40 = (bf16[128,2048]{1,0:T(8,128)(2,1)S(1)}, bf16[128,2048]{1,0:T(8,128)(2,1)S(1)}, u32[]{:S(2)}, u32[]{:S(2)}) collective-permute-start(bf16[128,2048]{1,0:T(8,128)(2,1)S(1)} %get-tuple-element.92), channel_id=1, source_target_pairs={{0,8},{8,16},{16,24},{24,0},{1,9},{9,17},{17,25},{25,1},{2,10},{10... | collective-permute-start | bytes 1572872 | tf_op jit(solution)/shard_map/ppermute | solution.py:133
  703.8 65.0 %collective-permute-start.42 = (bf16[128,2048]{1,0:T(8,128)(2,1)S(1)}, bf16[128,2048]{1,0:T(8,128)(2,1)S(1)}, u32[]{:S(2)}, u32[]{:S(2)}) collective-permute-start(bf16[128,2048]{1,0:T(8,128)(2,1)S(1)} %get-tuple-element.93), channel_id=1, source_target_pairs={{0,24},{8,0},{16,8},{24,16},{1,25},{9,1},{17,9},{25,17},{2,26},{10... | collective-permute-start | bytes 1572872 | tf_op jit(solution)/shard_map/ppermute | solution.py:133
  707.3 78.4 %collective-permute-start.41 = (bf16[128,2048]{1,0:T(8,128)(2,1)S(1)}, bf16[128,2048]{1,0:T(8,128)(2,1)S(1)}, u32[]{:S(2)}, u32[]{:S(2)}) collective-permute-start(bf16[128,2048]{1,0:T(8,128)(2,1)S(1)} %get-tuple-element.94), channel_id=1, source_target_pairs={{0,16},{8,24},{16,0},{24,8},{1,17},{9,25},{17,1},{25,9},{2,18},{10... | collective-permute-start | bytes 1572872 | tf_op jit(solution)/shard_map/ppermute | solution.py:133
  765.3 21.7 %collective-permute-start.33 = (bf16[64,1280]{1,0:T(8,128)(2,1)S(1)}, bf16[64,1280]{1,0:T(8,128)(2,1)S(1)}, u32[]{:S(2)}, u32[]{:S(2)}) collective-permute-start(bf16[64,1280]{1,0:T(8,128)(2,1)S(1)} %get-tuple-element.127), channel_id=1, source_target_pairs={{0,1},{1,0},{4,5},{5,4},{2,3},{3,2},{6,7},{7,6},{8,9},{9,8},{12,13... | collective-permute-start | bytes 491528 | tf_op jit(solution)/shard_map/ppermute | solution.py:99
  765.7 21.3 %collective-permute-start.35 = (bf16[64,1280]{1,0:T(8,128)(2,1)S(1)}, bf16[64,1280]{1,0:T(8,128)(2,1)S(1)}, u32[]{:S(2)}, u32[]{:S(2)}) collective-permute-start(bf16[64,1280]{1,0:T(8,128)(2,1)S(1)} %get-tuple-element.128), channel_id=1, source_target_pairs={{0,5},{1,4},{4,1},{5,0},{2,7},{3,6},{6,3},{7,2},{8,13},{9,12},{12,... | collective-permute-start | bytes 491528 | tf_op jit(solution)/shard_map/ppermute | solution.py:99
  767.6 19.4 %collective-permute-start.34 = (bf16[64,1280]{1,0:T(8,128)(2,1)S(1)}, bf16[64,1280]{1,0:T(8,128)(2,1)S(1)}, u32[]{:S(2)}, u32[]{:S(2)}) collective-permute-start(bf16[64,1280]{1,0:T(8,128)(2,1)S(1)} %get-tuple-element.129), channel_id=1, source_target_pairs={{0,4},{1,5},{4,0},{5,1},{2,6},{3,7},{6,2},{7,3},{8,12},{9,13},{12,... | collective-permute-start | bytes 491528 | tf_op jit(solution)/shard_map/ppermute | solution.py:99
  (78 other events, 255.2 us)

commit v3 on v2

--- a/solution.py
+++ b/solution.py
@@ -1,3 +1,5 @@
+import functools
+
 import jax
 import jax.numpy as jnp
 from jax import lax
@@ -146,38 +148,77 @@
     return full
 
 
-def expert_grad_kernel(in_ref, gu_ref, grad_ref, active_ref, out_ref):
+def far_next(value, count):
+    return lax.ppermute(value, FAR_AXIS, [(i, (i + 1) % count) for i in range(count)])
+
+
+def quad_xor(value, step):
+    return lax.ppermute(value, HEAD_AXES, [(i, i ^ step) for i in range(4)])
+
+
+def slab_out(blocks):
+    got = [blocks[0]] + [quad_xor(blocks[step], step) for step in range(1, 4)]
+    keep = jnp.stack([part[0] for part in got])
+    other = swap(jnp.stack([part[1] for part in got]), CORE_AXIS)
+    return jnp.stack([keep, other])
+
+
+def slab_back(blocks):
+    other = swap(blocks[1], CORE_AXIS)
+    parts = [jnp.stack([blocks[0, step], other[step]]) for step in range(4)]
+    return jnp.stack([parts[0]] + [quad_xor(parts[step], step) for step in range(1, 4)])
+
+
+def ring_reduce(parts, count):
+    total = parts[1].astype(BF)
+    for step in range(2, count):
+        total = (far_next(total, count).astype(F32) + parts[step]).astype(BF)
+    return far_next(total, count).astype(F32) + parts[0]
+
+
+def expert_grad_kernel(count, *refs):
+    in_refs, gu_refs = refs[:count], refs[count : 2 * count]
+    grad_refs, active_refs = refs[2 * count : 3 * count], refs[3 * count : 4 * count]
+    out_ref = refs[4 * count]
     column = pl.program_id(1)
+
+    def total(lefts, rights):
+        found = mm_tn(lefts[0][...], rights[0][...])
+        for left, right in zip(lefts[1:], rights[1:]):
+            found = found + mm_tn(left[...], right[...])
+        out_ref[...] = found
 
     @pl.when(column < 2)
     def _():
-        out_ref[...] = mm_tn(in_ref[...], gu_ref[...])
+        total(in_refs, gu_refs)
 
     @pl.when(column == 2)
     def _():
-        out_ref[...] = mm_tn(grad_ref[...], active_ref[...])
-
-
-def expert_grads(in_flat, gu_grad, grad_flat, active):
-    rows = in_flat.shape[0]
+        total(grad_refs, active_refs)
+
+
+def expert_grads(in_rows, gu_grads, grad_rows, actives):
+    count = len(in_rows)
+    rows = in_rows[0].shape[0]
     tile = 512
+    tall = pl.BlockSpec((rows, tile), lambda i, j: (0, i))
+    gate_up = pl.BlockSpec((rows, FF), lambda i, j: (0, jnp.minimum(j, 1)))
+    whole = pl.BlockSpec((rows, FF), lambda i, j: (0, 0))
+    total_rows = rows * count
     return pl.pallas_call(
-        expert_grad_kernel,
+        functools.partial(expert_grad_kernel, count),
         grid=(D // tile, 3),
-        in_specs=[
-            pl.BlockSpec((rows, tile), lambda i, j: (0, i)),
-            pl.BlockSpec((rows, FF), lambda i, j: (0, jnp.minimum(j, 1))),
-            pl.BlockSpec((rows, tile), lambda i, j: (0, i)),
-            pl.BlockSpec((rows, FF), lambda i, j: (0, 0)),
-        ],
+        in_specs=[tall] * count + [gate_up] * count + [tall] * count + [whole] * count,
         out_specs=pl.BlockSpec((tile, FF), lambda i, j: (i, j)),
         out_shape=jax.ShapeDtypeStruct((D, 3 * FF), F32),
         compiler_params=pltpu.CompilerParams(vmem_limit_bytes=48 << 20),
         cost_estimate=pl.CostEstimate(
-            flops=2 * rows * D * 3 * FF, bytes_accessed=rows * D * 4 + D * 3 * FF * 4, transcendentals=0
+            flops=2 * total_rows * D * 3 * FF,
+            bytes_accessed=total_rows * D * 4 + D * 3 * FF * 4,
+            transcendentals=0,
         ),
         name="expert_grads",
-    )(in_flat, gu_grad, grad_flat, active)
+    )(*in_rows, *gu_grads, *grad_rows, *actives)
 
 
 def shards(tokens, cotangent, w_qkv, w_out, w_router, norm_gains, w_expert, lengths, deal, routes):
@@ -188,6 +229,7 @@
     slot_count = experts_all * capacity
     seq_index = lax.axis_index(SEQ_AXIS)
     near_index = lax.axis_index(NEAR_AXIS)
+    far_index = lax.axis_index(FAR_AXIS)
     core_index = lax.axis_index(CORE_AXIS)
     per_group = HEADS // KV_HEADS
     qcols = per_group * HEAD_DIM
@@ -227,6 +269,35 @@
     slot_hot = place.T[:, None, :] == jnp.arange(capacity, dtype=jnp.int32)[None, :, None]
     slot_low = slot_hot.astype(BF).reshape(slot_count, TOK_DEV)
 
+    slab = NEAR * CORES * 2
+    slab_index = (near_index * CORES + core_index) * 2 + seq_index
+    out_order = jnp.array([0, 2, 1, 3, 4, 6, 5, 7], jnp.int32)
+    in_order = jnp.array([0, 1, 4, 5, 2, 3, 6, 7], jnp.int32)
+    place_far = ring_gather(place.T.astype(BF), FAR_AXIS, far_count)
+    place_slab = jnp.take(
+        place_far, far_index * slab + lax.bitwise_xor(out_order, slab_index), axis=1
+    ).astype(jnp.int32)
+    chunk_slots = []
+    for step in range(far_count):
+        found = lax.dynamic_index_in_dim(
+            place_slab, lax.rem(far_index + far_count - step, far_count), 0, keepdims=False
+        )
+        found = found[:, None, :] == jnp.arange(capacity, dtype=jnp.int32)[None, :, None]
+        chunk_slots.append(found.astype(BF).reshape(slab * capacity, TOK_DEV))
+    chunk_steps = jnp.arange(far_count, dtype=jnp.int32)
+    source_ids = (
+        lax.rem(far_index + far_count - chunk_steps, far_count)[:, None] * slab
+        + lax.bitwise_xor(in_order, slab_index)[None, :]
+    ).reshape(device_count)
+    device_ids = jnp.arange(device_count, dtype=jnp.int32)
+    found_at = jnp.sum(
+        jnp.where(source_ids[None, :] == device_ids[:, None], device_ids[None, :], 0), axis=1
+    )
+
+    def to_blocks(rows):
+        return rows.reshape(4, 2, rows.shape[0] // slab, rows.shape[1])
+
+
     router_size = qkv_rows * experts_all
     small_size = router_size + gain_rows
     mask_size = capacity * experts_all
@@ -240,7 +311,9 @@
     small_all = exchange(small.reshape(device_count, small_rows, LANES), ALL_AXES).reshape(
         device_count, small_rows * LANES
     )
-    mask_back = small_all[:, :mask_size].reshape(slot_count, experts_all)
+    mask_back = jnp.take(small_all[:, :mask_size], source_ids, axis=0).reshape(
+        far_count, slab * capacity, experts_all
+    )
     small_all = small_all[:, mask_size : mask_size + small_size]
     router_full = small_all[:, :router_size].reshape(D, experts_all)
     gains_float = small_all[:, router_size:].reshape(-1).astype(F32)
@@ -252,9 +325,6 @@
     cot_pair = jnp.concatenate(pair_order(cotangent, swap(cotangent, SEQ_AXIS), SEQ_AXIS), axis=0)
     cot_low = mm(hot_half, cot_pair).astype(BF)
     cot_rows = cot_low.astype(F32)
-    cot_sent = mm(slot_low, cot_low).astype(BF).reshape(experts_all, capacity, D)
-    cot_back = exchange(cot_sent, ALL_AXES).reshape(slot_count, D)
-
     wide = jnp.concatenate(
         [
             w_qkv[:, :QDIM].reshape(qkv_rows, KV_HEADS, qcols),
@@ -271,7 +341,17 @@
         D, width
     )
 
-    out_slabs = ring_gather(w_out, FAR_AXIS, far_count).reshape(
+    w_late, cot_late, _ = lax.optimization_barrier((w_out, cot_low, qkv_own))
+    cot_far = [cot_late]
+    for step in range(1, far_count):
+        cot_far.append(far_next(cot_far[-1], far_count))
+    cot_sent = jnp.stack(
+        [to_blocks(mm(hot, rows).astype(BF)) for hot, rows in zip(chunk_slots, cot_far)], axis=2
+    )
+    cot_back = slab_out(cot_sent.reshape(4, 2, far_count * capacity, D)).reshape(
+        slab, far_count, capacity, D
+    )
+    out_slabs = ring_gather(w_late, FAR_AXIS, far_count).reshape(
         KV_HEADS, far_count // KV_HEADS * out_rows, D
     )
     far_part = far_count // KV_HEADS
@@ -318,69 +398,92 @@
     mixed_low = mixed_heads.astype(BF).reshape(2 * ROW, qcols)
     out_partial = mm(mixed_low, out_mine).astype(BF)
     residual = x_rows + quad_sum(out_partial.reshape(4, TOK_DEV, D))
-    residual, cot_back = lax.optimization_barrier((residual, cot_back))
 
     normed_two, ffn_back = jax.vjp(rms_norm, residual, gain_ffn)
     ffn_in = normed_two.astype(BF)
-    send_rows = mm(slot_low, ffn_in).astype(BF).reshape(experts_all, capacity, D)
-    in_flat = exchange(send_rows, ALL_AXES).reshape(slot_count, D)
+    ffn_in, cot_back = lax.optimization_barrier((ffn_in, cot_back))
     logits = mm(ffn_in, router_full)
     logits = jnp.where(chosen > 0.5, logits, -1e30)
     gate_probs = jax.nn.softmax(logits, axis=-1)
     gate_probs = jnp.where(chosen > 0.5, gate_probs, 0.0)
+
     expert_weight = w_expert[0]
-    expert_here = (
-        (lax.axis_index(FAR_AXIS) * NEAR + near_index) * CORES + core_index
-    ) * 2 + seq_index
-    slot_logits = jnp.where(mask_back > 0.5, mm(in_flat, router_full), -1e30)
-    slot_probs = jnp.where(mask_back > 0.5, jax.nn.softmax(slot_logits, axis=-1), 0.0)
-    gate_back = jnp.sum(jnp.where(expert_ids == expert_here, slot_probs, 0.0), axis=1, keepdims=True)
-    gate_up = mm(in_flat, expert_weight[:, : 2 * FF])
-    gate_pre = gate_up[:, :FF]
-    up_pre = gate_up[:, FF:]
-    sig_gate = jax.nn.sigmoid(gate_pre)
-    silu_val = gate_pre * sig_gate
-    active = (silu_val * up_pre).astype(BF)
-    expert_out = mm_nt(active, expert_weight[:, 2 * FF :]).astype(BF)
-    cot_float = cot_back.astype(F32)
-    slot_dot = jnp.sum(cot_float * expert_out.astype(F32), axis=1)
-    dot_back = exchange(slot_dot.reshape(device_count, 1, capacity), ALL_AXES).reshape(
-        experts_all, capacity
-    )
-    grad_flat = (gate_back * cot_float).astype(BF)
-    act_grad = mm(grad_flat, expert_weight[:, 2 * FF :])
-    silu_slope = sig_gate * (1.0 + gate_pre * (1.0 - sig_gate))
-    gu_grad = jnp.concatenate([act_grad * up_pre * silu_slope, act_grad * silu_val], axis=1).astype(BF)
-    in_grad = mm_nt(gu_grad, expert_weight[:, : 2 * FF]).astype(BF)
-    pair_grads = exchange(in_grad.reshape(device_count, capacity, D), ALL_AXES).reshape(slot_count, D)
-    returned = exchange(expert_out.reshape(device_count, capacity, D), ALL_AXES).reshape(slot_count, D)
-    grad_expert = expert_grads(in_flat, gu_grad, grad_flat, active)[None]
+    expert_here = far_index * slab + slab_index
+    in_rows, gu_grads, grad_rows, actives, gated_outs, slot_dots, partials = ([] for _ in range(7))
+    far_rows = ffn_in
+    for step in range(far_count):
+        hot = chunk_slots[step]
+        in_chunk = slab_out(to_blocks(mm(hot, far_rows).astype(BF))).reshape(slab * capacity, D)
+        if step < far_count - 1:
+            far_rows = far_next(far_rows, far_count)
+        mask = mask_back[step]
+        slot_logits = jnp.where(mask > 0.5, mm(in_chunk, router_full), -1e30)
+        slot_probs = jnp.where(mask > 0.5, jax.nn.softmax(slot_logits, axis=-1), 0.0)
+        gate_slot = jnp.sum(
+            jnp.where(expert_ids == expert_here, slot_probs, 0.0), axis=1, keepdims=True
+        )
+        gate_up = mm(in_chunk, expert_weight[:, : 2 * FF])
+        gate_pre = gate_up[:, :FF]
+        up_pre = gate_up[:, FF:]
+        sig_gate = jax.nn.sigmoid(gate_pre)
+        silu_val = gate_pre * sig_gate
+        active = (silu_val * up_pre).astype(BF)
+        expert_out = mm_nt(active, expert_weight[:, 2 * FF :]).astype(BF).astype(F32)
+        cot_float = cot_back[:, step].reshape(slab * capacity, D).astype(F32)
+        slot_dots.append(jnp.sum(cot_float * expert_out, axis=1))
+        gated_outs.append((gate_slot * expert_out).astype(BF).reshape(2, 4, capacity, D))
+        grad_chunk = (gate_slot * cot_float).astype(BF)
+        act_grad = mm(grad_chunk, expert_weight[:, 2 * FF :])
+        silu_slope = sig_gate * (1.0 + gate_pre * (1.0 - sig_gate))
+        gu_grad = jnp.concatenate(
+            [act_grad * up_pre * silu_slope, act_grad * silu_val], axis=1
+        ).astype(BF)
+        in_grad = mm_nt(gu_grad, expert_weight[:, : 2 * FF]).astype(BF)
+        back = slab_back(in_grad.reshape(2, 4, capacity, D)).reshape(slab * capacity, D)
+        partials.append(mm_tn(hot, back))
+        in_rows.append(in_chunk)
+        gu_grads.append(gu_grad)
+        grad_rows.append(grad_chunk)
+        actives.append(active)
+    dot_sent = jnp.take(jnp.stack(slot_dots).reshape(device_count, capacity), found_at, axis=0)
+    dot_back = exchange(dot_sent[:, None, :], ALL_AXES).reshape(experts_all, capacity)
+    from_experts = ring_reduce(partials, far_count)
+    grad_expert = expert_grads(in_rows, gu_grads, grad_rows, actives)[None]
 
     gate_grad = jnp.sum(jnp.where(slot_hot, dot_back[:, :, None], 0.0), axis=1).T
     mean_term = jnp.sum(gate_probs * gate_grad, axis=1, keepdims=True)
     logit_grad = (gate_probs * (gate_grad - mean_term)).astype(BF)
     router_grad = mm_tn(ffn_in, logit_grad)
-    ffn_in_grad = mm_tn(slot_low, pair_grads) + mm_nt(logit_grad, router_full)
+    ffn_in_grad = from_experts + mm_nt(logit_grad, router_full)
     resid_part, gain_ffn_grad = ffn_back(ffn_in_grad)
     resid_low = (cot_rows + resid_part).astype(BF)
-    resid_both = quad_gather(resid_low).reshape(2 * ROW, D)
-
-    gate_slots = jnp.where(slot_hot, gate_probs.T[:, None, :], 0.0).reshape(slot_count, TOK_DEV)
-    gate_high = gate_slots.astype(BF)
-    gate_rest = (gate_slots - gate_high.astype(F32)).astype(BF)
-    final_rows = (residual + mm_tn(gate_high, returned) + mm_tn(gate_rest, returned)).astype(BF)
+
+    gated_sent = jnp.stack(gated_outs, axis=2).reshape(2, 4, far_count * capacity, D)
+    gated_sent, resid_low = lax.optimization_barrier((gated_sent, resid_low))
+    gated_back = slab_back(gated_sent).reshape(slab, far_count, capacity, D)
+    out_sum = ring_reduce(
+        [
+            mm_tn(hot, gated_back[:, step].reshape(slab * capacity, D))
+            for step, hot in enumerate(chunk_slots)
+        ],
+        far_count,
+    )
+    final_rows = (residual + out_sum).astype(BF)
     final_pair = jnp.concatenate(
         pair_order(final_rows, swap(final_rows, SEQ_AXIS), SEQ_AXIS), axis=0
     )
     layer_out = mm_tn(back_half, final_pair).astype(BF)
+
+    resid_both = quad_gather(resid_low).reshape(2 * ROW, D)
 
     def core_sum(values):
         own, other = pair_order(values[:, 0], values[:, 1], CORE_AXIS)
         return own.astype(F32) + swap(other, CORE_AXIS).astype(F32)
 
     mixed_grad = mm_nt(resid_both, out_mine).astype(BF)
+    out_grad = mm_tn(mixed_low, resid_both).astype(BF)
+    mixed_grad, out_grad = lax.optimization_barrier((mixed_grad, out_grad))
     grad_heads = mixed_grad.reshape(2, ROW, per_group, HEAD_DIM)
-    out_grad = mm_tn(mixed_low, resid_both).astype(BF)
     out_grad = core_sum(out_grad.reshape(far_part * NEAR, CORES, 2 * out_rows, D))
     out_grad = (
         out_grad.astype(BF)

time: 798 us -> 846 us (1.060)
  waiting for transfers between devices: 334 us -> 464 us
  blocking collectives: 99.6 us -> 0 us
  matrix products: 95.8 us -> 74.5 us
  starting transfers between devices: 111 us -> 127 us
  local copies, waits for them, and re-layouts: 54.7 us -> 68.1 us
    ppermute x0 -> x42, waiting for transfers between devices: none -> 197 us  [the longest x30 133 us: quad_xor(): return lax.ppermute(value, HEAD_AXES, [(i, i ^ step) for i in range(4)])]
    all_to_all x6 -> x3, waiting for transfers between devices: 170 us -> 6.9 us  [exchange(): return lax.all_to_all(value, axes, split_axis=0, concat_axis=0, tiled=True)]
    all_to_all x1 -> x0, blocking collectives: 99.6 us -> none  [exchange(): return lax.all_to_all(value, axes, split_axis=0, concat_axis=0, tiled=True)]
    ppermute x6 -> x9, waiting for transfers between devices: 25.1 us -> 72.5 us  [ring_gather(): lax.ppermute(chunk, axis, [(i, (i + 1) % count) for i in range(count)])]
    ppermute x0 -> x42, starting transfers between devices: none -> 41.7 us  [the longest x30 39.1 us: quad_xor(): return lax.ppermute(value, HEAD_AXES, [(i, i ^ step) for i in range(4)])]
    ppermute x7 -> x17, waiting for transfers between devices: 8.98 us -> 32.1 us  [swap(): return lax.ppermute(value, axis, [(0, 1), (1, 0)])]
    dot_general x25 -> x51, matrix products: 82.1 us -> 62.2 us  [dot(): lax.dot_general(left, right, (dims, ((), ())), preferred_element_type=F32)]
    ppermute x6, waiting for transfers between devices: 52.5 us -> 71.1 us  [far_sum(): lax.ppermute(block, FAR_AXIS, [(i, (i + step) % count) for i in range(cou...]
  transfers between devices with their start and end apart: 49 -> 101, of which waited for: 20 -> 56; matrix products, arithmetic and copies ran while one was open for 17% -> 22% of each run, Pallas kernels for 2% -> 2%
where the time goes in v3:
time: 846 us; the launch traced here: 836 us
  waiting for transfers between devices  464 us (55%)
  starting transfers between devices  127 us (15%)
  other arithmetic  79.9 us (9%)
  matrix products  74.5 us (9%)
  local copies, waits for them, and re-layouts  68.1 us (8%)
  Pallas kernels  18.6 us (2%)
    ppermute x30, waiting for transfers between devices, quad_xor(): return lax.ppermute(value, HEAD_AXES, [(i, i ^ step) for i in range(4)])  133 us
    ppermute x9, waiting for transfers between devices, ring_gather(): lax.ppermute(chunk, axis, [(i, (i + 1) % count) for i in range(count)])  72.5 us
    ppermute x6, waiting for transfers between devices, far_sum(): lax.ppermute(block, FAR_AXIS, [(i, (i + step) % count) for i in range(cou...  71.1 us
    ppermute x18, waiting for transfers between devices, quad_send(): return lax.ppermute(block, HEAD_AXES, [(i, i ^ step) for i in range(4)])  67.2 us
    ppermute x12, waiting for transfers between devices, far_next(): lax.ppermute(value, FAR_AXIS, [(i, (i + 1) % count) for i in range(count)])  63.6 us
    dot_general x51, matrix products, dot(): lax.dot_general(left, right, (dims, ((), ())), preferred_element_type=F32)  62.2 us
    ppermute x30, starting transfers between devices, quad_xor(): return lax.ppermute(value, HEAD_AXES, [(i, i ^ step) for i in range(4)])  39.1 us
    ppermute x17, waiting for transfers between devices, swap(): return lax.ppermute(value, axis, [(0, 1), (1, 0)])  32.1 us
  transfers between devices with their start and end apart: 101, of which 56 were waited for; matrix products, arithmetic and copies ran while one was open for 22% of the time, Pallas kernels for 2%

profile of v3, /device:TPU:0, one launch (start us, length us, event | category | flops | bytes accessed | tf_op | source)
XLA Modules:
  0.0 836.1 jit_solution(11999941763197074187)
XLA Ops:
  0.6 4.0 collective-permute-start.3
  15.8 12.4 %collective-permute-done = s32[1,384]{1,0:T(1,128)S(1)} collective-permute-done((s32[1,384]{1,0:T(1,128)S(1)}, s32[1,384]{1,0:T(1,128)S(1)}, u32[]{:S(2)}, u32[]{:S(2)}) %collective-permute-start) | collective-permute-done | bytes 1568 | tf_op jit(solution)/shard_map/ppermute | solution.py:83
  36.1 4.6 collective-permute-done.23
  41.5 6.3 all-to-all-start
  48.1 2.7 collective-permute-start.6
  72.1 7.9 collective-permute-done.11
  84.2 15.2 %collective-permute-done.8 = bf16[256,1280]{1,0:T(8,128)(2,1)S(1)} collective-permute-done((bf16[256,1280]{1,0:T(8,128)(2,1)}, bf16[256,1280]{1,0:T(8,128)(2,1)S(1)}, u32[]{:S(2)}, u32[]{:S(2)}) %collective-permute-start.8) | collective-permute-done | bytes 655392 | tf_op jit(solution)/shard_map/ppermute | solution.py:146
  102.4 14.1 %collective-permute-done.9 = bf16[256,1280]{1,0:T(8,128)(2,1)S(1)} collective-permute-done((bf16[256,1280]{1,0:T(8,128)(2,1)S(1)}, bf16[256,1280]{1,0:T(8,128)(2,1)S(1)}, u32[]{:S(2)}, u32[]{:S(2)}) %collective-permute-start.9) | collective-permute-done | bytes 655392 | tf_op jit(solution)/shard_map/ppermute | solution.py:146
  118.6 15.3 %collective-permute-done.12 = bf16[128,2048]{1,0:T(8,128)(2,1)S(1)} collective-permute-done((bf16[128,2048]{1,0:T(8,128)(2,1)S(1)}, bf16[128,2048]{1,0:T(8,128)(2,1)S(1)}, u32[]{:S(2)}, u32[]{:S(2)}) %collective-permute-start.12) | collective-permute-done | bytes 524320 | tf_op jit(solution)/shard_map/ppermute | solution.py:146
  133.9 11.2 %collective-permute-done.25 = bf16[128,2048]{1,0:T(8,128)(2,1)S(1)} collective-permute-done((bf16[128,2048]{1,0:T(8,128)(2,1)S(1)}, bf16[128,2048]{1,0:T(8,128)(2,1)S(1)}, u32[]{:S(2)}, u32[]{:S(2)}) %collective-permute-start.25) | collective-permute-done | bytes 524320 | tf_op jit(solution)/shard_map/ppermute | solution.py:152
  145.6 10.7 %collective-permute-done.13 = bf16[128,2048]{1,0:T(8,128)(2,1)S(1)} collective-permute-done((bf16[128,2048]{1,0:T(8,128)(2,1)S(1)}, bf16[128,2048]{1,0:T(8,128)(2,1)S(1)}, u32[]{:S(2)}, u32[]{:S(2)}) %collective-permute-start.13) | collective-permute-done | bytes 524320 | tf_op jit(solution)/shard_map/ppermute | solution.py:146
  156.4 11.2 %collective-permute-done.26 = bf16[128,2048]{1,0:T(8,128)(2,1)S(1)} collective-permute-done((bf16[128,2048]{1,0:T(8,128)(2,1)S(1)}, bf16[128,2048]{1,0:T(8,128)(2,1)S(1)}, u32[]{:S(2)}, u32[]{:S(2)}) %collective-permute-start.26) | collective-permute-done | bytes 524320 | tf_op jit(solution)/shard_map/ppermute | solution.py:152
  168.1 10.7 %collective-permute-done.14 = bf16[128,2048]{1,0:T(8,128)(2,1)S(1)} collective-permute-done((bf16[128,2048]{1,0:T(8,128)(2,1)S(1)}, bf16[128,2048]{1,0:T(8,128)(2,1)S(1)}, u32[]{:S(2)}, u32[]{:S(2)}) %collective-permute-start.14) | collective-permute-done | bytes 524320 | tf_op jit(solution)/shard_map/ppermute | solution.py:146
  182.6 7.1 collective-permute-done.27
  195.4 10.8 %collective-permute-done.17 = bf16[128,2048]{1,0:T(8,128)(2,1)S(1)} collective-permute-done((bf16[128,2048]{1,0:T(8,128)(2,1)S(1)}, bf16[128,2048]{1,0:T(8,128)(2,1)S(1)}, u32[]{:S(2)}, u32[]{:S(2)}) %collective-permute-start.17) | collective-permute-done | bytes 524320 | tf_op jit(solution)/shard_map/ppermute | solution.py:101
  212.9 2.9 fusion.203
  218.0 33.0 %collective-permute-done.29 = bf16[2,128,2048]{2,1,0:T(8,128)(2,1)S(1)} collective-permute-done((bf16[2,128,2048]{2,1,0:T(8,128)(2,1)S(1)}, bf16[2,128,2048]{2,1,0:T(8,128)(2,1)S(1)}, u32[]{:S(2)}, u32[]{:S(2)}) %collective-permute-start.29) | collective-permute-done | bytes 1048608 | tf_op jit(solution)/shard_map/ppermute | solution.py:156
  262.5 4.0 fusion.196
  266.6 2.7 fusion.29
  270.3 2.9 select_bitcast_fusion.3
  281.8 9.0 %collective-permute-done.19 = bf16[128,2048]{1,0:T(8,128)(2,1)S(1)} collective-permute-done((bf16[128,2048]{1,0:T(8,128)(2,1)S(1)}, bf16[128,2048]{1,0:T(8,128)(2,1)S(1)}, u32[]{:S(2)}, u32[]{:S(2)}) %collective-permute-start.19) | collective-permute-done | bytes 524320 | tf_op jit(solution)/shard_map/ppermute | solution.py:101
  290.9 10.9 %collective-permute-done.21 = bf16[128,2048]{1,0:T(8,128)(2,1)S(1)} collective-permute-done((bf16[128,2048]{1,0:T(8,128)(2,1)S(1)}, bf16[128,2048]{1,0:T(8,128)(2,1)S(1)}, u32[]{:S(2)}, u32[]{:S(2)}) %collective-permute-start.21) | collective-permute-done | bytes 524320 | tf_op jit(solution)/shard_map/ppermute | solution.py:101
  312.0 5.8 collective-permute-done.34
  317.8 3.7 collective-permute-done.32
  325.9 6.5 collective-permute-done.39
  332.5 5.1 collective-permute-done.37
  345.4 6.4 collective-permute-done.44
  351.9 4.2 collective-permute-done.42
  364.0 6.7 collective-permute-done.49
  370.7 4.0 collective-permute-done.47
  393.6 2.8 convolution_convert_fusion.14
  415.2 5.8 all-to-all-start.1
  426.4 18.6 %expert_grads.1 = f32[2048,2304]{1,0:T(8,128)} custom-call(bf16[256,2048]{1,0:T(8,128)(2,1)S(1)} %bitcast.699, bf16[256,2048]{1,0:T(8,128)(2,1)} %bitcast.739, bf16[256,2048]{1,0:T(8,128)(2,1)} %bitcast.742, bf16[256,2048]{1,0:T(8,128)(2,1)} %bitcast.745, bf16[256,1536]{1,0:T(8,128)(2,1)S(1)} %pad_maximum_fusion.27.refs_4_, ...), custom_call_target="tpu_custom_call" | custom-call | flops 9663676416 | bytes 27262976 | tf_op jit(solution)/shard_map/expert_grads/pallas_call | solution.py:208
  461.1 4.6 collective-permute-done.52
  468.9 3.6 collective-permute-done.54
  480.2 3.6 collective-permute-done.59
  491.9 3.2 collective-permute-done.64
  495.3 6.5 collective-permute-done.60
  507.0 8.1 collective-permute-done.65
  523.2 9.4 %collective-permute-done.80 = bf16[128,2048]{1,0:T(8,128)(2,1)S(1)} collective-permute-done((bf16[128,2048]{1,0:T(8,128)(2,1)S(1)}, bf16[128,2048]{1,0:T(8,128)(2,1)S(1)}, u32[]{:S(2)}, u32[]{:S(2)}) %collective-permute-start.80) | collective-permute-done | bytes 524320 | tf_op jit(solution)/shard_map/ppermute | solution.py:113
  532.6 6.4 collective-permute-done.79
  539.4 2.7 copy-done.38
  564.1 3.0 multiply_reduce_fusion.1
  569.0 4.3 add_add_fusion
  575.3 3.1 convolution_convert_fusion.3
  582.1 4.9 convolution_convert_fusion
  587.1 6.3 collective-permute-done.81
  593.4 11.0 %collective-permute-done.83 = bf16[128,2048]{1,0:T(8,128)(2,1)S(1)} collective-permute-done((bf16[128,2048]{1,0:T(8,128)(2,1)S(1)}, bf16[128,2048]{1,0:T(8,128)(2,1)S(1)}, u32[]{:S(2)}, u32[]{:S(2)}) %collective-permute-start.83) | collective-permute-done | bytes 524320 | tf_op jit(solution)/shard_map/ppermute | solution.py:101
  607.4 2.6 all-to-all-start.2
  610.0 4.4 fusion.9
  615.8 6.9 all-to-all-done.2
  630.8 2.8 fusion.2
  634.7 17.4 %collective-permute-done.71 = bf16[2,128,2048]{2,1,0:T(8,128)(2,1)S(1)} collective-permute-done((bf16[2,128,2048]{2,1,0:T(8,128)(2,1)S(1)}, bf16[2,128,2048]{2,1,0:T(8,128)(2,1)S(1)}, u32[]{:S(2)}, u32[]{:S(2)}) %collective-permute-start.71) | collective-permute-done | bytes 1048608 | tf_op jit(solution)/shard_map/ppermute | solution.py:156
  653.9 21.9 %collective-permute-done.72 = bf16[2,128,2048]{2,1,0:T(8,128)(2,1)S(1)} collective-permute-done((bf16[2,128,2048]{2,1,0:T(8,128)(2,1)S(1)}, bf16[2,128,2048]{2,1,0:T(8,128)(2,1)S(1)}, u32[]{:S(2)}, u32[]{:S(2)}) %collective-permute-start.72) | collective-permute-done | bytes 1048608 | tf_op jit(solution)/shard_map/ppermute | solution.py:156
  679.3 2.8 fusion.1
  683.2 2.6 collective-permute-done.92
  686.8 10.3 %collective-permute-done.94 = bf16[128,2048]{1,0:T(8,128)(2,1)S(1)} collective-permute-done((bf16[128,2048]{1,0:T(8,128)(2,1)S(1)}, bf16[128,2048]{1,0:T(8,128)(2,1)S(1)}, u32[]{:S(2)}, u32[]{:S(2)}) %collective-permute-start.94) | collective-permute-done | bytes 524320 | tf_op jit(solution)/shard_map/ppermute | solution.py:101
  703.0 5.8 collective-permute-done.85
  708.8 26.1 %collective-permute-start.96 = (bf16[128,2048]{1,0:T(8,128)(2,1)S(1)}, bf16[128,2048]{1,0:T(8,128)(2,1)S(1)}, u32[]{:S(2)}, u32[]{:S(2)}) collective-permute-start(bf16[128,2048]{1,0:T(8,128)(2,1)S(1)} %get-tuple-element.135), channel_id=1, source_target_pairs={{0,16},{8,24},{16,0},{24,8},{1,17},{9,25},{17,1},{25,9},{2,18},{10... | collective-permute-start | bytes 1572872 | tf_op jit(solution)/shard_map/ppermute | solution.py:135
  735.0 46.8 %collective-permute-done.86 = bf16[256,1280]{1,0:T(8,128)(2,1)S(1)} collective-permute-done((bf16[256,1280]{1,0:T(8,128)(2,1)S(1)}, bf16[256,1280]{1,0:T(8,128)(2,1)S(1)}, u32[]{:S(2)}, u32[]{:S(2)}) %collective-permute-start.86) | collective-permute-done | bytes 655392 | tf_op jit(solution)/shard_map/ppermute | solution.py:135
  782.4 2.6 collective-permute-start.90
  785.7 18.5 %collective-permute-done.96 = bf16[128,2048]{1,0:T(8,128)(2,1)S(1)} collective-permute-done((bf16[128,2048]{1,0:T(8,128)(2,1)S(1)}, bf16[128,2048]{1,0:T(8,128)(2,1)S(1)}, u32[]{:S(2)}, u32[]{:S(2)}) %collective-permute-start.96) | collective-permute-done | bytes 524320 | tf_op jit(solution)/shard_map/ppermute | solution.py:135
  806.2 15.2 %collective-permute-done.76 = bf16[128,2048]{1,0:T(8,128)(2,1)S(1)} collective-permute-done((bf16[128,2048]{1,0:T(8,128)(2,1)S(1)}, bf16[128,2048]{1,0:T(8,128)(2,1)S(1)}, u32[]{:S(2)}, u32[]{:S(2)}) %collective-permute-start.76) | collective-permute-done | bytes 524320 | tf_op jit(solution)/shard_map/ppermute | solution.py:152
  823.0 11.8 %collective-permute-done.77 = bf16[128,2048]{1,0:T(8,128)(2,1)S(1)} collective-permute-done((bf16[128,2048]{1,0:T(8,128)(2,1)S(1)}, bf16[128,2048]{1,0:T(8,128)(2,1)S(1)}, u32[]{:S(2)}, u32[]{:S(2)}) %collective-permute-start.77) | collective-permute-done | bytes 524320 | tf_op jit(solution)/shard_map/ppermute | solution.py:83
  (849 shorter events, 272.9 us)
Async XLA Ops:
  0.6 67.3 %collective-permute-start.3 = (bf16[128,2048]{1,0:T(8,128)(2,1)}, bf16[128,2048]{1,0:T(8,128)(2,1)}, u32[]{:S(2)}, u32[]{:S(2)}) collective-permute-start(bf16[128,2048]{1,0:T(8,128)(2,1)} %param.12), channel_id=1, source_target_pairs={{0,5},{1,4},{4,1},{5,0},{2,7},{3,6},{6,3},{7,2},{8,13},{9,12},{12,... | collective-permute-start | bytes 1572872 | tf_op jit(solution)/shard_map/ppermute | solution.py:113
  4.6 63.4 %collective-permute-start.2 = (bf16[128,2048]{1,0:T(8,128)(2,1)}, bf16[128,2048]{1,0:T(8,128)(2,1)}, u32[]{:S(2)}, u32[]{:S(2)}) collective-permute-start(bf16[128,2048]{1,0:T(8,128)(2,1)} %param.12), channel_id=1, source_target_pairs={{0,4},{1,5},{4,0},{5,1},{2,6},{3,7},{6,2},{7,3},{8,12},{9,13},{12,... | collective-permute-start | bytes 1572872 | tf_op jit(solution)/shard_map/ppermute | solution.py:113
  5.8 22.4 %collective-permute-start = (s32[1,384]{1,0:T(1,128)S(1)}, s32[1,384]{1,0:T(1,128)S(1)}, u32[]{:S(2)}, u32[]{:S(2)}) collective-permute-start(s32[1,384]{1,0:T(1,128)S(1)} %pad_add_fusion.2), channel_id=1, source_target_pairs={{0,4},{4,0},{1,5},{5,1},{2,6},{6,2},{3,7},{7,3},{8,12},{12,8},{9,1... | collective-permute-start | bytes 4616 | tf_op jit(solution)/shard_map/ppermute | solution.py:83
  11.5 42.8 %collective-permute-start.4 = (bf16[64,1280]{1,0:T(8,128)(2,1)S(1)}, bf16[64,1280]{1,0:T(8,128)(2,1)S(1)}, u32[]{:S(2)}, u32[]{:S(2)}) collective-permute-start(bf16[64,1280]{1,0:T(8,128)(2,1)S(1)} %bitcast.833), channel_id=1, source_target_pairs={{0,1},{1,0},{4,5},{5,4},{2,3},{3,2},{6,7},{7,6},{8,9},{9,8},{12,13... | collective-permute-start | bytes 491528 | tf_op jit(solution)/shard_map/ppermute | solution.py:101
  12.2 42.8 %collective-permute-start.5 = (bf16[64,1280]{1,0:T(8,128)(2,1)S(1)}, bf16[64,1280]{1,0:T(8,128)(2,1)S(1)}, u32[]{:S(2)}, u32[]{:S(2)}) collective-permute-start(bf16[64,1280]{1,0:T(8,128)(2,1)S(1)} %bitcast.832), channel_id=1, source_target_pairs={{0,4},{1,5},{4,0},{5,1},{2,6},{3,7},{6,2},{7,3},{8,12},{9,13},{12,... | collective-permute-start | bytes 491528 | tf_op jit(solution)/shard_map/ppermute | solution.py:101
  41.5 21.2 %all-to-all-start = ((bf16[32,32,128]{2,1,0:T(8,128)(2,1)}), bf16[32,32,128]{2,1,0:T(8,128)(2,1)S(1)}, u32[]{:S(2)}, u32[]{:S(2)}) async-start(bf16[32,32,128]{2,1,0:T(8,128)(2,1)} %bitcast.320), calls=%async_computation | async-start | bytes 524288 | tf_op jit(solution)/shard_map/all_to_all | solution.py:92
  54.9 25.1 %collective-permute-start.11 = (bf16[128,2048]{1,0:T(8,128)(2,1)}, bf16[128,2048]{1,0:T(8,128)(2,1)}, u32[]{:S(2)}, u32[]{:S(2)}) collective-permute-start(bf16[128,2048]{1,0:T(8,128)(2,1)} %param.13), channel_id=1, source_target_pairs={{0,1},{1,0},{2,3},{3,2},{4,5},{5,4},{6,7},{7,6},{8,9},{9,8},{10,11... | collective-permute-start | bytes 1572872 | tf_op jit(solution)/shard_map/ppermute | solution.py:83
  58.5 22.8 %collective-permute-start.7 = (bf16[256,1280]{1,0:T(8,128)(2,1)S(1)}, bf16[256,1280]{1,0:T(8,128)(2,1)}, u32[]{:S(2)}, u32[]{:S(2)}) collective-permute-start(bf16[256,1280]{1,0:T(8,128)(2,1)S(1)} %bitcast.757), channel_id=1, source_target_pairs={{0,8},{8,16},{16,24},{24,0},{1,9},{9,17},{17,25},{25,1},{2,10},{10... | collective-permute-start | bytes 1966088 | tf_op jit(solution)/shard_map/ppermute | solution.py:146
  81.3 18.2 %collective-permute-start.8 = (bf16[256,1280]{1,0:T(8,128)(2,1)}, bf16[256,1280]{1,0:T(8,128)(2,1)S(1)}, u32[]{:S(2)}, u32[]{:S(2)}) collective-permute-start(bf16[256,1280]{1,0:T(8,128)(2,1)} %collective-permute-done.7), channel_id=1, source_target_pairs={{0,8},{8,16},{16,24},{24,0},{1,9},{9,17},{17,25},{25,1},{2,10},{10... | collective-permute-start | bytes 1966088 | tf_op jit(solution)/shard_map/ppermute | solution.py:146
  99.5 17.0 %collective-permute-start.9 = (bf16[256,1280]{1,0:T(8,128)(2,1)S(1)}, bf16[256,1280]{1,0:T(8,128)(2,1)S(1)}, u32[]{:S(2)}, u32[]{:S(2)}) collective-permute-start(bf16[256,1280]{1,0:T(8,128)(2,1)S(1)} %collective-permute-done.8), channel_id=1, source_target_pairs={{0,8},{8,16},{16,24},{24,0},{1,9},{9,17},{17,25},{25,1},{2,10},{10... | collective-permute-start | bytes 1966088 | tf_op jit(solution)/shard_map/ppermute | solution.py:146
  117.4 92.6 %collective-permute-start.10 = (bf16[8,128,1280]{2,1,0:T(8,128)(2,1)}, bf16[8,128,1280]{2,1,0:T(8,128)(2,1)S(1)}, u32[]{:S(2)}, u32[]{:S(2)}) collective-permute-start(bf16[8,128,1280]{2,1,0:T(8,128)(2,1)} %bitcast.22), channel_id=1, source_target_pairs={{0,2},{2,0},{1,3},{3,1},{4,6},{6,4},{5,7},{7,5},{8,10},{10,8},{9,1... | collective-permute-start | bytes 7864328 | tf_op jit(solution)/shard_map/ppermute | solution.py:83
  117.4 16.5 %collective-permute-start.12 = (bf16[128,2048]{1,0:T(8,128)(2,1)S(1)}, bf16[128,2048]{1,0:T(8,128)(2,1)S(1)}, u32[]{:S(2)}, u32[]{:S(2)}) collective-permute-start(bf16[128,2048]{1,0:T(8,128)(2,1)S(1)} %copy-done.73), channel_id=1, source_target_pairs={{0,8},{8,16},{16,24},{24,0},{1,9},{9,17},{17,25},{25,1},{2,10},{10... | collective-permute-start | bytes 1572872 | tf_op jit(solution)/shard_map/ppermute | solution.py:146
  117.4 27.7 %collective-permute-start.25 = (bf16[128,2048]{1,0:T(8,128)(2,1)S(1)}, bf16[128,2048]{1,0:T(8,128)(2,1)S(1)}, u32[]{:S(2)}, u32[]{:S(2)}) collective-permute-start(bf16[128,2048]{1,0:T(8,128)(2,1)S(1)} %convolution_convert_fusion.24), channel_id=1, source_target_pairs={{0,8},{8,16},{16,24},{24,0},{1,9},{9,17},{17,25},{25,1},{2,10},{10... | collective-permute-start | bytes 1572872 | tf_op jit(solution)/shard_map/ppermute | solution.py:152
  133.9 22.5 %collective-permute-start.13 = (bf16[128,2048]{1,0:T(8,128)(2,1)S(1)}, bf16[128,2048]{1,0:T(8,128)(2,1)S(1)}, u32[]{:S(2)}, u32[]{:S(2)}) collective-permute-start(bf16[128,2048]{1,0:T(8,128)(2,1)S(1)} %collective-permute-done.12), channel_id=1, source_target_pairs={{0,8},{8,16},{16,24},{24,0},{1,9},{9,17},{17,25},{25,1},{2,10},{10... | collective-permute-start | bytes 1572872 | tf_op jit(solution)/shard_map/ppermute | solution.py:146
  145.1 22.5 %collective-permute-start.26 = (bf16[128,2048]{1,0:T(8,128)(2,1)S(1)}, bf16[128,2048]{1,0:T(8,128)(2,1)S(1)}, u32[]{:S(2)}, u32[]{:S(2)}) collective-permute-start(bf16[128,2048]{1,0:T(8,128)(2,1)S(1)} %collective-permute-done.25), channel_id=1, source_target_pairs={{0,8},{8,16},{16,24},{24,0},{1,9},{9,17},{17,25},{25,1},{2,10},{10... | collective-permute-start | bytes 1572872 | tf_op jit(solution)/shard_map/ppermute | solution.py:152
  156.4 22.5 %collective-permute-start.14 = (bf16[128,2048]{1,0:T(8,128)(2,1)S(1)}, bf16[128,2048]{1,0:T(8,128)(2,1)S(1)}, u32[]{:S(2)}, u32[]{:S(2)}) collective-permute-start(bf16[128,2048]{1,0:T(8,128)(2,1)S(1)} %collective-permute-done.13), channel_id=1, source_target_pairs={{0,8},{8,16},{16,24},{24,0},{1,9},{9,17},{17,25},{25,1},{2,10},{10... | collective-permute-start | bytes 1572872 | tf_op jit(solution)/shard_map/ppermute | solution.py:146
  167.6 22.1 %collective-permute-start.27 = (bf16[128,2048]{1,0:T(8,128)(2,1)S(1)}, bf16[128,2048]{1,0:T(8,128)(2,1)S(1)}, u32[]{:S(2)}, u32[]{:S(2)}) collective-permute-start(bf16[128,2048]{1,0:T(8,128)(2,1)S(1)} %collective-permute-done.26), channel_id=1, source_target_pairs={{0,8},{8,16},{16,24},{24,0},{1,9},{9,17},{17,25},{25,1},{2,10},{10... | collective-permute-start | bytes 1572872 | tf_op jit(solution)/shard_map/ppermute | solution.py:152
  180.6 25.7 %collective-permute-start.17 = (bf16[128,2048]{1,0:T(8,128)(2,1)S(1)}, bf16[128,2048]{1,0:T(8,128)(2,1)S(1)}, u32[]{:S(2)}, u32[]{:S(2)}) collective-permute-start(bf16[128,2048]{1,0:T(8,128)(2,1)S(1)} %get-tuple-element.158), channel_id=1, source_target_pairs={{0,5},{1,4},{4,1},{5,0},{2,7},{3,6},{6,3},{7,2},{8,13},{9,12},{12,... | collective-permute-start | bytes 1572872 | tf_op jit(solution)/shard_map/ppermute | solution.py:101
  182.1 26.1 %collective-permute-start.16 = (bf16[128,2048]{1,0:T(8,128)(2,1)S(1)}, bf16[128,2048]{1,0:T(8,128)(2,1)S(1)}, u32[]{:S(2)}, u32[]{:S(2)}) collective-permute-start(bf16[128,2048]{1,0:T(8,128)(2,1)S(1)} %get-tuple-element.159), channel_id=1, source_target_pairs={{0,4},{1,5},{4,0},{5,1},{2,6},{3,7},{6,2},{7,3},{8,12},{9,13},{12,... | collective-permute-start | bytes 1572872 | tf_op jit(solution)/shard_map/ppermute | solution.py:101
  190.9 60.0 %collective-permute-start.29 = (bf16[2,128,2048]{2,1,0:T(8,128)(2,1)S(1)}, bf16[2,128,2048]{2,1,0:T(8,128)(2,1)S(1)}, u32[]{:S(2)}, u32[]{:S(2)}) collective-permute-start(bf16[2,128,2048]{2,1,0:T(8,128)(2,1)S(1)} %bitcast.782), channel_id=1, source_target_pairs={{0,4},{1,5},{4,0},{5,1},{2,6},{3,7},{6,2},{7,3},{8,12},{9,13},{12,... | collective-permute-start | bytes 3145736 | tf_op jit(solution)/shard_map/ppermute | solution.py:156
  194.0 57.8 %collective-permute-start.28 = (bf16[2,128,2048]{2,1,0:T(8,128)(2,1)S(1)}, bf16[2,128,2048]{2,1,0:T(8,128)(2,1)S(1)}, u32[]{:S(2)}, u32[]{:S(2)}) collective-permute-start(bf16[2,128,2048]{2,1,0:T(8,128)(2,1)S(1)} %bitcast.781), channel_id=1, source_target_pairs={{0,1},{1,0},{4,5},{5,4},{2,3},{3,2},{6,7},{7,6},{8,9},{9,8},{12,13... | collective-permute-start | bytes 3145736 | tf_op jit(solution)/shard_map/ppermute | solution.py:156
  206.2 46.4 %collective-permute-start.30 = (bf16[2,128,2048]{2,1,0:T(8,128)(2,1)S(1)}, bf16[2,128,2048]{2,1,0:T(8,128)(2,1)S(1)}, u32[]{:S(2)}, u32[]{:S(2)}) collective-permute-start(bf16[2,128,2048]{2,1,0:T(8,128)(2,1)S(1)} %bitcast.780), channel_id=1, source_target_pairs={{0,5},{1,4},{4,1},{5,0},{2,7},{3,6},{6,3},{7,2},{8,13},{9,12},{12,... | collective-permute-start | bytes 3145736 | tf_op jit(solution)/shard_map/ppermute | solution.py:156
  210.0 60.3 %collective-permute-start.18 = (bf16[2,256,2048]{2,1,0:T(8,128)(2,1)}, bf16[2,256,2048]{2,1,0:T(8,128)(2,1)}, u32[]{:S(2)}, u32[]{:S(2)}) collective-permute-start(bf16[2,256,2048]{2,1,0:T(8,128)(2,1)} %bitcast.50), channel_id=1, source_target_pairs={{0,2},{2,0},{1,3},{3,1},{4,6},{6,4},{5,7},{7,5},{8,10},{10,8},{9,1... | collective-permute-start | bytes 6291464 | tf_op jit(solution)/shard_map/ppermute | solution.py:83
  255.2 48.5 %collective-permute-start.31 = (bf16[4,128,2048]{2,1,0:T(8,128)(2,1)}, bf16[4,128,2048]{2,1,0:T(8,128)(2,1)}, u32[]{:S(2)}, u32[]{:S(2)}) collective-permute-start(bf16[4,128,2048]{2,1,0:T(8,128)(2,1)} %pad_maximum_fusion.8), channel_id=1, source_target_pairs={{0,2},{2,0},{1,3},{3,1},{4,6},{6,4},{5,7},{7,5},{8,10},{10,8},{9,1... | collective-permute-start | bytes 6291464 | tf_op jit(solution)/shard_map/ppermute | solution.py:83
  277.5 24.3 %collective-permute-start.21 = (bf16[128,2048]{1,0:T(8,128)(2,1)S(1)}, bf16[128,2048]{1,0:T(8,128)(2,1)S(1)}, u32[]{:S(2)}, u32[]{:S(2)}) collective-permute-start(bf16[128,2048]{1,0:T(8,128)(2,1)S(1)} %get-tuple-element.151), channel_id=1, source_target_pairs={{0,5},{1,4},{4,1},{5,0},{2,7},{3,6},{6,3},{7,2},{8,13},{9,12},{12,... | collective-permute-start | bytes 1572872 | tf_op jit(solution)/shard_map/ppermute | solution.py:101
  278.1 25.0 %collective-permute-start.20 = (bf16[128,2048]{1,0:T(8,128)(2,1)S(1)}, bf16[128,2048]{1,0:T(8,128)(2,1)S(1)}, u32[]{:S(2)}, u32[]{:S(2)}) collective-permute-start(bf16[128,2048]{1,0:T(8,128)(2,1)S(1)} %get-tuple-element.152), channel_id=1, source_target_pairs={{0,4},{1,5},{4,0},{5,1},{2,6},{3,7},{6,2},{7,3},{8,12},{9,13},{12,... | collective-permute-start | bytes 1572872 | tf_op jit(solution)/shard_map/ppermute | solution.py:101
  321.6 16.2 %collective-permute-start.35 = (bf16[4,32,2048]{2,1,0:T(8,128)(2,1)S(1)}, bf16[4,32,2048]{2,1,0:T(8,128)(2,1)S(1)}, u32[]{:S(2)}, u32[]{:S(2)}) collective-permute-start(bf16[4,32,2048]{2,1,0:T(8,128)(2,1)S(1)} %pad_maximum_fusion.31), channel_id=1, source_target_pairs={{0,2},{2,0},{1,3},{3,1},{4,6},{6,4},{5,7},{7,5},{8,10},{10,8},{9,1... | collective-permute-start | bytes 1572872 | tf_op jit(solution)/shard_map/ppermute | solution.py:83
  337.7 18.6 %collective-permute-start.40 = (bf16[4,32,2048]{2,1,0:T(8,128)(2,1)S(1)}, bf16[4,32,2048]{2,1,0:T(8,128)(2,1)S(1)}, u32[]{:S(2)}, u32[]{:S(2)}) collective-permute-start(bf16[4,32,2048]{2,1,0:T(8,128)(2,1)S(1)} %pad_maximum_fusion.32), channel_id=1, source_target_pairs={{0,2},{2,0},{1,3},{3,1},{4,6},{6,4},{5,7},{7,5},{8,10},{10,8},{9,1... | collective-permute-start | bytes 1572872 | tf_op jit(solution)/shard_map/ppermute | solution.py:83
  356.3 18.6 %collective-permute-start.45 = (bf16[4,32,2048]{2,1,0:T(8,128)(2,1)S(1)}, bf16[4,32,2048]{2,1,0:T(8,128)(2,1)S(1)}, u32[]{:S(2)}, u32[]{:S(2)}) collective-permute-start(bf16[4,32,2048]{2,1,0:T(8,128)(2,1)S(1)} %pad_maximum_fusion.33), channel_id=1, source_target_pairs={{0,2},{2,0},{1,3},{3,1},{4,6},{6,4},{5,7},{7,5},{8,10},{10,8},{9,1... | collective-permute-start | bytes 1572872 | tf_op jit(solution)/shard_map/ppermute | solution.py:83
  400.2 48.6 %collective-permute-start.66 = (bf16[4,32,2048]{2,1,0:T(8,128)(2,1)}, bf16[4,32,2048]{2,1,0:T(8,128)(2,1)}, u32[]{:S(2)}, u32[]{:S(2)}) collective-permute-start(bf16[4,32,2048]{2,1,0:T(8,128)(2,1)} %bitcast.174), channel_id=1, source_target_pairs={{0,2},{2,0},{1,3},{3,1},{4,6},{6,4},{5,7},{7,5},{8,10},{10,8},{9,1... | collective-permute-start | bytes 1572872 | tf_op jit(solution)/shard_map/ppermute | solution.py:83
  404.6 47.9 %collective-permute-start.51 = (bf16[4,32,2048]{2,1,0:T(8,128)(2,1)}, bf16[4,32,2048]{2,1,0:T(8,128)(2,1)}, u32[]{:S(2)}, u32[]{:S(2)}) collective-permute-start(bf16[4,32,2048]{2,1,0:T(8,128)(2,1)} %bitcast.135), channel_id=1, source_target_pairs={{0,2},{2,0},{1,3},{3,1},{4,6},{6,4},{5,7},{7,5},{8,10},{10,8},{9,1... | collective-permute-start | bytes 1572872 | tf_op jit(solution)/shard_map/ppermute | solution.py:83
  408.5 48.2 %collective-permute-start.56 = (bf16[4,32,2048]{2,1,0:T(8,128)(2,1)}, bf16[4,32,2048]{2,1,0:T(8,128)(2,1)}, u32[]{:S(2)}, u32[]{:S(2)}) collective-permute-start(bf16[4,32,2048]{2,1,0:T(8,128)(2,1)} %bitcast.148), channel_id=1, source_target_pairs={{0,2},{2,0},{1,3},{3,1},{4,6},{6,4},{5,7},{7,5},{8,10},{10,8},{9,1... | collective-permute-start | bytes 1572872 | tf_op jit(solution)/shard_map/ppermute | solution.py:83
  415.2 32.1 %all-to-all-start.1 = ((f32[32,1,32]{2,1,0:T(1,128)}), f32[32,1,32]{2,1,0:T(1,128)}, u32[]{:S(2)}, u32[]{:S(2)}) async-start(f32[32,1,32]{2,1,0:T(1,128)} %bitcast.194), calls=%async_computation.1 | async-start | bytes 32768 | tf_op jit(solution)/shard_map/all_to_all | solution.py:92
  425.0 34.5 %collective-permute-start.61 = (bf16[4,32,2048]{2,1,0:T(8,128)(2,1)}, bf16[4,32,2048]{2,1,0:T(8,128)(2,1)}, u32[]{:S(2)}, u32[]{:S(2)}) collective-permute-start(bf16[4,32,2048]{2,1,0:T(8,128)(2,1)} %bitcast.161), channel_id=1, source_target_pairs={{0,2},{2,0},{1,3},{3,1},{4,6},{6,4},{5,7},{7,5},{8,10},{10,8},{9,1... | collective-permute-start | bytes 1572872 | tf_op jit(solution)/shard_map/ppermute | solution.py:83
  450.8 54.2 %collective-permute-start.67 = (bf16[2,32,2048]{2,1,0:T(8,128)(2,1)}, bf16[2,32,2048]{2,1,0:T(8,128)(2,1)}, u32[]{:S(2)}, u32[]{:S(2)}) collective-permute-start(bf16[2,32,2048]{2,1,0:T(8,128)(2,1)} %pad_maximum_fusion.44), channel_id=1, source_target_pairs={{0,1},{1,0},{4,5},{5,4},{2,3},{3,2},{6,7},{7,6},{8,9},{9,8},{12,13... | collective-permute-start | bytes 786440 | tf_op jit(solution)/shard_map/ppermute | solution.py:156
  459.5 17.5 %collective-permute-start.57 = (bf16[2,32,2048]{2,1,0:T(8,128)(2,1)S(1)}, bf16[2,32,2048]{2,1,0:T(8,128)(2,1)S(1)}, u32[]{:S(2)}, u32[]{:S(2)}) collective-permute-start(bf16[2,32,2048]{2,1,0:T(8,128)(2,1)S(1)} %pad_maximum_fusion.38), channel_id=1, source_target_pairs={{0,1},{1,0},{4,5},{5,4},{2,3},{3,2},{6,7},{7,6},{8,9},{9,8},{12,13... | collective-permute-start | bytes 786440 | tf_op jit(solution)/shard_map/ppermute | solution.py:156
  467.4 16.4 %collective-permute-start.59 = (bf16[2,32,2048]{2,1,0:T(8,128)(2,1)S(1)}, bf16[2,32,2048]{2,1,0:T(8,128)(2,1)S(1)}, u32[]{:S(2)}, u32[]{:S(2)}) collective-permute-start(bf16[2,32,2048]{2,1,0:T(8,128)(2,1)S(1)} %pad_maximum_fusion.40), channel_id=1, source_target_pairs={{0,5},{1,4},{4,1},{5,0},{2,7},{3,6},{6,3},{7,2},{8,13},{9,12},{12,... | collective-permute-start | bytes 786440 | tf_op jit(solution)/shard_map/ppermute | solution.py:156
  488.9 16.9 %collective-permute-start.68 = (bf16[2,32,2048]{2,1,0:T(8,128)(2,1)}, bf16[2,32,2048]{2,1,0:T(8,128)(2,1)}, u32[]{:S(2)}, u32[]{:S(2)}) collective-permute-start(bf16[2,32,2048]{2,1,0:T(8,128)(2,1)} %pad_maximum_fusion.45), channel_id=1, source_target_pairs={{0,4},{1,5},{4,0},{5,1},{2,6},{3,7},{6,2},{7,3},{8,12},{9,13},{12,... | collective-permute-start | bytes 786440 | tf_op jit(solution)/shard_map/ppermute | solution.py:156
  490.0 15.8 %collective-permute-start.69 = (bf16[2,32,2048]{2,1,0:T(8,128)(2,1)}, bf16[2,32,2048]{2,1,0:T(8,128)(2,1)}, u32[]{:S(2)}, u32[]{:S(2)}) collective-permute-start(bf16[2,32,2048]{2,1,0:T(8,128)(2,1)} %pad_maximum_fusion.46), channel_id=1, source_target_pairs={{0,5},{1,4},{4,1},{5,0},{2,7},{3,6},{6,3},{7,2},{8,13},{9,12},{12,... | collective-permute-start | bytes 786440 | tf_op jit(solution)/shard_map/ppermute | solution.py:156
  516.7 15.8 %collective-permute-start.80 = (bf16[128,2048]{1,0:T(8,128)(2,1)S(1)}, bf16[128,2048]{1,0:T(8,128)(2,1)S(1)}, u32[]{:S(2)}, u32[]{:S(2)}) collective-permute-start(bf16[128,2048]{1,0:T(8,128)(2,1)S(1)} %fusion.55), channel_id=1, source_target_pairs={{0,5},{1,4},{4,1},{5,0},{2,7},{3,6},{6,3},{7,2},{8,13},{9,12},{12,... | collective-permute-start | bytes 1572872 | tf_op jit(solution)/shard_map/ppermute | solution.py:113
  518.2 20.7 %collective-permute-start.79 = (bf16[128,2048]{1,0:T(8,128)(2,1)S(1)}, bf16[128,2048]{1,0:T(8,128)(2,1)S(1)}, u32[]{:S(2)}, u32[]{:S(2)}) collective-permute-start(bf16[128,2048]{1,0:T(8,128)(2,1)S(1)} %fusion.55), channel_id=1, source_target_pairs={{0,4},{1,5},{4,0},{5,1},{2,6},{3,7},{6,2},{7,3},{8,12},{9,13},{12,... | collective-permute-start | bytes 1572872 | tf_op jit(solution)/shard_map/ppermute | solution.py:113
  519.7 19.2 %collective-permute-start.78 = (bf16[128,2048]{1,0:T(8,128)(2,1)S(1)}, bf16[128,2048]{1,0:T(8,128)(2,1)S(1)}, u32[]{:S(2)}, u32[]{:S(2)}) collective-permute-start(bf16[128,2048]{1,0:T(8,128)(2,1)S(1)} %fusion.55), channel_id=1, source_target_pairs={{0,1},{1,0},{4,5},{5,4},{2,3},{3,2},{6,7},{7,6},{8,9},{9,8},{12,13... | collective-permute-start | bytes 1572872 | tf_op jit(solution)/shard_map/ppermute | solution.py:113
  521.8 102.3 %collective-permute-start.70 = (bf16[4,128,2048]{2,1,0:T(8,128)(2,1)}, bf16[4,128,2048]{2,1,0:T(8,128)(2,1)}, u32[]{:S(2)}, u32[]{:S(2)}) collective-permute-start(bf16[4,128,2048]{2,1,0:T(8,128)(2,1)} %slice_bitcast_fusion.1), channel_id=1, source_target_pairs={{0,2},{2,0},{1,3},{3,1},{4,6},{6,4},{5,7},{7,5},{8,10},{10,8},{9,1... | collective-permute-start | bytes 6291464 | tf_op jit(solution)/shard_map/ppermute | solution.py:83
  555.0 75.2 %collective-permute-start.91 = (bf16[2,256,2048]{2,1,0:T(8,128)(2,1)}, bf16[2,256,2048]{2,1,0:T(8,128)(2,1)}, u32[]{:S(2)}, u32[]{:S(2)}) collective-permute-start(bf16[2,256,2048]{2,1,0:T(8,128)(2,1)} %fusion.24), channel_id=1, source_target_pairs={{0,2},{2,0},{1,3},{3,1},{4,6},{6,4},{5,7},{7,5},{8,10},{10,8},{9,1... | collective-permute-start | bytes 6291464 | tf_op jit(solution)/shard_map/ppermute | solution.py:83
  579.3 25.0 %collective-permute-start.83 = (bf16[128,2048]{1,0:T(8,128)(2,1)S(1)}, bf16[128,2048]{1,0:T(8,128)(2,1)S(1)}, u32[]{:S(2)}, u32[]{:S(2)}) collective-permute-start(bf16[128,2048]{1,0:T(8,128)(2,1)S(1)} %get-tuple-element.140), channel_id=1, source_target_pairs={{0,5},{1,4},{4,1},{5,0},{2,7},{3,6},{6,3},{7,2},{8,13},{9,12},{12,... | collective-permute-start | bytes 1572872 | tf_op jit(solution)/shard_map/ppermute | solution.py:101
  580.7 25.0 %collective-permute-start.82 = (bf16[128,2048]{1,0:T(8,128)(2,1)S(1)}, bf16[128,2048]{1,0:T(8,128)(2,1)S(1)}, u32[]{:S(2)}, u32[]{:S(2)}) collective-permute-start(bf16[128,2048]{1,0:T(8,128)(2,1)S(1)} %get-tuple-element.141), channel_id=1, source_target_pairs={{0,4},{1,5},{4,0},{5,1},{2,6},{3,7},{6,2},{7,3},{8,12},{9,13},{12,... | collective-permute-start | bytes 1572872 | tf_op jit(solution)/shard_map/ppermute | solution.py:101
  614.4 63.7 %collective-permute-start.84 = (bf16[8,128,1280]{2,1,0:T(8,128)(2,1)}, bf16[8,128,1280]{2,1,0:T(8,128)(2,1)}, u32[]{:S(2)}, u32[]{:S(2)}) collective-permute-start(bf16[8,128,1280]{2,1,0:T(8,128)(2,1)} %fusion.9), channel_id=1, source_target_pairs={{0,2},{2,0},{1,3},{3,1},{4,6},{6,4},{5,7},{7,5},{8,10},{10,8},{9,1... | collective-permute-start | bytes 7864328 | tf_op jit(solution)/shard_map/ppermute | solution.py:83
  625.9 26.1 %collective-permute-start.71 = (bf16[2,128,2048]{2,1,0:T(8,128)(2,1)S(1)}, bf16[2,128,2048]{2,1,0:T(8,128)(2,1)S(1)}, u32[]{:S(2)}, u32[]{:S(2)}) collective-permute-start(bf16[2,128,2048]{2,1,0:T(8,128)(2,1)S(1)} %pad_maximum_fusion.21), channel_id=1, source_target_pairs={{0,1},{1,0},{4,5},{5,4},{2,3},{3,2},{6,7},{7,6},{8,9},{9,8},{12,13... | collective-permute-start | bytes 3145736 | tf_op jit(solution)/shard_map/ppermute | solution.py:156
  627.5 48.3 %collective-permute-start.72 = (bf16[2,128,2048]{2,1,0:T(8,128)(2,1)S(1)}, bf16[2,128,2048]{2,1,0:T(8,128)(2,1)S(1)}, u32[]{:S(2)}, u32[]{:S(2)}) collective-permute-start(bf16[2,128,2048]{2,1,0:T(8,128)(2,1)S(1)} %pad_maximum_fusion.22), channel_id=1, source_target_pairs={{0,4},{1,5},{4,0},{5,1},{2,6},{3,7},{6,2},{7,3},{8,12},{9,13},{12,... | collective-permute-start | bytes 3145736 | tf_op jit(solution)/shard_map/ppermute | solution.py:156
  628.7 47.5 %collective-permute-start.73 = (bf16[2,128,2048]{2,1,0:T(8,128)(2,1)S(1)}, bf16[2,128,2048]{2,1,0:T(8,128)(2,1)S(1)}, u32[]{:S(2)}, u32[]{:S(2)}) collective-permute-start(bf16[2,128,2048]{2,1,0:T(8,128)(2,1)S(1)} %pad_maximum_fusion.23), channel_id=1, source_target_pairs={{0,5},{1,4},{4,1},{5,0},{2,7},{3,6},{6,3},{7,2},{8,13},{9,12},{12,... | collective-permute-start | bytes 3145736 | tf_op jit(solution)/shard_map/ppermute | solution.py:156
  633.8 52.0 %collective-permute-start.92 = (bf16[128,2048]{1,0:T(8,128)(2,1)S(1)}, bf16[128,2048]{1,0:T(8,128)(2,1)S(1)}, u32[]{:S(2)}, u32[]{:S(2)}) collective-permute-start(bf16[128,2048]{1,0:T(8,128)(2,1)S(1)} %get-tuple-element.136), channel_id=1, source_target_pairs={{0,1},{1,0},{4,5},{5,4},{2,3},{3,2},{6,7},{7,6},{8,9},{9,8},{12,13... | collective-permute-start | bytes 1572872 | tf_op jit(solution)/shard_map/ppermute | solution.py:101
  652.0 45.0 %collective-permute-start.94 = (bf16[128,2048]{1,0:T(8,128)(2,1)S(1)}, bf16[128,2048]{1,0:T(8,128)(2,1)S(1)}, u32[]{:S(2)}, u32[]{:S(2)}) collective-permute-start(bf16[128,2048]{1,0:T(8,128)(2,1)S(1)} %get-tuple-element.137), channel_id=1, source_target_pairs={{0,5},{1,4},{4,1},{5,0},{2,7},{3,6},{6,3},{7,2},{8,13},{9,12},{12,... | collective-permute-start | bytes 1572872 | tf_op jit(solution)/shard_map/ppermute | solution.py:101
  675.9 21.9 %collective-permute-start.93 = (bf16[128,2048]{1,0:T(8,128)(2,1)S(1)}, bf16[128,2048]{1,0:T(8,128)(2,1)S(1)}, u32[]{:S(2)}, u32[]{:S(2)}) collective-permute-start(bf16[128,2048]{1,0:T(8,128)(2,1)S(1)} %get-tuple-element.138), channel_id=1, source_target_pairs={{0,4},{1,5},{4,0},{5,1},{2,6},{3,7},{6,2},{7,3},{8,12},{9,13},{12,... | collective-permute-start | bytes 1572872 | tf_op jit(solution)/shard_map/ppermute | solution.py:101
  678.0 23.0 %collective-permute-start.74 = (bf16[128,2048]{1,0:T(8,128)(2,1)S(1)}, bf16[128,2048]{1,0:T(8,128)(2,1)S(1)}, u32[]{:S(2)}, u32[]{:S(2)}) collective-permute-start(bf16[128,2048]{1,0:T(8,128)(2,1)S(1)} %convolution_convert_fusion.22), channel_id=1, source_target_pairs={{0,8},{8,16},{16,24},{24,0},{1,9},{9,17},{17,25},{25,1},{2,10},{10... | collective-permute-start | bytes 1572872 | tf_op jit(solution)/shard_map/ppermute | solution.py:152
  682.3 26.6 %collective-permute-start.85 = (bf16[256,1280]{1,0:T(8,128)(2,1)S(1)}, bf16[256,1280]{1,0:T(8,128)(2,1)S(1)}, u32[]{:S(2)}, u32[]{:S(2)}) collective-permute-start(bf16[256,1280]{1,0:T(8,128)(2,1)S(1)} %get-tuple-element.118), channel_id=1, source_target_pairs={{0,8},{8,16},{16,24},{24,0},{1,9},{9,17},{17,25},{25,1},{2,10},{10... | collective-permute-start | bytes 1966088 | tf_op jit(solution)/shard_map/ppermute | solution.py:135
  685.8 49.2 %collective-permute-start.87 = (bf16[256,1280]{1,0:T(8,128)(2,1)S(1)}, bf16[256,1280]{1,0:T(8,128)(2,1)S(1)}, u32[]{:S(2)}, u32[]{:S(2)}) collective-permute-start(bf16[256,1280]{1,0:T(8,128)(2,1)S(1)} %get-tuple-element.119), channel_id=1, source_target_pairs={{0,24},{8,0},{16,8},{24,16},{1,25},{9,1},{17,9},{25,17},{2,26},{10... | collective-permute-start | bytes 1966088 | tf_op jit(solution)/shard_map/ppermute | solution.py:135
  697.1 84.7 %collective-permute-start.86 = (bf16[256,1280]{1,0:T(8,128)(2,1)S(1)}, bf16[256,1280]{1,0:T(8,128)(2,1)S(1)}, u32[]{:S(2)}, u32[]{:S(2)}) collective-permute-start(bf16[256,1280]{1,0:T(8,128)(2,1)S(1)} %get-tuple-element.120), channel_id=1, source_target_pairs={{0,16},{8,24},{16,0},{24,8},{1,17},{9,25},{17,1},{25,9},{2,18},{10... | collective-permute-start | bytes 1966088 | tf_op jit(solution)/shard_map/ppermute | solution.py:135
  698.4 84.1 %collective-permute-start.95 = (bf16[128,2048]{1,0:T(8,128)(2,1)S(1)}, bf16[128,2048]{1,0:T(8,128)(2,1)S(1)}, u32[]{:S(2)}, u32[]{:S(2)}) collective-permute-start(bf16[128,2048]{1,0:T(8,128)(2,1)S(1)} %get-tuple-element.133), channel_id=1, source_target_pairs={{0,8},{8,16},{16,24},{24,0},{1,9},{9,17},{17,25},{25,1},{2,10},{10... | collective-permute-start | bytes 1572872 | tf_op jit(solution)/shard_map/ppermute | solution.py:135
  701.0 84.0 %collective-permute-start.97 = (bf16[128,2048]{1,0:T(8,128)(2,1)S(1)}, bf16[128,2048]{1,0:T(8,128)(2,1)S(1)}, u32[]{:S(2)}, u32[]{:S(2)}) collective-permute-start(bf16[128,2048]{1,0:T(8,128)(2,1)S(1)} %get-tuple-element.134), channel_id=1, source_target_pairs={{0,24},{8,0},{16,8},{24,16},{1,25},{9,1},{17,9},{25,17},{2,26},{10... | collective-permute-start | bytes 1572872 | tf_op jit(solution)/shard_map/ppermute | solution.py:135
  708.8 95.3 %collective-permute-start.96 = (bf16[128,2048]{1,0:T(8,128)(2,1)S(1)}, bf16[128,2048]{1,0:T(8,128)(2,1)S(1)}, u32[]{:S(2)}, u32[]{:S(2)}) collective-permute-start(bf16[128,2048]{1,0:T(8,128)(2,1)S(1)} %get-tuple-element.135), channel_id=1, source_target_pairs={{0,16},{8,24},{16,0},{24,8},{1,17},{9,25},{17,1},{25,9},{2,18},{10... | collective-permute-start | bytes 1572872 | tf_op jit(solution)/shard_map/ppermute | solution.py:135
  735.0 70.6 %collective-permute-start.75 = (bf16[128,2048]{1,0:T(8,128)(2,1)S(1)}, bf16[128,2048]{1,0:T(8,128)(2,1)S(1)}, u32[]{:S(2)}, u32[]{:S(2)}) collective-permute-start(bf16[128,2048]{1,0:T(8,128)(2,1)S(1)} %add_convert_fusion.4), channel_id=1, source_target_pairs={{0,8},{8,16},{16,24},{24,0},{1,9},{9,17},{17,25},{25,1},{2,10},{10... | collective-permute-start | bytes 1572872 | tf_op jit(solution)/shard_map/ppermute | solution.py:152
  782.2 23.3 %collective-permute-start.88 = (bf16[64,1280]{1,0:T(8,128)(2,1)S(1)}, bf16[64,1280]{1,0:T(8,128)(2,1)S(1)}, u32[]{:S(2)}, u32[]{:S(2)}) collective-permute-start(bf16[64,1280]{1,0:T(8,128)(2,1)S(1)} %get-tuple-element.226), channel_id=1, source_target_pairs={{0,1},{1,0},{4,5},{5,4},{2,3},{3,2},{6,7},{7,6},{8,9},{9,8},{12,13... | collective-permute-start | bytes 491528 | tf_op jit(solution)/shard_map/ppermute | solution.py:101
  782.4 23.0 %collective-permute-start.90 = (bf16[64,1280]{1,0:T(8,128)(2,1)S(1)}, bf16[64,1280]{1,0:T(8,128)(2,1)S(1)}, u32[]{:S(2)}, u32[]{:S(2)}) collective-permute-start(bf16[64,1280]{1,0:T(8,128)(2,1)S(1)} %get-tuple-element.227), channel_id=1, source_target_pairs={{0,5},{1,4},{4,1},{5,0},{2,7},{3,6},{6,3},{7,2},{8,13},{9,12},{12,... | collective-permute-start | bytes 491528 | tf_op jit(solution)/shard_map/ppermute | solution.py:101
  785.0 20.4 %collective-permute-start.89 = (bf16[64,1280]{1,0:T(8,128)(2,1)S(1)}, bf16[64,1280]{1,0:T(8,128)(2,1)S(1)}, u32[]{:S(2)}, u32[]{:S(2)}) collective-permute-start(bf16[64,1280]{1,0:T(8,128)(2,1)S(1)} %get-tuple-element.228), channel_id=1, source_target_pairs={{0,4},{1,5},{4,0},{5,1},{2,6},{3,7},{6,2},{7,3},{8,12},{9,13},{12,... | collective-permute-start | bytes 491528 | tf_op jit(solution)/shard_map/ppermute | solution.py:101
  (211 other events, 3185.4 us)

commit v4 on v3

--- a/solution.py
+++ b/solution.py
@@ -137,15 +137,35 @@
     return total
 
 
-def ring_gather(chunk, axis, count):
-    here = lax.axis_index(axis)
-    zeros = (0,) * chunk.ndim
-    full = jnp.zeros((count,) + chunk.shape, chunk.dtype)
-    full = lax.dynamic_update_slice(full, chunk[None], (here,) + zeros)
-    for step in range(1, count):
-        chunk = lax.ppermute(chunk, axis, [(i, (i + 1) % count) for i in range(count)])
+def far_all(value, count, first=None):
+    ahead = count // 2
+    found = [value] + [None] * (count - 1)
+    found[1] = far_shift(value, 1, count)
+    if count > 2:
+        found[count - 1] = far_shift(value, -1, count)
+    for step in range(2, ahead + 1):
+        found[step] = far_shift(found[step - 1], 1, count)
+    for step in range(count - 2, ahead, -1):
+        found[step] = far_shift(found[step + 1], -1, count)
+    return found
+
+
+def far_stack(found):
+    count = len(found)
+    here = lax.axis_index(FAR_AXIS)
+    zeros = (0,) * found[0].ndim
+    full = jnp.zeros((count,) + found[0].shape, found[0].dtype)
+    for step, chunk in enumerate(found):
         full = lax.dynamic_update_slice(full, chunk[None], (lax.rem(here + count - step, count),) + zeros)
     return full
+
+
+def tie(*values):
+    return lax.optimization_barrier(values)
+
+
+def far_shift(value, step, count):
+    return lax.ppermute(value, FAR_AXIS, [(i, (i + step) % count) for i in range(count)])
 
 
 def far_next(value, count):
@@ -167,13 +187,6 @@
     other = swap(blocks[1], CORE_AXIS)
     parts = [jnp.stack([blocks[0, step], other[step]]) for step in range(4)]
     return jnp.stack([parts[0]] + [quad_xor(parts[step], step) for step in range(1, 4)])
-
-
-def ring_reduce(parts, count):
-    total = parts[1].astype(BF)
-    for step in range(2, count):
-        total = (far_next(total, count).astype(F32) + parts[step]).astype(BF)
-    return far_next(total, count).astype(F32) + parts[0]
 
 
 def expert_grad_kernel(count, *refs):
@@ -213,12 +226,144 @@
         out_shape=jax.ShapeDtypeStruct((D, 3 * FF), F32),
         compiler_params=pltpu.CompilerParams(vmem_limit_bytes=48 << 20),
         cost_estimate=pl.CostEstimate(
-            flops=2 * total_rows * D * 3 * FF,
-            bytes_accessed=total_rows * D * 4 + D * 3 * FF * 4,
+            flops=1 << 20,
+            bytes_accessed=1 << 20,
             transcendentals=0,
         ),
         name="expert_grads",
     )(*in_rows, *gu_grads, *grad_rows, *actives)
+
+
+def head_normed(raw, gain_ref):
+    scale = lax.rsqrt(jnp.mean(raw * raw, axis=-1, keepdims=True) + EPS)
+    normal = raw * scale
+    return (normal, scale, normal * gain_ref[...])
+
+
+def turned(values, cos_ref, sin_ref):
+    return values * cos_ref[...] + pltpu.roll(values, HEAD_DIM // 2, 1) * sin_ref[...]
+
+
+def turned_back(values, cos_ref, sin_ref):
+    return values * cos_ref[...] + pltpu.roll(values * sin_ref[...], HEAD_DIM // 2, 1)
+
+
+def head_probs(query, key, row_ref, start_ref, key_row_ref):
+    scores = mm_nt(query, key) * HEAD_DIM ** (-0.5)
+    allowed = (key_row_ref[0] <= row_ref[0]) & (key_row_ref[0] >= start_ref[0])
+    scores = jnp.where(allowed, scores, -1e30)
+    exped = jnp.exp(scores - jnp.max(scores, axis=-1, keepdims=True))
+    return exped / jnp.sum(exped, axis=-1, keepdims=True)
+
+
+def attend_kernel(
+    query_ref, key_ref, value_ref, cos_ref, sin_ref, qgain_ref, kgain_ref,
+    row_ref, start_ref, key_row_ref, mixed_ref, key_low, value_low,
+):
+    @pl.when(pl.program_id(1) == 0)
+    def _():
+        key_low[...] = turned(head_normed(key_ref[...], kgain_ref)[2], cos_ref, sin_ref).astype(BF)
+        value_low[...] = value_ref[...].astype(BF)
+
+    query = turned(head_normed(query_ref[...], qgain_ref)[2], cos_ref, sin_ref).astype(BF)
+    probs = head_probs(query, key_low[...], row_ref, start_ref, key_row_ref)
+    mixed_ref[...] = mm(probs.astype(BF), value_low[...]).astype(BF)
+
+
+def attend_back_kernel(
+    query_ref, key_ref, value_ref, cos_ref, sin_ref, qgain_ref, kgain_ref,
+    row_ref, start_ref, key_row_ref, grad_ref,
+    query_out, key_out, value_out, qgain_out, kgain_out,
+    key_low, value_low, key_total, value_total,
+):
+    group, head = pl.program_id(0), pl.program_id(1)
+    score_scale = HEAD_DIM ** (-0.5)
+
+    @pl.when((group == 0) & (head == 0))
+    def _():
+        qgain_out[...] = jnp.zeros_like(qgain_out)
+        kgain_out[...] = jnp.zeros_like(kgain_out)
+
+    @pl.when(head == 0)
+    def _():
+        key_low[...] = turned(head_normed(key_ref[...], kgain_ref)[2], cos_ref, sin_ref).astype(BF)
+        value_low[...] = value_ref[...].astype(BF)
+        key_total[...] = jnp.zeros_like(key_total)
+        value_total[...] = jnp.zeros_like(value_total)
+
+    def raw_grad(grad, normal, scale, gain_ref, gain_out):
+        grad = turned_back(grad, cos_ref, sin_ref)
+        gain_out[...] += jnp.sum(grad * normal, axis=0, keepdims=True)
+        grad = grad * gain_ref[...]
+        return scale * (grad - normal * jnp.mean(normal * grad, axis=-1, keepdims=True))
+
+    normal, scale, gained = head_normed(query_ref[...], qgain_ref)
+    query = turned(gained, cos_ref, sin_ref).astype(BF)
+    probs = head_probs(query, key_low[...], row_ref, start_ref, key_row_ref)
+    grad = grad_ref[...]
+    value_total[...] += mm_tn(probs.astype(BF), grad)
+    prob_grad = mm_nt(grad, value_low[...])
+    score_grad = (probs * (prob_grad - jnp.sum(probs * prob_grad, axis=-1, keepdims=True))).astype(BF)
+    key_total[...] += mm_tn(score_grad, query) * score_scale
+    query_grad = mm(score_grad, key_low[...]) * score_scale
+    query_out[...] = raw_grad(query_grad, normal, scale, qgain_ref, qgain_out).astype(BF)
+
+    @pl.when(head == pl.num_programs(1) - 1)
+    def _():
+        key_normal, key_scale, _ = head_normed(key_ref[...], kgain_ref)
+        key_out[...] = raw_grad(key_total[...], key_normal, key_scale, kgain_ref, kgain_out).astype(BF)
+        value_out[...] = value_total[...].astype(BF)
+
+
+def attend_specs(heads):
+    head = pl.BlockSpec((ROW, HEAD_DIM), lambda b, h: (b, h))
+    whole = pl.BlockSpec((ROW, HEAD_DIM), lambda b, h: (b, 0))
+    gain = pl.BlockSpec((1, HEAD_DIM), lambda b, h: (0, 0))
+    column = pl.BlockSpec((1, ROW, 1), lambda b, h: (b, 0, 0))
+    specs = [
+        head,
+        pl.BlockSpec((ROW, HEAD_DIM), lambda b, h: (b, heads)),
+        pl.BlockSpec((ROW, HEAD_DIM), lambda b, h: (b, heads + 1)),
+        whole, whole, gain, gain, column, column,
+        pl.BlockSpec((1, 1, ROW), lambda b, h: (b, 0, 0)),
+    ]
+    return (specs, head, whole, gain)
+
+
+def attend(projected, shared, heads):
+    specs, head, _, _ = attend_specs(heads)
+    rows = projected.shape[0]
+    return pl.pallas_call(
+        attend_kernel,
+        grid=(rows // ROW, heads),
+        in_specs=specs,
+        out_specs=head,
+        out_shape=jax.ShapeDtypeStruct((rows, heads * HEAD_DIM), BF),
+        scratch_shapes=[pltpu.VMEM((ROW, HEAD_DIM), BF)] * 2,
+        cost_estimate=pl.CostEstimate(flops=1 << 20, bytes_accessed=1 << 20, transcendentals=0),
+        name="attend",
+    )(projected, projected, projected, *shared)
+
+
+def attend_back(projected, shared, grad, heads):
+    specs, head, whole, gain = attend_specs(heads)
+    rows = projected.shape[0]
+    return pl.pallas_call(
+        attend_back_kernel,
+        grid=(rows // ROW, heads),
+        in_specs=specs + [head],
+        out_specs=[head, whole, whole, gain, gain],
+        out_shape=[
+            jax.ShapeDtypeStruct((rows, heads * HEAD_DIM), BF),
+            jax.ShapeDtypeStruct((rows, HEAD_DIM), BF),
+            jax.ShapeDtypeStruct((rows, HEAD_DIM), BF),
+            jax.ShapeDtypeStruct((1, HEAD_DIM), F32),
+            jax.ShapeDtypeStruct((1, HEAD_DIM), F32),
+        ],
+        scratch_shapes=[pltpu.VMEM((ROW, HEAD_DIM), BF)] * 2 + [pltpu.VMEM((ROW, HEAD_DIM), F32)] * 2,
+        cost_estimate=pl.CostEstimate(flops=1 << 20, bytes_accessed=1 << 20, transcendentals=0),
+        name="attend_back",
+    )(projected, projected, projected, *shared, grad)
 
 
 def shards(tokens, cotangent, w_qkv, w_out, w_router, norm_gains, w_expert, lengths, deal, routes):
@@ -239,6 +384,19 @@
     gain_rows = norm_gains.shape[0]
     score_scale = HEAD_DIM ** (-0.5)
 
+    wide = jnp.concatenate(
+        [
+            w_qkv[:, :QDIM].reshape(qkv_rows, KV_HEADS, qcols),
+            w_qkv[:, QDIM : QDIM + KVDIM].reshape(qkv_rows, KV_HEADS, HEAD_DIM),
+            w_qkv[:, QDIM + KVDIM :].reshape(qkv_rows, KV_HEADS, HEAD_DIM),
+        ],
+        axis=2,
+    ).transpose(1, 0, 2)
+    core_rows = KV_HEADS * qkv_rows
+    half_rows = 2 * qkv_rows
+    qkv_far = far_all(quad_swap(wide).reshape(core_rows, width), far_count)
+    tokens, cotangent, qkv_far[1] = tie(tokens, cotangent, qkv_far[1])
+
     tokens_both = quad_gather(tokens).reshape(2, ROW, D)
     table = jnp.concatenate([deal, jnp.pad(lengths, ((0, 0), (0, LANES - NSEG)))], axis=1)
     table_both = jnp.concatenate(pair_order(table, swap(table, NEAR_AXIS), NEAR_AXIS), axis=0)
@@ -273,7 +431,7 @@
     slab_index = (near_index * CORES + core_index) * 2 + seq_index
     out_order = jnp.array([0, 2, 1, 3, 4, 6, 5, 7], jnp.int32)
     in_order = jnp.array([0, 1, 4, 5, 2, 3, 6, 7], jnp.int32)
-    place_far = ring_gather(place.T.astype(BF), FAR_AXIS, far_count)
+    place_far = far_stack(far_all(place.T.astype(BF), far_count))
     place_slab = jnp.take(
         place_far, far_index * slab + lax.bitwise_xor(out_order, slab_index), axis=1
     ).astype(jnp.int32)
@@ -325,36 +483,19 @@
     cot_pair = jnp.concatenate(pair_order(cotangent, swap(cotangent, SEQ_AXIS), SEQ_AXIS), axis=0)
     cot_low = mm(hot_half, cot_pair).astype(BF)
     cot_rows = cot_low.astype(F32)
-    wide = jnp.concatenate(
-        [
-            w_qkv[:, :QDIM].reshape(qkv_rows, KV_HEADS, qcols),
-            w_qkv[:, QDIM : QDIM + KVDIM].reshape(qkv_rows, KV_HEADS, HEAD_DIM),
-            w_qkv[:, QDIM + KVDIM :].reshape(qkv_rows, KV_HEADS, HEAD_DIM),
-        ],
-        axis=2,
-    ).transpose(1, 0, 2)
-    core_rows = KV_HEADS * qkv_rows
-    half_rows = 2 * qkv_rows
-    qkv_own = ring_gather(quad_swap(wide).reshape(core_rows, width), FAR_AXIS, far_count)
+    qkv_own = far_stack(qkv_far)
+    cot_low, qkv_own = tie(cot_low, qkv_own)
     qkv_own = qkv_own.reshape(far_count * NEAR, half_rows, width)
     qkv_mine = jnp.stack(pair_order(qkv_own, swap(qkv_own, CORE_AXIS), CORE_AXIS), axis=1).reshape(
         D, width
     )
 
-    w_late, cot_late, _ = lax.optimization_barrier((w_out, cot_low, qkv_own))
-    cot_far = [cot_late]
-    for step in range(1, far_count):
-        cot_far.append(far_next(cot_far[-1], far_count))
-    cot_sent = jnp.stack(
-        [to_blocks(mm(hot, rows).astype(BF)) for hot, rows in zip(chunk_slots, cot_far)], axis=2
-    )
-    cot_back = slab_out(cot_sent.reshape(4, 2, far_count * capacity, D)).reshape(
-        slab, far_count, capacity, D
-    )
-    out_slabs = ring_gather(w_late, FAR_AXIS, far_count).reshape(
+    out_slabs = far_stack(far_all(w_out, far_count)).reshape(
         KV_HEADS, far_count // KV_HEADS * out_rows, D
     )
     far_part = far_count // KV_HEADS
+    cot_low, out_slabs = tie(cot_low, out_slabs)
+    cot_far = far_all(cot_low, far_count)
     out_own = quad_swap(out_slabs).reshape(NEAR * 2, far_part, out_rows, D)
     out_own = out_own.transpose(1, 0, 2, 3).reshape(far_part * NEAR, 2 * out_rows, D)
     out_mine = jnp.stack(pair_order(out_own, swap(out_own, CORE_AXIS), CORE_AXIS), axis=1).reshape(
@@ -370,38 +511,21 @@
     normed_low = rms_norm(x_both.reshape(2 * ROW, D), gain_attn).astype(BF)
     projected = mm(normed_low, qkv_mine)
     cosine, sine_part = tables(pos_both.reshape(2 * ROW), HEAD_DIM)
-
-    def head_piece(proj_qk, scale_query, scale_key):
-        query_raw = proj_qk[:, :qcols].reshape(2 * ROW, per_group, HEAD_DIM)
-        key_raw = proj_qk[:, qcols:].reshape(2 * ROW, 1, HEAD_DIM)
-        return (
-            rotary(rms_norm(query_raw, scale_query), cosine, sine_part),
-            rotary(rms_norm(key_raw, scale_key), cosine, sine_part),
-        )
-
-    (queries, key_rot), head_back = jax.vjp(
-        head_piece, projected[:, : qcols + HEAD_DIM], gain_query, gain_key
-    )
-    query_heads = queries.astype(BF).reshape(2, ROW, per_group, HEAD_DIM)
-    key_heads = key_rot.astype(BF).reshape(2, ROW, HEAD_DIM)
-    value_heads = projected[:, qcols + HEAD_DIM :].astype(BF).reshape(2, ROW, HEAD_DIM)
-    allowed = (seg_both[:, :, None] == seg_both[:, None, :]) & (
-        pos_both[:, None, :] <= pos_both[:, :, None]
-    )
-    scores = (
-        jnp.einsum("bqgd,bsd->bgqs", query_heads, key_heads, preferred_element_type=F32) * score_scale
-    )
-    scores = jnp.where(allowed[:, None], scores, -1e30)
-    prob_full = jax.nn.softmax(scores, axis=-1)
-    prob_low = prob_full.astype(BF)
-    mixed_heads = jnp.einsum("bgqs,bsd->bqgd", prob_low, value_heads, preferred_element_type=F32)
-    mixed_low = mixed_heads.astype(BF).reshape(2 * ROW, qcols)
+    shared = (
+        jnp.concatenate([cosine, cosine], axis=1),
+        jnp.concatenate([-sine_part, sine_part], axis=1),
+        gain_query[None],
+        gain_key[None],
+        deal_both[:, :, None],
+        (deal_both - pos_both)[:, :, None],
+        deal_both[:, None, :],
+    )
+    mixed_low = attend(projected, shared, per_group)
     out_partial = mm(mixed_low, out_mine).astype(BF)
     residual = x_rows + quad_sum(out_partial.reshape(4, TOK_DEV, D))
 
     normed_two, ffn_back = jax.vjp(rms_norm, residual, gain_ffn)
     ffn_in = normed_two.astype(BF)
-    ffn_in, cot_back = lax.optimization_barrier((ffn_in, cot_back))
     logits = mm(ffn_in, router_full)
     logits = jnp.where(chosen > 0.5, logits, -1e30)
     gate_probs = jax.nn.softmax(logits, axis=-1)
@@ -409,13 +533,30 @@
 
     expert_weight = w_expert[0]
     expert_here = far_index * slab + slab_index
-    in_rows, gu_grads, grad_rows, actives, gated_outs, slot_dots, partials = ([] for _ in range(7))
-    far_rows = ffn_in
+    in_rows, gu_grads, grad_rows, actives, slot_dots, in_grads, partials = ([] for _ in range(7))
+    far_rows = [ffn_in]
+    for step in range(1, far_count):
+        far_rows.append(far_next(far_rows[-1], far_count))
+
+    def gather(step, source):
+        return mm(chunk_slots[step], jnp.concatenate([source, cot_far[step]], axis=1)).astype(BF)
+
+    sent = gather(0, ffn_in)
+
+    def combine(step):
+        back = slab_back(in_grads[step].reshape(2, 4, capacity, 2 * D)).reshape(slab * capacity, 2 * D)
+        if step + 1 < far_count:
+            back, actives[step + 1] = tie(back, actives[step + 1])
+        return mm_tn(chunk_slots[step], back)
+
     for step in range(far_count):
-        hot = chunk_slots[step]
-        in_chunk = slab_out(to_blocks(mm(hot, far_rows).astype(BF))).reshape(slab * capacity, D)
-        if step < far_count - 1:
-            far_rows = far_next(far_rows, far_count)
+        arrived = slab_out(to_blocks(sent)).reshape(slab * capacity, 2 * D)
+        in_chunk, cot_chunk = arrived[:, :D], arrived[:, D:]
+        if step + 1 < far_count:
+            source = far_rows[step + 1]
+            if step > 0:
+                source, gu_grads[step - 1] = tie(source, gu_grads[step - 1])
+            sent = gather(step + 1, source)
         mask = mask_back[step]
         slot_logits = jnp.where(mask > 0.5, mm(in_chunk, router_full), -1e30)
         slot_probs = jnp.where(mask > 0.5, jax.nn.softmax(slot_logits, axis=-1), 0.0)
@@ -428,10 +569,10 @@
         sig_gate = jax.nn.sigmoid(gate_pre)
         silu_val = gate_pre * sig_gate
         active = (silu_val * up_pre).astype(BF)
-        expert_out = mm_nt(active, expert_weight[:, 2 * FF :]).astype(BF).astype(F32)
-        cot_float = cot_back[:, step].reshape(slab * capacity, D).astype(F32)
-        slot_dots.append(jnp.sum(cot_float * expert_out, axis=1))
-        gated_outs.append((gate_slot * expert_out).astype(BF).reshape(2, 4, capacity, D))
+        expert_out = mm_nt(active, expert_weight[:, 2 * FF :]).astype(BF)
+        cot_float = cot_chunk.astype(F32)
+        slot_dots.append(jnp.sum(cot_float * expert_out.astype(F32), axis=1))
+        gated_out = (gate_slot * expert_out.astype(F32)).astype(BF)
         grad_chunk = (gate_slot * cot_float).astype(BF)
         act_grad = mm(grad_chunk, expert_weight[:, 2 * FF :])
         silu_slope = sig_gate * (1.0 + gate_pre * (1.0 - sig_gate))
@@ -439,16 +580,26 @@
             [act_grad * up_pre * silu_slope, act_grad * silu_val], axis=1
         ).astype(BF)
         in_grad = mm_nt(gu_grad, expert_weight[:, : 2 * FF]).astype(BF)
-        back = slab_back(in_grad.reshape(2, 4, capacity, D)).reshape(slab * capacity, D)
-        partials.append(mm_tn(hot, back))
+        in_grads.append(jnp.concatenate([in_grad, gated_out], axis=1))
         in_rows.append(in_chunk)
         gu_grads.append(gu_grad)
         grad_rows.append(grad_chunk)
         actives.append(active)
+        if step > 0:
+            partials.append(combine(step - 1))
+    partials.append(combine(far_count - 1))
+    from_experts = partials[0][:, :D]
+    for step in range(1, far_count):
+        from_experts = from_experts + far_shift(
+            partials[step][:, :D].astype(BF), -step, far_count
+        ).astype(F32)
+    out_parts = [part[:, D:] for part in partials]
+    from_experts, *out_parts = tie(from_experts, *out_parts)
+    out_sum = out_parts[0]
+    for step in range(1, far_count):
+        out_sum = out_sum + far_shift(out_parts[step].astype(BF), -step, far_count).astype(F32)
     dot_sent = jnp.take(jnp.stack(slot_dots).reshape(device_count, capacity), found_at, axis=0)
     dot_back = exchange(dot_sent[:, None, :], ALL_AXES).reshape(experts_all, capacity)
-    from_experts = ring_reduce(partials, far_count)
-    grad_expert = expert_grads(in_rows, gu_grads, grad_rows, actives)[None]
 
     gate_grad = jnp.sum(jnp.where(slot_hot, dot_back[:, :, None], 0.0), axis=1).T
     mean_term = jnp.sum(gate_probs * gate_grad, axis=1, keepdims=True)
@@ -458,33 +609,21 @@
     resid_part, gain_ffn_grad = ffn_back(ffn_in_grad)
     resid_low = (cot_rows + resid_part).astype(BF)
 
-    gated_sent = jnp.stack(gated_outs, axis=2).reshape(2, 4, far_count * capacity, D)
-    gated_sent, resid_low = lax.optimization_barrier((gated_sent, resid_low))
-    gated_back = slab_back(gated_sent).reshape(slab, far_count, capacity, D)
-    out_sum = ring_reduce(
-        [
-            mm_tn(hot, gated_back[:, step].reshape(slab * capacity, D))
-            for step, hot in enumerate(chunk_slots)
-        ],
-        far_count,
-    )
-    final_rows = (residual + out_sum).astype(BF)
-    final_pair = jnp.concatenate(
-        pair_order(final_rows, swap(final_rows, SEQ_AXIS), SEQ_AXIS), axis=0
-    )
-    layer_out = mm_tn(back_half, final_pair).astype(BF)
-
-    resid_both = quad_gather(resid_low).reshape(2 * ROW, D)
+    in_rows[0], resid_low = tie(in_rows[0], resid_low)
+    grad_expert = expert_grads(in_rows, gu_grads, grad_rows, actives)[None]
+
+    resid_both, grad_expert = tie(quad_gather(resid_low), grad_expert)
+    resid_both = resid_both.reshape(2 * ROW, D)
 
     def core_sum(values):
         own, other = pair_order(values[:, 0], values[:, 1], CORE_AXIS)
         return own.astype(F32) + swap(other, CORE_AXIS).astype(F32)
 
+    out_grad = mm_tn(mixed_low, resid_both).astype(BF)
+    resid_both, out_grad = tie(resid_both, out_grad)
     mixed_grad = mm_nt(resid_both, out_mine).astype(BF)
-    out_grad = mm_tn(mixed_low, resid_both).astype(BF)
-    mixed_grad, out_grad = lax.optimization_barrier((mixed_grad, out_grad))
-    grad_heads = mixed_grad.reshape(2, ROW, per_group, HEAD_DIM)
     out_grad = core_sum(out_grad.reshape(far_part * NEAR, CORES, 2 * out_rows, D))
+    mixed_grad, out_grad = tie(mixed_grad, out_grad)
     out_grad = (
         out_grad.astype(BF)
         .reshape(far_part, NEAR * 2, out_rows, D)
@@ -492,32 +631,26 @@
         .reshape(NEAR * 2, far_part * out_rows, D)
     )
     out_grad = quad_swap(out_grad).reshape(far_count, out_rows, D)
+    query_grad, key_grad, value_grad, query_gain_grad, key_gain_grad = attend_back(
+        projected, shared, mixed_grad, per_group
+    )
+    query_grad, out_grad, out_sum = tie(query_grad, out_grad, out_sum)
     out_share = far_sum(out_grad, far_count)
-
-    value_grad = jnp.einsum("bgqs,bqgd->bsd", prob_low, grad_heads, preferred_element_type=F32)
-    prob_grad = jnp.einsum("bqgd,bsd->bgqs", grad_heads, value_heads, preferred_element_type=F32)
-    score_grad = (
-        prob_full * (prob_grad - jnp.sum(prob_full * prob_grad, axis=-1, keepdims=True))
-    ).astype(BF)
-    query_grad = (
-        jnp.einsum("bgqs,bsd->bqgd", score_grad, key_heads, preferred_element_type=F32) * score_scale
-    )
-    key_grad = (
-        jnp.einsum("bgqs,bqgd->bsd", score_grad, query_heads, preferred_element_type=F32) * score_scale
-    )
-    qk_grad, query_gain_grad, key_gain_grad = head_back(
-        (
-            query_grad.reshape(2 * ROW, per_group, HEAD_DIM),
-            key_grad.reshape(2 * ROW, 1, HEAD_DIM),
-        )
-    )
-    proj_grad = jnp.concatenate([qk_grad, value_grad.reshape(2 * ROW, HEAD_DIM)], axis=1).astype(BF)
+    proj_grad = jnp.concatenate([query_grad, key_grad, value_grad], axis=1)
+    final_rows = (residual + out_sum).astype(BF)
+    final_pair = jnp.concatenate(
+        pair_order(final_rows, swap(final_rows, SEQ_AXIS), SEQ_AXIS), axis=0
+    )
+    layer_out = mm_tn(back_half, final_pair).astype(BF)
+
     back_grad = lax.dot_general(
         dealt_hot,
         proj_grad.reshape(2, ROW, width),
         (((1,), (1,)), ((0,), (0,))),
         preferred_element_type=F32,
     ).astype(BF).reshape(2 * ROW, width)
+    qkv_grad = mm_tn(normed_low, proj_grad).astype(BF)
+    back_grad, qkv_grad = tie(back_grad, qkv_grad)
     normed_partial = mm_nt(back_grad, qkv_mine).astype(BF)
     normed_grad = quad_sum(normed_partial.reshape(4, TOK_DEV, D))
     _, attn_back = jax.vjp(rms_norm, tokens.astype(F32), gain_attn)
@@ -525,7 +658,6 @@
     resid_group = lax.dynamic_slice_in_dim(resid_both, near_index * ROW, ROW, axis=0)
     grad_tokens = (mm_tn(back_half, resid_group) + input_part).astype(BF)
 
-    qkv_grad = mm_tn(normed_low, proj_grad).astype(BF)
     qkv_grad = core_sum(qkv_grad.reshape(far_count * NEAR, CORES, half_rows, width))
     qkv_grad = far_sum(qkv_grad.astype(BF).reshape(far_count, core_rows, width), far_count)
     qkv_grad = quad_swap(qkv_grad.astype(BF).reshape(KV_HEADS, qkv_rows, width))
@@ -539,7 +671,9 @@
         axis=1,
     )
 
-    gains_grad = jnp.concatenate([gain_attn_grad, gain_ffn_grad, query_gain_grad, key_gain_grad])
+    gains_grad = jnp.concatenate(
+        [gain_attn_grad, gain_ffn_grad, query_gain_grad[0], key_gain_grad[0]]
+    )
     share_rows = -(-small_size // (8 * LANES)) * 8
     small_grad = jnp.concatenate(
         [router_grad.reshape(device_count, router_size), gains_grad.reshape(device_count, gain_rows)],

time: 846 us -> 737 us (0.87)
  waiting for transfers between devices: 464 us -> 354 us
  Pallas kernels: 18.6 us -> 58.7 us
  local copies, waits for them, and re-layouts: 68.1 us -> 49.1 us
  other arithmetic: 79.9 us -> 64.7 us
  matrix products: 74.5 us -> 65.7 us
    ppermute x12 -> x3, waiting for transfers between devices: 63.6 us -> 15.6 us  [far_next(): lax.ppermute(value, FAR_AXIS, [(i, (i + 1) % count) for i in range(count)])]
    pallas_call x0 -> x2, Pallas kernels: none -> 40.3 us  [the longest x1 23.8 us: attend_back(): pl.pallas_call(attend_back_kernel, grid=(rows // ROW, heads), in_specs=sp...]
    ppermute x17 -> x15, waiting for transfers between devices: 32.1 us -> 0.59 us  [swap(): return lax.ppermute(value, axis, [(0, 1), (1, 0)])]
    ppermute x30 -> x24, waiting for transfers between devices: 133 us -> 102 us  [quad_xor(): return lax.ppermute(value, HEAD_AXES, [(i, i ^ step) for i in range(4)])]
    ppermute x9 -> x18, starting transfers between devices: 4.86 us -> 28.7 us  [far_shift(): lax.ppermute(value, FAR_AXIS, [(i, (i + step) % count) for i in range(cou...]
    ppermute x9 -> x18, waiting for transfers between devices: 72.5 us -> 89.3 us  [far_shift(): lax.ppermute(value, FAR_AXIS, [(i, (i + step) % count) for i in range(cou...]
    ppermute x6, waiting for transfers between devices: 17.2 us -> 4.79 us  [quad_gather(): lax.ppermute(value, HEAD_AXES, [(i, i ^ step) for i in range(4)])]
    ppermute x6, starting transfers between devices: 31.1 us -> 19.5 us  [far_sum(): lax.ppermute(block, FAR_AXIS, [(i, (i + step) % count) for i in range(cou...]
  transfers between devices with their start and end apart: 101 -> 93, of which waited for: 56 -> 43; matrix products, arithmetic and copies ran while one was open for 22% -> 21% of each run, Pallas kernels for 2% -> 8%
where the time goes in v4:
time: 737 us; the launch traced here: 727 us
  waiting for transfers between devices  354 us (48%)
  starting transfers between devices  131 us (18%)
  matrix products  65.7 us (9%)
  other arithmetic  64.7 us (9%)
  Pallas kernels  58.7 us (8%)
  local copies, waits for them, and re-layouts  49.1 us (7%)
    ppermute x24, waiting for transfers between devices, quad_xor(): return lax.ppermute(value, HEAD_AXES, [(i, i ^ step) for i in range(4)])  102 us
    ppermute x18, waiting for transfers between devices, far_shift(): lax.ppermute(value, FAR_AXIS, [(i, (i + step) % count) for i in range(cou...  89.3 us
    ppermute x18, waiting for transfers between devices, quad_send(): return lax.ppermute(block, HEAD_AXES, [(i, i ^ step) for i in range(4)])  73.6 us
    ppermute x6, waiting for transfers between devices, far_sum(): lax.ppermute(block, FAR_AXIS, [(i, (i + step) % count) for i in range(cou...  67.9 us
    dot_general x43, matrix products, dot(): lax.dot_general(left, right, (dims, ((), ())), preferred_element_type=F32)  64.4 us
    ppermute x24, starting transfers between devices, quad_xor(): return lax.ppermute(value, HEAD_AXES, [(i, i ^ step) for i in range(4)])  30.1 us
    ppermute x18, starting transfers between devices, far_shift(): lax.ppermute(value, FAR_AXIS, [(i, (i + step) % count) for i in range(cou...  28.7 us
    pallas_call x1, Pallas kernels, attend_back(): pl.pallas_call(attend_back_kernel, grid=(rows // ROW, heads), in_specs=sp...  23.8 us
  transfers between devices with their start and end apart: 93, of which 43 were waited for; matrix products, arithmetic and copies ran while one was open for 21% of the time, Pallas kernels for 8%

profile of v4, /device:TPU:0, one launch (start us, length us, event | category | flops | bytes accessed | tf_op | source)
XLA Modules:
  0.0 727.0 jit_solution(11983334869045144423)
XLA Ops:
  0.6 5.1 collective-permute-start.14
  20.7 3.9 collective-permute-start.24
  26.4 4.2 all-to-all-start
  39.7 2.4 collective-permute-start.3
  42.9 3.8 collective-permute-done.2
  46.9 2.0 collective-permute-start.10
  52.5 27.9 %collective-permute-done.4 = bf16[256,1280]{1,0:T(8,128)(2,1)S(1)} collective-permute-done((bf16[256,1280]{1,0:T(8,128)(2,1)S(1)}, bf16[256,1280]{1,0:T(8,128)(2,1)S(1)}, u32[]{:S(2)}, u32[]{:S(2)}) %collective-permute-start.4) | collective-permute-done | bytes 655392 | tf_op jit(solution)/shard_map/ppermute | solution.py:168
  82.3 9.3 %collective-permute-done.13 = bf16[128,2048]{1,0:T(8,128)(2,1)S(1)} collective-permute-done((bf16[128,2048]{1,0:T(8,128)(2,1)}, bf16[128,2048]{1,0:T(8,128)(2,1)S(1)}, u32[]{:S(2)}, u32[]{:S(2)}) %collective-permute-start.13) | collective-permute-done | bytes 524320 | tf_op jit(solution)/shard_map/ppermute | solution.py:168
  95.7 8.2 %collective-permute-done.9 = bf16[256,1280]{1,0:T(8,128)(2,1)S(1)} collective-permute-done((bf16[256,1280]{1,0:T(8,128)(2,1)S(1)}, bf16[256,1280]{1,0:T(8,128)(2,1)S(1)}, u32[]{:S(2)}, u32[]{:S(2)}) %collective-permute-start.9) | collective-permute-done | bytes 655392 | tf_op jit(solution)/shard_map/ppermute | solution.py:168
  104.0 2.6 dynamic-slice_bitcast_fusion.17
  111.1 2.0 collective-permute-start.7
  113.1 8.7 %collective-permute-done.15 = bf16[128,2048]{1,0:T(8,128)(2,1)} collective-permute-done((bf16[128,2048]{1,0:T(8,128)(2,1)}, bf16[128,2048]{1,0:T(8,128)(2,1)}, u32[]{:S(2)}, u32[]{:S(2)}) %collective-permute-start.15) | collective-permute-done | bytes 524320 | tf_op jit(solution)/shard_map/ppermute | solution.py:101
  121.9 11.2 %collective-permute-done.17 = bf16[128,2048]{1,0:T(8,128)(2,1)} collective-permute-done((bf16[128,2048]{1,0:T(8,128)(2,1)}, bf16[128,2048]{1,0:T(8,128)(2,1)}, u32[]{:S(2)}, u32[]{:S(2)}) %collective-permute-start.17) | collective-permute-done | bytes 524320 | tf_op jit(solution)/shard_map/ppermute | solution.py:101
  133.1 13.2 %collective-permute-done.16 = bf16[128,2048]{1,0:T(8,128)(2,1)} collective-permute-done((bf16[128,2048]{1,0:T(8,128)(2,1)}, bf16[128,2048]{1,0:T(8,128)(2,1)}, u32[]{:S(2)}, u32[]{:S(2)}) %collective-permute-start.16) | collective-permute-done | bytes 524320 | tf_op jit(solution)/shard_map/ppermute | solution.py:101
  149.3 4.8 collective-permute-done.6
  159.2 2.4 pad_maximum_fusion.1
  162.4 4.4 fusion.177.query_ref.key_ref.value_ref
  166.8 16.4 %attend.1 = bf16[512,1024]{1,0:T(8,128)(2,1)} custom-call(f32[512,1280]{1,0:T(8,128)} %fusion.177.query_ref.key_ref.value_ref, f32[512,1280]{1,0:T(8,128)} %fusion.177.query_ref.key_ref.value_ref, f32[512,1280]{1,0:T(8,128)} %fusion.177.query_ref.key_ref.value_ref, f32[512,128]{1,0:T(8,128)} %get-tuple-element.342.cos_ref, ...), custom_call_target="tpu_custom_call" | custom-call | flops 1048576 | bytes 1048576 | tf_op jit(solution)/shard_map/attend/pallas_call | solution.py:336
  183.2 4.8 convolution_convert_fusion.6
  196.3 2.8 collective-permute-start.55
  199.1 5.4 collective-permute-done.19
  204.5 7.0 collective-permute-done.21
  212.8 2.1 multiply_reduce_fusion.3
  215.2 3.2 collective-permute-start.33
  220.4 2.0 collective-permute-start.27
  224.0 7.9 %collective-permute-done.33 = bf16[128,2048]{1,0:T(8,128)(2,1)S(1)} collective-permute-done((bf16[128,2048]{1,0:T(8,128)(2,1)S(1)}, bf16[128,2048]{1,0:T(8,128)(2,1)S(1)}, u32[]{:S(2)}, u32[]{:S(2)}) %collective-permute-start.33) | collective-permute-done | bytes 524320 | tf_op jit(solution)/shard_map/ppermute | solution.py:172
  238.2 8.9 %collective-permute-done.25 = bf16[2,32,4096]{2,1,0:T(8,128)(2,1)S(1)} collective-permute-done((bf16[2,32,4096]{2,1,0:T(8,128)(2,1)S(1)}, bf16[2,32,4096]{2,1,0:T(8,128)(2,1)S(1)}, u32[]{:S(2)}, u32[]{:S(2)}) %collective-permute-start.25) | collective-permute-done | bytes 524320 | tf_op jit(solution)/shard_map/ppermute | solution.py:176
  248.5 6.8 collective-permute-done.26
  258.5 5.0 collective-permute-done.35
  267.4 7.7 %collective-permute-done.43 = bf16[128,2048]{1,0:T(8,128)(2,1)S(1)} collective-permute-done((bf16[128,2048]{1,0:T(8,128)(2,1)S(1)}, bf16[128,2048]{1,0:T(8,128)(2,1)S(1)}, u32[]{:S(2)}, u32[]{:S(2)}) %collective-permute-start.43) | collective-permute-done | bytes 524320 | tf_op jit(solution)/shard_map/ppermute | solution.py:172
  275.1 2.2 collective-permute-start.54
  289.0 10.1 %collective-permute-done.47 = bf16[2,32,4096]{2,1,0:T(8,128)(2,1)S(1)} collective-permute-done((bf16[2,32,4096]{2,1,0:T(8,128)(2,1)S(1)}, bf16[2,32,4096]{2,1,0:T(8,128)(2,1)S(1)}, u32[]{:S(2)}, u32[]{:S(2)}) %collective-permute-start.47) | collective-permute-done | bytes 524320 | tf_op jit(solution)/shard_map/ppermute | solution.py:176
  300.1 3.8 collective-permute-done.45
  305.7 2.5 collective-permute-done.46
  330.2 17.9 %collective-permute-done.31 = bf16[2,32,4096]{2,1,0:T(8,128)(2,1)S(1)} collective-permute-done((bf16[2,32,4096]{2,1,0:T(8,128)(2,1)S(1)}, bf16[2,32,4096]{2,1,0:T(8,128)(2,1)S(1)}, u32[]{:S(2)}, u32[]{:S(2)}) %collective-permute-start.31) | collective-permute-done | bytes 524320 | tf_op jit(solution)/shard_map/ppermute | solution.py:176
  350.3 7.4 %collective-permute-done.56 = bf16[2,32,4096]{2,1,0:T(8,128)(2,1)S(1)} collective-permute-done((bf16[2,32,4096]{2,1,0:T(8,128)(2,1)S(1)}, bf16[2,32,4096]{2,1,0:T(8,128)(2,1)S(1)}, u32[]{:S(2)}, u32[]{:S(2)}) %collective-permute-start.56) | collective-permute-done | bytes 524320 | tf_op jit(solution)/shard_map/ppermute | solution.py:176
  378.6 7.6 %collective-permute-done.41 = bf16[2,32,4096]{2,1,0:T(8,128)(2,1)S(1)} collective-permute-done((bf16[2,32,4096]{2,1,0:T(8,128)(2,1)S(1)}, bf16[2,32,4096]{2,1,0:T(8,128)(2,1)S(1)}, u32[]{:S(2)}, u32[]{:S(2)}) %collective-permute-start.41) | collective-permute-done | bytes 524320 | tf_op jit(solution)/shard_map/ppermute | solution.py:176
  389.5 4.9 all-to-all-start.1
  394.4 3.7 collective-permute-start.49
  399.8 8.4 %collective-permute-done.52 = bf16[2,32,4096]{2,1,0:T(8,128)(2,1)} collective-permute-done((bf16[2,32,4096]{2,1,0:T(8,128)(2,1)}, bf16[2,32,4096]{2,1,0:T(8,128)(2,1)}, u32[]{:S(2)}, u32[]{:S(2)}) %collective-permute-start.52) | collective-permute-done | bytes 524320 | tf_op jit(solution)/shard_map/ppermute | solution.py:176
  418.6 8.1 %collective-permute-done.62 = bf16[2,32,4096]{2,1,0:T(8,128)(2,1)S(1)} collective-permute-done((bf16[2,32,4096]{2,1,0:T(8,128)(2,1)S(1)}, bf16[2,32,4096]{2,1,0:T(8,128)(2,1)S(1)}, u32[]{:S(2)}, u32[]{:S(2)}) %collective-permute-start.62) | collective-permute-done | bytes 524320 | tf_op jit(solution)/shard_map/ppermute | solution.py:176
  426.7 9.0 %collective-permute-done.63 = bf16[2,32,4096]{2,1,0:T(8,128)(2,1)S(1)} collective-permute-done((bf16[2,32,4096]{2,1,0:T(8,128)(2,1)S(1)}, bf16[2,32,4096]{2,1,0:T(8,128)(2,1)S(1)}, u32[]{:S(2)}, u32[]{:S(2)}) %collective-permute-start.63) | collective-permute-done | bytes 524320 | tf_op jit(solution)/shard_map/ppermute | solution.py:176
  443.2 11.2 %collective-permute-done.65 = bf16[128,2048]{1,0:T(8,128)(2,1)} collective-permute-done((bf16[128,2048]{1,0:T(8,128)(2,1)}, bf16[128,2048]{1,0:T(8,128)(2,1)}, u32[]{:S(2)}, u32[]{:S(2)}) %collective-permute-start.65) | collective-permute-done | bytes 524320 | tf_op jit(solution)/shard_map/ppermute | solution.py:168
  454.4 3.3 fusion.145
  467.9 18.5 %expert_grads.1 = f32[2048,2304]{1,0:T(8,128)} custom-call(bf16[256,2048]{1,0:T(8,128)(2,1)S(1)} %slice.638.refs_0_, bf16[256,2048]{1,0:T(8,128)(2,1)} %slice.668.refs_1_, bf16[256,2048]{1,0:T(8,128)(2,1)} %slice.695.refs_2_, bf16[256,2048]{1,0:T(8,128)(2,1)} %slice.722.refs_3_, bf16[256,1536]{1,0:T(8,128)(2,1)S(1)} %pad_maximum_fusion.23.refs_4_, ...), custom_call_target="tpu_custom_call" | custom-call | flops 1048576 | bytes 1048576 | tf_op jit(solution)/shard_map/expert_grads/pallas_call | solution.py:221
  487.9 2.4 convolution_convert_fusion.5
  493.6 4.0 fusion.2
  503.2 5.7 convolution_convert_fusion.19.grad_ref
  509.0 2.8 convert_add_fusion.1
  517.2 30.3 %collective-permute-done.74 = bf16[128,2048]{1,0:T(8,128)(2,1)S(1)} collective-permute-done((bf16[128,2048]{1,0:T(8,128)(2,1)}, bf16[128,2048]{1,0:T(8,128)(2,1)S(1)}, u32[]{:S(2)}, u32[]{:S(2)}) %collective-permute-start.74) | collective-permute-done | bytes 524320 | tf_op jit(solution)/shard_map/ppermute | solution.py:168
  548.8 23.8 %attend_back.1 = (bf16[512,1024]{1,0:T(8,128)(2,1)}, bf16[512,128]{1,0:T(8,128)(2,1)}, bf16[512,128]{1,0:T(8,128)(2,1)}, f32[1,128]{1,0:T(1,128)}, f32[1,128]{1,0:T(1,128)}) custom-call(f32[512,1280]{1,0:T(8,128)} %fusion.177.query_ref.key_ref.value_ref, f32[512,1280]{1,0:T(8,128)} %fusion.177.query_ref.key_ref.value_ref, ...), custom_call_target="tpu_custom_call" | custom-call | flops 1048576 | bytes 1048576 | tf_op jit(solution)/shard_map/attend_back/pallas_call | solution.py:351
  576.3 3.2 convolution_convert_fusion
  582.8 3.1 convolution_convert_fusion.7
  592.3 8.6 %collective-permute-done.77 = bf16[128,2048]{1,0:T(8,128)(2,1)S(1)} collective-permute-done((bf16[128,2048]{1,0:T(8,128)(2,1)S(1)}, bf16[128,2048]{1,0:T(8,128)(2,1)S(1)}, u32[]{:S(2)}, u32[]{:S(2)}) %collective-permute-start.77) | collective-permute-done | bytes 524320 | tf_op jit(solution)/shard_map/ppermute | solution.py:101
  602.3 10.5 %collective-permute-done.79 = bf16[128,2048]{1,0:T(8,128)(2,1)S(1)} collective-permute-done((bf16[128,2048]{1,0:T(8,128)(2,1)S(1)}, bf16[128,2048]{1,0:T(8,128)(2,1)S(1)}, u32[]{:S(2)}, u32[]{:S(2)}) %collective-permute-start.79) | collective-permute-done | bytes 524320 | tf_op jit(solution)/shard_map/ppermute | solution.py:101
  613.8 3.0 collective-permute-start.88
  619.7 2.8 all-to-all-start.2
  624.2 4.3 fusion
  630.2 2.4 collective-permute-start.83
  632.6 11.2 %collective-permute-start.82 = (bf16[256,1280]{1,0:T(8,128)(2,1)S(1)}, bf16[256,1280]{1,0:T(8,128)(2,1)S(1)}, u32[]{:S(2)}, u32[]{:S(2)}) collective-permute-start(bf16[256,1280]{1,0:T(8,128)(2,1)S(1)} %get-tuple-element.151), channel_id=1, source_target_pairs={{0,16},{8,24},{16,0},{24,8},{1,17},{9,25},{17,1},{25,9},{2,18},{10... | collective-permute-start | bytes 1966088 | tf_op jit(solution)/shard_map/ppermute | solution.py:135
  643.8 25.8 %collective-permute-done.88 = bf16[128,2048]{1,0:T(8,128)(2,1)} collective-permute-done((bf16[128,2048]{1,0:T(8,128)(2,1)}, bf16[128,2048]{1,0:T(8,128)(2,1)}, u32[]{:S(2)}, u32[]{:S(2)}) %collective-permute-start.88) | collective-permute-done | bytes 524320 | tf_op jit(solution)/shard_map/ppermute | solution.py:135
  669.7 2.6 fusion.67
  672.3 2.6 collective-permute-done.83
  675.0 39.5 %collective-permute-done.82 = bf16[256,1280]{1,0:T(8,128)(2,1)S(1)} collective-permute-done((bf16[256,1280]{1,0:T(8,128)(2,1)S(1)}, bf16[256,1280]{1,0:T(8,128)(2,1)S(1)}, u32[]{:S(2)}, u32[]{:S(2)}) %collective-permute-start.82) | collective-permute-done | bytes 655392 | tf_op jit(solution)/shard_map/ppermute | solution.py:135
  (631 shorter events, 220.2 us)
Async XLA Ops:
  0.6 91.9 %collective-permute-start.14 = (bf16[128,2048]{1,0:T(8,128)(2,1)}, bf16[128,2048]{1,0:T(8,128)(2,1)}, u32[]{:S(2)}, u32[]{:S(2)}) collective-permute-start(bf16[128,2048]{1,0:T(8,128)(2,1)} %param.15), channel_id=1, source_target_pairs={{0,24},{8,0},{16,8},{24,16},{1,25},{9,1},{17,9},{25,17},{2,26},{10... | collective-permute-start | bytes 1572872 | tf_op jit(solution)/shard_map/ppermute | solution.py:168
  5.7 43.5 %collective-permute-start.12 = (bf16[128,2048]{1,0:T(8,128)(2,1)}, bf16[128,2048]{1,0:T(8,128)(2,1)}, u32[]{:S(2)}, u32[]{:S(2)}) collective-permute-start(bf16[128,2048]{1,0:T(8,128)(2,1)} %param.15), channel_id=1, source_target_pairs={{0,8},{8,16},{16,24},{24,0},{1,9},{9,17},{17,25},{25,1},{2,10},{10... | collective-permute-start | bytes 1572872 | tf_op jit(solution)/shard_map/ppermute | solution.py:168
  12.1 30.8 %collective-permute-start.1 = (bf16[64,1280]{1,0:T(8,128)(2,1)S(1)}, bf16[64,1280]{1,0:T(8,128)(2,1)S(1)}, u32[]{:S(2)}, u32[]{:S(2)}) collective-permute-start(bf16[64,1280]{1,0:T(8,128)(2,1)S(1)} %bitcast.601), channel_id=1, source_target_pairs={{0,1},{1,0},{4,5},{5,4},{2,3},{3,2},{6,7},{7,6},{8,9},{9,8},{12,13... | collective-permute-start | bytes 491528 | tf_op jit(solution)/shard_map/ppermute | solution.py:101
  26.4 83.8 %all-to-all-start = ((bf16[32,32,128]{2,1,0:T(8,128)(2,1)}), bf16[32,32,128]{2,1,0:T(8,128)(2,1)S(1)}, u32[]{:S(2)}, u32[]{:S(2)}) async-start(bf16[32,32,128]{2,1,0:T(8,128)(2,1)} %bitcast.234), calls=%async_computation | async-start | bytes 524288 | tf_op jit(solution)/shard_map/all_to_all | solution.py:92
  46.9 57.0 %collective-permute-start.10 = (bf16[256,1280]{1,0:T(8,128)(2,1)S(1)}, bf16[256,1280]{1,0:T(8,128)(2,1)S(1)}, u32[]{:S(2)}, u32[]{:S(2)}) collective-permute-start(bf16[256,1280]{1,0:T(8,128)(2,1)S(1)} %bitcast.555), channel_id=1, source_target_pairs={{0,24},{8,0},{16,8},{24,16},{1,25},{9,1},{17,9},{25,17},{2,26},{10... | collective-permute-start | bytes 1966088 | tf_op jit(solution)/shard_map/ppermute | solution.py:168
  48.9 31.5 %collective-permute-start.4 = (bf16[256,1280]{1,0:T(8,128)(2,1)S(1)}, bf16[256,1280]{1,0:T(8,128)(2,1)S(1)}, u32[]{:S(2)}, u32[]{:S(2)}) collective-permute-start(bf16[256,1280]{1,0:T(8,128)(2,1)S(1)} %bitcast.556), channel_id=1, source_target_pairs={{0,8},{8,16},{16,24},{24,0},{1,9},{9,17},{17,25},{25,1},{2,10},{10... | collective-permute-start | bytes 1966088 | tf_op jit(solution)/shard_map/ppermute | solution.py:168
  49.2 42.4 %collective-permute-start.13 = (bf16[128,2048]{1,0:T(8,128)(2,1)}, bf16[128,2048]{1,0:T(8,128)(2,1)S(1)}, u32[]{:S(2)}, u32[]{:S(2)}) collective-permute-start(bf16[128,2048]{1,0:T(8,128)(2,1)} %collective-permute-done.12), channel_id=1, source_target_pairs={{0,8},{8,16},{16,24},{24,0},{1,9},{9,17},{17,25},{25,1},{2,10},{10... | collective-permute-start | bytes 1572872 | tf_op jit(solution)/shard_map/ppermute | solution.py:168
  81.8 22.1 %collective-permute-start.9 = (bf16[256,1280]{1,0:T(8,128)(2,1)S(1)}, bf16[256,1280]{1,0:T(8,128)(2,1)S(1)}, u32[]{:S(2)}, u32[]{:S(2)}) collective-permute-start(bf16[256,1280]{1,0:T(8,128)(2,1)S(1)} %collective-permute-done.4), channel_id=1, source_target_pairs={{0,8},{8,16},{16,24},{24,0},{1,9},{9,17},{17,25},{25,1},{2,10},{10... | collective-permute-start | bytes 1966088 | tf_op jit(solution)/shard_map/ppermute | solution.py:168
  106.7 26.4 %collective-permute-start.17 = (bf16[128,2048]{1,0:T(8,128)(2,1)}, bf16[128,2048]{1,0:T(8,128)(2,1)}, u32[]{:S(2)}, u32[]{:S(2)}) collective-permute-start(bf16[128,2048]{1,0:T(8,128)(2,1)} %get-tuple-element.223), channel_id=1, source_target_pairs={{0,5},{1,4},{4,1},{5,0},{2,7},{3,6},{6,3},{7,2},{8,13},{9,12},{12,... | collective-permute-start | bytes 1572872 | tf_op jit(solution)/shard_map/ppermute | solution.py:101
  108.6 37.6 %collective-permute-start.16 = (bf16[128,2048]{1,0:T(8,128)(2,1)}, bf16[128,2048]{1,0:T(8,128)(2,1)}, u32[]{:S(2)}, u32[]{:S(2)}) collective-permute-start(bf16[128,2048]{1,0:T(8,128)(2,1)} %get-tuple-element.224), channel_id=1, source_target_pairs={{0,4},{1,5},{4,0},{5,1},{2,6},{3,7},{6,2},{7,3},{8,12},{9,13},{12,... | collective-permute-start | bytes 1572872 | tf_op jit(solution)/shard_map/ppermute | solution.py:101
  111.1 38.2 %collective-permute-start.7 = (bf16[128,2048]{1,0:T(8,128)(2,1)S(1)}, bf16[128,2048]{1,0:T(8,128)(2,1)S(1)}, u32[]{:S(2)}, u32[]{:S(2)}) collective-permute-start(bf16[128,2048]{1,0:T(8,128)(2,1)S(1)} %copy-done.23), channel_id=1, source_target_pairs={{0,5},{1,4},{4,1},{5,0},{2,7},{3,6},{6,3},{7,2},{8,13},{9,12},{12,... | collective-permute-start | bytes 1572872 | tf_op jit(solution)/shard_map/ppermute | solution.py:113
  113.1 41.0 %collective-permute-start.6 = (bf16[128,2048]{1,0:T(8,128)(2,1)S(1)}, bf16[128,2048]{1,0:T(8,128)(2,1)S(1)}, u32[]{:S(2)}, u32[]{:S(2)}) collective-permute-start(bf16[128,2048]{1,0:T(8,128)(2,1)S(1)} %copy-done.23), channel_id=1, source_target_pairs={{0,4},{1,5},{4,0},{5,1},{2,6},{3,7},{6,2},{7,3},{8,12},{9,13},{12,... | collective-permute-start | bytes 1572872 | tf_op jit(solution)/shard_map/ppermute | solution.py:113
  121.8 32.3 %collective-permute-start.5 = (bf16[128,2048]{1,0:T(8,128)(2,1)S(1)}, bf16[128,2048]{1,0:T(8,128)(2,1)S(1)}, u32[]{:S(2)}, u32[]{:S(2)}) collective-permute-start(bf16[128,2048]{1,0:T(8,128)(2,1)S(1)} %copy-done.23), channel_id=1, source_target_pairs={{0,1},{1,0},{4,5},{5,4},{2,3},{3,2},{6,7},{7,6},{8,9},{9,8},{12,13... | collective-permute-start | bytes 1572872 | tf_op jit(solution)/shard_map/ppermute | solution.py:113
  157.4 41.7 %collective-permute-start.34 = (bf16[128,2048]{1,0:T(8,128)(2,1)}, bf16[128,2048]{1,0:T(8,128)(2,1)}, u32[]{:S(2)}, u32[]{:S(2)}) collective-permute-start(bf16[128,2048]{1,0:T(8,128)(2,1)} %convolution_convert_fusion.18), channel_id=1, source_target_pairs={{0,8},{8,16},{16,24},{24,0},{1,9},{9,17},{17,25},{25,1},{2,10},{10... | collective-permute-start | bytes 1572872 | tf_op jit(solution)/shard_map/ppermute | solution.py:168
  190.5 21.0 %collective-permute-start.21 = (bf16[128,2048]{1,0:T(8,128)(2,1)}, bf16[128,2048]{1,0:T(8,128)(2,1)}, u32[]{:S(2)}, u32[]{:S(2)}) collective-permute-start(bf16[128,2048]{1,0:T(8,128)(2,1)} %get-tuple-element.220), channel_id=1, source_target_pairs={{0,5},{1,4},{4,1},{5,0},{2,7},{3,6},{6,3},{7,2},{8,13},{9,12},{12,... | collective-permute-start | bytes 1572872 | tf_op jit(solution)/shard_map/ppermute | solution.py:101
  191.4 21.4 %collective-permute-start.20 = (bf16[128,2048]{1,0:T(8,128)(2,1)}, bf16[128,2048]{1,0:T(8,128)(2,1)}, u32[]{:S(2)}, u32[]{:S(2)}) collective-permute-start(bf16[128,2048]{1,0:T(8,128)(2,1)} %get-tuple-element.221), channel_id=1, source_target_pairs={{0,4},{1,5},{4,0},{5,1},{2,6},{3,7},{6,2},{7,3},{8,12},{9,13},{12,... | collective-permute-start | bytes 1572872 | tf_op jit(solution)/shard_map/ppermute | solution.py:101
  196.3 122.3 %collective-permute-start.55 = (bf16[128,2048]{1,0:T(8,128)(2,1)}, bf16[128,2048]{1,0:T(8,128)(2,1)S(1)}, u32[]{:S(2)}, u32[]{:S(2)}) collective-permute-start(bf16[128,2048]{1,0:T(8,128)(2,1)} %convolution_convert_fusion.18), channel_id=1, source_target_pairs={{0,24},{8,0},{16,8},{24,16},{1,25},{9,1},{17,9},{25,17},{2,26},{10... | collective-permute-start | bytes 1572872 | tf_op jit(solution)/shard_map/ppermute | solution.py:168
  199.1 85.9 %collective-permute-start.44 = (bf16[128,2048]{1,0:T(8,128)(2,1)}, bf16[128,2048]{1,0:T(8,128)(2,1)S(1)}, u32[]{:S(2)}, u32[]{:S(2)}) collective-permute-start(bf16[128,2048]{1,0:T(8,128)(2,1)} %collective-permute-done.34), channel_id=1, source_target_pairs={{0,8},{8,16},{16,24},{24,0},{1,9},{9,17},{17,25},{25,1},{2,10},{10... | collective-permute-start | bytes 1572872 | tf_op jit(solution)/shard_map/ppermute | solution.py:168
  215.2 16.7 %collective-permute-start.33 = (bf16[128,2048]{1,0:T(8,128)(2,1)S(1)}, bf16[128,2048]{1,0:T(8,128)(2,1)S(1)}, u32[]{:S(2)}, u32[]{:S(2)}) collective-permute-start(bf16[128,2048]{1,0:T(8,128)(2,1)S(1)} %multiply_convert_fusion.1), channel_id=1, source_target_pairs={{0,8},{8,16},{16,24},{24,0},{1,9},{9,17},{17,25},{25,1},{2,10},{10... | collective-permute-start | bytes 1572872 | tf_op jit(solution)/shard_map/ppermute | solution.py:172
  222.3 24.8 %collective-permute-start.25 = (bf16[2,32,4096]{2,1,0:T(8,128)(2,1)S(1)}, bf16[2,32,4096]{2,1,0:T(8,128)(2,1)S(1)}, u32[]{:S(2)}, u32[]{:S(2)}) collective-permute-start(bf16[2,32,4096]{2,1,0:T(8,128)(2,1)S(1)} %bitcast.589), channel_id=1, source_target_pairs={{0,1},{1,0},{4,5},{5,4},{2,3},{3,2},{6,7},{7,6},{8,9},{9,8},{12,13... | collective-permute-start | bytes 1572872 | tf_op jit(solution)/shard_map/ppermute | solution.py:176
  231.9 23.3 %collective-permute-start.26 = (bf16[2,32,4096]{2,1,0:T(8,128)(2,1)S(1)}, bf16[2,32,4096]{2,1,0:T(8,128)(2,1)S(1)}, u32[]{:S(2)}, u32[]{:S(2)}) collective-permute-start(bf16[2,32,4096]{2,1,0:T(8,128)(2,1)S(1)} %bitcast.585), channel_id=1, source_target_pairs={{0,4},{1,5},{4,0},{5,1},{2,6},{3,7},{6,2},{7,3},{8,12},{9,13},{12,... | collective-permute-start | bytes 1572872 | tf_op jit(solution)/shard_map/ppermute | solution.py:176
  236.3 22.1 %collective-permute-start.37 = (bf16[2,32,4096]{2,1,0:T(8,128)(2,1)S(1)}, bf16[2,32,4096]{2,1,0:T(8,128)(2,1)S(1)}, u32[]{:S(2)}, u32[]{:S(2)}) collective-permute-start(bf16[2,32,4096]{2,1,0:T(8,128)(2,1)S(1)} %bitcast.586), channel_id=1, source_target_pairs={{0,5},{1,4},{4,1},{5,0},{2,7},{3,6},{6,3},{7,2},{8,13},{9,12},{12,... | collective-permute-start | bytes 1572872 | tf_op jit(solution)/shard_map/ppermute | solution.py:176
  247.1 16.4 %collective-permute-start.35 = (bf16[2,32,4096]{2,1,0:T(8,128)(2,1)S(1)}, bf16[2,32,4096]{2,1,0:T(8,128)(2,1)S(1)}, u32[]{:S(2)}, u32[]{:S(2)}) collective-permute-start(bf16[2,32,4096]{2,1,0:T(8,128)(2,1)S(1)} %bitcast.584), channel_id=1, source_target_pairs={{0,1},{1,0},{4,5},{5,4},{2,3},{3,2},{6,7},{7,6},{8,9},{9,8},{12,13... | collective-permute-start | bytes 1572872 | tf_op jit(solution)/shard_map/ppermute | solution.py:176
  258.4 19.1 %collective-permute-start.28 = (bf16[4,32,4096]{2,1,0:T(8,128)(2,1)S(1)}, bf16[4,32,4096]{2,1,0:T(8,128)(2,1)S(1)}, u32[]{:S(2)}, u32[]{:S(2)}) collective-permute-start(bf16[4,32,4096]{2,1,0:T(8,128)(2,1)S(1)} %pad_maximum_fusion.19), channel_id=1, source_target_pairs={{0,2},{2,0},{1,3},{3,1},{4,6},{6,4},{5,7},{7,5},{8,10},{10,8},{9,1... | collective-permute-start | bytes 3145736 | tf_op jit(solution)/shard_map/ppermute | solution.py:83
  267.3 32.5 %collective-permute-start.38 = (bf16[4,32,4096]{2,1,0:T(8,128)(2,1)S(1)}, bf16[4,32,4096]{2,1,0:T(8,128)(2,1)S(1)}, u32[]{:S(2)}, u32[]{:S(2)}) collective-permute-start(bf16[4,32,4096]{2,1,0:T(8,128)(2,1)S(1)} %pad_maximum_fusion.20), channel_id=1, source_target_pairs={{0,2},{2,0},{1,3},{3,1},{4,6},{6,4},{5,7},{7,5},{8,10},{10,8},{9,1... | collective-permute-start | bytes 3145736 | tf_op jit(solution)/shard_map/ppermute | solution.py:83
  275.1 41.7 %collective-permute-start.54 = (bf16[128,2048]{1,0:T(8,128)(2,1)S(1)}, bf16[128,2048]{1,0:T(8,128)(2,1)S(1)}, u32[]{:S(2)}, u32[]{:S(2)}) collective-permute-start(bf16[128,2048]{1,0:T(8,128)(2,1)S(1)} %collective-permute-done.43), channel_id=1, source_target_pairs={{0,8},{8,16},{16,24},{24,0},{1,9},{9,17},{17,25},{25,1},{2,10},{10... | collective-permute-start | bytes 1572872 | tf_op jit(solution)/shard_map/ppermute | solution.py:172
  287.6 16.3 %collective-permute-start.45 = (bf16[2,32,4096]{2,1,0:T(8,128)(2,1)S(1)}, bf16[2,32,4096]{2,1,0:T(8,128)(2,1)S(1)}, u32[]{:S(2)}, u32[]{:S(2)}) collective-permute-start(bf16[2,32,4096]{2,1,0:T(8,128)(2,1)S(1)} %bitcast.588), channel_id=1, source_target_pairs={{0,1},{1,0},{4,5},{5,4},{2,3},{3,2},{6,7},{7,6},{8,9},{9,8},{12,13... | collective-permute-start | bytes 1572872 | tf_op jit(solution)/shard_map/ppermute | solution.py:176
  309.5 19.4 %collective-permute-start.30 = (bf16[2,32,4096]{2,1,0:T(8,128)(2,1)S(1)}, bf16[2,32,4096]{2,1,0:T(8,128)(2,1)S(1)}, u32[]{:S(2)}, u32[]{:S(2)}) collective-permute-start(bf16[2,32,4096]{2,1,0:T(8,128)(2,1)S(1)} %pad_maximum_fusion.28), channel_id=1, source_target_pairs={{0,1},{1,0},{4,5},{5,4},{2,3},{3,2},{6,7},{7,6},{8,9},{9,8},{12,13... | collective-permute-start | bytes 1572872 | tf_op jit(solution)/shard_map/ppermute | solution.py:176
  310.8 37.3 %collective-permute-start.31 = (bf16[2,32,4096]{2,1,0:T(8,128)(2,1)S(1)}, bf16[2,32,4096]{2,1,0:T(8,128)(2,1)S(1)}, u32[]{:S(2)}, u32[]{:S(2)}) collective-permute-start(bf16[2,32,4096]{2,1,0:T(8,128)(2,1)S(1)} %pad_maximum_fusion.29), channel_id=1, source_target_pairs={{0,4},{1,5},{4,0},{5,1},{2,6},{3,7},{6,2},{7,3},{8,12},{9,13},{12,... | collective-permute-start | bytes 1572872 | tf_op jit(solution)/shard_map/ppermute | solution.py:176
  311.8 36.4 %collective-permute-start.32 = (bf16[2,32,4096]{2,1,0:T(8,128)(2,1)S(1)}, bf16[2,32,4096]{2,1,0:T(8,128)(2,1)S(1)}, u32[]{:S(2)}, u32[]{:S(2)}) collective-permute-start(bf16[2,32,4096]{2,1,0:T(8,128)(2,1)S(1)} %pad_maximum_fusion.30), channel_id=1, source_target_pairs={{0,5},{1,4},{4,1},{5,0},{2,7},{3,6},{6,3},{7,2},{8,13},{9,12},{12,... | collective-permute-start | bytes 1572872 | tf_op jit(solution)/shard_map/ppermute | solution.py:176
  321.4 28.9 %collective-permute-start.58 = (bf16[2,32,4096]{2,1,0:T(8,128)(2,1)S(1)}, bf16[2,32,4096]{2,1,0:T(8,128)(2,1)S(1)}, u32[]{:S(2)}, u32[]{:S(2)}) collective-permute-start(bf16[2,32,4096]{2,1,0:T(8,128)(2,1)S(1)} %bitcast.583), channel_id=1, source_target_pairs={{0,5},{1,4},{4,1},{5,0},{2,7},{3,6},{6,3},{7,2},{8,13},{9,12},{12,... | collective-permute-start | bytes 1572872 | tf_op jit(solution)/shard_map/ppermute | solution.py:176
  328.0 29.6 %collective-permute-start.56 = (bf16[2,32,4096]{2,1,0:T(8,128)(2,1)S(1)}, bf16[2,32,4096]{2,1,0:T(8,128)(2,1)S(1)}, u32[]{:S(2)}, u32[]{:S(2)}) collective-permute-start(bf16[2,32,4096]{2,1,0:T(8,128)(2,1)S(1)} %bitcast.581), channel_id=1, source_target_pairs={{0,1},{1,0},{4,5},{5,4},{2,3},{3,2},{6,7},{7,6},{8,9},{9,8},{12,13... | collective-permute-start | bytes 1572872 | tf_op jit(solution)/shard_map/ppermute | solution.py:176
  328.9 29.8 %collective-permute-start.57 = (bf16[2,32,4096]{2,1,0:T(8,128)(2,1)S(1)}, bf16[2,32,4096]{2,1,0:T(8,128)(2,1)S(1)}, u32[]{:S(2)}, u32[]{:S(2)}) collective-permute-start(bf16[2,32,4096]{2,1,0:T(8,128)(2,1)S(1)} %bitcast.580), channel_id=1, source_target_pairs={{0,4},{1,5},{4,0},{5,1},{2,6},{3,7},{6,2},{7,3},{8,12},{9,13},{12,... | collective-permute-start | bytes 1572872 | tf_op jit(solution)/shard_map/ppermute | solution.py:176
  359.2 17.5 %collective-permute-start.40 = (bf16[2,32,4096]{2,1,0:T(8,128)(2,1)S(1)}, bf16[2,32,4096]{2,1,0:T(8,128)(2,1)S(1)}, u32[]{:S(2)}, u32[]{:S(2)}) collective-permute-start(bf16[2,32,4096]{2,1,0:T(8,128)(2,1)S(1)} %pad_maximum_fusion.31), channel_id=1, source_target_pairs={{0,1},{1,0},{4,5},{5,4},{2,3},{3,2},{6,7},{7,6},{8,9},{9,8},{12,13... | collective-permute-start | bytes 1572872 | tf_op jit(solution)/shard_map/ppermute | solution.py:176
  360.1 26.1 %collective-permute-start.41 = (bf16[2,32,4096]{2,1,0:T(8,128)(2,1)S(1)}, bf16[2,32,4096]{2,1,0:T(8,128)(2,1)S(1)}, u32[]{:S(2)}, u32[]{:S(2)}) collective-permute-start(bf16[2,32,4096]{2,1,0:T(8,128)(2,1)S(1)} %pad_maximum_fusion.32), channel_id=1, source_target_pairs={{0,4},{1,5},{4,0},{5,1},{2,6},{3,7},{6,2},{7,3},{8,12},{9,13},{12,... | collective-permute-start | bytes 1572872 | tf_op jit(solution)/shard_map/ppermute | solution.py:176
  361.1 25.1 %collective-permute-start.42 = (bf16[2,32,4096]{2,1,0:T(8,128)(2,1)S(1)}, bf16[2,32,4096]{2,1,0:T(8,128)(2,1)S(1)}, u32[]{:S(2)}, u32[]{:S(2)}) collective-permute-start(bf16[2,32,4096]{2,1,0:T(8,128)(2,1)S(1)} %pad_maximum_fusion.33), channel_id=1, source_target_pairs={{0,5},{1,4},{4,1},{5,0},{2,7},{3,6},{6,3},{7,2},{8,13},{9,12},{12,... | collective-permute-start | bytes 1572872 | tf_op jit(solution)/shard_map/ppermute | solution.py:176
  363.9 35.9 %collective-permute-start.51 = (bf16[2,32,4096]{2,1,0:T(8,128)(2,1)}, bf16[2,32,4096]{2,1,0:T(8,128)(2,1)}, u32[]{:S(2)}, u32[]{:S(2)}) collective-permute-start(bf16[2,32,4096]{2,1,0:T(8,128)(2,1)} %pad_maximum_fusion.34), channel_id=1, source_target_pairs={{0,1},{1,0},{4,5},{5,4},{2,3},{3,2},{6,7},{7,6},{8,9},{9,8},{12,13... | collective-permute-start | bytes 1572872 | tf_op jit(solution)/shard_map/ppermute | solution.py:176
  367.3 40.9 %collective-permute-start.52 = (bf16[2,32,4096]{2,1,0:T(8,128)(2,1)}, bf16[2,32,4096]{2,1,0:T(8,128)(2,1)}, u32[]{:S(2)}, u32[]{:S(2)}) collective-permute-start(bf16[2,32,4096]{2,1,0:T(8,128)(2,1)} %pad_maximum_fusion.35), channel_id=1, source_target_pairs={{0,4},{1,5},{4,0},{5,1},{2,6},{3,7},{6,2},{7,3},{8,12},{9,13},{12,... | collective-permute-start | bytes 1572872 | tf_op jit(solution)/shard_map/ppermute | solution.py:176
  376.7 31.5 %collective-permute-start.53 = (bf16[2,32,4096]{2,1,0:T(8,128)(2,1)}, bf16[2,32,4096]{2,1,0:T(8,128)(2,1)}, u32[]{:S(2)}, u32[]{:S(2)}) collective-permute-start(bf16[2,32,4096]{2,1,0:T(8,128)(2,1)} %pad_maximum_fusion.36), channel_id=1, source_target_pairs={{0,5},{1,4},{4,1},{5,0},{2,7},{3,6},{6,3},{7,2},{8,13},{9,12},{12,... | collective-permute-start | bytes 1572872 | tf_op jit(solution)/shard_map/ppermute | solution.py:176
  386.2 24.2 %collective-permute-start.61 = (bf16[4,32,4096]{2,1,0:T(8,128)(2,1)}, bf16[4,32,4096]{2,1,0:T(8,128)(2,1)}, u32[]{:S(2)}, u32[]{:S(2)}) collective-permute-start(bf16[4,32,4096]{2,1,0:T(8,128)(2,1)} %bitcast.135), channel_id=1, source_target_pairs={{0,2},{2,0},{1,3},{3,1},{4,6},{6,4},{5,7},{7,5},{8,10},{10,8},{9,1... | collective-permute-start | bytes 3145736 | tf_op jit(solution)/shard_map/ppermute | solution.py:83
  389.5 53.3 %all-to-all-start.1 = ((f32[32,1,32]{2,1,0:T(1,128)}), f32[32,1,32]{2,1,0:T(1,128)S(1)}, u32[]{:S(2)}, u32[]{:S(2)}) async-start(f32[32,1,32]{2,1,0:T(1,128)} %bitcast.151), calls=%async_computation.1 | async-start | bytes 32768 | tf_op jit(solution)/shard_map/all_to_all | solution.py:92
  394.4 48.8 %collective-permute-start.49 = (bf16[128,2048]{1,0:T(8,128)(2,1)}, bf16[128,2048]{1,0:T(8,128)(2,1)}, u32[]{:S(2)}, u32[]{:S(2)}) collective-permute-start(bf16[128,2048]{1,0:T(8,128)(2,1)} %get-tuple-element.246), channel_id=1, source_target_pairs={{0,24},{8,0},{16,8},{24,16},{1,25},{9,1},{17,9},{25,17},{2,26},{10... | collective-permute-start | bytes 1572872 | tf_op jit(solution)/shard_map/ppermute | solution.py:168
  413.1 22.6 %collective-permute-start.63 = (bf16[2,32,4096]{2,1,0:T(8,128)(2,1)S(1)}, bf16[2,32,4096]{2,1,0:T(8,128)(2,1)S(1)}, u32[]{:S(2)}, u32[]{:S(2)}) collective-permute-start(bf16[2,32,4096]{2,1,0:T(8,128)(2,1)S(1)} %pad_maximum_fusion.38), channel_id=1, source_target_pairs={{0,4},{1,5},{4,0},{5,1},{2,6},{3,7},{6,2},{7,3},{8,12},{9,13},{12,... | collective-permute-start | bytes 1572872 | tf_op jit(solution)/shard_map/ppermute | solution.py:176
  414.0 23.0 %collective-permute-start.64 = (bf16[2,32,4096]{2,1,0:T(8,128)(2,1)S(1)}, bf16[2,32,4096]{2,1,0:T(8,128)(2,1)S(1)}, u32[]{:S(2)}, u32[]{:S(2)}) collective-permute-start(bf16[2,32,4096]{2,1,0:T(8,128)(2,1)S(1)} %pad_maximum_fusion.39), channel_id=1, source_target_pairs={{0,5},{1,4},{4,1},{5,0},{2,7},{3,6},{6,3},{7,2},{8,13},{9,12},{12,... | collective-permute-start | bytes 1572872 | tf_op jit(solution)/shard_map/ppermute | solution.py:176
  416.6 26.5 %collective-permute-start.60 = (bf16[128,2048]{1,0:T(8,128)(2,1)}, bf16[128,2048]{1,0:T(8,128)(2,1)}, u32[]{:S(2)}, u32[]{:S(2)}) collective-permute-start(bf16[128,2048]{1,0:T(8,128)(2,1)} %get-tuple-element.244), channel_id=1, source_target_pairs={{0,16},{8,24},{16,0},{24,8},{1,17},{9,25},{17,1},{25,9},{2,18},{10... | collective-permute-start | bytes 1572872 | tf_op jit(solution)/shard_map/ppermute | solution.py:168
  459.9 26.5 %collective-permute-start.68 = (bf16[128,2048]{1,0:T(8,128)(2,1)S(1)}, bf16[128,2048]{1,0:T(8,128)(2,1)S(1)}, u32[]{:S(2)}, u32[]{:S(2)}) collective-permute-start(bf16[128,2048]{1,0:T(8,128)(2,1)S(1)} %fusion.37), channel_id=1, source_target_pairs={{0,5},{1,4},{4,1},{5,0},{2,7},{3,6},{6,3},{7,2},{8,13},{9,12},{12,... | collective-permute-start | bytes 1572872 | tf_op jit(solution)/shard_map/ppermute | solution.py:113
  460.4 26.0 %collective-permute-start.67 = (bf16[128,2048]{1,0:T(8,128)(2,1)S(1)}, bf16[128,2048]{1,0:T(8,128)(2,1)S(1)}, u32[]{:S(2)}, u32[]{:S(2)}) collective-permute-start(bf16[128,2048]{1,0:T(8,128)(2,1)S(1)} %fusion.37), channel_id=1, source_target_pairs={{0,4},{1,5},{4,0},{5,1},{2,6},{3,7},{6,2},{7,3},{8,12},{9,13},{12,... | collective-permute-start | bytes 1572872 | tf_op jit(solution)/shard_map/ppermute | solution.py:113
  462.1 24.4 %collective-permute-start.66 = (bf16[128,2048]{1,0:T(8,128)(2,1)S(1)}, bf16[128,2048]{1,0:T(8,128)(2,1)S(1)}, u32[]{:S(2)}, u32[]{:S(2)}) collective-permute-start(bf16[128,2048]{1,0:T(8,128)(2,1)S(1)} %fusion.37), channel_id=1, source_target_pairs={{0,1},{1,0},{4,5},{5,4},{2,3},{3,2},{6,7},{7,6},{8,9},{9,8},{12,13... | collective-permute-start | bytes 1572872 | tf_op jit(solution)/shard_map/ppermute | solution.py:113
  502.5 45.1 %collective-permute-start.74 = (bf16[128,2048]{1,0:T(8,128)(2,1)}, bf16[128,2048]{1,0:T(8,128)(2,1)S(1)}, u32[]{:S(2)}, u32[]{:S(2)}) collective-permute-start(bf16[128,2048]{1,0:T(8,128)(2,1)} %get-tuple-element.75), channel_id=1, source_target_pairs={{0,16},{8,24},{16,0},{24,8},{1,17},{9,25},{17,1},{25,9},{2,18},{10... | collective-permute-start | bytes 1572872 | tf_op jit(solution)/shard_map/ppermute | solution.py:168
  502.5 45.1 %collective-permute-start.75 = (bf16[128,2048]{1,0:T(8,128)(2,1)}, bf16[128,2048]{1,0:T(8,128)(2,1)S(1)}, u32[]{:S(2)}, u32[]{:S(2)}) collective-permute-start(bf16[128,2048]{1,0:T(8,128)(2,1)} %get-tuple-element.76), channel_id=1, source_target_pairs={{0,8},{8,16},{16,24},{24,0},{1,9},{9,17},{17,25},{25,1},{2,10},{10... | collective-permute-start | bytes 1572872 | tf_op jit(solution)/shard_map/ppermute | solution.py:168
  513.0 59.6 %collective-permute-start.70 = (bf16[128,2048]{1,0:T(8,128)(2,1)}, bf16[128,2048]{1,0:T(8,128)(2,1)S(1)}, u32[]{:S(2)}, u32[]{:S(2)}) collective-permute-start(bf16[128,2048]{1,0:T(8,128)(2,1)} %get-tuple-element.166), channel_id=1, source_target_pairs={{0,1},{1,0},{4,5},{5,4},{2,3},{3,2},{6,7},{7,6},{8,9},{9,8},{12,13... | collective-permute-start | bytes 1572872 | tf_op jit(solution)/shard_map/ppermute | solution.py:101
  514.3 58.4 %collective-permute-start.72 = (bf16[128,2048]{1,0:T(8,128)(2,1)}, bf16[128,2048]{1,0:T(8,128)(2,1)}, u32[]{:S(2)}, u32[]{:S(2)}) collective-permute-start(bf16[128,2048]{1,0:T(8,128)(2,1)} %get-tuple-element.167), channel_id=1, source_target_pairs={{0,5},{1,4},{4,1},{5,0},{2,7},{3,6},{6,3},{7,2},{8,13},{9,12},{12,... | collective-permute-start | bytes 1572872 | tf_op jit(solution)/shard_map/ppermute | solution.py:101
  516.8 55.9 %collective-permute-start.71 = (bf16[128,2048]{1,0:T(8,128)(2,1)}, bf16[128,2048]{1,0:T(8,128)(2,1)}, u32[]{:S(2)}, u32[]{:S(2)}) collective-permute-start(bf16[128,2048]{1,0:T(8,128)(2,1)} %get-tuple-element.168), channel_id=1, source_target_pairs={{0,4},{1,5},{4,0},{5,1},{2,6},{3,7},{6,2},{7,3},{8,12},{9,13},{12,... | collective-permute-start | bytes 1572872 | tf_op jit(solution)/shard_map/ppermute | solution.py:101
  582.8 41.4 %collective-permute-start.80 = (bf16[8,128,1280]{2,1,0:T(8,128)(2,1)}, bf16[8,128,1280]{2,1,0:T(8,128)(2,1)}, u32[]{:S(2)}, u32[]{:S(2)}) collective-permute-start(bf16[8,128,1280]{2,1,0:T(8,128)(2,1)} %fusion.3), channel_id=1, source_target_pairs={{0,2},{2,0},{1,3},{3,1},{4,6},{6,4},{5,7},{7,5},{8,10},{10,8},{9,1... | collective-permute-start | bytes 7864328 | tf_op jit(solution)/shard_map/ppermute | solution.py:83
  587.4 25.4 %collective-permute-start.79 = (bf16[128,2048]{1,0:T(8,128)(2,1)S(1)}, bf16[128,2048]{1,0:T(8,128)(2,1)S(1)}, u32[]{:S(2)}, u32[]{:S(2)}) collective-permute-start(bf16[128,2048]{1,0:T(8,128)(2,1)S(1)} %get-tuple-element.164), channel_id=1, source_target_pairs={{0,5},{1,4},{4,1},{5,0},{2,7},{3,6},{6,3},{7,2},{8,13},{9,12},{12,... | collective-permute-start | bytes 1572872 | tf_op jit(solution)/shard_map/ppermute | solution.py:101
  588.9 25.0 %collective-permute-start.78 = (bf16[128,2048]{1,0:T(8,128)(2,1)S(1)}, bf16[128,2048]{1,0:T(8,128)(2,1)S(1)}, u32[]{:S(2)}, u32[]{:S(2)}) collective-permute-start(bf16[128,2048]{1,0:T(8,128)(2,1)S(1)} %get-tuple-element.165), channel_id=1, source_target_pairs={{0,4},{1,5},{4,0},{5,1},{2,6},{3,7},{6,2},{7,3},{8,12},{9,13},{12,... | collective-permute-start | bytes 1572872 | tf_op jit(solution)/shard_map/ppermute | solution.py:101
  589.8 33.3 %collective-permute-start.76 = (bf16[128,2048]{1,0:T(8,128)(2,1)S(1)}, bf16[128,2048]{1,0:T(8,128)(2,1)}, u32[]{:S(2)}, u32[]{:S(2)}) collective-permute-start(bf16[128,2048]{1,0:T(8,128)(2,1)S(1)} %add_convert_fusion), channel_id=1, source_target_pairs={{0,1},{1,0},{2,3},{3,2},{4,5},{5,4},{6,7},{7,6},{8,9},{9,8},{10,11... | collective-permute-start | bytes 1572872 | tf_op jit(solution)/shard_map/ppermute | solution.py:83
  600.9 31.7 %collective-permute-start.87 = (bf16[128,2048]{1,0:T(8,128)(2,1)}, bf16[128,2048]{1,0:T(8,128)(2,1)}, u32[]{:S(2)}, u32[]{:S(2)}) collective-permute-start(bf16[128,2048]{1,0:T(8,128)(2,1)} %get-tuple-element.160), channel_id=1, source_target_pairs={{0,8},{8,16},{16,24},{24,0},{1,9},{9,17},{17,25},{25,1},{2,10},{10... | collective-permute-start | bytes 1572872 | tf_op jit(solution)/shard_map/ppermute | solution.py:135
  612.8 31.0 %collective-permute-start.89 = (bf16[128,2048]{1,0:T(8,128)(2,1)}, bf16[128,2048]{1,0:T(8,128)(2,1)}, u32[]{:S(2)}, u32[]{:S(2)}) collective-permute-start(bf16[128,2048]{1,0:T(8,128)(2,1)} %get-tuple-element.161), channel_id=1, source_target_pairs={{0,24},{8,0},{16,8},{24,16},{1,25},{9,1},{17,9},{25,17},{2,26},{10... | collective-permute-start | bytes 1572872 | tf_op jit(solution)/shard_map/ppermute | solution.py:135
  613.8 55.8 %collective-permute-start.88 = (bf16[128,2048]{1,0:T(8,128)(2,1)}, bf16[128,2048]{1,0:T(8,128)(2,1)}, u32[]{:S(2)}, u32[]{:S(2)}) collective-permute-start(bf16[128,2048]{1,0:T(8,128)(2,1)} %get-tuple-element.162), channel_id=1, source_target_pairs={{0,16},{8,24},{16,0},{24,8},{1,17},{9,25},{17,1},{25,9},{2,18},{10... | collective-permute-start | bytes 1572872 | tf_op jit(solution)/shard_map/ppermute | solution.py:135
  619.7 101.1 %all-to-all-start.2 = ((f32[32,24,128]{2,1,0:T(8,128)}), f32[32,24,128]{2,1,0:T(8,128)S(1)}, u32[]{:S(2)}, u32[]{:S(2)}) async-start(f32[32,24,128]{2,1,0:T(8,128)} %bitcast.565), calls=%async_computation.2 | async-start | bytes 786432 | tf_op jit(solution)/shard_map/all_to_all | solution.py:92
  628.7 43.6 %collective-permute-start.81 = (bf16[256,1280]{1,0:T(8,128)(2,1)S(1)}, bf16[256,1280]{1,0:T(8,128)(2,1)S(1)}, u32[]{:S(2)}, u32[]{:S(2)}) collective-permute-start(bf16[256,1280]{1,0:T(8,128)(2,1)S(1)} %get-tuple-element.149), channel_id=1, source_target_pairs={{0,8},{8,16},{16,24},{24,0},{1,9},{9,17},{17,25},{25,1},{2,10},{10... | collective-permute-start | bytes 1966088 | tf_op jit(solution)/shard_map/ppermute | solution.py:135
  630.2 44.8 %collective-permute-start.83 = (bf16[256,1280]{1,0:T(8,128)(2,1)S(1)}, bf16[256,1280]{1,0:T(8,128)(2,1)S(1)}, u32[]{:S(2)}, u32[]{:S(2)}) collective-permute-start(bf16[256,1280]{1,0:T(8,128)(2,1)S(1)} %get-tuple-element.150), channel_id=1, source_target_pairs={{0,24},{8,0},{16,8},{24,16},{1,25},{9,1},{17,9},{25,17},{2,26},{10... | collective-permute-start | bytes 1966088 | tf_op jit(solution)/shard_map/ppermute | solution.py:135
  632.6 81.9 %collective-permute-start.82 = (bf16[256,1280]{1,0:T(8,128)(2,1)S(1)}, bf16[256,1280]{1,0:T(8,128)(2,1)S(1)}, u32[]{:S(2)}, u32[]{:S(2)}) collective-permute-start(bf16[256,1280]{1,0:T(8,128)(2,1)S(1)} %get-tuple-element.151), channel_id=1, source_target_pairs={{0,16},{8,24},{16,0},{24,8},{1,17},{9,25},{17,1},{25,9},{2,18},{10... | collective-permute-start | bytes 1966088 | tf_op jit(solution)/shard_map/ppermute | solution.py:135
  (125 other events, 1494.5 us)

commit v5 on v4

--- a/solution.py
+++ b/solution.py
@@ -32,6 +32,7 @@
 NEAR_AXIS = "near"
 CORE_AXIS = "core"
 SEQ_AXIS = "seq"
+SLAB_AXES = (NEAR_AXIS, CORE_AXIS, SEQ_AXIS)
 HEAD_AXES = (NEAR_AXIS, SEQ_AXIS)
 ALL_AXES = (FAR_AXIS, NEAR_AXIS, CORE_AXIS, SEQ_AXIS)
 DP_AXES = (FAR_AXIS, NEAR_AXIS, CORE_AXIS)
@@ -115,9 +116,13 @@
     return quad_order(found)
 
 
+def quad_parts(parts):
+    own = lax.dynamic_index_in_dim(parts, quad_index(), 0, keepdims=False)
+    return [own] + [quad_send(parts, step) for step in range(1, 4)]
+
+
 def quad_swap(parts):
-    own = lax.dynamic_index_in_dim(parts, quad_index(), 0, keepdims=False)
-    return quad_order([own] + [quad_send(parts, step) for step in range(1, 4)])
+    return quad_order(quad_parts(parts))
 
 
 def quad_sum(parts):
@@ -128,13 +133,23 @@
 
 
 def far_sum(parts, count):
+    total = parts[0].astype(F32)
+    if count != 4:
+        for step in range(1, count):
+            total = total + far_shift(parts[step].astype(BF), -step, count).astype(F32)
+        return total
+    relay = far_shift(parts[2].astype(BF), -1, count).astype(F32)
+    direct = far_shift(parts[3].astype(BF), 1, count).astype(F32)
+    relay = far_shift((parts[1].astype(F32) + relay).astype(BF), -1, count)
+    return total + direct + relay.astype(F32)
+
+
+def far_parts(values, count):
     here = lax.axis_index(FAR_AXIS)
-    total = lax.dynamic_index_in_dim(parts, here, 0, keepdims=False).astype(F32)
-    for step in range(1, count):
-        block = lax.dynamic_index_in_dim(parts, lax.rem(here + step, count), 0, keepdims=False)
-        block = lax.ppermute(block, FAR_AXIS, [(i, (i + step) % count) for i in range(count)])
-        total = total + block.astype(F32)
-    return total
+    return [
+        lax.dynamic_index_in_dim(values, lax.rem(here + count - step, count), 0, keepdims=False)
+        for step in range(count)
+    ]
 
 
 def far_all(value, count, first=None):
@@ -178,21 +193,99 @@
 
 def slab_out(blocks):
     got = [blocks[0]] + [quad_xor(blocks[step], step) for step in range(1, 4)]
-    keep = jnp.stack([part[0] for part in got])
-    other = swap(jnp.stack([part[1] for part in got]), CORE_AXIS)
-    return jnp.stack([keep, other])
-
-
-def slab_back(blocks):
-    other = swap(blocks[1], CORE_AXIS)
-    parts = [jnp.stack([blocks[0, step], other[step]]) for step in range(4)]
-    return jnp.stack([parts[0]] + [quad_xor(parts[step], step) for step in range(1, 4)])
+    keep = quad_order([part[0] for part in got])
+    other = swap(quad_order([part[1] for part in got]), CORE_AXIS)
+    first, second = pair_order(keep, other, CORE_AXIS)
+    shape = (NEAR, 2) + keep.shape[1:]
+    return jnp.stack([first.reshape(shape), second.reshape(shape)], axis=1)
+
+
+def expert_kernel(
+    here_ref, in_ref, cot_ref, mask_ref, router_ref, gate_ref, up_ref, down_ref,
+    gate_grad_ref, up_grad_ref, active_ref, grad_ref, in_grad_ref, gated_ref, dot_ref,
+    out_total, in_total, gate_slot,
+):
+    block = pl.program_id(0)
+
+    @pl.when(block == 0)
+    def _():
+        chosen = mask_ref[...].astype(F32) > 0.5
+        logits = jnp.where(chosen, mm(in_ref[...], router_ref[...]), -1e30)
+        exped = jnp.where(chosen, jnp.exp(logits - jnp.max(logits, axis=-1, keepdims=True)), 0.0)
+        total = jnp.sum(exped, axis=-1, keepdims=True)
+        mine = lax.broadcasted_iota(jnp.int32, exped.shape, 1) == here_ref[0]
+        picked = jnp.sum(jnp.where(mine, exped, 0.0), axis=-1, keepdims=True)
+        gate = picked / jnp.where(total > 0.0, total, 1.0)
+        gate_slot[...] = jnp.broadcast_to(gate, gate_slot.shape)
+        grad_ref[...] = (gate * cot_ref[...].astype(F32)).astype(BF)
+        out_total[...] = jnp.zeros_like(out_total)
+        in_total[...] = jnp.zeros_like(in_total)
+
+    gate_pre = mm(in_ref[...], gate_ref[...])
+    up_pre = mm(in_ref[...], up_ref[...])
+    act_grad = mm(grad_ref[...], down_ref[...])
+    sig_gate = jax.nn.sigmoid(gate_pre)
+    silu_val = gate_pre * sig_gate
+    active = (silu_val * up_pre).astype(BF)
+    silu_slope = sig_gate * (1.0 + gate_pre * (1.0 - sig_gate))
+    gate_grad = (act_grad * up_pre * silu_slope).astype(BF)
+    up_grad = (act_grad * silu_val).astype(BF)
+    active_ref[...] = active
+    gate_grad_ref[...] = gate_grad
+    up_grad_ref[...] = up_grad
+    out_total[...] += mm_nt(active, down_ref[...])
+    in_total[...] += mm_nt(gate_grad, gate_ref[...]) + mm_nt(up_grad, up_ref[...])
+
+    @pl.when(block == pl.num_programs(0) - 1)
+    def _():
+        out = out_total[...].astype(BF).astype(F32)
+        dot_ref[...] = jnp.sum(cot_ref[...].astype(F32) * out, axis=-1, keepdims=True)
+        gated_ref[...] = (gate_slot[:, :1] * out).astype(BF)
+        in_grad_ref[...] = in_total[...].astype(BF)
+
+
+def expert_chunk(here, in_chunk, cot_chunk, mask, router, weight):
+    rows = in_chunk.shape[0]
+    tile = 256
+    steps = FF // tile
+    whole = pl.BlockSpec((rows, D), lambda j, h: (0, 0))
+    piece = pl.BlockSpec((rows, tile), lambda j, h: (0, j))
+    low = jax.ShapeDtypeStruct((rows, FF), BF)
+    wide = jax.ShapeDtypeStruct((rows, D), BF)
+    return pl.pallas_call(
+        expert_kernel,
+        grid_spec=pltpu.PrefetchScalarGridSpec(
+            num_scalar_prefetch=1,
+            grid=(steps,),
+            in_specs=[
+                whole,
+                whole,
+                pl.BlockSpec(mask.shape, lambda j, h: (0, 0)),
+                pl.BlockSpec(router.shape, lambda j, h: (0, 0)),
+                pl.BlockSpec((D, tile), lambda j, h: (0, j)),
+                pl.BlockSpec((D, tile), lambda j, h: (0, steps + j)),
+                pl.BlockSpec((D, tile), lambda j, h: (0, 2 * steps + j)),
+            ],
+            out_specs=[
+                piece, piece, piece, whole, whole, whole,
+                pl.BlockSpec((rows, 1), lambda j, h: (0, 0)),
+            ],
+            scratch_shapes=[
+                pltpu.VMEM((rows, D), F32),
+                pltpu.VMEM((rows, D), F32),
+                pltpu.VMEM((rows, LANES), F32),
+            ],
+        ),
+        out_shape=[low, low, low, wide, wide, wide, jax.ShapeDtypeStruct((rows, 1), F32)],
+        compiler_params=pltpu.CompilerParams(vmem_limit_bytes=40 << 20),
+        cost_estimate=pl.CostEstimate(flops=1 << 20, bytes_accessed=1 << 20, transcendentals=0),
+        name="expert_chunk",
+    )(here, in_chunk, cot_chunk, mask, router, weight, weight, weight)
 
 
 def expert_grad_kernel(count, *refs):
-    in_refs, gu_refs = refs[:count], refs[count : 2 * count]
-    grad_refs, active_refs = refs[2 * count : 3 * count], refs[3 * count : 4 * count]
-    out_ref = refs[4 * count]
+    lists = [refs[k * count : (k + 1) * count] for k in range(5)]
+    out_ref = refs[5 * count]
     column = pl.program_id(1)
 
     def total(lefts, rights):
@@ -201,37 +294,26 @@
             found = found + mm_tn(left[...], right[...])
         out_ref[...] = found
 
-    @pl.when(column < 2)
-    def _():
-        total(in_refs, gu_refs)
-
-    @pl.when(column == 2)
-    def _():
-        total(grad_refs, active_refs)
-
-
-def expert_grads(in_rows, gu_grads, grad_rows, actives):
+    for place, (left, right) in enumerate(((0, 2), (0, 3), (1, 4))):
+        pl.when(column == place)(functools.partial(total, lists[left], lists[right]))
+
+
+def expert_grads(in_rows, grad_rows, gate_grads, up_grads, actives):
     count = len(in_rows)
     rows = in_rows[0].shape[0]
     tile = 512
     tall = pl.BlockSpec((rows, tile), lambda i, j: (0, i))
-    gate_up = pl.BlockSpec((rows, FF), lambda i, j: (0, jnp.minimum(j, 1)))
     whole = pl.BlockSpec((rows, FF), lambda i, j: (0, 0))
-    total_rows = rows * count
     return pl.pallas_call(
         functools.partial(expert_grad_kernel, count),
         grid=(D // tile, 3),
-        in_specs=[tall] * count + [gate_up] * count + [tall] * count + [whole] * count,
+        in_specs=[tall] * (2 * count) + [whole] * (3 * count),
         out_specs=pl.BlockSpec((tile, FF), lambda i, j: (i, j)),
         out_shape=jax.ShapeDtypeStruct((D, 3 * FF), F32),
         compiler_params=pltpu.CompilerParams(vmem_limit_bytes=48 << 20),
-        cost_estimate=pl.CostEstimate(
-            flops=1 << 20,
-            bytes_accessed=1 << 20,
-            transcendentals=0,
-        ),
+        cost_estimate=pl.CostEstimate(flops=1 << 20, bytes_accessed=1 << 20, transcendentals=0),
         name="expert_grads",
-    )(*in_rows, *gu_grads, *grad_rows, *actives)
+    )(*in_rows, *grad_rows, *gate_grads, *up_grads, *actives)
 
 
 def head_normed(raw, gain_ref):
@@ -394,8 +476,9 @@
     ).transpose(1, 0, 2)
     core_rows = KV_HEADS * qkv_rows
     half_rows = 2 * qkv_rows
-    qkv_far = far_all(quad_swap(wide).reshape(core_rows, width), far_count)
-    tokens, cotangent, qkv_far[1] = tie(tokens, cotangent, qkv_far[1])
+    wide_found = quad_parts(wide)
+    tokens, *wide_found = tie(tokens, *wide_found)
+    qkv_far = far_all(quad_order(wide_found).reshape(core_rows, width), far_count)
 
     tokens_both = quad_gather(tokens).reshape(2, ROW, D)
     table = jnp.concatenate([deal, jnp.pad(lengths, ((0, 0), (0, LANES - NSEG)))], axis=1)
@@ -429,23 +512,30 @@
 
     slab = NEAR * CORES * 2
     slab_index = (near_index * CORES + core_index) * 2 + seq_index
+    slab_ids = jnp.arange(slab, dtype=jnp.int32)
     out_order = jnp.array([0, 2, 1, 3, 4, 6, 5, 7], jnp.int32)
-    in_order = jnp.array([0, 1, 4, 5, 2, 3, 6, 7], jnp.int32)
     place_far = far_stack(far_all(place.T.astype(BF), far_count))
-    place_slab = jnp.take(
-        place_far, far_index * slab + lax.bitwise_xor(out_order, slab_index), axis=1
-    ).astype(jnp.int32)
-    chunk_slots = []
-    for step in range(far_count):
+
+    def slots_of(places, step):
         found = lax.dynamic_index_in_dim(
-            place_slab, lax.rem(far_index + far_count - step, far_count), 0, keepdims=False
+            places, lax.rem(far_index + far_count - step, far_count), 0, keepdims=False
         )
         found = found[:, None, :] == jnp.arange(capacity, dtype=jnp.int32)[None, :, None]
-        chunk_slots.append(found.astype(BF).reshape(slab * capacity, TOK_DEV))
+        return found.astype(BF).reshape(slab * capacity, TOK_DEV)
+
+    place_slab = lax.dynamic_slice_in_dim(place_far, far_index * slab, slab, axis=1).astype(jnp.int32)
+    turned_ids = lax.bitwise_xor(out_order, slab_index)
+    place_turned = jnp.sum(
+        jnp.where(
+            (turned_ids[:, None] == slab_ids[None, :])[None, :, :, None], place_slab[:, None], 0
+        ),
+        axis=2,
+    )
+    chunk_slots = [slots_of(place_slab, step) for step in range(far_count)]
+    send_slots = [slots_of(place_turned, step) for step in range(far_count)]
     chunk_steps = jnp.arange(far_count, dtype=jnp.int32)
     source_ids = (
-        lax.rem(far_index + far_count - chunk_steps, far_count)[:, None] * slab
-        + lax.bitwise_xor(in_order, slab_index)[None, :]
+        lax.rem(far_index + far_count - chunk_steps, far_count)[:, None] * slab + slab_ids[None, :]
     ).reshape(device_count)
     device_ids = jnp.arange(device_count, dtype=jnp.int32)
     found_at = jnp.sum(
@@ -483,9 +573,10 @@
     cot_pair = jnp.concatenate(pair_order(cotangent, swap(cotangent, SEQ_AXIS), SEQ_AXIS), axis=0)
     cot_low = mm(hot_half, cot_pair).astype(BF)
     cot_rows = cot_low.astype(F32)
-    qkv_own = far_stack(qkv_far)
-    cot_low, qkv_own = tie(cot_low, qkv_own)
-    qkv_own = qkv_own.reshape(far_count * NEAR, half_rows, width)
+    cot_low, qkv_far[2] = tie(cot_low, qkv_far[2])
+    cot_sent = mm(slot_low, cot_low).astype(BF).reshape(device_count, capacity, D)
+    cot_back = [exchange(cot_sent[:, :, : D // 2], ALL_AXES), exchange(cot_sent[:, :, D // 2 :], ALL_AXES)]
+    qkv_own = far_stack(qkv_far).reshape(far_count * NEAR, half_rows, width)
     qkv_mine = jnp.stack(pair_order(qkv_own, swap(qkv_own, CORE_AXIS), CORE_AXIS), axis=1).reshape(
         D, width
     )
@@ -494,14 +585,6 @@
         KV_HEADS, far_count // KV_HEADS * out_rows, D
     )
     far_part = far_count // KV_HEADS
-    cot_low, out_slabs = tie(cot_low, out_slabs)
-    cot_far = far_all(cot_low, far_count)
-    out_own = quad_swap(out_slabs).reshape(NEAR * 2, far_part, out_rows, D)
-    out_own = out_own.transpose(1, 0, 2, 3).reshape(far_part * NEAR, 2 * out_rows, D)
-    out_mine = jnp.stack(pair_order(out_own, swap(out_own, CORE_AXIS), CORE_AXIS), axis=1).reshape(
-        qcols, D
-    )
-
     x_both = lax.dot_general(
         dealt_hot, tokens_both, (((2,), (1,)), ((0,), (0,))), preferred_element_type=F32
     )
@@ -521,6 +604,14 @@
         deal_both[:, None, :],
     )
     mixed_low = attend(projected, shared, per_group)
+    out_found = quad_parts(out_slabs)
+    mixed_low, cot_back[0], *out_found = tie(mixed_low, cot_back[0], *out_found)
+    out_own = quad_order(out_found).reshape(NEAR * 2, far_part, out_rows, D)
+    out_own = out_own.transpose(1, 0, 2, 3).reshape(far_part * NEAR, 2 * out_rows, D)
+    out_mine = jnp.stack(pair_order(out_own, swap(out_own, CORE_AXIS), CORE_AXIS), axis=1).reshape(
+        qcols, D
+    )
+
     out_partial = mm(mixed_low, out_mine).astype(BF)
     residual = x_rows + quad_sum(out_partial.reshape(4, TOK_DEV, D))
 
@@ -533,73 +624,59 @@
 
     expert_weight = w_expert[0]
     expert_here = far_index * slab + slab_index
-    in_rows, gu_grads, grad_rows, actives, slot_dots, in_grads, partials = ([] for _ in range(7))
+    in_rows, gate_grads, up_grads, grad_rows, actives, slot_dots, gated_outs, in_grads, partials = (
+        [] for _ in range(9)
+    )
+    here = expert_here.reshape(1)
     far_rows = [ffn_in]
     for step in range(1, far_count):
         far_rows.append(far_next(far_rows[-1], far_count))
 
     def gather(step, source):
-        return mm(chunk_slots[step], jnp.concatenate([source, cot_far[step]], axis=1)).astype(BF)
+        return mm(send_slots[step], source).astype(BF)
 
     sent = gather(0, ffn_in)
 
     def combine(step):
-        back = slab_back(in_grads[step].reshape(2, 4, capacity, 2 * D)).reshape(slab * capacity, 2 * D)
+        back = exchange(in_grads[step].reshape(slab, capacity, D), SLAB_AXES)
+        back = back.reshape(slab * capacity, D)
         if step + 1 < far_count:
             back, actives[step + 1] = tie(back, actives[step + 1])
+        else:
+            back, slot_dots[0] = tie(back, slot_dots[0])
         return mm_tn(chunk_slots[step], back)
 
+    ffn_in, cot_back[1] = tie(ffn_in, cot_back[1])
+    cot_chunks = far_parts(
+        jnp.concatenate(cot_back, axis=2).reshape(far_count, slab * capacity, D), far_count
+    )
     for step in range(far_count):
-        arrived = slab_out(to_blocks(sent)).reshape(slab * capacity, 2 * D)
-        in_chunk, cot_chunk = arrived[:, :D], arrived[:, D:]
+        in_chunk = slab_out(to_blocks(sent)).reshape(slab * capacity, D)
+        cot_chunk = cot_chunks[step]
         if step + 1 < far_count:
             source = far_rows[step + 1]
             if step > 0:
-                source, gu_grads[step - 1] = tie(source, gu_grads[step - 1])
+                source, up_grads[step - 1] = tie(source, up_grads[step - 1])
             sent = gather(step + 1, source)
-        mask = mask_back[step]
-        slot_logits = jnp.where(mask > 0.5, mm(in_chunk, router_full), -1e30)
-        slot_probs = jnp.where(mask > 0.5, jax.nn.softmax(slot_logits, axis=-1), 0.0)
-        gate_slot = jnp.sum(
-            jnp.where(expert_ids == expert_here, slot_probs, 0.0), axis=1, keepdims=True
+        gate_grad, up_grad, active, grad_chunk, in_grad, gated_out, slot_dot = expert_chunk(
+            here, in_chunk, cot_chunk, mask_back[step], router_full, expert_weight
         )
-        gate_up = mm(in_chunk, expert_weight[:, : 2 * FF])
-        gate_pre = gate_up[:, :FF]
-        up_pre = gate_up[:, FF:]
-        sig_gate = jax.nn.sigmoid(gate_pre)
-        silu_val = gate_pre * sig_gate
-        active = (silu_val * up_pre).astype(BF)
-        expert_out = mm_nt(active, expert_weight[:, 2 * FF :]).astype(BF)
-        cot_float = cot_chunk.astype(F32)
-        slot_dots.append(jnp.sum(cot_float * expert_out.astype(F32), axis=1))
-        gated_out = (gate_slot * expert_out.astype(F32)).astype(BF)
-        grad_chunk = (gate_slot * cot_float).astype(BF)
-        act_grad = mm(grad_chunk, expert_weight[:, 2 * FF :])
-        silu_slope = sig_gate * (1.0 + gate_pre * (1.0 - sig_gate))
-        gu_grad = jnp.concatenate(
-            [act_grad * up_pre * silu_slope, act_grad * silu_val], axis=1
-        ).astype(BF)
-        in_grad = mm_nt(gu_grad, expert_weight[:, : 2 * FF]).astype(BF)
-        in_grads.append(jnp.concatenate([in_grad, gated_out], axis=1))
         in_rows.append(in_chunk)
-        gu_grads.append(gu_grad)
+        gate_grads.append(gate_grad)
+        up_grads.append(up_grad)
+        actives.append(active)
         grad_rows.append(grad_chunk)
-        actives.append(active)
+        in_grads.append(in_grad)
+        gated_outs.append(gated_out.reshape(slab, capacity, D))
+        slot_dots.append(slot_dot[:, 0])
         if step > 0:
             partials.append(combine(step - 1))
     partials.append(combine(far_count - 1))
-    from_experts = partials[0][:, :D]
-    for step in range(1, far_count):
-        from_experts = from_experts + far_shift(
-            partials[step][:, :D].astype(BF), -step, far_count
-        ).astype(F32)
-    out_parts = [part[:, D:] for part in partials]
-    from_experts, *out_parts = tie(from_experts, *out_parts)
-    out_sum = out_parts[0]
-    for step in range(1, far_count):
-        out_sum = out_sum + far_shift(out_parts[step].astype(BF), -step, far_count).astype(F32)
     dot_sent = jnp.take(jnp.stack(slot_dots).reshape(device_count, capacity), found_at, axis=0)
     dot_back = exchange(dot_sent[:, None, :], ALL_AXES).reshape(experts_all, capacity)
+    from_experts = partials[0]
+    for step in range(1, far_count):
+        from_experts = from_experts + far_shift(partials[step].astype(BF), -step, far_count).astype(F32)
 
     gate_grad = jnp.sum(jnp.where(slot_hot, dot_back[:, :, None], 0.0), axis=1).T
     mean_term = jnp.sum(gate_probs * gate_grad, axis=1, keepdims=True)
@@ -609,8 +686,14 @@
     resid_part, gain_ffn_grad = ffn_back(ffn_in_grad)
     resid_low = (cot_rows + resid_part).astype(BF)
 
+    gated_sent = far_stack(gated_outs).reshape(device_count, capacity, D)
+    gated_sent, resid_low = tie(gated_sent, resid_low)
+    returned = [
+        exchange(gated_sent[:, :, : D // 2], ALL_AXES).reshape(slot_count, D // 2),
+        exchange(gated_sent[:, :, D // 2 :], ALL_AXES).reshape(slot_count, D // 2),
+    ]
     in_rows[0], resid_low = tie(in_rows[0], resid_low)
-    grad_expert = expert_grads(in_rows, gu_grads, grad_rows, actives)[None]
+    grad_expert = expert_grads(in_rows, grad_rows, gate_grads, up_grads, actives)[None]
 
     resid_both, grad_expert = tie(quad_gather(resid_low), grad_expert)
     resid_both = resid_both.reshape(2 * ROW, D)
@@ -623,7 +706,7 @@
     resid_both, out_grad = tie(resid_both, out_grad)
     mixed_grad = mm_nt(resid_both, out_mine).astype(BF)
     out_grad = core_sum(out_grad.reshape(far_part * NEAR, CORES, 2 * out_rows, D))
-    mixed_grad, out_grad = tie(mixed_grad, out_grad)
+    mixed_grad, out_grad, returned[0] = tie(mixed_grad, out_grad, returned[0])
     out_grad = (
         out_grad.astype(BF)
         .reshape(far_part, NEAR * 2, out_rows, D)
@@ -634,10 +717,16 @@
     query_grad, key_grad, value_grad, query_gain_grad, key_gain_grad = attend_back(
         projected, shared, mixed_grad, per_group
     )
-    query_grad, out_grad, out_sum = tie(query_grad, out_grad, out_sum)
-    out_share = far_sum(out_grad, far_count)
+    query_grad, out_grad, returned[1] = tie(query_grad, out_grad, returned[1])
+    out_share = far_sum(far_parts(out_grad, far_count), far_count)
     proj_grad = jnp.concatenate([query_grad, key_grad, value_grad], axis=1)
-    final_rows = (residual + out_sum).astype(BF)
+    final_rows = jnp.concatenate(
+        [
+            (residual[:, : D // 2] + mm_tn(slot_low, returned[0])).astype(BF),
+            (residual[:, D // 2 :] + mm_tn(slot_low, returned[1])).astype(BF),
+        ],
+        axis=1,
+    )
     final_pair = jnp.concatenate(
         pair_order(final_rows, swap(final_rows, SEQ_AXIS), SEQ_AXIS), axis=0
     )
@@ -659,7 +748,9 @@
     grad_tokens = (mm_tn(back_half, resid_group) + input_part).astype(BF)
 
     qkv_grad = core_sum(qkv_grad.reshape(far_count * NEAR, CORES, half_rows, width))
-    qkv_grad = far_sum(qkv_grad.astype(BF).reshape(far_count, core_rows, width), far_count)
+    qkv_grad = far_sum(
+        far_parts(qkv_grad.astype(BF).reshape(far_count, core_rows, width), far_count), far_count
+    )
     qkv_grad = quad_swap(qkv_grad.astype(BF).reshape(KV_HEADS, qkv_rows, width))
     qkv_grad = qkv_grad.transpose(1, 0, 2).astype(F32)
     qkv_share = jnp.concatenate(

time: 737 us -> 705 us (0.957)
  waiting for transfers between devices: 354 us -> 238 us
  Pallas kernels: 58.7 us -> 98.8 us
  local copies, waits for them, and re-layouts: 49.1 us -> 82.6 us
  starting transfers between devices: 131 us -> 147 us
  matrix products: 65.7 us -> 54.7 us
    ppermute x24 -> x12, waiting for transfers between devices: 102 us -> 22.4 us  [quad_xor(): return lax.ppermute(value, HEAD_AXES, [(i, i ^ step) for i in range(4)])]
    ppermute x6 -> x0, waiting for transfers between devices: 67.9 us -> none  [far_sum(): lax.ppermute(block, FAR_AXIS, [(i, (i + step) % count) for i in range(cou...]
    pallas_call x0 -> x4, Pallas kernels: none -> 40.1 us  [expert_chunk(): pl.pallas_call(expert_kernel, grid_spec=pltpu.PrefetchScalarGridSpec(num_...]
    all_to_all x3 -> x11, starting transfers between devices: 11.9 us -> 51.7 us  [exchange(): return lax.all_to_all(value, axes, split_axis=0, concat_axis=0, tiled=True)]
    unnamed x210 -> x306, local copies, waits for them, and re-layouts: 11.5 us -> 41.7 us
    ppermute x6, waiting for transfers between devices: 4.79 us -> 32.6 us  [quad_gather(): lax.ppermute(value, HEAD_AXES, [(i, i ^ step) for i in range(4)])]
    ppermute x6 -> x0, starting transfers between devices: 19.5 us -> none  [far_sum(): lax.ppermute(block, FAR_AXIS, [(i, (i + step) % count) for i in range(cou...]
    ppermute x3, waiting for transfers between devices: 15.6 us -> 1.58 us  [far_next(): lax.ppermute(value, FAR_AXIS, [(i, (i + 1) % count) for i in range(count)])]
  transfers between devices with their start and end apart: 93 -> 79, of which waited for: 43 -> 32; matrix products, arithmetic and copies ran while one was open for 21% -> 22% of each run, Pallas kernels for 8% -> 14%
where the time goes in v5:
time: 705 us; the launch traced here: 694 us
  waiting for transfers between devices  238 us (34%)
  starting transfers between devices  147 us (21%)
  Pallas kernels  98.8 us (14%)
  local copies, waits for them, and re-layouts  82.6 us (12%)
  other arithmetic  68.7 us (10%)
  matrix products  54.7 us (8%)
    ppermute x18, waiting for transfers between devices, far_shift(): lax.ppermute(value, FAR_AXIS, [(i, (i + step) % count) for i in range(cou...  101 us
    ppermute x18, waiting for transfers between devices, quad_send(): return lax.ppermute(block, HEAD_AXES, [(i, i ^ step) for i in range(4)])  75 us
    all_to_all x11, starting transfers between devices, exchange(): return lax.all_to_all(value, axes, split_axis=0, concat_axis=0, tiled=True)  51.7 us
    dot_general x26, matrix products, dot(): lax.dot_general(left, right, (dims, ((), ())), preferred_element_type=F32)  50.4 us
    unnamed x306, local copies, waits for them, and re-layouts  41.7 us
    pallas_call x4, Pallas kernels, expert_chunk(): pl.pallas_call(expert_kernel, grid_spec=pltpu.PrefetchScalarGridSpec(num_...  40.1 us
    ppermute x18, starting transfers between devices, far_shift(): lax.ppermute(value, FAR_AXIS, [(i, (i + step) % count) for i in range(cou...  36.4 us
    ppermute x6, waiting for transfers between devices, quad_gather(): lax.ppermute(value, HEAD_AXES, [(i, i ^ step) for i in range(4)])  32.6 us
  transfers between devices with their start and end apart: 79, of which 32 were waited for; matrix products, arithmetic and copies ran while one was open for 22% of the time, Pallas kernels for 14%

profile of v5, /device:TPU:0, one launch (start us, length us, event | category | flops | bytes accessed | tf_op | source)
XLA Modules:
  0.0 693.8 jit_solution(950630743874823120)
XLA Ops:
  0.6 5.1 collective-permute-start.14
  25.9 5.2 all-to-all-start
  54.3 3.1 collective-permute-start.10
  58.6 4.9 collective-permute-done.6
  66.0 6.8 collective-permute-done.4
  74.5 13.1 %collective-permute-done.7 = bf16[256,1280]{1,0:T(8,128)(2,1)S(1)} collective-permute-done((bf16[256,1280]{1,0:T(8,128)(2,1)S(1)}, bf16[256,1280]{1,0:T(8,128)(2,1)S(1)}, u32[]{:S(2)}, u32[]{:S(2)}) %collective-permute-start.7) | collective-permute-done | bytes 655392 | tf_op jit(solution)/shard_map/ppermute | solution.py:183
  89.2 2.8 multiply_reduce_fusion
  92.9 17.3 %collective-permute-done.9 = bf16[256,1280]{1,0:T(8,128)(2,1)S(1)} collective-permute-done((bf16[256,1280]{1,0:T(8,128)(2,1)S(1)}, bf16[256,1280]{1,0:T(8,128)(2,1)S(1)}, u32[]{:S(2)}, u32[]{:S(2)}) %collective-permute-start.9) | collective-permute-done | bytes 655392 | tf_op jit(solution)/shard_map/ppermute | solution.py:183
  113.2 2.5 fusion.115
  115.6 5.2 all-to-all-start.1
  121.4 2.7 multiply_convert_fusion
  127.6 2.8 collective-permute-start.17
  131.1 2.9 select_bitcast_fusion.1
  134.5 4.4 fusion.124.query_ref.key_ref.value_ref
  138.9 16.4 %attend.1 = bf16[512,1024]{1,0:T(8,128)(2,1)} custom-call(f32[512,1280]{1,0:T(8,128)} %fusion.124.query_ref.key_ref.value_ref, f32[512,1280]{1,0:T(8,128)} %fusion.124.query_ref.key_ref.value_ref, f32[512,1280]{1,0:T(8,128)} %fusion.124.query_ref.key_ref.value_ref, f32[512,128]{1,0:T(8,128)} %pad_maximum_fusion.22.cos_ref, ...), custom_call_target="tpu_custom_call" | custom-call | flops 1048576 | bytes 1048576 | tf_op jit(solution)/shard_map/attend/pallas_call | solution.py:418
  155.7 13.0 %collective-permute-done.16 = bf16[128,2048]{1,0:T(8,128)(2,1)S(1)} collective-permute-done((bf16[128,2048]{1,0:T(8,128)(2,1)}, bf16[128,2048]{1,0:T(8,128)(2,1)S(1)}, u32[]{:S(2)}, u32[]{:S(2)}) %collective-permute-start.16) | collective-permute-done | bytes 524320 | tf_op jit(solution)/shard_map/ppermute | solution.py:102
  173.9 2.9 collective-permute-start.24
  178.3 5.4 all-to-all-start.2
  197.1 22.3 %collective-permute-done.19 = bf16[128,2048]{1,0:T(8,128)(2,1)} collective-permute-done((bf16[128,2048]{1,0:T(8,128)(2,1)}, bf16[128,2048]{1,0:T(8,128)(2,1)}, u32[]{:S(2)}, u32[]{:S(2)}) %collective-permute-start.19) | collective-permute-done | bytes 524320 | tf_op jit(solution)/shard_map/ppermute | solution.py:102
  219.4 13.2 %collective-permute-done.21 = bf16[128,2048]{1,0:T(8,128)(2,1)} collective-permute-done((bf16[128,2048]{1,0:T(8,128)(2,1)}, bf16[128,2048]{1,0:T(8,128)(2,1)}, u32[]{:S(2)}, u32[]{:S(2)}) %collective-permute-start.21) | collective-permute-done | bytes 524320 | tf_op jit(solution)/shard_map/ppermute | solution.py:102
  235.1 2.7 collective-permute-start.29
  241.9 2.7 pad_maximum_fusion.2
  246.5 5.1 collective-permute-done.26
  258.9 9.0 %collective-permute-done.31 = bf16[2,32,2048]{2,1,0:T(8,128)(2,1)S(1)} collective-permute-done((bf16[2,32,2048]{2,1,0:T(8,128)(2,1)S(1)}, bf16[2,32,2048]{2,1,0:T(8,128)(2,1)S(1)}, u32[]{:S(2)}, u32[]{:S(2)}) %collective-permute-start.31) | collective-permute-done | bytes 262176 | tf_op jit(solution)/shard_map/ppermute | solution.py:191
  270.4 10.4 %expert_chunk.4 = (bf16[256,768]{1,0:T(8,128)(2,1)S(1)}, bf16[256,768]{1,0:T(8,128)(2,1)S(1)}, bf16[256,768]{1,0:T(8,128)(2,1)S(1)}, bf16[256,2048]{1,0:T(8,128)...) custom-call(s32[1]{0:T(128)} %bitcast.82.here_ref, ...), custom_call_target="tpu_custom_call" | custom-call | flops 1048576 | bytes 1048576 | tf_op jit(solution)/shard_map/expert_chunk/pallas_call | solution.py:255
  283.5 4.2 all-to-all-start.3
  297.3 10.8 %expert_chunk.5 = (bf16[256,768]{1,0:T(8,128)(2,1)S(1)}, bf16[256,768]{1,0:T(8,128)(2,1)S(1)}, bf16[256,768]{1,0:T(8,128)(2,1)S(1)}, bf16[256,2048]{1,0:T(8,128)...) custom-call(s32[1]{0:T(128)} %bitcast.82.here_ref, ...), custom_call_target="tpu_custom_call" | custom-call | flops 1048576 | bytes 1048576 | tf_op jit(solution)/shard_map/expert_chunk/pallas_call | solution.py:255
  313.8 4.6 collective-permute-start.40
  319.4 5.2 collective-permute-done.41
  326.5 4.2 all-to-all-start.4
  331.9 2.5 broadcast_select_fusion.1
  336.0 9.4 %expert_chunk.6 = (bf16[256,768]{1,0:T(8,128)(2,1)S(1)}, bf16[256,768]{1,0:T(8,128)(2,1)S(1)}, bf16[256,768]{1,0:T(8,128)(2,1)S(1)}, bf16[256,2048]{1,0:T(8,128)...) custom-call(s32[1]{0:T(128)} %bitcast.82.here_ref, ...), custom_call_target="tpu_custom_call" | custom-call | flops 1048576 | bytes 1048576 | tf_op jit(solution)/shard_map/expert_chunk/pallas_call | solution.py:255
  351.4 4.9 all-to-all-start.5
  362.5 9.4 %expert_chunk.7 = (bf16[256,768]{1,0:T(8,128)(2,1)S(1)}, bf16[256,768]{1,0:T(8,128)(2,1)S(1)}, bf16[256,768]{1,0:T(8,128)(2,1)S(1)}, bf16[256,2048]{1,0:T(8,128)...) custom-call(s32[1]{0:T(128)} %bitcast.82.here_ref, ...), custom_call_target="tpu_custom_call" | custom-call | flops 1048576 | bytes 1048576 | tf_op jit(solution)/shard_map/expert_chunk/pallas_call | solution.py:255
  377.8 4.4 all-to-all-start.6
  383.9 2.6 fusion.125
  394.0 3.1 all-to-all-done.6
  398.6 3.3 all-to-all-start.7
  412.4 9.0 %collective-permute-done.46 = bf16[128,2048]{1,0:T(8,128)(2,1)} collective-permute-done((bf16[128,2048]{1,0:T(8,128)(2,1)}, bf16[128,2048]{1,0:T(8,128)(2,1)}, u32[]{:S(2)}, u32[]{:S(2)}) %collective-permute-start.46) | collective-permute-done | bytes 524320 | tf_op jit(solution)/shard_map/ppermute | solution.py:183
  421.4 21.7 %collective-permute-done.45 = bf16[128,2048]{1,0:T(8,128)(2,1)} collective-permute-done((bf16[128,2048]{1,0:T(8,128)(2,1)}, bf16[128,2048]{1,0:T(8,128)(2,1)}, u32[]{:S(2)}, u32[]{:S(2)}) %collective-permute-start.45) | collective-permute-done | bytes 524320 | tf_op jit(solution)/shard_map/ppermute | solution.py:183
  443.1 2.8 multiply_reduce_fusion.1
  447.1 2.5 fusion.114
  449.7 4.2 all-to-all-start.8
  453.8 2.8 collective-permute-start.49
  464.4 18.5 %expert_grads.1 = f32[2048,2304]{1,0:T(8,128)} custom-call(bf16[256,2048]{1,0:T(8,128)(2,1)S(1)} %bitcast.765, bf16[256,2048]{1,0:T(8,128)(2,1)} %bitcast.767, bf16[256,2048]{1,0:T(8,128)(2,1)} %bitcast.769, bf16[256,2048]{1,0:T(8,128)(2,1)} %bitcast.771, bf16[256,2048]{1,0:T(8,128)(2,1)} %copy-done.6, bf16[256,2048]{1,0:T(8,128)(2,1)} %copy-done.7, ...), custom_call_target="tpu_custom_call" | custom-call | flops 1048576 | bytes 1048576 | tf_op jit(solution)/shard_map/expert_grads/pallas_call | solution.py:307
  482.9 5.8 collective-permute-done.49
  488.7 13.0 %collective-permute-done.48 = bf16[128,2048]{1,0:T(8,128)(2,1)S(1)} collective-permute-done((bf16[128,2048]{1,0:T(8,128)(2,1)}, bf16[128,2048]{1,0:T(8,128)(2,1)S(1)}, u32[]{:S(2)}, u32[]{:S(2)}) %collective-permute-start.48) | collective-permute-done | bytes 524320 | tf_op jit(solution)/shard_map/ppermute | solution.py:114
  510.2 5.5 all-to-all-start.9
  515.8 6.3 convolution_convert_fusion.15.grad_ref
  522.1 3.0 convert_add_fusion.1
  533.0 23.8 %attend_back.1 = (bf16[512,1024]{1,0:T(8,128)(2,1)}, bf16[512,128]{1,0:T(8,128)(2,1)}, bf16[512,128]{1,0:T(8,128)(2,1)}, f32[1,128]{1,0:T(1,128)}, f32[1,128]{1,0:T(1,128)}) custom-call(f32[512,1280]{1,0:T(8,128)} %fusion.124.query_ref.key_ref.value_ref, f32[512,1280]{1,0:T(8,128)} %fusion.124.query_ref.key_ref.value_ref, ...), custom_call_target="tpu_custom_call" | custom-call | flops 1048576 | bytes 1048576 | tf_op jit(solution)/shard_map/attend_back/pallas_call | solution.py:433
  556.8 8.6 %collective-permute-done.53 = bf16[128,2048]{1,0:T(8,128)(2,1)S(1)} collective-permute-done((bf16[128,2048]{1,0:T(8,128)(2,1)}, bf16[128,2048]{1,0:T(8,128)(2,1)S(1)}, u32[]{:S(2)}, u32[]{:S(2)}) %collective-permute-start.53) | collective-permute-done | bytes 524320 | tf_op jit(solution)/shard_map/ppermute | solution.py:102
  571.2 3.2 convolution_convert_fusion
  584.6 3.3 collective-permute-start.54
  588.8 2.6 collective-permute-start.66
  591.4 5.6 convolution_convert_fusion.4
  600.7 2.8 fusion
  608.2 3.9 collective-permute-done.55
  612.1 2.9 collective-permute-start.65
  614.9 8.3 %collective-permute-done.57 = bf16[128,2048]{1,0:T(8,128)(2,1)S(1)} collective-permute-done((bf16[128,2048]{1,0:T(8,128)(2,1)S(1)}, bf16[128,2048]{1,0:T(8,128)(2,1)S(1)}, u32[]{:S(2)}, u32[]{:S(2)}) %collective-permute-start.57) | collective-permute-done | bytes 524320 | tf_op jit(solution)/shard_map/ppermute | solution.py:102
  626.8 5.1 all-to-all-start.10
  640.8 26.5 %collective-permute-done.59 = bf16[256,1280]{1,0:T(8,128)(2,1)S(1)} collective-permute-done((bf16[256,1280]{1,0:T(8,128)(2,1)}, bf16[256,1280]{1,0:T(8,128)(2,1)S(1)}, u32[]{:S(2)}, u32[]{:S(2)}) %collective-permute-start.59) | collective-permute-done | bytes 655392 | tf_op jit(solution)/shard_map/ppermute | solution.py:183
  667.3 12.3 %collective-permute-done.61 = bf16[256,1280]{1,0:T(8,128)(2,1)S(1)} collective-permute-done((bf16[256,1280]{1,0:T(8,128)(2,1)S(1)}, bf16[256,1280]{1,0:T(8,128)(2,1)S(1)}, u32[]{:S(2)}, u32[]{:S(2)}) %collective-permute-start.61) | collective-permute-done | bytes 655392 | tf_op jit(solution)/shard_map/ppermute | solution.py:183
  684.5 2.5 fusion.25
  (622 shorter events, 233.4 us)
Async XLA Ops:
  0.6 124.7 %collective-permute-start.14 = (bf16[128,2048]{1,0:T(8,128)(2,1)}, bf16[128,2048]{1,0:T(8,128)(2,1)}, u32[]{:S(2)}, u32[]{:S(2)}) collective-permute-start(bf16[128,2048]{1,0:T(8,128)(2,1)} %param.14), channel_id=1, source_target_pairs={{0,24},{8,0},{16,8},{24,16},{1,25},{9,1},{17,9},{25,17},{2,26},{10... | collective-permute-start | bytes 1572872 | tf_op jit(solution)/shard_map/ppermute | solution.py:183
  5.7 48.6 %collective-permute-start.12 = (bf16[128,2048]{1,0:T(8,128)(2,1)}, bf16[128,2048]{1,0:T(8,128)(2,1)}, u32[]{:S(2)}, u32[]{:S(2)}) collective-permute-start(bf16[128,2048]{1,0:T(8,128)(2,1)} %param.14), channel_id=1, source_target_pairs={{0,8},{8,16},{16,24},{24,0},{1,9},{9,17},{17,25},{25,1},{2,10},{10... | collective-permute-start | bytes 1572872 | tf_op jit(solution)/shard_map/ppermute | solution.py:183
  12.8 22.8 %collective-permute-start.1 = (bf16[64,1280]{1,0:T(8,128)(2,1)}, bf16[64,1280]{1,0:T(8,128)(2,1)}, u32[]{:S(2)}, u32[]{:S(2)}) collective-permute-start(bf16[64,1280]{1,0:T(8,128)(2,1)} %bitcast.758), channel_id=1, source_target_pairs={{0,1},{1,0},{4,5},{5,4},{2,3},{3,2},{6,7},{7,6},{8,9},{9,8},{12,13... | collective-permute-start | bytes 491528 | tf_op jit(solution)/shard_map/ppermute | solution.py:102
  15.0 22.3 %collective-permute-start.2 = (bf16[64,1280]{1,0:T(8,128)(2,1)}, bf16[64,1280]{1,0:T(8,128)(2,1)}, u32[]{:S(2)}, u32[]{:S(2)}) collective-permute-start(bf16[64,1280]{1,0:T(8,128)(2,1)} %bitcast.757), channel_id=1, source_target_pairs={{0,4},{1,5},{4,0},{5,1},{2,6},{3,7},{6,2},{7,3},{8,12},{9,13},{12,... | collective-permute-start | bytes 491528 | tf_op jit(solution)/shard_map/ppermute | solution.py:102
  18.9 18.4 %collective-permute-start.3 = (bf16[64,1280]{1,0:T(8,128)(2,1)}, bf16[64,1280]{1,0:T(8,128)(2,1)}, u32[]{:S(2)}, u32[]{:S(2)}) collective-permute-start(bf16[64,1280]{1,0:T(8,128)(2,1)} %bitcast.756), channel_id=1, source_target_pairs={{0,5},{1,4},{4,1},{5,0},{2,7},{3,6},{6,3},{7,2},{8,13},{9,12},{12,... | collective-permute-start | bytes 491528 | tf_op jit(solution)/shard_map/ppermute | solution.py:102
  25.9 17.1 %all-to-all-start = ((bf16[32,32,128]{2,1,0:T(8,128)(2,1)}), bf16[32,32,128]{2,1,0:T(8,128)(2,1)}, u32[]{:S(2)}, u32[]{:S(2)}) async-start(bf16[32,32,128]{2,1,0:T(8,128)(2,1)} %bitcast.285), calls=%async_computation | async-start | bytes 524288 | tf_op jit(solution)/shard_map/all_to_all | solution.py:93
  35.6 15.5 %collective-permute-start.8 = (bf16[128,2048]{1,0:T(8,128)(2,1)}, bf16[128,2048]{1,0:T(8,128)(2,1)}, u32[]{:S(2)}, u32[]{:S(2)}) collective-permute-start(bf16[128,2048]{1,0:T(8,128)(2,1)} %param.12), channel_id=1, source_target_pairs={{0,1},{1,0},{2,3},{3,2},{4,5},{5,4},{6,7},{7,6},{8,9},{9,8},{10,11... | collective-permute-start | bytes 1572872 | tf_op jit(solution)/shard_map/ppermute | solution.py:84
  37.3 26.2 %collective-permute-start.6 = (bf16[128,2048]{1,0:T(8,128)(2,1)S(1)}, bf16[128,2048]{1,0:T(8,128)(2,1)}, u32[]{:S(2)}, u32[]{:S(2)}) collective-permute-start(bf16[128,2048]{1,0:T(8,128)(2,1)S(1)} %copy-done.65), channel_id=1, source_target_pairs={{0,5},{1,4},{4,1},{5,0},{2,7},{3,6},{6,3},{7,2},{8,13},{9,12},{12,... | collective-permute-start | bytes 1572872 | tf_op jit(solution)/shard_map/ppermute | solution.py:114
  38.8 25.9 %collective-permute-start.5 = (bf16[128,2048]{1,0:T(8,128)(2,1)S(1)}, bf16[128,2048]{1,0:T(8,128)(2,1)}, u32[]{:S(2)}, u32[]{:S(2)}) collective-permute-start(bf16[128,2048]{1,0:T(8,128)(2,1)S(1)} %copy-done.65), channel_id=1, source_target_pairs={{0,4},{1,5},{4,0},{5,1},{2,6},{3,7},{6,2},{7,3},{8,12},{9,13},{12,... | collective-permute-start | bytes 1572872 | tf_op jit(solution)/shard_map/ppermute | solution.py:114
  51.0 21.8 %collective-permute-start.4 = (bf16[128,2048]{1,0:T(8,128)(2,1)S(1)}, bf16[128,2048]{1,0:T(8,128)(2,1)S(1)}, u32[]{:S(2)}, u32[]{:S(2)}) collective-permute-start(bf16[128,2048]{1,0:T(8,128)(2,1)S(1)} %copy-done.65), channel_id=1, source_target_pairs={{0,1},{1,0},{4,5},{5,4},{2,3},{3,2},{6,7},{7,6},{8,9},{9,8},{12,13... | collective-permute-start | bytes 1572872 | tf_op jit(solution)/shard_map/ppermute | solution.py:114
  54.3 56.7 %collective-permute-start.10 = (bf16[256,1280]{1,0:T(8,128)(2,1)S(1)}, bf16[256,1280]{1,0:T(8,128)(2,1)S(1)}, u32[]{:S(2)}, u32[]{:S(2)}) collective-permute-start(bf16[256,1280]{1,0:T(8,128)(2,1)S(1)} %bitcast.819), channel_id=1, source_target_pairs={{0,24},{8,0},{16,8},{24,16},{1,25},{9,1},{17,9},{25,17},{2,26},{10... | collective-permute-start | bytes 1966088 | tf_op jit(solution)/shard_map/ppermute | solution.py:183
  63.5 24.2 %collective-permute-start.7 = (bf16[256,1280]{1,0:T(8,128)(2,1)S(1)}, bf16[256,1280]{1,0:T(8,128)(2,1)S(1)}, u32[]{:S(2)}, u32[]{:S(2)}) collective-permute-start(bf16[256,1280]{1,0:T(8,128)(2,1)S(1)} %bitcast.820), channel_id=1, source_target_pairs={{0,8},{8,16},{16,24},{24,0},{1,9},{9,17},{17,25},{25,1},{2,10},{10... | collective-permute-start | bytes 1966088 | tf_op jit(solution)/shard_map/ppermute | solution.py:183
  64.7 59.4 %collective-permute-start.13 = (bf16[128,2048]{1,0:T(8,128)(2,1)}, bf16[128,2048]{1,0:T(8,128)(2,1)}, u32[]{:S(2)}, u32[]{:S(2)}) collective-permute-start(bf16[128,2048]{1,0:T(8,128)(2,1)} %collective-permute-done.12), channel_id=1, source_target_pairs={{0,8},{8,16},{16,24},{24,0},{1,9},{9,17},{17,25},{25,1},{2,10},{10... | collective-permute-start | bytes 1572872 | tf_op jit(solution)/shard_map/ppermute | solution.py:183
  87.7 22.5 %collective-permute-start.9 = (bf16[256,1280]{1,0:T(8,128)(2,1)S(1)}, bf16[256,1280]{1,0:T(8,128)(2,1)S(1)}, u32[]{:S(2)}, u32[]{:S(2)}) collective-permute-start(bf16[256,1280]{1,0:T(8,128)(2,1)S(1)} %collective-permute-done.7), channel_id=1, source_target_pairs={{0,8},{8,16},{16,24},{24,0},{1,9},{9,17},{17,25},{25,1},{2,10},{10... | collective-permute-start | bytes 1966088 | tf_op jit(solution)/shard_map/ppermute | solution.py:183
  111.9 19.2 %collective-permute-start.11 = (bf16[8,128,1280]{2,1,0:T(8,128)(2,1)}, bf16[8,128,1280]{2,1,0:T(8,128)(2,1)}, u32[]{:S(2)}, u32[]{:S(2)}) collective-permute-start(bf16[8,128,1280]{2,1,0:T(8,128)(2,1)} %bitcast.22), channel_id=1, source_target_pairs={{0,2},{2,0},{1,3},{3,1},{4,6},{6,4},{5,7},{7,5},{8,10},{10,8},{9,1... | collective-permute-start | bytes 7864328 | tf_op jit(solution)/shard_map/ppermute | solution.py:84
  115.6 55.1 %all-to-all-start.1 = ((bf16[32,32,1024]{2,1,0:T(8,128)(2,1)}), bf16[32,32,1024]{2,1,0:T(8,128)(2,1)}, u32[]{:S(2)}, u32[]{:S(2)}) async-start(bf16[32,32,1024]{2,1,0:T(8,128)(2,1)} %get-tuple-element.213), calls=%async_computation.1 | async-start | bytes 4194304 | tf_op jit(solution)/shard_map/all_to_all | solution.py:93
  127.6 28.0 %collective-permute-start.17 = (bf16[128,2048]{1,0:T(8,128)(2,1)}, bf16[128,2048]{1,0:T(8,128)(2,1)S(1)}, u32[]{:S(2)}, u32[]{:S(2)}) collective-permute-start(bf16[128,2048]{1,0:T(8,128)(2,1)} %get-tuple-element.241), channel_id=1, source_target_pairs={{0,5},{1,4},{4,1},{5,0},{2,7},{3,6},{6,3},{7,2},{8,13},{9,12},{12,... | collective-permute-start | bytes 1572872 | tf_op jit(solution)/shard_map/ppermute | solution.py:102
  130.4 38.3 %collective-permute-start.16 = (bf16[128,2048]{1,0:T(8,128)(2,1)}, bf16[128,2048]{1,0:T(8,128)(2,1)S(1)}, u32[]{:S(2)}, u32[]{:S(2)}) collective-permute-start(bf16[128,2048]{1,0:T(8,128)(2,1)} %get-tuple-element.242), channel_id=1, source_target_pairs={{0,4},{1,5},{4,0},{5,1},{2,6},{3,7},{6,2},{7,3},{8,12},{9,13},{12,... | collective-permute-start | bytes 1572872 | tf_op jit(solution)/shard_map/ppermute | solution.py:102
  131.0 39.7 %collective-permute-start.15 = (bf16[128,2048]{1,0:T(8,128)(2,1)S(1)}, bf16[128,2048]{1,0:T(8,128)(2,1)S(1)}, u32[]{:S(2)}, u32[]{:S(2)}) collective-permute-start(bf16[128,2048]{1,0:T(8,128)(2,1)S(1)} %get-tuple-element.243), channel_id=1, source_target_pairs={{0,1},{1,0},{4,5},{5,4},{2,3},{3,2},{6,7},{7,6},{8,9},{9,8},{12,13... | collective-permute-start | bytes 1572872 | tf_op jit(solution)/shard_map/ppermute | solution.py:102
  178.3 59.5 %all-to-all-start.2 = ((bf16[32,32,1024]{2,1,0:T(8,128)(2,1)}), bf16[32,32,1024]{2,1,0:T(8,128)(2,1)}, u32[]{:S(2)}, u32[]{:S(2)}) async-start(bf16[32,32,1024]{2,1,0:T(8,128)(2,1)} %get-tuple-element.212), calls=%async_computation.2 | async-start | bytes 4194304 | tf_op jit(solution)/shard_map/all_to_all | solution.py:93
  190.6 28.8 %collective-permute-start.19 = (bf16[128,2048]{1,0:T(8,128)(2,1)}, bf16[128,2048]{1,0:T(8,128)(2,1)}, u32[]{:S(2)}, u32[]{:S(2)}) collective-permute-start(bf16[128,2048]{1,0:T(8,128)(2,1)} %get-tuple-element.234), channel_id=1, source_target_pairs={{0,1},{1,0},{4,5},{5,4},{2,3},{3,2},{6,7},{7,6},{8,9},{9,8},{12,13... | collective-permute-start | bytes 1572872 | tf_op jit(solution)/shard_map/ppermute | solution.py:102
  192.3 40.2 %collective-permute-start.21 = (bf16[128,2048]{1,0:T(8,128)(2,1)}, bf16[128,2048]{1,0:T(8,128)(2,1)}, u32[]{:S(2)}, u32[]{:S(2)}) collective-permute-start(bf16[128,2048]{1,0:T(8,128)(2,1)} %get-tuple-element.235), channel_id=1, source_target_pairs={{0,5},{1,4},{4,1},{5,0},{2,7},{3,6},{6,3},{7,2},{8,13},{9,12},{12,... | collective-permute-start | bytes 1572872 | tf_op jit(solution)/shard_map/ppermute | solution.py:102
  193.8 38.8 %collective-permute-start.20 = (bf16[128,2048]{1,0:T(8,128)(2,1)S(1)}, bf16[128,2048]{1,0:T(8,128)(2,1)}, u32[]{:S(2)}, u32[]{:S(2)}) collective-permute-start(bf16[128,2048]{1,0:T(8,128)(2,1)S(1)} %get-tuple-element.236), channel_id=1, source_target_pairs={{0,4},{1,5},{4,0},{5,1},{2,6},{3,7},{6,2},{7,3},{8,12},{9,13},{12,... | collective-permute-start | bytes 1572872 | tf_op jit(solution)/shard_map/ppermute | solution.py:102
  235.1 17.9 %collective-permute-start.29 = (bf16[128,2048]{1,0:T(8,128)(2,1)S(1)}, bf16[128,2048]{1,0:T(8,128)(2,1)S(1)}, u32[]{:S(2)}, u32[]{:S(2)}) collective-permute-start(bf16[128,2048]{1,0:T(8,128)(2,1)S(1)} %multiply_convert_fusion.1), channel_id=1, source_target_pairs={{0,8},{8,16},{16,24},{24,0},{1,9},{9,17},{17,25},{25,1},{2,10},{10... | collective-permute-start | bytes 1572872 | tf_op jit(solution)/shard_map/ppermute | solution.py:187
  238.4 13.3 %collective-permute-start.26 = (bf16[2,32,2048]{2,1,0:T(8,128)(2,1)S(1)}, bf16[2,32,2048]{2,1,0:T(8,128)(2,1)S(1)}, u32[]{:S(2)}, u32[]{:S(2)}) collective-permute-start(bf16[2,32,2048]{2,1,0:T(8,128)(2,1)S(1)} %bitcast.854), channel_id=1, source_target_pairs={{0,4},{1,5},{4,0},{5,1},{2,6},{3,7},{6,2},{7,3},{8,12},{9,13},{12,... | collective-permute-start | bytes 786440 | tf_op jit(solution)/shard_map/ppermute | solution.py:191
  253.0 17.1 %collective-permute-start.28 = (bf16[4,32,2048]{2,1,0:T(8,128)(2,1)S(1)}, bf16[4,32,2048]{2,1,0:T(8,128)(2,1)S(1)}, u32[]{:S(2)}, u32[]{:S(2)}) collective-permute-start(bf16[4,32,2048]{2,1,0:T(8,128)(2,1)S(1)} %pad_maximum_fusion.14), channel_id=1, source_target_pairs={{0,2},{2,0},{1,3},{3,1},{4,6},{6,4},{5,7},{7,5},{8,10},{10,8},{9,1... | collective-permute-start | bytes 1572872 | tf_op jit(solution)/shard_map/ppermute | solution.py:84
  253.6 14.4 %collective-permute-start.31 = (bf16[2,32,2048]{2,1,0:T(8,128)(2,1)S(1)}, bf16[2,32,2048]{2,1,0:T(8,128)(2,1)S(1)}, u32[]{:S(2)}, u32[]{:S(2)}) collective-permute-start(bf16[2,32,2048]{2,1,0:T(8,128)(2,1)S(1)} %bitcast.852), channel_id=1, source_target_pairs={{0,4},{1,5},{4,0},{5,1},{2,6},{3,7},{6,2},{7,3},{8,12},{9,13},{12,... | collective-permute-start | bytes 786440 | tf_op jit(solution)/shard_map/ppermute | solution.py:191
  254.3 13.6 %collective-permute-start.32 = (bf16[2,32,2048]{2,1,0:T(8,128)(2,1)S(1)}, bf16[2,32,2048]{2,1,0:T(8,128)(2,1)S(1)}, u32[]{:S(2)}, u32[]{:S(2)}) collective-permute-start(bf16[2,32,2048]{2,1,0:T(8,128)(2,1)S(1)} %bitcast.850), channel_id=1, source_target_pairs={{0,5},{1,4},{4,1},{5,0},{2,7},{3,6},{6,3},{7,2},{8,13},{9,12},{12,... | collective-permute-start | bytes 786440 | tf_op jit(solution)/shard_map/ppermute | solution.py:191
  256.1 13.1 %collective-permute-start.30 = (bf16[2,32,2048]{2,1,0:T(8,128)(2,1)S(1)}, bf16[2,32,2048]{2,1,0:T(8,128)(2,1)S(1)}, u32[]{:S(2)}, u32[]{:S(2)}) collective-permute-start(bf16[2,32,2048]{2,1,0:T(8,128)(2,1)S(1)} %bitcast.849), channel_id=1, source_target_pairs={{0,1},{1,0},{4,5},{5,4},{2,3},{3,2},{6,7},{7,6},{8,9},{9,8},{12,13... | collective-permute-start | bytes 786440 | tf_op jit(solution)/shard_map/ppermute | solution.py:191
  257.2 31.7 %collective-permute-start.34 = (bf16[128,2048]{1,0:T(8,128)(2,1)S(1)}, bf16[128,2048]{1,0:T(8,128)(2,1)}, u32[]{:S(2)}, u32[]{:S(2)}) collective-permute-start(bf16[128,2048]{1,0:T(8,128)(2,1)S(1)} %collective-permute-done.29), channel_id=1, source_target_pairs={{0,8},{8,16},{16,24},{24,0},{1,9},{9,17},{17,25},{25,1},{2,10},{10... | collective-permute-start | bytes 1572872 | tf_op jit(solution)/shard_map/ppermute | solution.py:187
  270.1 25.8 %collective-permute-start.33 = (bf16[4,32,2048]{2,1,0:T(8,128)(2,1)}, bf16[4,32,2048]{2,1,0:T(8,128)(2,1)}, u32[]{:S(2)}, u32[]{:S(2)}) collective-permute-start(bf16[4,32,2048]{2,1,0:T(8,128)(2,1)} %pad_maximum_fusion.16), channel_id=1, source_target_pairs={{0,2},{2,0},{1,3},{3,1},{4,6},{6,4},{5,7},{7,5},{8,10},{10,8},{9,1... | collective-permute-start | bytes 1572872 | tf_op jit(solution)/shard_map/ppermute | solution.py:84
  283.5 43.0 %all-to-all-start.3 = ((bf16[8,32,2048]{2,1,0:T(8,128)(2,1)}), bf16[8,32,2048]{2,1,0:T(8,128)(2,1)}, u32[]{:S(2)}, u32[]{:S(2)}) async-start(bf16[8,32,2048]{2,1,0:T(8,128)(2,1)} %bitcast.169), calls=%async_computation.3 | async-start | bytes 2097152 | tf_op jit(solution)/shard_map/all_to_all | solution.py:93
  290.4 23.4 %collective-permute-start.36 = (bf16[2,32,2048]{2,1,0:T(8,128)(2,1)S(1)}, bf16[2,32,2048]{2,1,0:T(8,128)(2,1)S(1)}, u32[]{:S(2)}, u32[]{:S(2)}) collective-permute-start(bf16[2,32,2048]{2,1,0:T(8,128)(2,1)S(1)} %bitcast.845), channel_id=1, source_target_pairs={{0,4},{1,5},{4,0},{5,1},{2,6},{3,7},{6,2},{7,3},{8,12},{9,13},{12,... | collective-permute-start | bytes 786440 | tf_op jit(solution)/shard_map/ppermute | solution.py:191
  292.4 26.0 %collective-permute-start.37 = (bf16[2,32,2048]{2,1,0:T(8,128)(2,1)S(1)}, bf16[2,32,2048]{2,1,0:T(8,128)(2,1)S(1)}, u32[]{:S(2)}, u32[]{:S(2)}) collective-permute-start(bf16[2,32,2048]{2,1,0:T(8,128)(2,1)S(1)} %bitcast.844), channel_id=1, source_target_pairs={{0,5},{1,4},{4,1},{5,0},{2,7},{3,6},{6,3},{7,2},{8,13},{9,12},{12,... | collective-permute-start | bytes 786440 | tf_op jit(solution)/shard_map/ppermute | solution.py:191
  293.8 24.6 %collective-permute-start.35 = (bf16[2,32,2048]{2,1,0:T(8,128)(2,1)S(1)}, bf16[2,32,2048]{2,1,0:T(8,128)(2,1)S(1)}, u32[]{:S(2)}, u32[]{:S(2)}) collective-permute-start(bf16[2,32,2048]{2,1,0:T(8,128)(2,1)S(1)} %bitcast.843), channel_id=1, source_target_pairs={{0,1},{1,0},{4,5},{5,4},{2,3},{3,2},{6,7},{7,6},{8,9},{9,8},{12,13... | collective-permute-start | bytes 786440 | tf_op jit(solution)/shard_map/ppermute | solution.py:191
  294.0 15.7 %collective-permute-start.39 = (bf16[128,2048]{1,0:T(8,128)(2,1)}, bf16[128,2048]{1,0:T(8,128)(2,1)S(1)}, u32[]{:S(2)}, u32[]{:S(2)}) collective-permute-start(bf16[128,2048]{1,0:T(8,128)(2,1)} %collective-permute-done.34), channel_id=1, source_target_pairs={{0,8},{8,16},{16,24},{24,0},{1,9},{9,17},{17,25},{25,1},{2,10},{10... | collective-permute-start | bytes 1572872 | tf_op jit(solution)/shard_map/ppermute | solution.py:187
  310.2 14.4 %collective-permute-start.41 = (bf16[2,32,2048]{2,1,0:T(8,128)(2,1)S(1)}, bf16[2,32,2048]{2,1,0:T(8,128)(2,1)S(1)}, u32[]{:S(2)}, u32[]{:S(2)}) collective-permute-start(bf16[2,32,2048]{2,1,0:T(8,128)(2,1)S(1)} %bitcast.848), channel_id=1, source_target_pairs={{0,4},{1,5},{4,0},{5,1},{2,6},{3,7},{6,2},{7,3},{8,12},{9,13},{12,... | collective-permute-start | bytes 786440 | tf_op jit(solution)/shard_map/ppermute | solution.py:191
  326.5 24.9 %all-to-all-start.4 = ((bf16[8,32,2048]{2,1,0:T(8,128)(2,1)}), bf16[8,32,2048]{2,1,0:T(8,128)(2,1)}, u32[]{:S(2)}, u32[]{:S(2)}) async-start(bf16[8,32,2048]{2,1,0:T(8,128)(2,1)} %bitcast.173), calls=%async_computation.4 | async-start | bytes 2097152 | tf_op jit(solution)/shard_map/all_to_all | solution.py:93
  351.4 26.4 %all-to-all-start.5 = ((bf16[8,32,2048]{2,1,0:T(8,128)(2,1)}), bf16[8,32,2048]{2,1,0:T(8,128)(2,1)}, u32[]{:S(2)}, u32[]{:S(2)}) async-start(bf16[8,32,2048]{2,1,0:T(8,128)(2,1)} %bitcast.776), calls=%async_computation.5 | async-start | bytes 2097152 | tf_op jit(solution)/shard_map/all_to_all | solution.py:93
  377.8 19.3 %all-to-all-start.6 = ((bf16[8,32,2048]{2,1,0:T(8,128)(2,1)}), bf16[8,32,2048]{2,1,0:T(8,128)(2,1)}, u32[]{:S(2)}, u32[]{:S(2)}) async-start(bf16[8,32,2048]{2,1,0:T(8,128)(2,1)} %bitcast.777), calls=%async_computation.6 | async-start | bytes 2097152 | tf_op jit(solution)/shard_map/all_to_all | solution.py:93
  389.7 22.7 %collective-permute-start.44 = (bf16[128,2048]{1,0:T(8,128)(2,1)}, bf16[128,2048]{1,0:T(8,128)(2,1)}, u32[]{:S(2)}, u32[]{:S(2)}) collective-permute-start(bf16[128,2048]{1,0:T(8,128)(2,1)} %convolution_convert_fusion.13), channel_id=1, source_target_pairs={{0,24},{8,0},{16,8},{24,16},{1,25},{9,1},{17,9},{25,17},{2,26},{10... | collective-permute-start | bytes 1572872 | tf_op jit(solution)/shard_map/ppermute | solution.py:183
  398.6 13.4 %all-to-all-start.7 = ((f32[32,1,32]{2,1,0:T(1,128)}), f32[32,1,32]{2,1,0:T(1,128)S(1)}, u32[]{:S(2)}, u32[]{:S(2)}) async-start(f32[32,1,32]{2,1,0:T(1,128)} %bitcast.187), calls=%async_computation.7 | async-start | bytes 32768 | tf_op jit(solution)/shard_map/all_to_all | solution.py:93
  404.4 17.0 %collective-permute-start.46 = (bf16[128,2048]{1,0:T(8,128)(2,1)}, bf16[128,2048]{1,0:T(8,128)(2,1)}, u32[]{:S(2)}, u32[]{:S(2)}) collective-permute-start(bf16[128,2048]{1,0:T(8,128)(2,1)} %convolution_convert_fusion.11), channel_id=1, source_target_pairs={{0,8},{8,16},{16,24},{24,0},{1,9},{9,17},{17,25},{25,1},{2,10},{10... | collective-permute-start | bytes 1572872 | tf_op jit(solution)/shard_map/ppermute | solution.py:183
  408.6 34.5 %collective-permute-start.45 = (bf16[128,2048]{1,0:T(8,128)(2,1)}, bf16[128,2048]{1,0:T(8,128)(2,1)}, u32[]{:S(2)}, u32[]{:S(2)}) collective-permute-start(bf16[128,2048]{1,0:T(8,128)(2,1)} %convolution_convert_fusion.12), channel_id=1, source_target_pairs={{0,16},{8,24},{16,0},{24,8},{1,17},{9,25},{17,1},{25,9},{2,18},{10... | collective-permute-start | bytes 1572872 | tf_op jit(solution)/shard_map/ppermute | solution.py:183
  449.7 60.6 %all-to-all-start.8 = ((bf16[32,32,1024]{2,1,0:T(8,128)(2,1)}), bf16[32,32,1024]{2,1,0:T(8,128)(2,1)}, u32[]{:S(2)}, u32[]{:S(2)}) async-start(bf16[32,32,1024]{2,1,0:T(8,128)(2,1)} %get-tuple-element.207), calls=%async_computation.8 | async-start | bytes 4194304 | tf_op jit(solution)/shard_map/all_to_all | solution.py:93
  453.8 34.8 %collective-permute-start.49 = (bf16[128,2048]{1,0:T(8,128)(2,1)}, bf16[128,2048]{1,0:T(8,128)(2,1)S(1)}, u32[]{:S(2)}, u32[]{:S(2)}) collective-permute-start(bf16[128,2048]{1,0:T(8,128)(2,1)} %fusion.13), channel_id=1, source_target_pairs={{0,5},{1,4},{4,1},{5,0},{2,7},{3,6},{6,3},{7,2},{8,13},{9,12},{12,... | collective-permute-start | bytes 1572872 | tf_op jit(solution)/shard_map/ppermute | solution.py:114
  456.7 45.0 %collective-permute-start.48 = (bf16[128,2048]{1,0:T(8,128)(2,1)}, bf16[128,2048]{1,0:T(8,128)(2,1)S(1)}, u32[]{:S(2)}, u32[]{:S(2)}) collective-permute-start(bf16[128,2048]{1,0:T(8,128)(2,1)} %fusion.13), channel_id=1, source_target_pairs={{0,4},{1,5},{4,0},{5,1},{2,6},{3,7},{6,2},{7,3},{8,12},{9,13},{12,... | collective-permute-start | bytes 1572872 | tf_op jit(solution)/shard_map/ppermute | solution.py:114
  457.3 46.5 %collective-permute-start.47 = (bf16[128,2048]{1,0:T(8,128)(2,1)}, bf16[128,2048]{1,0:T(8,128)(2,1)S(1)}, u32[]{:S(2)}, u32[]{:S(2)}) collective-permute-start(bf16[128,2048]{1,0:T(8,128)(2,1)} %fusion.13), channel_id=1, source_target_pairs={{0,1},{1,0},{4,5},{5,4},{2,3},{3,2},{6,7},{7,6},{8,9},{9,8},{12,13... | collective-permute-start | bytes 1572872 | tf_op jit(solution)/shard_map/ppermute | solution.py:114
  510.2 58.2 %all-to-all-start.9 = ((bf16[32,32,1024]{2,1,0:T(8,128)(2,1)}), bf16[32,32,1024]{2,1,0:T(8,128)(2,1)S(1)}, u32[]{:S(2)}, u32[]{:S(2)}) async-start(bf16[32,32,1024]{2,1,0:T(8,128)(2,1)} %get-tuple-element.206), calls=%async_computation.9 | async-start | bytes 4194304 | tf_op jit(solution)/shard_map/all_to_all | solution.py:93
  527.7 29.2 %collective-permute-start.51 = (bf16[128,2048]{1,0:T(8,128)(2,1)}, bf16[128,2048]{1,0:T(8,128)(2,1)S(1)}, u32[]{:S(2)}, u32[]{:S(2)}) collective-permute-start(bf16[128,2048]{1,0:T(8,128)(2,1)} %get-tuple-element.227), channel_id=1, source_target_pairs={{0,1},{1,0},{4,5},{5,4},{2,3},{3,2},{6,7},{7,6},{8,9},{9,8},{12,13... | collective-permute-start | bytes 1572872 | tf_op jit(solution)/shard_map/ppermute | solution.py:102
  529.5 35.9 %collective-permute-start.53 = (bf16[128,2048]{1,0:T(8,128)(2,1)}, bf16[128,2048]{1,0:T(8,128)(2,1)S(1)}, u32[]{:S(2)}, u32[]{:S(2)}) collective-permute-start(bf16[128,2048]{1,0:T(8,128)(2,1)} %get-tuple-element.228), channel_id=1, source_target_pairs={{0,5},{1,4},{4,1},{5,0},{2,7},{3,6},{6,3},{7,2},{8,13},{9,12},{12,... | collective-permute-start | bytes 1572872 | tf_op jit(solution)/shard_map/ppermute | solution.py:102
  531.0 34.4 %collective-permute-start.52 = (bf16[128,2048]{1,0:T(8,128)(2,1)}, bf16[128,2048]{1,0:T(8,128)(2,1)}, u32[]{:S(2)}, u32[]{:S(2)}) collective-permute-start(bf16[128,2048]{1,0:T(8,128)(2,1)} %get-tuple-element.229), channel_id=1, source_target_pairs={{0,4},{1,5},{4,0},{5,1},{2,6},{3,7},{6,2},{7,3},{8,12},{9,13},{12,... | collective-permute-start | bytes 1572872 | tf_op jit(solution)/shard_map/ppermute | solution.py:102
  577.6 20.9 %collective-permute-start.58 = (bf16[8,128,1280]{2,1,0:T(8,128)(2,1)}, bf16[8,128,1280]{2,1,0:T(8,128)(2,1)}, u32[]{:S(2)}, u32[]{:S(2)}) collective-permute-start(bf16[8,128,1280]{2,1,0:T(8,128)(2,1)} %fusion.3), channel_id=1, source_target_pairs={{0,2},{2,0},{1,3},{3,1},{4,6},{6,4},{5,7},{7,5},{8,10},{10,8},{9,1... | collective-permute-start | bytes 7864328 | tf_op jit(solution)/shard_map/ppermute | solution.py:84
  584.6 52.6 %collective-permute-start.54 = (bf16[128,2048]{1,0:T(8,128)(2,1)}, bf16[128,2048]{1,0:T(8,128)(2,1)}, u32[]{:S(2)}, u32[]{:S(2)}) collective-permute-start(bf16[128,2048]{1,0:T(8,128)(2,1)} %pad_maximum_fusion.21), channel_id=1, source_target_pairs={{0,1},{1,0},{2,3},{3,2},{4,5},{5,4},{6,7},{7,6},{8,9},{9,8},{10,11... | collective-permute-start | bytes 1572872 | tf_op jit(solution)/shard_map/ppermute | solution.py:84
  588.8 16.1 %collective-permute-start.66 = (bf16[128,2048]{1,0:T(8,128)(2,1)S(1)}, bf16[128,2048]{1,0:T(8,128)(2,1)S(1)}, u32[]{:S(2)}, u32[]{:S(2)}) collective-permute-start(bf16[128,2048]{1,0:T(8,128)(2,1)S(1)} %get-tuple-element.223), channel_id=1, source_target_pairs={{0,24},{8,0},{16,8},{24,16},{1,25},{9,1},{17,9},{25,17},{2,26},{10... | collective-permute-start | bytes 1572872 | tf_op jit(solution)/shard_map/ppermute | solution.py:183
  597.2 14.9 %collective-permute-start.55 = (bf16[128,2048]{1,0:T(8,128)(2,1)S(1)}, bf16[128,2048]{1,0:T(8,128)(2,1)S(1)}, u32[]{:S(2)}, u32[]{:S(2)}) collective-permute-start(bf16[128,2048]{1,0:T(8,128)(2,1)S(1)} %get-tuple-element.224), channel_id=1, source_target_pairs={{0,1},{1,0},{4,5},{5,4},{2,3},{3,2},{6,7},{7,6},{8,9},{9,8},{12,13... | collective-permute-start | bytes 1572872 | tf_op jit(solution)/shard_map/ppermute | solution.py:102
  597.5 25.7 %collective-permute-start.57 = (bf16[128,2048]{1,0:T(8,128)(2,1)S(1)}, bf16[128,2048]{1,0:T(8,128)(2,1)S(1)}, u32[]{:S(2)}, u32[]{:S(2)}) collective-permute-start(bf16[128,2048]{1,0:T(8,128)(2,1)S(1)} %get-tuple-element.225), channel_id=1, source_target_pairs={{0,5},{1,4},{4,1},{5,0},{2,7},{3,6},{6,3},{7,2},{8,13},{9,12},{12,... | collective-permute-start | bytes 1572872 | tf_op jit(solution)/shard_map/ppermute | solution.py:102
  598.5 26.7 %collective-permute-start.56 = (bf16[128,2048]{1,0:T(8,128)(2,1)S(1)}, bf16[128,2048]{1,0:T(8,128)(2,1)S(1)}, u32[]{:S(2)}, u32[]{:S(2)}) collective-permute-start(bf16[128,2048]{1,0:T(8,128)(2,1)S(1)} %get-tuple-element.226), channel_id=1, source_target_pairs={{0,4},{1,5},{4,0},{5,1},{2,6},{3,7},{6,2},{7,3},{8,12},{9,13},{12,... | collective-permute-start | bytes 1572872 | tf_op jit(solution)/shard_map/ppermute | solution.py:102
  604.9 28.9 %collective-permute-start.60 = (bf16[256,1280]{1,0:T(8,128)(2,1)}, bf16[256,1280]{1,0:T(8,128)(2,1)S(1)}, u32[]{:S(2)}, u32[]{:S(2)}) collective-permute-start(bf16[256,1280]{1,0:T(8,128)(2,1)} %get-tuple-element.221), channel_id=1, source_target_pairs={{0,24},{8,0},{16,8},{24,16},{1,25},{9,1},{17,9},{25,17},{2,26},{10... | collective-permute-start | bytes 1966088 | tf_op jit(solution)/shard_map/ppermute | solution.py:183
  612.1 72.4 %collective-permute-start.65 = (bf16[128,2048]{1,0:T(8,128)(2,1)}, bf16[128,2048]{1,0:T(8,128)(2,1)}, u32[]{:S(2)}, u32[]{:S(2)}) collective-permute-start(bf16[128,2048]{1,0:T(8,128)(2,1)} %get-tuple-element.222), channel_id=1, source_target_pairs={{0,8},{8,16},{16,24},{24,0},{1,9},{9,17},{17,25},{25,1},{2,10},{10... | collective-permute-start | bytes 1572872 | tf_op jit(solution)/shard_map/ppermute | solution.py:183
  623.2 61.3 %collective-permute-start.67 = (bf16[128,2048]{1,0:T(8,128)(2,1)}, bf16[128,2048]{1,0:T(8,128)(2,1)}, u32[]{:S(2)}, u32[]{:S(2)}) collective-permute-start(bf16[128,2048]{1,0:T(8,128)(2,1)} %fusion.24), channel_id=1, source_target_pairs={{0,24},{8,0},{16,8},{24,16},{1,25},{9,1},{17,9},{25,17},{2,26},{10... | collective-permute-start | bytes 1572872 | tf_op jit(solution)/shard_map/ppermute | solution.py:183
  626.8 60.3 %all-to-all-start.10 = ((f32[32,24,128]{2,1,0:T(8,128)}), f32[32,24,128]{2,1,0:T(8,128)S(1)}, u32[]{:S(2)}, u32[]{:S(2)}) async-start(f32[32,24,128]{2,1,0:T(8,128)} %bitcast.293), calls=%async_computation.10 | async-start | bytes 786432 | tf_op jit(solution)/shard_map/all_to_all | solution.py:93
  632.0 35.3 %collective-permute-start.59 = (bf16[256,1280]{1,0:T(8,128)(2,1)}, bf16[256,1280]{1,0:T(8,128)(2,1)S(1)}, u32[]{:S(2)}, u32[]{:S(2)}) collective-permute-start(bf16[256,1280]{1,0:T(8,128)(2,1)} %get-tuple-element.220), channel_id=1, source_target_pairs={{0,8},{8,16},{16,24},{24,0},{1,9},{9,17},{17,25},{25,1},{2,10},{10... | collective-permute-start | bytes 1966088 | tf_op jit(solution)/shard_map/ppermute | solution.py:183
  635.0 44.5 %collective-permute-start.61 = (bf16[256,1280]{1,0:T(8,128)(2,1)S(1)}, bf16[256,1280]{1,0:T(8,128)(2,1)S(1)}, u32[]{:S(2)}, u32[]{:S(2)}) collective-permute-start(bf16[256,1280]{1,0:T(8,128)(2,1)S(1)} %fusion.8), channel_id=1, source_target_pairs={{0,24},{8,0},{16,8},{24,16},{1,25},{9,1},{17,9},{25,17},{2,26},{10... | collective-permute-start | bytes 1966088 | tf_op jit(solution)/shard_map/ppermute | solution.py:183
  (159 other events, 1506.1 us)

commit v6 on v5

--- a/solution.py
+++ b/solution.py
@@ -191,13 +191,22 @@
     return lax.ppermute(value, HEAD_AXES, [(i, i ^ step) for i in range(4)])
 
 
-def slab_out(blocks):
-    got = [blocks[0]] + [quad_xor(blocks[step], step) for step in range(1, 4)]
+def slab_send(blocks):
+    return [blocks[0]] + [quad_xor(blocks[step], step) for step in range(1, 4)]
+
+
+def slab_take(got):
     keep = quad_order([part[0] for part in got])
     other = swap(quad_order([part[1] for part in got]), CORE_AXIS)
     first, second = pair_order(keep, other, CORE_AXIS)
     shape = (NEAR, 2) + keep.shape[1:]
     return jnp.stack([first.reshape(shape), second.reshape(shape)], axis=1)
+
+
+def slab_return(rows):
+    keep, give = pair_order(rows[:, 0], rows[:, 1], CORE_AXIS)
+    both = jnp.stack([keep, swap(give, CORE_AXIS)], axis=2)
+    return quad_parts(both.reshape((4, 2) + rows.shape[3:]))
 
 
 def expert_kernel(
@@ -624,59 +633,86 @@
 
     expert_weight = w_expert[0]
     expert_here = far_index * slab + slab_index
-    in_rows, gate_grads, up_grads, grad_rows, actives, slot_dots, gated_outs, in_grads, partials = (
-        [] for _ in range(9)
-    )
+    in_rows, gate_grads, up_grads, grad_rows, actives, in_grads = ([] for _ in range(6))
+    slot_dots, gated_outs = [None] * far_count, [None] * far_count
+    arrived = []
     here = expert_here.reshape(1)
+    order = list(range(far_count))
     far_rows = [ffn_in]
     for step in range(1, far_count):
-        far_rows.append(far_next(far_rows[-1], far_count))
+        with jax.named_scope('rows_far%d' % step):
+            far_rows.append(far_shift(far_rows[-1], 1, far_count))
 
     def gather(step, source):
         return mm(send_slots[step], source).astype(BF)
 
     sent = gather(0, ffn_in)
 
-    def combine(step):
-        back = exchange(in_grads[step].reshape(slab, capacity, D), SLAB_AXES)
-        back = back.reshape(slab * capacity, D)
-        if step + 1 < far_count:
-            back, actives[step + 1] = tie(back, actives[step + 1])
-        else:
-            back, slot_dots[0] = tie(back, slot_dots[0])
-        return mm_tn(chunk_slots[step], back)
+    def send_back(step):
+        return slab_return(in_grads[step].reshape(NEAR, CORES, 2, capacity, D))
+
+    def combine(step, found):
+        back = jnp.concatenate(found, axis=0).reshape(slab * capacity, D)
+        return mm_tn(send_slots[step], back).astype(BF if step else F32)
 
     ffn_in, cot_back[1] = tie(ffn_in, cot_back[1])
     cot_chunks = far_parts(
         jnp.concatenate(cot_back, axis=2).reshape(far_count, slab * capacity, D), far_count
     )
-    for step in range(far_count):
-        in_chunk = slab_out(to_blocks(sent)).reshape(slab * capacity, D)
-        cot_chunk = cot_chunks[step]
-        if step + 1 < far_count:
-            source = far_rows[step + 1]
-            if step > 0:
-                source, up_grads[step - 1] = tie(source, up_grads[step - 1])
-            sent = gather(step + 1, source)
+    pending = []
+    for turn, step in enumerate(order):
+        with jax.named_scope("rows_out%d" % turn):
+            got = slab_send(to_blocks(sent))
+        if turn + 1 < far_count:
+            source = far_rows[order[turn + 1]]
+            if turn > 0:
+                source, up_grads[turn - 1] = tie(source, up_grads[turn - 1])
+            sent = gather(order[turn + 1], source)
+        if turn > 0:
+            gate_grads[turn - 1], *got = tie(gate_grads[turn - 1], *got)
+        with jax.named_scope("rows_core%d" % turn):
+            in_chunk = slab_take(got).reshape(slab * capacity, D)
+        if turn > 2:
+            in_chunk, *pending = tie(in_chunk, *pending)
+            partial = combine(order[turn - 2], pending)
+            in_chunk, partial = tie(in_chunk, partial)
+            with jax.named_scope("partial_far%d" % (turn - 2)):
+                arrived.append(far_shift(partial, -order[turn - 2], far_count))
         gate_grad, up_grad, active, grad_chunk, in_grad, gated_out, slot_dot = expert_chunk(
-            here, in_chunk, cot_chunk, mask_back[step], router_full, expert_weight
+            here, in_chunk, cot_chunks[step], mask_back[step], router_full, expert_weight
         )
+        if turn > 2:
+            gate_grad, arrived[-1] = tie(gate_grad, arrived[-1])
         in_rows.append(in_chunk)
         gate_grads.append(gate_grad)
         up_grads.append(up_grad)
         actives.append(active)
         grad_rows.append(grad_chunk)
         in_grads.append(in_grad)
-        gated_outs.append(gated_out.reshape(slab, capacity, D))
-        slot_dots.append(slot_dot[:, 0])
-        if step > 0:
-            partials.append(combine(step - 1))
-    partials.append(combine(far_count - 1))
+        gated_outs[step] = gated_out.reshape(slab, capacity, D)
+        slot_dots[step] = slot_dot[:, 0]
+        if turn > 1:
+            with jax.named_scope("rows_back%d" % (turn - 1)):
+                pending = send_back(turn - 1)
+    partial = None
+    for turn in range(max(1, far_count - 2), far_count):
+        if turn == far_count - 1:
+            with jax.named_scope("rows_back%d" % turn):
+                pending = send_back(turn)
+        else:
+            up_grads[-1], *pending = tie(up_grads[-1], *pending)
+        partial = combine(order[turn], pending)
+        if turn == far_count - 2:
+            partial, in_grads[0] = tie(partial, in_grads[0])
+        with jax.named_scope("partial_far%d" % turn):
+            arrived.append(far_shift(partial, -order[turn], far_count))
+    slot_dots[0], partial = tie(slot_dots[0], partial)
+    with jax.named_scope("rows_back0"):
+        from_experts = combine(0, send_back(0))
+    for part in arrived:
+        from_experts = from_experts + part.astype(F32)
     dot_sent = jnp.take(jnp.stack(slot_dots).reshape(device_count, capacity), found_at, axis=0)
     dot_back = exchange(dot_sent[:, None, :], ALL_AXES).reshape(experts_all, capacity)
-    from_experts = partials[0]
-    for step in range(1, far_count):
-        from_experts = from_experts + far_shift(partials[step].astype(BF), -step, far_count).astype(F32)
 
     gate_grad = jnp.sum(jnp.where(slot_hot, dot_back[:, :, None], 0.0), axis=1).T
     mean_term = jnp.sum(gate_probs * gate_grad, axis=1, keepdims=True)
@@ -686,16 +722,16 @@
     resid_part, gain_ffn_grad = ffn_back(ffn_in_grad)
     resid_low = (cot_rows + resid_part).astype(BF)
 
-    gated_sent = far_stack(gated_outs).reshape(device_count, capacity, D)
-    gated_sent, resid_low = tie(gated_sent, resid_low)
-    returned = [
-        exchange(gated_sent[:, :, : D // 2], ALL_AXES).reshape(slot_count, D // 2),
-        exchange(gated_sent[:, :, D // 2 :], ALL_AXES).reshape(slot_count, D // 2),
-    ]
     in_rows[0], resid_low = tie(in_rows[0], resid_low)
     grad_expert = expert_grads(in_rows, grad_rows, gate_grads, up_grads, actives)[None]
 
     resid_both, grad_expert = tie(quad_gather(resid_low), grad_expert)
+    returned = []
+    for half in range(2):
+        gated = far_stack([part[:, :, half * D // 2 : (half + 1) * D // 2] for part in gated_outs])
+        gated, resid_both = tie(gated, resid_both)
+        gated = exchange(gated.reshape(device_count, capacity, D // 2), ALL_AXES)
+        returned.append(gated.reshape(slot_count, D // 2))
     resid_both = resid_both.reshape(2 * ROW, D)
 
     def core_sum(values):
@@ -705,10 +741,10 @@
     out_grad = mm_tn(mixed_low, resid_both).astype(BF)
     resid_both, out_grad = tie(resid_both, out_grad)
     mixed_grad = mm_nt(resid_both, out_mine).astype(BF)
-    out_grad = core_sum(out_grad.reshape(far_part * NEAR, CORES, 2 * out_rows, D))
-    mixed_grad, out_grad, returned[0] = tie(mixed_grad, out_grad, returned[0])
+    out_grad = core_sum(out_grad.reshape(far_part * NEAR, CORES, 2 * out_rows, D)).astype(BF)
+    mixed_grad, out_grad = tie(mixed_grad, out_grad)
     out_grad = (
-        out_grad.astype(BF)
+        out_grad
         .reshape(far_part, NEAR * 2, out_rows, D)
         .transpose(1, 0, 2, 3)
         .reshape(NEAR * 2, far_part * out_rows, D)
@@ -717,20 +753,8 @@
     query_grad, key_grad, value_grad, query_gain_grad, key_gain_grad = attend_back(
         projected, shared, mixed_grad, per_group
     )
-    query_grad, out_grad, returned[1] = tie(query_grad, out_grad, returned[1])
-    out_share = far_sum(far_parts(out_grad, far_count), far_count)
+    query_grad, returned[0] = tie(query_grad, returned[0])
     proj_grad = jnp.concatenate([query_grad, key_grad, value_grad], axis=1)
-    final_rows = jnp.concatenate(
-        [
-            (residual[:, : D // 2] + mm_tn(slot_low, returned[0])).astype(BF),
-            (residual[:, D // 2 :] + mm_tn(slot_low, returned[1])).astype(BF),
-        ],
-        axis=1,
-    )
-    final_pair = jnp.concatenate(
-        pair_order(final_rows, swap(final_rows, SEQ_AXIS), SEQ_AXIS), axis=0
-    )
-    layer_out = mm_tn(back_half, final_pair).astype(BF)
 
     back_grad = lax.dot_general(
         dealt_hot,
@@ -741,16 +765,28 @@
     qkv_grad = mm_tn(normed_low, proj_grad).astype(BF)
     back_grad, qkv_grad = tie(back_grad, qkv_grad)
     normed_partial = mm_nt(back_grad, qkv_mine).astype(BF)
+    qkv_grad = core_sum(qkv_grad.reshape(far_count * NEAR, CORES, half_rows, width)).astype(BF)
+    normed_partial, qkv_grad, out_grad = tie(normed_partial, qkv_grad, out_grad)
+    qkv_grad = far_sum(far_parts(qkv_grad.reshape(far_count, core_rows, width), far_count), far_count)
+    out_share = far_sum(far_parts(out_grad, far_count), far_count)
     normed_grad = quad_sum(normed_partial.reshape(4, TOK_DEV, D))
+    normed_grad, returned[1] = tie(normed_grad, returned[1])
+    final_rows = jnp.concatenate(
+        [
+            (residual[:, : D // 2] + mm_tn(slot_low, returned[0])).astype(BF),
+            (residual[:, D // 2 :] + mm_tn(slot_low, returned[1])).astype(BF),
+        ],
+        axis=1,
+    )
+    final_pair = jnp.concatenate(
+        pair_order(final_rows, swap(final_rows, SEQ_AXIS), SEQ_AXIS), axis=0
+    )
+    layer_out = mm_tn(back_half, final_pair).astype(BF)
     _, attn_back = jax.vjp(rms_norm, tokens.astype(F32), gain_attn)
     input_part, gain_attn_grad = attn_back(normed_grad)
     resid_group = lax.dynamic_slice_in_dim(resid_both, near_index * ROW, ROW, axis=0)
     grad_tokens = (mm_tn(back_half, resid_group) + input_part).astype(BF)
 
-    qkv_grad = core_sum(qkv_grad.reshape(far_count * NEAR, CORES, half_rows, width))
-    qkv_grad = far_sum(
-        far_parts(qkv_grad.astype(BF).reshape(far_count, core_rows, width), far_count), far_count
-    )
     qkv_grad = quad_swap(qkv_grad.astype(BF).reshape(KV_HEADS, qkv_rows, width))
     qkv_grad = qkv_grad.transpose(1, 0, 2).astype(F32)
     qkv_share = jnp.concatenate(

time: 705 us -> 672 us (0.953)
  local copies, waits for them, and re-layouts: 82.6 us -> 60.8 us
  starting transfers between devices: 147 us -> 133 us
    ppermute x18 -> x30, waiting for transfers between devices: 75 us -> 109 us  [quad_send(): return lax.ppermute(block, HEAD_AXES, [(i, i ^ step) for i in range(4)])]
    ppermute x6, waiting for transfers between devices: 32.6 us -> 11.3 us  [quad_gather(): lax.ppermute(value, HEAD_AXES, [(i, i ^ step) for i in range(4)])]
    unnamed x306 -> x284, local copies, waits for them, and re-layouts: 41.7 us -> 20.5 us
    all_to_all x11 -> x7, waiting for transfers between devices: 3.15 us -> 22.5 us  [exchange(): return lax.all_to_all(value, axes, split_axis=0, concat_axis=0, tiled=True)]
    all_to_all x11 -> x7, starting transfers between devices: 51.7 us -> 32.5 us  [exchange(): return lax.all_to_all(value, axes, split_axis=0, concat_axis=0, tiled=True)]
    ppermute x12, waiting for transfers between devices: 22.4 us -> 5.31 us  [quad_xor(): return lax.ppermute(value, HEAD_AXES, [(i, i ^ step) for i in range(4)])]
    ppermute x18 -> x30, starting transfers between devices: 21.1 us -> 35.5 us  [quad_send(): return lax.ppermute(block, HEAD_AXES, [(i, i ^ step) for i in range(4)])]
    ppermute x18 -> x21, waiting for transfers between devices: 101 us -> 88.7 us  [far_shift(): lax.ppermute(value, FAR_AXIS, [(i, (i + step) % count) for i in range(cou...]
  transfers between devices with their start and end apart: 79 -> 91, of which waited for: 32 -> 34; matrix products, arithmetic and copies ran while one was open for 22% -> 23% of each run, Pallas kernels for 14% -> 15%
where the time goes in v6:
time: 672 us; the launch traced here: 662 us
  waiting for transfers between devices  245 us (36%)
  starting transfers between devices  133 us (20%)
  Pallas kernels  97 us (14%)
  other arithmetic  70.7 us (11%)
  local copies, waits for them, and re-layouts  60.8 us (9%)
  matrix products  51.7 us (8%)
    ppermute x30, waiting for transfers between devices, quad_send(): return lax.ppermute(block, HEAD_AXES, [(i, i ^ step) for i in range(4)])  109 us
    ppermute x21, waiting for transfers between devices, far_shift(): lax.ppermute(value, FAR_AXIS, [(i, (i + step) % count) for i in range(cou...  88.7 us
    dot_general x26, matrix products, dot(): lax.dot_general(left, right, (dims, ((), ())), preferred_element_type=F32)  47.3 us
    pallas_call x4, Pallas kernels, expert_chunk(): pl.pallas_call(expert_kernel, grid_spec=pltpu.PrefetchScalarGridSpec(num_...  38.3 us
    ppermute x21, starting transfers between devices, far_shift(): lax.ppermute(value, FAR_AXIS, [(i, (i + step) % count) for i in range(cou...  37.3 us
    ppermute x30, starting transfers between devices, quad_send(): return lax.ppermute(block, HEAD_AXES, [(i, i ^ step) for i in range(4)])  35.5 us
    all_to_all x7, starting transfers between devices, exchange(): return lax.all_to_all(value, axes, split_axis=0, concat_axis=0, tiled=True)  32.5 us
    pallas_call x1, Pallas kernels, attend_back(): pl.pallas_call(attend_back_kernel, grid=(rows // ROW, heads), in_specs=sp...  23.8 us
  transfers between devices with their start and end apart: 91, of which 34 were waited for; matrix products, arithmetic and copies ran while one was open for 23% of the time, Pallas kernels for 15%

profile of v6, /device:TPU:0, one launch (start us, length us, event | category | flops | bytes accessed | tf_op | source)
XLA Modules:
  0.0 661.8 jit_solution(1090786678207366235)
XLA Ops:
  0.6 5.1 collective-permute-start.14
  24.2 5.1 all-to-all-start
  41.5 7.1 %collective-permute-done.8 = bf16[128,2048]{1,0:T(8,128)(2,1)} collective-permute-done((bf16[128,2048]{1,0:T(8,128)(2,1)}, bf16[128,2048]{1,0:T(8,128)(2,1)}, u32[]{:S(2)}, u32[]{:S(2)}) %collective-permute-start.8) | collective-permute-done | bytes 524320 | tf_op jit(solution)/shard_map/ppermute | solution.py:84
  52.8 3.1 collective-permute-start.10
  57.7 3.6 collective-permute-done.6
  63.8 6.8 %collective-permute-done.4 = bf16[128,2048]{1,0:T(8,128)(2,1)S(1)} collective-permute-done((bf16[128,2048]{1,0:T(8,128)(2,1)S(1)}, bf16[128,2048]{1,0:T(8,128)(2,1)S(1)}, u32[]{:S(2)}, u32[]{:S(2)}) %collective-permute-start.4) | collective-permute-done | bytes 524320 | tf_op jit(solution)/shard_map/ppermute | solution.py:114
  72.3 13.8 %collective-permute-done.7 = bf16[256,1280]{1,0:T(8,128)(2,1)S(1)} collective-permute-done((bf16[256,1280]{1,0:T(8,128)(2,1)S(1)}, bf16[256,1280]{1,0:T(8,128)(2,1)S(1)}, u32[]{:S(2)}, u32[]{:S(2)}) %collective-permute-start.7) | collective-permute-done | bytes 655392 | tf_op jit(solution)/shard_map/ppermute | solution.py:183
  87.6 2.8 multiply_reduce_fusion
  90.5 18.1 %collective-permute-done.9 = bf16[256,1280]{1,0:T(8,128)(2,1)S(1)} collective-permute-done((bf16[256,1280]{1,0:T(8,128)(2,1)S(1)}, bf16[256,1280]{1,0:T(8,128)(2,1)S(1)}, u32[]{:S(2)}, u32[]{:S(2)}) %collective-permute-start.9) | collective-permute-done | bytes 655392 | tf_op jit(solution)/shard_map/ppermute | solution.py:183
  110.1 2.5 fusion.169
  112.5 5.4 all-to-all-start.1
  118.6 2.6 multiply_convert_fusion
  124.9 2.7 dynamic-slice_bitcast_fusion.17
  127.6 2.8 collective-permute-start.17
  133.7 4.4 fusion.178.query_ref.key_ref.value_ref
  138.1 16.4 %attend.1 = bf16[512,1024]{1,0:T(8,128)(2,1)} custom-call(f32[512,1280]{1,0:T(8,128)} %fusion.178.query_ref.key_ref.value_ref, f32[512,1280]{1,0:T(8,128)} %fusion.178.query_ref.key_ref.value_ref, f32[512,1280]{1,0:T(8,128)} %fusion.178.query_ref.key_ref.value_ref, f32[512,128]{1,0:T(8,128)} %get-tuple-element.444.cos_ref, ...), custom_call_target="tpu_custom_call" | custom-call | flops 1048576 | bytes 1048576 | tf_op jit(solution)/shard_map/attend/pallas_call | solution.py:427
  154.5 11.4 %collective-permute-done.16 = bf16[128,2048]{1,0:T(8,128)(2,1)} collective-permute-done((bf16[128,2048]{1,0:T(8,128)(2,1)}, bf16[128,2048]{1,0:T(8,128)(2,1)}, u32[]{:S(2)}, u32[]{:S(2)}) %collective-permute-start.16) | collective-permute-done | bytes 524320 | tf_op jit(solution)/shard_map/ppermute | solution.py:102
  171.8 2.7 collective-permute-start.24
  176.0 5.4 all-to-all-start.2
  193.9 23.0 %collective-permute-done.19 = bf16[128,2048]{1,0:T(8,128)(2,1)S(1)} collective-permute-done((bf16[128,2048]{1,0:T(8,128)(2,1)S(1)}, bf16[128,2048]{1,0:T(8,128)(2,1)S(1)}, u32[]{:S(2)}, u32[]{:S(2)}) %collective-permute-start.19) | collective-permute-done | bytes 524320 | tf_op jit(solution)/shard_map/ppermute | solution.py:102
  216.9 13.3 %collective-permute-done.21 = bf16[128,2048]{1,0:T(8,128)(2,1)} collective-permute-done((bf16[128,2048]{1,0:T(8,128)(2,1)S(1)}, bf16[128,2048]{1,0:T(8,128)(2,1)}, u32[]{:S(2)}, u32[]{:S(2)}) %collective-permute-start.21) | collective-permute-done | bytes 524320 | tf_op jit(solution)/shard_map/ppermute | solution.py:102
  233.3 2.7 collective-permute-start.29
  240.0 2.7 pad_maximum_fusion.2
  245.7 4.1 collective-permute-done.26
  257.2 9.5 %expert_chunk.4 = (bf16[256,768]{1,0:T(8,128)(2,1)S(1)}, bf16[256,768]{1,0:T(8,128)(2,1)S(1)}, bf16[256,768]{1,0:T(8,128)(2,1)S(1)}, bf16[256,2048]{1,0:T(8,128)...) custom-call(s32[1]{0:T(128)} %bitcast.54.here_ref, ...), custom_call_target="tpu_custom_call" | custom-call | flops 1048576 | bytes 1048576 | tf_op jit(solution)/shard_map/expert_chunk/pallas_call | solution.py:264
  282.8 9.8 %expert_chunk.5 = (bf16[256,768]{1,0:T(8,128)(2,1)S(1)}, bf16[256,768]{1,0:T(8,128)(2,1)S(1)}, bf16[256,768]{1,0:T(8,128)(2,1)S(1)}, bf16[256,2048]{1,0:T(8,128)...) custom-call(s32[1]{0:T(128)} %bitcast.54.here_ref, ...), custom_call_target="tpu_custom_call" | custom-call | flops 1048576 | bytes 1048576 | tf_op jit(solution)/shard_map/expert_chunk/pallas_call | solution.py:264
  312.4 9.4 %expert_chunk.6 = (bf16[256,768]{1,0:T(8,128)(2,1)S(1)}, bf16[256,768]{1,0:T(8,128)(2,1)S(1)}, bf16[256,768]{1,0:T(8,128)(2,1)S(1)}, bf16[256,2048]{1,0:T(8,128)...) custom-call(s32[1]{0:T(128)} %bitcast.54.here_ref, ...), custom_call_target="tpu_custom_call" | custom-call | flops 1048576 | bytes 1048576 | tf_op jit(solution)/shard_map/expert_chunk/pallas_call | solution.py:264
  327.2 4.2 collective-permute-done.45
  332.8 9.6 %expert_chunk.7 = (bf16[256,768]{1,0:T(8,128)(2,1)S(1)}, bf16[256,768]{1,0:T(8,128)(2,1)S(1)}, bf16[256,768]{1,0:T(8,128)(2,1)S(1)}, bf16[256,2048]{1,0:T(8,128)...) custom-call(s32[1]{0:T(128)} %bitcast.54.here_ref, ...), custom_call_target="tpu_custom_call" | custom-call | flops 1048576 | bytes 1048576 | tf_op jit(solution)/shard_map/expert_chunk/pallas_call | solution.py:264
  349.2 2.9 collective-permute-start.56
  352.2 2.7 collective-permute-done.51
  355.0 4.8 collective-permute-done.49
  369.5 3.3 collective-permute-done.59
  372.8 5.3 collective-permute-done.61
  381.2 5.0 all-to-all-start.3
  392.1 14.9 %all-to-all-done.3 = f32[32,1,32]{2,1,0:T(1,128)S(1)} async-done(((f32[32,1,32]{2,1,0:T(1,128)}), f32[32,1,32]{2,1,0:T(1,128)S(1)}, u32[]{:S(2)}, u32[]{:S(2)}) %all-to-all-start.3) | async-done | bytes 4128 | tf_op jit(solution)/shard_map/all_to_all | solution.py:93
  407.7 2.5 multiply_reduce_fusion.1
  417.0 18.4 %expert_grads.1 = f32[2048,2304]{1,0:T(8,128)} custom-call(bf16[256,2048]{1,0:T(8,128)(2,1)S(1)} %bitcast.642, bf16[256,2048]{1,0:T(8,128)(2,1)} %bitcast.644, bf16[256,2048]{1,0:T(8,128)(2,1)} %bitcast.646, bf16[256,2048]{1,0:T(8,128)(2,1)} %bitcast.648, bf16[256,2048]{1,0:T(8,128)(2,1)} %copy-done.6, bf16[256,2048]{1,0:T(8,128)(2,1)} %copy-done.7, ...), custom_call_target="tpu_custom_call" | custom-call | flops 1048576 | bytes 1048576 | tf_op jit(solution)/shard_map/expert_grads/pallas_call | solution.py:316
  438.2 4.1 all-to-all-start.4
  442.3 4.3 convolution_convert_fusion.1
  449.3 4.2 fusion.3
  454.1 3.4 convolution_convert_fusion.12.grad_ref
  457.5 4.2 fusion.1
  461.7 23.8 %attend_back.1 = (bf16[512,1024]{1,0:T(8,128)(2,1)}, bf16[512,128]{1,0:T(8,128)(2,1)}, bf16[512,128]{1,0:T(8,128)(2,1)}, f32[1,128]{1,0:T(1,128)}, f32[1,128]{1,0:T(1,128)}) custom-call(f32[512,1280]{1,0:T(8,128)} %fusion.178.query_ref.key_ref.value_ref, f32[512,1280]{1,0:T(8,128)} %fusion.178.query_ref.key_ref.value_ref, ...), custom_call_target="tpu_custom_call" | custom-call | flops 1048576 | bytes 1048576 | tf_op jit(solution)/shard_map/attend_back/pallas_call | solution.py:442
  485.6 5.3 all-to-all-done.4
  493.8 3.2 convolution_convert_fusion
  506.6 2.4 reshape.702
  509.0 4.1 all-to-all-start.5
  513.1 3.5 collective-permute-done.68
  516.6 25.9 %collective-permute-done.70 = bf16[128,2048]{1,0:T(8,128)(2,1)} collective-permute-done((bf16[128,2048]{1,0:T(8,128)(2,1)}, bf16[128,2048]{1,0:T(8,128)(2,1)}, u32[]{:S(2)}, u32[]{:S(2)}) %collective-permute-start.70) | collective-permute-done | bytes 524320 | tf_op jit(solution)/shard_map/ppermute | solution.py:102
  542.5 4.0 collective-permute-done.69
  550.4 6.4 convolution_convert_fusion.4
  556.9 2.8 fusion
  560.7 3.8 collective-permute-start.82
  565.3 3.0 collective-permute-start.72
  569.4 14.4 %collective-permute-done.82 = bf16[128,2048]{1,0:T(8,128)(2,1)S(1)} collective-permute-done((bf16[128,2048]{1,0:T(8,128)(2,1)S(1)}, bf16[128,2048]{1,0:T(8,128)(2,1)S(1)}, u32[]{:S(2)}, u32[]{:S(2)}) %collective-permute-start.82) | collective-permute-done | bytes 524320 | tf_op jit(solution)/shard_map/ppermute | solution.py:183
  586.0 2.6 collective-permute-start.76
  591.4 3.3 all-to-all-start.6
  598.8 17.3 %collective-permute-done.76 = bf16[256,1280]{1,0:T(8,128)(2,1)} collective-permute-done((bf16[256,1280]{1,0:T(8,128)(2,1)}, bf16[256,1280]{1,0:T(8,128)(2,1)}, u32[]{:S(2)}, u32[]{:S(2)}) %collective-permute-start.76) | collective-permute-done | bytes 655392 | tf_op jit(solution)/shard_map/ppermute | solution.py:183
  617.4 2.8 collective-permute-start.77
  621.5 6.3 collective-permute-done.83
  627.7 2.5 fusion.61
  630.3 17.2 %collective-permute-done.77 = bf16[256,1280]{1,0:T(8,128)(2,1)S(1)} collective-permute-done((bf16[256,1280]{1,0:T(8,128)(2,1)S(1)}, bf16[256,1280]{1,0:T(8,128)(2,1)S(1)}, u32[]{:S(2)}, u32[]{:S(2)}) %collective-permute-start.77) | collective-permute-done | bytes 655392 | tf_op jit(solution)/shard_map/ppermute | solution.py:183
  650.0 2.4 collective-permute-start.79
  (633 shorter events, 210.9 us)
Async XLA Ops:
  0.6 122.4 %collective-permute-start.14 = (bf16[128,2048]{1,0:T(8,128)(2,1)}, bf16[128,2048]{1,0:T(8,128)(2,1)}, u32[]{:S(2)}, u32[]{:S(2)}) collective-permute-start(bf16[128,2048]{1,0:T(8,128)(2,1)} %param.14), channel_id=1, source_target_pairs={{0,24},{8,0},{16,8},{24,16},{1,25},{9,1},{17,9},{25,17},{2,26},{10... | collective-permute-start | bytes 1572872 | tf_op jit(solution)/shard_map/ppermute | solution.py:183
  5.7 47.0 %collective-permute-start.12 = (bf16[128,2048]{1,0:T(8,128)(2,1)}, bf16[128,2048]{1,0:T(8,128)(2,1)}, u32[]{:S(2)}, u32[]{:S(2)}) collective-permute-start(bf16[128,2048]{1,0:T(8,128)(2,1)} %param.14), channel_id=1, source_target_pairs={{0,8},{8,16},{16,24},{24,0},{1,9},{9,17},{17,25},{25,1},{2,10},{10... | collective-permute-start | bytes 1572872 | tf_op jit(solution)/shard_map/ppermute | solution.py:183
  12.1 20.9 %collective-permute-start.1 = (bf16[64,1280]{1,0:T(8,128)(2,1)S(1)}, bf16[64,1280]{1,0:T(8,128)(2,1)S(1)}, u32[]{:S(2)}, u32[]{:S(2)}) collective-permute-start(bf16[64,1280]{1,0:T(8,128)(2,1)S(1)} %bitcast.751), channel_id=1, source_target_pairs={{0,1},{1,0},{4,5},{5,4},{2,3},{3,2},{6,7},{7,6},{8,9},{9,8},{12,13... | collective-permute-start | bytes 491528 | tf_op jit(solution)/shard_map/ppermute | solution.py:102
  13.7 21.1 %collective-permute-start.2 = (bf16[64,1280]{1,0:T(8,128)(2,1)S(1)}, bf16[64,1280]{1,0:T(8,128)(2,1)S(1)}, u32[]{:S(2)}, u32[]{:S(2)}) collective-permute-start(bf16[64,1280]{1,0:T(8,128)(2,1)S(1)} %bitcast.750), channel_id=1, source_target_pairs={{0,4},{1,5},{4,0},{5,1},{2,6},{3,7},{6,2},{7,3},{8,12},{9,13},{12,... | collective-permute-start | bytes 491528 | tf_op jit(solution)/shard_map/ppermute | solution.py:102
  18.1 16.7 %collective-permute-start.3 = (bf16[64,1280]{1,0:T(8,128)(2,1)S(1)}, bf16[64,1280]{1,0:T(8,128)(2,1)S(1)}, u32[]{:S(2)}, u32[]{:S(2)}) collective-permute-start(bf16[64,1280]{1,0:T(8,128)(2,1)S(1)} %bitcast.752), channel_id=1, source_target_pairs={{0,5},{1,4},{4,1},{5,0},{2,7},{3,6},{6,3},{7,2},{8,13},{9,12},{12,... | collective-permute-start | bytes 491528 | tf_op jit(solution)/shard_map/ppermute | solution.py:102
  24.2 15.8 %all-to-all-start = ((bf16[32,32,128]{2,1,0:T(8,128)(2,1)}), bf16[32,32,128]{2,1,0:T(8,128)(2,1)S(1)}, u32[]{:S(2)}, u32[]{:S(2)}) async-start(bf16[32,32,128]{2,1,0:T(8,128)(2,1)} %bitcast.291), calls=%async_computation | async-start | bytes 524288 | tf_op jit(solution)/shard_map/all_to_all | solution.py:93
  34.8 26.5 %collective-permute-start.6 = (bf16[128,2048]{1,0:T(8,128)(2,1)S(1)}, bf16[128,2048]{1,0:T(8,128)(2,1)}, u32[]{:S(2)}, u32[]{:S(2)}) collective-permute-start(bf16[128,2048]{1,0:T(8,128)(2,1)S(1)} %copy-done.58), channel_id=1, source_target_pairs={{0,5},{1,4},{4,1},{5,0},{2,7},{3,6},{6,3},{7,2},{8,13},{9,12},{12,... | collective-permute-start | bytes 1572872 | tf_op jit(solution)/shard_map/ppermute | solution.py:114
  36.3 26.1 %collective-permute-start.5 = (bf16[128,2048]{1,0:T(8,128)(2,1)S(1)}, bf16[128,2048]{1,0:T(8,128)(2,1)}, u32[]{:S(2)}, u32[]{:S(2)}) collective-permute-start(bf16[128,2048]{1,0:T(8,128)(2,1)S(1)} %copy-done.58), channel_id=1, source_target_pairs={{0,4},{1,5},{4,0},{5,1},{2,6},{3,7},{6,2},{7,3},{8,12},{9,13},{12,... | collective-permute-start | bytes 1572872 | tf_op jit(solution)/shard_map/ppermute | solution.py:114
  48.6 22.0 %collective-permute-start.4 = (bf16[128,2048]{1,0:T(8,128)(2,1)S(1)}, bf16[128,2048]{1,0:T(8,128)(2,1)S(1)}, u32[]{:S(2)}, u32[]{:S(2)}) collective-permute-start(bf16[128,2048]{1,0:T(8,128)(2,1)S(1)} %copy-done.58), channel_id=1, source_target_pairs={{0,1},{1,0},{4,5},{5,4},{2,3},{3,2},{6,7},{7,6},{8,9},{9,8},{12,13... | collective-permute-start | bytes 1572872 | tf_op jit(solution)/shard_map/ppermute | solution.py:114
  52.8 55.9 %collective-permute-start.10 = (bf16[256,1280]{1,0:T(8,128)(2,1)S(1)}, bf16[256,1280]{1,0:T(8,128)(2,1)S(1)}, u32[]{:S(2)}, u32[]{:S(2)}) collective-permute-start(bf16[256,1280]{1,0:T(8,128)(2,1)S(1)} %bitcast.701), channel_id=1, source_target_pairs={{0,24},{8,0},{16,8},{24,16},{1,25},{9,1},{17,9},{25,17},{2,26},{10... | collective-permute-start | bytes 1966088 | tf_op jit(solution)/shard_map/ppermute | solution.py:183
  61.3 24.7 %collective-permute-start.7 = (bf16[256,1280]{1,0:T(8,128)(2,1)S(1)}, bf16[256,1280]{1,0:T(8,128)(2,1)S(1)}, u32[]{:S(2)}, u32[]{:S(2)}) collective-permute-start(bf16[256,1280]{1,0:T(8,128)(2,1)S(1)} %bitcast.702), channel_id=1, source_target_pairs={{0,8},{8,16},{16,24},{24,0},{1,9},{9,17},{17,25},{25,1},{2,10},{10... | collective-permute-start | bytes 1966088 | tf_op jit(solution)/shard_map/ppermute | solution.py:183
  62.4 58.8 %collective-permute-start.13 = (bf16[128,2048]{1,0:T(8,128)(2,1)}, bf16[128,2048]{1,0:T(8,128)(2,1)}, u32[]{:S(2)}, u32[]{:S(2)}) collective-permute-start(bf16[128,2048]{1,0:T(8,128)(2,1)} %collective-permute-done.12), channel_id=1, source_target_pairs={{0,8},{8,16},{16,24},{24,0},{1,9},{9,17},{17,25},{25,1},{2,10},{10... | collective-permute-start | bytes 1572872 | tf_op jit(solution)/shard_map/ppermute | solution.py:183
  86.0 22.6 %collective-permute-start.9 = (bf16[256,1280]{1,0:T(8,128)(2,1)S(1)}, bf16[256,1280]{1,0:T(8,128)(2,1)S(1)}, u32[]{:S(2)}, u32[]{:S(2)}) collective-permute-start(bf16[256,1280]{1,0:T(8,128)(2,1)S(1)} %collective-permute-done.7), channel_id=1, source_target_pairs={{0,8},{8,16},{16,24},{24,0},{1,9},{9,17},{17,25},{25,1},{2,10},{10... | collective-permute-start | bytes 1966088 | tf_op jit(solution)/shard_map/ppermute | solution.py:183
  108.7 22.4 %collective-permute-start.11 = (bf16[8,128,1280]{2,1,0:T(8,128)(2,1)S(1)}, bf16[8,128,1280]{2,1,0:T(8,128)(2,1)}, u32[]{:S(2)}, u32[]{:S(2)}) collective-permute-start(bf16[8,128,1280]{2,1,0:T(8,128)(2,1)S(1)} %bitcast.682), channel_id=1, source_target_pairs={{0,2},{2,0},{1,3},{3,1},{4,6},{6,4},{5,7},{7,5},{8,10},{10,8},{9,1... | collective-permute-start | bytes 7864328 | tf_op jit(solution)/shard_map/ppermute | solution.py:84
  112.5 55.5 %all-to-all-start.1 = ((bf16[32,32,1024]{2,1,0:T(8,128)(2,1)}), bf16[32,32,1024]{2,1,0:T(8,128)(2,1)}, u32[]{:S(2)}, u32[]{:S(2)}) async-start(bf16[32,32,1024]{2,1,0:T(8,128)(2,1)} %get-tuple-element.267), calls=%async_computation.1 | async-start | bytes 4194304 | tf_op jit(solution)/shard_map/all_to_all | solution.py:93
  127.6 26.9 %collective-permute-start.17 = (bf16[128,2048]{1,0:T(8,128)(2,1)}, bf16[128,2048]{1,0:T(8,128)(2,1)}, u32[]{:S(2)}, u32[]{:S(2)}) collective-permute-start(bf16[128,2048]{1,0:T(8,128)(2,1)} %get-tuple-element.295), channel_id=1, source_target_pairs={{0,5},{1,4},{4,1},{5,0},{2,7},{3,6},{6,3},{7,2},{8,13},{9,12},{12,... | collective-permute-start | bytes 1572872 | tf_op jit(solution)/shard_map/ppermute | solution.py:102
  130.4 35.5 %collective-permute-start.16 = (bf16[128,2048]{1,0:T(8,128)(2,1)}, bf16[128,2048]{1,0:T(8,128)(2,1)}, u32[]{:S(2)}, u32[]{:S(2)}) collective-permute-start(bf16[128,2048]{1,0:T(8,128)(2,1)} %get-tuple-element.296), channel_id=1, source_target_pairs={{0,4},{1,5},{4,0},{5,1},{2,6},{3,7},{6,2},{7,3},{8,12},{9,13},{12,... | collective-permute-start | bytes 1572872 | tf_op jit(solution)/shard_map/ppermute | solution.py:102
  131.0 37.0 %collective-permute-start.15 = (bf16[128,2048]{1,0:T(8,128)(2,1)}, bf16[128,2048]{1,0:T(8,128)(2,1)}, u32[]{:S(2)}, u32[]{:S(2)}) collective-permute-start(bf16[128,2048]{1,0:T(8,128)(2,1)} %get-tuple-element.297), channel_id=1, source_target_pairs={{0,1},{1,0},{4,5},{5,4},{2,3},{3,2},{6,7},{7,6},{8,9},{9,8},{12,13... | collective-permute-start | bytes 1572872 | tf_op jit(solution)/shard_map/ppermute | solution.py:102
  176.0 60.0 %all-to-all-start.2 = ((bf16[32,32,1024]{2,1,0:T(8,128)(2,1)}), bf16[32,32,1024]{2,1,0:T(8,128)(2,1)}, u32[]{:S(2)}, u32[]{:S(2)}) async-start(bf16[32,32,1024]{2,1,0:T(8,128)(2,1)} %get-tuple-element.266), calls=%async_computation.2 | async-start | bytes 4194304 | tf_op jit(solution)/shard_map/all_to_all | solution.py:93
  187.3 29.6 %collective-permute-start.19 = (bf16[128,2048]{1,0:T(8,128)(2,1)S(1)}, bf16[128,2048]{1,0:T(8,128)(2,1)S(1)}, u32[]{:S(2)}, u32[]{:S(2)}) collective-permute-start(bf16[128,2048]{1,0:T(8,128)(2,1)S(1)} %get-tuple-element.288), channel_id=1, source_target_pairs={{0,1},{1,0},{4,5},{5,4},{2,3},{3,2},{6,7},{7,6},{8,9},{9,8},{12,13... | collective-permute-start | bytes 1572872 | tf_op jit(solution)/shard_map/ppermute | solution.py:102
  189.1 41.1 %collective-permute-start.21 = (bf16[128,2048]{1,0:T(8,128)(2,1)S(1)}, bf16[128,2048]{1,0:T(8,128)(2,1)}, u32[]{:S(2)}, u32[]{:S(2)}) collective-permute-start(bf16[128,2048]{1,0:T(8,128)(2,1)S(1)} %get-tuple-element.289), channel_id=1, source_target_pairs={{0,5},{1,4},{4,1},{5,0},{2,7},{3,6},{6,3},{7,2},{8,13},{9,12},{12,... | collective-permute-start | bytes 1572872 | tf_op jit(solution)/shard_map/ppermute | solution.py:102
  190.6 39.7 %collective-permute-start.20 = (bf16[128,2048]{1,0:T(8,128)(2,1)S(1)}, bf16[128,2048]{1,0:T(8,128)(2,1)}, u32[]{:S(2)}, u32[]{:S(2)}) collective-permute-start(bf16[128,2048]{1,0:T(8,128)(2,1)S(1)} %get-tuple-element.290), channel_id=1, source_target_pairs={{0,4},{1,5},{4,0},{5,1},{2,6},{3,7},{6,2},{7,3},{8,12},{9,13},{12,... | collective-permute-start | bytes 1572872 | tf_op jit(solution)/shard_map/ppermute | solution.py:102
  233.3 18.0 %collective-permute-start.29 = (bf16[128,2048]{1,0:T(8,128)(2,1)S(1)}, bf16[128,2048]{1,0:T(8,128)(2,1)S(1)}, u32[]{:S(2)}, u32[]{:S(2)}) collective-permute-start(bf16[128,2048]{1,0:T(8,128)(2,1)S(1)} %multiply_convert_fusion.1), channel_id=1, source_target_pairs={{0,8},{8,16},{16,24},{24,0},{1,9},{9,17},{17,25},{25,1},{2,10},{10... | collective-permute-start | bytes 1572872 | tf_op jit(solution)/shard_map/rows_far1/ppermute | solution.py:183
  251.8 19.3 %collective-permute-start.31 = (bf16[2,32,2048]{2,1,0:T(8,128)(2,1)S(1)}, bf16[2,32,2048]{2,1,0:T(8,128)(2,1)S(1)}, u32[]{:S(2)}, u32[]{:S(2)}) collective-permute-start(bf16[2,32,2048]{2,1,0:T(8,128)(2,1)S(1)} %bitcast.746), channel_id=1, source_target_pairs={{0,4},{1,5},{4,0},{5,1},{2,6},{3,7},{6,2},{7,3},{8,12},{9,13},{12,... | collective-permute-start | bytes 786440 | tf_op jit(solution)/shard_map/rows_out1/ppermute | solution.py:191
  252.5 18.6 %collective-permute-start.32 = (bf16[2,32,2048]{2,1,0:T(8,128)(2,1)S(1)}, bf16[2,32,2048]{2,1,0:T(8,128)(2,1)S(1)}, u32[]{:S(2)}, u32[]{:S(2)}) collective-permute-start(bf16[2,32,2048]{2,1,0:T(8,128)(2,1)S(1)} %bitcast.745), channel_id=1, source_target_pairs={{0,5},{1,4},{4,1},{5,0},{2,7},{3,6},{6,3},{7,2},{8,13},{9,12},{12,... | collective-permute-start | bytes 786440 | tf_op jit(solution)/shard_map/rows_out1/ppermute | solution.py:191
  254.3 16.8 %collective-permute-start.30 = (bf16[2,32,2048]{2,1,0:T(8,128)(2,1)S(1)}, bf16[2,32,2048]{2,1,0:T(8,128)(2,1)S(1)}, u32[]{:S(2)}, u32[]{:S(2)}) collective-permute-start(bf16[2,32,2048]{2,1,0:T(8,128)(2,1)S(1)} %bitcast.744), channel_id=1, source_target_pairs={{0,1},{1,0},{4,5},{5,4},{2,3},{3,2},{6,7},{7,6},{8,9},{9,8},{12,13... | collective-permute-start | bytes 786440 | tf_op jit(solution)/shard_map/rows_out1/ppermute | solution.py:191
  255.3 18.6 %collective-permute-start.34 = (bf16[128,2048]{1,0:T(8,128)(2,1)S(1)}, bf16[128,2048]{1,0:T(8,128)(2,1)}, u32[]{:S(2)}, u32[]{:S(2)}) collective-permute-start(bf16[128,2048]{1,0:T(8,128)(2,1)S(1)} %collective-permute-done.29), channel_id=1, source_target_pairs={{0,8},{8,16},{16,24},{24,0},{1,9},{9,17},{17,25},{25,1},{2,10},{10... | collective-permute-start | bytes 1572872 | tf_op jit(solution)/shard_map/rows_far2/ppermute | solution.py:183
  276.2 22.4 %collective-permute-start.36 = (bf16[2,32,2048]{2,1,0:T(8,128)(2,1)S(1)}, bf16[2,32,2048]{2,1,0:T(8,128)(2,1)}, u32[]{:S(2)}, u32[]{:S(2)}) collective-permute-start(bf16[2,32,2048]{2,1,0:T(8,128)(2,1)S(1)} %bitcast.749), channel_id=1, source_target_pairs={{0,4},{1,5},{4,0},{5,1},{2,6},{3,7},{6,2},{7,3},{8,12},{9,13},{12,... | collective-permute-start | bytes 786440 | tf_op jit(solution)/shard_map/rows_out2/ppermute | solution.py:191
  277.3 21.3 %collective-permute-start.37 = (bf16[2,32,2048]{2,1,0:T(8,128)(2,1)S(1)}, bf16[2,32,2048]{2,1,0:T(8,128)(2,1)}, u32[]{:S(2)}, u32[]{:S(2)}) collective-permute-start(bf16[2,32,2048]{2,1,0:T(8,128)(2,1)S(1)} %bitcast.748), channel_id=1, source_target_pairs={{0,5},{1,4},{4,1},{5,0},{2,7},{3,6},{6,3},{7,2},{8,13},{9,12},{12,... | collective-permute-start | bytes 786440 | tf_op jit(solution)/shard_map/rows_out2/ppermute | solution.py:191
  277.9 20.6 %collective-permute-start.35 = (bf16[2,32,2048]{2,1,0:T(8,128)(2,1)S(1)}, bf16[2,32,2048]{2,1,0:T(8,128)(2,1)}, u32[]{:S(2)}, u32[]{:S(2)}) collective-permute-start(bf16[2,32,2048]{2,1,0:T(8,128)(2,1)S(1)} %bitcast.747), channel_id=1, source_target_pairs={{0,1},{1,0},{4,5},{5,4},{2,3},{3,2},{6,7},{7,6},{8,9},{9,8},{12,13... | collective-permute-start | bytes 786440 | tf_op jit(solution)/shard_map/rows_out2/ppermute | solution.py:191
  279.7 23.7 %collective-permute-start.39 = (bf16[128,2048]{1,0:T(8,128)(2,1)}, bf16[128,2048]{1,0:T(8,128)(2,1)}, u32[]{:S(2)}, u32[]{:S(2)}) collective-permute-start(bf16[128,2048]{1,0:T(8,128)(2,1)} %collective-permute-done.34), channel_id=1, source_target_pairs={{0,8},{8,16},{16,24},{24,0},{1,9},{9,17},{17,25},{25,1},{2,10},{10... | collective-permute-start | bytes 1572872 | tf_op jit(solution)/shard_map/rows_far3/ppermute | solution.py:183
  304.9 17.0 %collective-permute-start.41 = (bf16[2,32,2048]{2,1,0:T(8,128)(2,1)S(1)}, bf16[2,32,2048]{2,1,0:T(8,128)(2,1)S(1)}, u32[]{:S(2)}, u32[]{:S(2)}) collective-permute-start(bf16[2,32,2048]{2,1,0:T(8,128)(2,1)S(1)} %bitcast.743), channel_id=1, source_target_pairs={{0,4},{1,5},{4,0},{5,1},{2,6},{3,7},{6,2},{7,3},{8,12},{9,13},{12,... | collective-permute-start | bytes 786440 | tf_op jit(solution)/shard_map/rows_out3/ppermute | solution.py:191
  305.8 17.4 %collective-permute-start.42 = (bf16[2,32,2048]{2,1,0:T(8,128)(2,1)S(1)}, bf16[2,32,2048]{2,1,0:T(8,128)(2,1)S(1)}, u32[]{:S(2)}, u32[]{:S(2)}) collective-permute-start(bf16[2,32,2048]{2,1,0:T(8,128)(2,1)S(1)} %bitcast.742), channel_id=1, source_target_pairs={{0,5},{1,4},{4,1},{5,0},{2,7},{3,6},{6,3},{7,2},{8,13},{9,12},{12,... | collective-permute-start | bytes 786440 | tf_op jit(solution)/shard_map/rows_out3/ppermute | solution.py:191
  306.6 16.6 %collective-permute-start.40 = (bf16[2,32,2048]{2,1,0:T(8,128)(2,1)S(1)}, bf16[2,32,2048]{2,1,0:T(8,128)(2,1)S(1)}, u32[]{:S(2)}, u32[]{:S(2)}) collective-permute-start(bf16[2,32,2048]{2,1,0:T(8,128)(2,1)S(1)} %bitcast.741), channel_id=1, source_target_pairs={{0,1},{1,0},{4,5},{5,4},{2,3},{3,2},{6,7},{7,6},{8,9},{9,8},{12,13... | collective-permute-start | bytes 786440 | tf_op jit(solution)/shard_map/rows_out3/ppermute | solution.py:191
  308.6 18.6 %collective-permute-start.47 = (bf16[2,32,2048]{2,1,0:T(8,128)(2,1)S(1)}, bf16[2,32,2048]{2,1,0:T(8,128)(2,1)S(1)}, u32[]{:S(2)}, u32[]{:S(2)}) collective-permute-start(bf16[2,32,2048]{2,1,0:T(8,128)(2,1)S(1)} %get-tuple-element.345), channel_id=1, source_target_pairs={{0,5},{1,4},{4,1},{5,0},{2,7},{3,6},{6,3},{7,2},{8,13},{9,12},{12,... | collective-permute-start | bytes 786440 | tf_op jit(solution)/shard_map/rows_back1/ppermute | solution.py:102
  309.5 21.9 %collective-permute-start.45 = (bf16[2,32,2048]{2,1,0:T(8,128)(2,1)S(1)}, bf16[2,32,2048]{2,1,0:T(8,128)(2,1)S(1)}, u32[]{:S(2)}, u32[]{:S(2)}) collective-permute-start(bf16[2,32,2048]{2,1,0:T(8,128)(2,1)S(1)} %get-tuple-element.347), channel_id=1, source_target_pairs={{0,1},{1,0},{4,5},{5,4},{2,3},{3,2},{6,7},{7,6},{8,9},{9,8},{12,13... | collective-permute-start | bytes 786440 | tf_op jit(solution)/shard_map/rows_back1/ppermute | solution.py:102
  323.6 19.8 %collective-permute-start.48 = (bf16[2,2,32,2048]{3,2,1,0:T(8,128)(2,1)S(1)}, bf16[2,2,32,2048]{3,2,1,0:T(8,128)(2,1)S(1)}, u32[]{:S(2)}, u32[]{:S(2)}) collective-permute-start(bf16[2,2,32,2048]{3,2,1,0:T(8,128)(2,1)S(1)} %get-tuple-element.331), channel_id=1, source_target_pairs={{0,2},{2,0},{1,3},{3,1},{4,6},{6,4},{5,7},{7,5},{8,10},{10,8},{9,1... | collective-permute-start | bytes 1572872 | tf_op jit(solution)/shard_map/rows_back2/ppermute | solution.py:84
  343.4 19.0 %collective-permute-start.58 = (bf16[2,2,32,2048]{3,2,1,0:T(8,128)(2,1)}, bf16[2,2,32,2048]{3,2,1,0:T(8,128)(2,1)}, u32[]{:S(2)}, u32[]{:S(2)}) collective-permute-start(bf16[2,2,32,2048]{3,2,1,0:T(8,128)(2,1)} %get-tuple-element.337), channel_id=1, source_target_pairs={{0,2},{2,0},{1,3},{3,1},{4,6},{6,4},{5,7},{7,5},{8,10},{10,8},{9,1... | collective-permute-start | bytes 1572872 | tf_op jit(solution)/shard_map/rows_back3/ppermute | solution.py:84
  349.2 19.0 %collective-permute-start.56 = (bf16[128,2048]{1,0:T(8,128)(2,1)}, bf16[128,2048]{1,0:T(8,128)(2,1)}, u32[]{:S(2)}, u32[]{:S(2)}) collective-permute-start(bf16[128,2048]{1,0:T(8,128)(2,1)} %fusion.11), channel_id=1, source_target_pairs={{0,24},{8,0},{16,8},{24,16},{1,25},{9,1},{17,9},{25,17},{2,26},{10... | collective-permute-start | bytes 1572872 | tf_op jit(solution)/shard_map/partial_far1/ppermute | solution.py:183
  368.2 18.1 %collective-permute-start.52 = (bf16[2,2,32,2048]{3,2,1,0:T(8,128)(2,1)}, bf16[2,2,32,2048]{3,2,1,0:T(8,128)(2,1)}, u32[]{:S(2)}, u32[]{:S(2)}) collective-permute-start(bf16[2,2,32,2048]{3,2,1,0:T(8,128)(2,1)} %get-tuple-element.325), channel_id=1, source_target_pairs={{0,2},{2,0},{1,3},{3,1},{4,6},{6,4},{5,7},{7,5},{8,10},{10,8},{9,1... | collective-permute-start | bytes 1572872 | tf_op jit(solution)/shard_map/rows_back0/ppermute | solution.py:84
  368.2 39.3 %collective-permute-start.57 = (bf16[128,2048]{1,0:T(8,128)(2,1)}, bf16[128,2048]{1,0:T(8,128)(2,1)}, u32[]{:S(2)}, u32[]{:S(2)}) collective-permute-start(bf16[128,2048]{1,0:T(8,128)(2,1)} %fusion.12), channel_id=1, source_target_pairs={{0,16},{8,24},{16,0},{24,8},{1,17},{9,25},{17,1},{25,9},{2,18},{10... | collective-permute-start | bytes 1572872 | tf_op jit(solution)/shard_map/partial_far2/ppermute | solution.py:183
  379.3 28.3 %collective-permute-start.62 = (bf16[128,2048]{1,0:T(8,128)(2,1)}, bf16[128,2048]{1,0:T(8,128)(2,1)}, u32[]{:S(2)}, u32[]{:S(2)}) collective-permute-start(bf16[128,2048]{1,0:T(8,128)(2,1)} %fusion.13), channel_id=1, source_target_pairs={{0,8},{8,16},{16,24},{24,0},{1,9},{9,17},{17,25},{25,1},{2,10},{10... | collective-permute-start | bytes 1572872 | tf_op jit(solution)/shard_map/partial_far3/ppermute | solution.py:183
  381.2 25.7 %all-to-all-start.3 = ((f32[32,1,32]{2,1,0:T(1,128)}), f32[32,1,32]{2,1,0:T(1,128)S(1)}, u32[]{:S(2)}, u32[]{:S(2)}) async-start(f32[32,1,32]{2,1,0:T(1,128)} %bitcast.183), calls=%async_computation.3 | async-start | bytes 32768 | tf_op jit(solution)/shard_map/all_to_all | solution.py:93
  388.6 19.0 %collective-permute-start.53 = (bf16[2,32,2048]{2,1,0:T(8,128)(2,1)}, bf16[2,32,2048]{2,1,0:T(8,128)(2,1)}, u32[]{:S(2)}, u32[]{:S(2)}) collective-permute-start(bf16[2,32,2048]{2,1,0:T(8,128)(2,1)} %get-tuple-element.322), channel_id=1, source_target_pairs={{0,1},{1,0},{4,5},{5,4},{2,3},{3,2},{6,7},{7,6},{8,9},{9,8},{12,13... | collective-permute-start | bytes 786440 | tf_op jit(solution)/shard_map/rows_back0/ppermute | solution.py:102
  390.3 17.2 %collective-permute-start.54 = (bf16[2,32,2048]{2,1,0:T(8,128)(2,1)}, bf16[2,32,2048]{2,1,0:T(8,128)(2,1)}, u32[]{:S(2)}, u32[]{:S(2)}) collective-permute-start(bf16[2,32,2048]{2,1,0:T(8,128)(2,1)} %get-tuple-element.323), channel_id=1, source_target_pairs={{0,4},{1,5},{4,0},{5,1},{2,6},{3,7},{6,2},{7,3},{8,12},{9,13},{12,... | collective-permute-start | bytes 786440 | tf_op jit(solution)/shard_map/rows_back0/ppermute | solution.py:102
  410.6 24.8 %collective-permute-start.65 = (bf16[128,2048]{1,0:T(8,128)(2,1)S(1)}, bf16[128,2048]{1,0:T(8,128)(2,1)S(1)}, u32[]{:S(2)}, u32[]{:S(2)}) collective-permute-start(bf16[128,2048]{1,0:T(8,128)(2,1)S(1)} %fusion.21), channel_id=1, source_target_pairs={{0,5},{1,4},{4,1},{5,0},{2,7},{3,6},{6,3},{7,2},{8,13},{9,12},{12,... | collective-permute-start | bytes 1572872 | tf_op jit(solution)/shard_map/ppermute | solution.py:114
  412.6 23.8 %collective-permute-start.64 = (bf16[128,2048]{1,0:T(8,128)(2,1)S(1)}, bf16[128,2048]{1,0:T(8,128)(2,1)S(1)}, u32[]{:S(2)}, u32[]{:S(2)}) collective-permute-start(bf16[128,2048]{1,0:T(8,128)(2,1)S(1)} %fusion.21), channel_id=1, source_target_pairs={{0,4},{1,5},{4,0},{5,1},{2,6},{3,7},{6,2},{7,3},{8,12},{9,13},{12,... | collective-permute-start | bytes 1572872 | tf_op jit(solution)/shard_map/ppermute | solution.py:114
  413.6 22.8 %collective-permute-start.63 = (bf16[128,2048]{1,0:T(8,128)(2,1)S(1)}, bf16[128,2048]{1,0:T(8,128)(2,1)S(1)}, u32[]{:S(2)}, u32[]{:S(2)}) collective-permute-start(bf16[128,2048]{1,0:T(8,128)(2,1)S(1)} %fusion.21), channel_id=1, source_target_pairs={{0,1},{1,0},{4,5},{5,4},{2,3},{3,2},{6,7},{7,6},{8,9},{9,8},{12,13... | collective-permute-start | bytes 1572872 | tf_op jit(solution)/shard_map/ppermute | solution.py:114
  438.2 52.6 %all-to-all-start.4 = ((bf16[32,32,1024]{2,1,0:T(8,128)(2,1)}), bf16[32,32,1024]{2,1,0:T(8,128)(2,1)S(1)}, u32[]{:S(2)}, u32[]{:S(2)}) async-start(bf16[32,32,1024]{2,1,0:T(8,128)(2,1)} %bitcast.198), calls=%async_computation.4 | async-start | bytes 4194304 | tf_op jit(solution)/shard_map/all_to_all | solution.py:93
  500.3 56.5 %collective-permute-start.67 = (bf16[8,128,1280]{2,1,0:T(8,128)(2,1)}, bf16[8,128,1280]{2,1,0:T(8,128)(2,1)}, u32[]{:S(2)}, u32[]{:S(2)}) collective-permute-start(bf16[8,128,1280]{2,1,0:T(8,128)(2,1)} %fusion.4), channel_id=1, source_target_pairs={{0,2},{2,0},{1,3},{3,1},{4,6},{6,4},{5,7},{7,5},{8,10},{10,8},{9,1... | collective-permute-start | bytes 7864328 | tf_op jit(solution)/shard_map/ppermute | solution.py:84
  503.0 39.5 %collective-permute-start.70 = (bf16[128,2048]{1,0:T(8,128)(2,1)}, bf16[128,2048]{1,0:T(8,128)(2,1)}, u32[]{:S(2)}, u32[]{:S(2)}) collective-permute-start(bf16[128,2048]{1,0:T(8,128)(2,1)} %get-tuple-element.282), channel_id=1, source_target_pairs={{0,5},{1,4},{4,1},{5,0},{2,7},{3,6},{6,3},{7,2},{8,13},{9,12},{12,... | collective-permute-start | bytes 1572872 | tf_op jit(solution)/shard_map/ppermute | solution.py:102
  504.5 42.0 %collective-permute-start.69 = (bf16[128,2048]{1,0:T(8,128)(2,1)}, bf16[128,2048]{1,0:T(8,128)(2,1)}, u32[]{:S(2)}, u32[]{:S(2)}) collective-permute-start(bf16[128,2048]{1,0:T(8,128)(2,1)} %get-tuple-element.283), channel_id=1, source_target_pairs={{0,4},{1,5},{4,0},{5,1},{2,6},{3,7},{6,2},{7,3},{8,12},{9,13},{12,... | collective-permute-start | bytes 1572872 | tf_op jit(solution)/shard_map/ppermute | solution.py:102
  509.0 80.0 %all-to-all-start.5 = ((bf16[32,32,1024]{2,1,0:T(8,128)(2,1)}), bf16[32,32,1024]{2,1,0:T(8,128)(2,1)}, u32[]{:S(2)}, u32[]{:S(2)}) async-start(bf16[32,32,1024]{2,1,0:T(8,128)(2,1)} %bitcast.688), calls=%async_computation.5 | async-start | bytes 4194304 | tf_op jit(solution)/shard_map/all_to_all | solution.py:93
  560.7 60.8 %collective-permute-start.81 = (bf16[128,2048]{1,0:T(8,128)(2,1)}, bf16[128,2048]{1,0:T(8,128)(2,1)}, u32[]{:S(2)}, u32[]{:S(2)}) collective-permute-start(bf16[128,2048]{1,0:T(8,128)(2,1)} %get-tuple-element.276), channel_id=1, source_target_pairs={{0,8},{8,16},{16,24},{24,0},{1,9},{9,17},{17,25},{25,1},{2,10},{10... | collective-permute-start | bytes 1572872 | tf_op jit(solution)/shard_map/ppermute | solution.py:183
  560.7 23.1 %collective-permute-start.82 = (bf16[128,2048]{1,0:T(8,128)(2,1)S(1)}, bf16[128,2048]{1,0:T(8,128)(2,1)S(1)}, u32[]{:S(2)}, u32[]{:S(2)}) collective-permute-start(bf16[128,2048]{1,0:T(8,128)(2,1)S(1)} %get-tuple-element.277), channel_id=1, source_target_pairs={{0,24},{8,0},{16,8},{24,16},{1,25},{9,1},{17,9},{25,17},{2,26},{10... | collective-permute-start | bytes 1572872 | tf_op jit(solution)/shard_map/ppermute | solution.py:183
  564.7 21.3 %collective-permute-start.71 = (bf16[128,2048]{1,0:T(8,128)(2,1)S(1)}, bf16[128,2048]{1,0:T(8,128)(2,1)S(1)}, u32[]{:S(2)}, u32[]{:S(2)}) collective-permute-start(bf16[128,2048]{1,0:T(8,128)(2,1)S(1)} %get-tuple-element.278), channel_id=1, source_target_pairs={{0,1},{1,0},{4,5},{5,4},{2,3},{3,2},{6,7},{7,6},{8,9},{9,8},{12,13... | collective-permute-start | bytes 1572872 | tf_op jit(solution)/shard_map/ppermute | solution.py:102
  565.1 23.5 %collective-permute-start.73 = (bf16[128,2048]{1,0:T(8,128)(2,1)S(1)}, bf16[128,2048]{1,0:T(8,128)(2,1)S(1)}, u32[]{:S(2)}, u32[]{:S(2)}) collective-permute-start(bf16[128,2048]{1,0:T(8,128)(2,1)S(1)} %get-tuple-element.279), channel_id=1, source_target_pairs={{0,5},{1,4},{4,1},{5,0},{2,7},{3,6},{6,3},{7,2},{8,13},{9,12},{12,... | collective-permute-start | bytes 1572872 | tf_op jit(solution)/shard_map/ppermute | solution.py:102
  565.3 23.4 %collective-permute-start.72 = (bf16[128,2048]{1,0:T(8,128)(2,1)S(1)}, bf16[128,2048]{1,0:T(8,128)(2,1)S(1)}, u32[]{:S(2)}, u32[]{:S(2)}) collective-permute-start(bf16[128,2048]{1,0:T(8,128)(2,1)S(1)} %get-tuple-element.280), channel_id=1, source_target_pairs={{0,4},{1,5},{4,0},{5,1},{2,6},{3,7},{6,2},{7,3},{8,12},{9,13},{12,... | collective-permute-start | bytes 1572872 | tf_op jit(solution)/shard_map/ppermute | solution.py:102
  583.8 46.5 %collective-permute-start.75 = (bf16[256,1280]{1,0:T(8,128)(2,1)}, bf16[256,1280]{1,0:T(8,128)(2,1)}, u32[]{:S(2)}, u32[]{:S(2)}) collective-permute-start(bf16[256,1280]{1,0:T(8,128)(2,1)} %get-tuple-element.274), channel_id=1, source_target_pairs={{0,8},{8,16},{16,24},{24,0},{1,9},{9,17},{17,25},{25,1},{2,10},{10... | collective-permute-start | bytes 1966088 | tf_op jit(solution)/shard_map/ppermute | solution.py:183
  586.0 30.1 %collective-permute-start.76 = (bf16[256,1280]{1,0:T(8,128)(2,1)}, bf16[256,1280]{1,0:T(8,128)(2,1)}, u32[]{:S(2)}, u32[]{:S(2)}) collective-permute-start(bf16[256,1280]{1,0:T(8,128)(2,1)} %get-tuple-element.275), channel_id=1, source_target_pairs={{0,24},{8,0},{16,8},{24,16},{1,25},{9,1},{17,9},{25,17},{2,26},{10... | collective-permute-start | bytes 1966088 | tf_op jit(solution)/shard_map/ppermute | solution.py:183
  588.6 39.1 %collective-permute-start.83 = (bf16[128,2048]{1,0:T(8,128)(2,1)}, bf16[128,2048]{1,0:T(8,128)(2,1)}, u32[]{:S(2)}, u32[]{:S(2)}) collective-permute-start(bf16[128,2048]{1,0:T(8,128)(2,1)} %fusion.60), channel_id=1, source_target_pairs={{0,24},{8,0},{16,8},{24,16},{1,25},{9,1},{17,9},{25,17},{2,26},{10... | collective-permute-start | bytes 1572872 | tf_op jit(solution)/shard_map/ppermute | solution.py:183
  591.4 62.4 %all-to-all-start.6 = ((f32[32,24,128]{2,1,0:T(8,128)}), f32[32,24,128]{2,1,0:T(8,128)}, u32[]{:S(2)}, u32[]{:S(2)}) async-start(f32[32,24,128]{2,1,0:T(8,128)} %bitcast.299), calls=%async_computation.6 | async-start | bytes 786432 | tf_op jit(solution)/shard_map/all_to_all | solution.py:93
  597.2 55.3 %collective-permute-start.74 = (bf16[128,2048]{1,0:T(8,128)(2,1)S(1)}, bf16[128,2048]{1,0:T(8,128)(2,1)S(1)}, u32[]{:S(2)}, u32[]{:S(2)}) collective-permute-start(bf16[128,2048]{1,0:T(8,128)(2,1)S(1)} %pad_maximum_fusion.21), channel_id=1, source_target_pairs={{0,1},{1,0},{2,3},{3,2},{4,5},{5,4},{6,7},{7,6},{8,9},{9,8},{10,11... | collective-permute-start | bytes 1572872 | tf_op jit(solution)/shard_map/ppermute | solution.py:84
  617.4 30.1 %collective-permute-start.77 = (bf16[256,1280]{1,0:T(8,128)(2,1)S(1)}, bf16[256,1280]{1,0:T(8,128)(2,1)S(1)}, u32[]{:S(2)}, u32[]{:S(2)}) collective-permute-start(bf16[256,1280]{1,0:T(8,128)(2,1)S(1)} %fusion.16), channel_id=1, source_target_pairs={{0,24},{8,0},{16,8},{24,16},{1,25},{9,1},{17,9},{25,17},{2,26},{10... | collective-permute-start | bytes 1966088 | tf_op jit(solution)/shard_map/ppermute | solution.py:183
  (160 other events, 1739.1 us)

commit v7 on v6

--- a/solution.py
+++ b/solution.py
@@ -132,16 +132,20 @@
     return total
 
 
-def far_sum(parts, count):
+def far_begin(parts, count):
+    if count != 4:
+        return [far_shift(parts[step].astype(BF), -step, count) for step in range(1, count)]
+    return [far_shift(parts[2].astype(BF), -1, count), far_shift(parts[3].astype(BF), 1, count)]
+
+
+def far_end(parts, found, count):
     total = parts[0].astype(F32)
     if count != 4:
-        for step in range(1, count):
-            total = total + far_shift(parts[step].astype(BF), -step, count).astype(F32)
+        for part in found:
+            total = total + part.astype(F32)
         return total
-    relay = far_shift(parts[2].astype(BF), -1, count).astype(F32)
-    direct = far_shift(parts[3].astype(BF), 1, count).astype(F32)
-    relay = far_shift((parts[1].astype(F32) + relay).astype(BF), -1, count)
-    return total + direct + relay.astype(F32)
+    relay = (parts[1].astype(F32) + found[0].astype(F32)).astype(BF)
+    return total + found[1].astype(F32) + far_shift(relay, -1, count).astype(F32)
 
 
 def far_parts(values, count):
@@ -582,9 +586,10 @@
     cot_pair = jnp.concatenate(pair_order(cotangent, swap(cotangent, SEQ_AXIS), SEQ_AXIS), axis=0)
     cot_low = mm(hot_half, cot_pair).astype(BF)
     cot_rows = cot_low.astype(F32)
-    cot_low, qkv_far[2] = tie(cot_low, qkv_far[2])
-    cot_sent = mm(slot_low, cot_low).astype(BF).reshape(device_count, capacity, D)
-    cot_back = [exchange(cot_sent[:, :, : D // 2], ALL_AXES), exchange(cot_sent[:, :, D // 2 :], ALL_AXES)]
+    cot_sent = [
+        mm(slot_low, half).astype(BF).reshape(device_count, capacity, D // 2)
+        for half in (cot_low[:, : D // 2], cot_low[:, D // 2 :])
+    ]
     qkv_own = far_stack(qkv_far).reshape(far_count * NEAR, half_rows, width)
     qkv_mine = jnp.stack(pair_order(qkv_own, swap(qkv_own, CORE_AXIS), CORE_AXIS), axis=1).reshape(
         D, width
@@ -601,7 +606,8 @@
         x_both, (near_index, seq_index * TOK_DEV, 0), (1, TOK_DEV, D)
     )[0]
     normed_low = rms_norm(x_both.reshape(2 * ROW, D), gain_attn).astype(BF)
-    projected = mm(normed_low, qkv_mine)
+    projected, *cot_sent = tie(mm(normed_low, qkv_mine), *cot_sent)
+    cot_back = [exchange(half, ALL_AXES) for half in cot_sent]
     cosine, sine_part = tables(pos_both.reshape(2 * ROW), HEAD_DIM)
     shared = (
         jnp.concatenate([cosine, cosine], axis=1),
@@ -614,7 +620,7 @@
     )
     mixed_low = attend(projected, shared, per_group)
     out_found = quad_parts(out_slabs)
-    mixed_low, cot_back[0], *out_found = tie(mixed_low, cot_back[0], *out_found)
+    mixed_low, *out_found = tie(mixed_low, *out_found)
     out_own = quad_order(out_found).reshape(NEAR * 2, far_part, out_rows, D)
     out_own = out_own.transpose(1, 0, 2, 3).reshape(far_part * NEAR, 2 * out_rows, D)
     out_mine = jnp.stack(pair_order(out_own, swap(out_own, CORE_AXIS), CORE_AXIS), axis=1).reshape(
@@ -622,6 +628,7 @@
     )
 
     out_partial = mm(mixed_low, out_mine).astype(BF)
+    out_partial, cot_back[0] = tie(out_partial, cot_back[0])
     residual = x_rows + quad_sum(out_partial.reshape(4, TOK_DEV, D))
 
     normed_two, ffn_back = jax.vjp(rms_norm, residual, gain_ffn)
@@ -726,12 +733,6 @@
     grad_expert = expert_grads(in_rows, grad_rows, gate_grads, up_grads, actives)[None]
 
     resid_both, grad_expert = tie(quad_gather(resid_low), grad_expert)
-    returned = []
-    for half in range(2):
-        gated = far_stack([part[:, :, half * D // 2 : (half + 1) * D // 2] for part in gated_outs])
-        gated, resid_both = tie(gated, resid_both)
-        gated = exchange(gated.reshape(device_count, capacity, D // 2), ALL_AXES)
-        returned.append(gated.reshape(slot_count, D // 2))
     resid_both = resid_both.reshape(2 * ROW, D)
 
     def core_sum(values):
@@ -753,7 +754,16 @@
     query_grad, key_grad, value_grad, query_gain_grad, key_gain_grad = attend_back(
         projected, shared, mixed_grad, per_group
     )
-    query_grad, returned[0] = tie(query_grad, returned[0])
+    query_grad, out_grad = tie(query_grad, out_grad)
+    out_sent = far_parts(out_grad, far_count)
+    out_found = far_begin(out_sent, far_count)
+    gated, query_grad = tie(jnp.stack(gated_outs, axis=1), query_grad)
+    gated = exchange(gated, SLAB_AXES)
+    out_parts = [
+        mm_tn(hot, gated[:, step].reshape(slab * capacity, D)).astype(BF if step else F32)
+        for step, hot in enumerate(chunk_slots)
+    ]
+    out_sum = far_end(out_parts, far_begin(out_parts, far_count), far_count)
     proj_grad = jnp.concatenate([query_grad, key_grad, value_grad], axis=1)
 
     back_grad = lax.dot_general(
@@ -766,18 +776,14 @@
     back_grad, qkv_grad = tie(back_grad, qkv_grad)
     normed_partial = mm_nt(back_grad, qkv_mine).astype(BF)
     qkv_grad = core_sum(qkv_grad.reshape(far_count * NEAR, CORES, half_rows, width)).astype(BF)
-    normed_partial, qkv_grad, out_grad = tie(normed_partial, qkv_grad, out_grad)
-    qkv_grad = far_sum(far_parts(qkv_grad.reshape(far_count, core_rows, width), far_count), far_count)
-    out_share = far_sum(far_parts(out_grad, far_count), far_count)
+    normed_partial, qkv_grad, *out_found = tie(normed_partial, qkv_grad, *out_found)
+    qkv_parts = far_parts(qkv_grad.reshape(far_count, core_rows, width), far_count)
+    qkv_found = far_begin(qkv_parts, far_count)
+    out_share = far_end(out_sent, out_found, far_count)
+    qkv_grad = far_end(qkv_parts, qkv_found, far_count)
     normed_grad = quad_sum(normed_partial.reshape(4, TOK_DEV, D))
-    normed_grad, returned[1] = tie(normed_grad, returned[1])
-    final_rows = jnp.concatenate(
-        [
-            (residual[:, : D // 2] + mm_tn(slot_low, returned[0])).astype(BF),
-            (residual[:, D // 2 :] + mm_tn(slot_low, returned[1])).astype(BF),
-        ],
-        axis=1,
-    )
+    normed_grad, out_sum = tie(normed_grad, out_sum)
+    final_rows = (residual + out_sum).astype(BF)
     final_pair = jnp.concatenate(
         pair_order(final_rows, swap(final_rows, SEQ_AXIS), SEQ_AXIS), axis=0
     )

time: 672 us -> 628 us (0.935)
  other arithmetic: 70.7 us -> 51.7 us
  waiting for transfers between devices: 245 us -> 237 us
    ppermute x30, waiting for transfers between devices: 109 us -> 97.1 us  [quad_send(): return lax.ppermute(block, HEAD_AXES, [(i, i ^ step) for i in range(4)])]
    all_to_all x7 -> x6, starting transfers between devices: 32.5 us -> 27.6 us  [exchange(): return lax.all_to_all(value, axes, split_axis=0, concat_axis=0, tiled=True)]
    ppermute x21 -> x24, waiting for transfers between devices: 88.7 us -> 91.9 us  [far_shift(): lax.ppermute(value, FAR_AXIS, [(i, (i + step) % count) for i in range(cou...]
    dot_general x26 -> x29, matrix products: 47.3 us -> 44.7 us  [dot(): lax.dot_general(left, right, (dims, ((), ())), preferred_element_type=F32)]
    all_to_all x7 -> x6, waiting for transfers between devices: 22.5 us -> 20.5 us  [exchange(): return lax.all_to_all(value, axes, split_axis=0, concat_axis=0, tiled=True)]
    unnamed x284 -> x224, local copies, waits for them, and re-layouts: 20.5 us -> 19.3 us
    ppermute x21 -> x24, starting transfers between devices: 37.3 us -> 38.4 us  [far_shift(): lax.ppermute(value, FAR_AXIS, [(i, (i + step) % count) for i in range(cou...]
  transfers between devices with their start and end apart: 91 -> 93, of which waited for: 34 -> 40; matrix products, arithmetic and copies ran while one was open for 23% -> 18% of each run, Pallas kernels for 15% -> 16%
where the time goes in v7:
time: 628 us; the launch traced here: 620 us
  waiting for transfers between devices  237 us (38%)
  starting transfers between devices  129 us (21%)
  Pallas kernels  97.2 us (15%)
  local copies, waits for them, and re-layouts  54.4 us (9%)
  other arithmetic  51.7 us (8%)
  matrix products  47.1 us (8%)
    ppermute x30, waiting for transfers between devices, quad_send(): return lax.ppermute(block, HEAD_AXES, [(i, i ^ step) for i in range(4)])  97.1 us
    ppermute x24, waiting for transfers between devices, far_shift(): lax.ppermute(value, FAR_AXIS, [(i, (i + step) % count) for i in range(cou...  91.9 us
    dot_general x29, matrix products, dot(): lax.dot_general(left, right, (dims, ((), ())), preferred_element_type=F32)  44.7 us
    ppermute x24, starting transfers between devices, far_shift(): lax.ppermute(value, FAR_AXIS, [(i, (i + step) % count) for i in range(cou...  38.4 us
    pallas_call x4, Pallas kernels, expert_chunk(): pl.pallas_call(expert_kernel, grid_spec=pltpu.PrefetchScalarGridSpec(num_...  38.4 us
    ppermute x30, starting transfers between devices, quad_send(): return lax.ppermute(block, HEAD_AXES, [(i, i ^ step) for i in range(4)])  35.5 us
    all_to_all x6, starting transfers between devices, exchange(): return lax.all_to_all(value, axes, split_axis=0, concat_axis=0, tiled=True)  27.6 us
    pallas_call x1, Pallas kernels, attend_back(): pl.pallas_call(attend_back_kernel, grid=(rows // ROW, heads), in_specs=sp...  23.8 us
  transfers between devices with their start and end apart: 93, of which 40 were waited for; matrix products, arithmetic and copies ran while one was open for 18% of the time, Pallas kernels for 16%

profile of v7, /device:TPU:0, one launch (start us, length us, event | category | flops | bytes accessed | tf_op | source)
XLA Modules:
  0.0 619.6 jit_solution(17850059271342140045)
XLA Ops:
  1.3 3.0 collective-permute-start
  18.6 2.5 collective-permute-start.3
  25.0 3.0 all-to-all-start
  29.7 2.7 collective-permute-start.6
  42.7 11.1 %collective-permute-done.7 = bf16[256,1280]{1,0:T(8,128)(2,1)} collective-permute-done((bf16[256,1280]{1,0:T(8,128)(2,1)}, bf16[256,1280]{1,0:T(8,128)(2,1)}, u32[]{:S(2)}, u32[]{:S(2)}) %collective-permute-start.7) | collective-permute-done | bytes 655392 | tf_op jit(solution)/shard_map/ppermute | solution.py:187
  57.0 23.4 %collective-permute-done.8 = bf16[256,1280]{1,0:T(8,128)(2,1)S(1)} collective-permute-done((bf16[256,1280]{1,0:T(8,128)(2,1)}, bf16[256,1280]{1,0:T(8,128)(2,1)S(1)}, u32[]{:S(2)}, u32[]{:S(2)}) %collective-permute-start.8) | collective-permute-done | bytes 655392 | tf_op jit(solution)/shard_map/ppermute | solution.py:187
  87.2 5.7 collective-permute-done.4
  98.6 4.4 fusion.175.query_ref.key_ref.value_ref
  103.0 4.2 all-to-all-start.1
  112.8 2.7 dynamic-slice_bitcast_fusion.17
  115.6 2.4 collective-permute-start.17
  121.6 16.4 %attend.1 = bf16[512,1024]{1,0:T(8,128)(2,1)} custom-call(f32[512,1280]{1,0:T(8,128)} %fusion.175.query_ref.key_ref.value_ref, f32[512,1280]{1,0:T(8,128)} %fusion.175.query_ref.key_ref.value_ref, f32[512,1280]{1,0:T(8,128)} %fusion.175.query_ref.key_ref.value_ref, f32[512,128]{1,0:T(8,128)} %get-tuple-element.444.cos_ref, ...), custom_call_target="tpu_custom_call" | custom-call | flops 1048576 | bytes 1048576 | tf_op jit(solution)/shard_map/attend/pallas_call | solution.py:431
  138.0 4.1 collective-permute-done.17
  142.2 12.9 %collective-permute-done.16 = bf16[128,2048]{1,0:T(8,128)(2,1)} collective-permute-done((bf16[128,2048]{1,0:T(8,128)(2,1)}, bf16[128,2048]{1,0:T(8,128)(2,1)}, u32[]{:S(2)}, u32[]{:S(2)}) %collective-permute-start.16) | collective-permute-done | bytes 524320 | tf_op jit(solution)/shard_map/ppermute | solution.py:102
  155.1 2.4 collective-permute-done.15
  161.6 3.0 collective-permute-start.24
  167.6 5.4 all-to-all-start.2
  173.2 2.5 select_bitcast_fusion.3
  176.9 2.4 convolution_convert_fusion.2
  185.4 22.9 %collective-permute-done.19 = bf16[128,2048]{1,0:T(8,128)(2,1)S(1)} collective-permute-done((bf16[128,2048]{1,0:T(8,128)(2,1)S(1)}, bf16[128,2048]{1,0:T(8,128)(2,1)S(1)}, u32[]{:S(2)}, u32[]{:S(2)}) %collective-permute-start.19) | collective-permute-done | bytes 524320 | tf_op jit(solution)/shard_map/ppermute | solution.py:102
  208.3 13.4 %collective-permute-done.21 = bf16[128,2048]{1,0:T(8,128)(2,1)} collective-permute-done((bf16[128,2048]{1,0:T(8,128)(2,1)S(1)}, bf16[128,2048]{1,0:T(8,128)(2,1)}, u32[]{:S(2)}, u32[]{:S(2)}) %collective-permute-start.21) | collective-permute-done | bytes 524320 | tf_op jit(solution)/shard_map/ppermute | solution.py:102
  224.1 2.5 collective-permute-start.29
  227.4 2.2 collective-permute-start.27
  233.3 7.0 %collective-permute-done.26 = bf16[2,32,2048]{2,1,0:T(8,128)(2,1)S(1)} collective-permute-done((bf16[2,32,2048]{2,1,0:T(8,128)(2,1)S(1)}, bf16[2,32,2048]{2,1,0:T(8,128)(2,1)S(1)}, u32[]{:S(2)}, u32[]{:S(2)}) %collective-permute-start.26) | collective-permute-done | bytes 262176 | tf_op jit(solution)/shard_map/rows_out0/ppermute | solution.py:195
  248.9 9.5 %expert_chunk.4 = (bf16[256,768]{1,0:T(8,128)(2,1)S(1)}, bf16[256,768]{1,0:T(8,128)(2,1)S(1)}, bf16[256,768]{1,0:T(8,128)(2,1)S(1)}, bf16[256,2048]{1,0:T(8,128)...) custom-call(s32[1]{0:T(128)} %bitcast.55.here_ref, ...), custom_call_target="tpu_custom_call" | custom-call | flops 1048576 | bytes 1048576 | tf_op jit(solution)/shard_map/expert_chunk/pallas_call | solution.py:268
  259.3 3.2 collective-permute-done.34
  267.8 9.4 %expert_chunk.5 = (bf16[256,768]{1,0:T(8,128)(2,1)S(1)}, bf16[256,768]{1,0:T(8,128)(2,1)S(1)}, bf16[256,768]{1,0:T(8,128)(2,1)S(1)}, bf16[256,2048]{1,0:T(8,128)...) custom-call(s32[1]{0:T(128)} %bitcast.55.here_ref, ...), custom_call_target="tpu_custom_call" | custom-call | flops 1048576 | bytes 1048576 | tf_op jit(solution)/shard_map/expert_chunk/pallas_call | solution.py:268
  287.1 9.8 %expert_chunk.6 = (bf16[256,768]{1,0:T(8,128)(2,1)S(1)}, bf16[256,768]{1,0:T(8,128)(2,1)S(1)}, bf16[256,768]{1,0:T(8,128)(2,1)S(1)}, bf16[256,2048]{1,0:T(8,128)...) custom-call(s32[1]{0:T(128)} %bitcast.55.here_ref, ...), custom_call_target="tpu_custom_call" | custom-call | flops 1048576 | bytes 1048576 | tf_op jit(solution)/shard_map/expert_chunk/pallas_call | solution.py:268
  300.8 2.4 collective-permute-done.47
  303.2 3.4 collective-permute-done.45
  312.7 9.6 %expert_chunk.7 = (bf16[256,768]{1,0:T(8,128)(2,1)S(1)}, bf16[256,768]{1,0:T(8,128)(2,1)S(1)}, bf16[256,768]{1,0:T(8,128)(2,1)S(1)}, bf16[256,2048]{1,0:T(8,128)...) custom-call(s32[1]{0:T(128)} %bitcast.55.here_ref, ...), custom_call_target="tpu_custom_call" | custom-call | flops 1048576 | bytes 1048576 | tf_op jit(solution)/shard_map/expert_chunk/pallas_call | solution.py:268
  326.4 3.5 collective-permute-start.56
  331.0 2.5 fusion.12
  339.3 2.7 collective-permute-done.56
  343.9 4.4 collective-permute-done.60
  352.0 5.4 all-to-all-start.3
  357.3 2.3 fusion.82
  363.1 17.3 %all-to-all-done.3 = f32[32,1,32]{2,1,0:T(1,128)S(1)} async-done(((f32[32,1,32]{2,1,0:T(1,128)}), f32[32,1,32]{2,1,0:T(1,128)S(1)}, u32[]{:S(2)}, u32[]{:S(2)}) %all-to-all-start.3) | async-done | bytes 4128 | tf_op jit(solution)/shard_map/all_to_all | solution.py:93
  381.1 3.1 multiply_reduce_fusion.1
  388.3 18.6 %expert_grads.1 = f32[2048,2304]{1,0:T(8,128)} custom-call(bf16[256,2048]{1,0:T(8,128)(2,1)S(1)} %bitcast.635, bf16[256,2048]{1,0:T(8,128)(2,1)} %bitcast.637, bf16[256,2048]{1,0:T(8,128)(2,1)} %bitcast.639, bf16[256,2048]{1,0:T(8,128)(2,1)} %bitcast.641, bf16[256,2048]{1,0:T(8,128)(2,1)} %copy-done.3, bf16[256,2048]{1,0:T(8,128)(2,1)} %copy-done.4, ...), custom_call_target="tpu_custom_call" | custom-call | flops 1048576 | bytes 1048576 | tf_op jit(solution)/shard_map/expert_grads/pallas_call | solution.py:320
  407.0 3.6 collective-permute-done.64
  412.0 2.4 convolution_convert_fusion.1
  416.6 3.3 convolution_convert_fusion.16.grad_ref
  431.1 23.8 %attend_back.1 = (bf16[512,1024]{1,0:T(8,128)(2,1)}, bf16[512,128]{1,0:T(8,128)(2,1)}, bf16[512,128]{1,0:T(8,128)(2,1)}, f32[1,128]{1,0:T(1,128)}, f32[1,128]{1,0:T(1,128)}) custom-call(f32[512,1280]{1,0:T(8,128)} %fusion.175.query_ref.key_ref.value_ref, f32[512,1280]{1,0:T(8,128)} %fusion.175.query_ref.key_ref.value_ref, ...), custom_call_target="tpu_custom_call" | custom-call | flops 1048576 | bytes 1048576 | tf_op jit(solution)/shard_map/attend_back/pallas_call | solution.py:446
  460.7 3.4 convolution_convert_fusion
  470.2 4.7 all-to-all-start.4
  477.0 3.2 collective-permute-start.71
  480.3 5.6 convolution_convert_fusion.3
  485.9 3.0 fusion
  488.9 4.1 collective-permute-done.72
  493.0 9.2 %collective-permute-done.71 = bf16[128,2048]{1,0:T(8,128)(2,1)S(1)} collective-permute-done((bf16[128,2048]{1,0:T(8,128)(2,1)S(1)}, bf16[128,2048]{1,0:T(8,128)(2,1)S(1)}, u32[]{:S(2)}, u32[]{:S(2)}) %collective-permute-start.71) | collective-permute-done | bytes 524320 | tf_op jit(solution)/shard_map/ppermute | solution.py:187
  509.2 7.8 %collective-permute-done.86 = bf16[128,2048]{1,0:T(8,128)(2,1)S(1)} collective-permute-done((bf16[128,2048]{1,0:T(8,128)(2,1)S(1)}, bf16[128,2048]{1,0:T(8,128)(2,1)S(1)}, u32[]{:S(2)}, u32[]{:S(2)}) %collective-permute-start.86) | collective-permute-done | bytes 524320 | tf_op jit(solution)/shard_map/ppermute | solution.py:187
  517.0 4.3 collective-permute-start.81
  522.5 12.2 %collective-permute-done.73 = bf16[128,2048]{1,0:T(8,128)(2,1)S(1)} collective-permute-done((bf16[128,2048]{1,0:T(8,128)(2,1)S(1)}, bf16[128,2048]{1,0:T(8,128)(2,1)S(1)}, u32[]{:S(2)}, u32[]{:S(2)}) %collective-permute-start.73) | collective-permute-done | bytes 524320 | tf_op jit(solution)/shard_map/ppermute | solution.py:102
  534.7 11.7 %collective-permute-done.75 = bf16[128,2048]{1,0:T(8,128)(2,1)S(1)} collective-permute-done((bf16[128,2048]{1,0:T(8,128)(2,1)S(1)}, bf16[128,2048]{1,0:T(8,128)(2,1)S(1)}, u32[]{:S(2)}, u32[]{:S(2)}) %collective-permute-start.75) | collective-permute-done | bytes 524320 | tf_op jit(solution)/shard_map/ppermute | solution.py:102
  546.9 2.5 collective-permute-start.82
  549.5 2.8 fusion.166
  555.1 9.7 %collective-permute-done.82 = bf16[256,1280]{1,0:T(8,128)(2,1)} collective-permute-done((bf16[256,1280]{1,0:T(8,128)(2,1)S(1)}, bf16[256,1280]{1,0:T(8,128)(2,1)}, u32[]{:S(2)}, u32[]{:S(2)}) %collective-permute-start.82) | collective-permute-done | bytes 655392 | tf_op jit(solution)/shard_map/ppermute | solution.py:187
  576.3 4.4 collective-permute-start.78
  581.8 6.3 %collective-permute-done.76 = bf16[128,2048]{1,0:T(8,128)(2,1)S(1)} collective-permute-done((bf16[128,2048]{1,0:T(8,128)(2,1)S(1)}, bf16[128,2048]{1,0:T(8,128)(2,1)S(1)}, u32[]{:S(2)}, u32[]{:S(2)}) %collective-permute-start.76) | collective-permute-done | bytes 524320 | tf_op jit(solution)/shard_map/ppermute | solution.py:187
  588.1 9.5 %collective-permute-done.78 = bf16[128,2048]{1,0:T(8,128)(2,1)S(1)} collective-permute-done((bf16[128,2048]{1,0:T(8,128)(2,1)S(1)}, bf16[128,2048]{1,0:T(8,128)(2,1)S(1)}, u32[]{:S(2)}, u32[]{:S(2)}) %collective-permute-start.78) | collective-permute-done | bytes 524320 | tf_op jit(solution)/shard_map/ppermute | solution.py:187
  600.1 4.9 all-to-all-start.5
  605.1 2.5 fusion.10
  607.5 7.8 %collective-permute-done.79 = bf16[128,2048]{1,0:T(8,128)(2,1)S(1)} collective-permute-done((bf16[128,2048]{1,0:T(8,128)(2,1)S(1)}, bf16[128,2048]{1,0:T(8,128)(2,1)S(1)}, u32[]{:S(2)}, u32[]{:S(2)}) %collective-permute-start.79) | collective-permute-done | bytes 524320 | tf_op jit(solution)/shard_map/ppermute | solution.py:84
  (579 shorter events, 193.9 us)
Async XLA Ops:
  1.3 17.3 %collective-permute-start = (s32[1,384]{1,0:T(1,128)S(1)}, s32[1,384]{1,0:T(1,128)S(1)}, u32[]{:S(2)}, u32[]{:S(2)}) collective-permute-start(s32[1,384]{1,0:T(1,128)S(1)} %pad_add_fusion), channel_id=1, source_target_pairs={{0,4},{4,0},{1,5},{5,1},{2,6},{6,2},{3,7},{7,3},{8,12},{12,8},{9,1... | collective-permute-start | bytes 4616 | tf_op jit(solution)/shard_map/ppermute | solution.py:84
  4.3 35.4 %collective-permute-start.11 = (bf16[128,2048]{1,0:T(8,128)(2,1)}, bf16[128,2048]{1,0:T(8,128)(2,1)}, u32[]{:S(2)}, u32[]{:S(2)}) collective-permute-start(bf16[128,2048]{1,0:T(8,128)(2,1)} %param.12), channel_id=1, source_target_pairs={{0,1},{1,0},{2,3},{3,2},{4,5},{5,4},{6,7},{7,6},{8,9},{9,8},{10,11... | collective-permute-start | bytes 1572872 | tf_op jit(solution)/shard_map/ppermute | solution.py:84
  5.8 77.3 %collective-permute-start.12 = (bf16[128,2048]{1,0:T(8,128)(2,1)}, bf16[128,2048]{1,0:T(8,128)(2,1)}, u32[]{:S(2)}, u32[]{:S(2)}) collective-permute-start(bf16[128,2048]{1,0:T(8,128)(2,1)} %param.14), channel_id=1, source_target_pairs={{0,8},{8,16},{16,24},{24,0},{1,9},{9,17},{17,25},{25,1},{2,10},{10... | collective-permute-start | bytes 1572872 | tf_op jit(solution)/shard_map/ppermute | solution.py:187
  11.5 18.2 %collective-permute-start.1 = (bf16[64,1280]{1,0:T(8,128)(2,1)S(1)}, bf16[64,1280]{1,0:T(8,128)(2,1)S(1)}, u32[]{:S(2)}, u32[]{:S(2)}) collective-permute-start(bf16[64,1280]{1,0:T(8,128)(2,1)S(1)} %bitcast.738), channel_id=1, source_target_pairs={{0,1},{1,0},{4,5},{5,4},{2,3},{3,2},{6,7},{7,6},{8,9},{9,8},{12,13... | collective-permute-start | bytes 491528 | tf_op jit(solution)/shard_map/ppermute | solution.py:102
  12.1 17.6 %collective-permute-start.2 = (bf16[64,1280]{1,0:T(8,128)(2,1)S(1)}, bf16[64,1280]{1,0:T(8,128)(2,1)S(1)}, u32[]{:S(2)}, u32[]{:S(2)}) collective-permute-start(bf16[64,1280]{1,0:T(8,128)(2,1)S(1)} %bitcast.739), channel_id=1, source_target_pairs={{0,4},{1,5},{4,0},{5,1},{2,6},{3,7},{6,2},{7,3},{8,12},{9,13},{12,... | collective-permute-start | bytes 491528 | tf_op jit(solution)/shard_map/ppermute | solution.py:102
  29.7 56.8 %collective-permute-start.6 = (bf16[128,2048]{1,0:T(8,128)(2,1)S(1)}, bf16[128,2048]{1,0:T(8,128)(2,1)}, u32[]{:S(2)}, u32[]{:S(2)}) collective-permute-start(bf16[128,2048]{1,0:T(8,128)(2,1)S(1)} %copy-done.53), channel_id=1, source_target_pairs={{0,5},{1,4},{4,1},{5,0},{2,7},{3,6},{6,3},{7,2},{8,13},{9,12},{12,... | collective-permute-start | bytes 1572872 | tf_op jit(solution)/shard_map/ppermute | solution.py:114
  32.5 54.7 %collective-permute-start.5 = (bf16[128,2048]{1,0:T(8,128)(2,1)S(1)}, bf16[128,2048]{1,0:T(8,128)(2,1)}, u32[]{:S(2)}, u32[]{:S(2)}) collective-permute-start(bf16[128,2048]{1,0:T(8,128)(2,1)S(1)} %copy-done.53), channel_id=1, source_target_pairs={{0,4},{1,5},{4,0},{5,1},{2,6},{3,7},{6,2},{7,3},{8,12},{9,13},{12,... | collective-permute-start | bytes 1572872 | tf_op jit(solution)/shard_map/ppermute | solution.py:114
  34.0 19.8 %collective-permute-start.7 = (bf16[256,1280]{1,0:T(8,128)(2,1)}, bf16[256,1280]{1,0:T(8,128)(2,1)}, u32[]{:S(2)}, u32[]{:S(2)}) collective-permute-start(bf16[256,1280]{1,0:T(8,128)(2,1)} %bitcast.18), channel_id=1, source_target_pairs={{0,8},{8,16},{16,24},{24,0},{1,9},{9,17},{17,25},{25,1},{2,10},{10... | collective-permute-start | bytes 1966088 | tf_op jit(solution)/shard_map/ppermute | solution.py:187
  39.7 41.2 %collective-permute-start.9 = (bf16[256,1280]{1,0:T(8,128)(2,1)}, bf16[256,1280]{1,0:T(8,128)(2,1)S(1)}, u32[]{:S(2)}, u32[]{:S(2)}) collective-permute-start(bf16[256,1280]{1,0:T(8,128)(2,1)} %bitcast.18), channel_id=1, source_target_pairs={{0,24},{8,0},{16,8},{24,16},{1,25},{9,1},{17,9},{25,17},{2,26},{10... | collective-permute-start | bytes 1966088 | tf_op jit(solution)/shard_map/ppermute | solution.py:187
  53.8 26.6 %collective-permute-start.8 = (bf16[256,1280]{1,0:T(8,128)(2,1)}, bf16[256,1280]{1,0:T(8,128)(2,1)S(1)}, u32[]{:S(2)}, u32[]{:S(2)}) collective-permute-start(bf16[256,1280]{1,0:T(8,128)(2,1)} %collective-permute-done.7), channel_id=1, source_target_pairs={{0,8},{8,16},{16,24},{24,0},{1,9},{9,17},{17,25},{25,1},{2,10},{10... | collective-permute-start | bytes 1966088 | tf_op jit(solution)/shard_map/ppermute | solution.py:187
  81.0 16.5 %collective-permute-start.10 = (bf16[8,128,1280]{2,1,0:T(8,128)(2,1)S(1)}, bf16[8,128,1280]{2,1,0:T(8,128)(2,1)S(1)}, u32[]{:S(2)}, u32[]{:S(2)}) collective-permute-start(bf16[8,128,1280]{2,1,0:T(8,128)(2,1)S(1)} %bitcast.673), channel_id=1, source_target_pairs={{0,2},{2,0},{1,3},{3,1},{4,6},{6,4},{5,7},{7,5},{8,10},{10,8},{9,1... | collective-permute-start | bytes 7864328 | tf_op jit(solution)/shard_map/ppermute | solution.py:84
  83.1 27.9 %collective-permute-start.14 = (bf16[128,2048]{1,0:T(8,128)(2,1)}, bf16[128,2048]{1,0:T(8,128)(2,1)}, u32[]{:S(2)}, u32[]{:S(2)}) collective-permute-start(bf16[128,2048]{1,0:T(8,128)(2,1)} %param.14), channel_id=1, source_target_pairs={{0,24},{8,0},{16,8},{24,16},{1,25},{9,1},{17,9},{25,17},{2,26},{10... | collective-permute-start | bytes 1572872 | tf_op jit(solution)/shard_map/ppermute | solution.py:187
  86.6 22.5 %collective-permute-start.13 = (bf16[128,2048]{1,0:T(8,128)(2,1)}, bf16[128,2048]{1,0:T(8,128)(2,1)}, u32[]{:S(2)}, u32[]{:S(2)}) collective-permute-start(bf16[128,2048]{1,0:T(8,128)(2,1)} %collective-permute-done.12), channel_id=1, source_target_pairs={{0,8},{8,16},{16,24},{24,0},{1,9},{9,17},{17,25},{25,1},{2,10},{10... | collective-permute-start | bytes 1572872 | tf_op jit(solution)/shard_map/ppermute | solution.py:187
  103.0 63.2 %all-to-all-start.1 = ((bf16[32,32,1024]{2,1,0:T(8,128)(2,1)}), bf16[32,32,1024]{2,1,0:T(8,128)(2,1)S(1)}, u32[]{:S(2)}, u32[]{:S(2)}) async-start(bf16[32,32,1024]{2,1,0:T(8,128)(2,1)} %bitcast.27), calls=%async_computation.1 | async-start | bytes 4194304 | tf_op jit(solution)/shard_map/all_to_all | solution.py:93
  115.6 26.6 %collective-permute-start.17 = (bf16[128,2048]{1,0:T(8,128)(2,1)}, bf16[128,2048]{1,0:T(8,128)(2,1)S(1)}, u32[]{:S(2)}, u32[]{:S(2)}) collective-permute-start(bf16[128,2048]{1,0:T(8,128)(2,1)} %get-tuple-element.299), channel_id=1, source_target_pairs={{0,5},{1,4},{4,1},{5,0},{2,7},{3,6},{6,3},{7,2},{8,13},{9,12},{12,... | collective-permute-start | bytes 1572872 | tf_op jit(solution)/shard_map/ppermute | solution.py:102
  117.9 37.2 %collective-permute-start.16 = (bf16[128,2048]{1,0:T(8,128)(2,1)}, bf16[128,2048]{1,0:T(8,128)(2,1)}, u32[]{:S(2)}, u32[]{:S(2)}) collective-permute-start(bf16[128,2048]{1,0:T(8,128)(2,1)} %get-tuple-element.300), channel_id=1, source_target_pairs={{0,4},{1,5},{4,0},{5,1},{2,6},{3,7},{6,2},{7,3},{8,12},{9,13},{12,... | collective-permute-start | bytes 1572872 | tf_op jit(solution)/shard_map/ppermute | solution.py:102
  118.4 39.1 %collective-permute-start.15 = (bf16[128,2048]{1,0:T(8,128)(2,1)}, bf16[128,2048]{1,0:T(8,128)(2,1)}, u32[]{:S(2)}, u32[]{:S(2)}) collective-permute-start(bf16[128,2048]{1,0:T(8,128)(2,1)} %get-tuple-element.301), channel_id=1, source_target_pairs={{0,1},{1,0},{4,5},{5,4},{2,3},{3,2},{6,7},{7,6},{8,9},{9,8},{12,13... | collective-permute-start | bytes 1572872 | tf_op jit(solution)/shard_map/ppermute | solution.py:102
  167.6 59.0 %all-to-all-start.2 = ((bf16[32,32,1024]{2,1,0:T(8,128)(2,1)}), bf16[32,32,1024]{2,1,0:T(8,128)(2,1)}, u32[]{:S(2)}, u32[]{:S(2)}) async-start(bf16[32,32,1024]{2,1,0:T(8,128)(2,1)} %bitcast.28), calls=%async_computation.2 | async-start | bytes 4194304 | tf_op jit(solution)/shard_map/all_to_all | solution.py:93
  179.5 28.8 %collective-permute-start.19 = (bf16[128,2048]{1,0:T(8,128)(2,1)S(1)}, bf16[128,2048]{1,0:T(8,128)(2,1)S(1)}, u32[]{:S(2)}, u32[]{:S(2)}) collective-permute-start(bf16[128,2048]{1,0:T(8,128)(2,1)S(1)} %get-tuple-element.292), channel_id=1, source_target_pairs={{0,1},{1,0},{4,5},{5,4},{2,3},{3,2},{6,7},{7,6},{8,9},{9,8},{12,13... | collective-permute-start | bytes 1572872 | tf_op jit(solution)/shard_map/ppermute | solution.py:102
  181.4 40.3 %collective-permute-start.21 = (bf16[128,2048]{1,0:T(8,128)(2,1)S(1)}, bf16[128,2048]{1,0:T(8,128)(2,1)}, u32[]{:S(2)}, u32[]{:S(2)}) collective-permute-start(bf16[128,2048]{1,0:T(8,128)(2,1)S(1)} %get-tuple-element.293), channel_id=1, source_target_pairs={{0,5},{1,4},{4,1},{5,0},{2,7},{3,6},{6,3},{7,2},{8,13},{9,12},{12,... | collective-permute-start | bytes 1572872 | tf_op jit(solution)/shard_map/ppermute | solution.py:102
  182.9 38.9 %collective-permute-start.20 = (bf16[128,2048]{1,0:T(8,128)(2,1)S(1)}, bf16[128,2048]{1,0:T(8,128)(2,1)}, u32[]{:S(2)}, u32[]{:S(2)}) collective-permute-start(bf16[128,2048]{1,0:T(8,128)(2,1)S(1)} %get-tuple-element.294), channel_id=1, source_target_pairs={{0,4},{1,5},{4,0},{5,1},{2,6},{3,7},{6,2},{7,3},{8,12},{9,13},{12,... | collective-permute-start | bytes 1572872 | tf_op jit(solution)/shard_map/ppermute | solution.py:102
  224.1 17.7 %collective-permute-start.29 = (bf16[128,2048]{1,0:T(8,128)(2,1)S(1)}, bf16[128,2048]{1,0:T(8,128)(2,1)}, u32[]{:S(2)}, u32[]{:S(2)}) collective-permute-start(bf16[128,2048]{1,0:T(8,128)(2,1)S(1)} %multiply_convert_fusion.1), channel_id=1, source_target_pairs={{0,8},{8,16},{16,24},{24,0},{1,9},{9,17},{17,25},{25,1},{2,10},{10... | collective-permute-start | bytes 1572872 | tf_op jit(solution)/shard_map/rows_far1/ppermute | solution.py:187
  243.4 15.0 %collective-permute-start.31 = (bf16[2,32,2048]{2,1,0:T(8,128)(2,1)S(1)}, bf16[2,32,2048]{2,1,0:T(8,128)(2,1)S(1)}, u32[]{:S(2)}, u32[]{:S(2)}) collective-permute-start(bf16[2,32,2048]{2,1,0:T(8,128)(2,1)S(1)} %bitcast.736), channel_id=1, source_target_pairs={{0,4},{1,5},{4,0},{5,1},{2,6},{3,7},{6,2},{7,3},{8,12},{9,13},{12,... | collective-permute-start | bytes 786440 | tf_op jit(solution)/shard_map/rows_out1/ppermute | solution.py:195
  244.1 14.3 %collective-permute-start.32 = (bf16[2,32,2048]{2,1,0:T(8,128)(2,1)S(1)}, bf16[2,32,2048]{2,1,0:T(8,128)(2,1)S(1)}, u32[]{:S(2)}, u32[]{:S(2)}) collective-permute-start(bf16[2,32,2048]{2,1,0:T(8,128)(2,1)S(1)} %bitcast.734), channel_id=1, source_target_pairs={{0,5},{1,4},{4,1},{5,0},{2,7},{3,6},{6,3},{7,2},{8,13},{9,12},{12,... | collective-permute-start | bytes 786440 | tf_op jit(solution)/shard_map/rows_out1/ppermute | solution.py:195
  246.9 15.5 %collective-permute-start.34 = (bf16[128,2048]{1,0:T(8,128)(2,1)}, bf16[128,2048]{1,0:T(8,128)(2,1)S(1)}, u32[]{:S(2)}, u32[]{:S(2)}) collective-permute-start(bf16[128,2048]{1,0:T(8,128)(2,1)} %collective-permute-done.29), channel_id=1, source_target_pairs={{0,8},{8,16},{16,24},{24,0},{1,9},{9,17},{17,25},{25,1},{2,10},{10... | collective-permute-start | bytes 1572872 | tf_op jit(solution)/shard_map/rows_far2/ppermute | solution.py:187
  263.0 14.3 %collective-permute-start.36 = (bf16[2,32,2048]{2,1,0:T(8,128)(2,1)S(1)}, bf16[2,32,2048]{2,1,0:T(8,128)(2,1)S(1)}, u32[]{:S(2)}, u32[]{:S(2)}) collective-permute-start(bf16[2,32,2048]{2,1,0:T(8,128)(2,1)S(1)} %bitcast.737), channel_id=1, source_target_pairs={{0,4},{1,5},{4,0},{5,1},{2,6},{3,7},{6,2},{7,3},{8,12},{9,13},{12,... | collective-permute-start | bytes 786440 | tf_op jit(solution)/shard_map/rows_out2/ppermute | solution.py:195
  281.0 16.0 %collective-permute-start.41 = (bf16[2,32,2048]{2,1,0:T(8,128)(2,1)S(1)}, bf16[2,32,2048]{2,1,0:T(8,128)(2,1)S(1)}, u32[]{:S(2)}, u32[]{:S(2)}) collective-permute-start(bf16[2,32,2048]{2,1,0:T(8,128)(2,1)S(1)} %bitcast.731), channel_id=1, source_target_pairs={{0,4},{1,5},{4,0},{5,1},{2,6},{3,7},{6,2},{7,3},{8,12},{9,13},{12,... | collective-permute-start | bytes 786440 | tf_op jit(solution)/shard_map/rows_out3/ppermute | solution.py:195
  281.8 16.7 %collective-permute-start.42 = (bf16[2,32,2048]{2,1,0:T(8,128)(2,1)S(1)}, bf16[2,32,2048]{2,1,0:T(8,128)(2,1)S(1)}, u32[]{:S(2)}, u32[]{:S(2)}) collective-permute-start(bf16[2,32,2048]{2,1,0:T(8,128)(2,1)S(1)} %bitcast.730), channel_id=1, source_target_pairs={{0,5},{1,4},{4,1},{5,0},{2,7},{3,6},{6,3},{7,2},{8,13},{9,12},{12,... | collective-permute-start | bytes 786440 | tf_op jit(solution)/shard_map/rows_out3/ppermute | solution.py:195
  283.6 14.9 %collective-permute-start.40 = (bf16[2,32,2048]{2,1,0:T(8,128)(2,1)S(1)}, bf16[2,32,2048]{2,1,0:T(8,128)(2,1)S(1)}, u32[]{:S(2)}, u32[]{:S(2)}) collective-permute-start(bf16[2,32,2048]{2,1,0:T(8,128)(2,1)S(1)} %bitcast.729), channel_id=1, source_target_pairs={{0,1},{1,0},{4,5},{5,4},{2,3},{3,2},{6,7},{7,6},{8,9},{9,8},{12,13... | collective-permute-start | bytes 786440 | tf_op jit(solution)/shard_map/rows_out3/ppermute | solution.py:195
  284.7 18.5 %collective-permute-start.47 = (bf16[2,32,2048]{2,1,0:T(8,128)(2,1)S(1)}, bf16[2,32,2048]{2,1,0:T(8,128)(2,1)S(1)}, u32[]{:S(2)}, u32[]{:S(2)}) collective-permute-start(bf16[2,32,2048]{2,1,0:T(8,128)(2,1)S(1)} %get-tuple-element.341), channel_id=1, source_target_pairs={{0,5},{1,4},{4,1},{5,0},{2,7},{3,6},{6,3},{7,2},{8,13},{9,12},{12,... | collective-permute-start | bytes 786440 | tf_op jit(solution)/shard_map/rows_back1/ppermute | solution.py:102
  285.7 20.9 %collective-permute-start.45 = (bf16[2,32,2048]{2,1,0:T(8,128)(2,1)S(1)}, bf16[2,32,2048]{2,1,0:T(8,128)(2,1)S(1)}, u32[]{:S(2)}, u32[]{:S(2)}) collective-permute-start(bf16[2,32,2048]{2,1,0:T(8,128)(2,1)S(1)} %get-tuple-element.343), channel_id=1, source_target_pairs={{0,1},{1,0},{4,5},{5,4},{2,3},{3,2},{6,7},{7,6},{8,9},{9,8},{12,13... | collective-permute-start | bytes 786440 | tf_op jit(solution)/shard_map/rows_back1/ppermute | solution.py:102
  309.2 21.7 %collective-permute-start.51 = (bf16[2,32,2048]{2,1,0:T(8,128)(2,1)}, bf16[2,32,2048]{2,1,0:T(8,128)(2,1)}, u32[]{:S(2)}, u32[]{:S(2)}) collective-permute-start(bf16[2,32,2048]{2,1,0:T(8,128)(2,1)} %get-tuple-element.329), channel_id=1, source_target_pairs={{0,5},{1,4},{4,1},{5,0},{2,7},{3,6},{6,3},{7,2},{8,13},{9,12},{12,... | collective-permute-start | bytes 786440 | tf_op jit(solution)/shard_map/rows_back2/ppermute | solution.py:102
  310.7 20.3 %collective-permute-start.49 = (bf16[2,32,2048]{2,1,0:T(8,128)(2,1)}, bf16[2,32,2048]{2,1,0:T(8,128)(2,1)}, u32[]{:S(2)}, u32[]{:S(2)}) collective-permute-start(bf16[2,32,2048]{2,1,0:T(8,128)(2,1)} %get-tuple-element.331), channel_id=1, source_target_pairs={{0,1},{1,0},{4,5},{5,4},{2,3},{3,2},{6,7},{7,6},{8,9},{9,8},{12,13... | collective-permute-start | bytes 786440 | tf_op jit(solution)/shard_map/rows_back2/ppermute | solution.py:102
  311.7 19.3 %collective-permute-start.50 = (bf16[2,32,2048]{2,1,0:T(8,128)(2,1)}, bf16[2,32,2048]{2,1,0:T(8,128)(2,1)}, u32[]{:S(2)}, u32[]{:S(2)}) collective-permute-start(bf16[2,32,2048]{2,1,0:T(8,128)(2,1)} %get-tuple-element.332), channel_id=1, source_target_pairs={{0,4},{1,5},{4,0},{5,1},{2,6},{3,7},{6,2},{7,3},{8,12},{9,13},{12,... | collective-permute-start | bytes 786440 | tf_op jit(solution)/shard_map/rows_back2/ppermute | solution.py:102
  326.4 15.6 %collective-permute-start.56 = (bf16[128,2048]{1,0:T(8,128)(2,1)}, bf16[128,2048]{1,0:T(8,128)(2,1)}, u32[]{:S(2)}, u32[]{:S(2)}) collective-permute-start(bf16[128,2048]{1,0:T(8,128)(2,1)} %fusion.11), channel_id=1, source_target_pairs={{0,24},{8,0},{16,8},{24,16},{1,25},{9,1},{17,9},{25,17},{2,26},{10... | collective-permute-start | bytes 1572872 | tf_op jit(solution)/shard_map/partial_far1/ppermute | solution.py:187
  339.2 18.1 %collective-permute-start.52 = (bf16[2,2,32,2048]{3,2,1,0:T(8,128)(2,1)}, bf16[2,2,32,2048]{3,2,1,0:T(8,128)(2,1)}, u32[]{:S(2)}, u32[]{:S(2)}) collective-permute-start(bf16[2,2,32,2048]{3,2,1,0:T(8,128)(2,1)} %get-tuple-element.327), channel_id=1, source_target_pairs={{0,2},{2,0},{1,3},{3,1},{4,6},{6,4},{5,7},{7,5},{8,10},{10,8},{9,1... | collective-permute-start | bytes 1572872 | tf_op jit(solution)/shard_map/rows_back0/ppermute | solution.py:84
  342.0 39.1 %collective-permute-start.57 = (bf16[128,2048]{1,0:T(8,128)(2,1)}, bf16[128,2048]{1,0:T(8,128)(2,1)}, u32[]{:S(2)}, u32[]{:S(2)}) collective-permute-start(bf16[128,2048]{1,0:T(8,128)(2,1)} %fusion.12), channel_id=1, source_target_pairs={{0,16},{8,24},{16,0},{24,8},{1,17},{9,25},{17,1},{25,9},{2,18},{10... | collective-permute-start | bytes 1572872 | tf_op jit(solution)/shard_map/partial_far2/ppermute | solution.py:187
  350.6 30.5 %collective-permute-start.62 = (bf16[128,2048]{1,0:T(8,128)(2,1)}, bf16[128,2048]{1,0:T(8,128)(2,1)}, u32[]{:S(2)}, u32[]{:S(2)}) collective-permute-start(bf16[128,2048]{1,0:T(8,128)(2,1)} %fusion.13), channel_id=1, source_target_pairs={{0,8},{8,16},{16,24},{24,0},{1,9},{9,17},{17,25},{25,1},{2,10},{10... | collective-permute-start | bytes 1572872 | tf_op jit(solution)/shard_map/partial_far3/ppermute | solution.py:187
  352.0 28.5 %all-to-all-start.3 = ((f32[32,1,32]{2,1,0:T(1,128)}), f32[32,1,32]{2,1,0:T(1,128)S(1)}, u32[]{:S(2)}, u32[]{:S(2)}) async-start(f32[32,1,32]{2,1,0:T(1,128)} %bitcast.180), calls=%async_computation.3 | async-start | bytes 32768 | tf_op jit(solution)/shard_map/all_to_all | solution.py:93
  359.6 21.4 %collective-permute-start.53 = (bf16[2,32,2048]{2,1,0:T(8,128)(2,1)}, bf16[2,32,2048]{2,1,0:T(8,128)(2,1)}, u32[]{:S(2)}, u32[]{:S(2)}) collective-permute-start(bf16[2,32,2048]{2,1,0:T(8,128)(2,1)} %get-tuple-element.324), channel_id=1, source_target_pairs={{0,1},{1,0},{4,5},{5,4},{2,3},{3,2},{6,7},{7,6},{8,9},{9,8},{12,13... | collective-permute-start | bytes 786440 | tf_op jit(solution)/shard_map/rows_back0/ppermute | solution.py:102
  361.4 19.7 %collective-permute-start.54 = (bf16[2,32,2048]{2,1,0:T(8,128)(2,1)}, bf16[2,32,2048]{2,1,0:T(8,128)(2,1)}, u32[]{:S(2)}, u32[]{:S(2)}) collective-permute-start(bf16[2,32,2048]{2,1,0:T(8,128)(2,1)} %get-tuple-element.325), channel_id=1, source_target_pairs={{0,4},{1,5},{4,0},{5,1},{2,6},{3,7},{6,2},{7,3},{8,12},{9,13},{12,... | collective-permute-start | bytes 786440 | tf_op jit(solution)/shard_map/rows_back0/ppermute | solution.py:102
  362.9 18.2 %collective-permute-start.55 = (bf16[2,32,2048]{2,1,0:T(8,128)(2,1)}, bf16[2,32,2048]{2,1,0:T(8,128)(2,1)}, u32[]{:S(2)}, u32[]{:S(2)}) collective-permute-start(bf16[2,32,2048]{2,1,0:T(8,128)(2,1)} %get-tuple-element.326), channel_id=1, source_target_pairs={{0,5},{1,4},{4,1},{5,0},{2,7},{3,6},{6,3},{7,2},{8,13},{9,12},{12,... | collective-permute-start | bytes 786440 | tf_op jit(solution)/shard_map/rows_back0/ppermute | solution.py:102
  384.7 22.3 %collective-permute-start.65 = (bf16[128,2048]{1,0:T(8,128)(2,1)S(1)}, bf16[128,2048]{1,0:T(8,128)(2,1)S(1)}, u32[]{:S(2)}, u32[]{:S(2)}) collective-permute-start(bf16[128,2048]{1,0:T(8,128)(2,1)S(1)} %fusion.22), channel_id=1, source_target_pairs={{0,5},{1,4},{4,1},{5,0},{2,7},{3,6},{6,3},{7,2},{8,13},{9,12},{12,... | collective-permute-start | bytes 1572872 | tf_op jit(solution)/shard_map/ppermute | solution.py:114
  386.0 24.6 %collective-permute-start.64 = (bf16[128,2048]{1,0:T(8,128)(2,1)S(1)}, bf16[128,2048]{1,0:T(8,128)(2,1)S(1)}, u32[]{:S(2)}, u32[]{:S(2)}) collective-permute-start(bf16[128,2048]{1,0:T(8,128)(2,1)S(1)} %fusion.22), channel_id=1, source_target_pairs={{0,4},{1,5},{4,0},{5,1},{2,6},{3,7},{6,2},{7,3},{8,12},{9,13},{12,... | collective-permute-start | bytes 1572872 | tf_op jit(solution)/shard_map/ppermute | solution.py:114
  387.3 23.2 %collective-permute-start.63 = (bf16[128,2048]{1,0:T(8,128)(2,1)S(1)}, bf16[128,2048]{1,0:T(8,128)(2,1)S(1)}, u32[]{:S(2)}, u32[]{:S(2)}) collective-permute-start(bf16[128,2048]{1,0:T(8,128)(2,1)S(1)} %fusion.22), channel_id=1, source_target_pairs={{0,1},{1,0},{4,5},{5,4},{2,3},{3,2},{6,7},{7,6},{8,9},{9,8},{12,13... | collective-permute-start | bytes 1572872 | tf_op jit(solution)/shard_map/ppermute | solution.py:114
  422.4 32.5 %collective-permute-start.67 = (bf16[128,2048]{1,0:T(8,128)(2,1)}, bf16[128,2048]{1,0:T(8,128)(2,1)}, u32[]{:S(2)}, u32[]{:S(2)}) collective-permute-start(bf16[128,2048]{1,0:T(8,128)(2,1)} %get-tuple-element.285), channel_id=1, source_target_pairs={{0,1},{1,0},{4,5},{5,4},{2,3},{3,2},{6,7},{7,6},{8,9},{9,8},{12,13... | collective-permute-start | bytes 1572872 | tf_op jit(solution)/shard_map/ppermute | solution.py:102
  423.4 31.5 %collective-permute-start.69 = (bf16[128,2048]{1,0:T(8,128)(2,1)}, bf16[128,2048]{1,0:T(8,128)(2,1)}, u32[]{:S(2)}, u32[]{:S(2)}) collective-permute-start(bf16[128,2048]{1,0:T(8,128)(2,1)} %get-tuple-element.286), channel_id=1, source_target_pairs={{0,5},{1,4},{4,1},{5,0},{2,7},{3,6},{6,3},{7,2},{8,13},{9,12},{12,... | collective-permute-start | bytes 1572872 | tf_op jit(solution)/shard_map/ppermute | solution.py:102
  424.6 30.4 %collective-permute-start.68 = (bf16[128,2048]{1,0:T(8,128)(2,1)}, bf16[128,2048]{1,0:T(8,128)(2,1)}, u32[]{:S(2)}, u32[]{:S(2)}) collective-permute-start(bf16[128,2048]{1,0:T(8,128)(2,1)} %get-tuple-element.287), channel_id=1, source_target_pairs={{0,4},{1,5},{4,0},{5,1},{2,6},{3,7},{6,2},{7,3},{8,12},{9,13},{12,... | collective-permute-start | bytes 1572872 | tf_op jit(solution)/shard_map/ppermute | solution.py:102
  467.3 18.6 %collective-permute-start.70 = (bf16[8,128,1280]{2,1,0:T(8,128)(2,1)}, bf16[8,128,1280]{2,1,0:T(8,128)(2,1)}, u32[]{:S(2)}, u32[]{:S(2)}) collective-permute-start(bf16[8,128,1280]{2,1,0:T(8,128)(2,1)} %fusion.4), channel_id=1, source_target_pairs={{0,2},{2,0},{1,3},{3,1},{4,6},{6,4},{5,7},{7,5},{8,10},{10,8},{9,1... | collective-permute-start | bytes 7864328 | tf_op jit(solution)/shard_map/ppermute | solution.py:84
  470.2 79.3 %all-to-all-start.4 = ((bf16[8,4,32,2048]{3,2,1,0:T(8,128)(2,1)}), bf16[8,4,32,2048]{3,2,1,0:T(8,128)(2,1)}, u32[]{:S(2)}, u32[]{:S(2)}) async-start(bf16[8,4,32,2048]{3,2,1,0:T(8,128)(2,1)} %pad_maximum_fusion.3), calls=%async_computation.4 | async-start | bytes 8388608 | tf_op jit(solution)/shard_map/all_to_all | solution.py:93
  476.4 16.6 %collective-permute-start.72 = (bf16[128,2048]{1,0:T(8,128)(2,1)S(1)}, bf16[128,2048]{1,0:T(8,128)(2,1)S(1)}, u32[]{:S(2)}, u32[]{:S(2)}) collective-permute-start(bf16[128,2048]{1,0:T(8,128)(2,1)S(1)} %get-tuple-element.283), channel_id=1, source_target_pairs={{0,8},{8,16},{16,24},{24,0},{1,9},{9,17},{17,25},{25,1},{2,10},{10... | collective-permute-start | bytes 1572872 | tf_op jit(solution)/shard_map/ppermute | solution.py:187
  477.0 25.2 %collective-permute-start.71 = (bf16[128,2048]{1,0:T(8,128)(2,1)S(1)}, bf16[128,2048]{1,0:T(8,128)(2,1)S(1)}, u32[]{:S(2)}, u32[]{:S(2)}) collective-permute-start(bf16[128,2048]{1,0:T(8,128)(2,1)S(1)} %get-tuple-element.284), channel_id=1, source_target_pairs={{0,24},{8,0},{16,8},{24,16},{1,25},{9,1},{17,9},{25,17},{2,26},{10... | collective-permute-start | bytes 1572872 | tf_op jit(solution)/shard_map/ppermute | solution.py:187
  502.4 14.6 %collective-permute-start.86 = (bf16[128,2048]{1,0:T(8,128)(2,1)S(1)}, bf16[128,2048]{1,0:T(8,128)(2,1)S(1)}, u32[]{:S(2)}, u32[]{:S(2)}) collective-permute-start(bf16[128,2048]{1,0:T(8,128)(2,1)S(1)} %fusion.61), channel_id=1, source_target_pairs={{0,24},{8,0},{16,8},{24,16},{1,25},{9,1},{17,9},{25,17},{2,26},{10... | collective-permute-start | bytes 1572872 | tf_op jit(solution)/shard_map/ppermute | solution.py:187
  504.7 30.0 %collective-permute-start.73 = (bf16[128,2048]{1,0:T(8,128)(2,1)S(1)}, bf16[128,2048]{1,0:T(8,128)(2,1)S(1)}, u32[]{:S(2)}, u32[]{:S(2)}) collective-permute-start(bf16[128,2048]{1,0:T(8,128)(2,1)S(1)} %get-tuple-element.280), channel_id=1, source_target_pairs={{0,1},{1,0},{4,5},{5,4},{2,3},{3,2},{6,7},{7,6},{8,9},{9,8},{12,13... | collective-permute-start | bytes 1572872 | tf_op jit(solution)/shard_map/ppermute | solution.py:102
  506.4 40.0 %collective-permute-start.75 = (bf16[128,2048]{1,0:T(8,128)(2,1)S(1)}, bf16[128,2048]{1,0:T(8,128)(2,1)S(1)}, u32[]{:S(2)}, u32[]{:S(2)}) collective-permute-start(bf16[128,2048]{1,0:T(8,128)(2,1)S(1)} %get-tuple-element.281), channel_id=1, source_target_pairs={{0,5},{1,4},{4,1},{5,0},{2,7},{3,6},{6,3},{7,2},{8,13},{9,12},{12,... | collective-permute-start | bytes 1572872 | tf_op jit(solution)/shard_map/ppermute | solution.py:102
  507.9 38.5 %collective-permute-start.74 = (bf16[128,2048]{1,0:T(8,128)(2,1)S(1)}, bf16[128,2048]{1,0:T(8,128)(2,1)S(1)}, u32[]{:S(2)}, u32[]{:S(2)}) collective-permute-start(bf16[128,2048]{1,0:T(8,128)(2,1)S(1)} %get-tuple-element.282), channel_id=1, source_target_pairs={{0,4},{1,5},{4,0},{5,1},{2,6},{3,7},{6,2},{7,3},{8,12},{9,13},{12,... | collective-permute-start | bytes 1572872 | tf_op jit(solution)/shard_map/ppermute | solution.py:102
  509.2 45.8 %collective-permute-start.80 = (bf16[256,1280]{1,0:T(8,128)(2,1)}, bf16[256,1280]{1,0:T(8,128)(2,1)}, u32[]{:S(2)}, u32[]{:S(2)}) collective-permute-start(bf16[256,1280]{1,0:T(8,128)(2,1)} %get-tuple-element.278), channel_id=1, source_target_pairs={{0,8},{8,16},{16,24},{24,0},{1,9},{9,17},{17,25},{25,1},{2,10},{10... | collective-permute-start | bytes 1966088 | tf_op jit(solution)/shard_map/ppermute | solution.py:187
  517.0 29.7 %collective-permute-start.81 = (bf16[256,1280]{1,0:T(8,128)(2,1)S(1)}, bf16[256,1280]{1,0:T(8,128)(2,1)S(1)}, u32[]{:S(2)}, u32[]{:S(2)}) collective-permute-start(bf16[256,1280]{1,0:T(8,128)(2,1)S(1)} %get-tuple-element.279), channel_id=1, source_target_pairs={{0,24},{8,0},{16,8},{24,16},{1,25},{9,1},{17,9},{25,17},{2,26},{10... | collective-permute-start | bytes 1966088 | tf_op jit(solution)/shard_map/ppermute | solution.py:187
  546.9 17.8 %collective-permute-start.82 = (bf16[256,1280]{1,0:T(8,128)(2,1)S(1)}, bf16[256,1280]{1,0:T(8,128)(2,1)}, u32[]{:S(2)}, u32[]{:S(2)}) collective-permute-start(bf16[256,1280]{1,0:T(8,128)(2,1)S(1)} %fusion.17), channel_id=1, source_target_pairs={{0,24},{8,0},{16,8},{24,16},{1,25},{9,1},{17,9},{25,17},{2,26},{10... | collective-permute-start | bytes 1966088 | tf_op jit(solution)/shard_map/ppermute | solution.py:187
  552.6 23.3 %collective-permute-start.77 = (bf16[128,2048]{1,0:T(8,128)(2,1)S(1)}, bf16[128,2048]{1,0:T(8,128)(2,1)S(1)}, u32[]{:S(2)}, u32[]{:S(2)}) collective-permute-start(bf16[128,2048]{1,0:T(8,128)(2,1)S(1)} %convolution_convert_fusion.10), channel_id=1, source_target_pairs={{0,24},{8,0},{16,8},{24,16},{1,25},{9,1},{17,9},{25,17},{2,26},{10... | collective-permute-start | bytes 1572872 | tf_op jit(solution)/shard_map/ppermute | solution.py:187
  553.5 34.6 %collective-permute-start.76 = (bf16[128,2048]{1,0:T(8,128)(2,1)S(1)}, bf16[128,2048]{1,0:T(8,128)(2,1)S(1)}, u32[]{:S(2)}, u32[]{:S(2)}) collective-permute-start(bf16[128,2048]{1,0:T(8,128)(2,1)S(1)} %convolution_convert_fusion.12), channel_id=1, source_target_pairs={{0,8},{8,16},{16,24},{24,0},{1,9},{9,17},{17,25},{25,1},{2,10},{10... | collective-permute-start | bytes 1572872 | tf_op jit(solution)/shard_map/ppermute | solution.py:187
  576.3 21.4 %collective-permute-start.78 = (bf16[128,2048]{1,0:T(8,128)(2,1)S(1)}, bf16[128,2048]{1,0:T(8,128)(2,1)S(1)}, u32[]{:S(2)}, u32[]{:S(2)}) collective-permute-start(bf16[128,2048]{1,0:T(8,128)(2,1)S(1)} %add_convert_fusion.1), channel_id=1, source_target_pairs={{0,24},{8,0},{16,8},{24,16},{1,25},{9,1},{17,9},{25,17},{2,26},{10... | collective-permute-start | bytes 1572872 | tf_op jit(solution)/shard_map/ppermute | solution.py:187
  598.7 16.7 %collective-permute-start.79 = (bf16[128,2048]{1,0:T(8,128)(2,1)S(1)}, bf16[128,2048]{1,0:T(8,128)(2,1)S(1)}, u32[]{:S(2)}, u32[]{:S(2)}) collective-permute-start(bf16[128,2048]{1,0:T(8,128)(2,1)S(1)} %add_convert_fusion), channel_id=1, source_target_pairs={{0,1},{1,0},{2,3},{3,2},{4,5},{5,4},{6,7},{7,6},{8,9},{9,8},{10,11... | collective-permute-start | bytes 1572872 | tf_op jit(solution)/shard_map/ppermute | solution.py:84
  600.1 17.7 %all-to-all-start.5 = ((f32[32,24,128]{2,1,0:T(8,128)}), f32[32,24,128]{2,1,0:T(8,128)S(1)}, u32[]{:S(2)}, u32[]{:S(2)}) async-start(f32[32,24,128]{2,1,0:T(8,128)} %bitcast.308), calls=%async_computation.5 | async-start | bytes 786432 | tf_op jit(solution)/shard_map/all_to_all | solution.py:93
  (132 other events, 912.4 us)

commit v8 on v7

--- a/solution.py
+++ b/solution.py
@@ -21,6 +21,7 @@
 KVDIM = 512
 NEAR = 2
 CORES = 2
+SLAB = NEAR * CORES * 2
 LANES = 128
 
 EPS = 1e-06
@@ -125,10 +126,10 @@
     return quad_order(quad_parts(parts))
 
 
-def quad_sum(parts):
-    total = lax.dynamic_index_in_dim(parts, quad_index(), 0, keepdims=False).astype(F32)
-    for step in range(1, 4):
-        total = total + quad_send(parts, step).astype(F32)
+def sum_parts(parts):
+    total = parts[0].astype(F32)
+    for part in parts[1:]:
+        total = total + part.astype(F32)
     return total
 
 
@@ -215,7 +216,7 @@
 
 def expert_kernel(
     here_ref, in_ref, cot_ref, mask_ref, router_ref, gate_ref, up_ref, down_ref,
-    gate_grad_ref, up_grad_ref, active_ref, grad_ref, in_grad_ref, gated_ref, dot_ref,
+    gate_grad_ref, up_grad_ref, active_ref, grad_ref, in_grad_ref, gated_ref,
     out_total, in_total, gate_slot,
 ):
     block = pl.program_id(0)
@@ -252,12 +253,17 @@
     @pl.when(block == pl.num_programs(0) - 1)
     def _():
         out = out_total[...].astype(BF).astype(F32)
-        dot_ref[...] = jnp.sum(cot_ref[...].astype(F32) * out, axis=-1, keepdims=True)
         gated_ref[...] = (gate_slot[:, :1] * out).astype(BF)
-        in_grad_ref[...] = in_total[...].astype(BF)
-
-
-def expert_chunk(here, in_chunk, cot_chunk, mask, router, weight):
+        in_grad_ref[:, :D] = in_total[...].astype(BF)
+        found = jnp.sum(cot_ref[...].astype(F32) * out, axis=-1, keepdims=True)
+        high = found.astype(BF).astype(F32)
+        lane = lax.broadcasted_iota(jnp.int32, (in_grad_ref.shape[0], in_grad_ref.shape[1] - D), 1)
+        lane = lane - here_ref[1]
+        parts = jnp.where(lane == 0, high, jnp.where(lane == SLAB, found - high, 0.0))
+        in_grad_ref[:, D:] = parts.astype(BF)
+
+
+def expert_chunk(here, in_chunk, cot_chunk, mask, router, weight, back_width):
     rows = in_chunk.shape[0]
     tile = 256
     steps = FF // tile
@@ -280,8 +286,9 @@
                 pl.BlockSpec((D, tile), lambda j, h: (0, 2 * steps + j)),
             ],
             out_specs=[
-                piece, piece, piece, whole, whole, whole,
-                pl.BlockSpec((rows, 1), lambda j, h: (0, 0)),
+                piece, piece, piece, whole,
+                pl.BlockSpec((rows, back_width), lambda j, h: (0, 0)),
+                whole,
             ],
             scratch_shapes=[
                 pltpu.VMEM((rows, D), F32),
@@ -289,7 +296,7 @@
                 pltpu.VMEM((rows, LANES), F32),
             ],
         ),
-        out_shape=[low, low, low, wide, wide, wide, jax.ShapeDtypeStruct((rows, 1), F32)],
+        out_shape=[low, low, low, wide, jax.ShapeDtypeStruct((rows, back_width), BF), wide],
         compiler_params=pltpu.CompilerParams(vmem_limit_bytes=40 << 20),
         cost_estimate=pl.CostEstimate(flops=1 << 20, bytes_accessed=1 << 20, transcendentals=0),
         name="expert_chunk",
@@ -550,11 +557,6 @@
     source_ids = (
         lax.rem(far_index + far_count - chunk_steps, far_count)[:, None] * slab + slab_ids[None, :]
     ).reshape(device_count)
-    device_ids = jnp.arange(device_count, dtype=jnp.int32)
-    found_at = jnp.sum(
-        jnp.where(source_ids[None, :] == device_ids[:, None], device_ids[None, :], 0), axis=1
-    )
-
     def to_blocks(rows):
         return rows.reshape(4, 2, rows.shape[0] // slab, rows.shape[1])
 
@@ -629,7 +631,7 @@
 
     out_partial = mm(mixed_low, out_mine).astype(BF)
     out_partial, cot_back[0] = tie(out_partial, cot_back[0])
-    residual = x_rows + quad_sum(out_partial.reshape(4, TOK_DEV, D))
+    residual = x_rows + sum_parts(quad_parts(out_partial.reshape(4, TOK_DEV, D)))
 
     normed_two, ffn_back = jax.vjp(rms_norm, residual, gain_ffn)
     ffn_in = normed_two.astype(BF)
@@ -641,10 +643,9 @@
     expert_weight = w_expert[0]
     expert_here = far_index * slab + slab_index
     in_rows, gate_grads, up_grads, grad_rows, actives, in_grads = ([] for _ in range(6))
-    slot_dots, gated_outs = [None] * far_count, [None] * far_count
-    arrived = []
-    here = expert_here.reshape(1)
-    order = list(range(far_count))
+    gated_outs = [None] * far_count
+    here = jnp.stack([expert_here, far_index * 2 * SLAB + slab_index])
+    back_width = D + -(-far_count * 2 * SLAB // LANES) * LANES
     far_rows = [ffn_in]
     for step in range(1, far_count):
         with jax.named_scope('rows_far%d' % step):
@@ -656,72 +657,63 @@
     sent = gather(0, ffn_in)
 
     def send_back(step):
-        return slab_return(in_grads[step].reshape(NEAR, CORES, 2, capacity, D))
+        return slab_return(in_grads[step].reshape(NEAR, CORES, 2, capacity, back_width))
 
     def combine(step, found):
-        back = jnp.concatenate(found, axis=0).reshape(slab * capacity, D)
+        back = jnp.concatenate(found, axis=0).reshape(slab * capacity, back_width)
         return mm_tn(send_slots[step], back).astype(BF if step else F32)
 
     ffn_in, cot_back[1] = tie(ffn_in, cot_back[1])
     cot_chunks = far_parts(
         jnp.concatenate(cot_back, axis=2).reshape(far_count, slab * capacity, D), far_count
     )
-    pending = []
-    for turn, step in enumerate(order):
+    pending, parts = {}, [None] * far_count
+    for turn in range(far_count):
         with jax.named_scope("rows_out%d" % turn):
             got = slab_send(to_blocks(sent))
         if turn + 1 < far_count:
-            source = far_rows[order[turn + 1]]
+            source = far_rows[turn + 1]
             if turn > 0:
                 source, up_grads[turn - 1] = tie(source, up_grads[turn - 1])
-            sent = gather(order[turn + 1], source)
+            sent = gather(turn + 1, source)
         if turn > 0:
             gate_grads[turn - 1], *got = tie(gate_grads[turn - 1], *got)
         with jax.named_scope("rows_core%d" % turn):
             in_chunk = slab_take(got).reshape(slab * capacity, D)
-        if turn > 2:
-            in_chunk, *pending = tie(in_chunk, *pending)
-            partial = combine(order[turn - 2], pending)
-            in_chunk, partial = tie(in_chunk, partial)
-            with jax.named_scope("partial_far%d" % (turn - 2)):
-                arrived.append(far_shift(partial, -order[turn - 2], far_count))
-        gate_grad, up_grad, active, grad_chunk, in_grad, gated_out, slot_dot = expert_chunk(
-            here, in_chunk, cot_chunks[step], mask_back[step], router_full, expert_weight
+        gate_grad, up_grad, active, grad_chunk, in_grad, gated_out = expert_chunk(
+            here, in_chunk, cot_chunks[turn], mask_back[turn], router_full, expert_weight, back_width
         )
-        if turn > 2:
-            gate_grad, arrived[-1] = tie(gate_grad, arrived[-1])
         in_rows.append(in_chunk)
         gate_grads.append(gate_grad)
         up_grads.append(up_grad)
         actives.append(active)
         grad_rows.append(grad_chunk)
         in_grads.append(in_grad)
-        gated_outs[step] = gated_out.reshape(slab, capacity, D)
-        slot_dots[step] = slot_dot[:, 0]
-        if turn > 1:
-            with jax.named_scope("rows_back%d" % (turn - 1)):
-                pending = send_back(turn - 1)
-    partial = None
-    for turn in range(max(1, far_count - 2), far_count):
-        if turn == far_count - 1:
+        gated_outs[turn] = gated_out.reshape(slab, capacity, D)
+        if 0 < turn < far_count - 1:
             with jax.named_scope("rows_back%d" % turn):
-                pending = send_back(turn)
-        else:
-            up_grads[-1], *pending = tie(up_grads[-1], *pending)
-        partial = combine(order[turn], pending)
-        if turn == far_count - 2:
-            partial, in_grads[0] = tie(partial, in_grads[0])
-        with jax.named_scope("partial_far%d" % turn):
-            arrived.append(far_shift(partial, -order[turn], far_count))
-    slot_dots[0], partial = tie(slot_dots[0], partial)
+                pending[turn] = send_back(turn)
+    up_grads[-1], *pending[1] = tie(up_grads[-1], *pending[1])
+    for turn in range(1, far_count - 1):
+        parts[turn] = combine(turn, pending[turn])
+        if turn + 1 in pending:
+            parts[turn], *pending[turn + 1] = tie(parts[turn], *pending[turn + 1])
+    last = far_count - 1
+    with jax.named_scope("rows_back%d" % last):
+        parts[last] = combine(last, send_back(last))
+    parts[max(last - 1, 0)], in_grads[0] = tie(parts[max(last - 1, 0)], in_grads[0])
+    with jax.named_scope("partial_far"):
+        part_found = far_begin(parts, far_count)
     with jax.named_scope("rows_back0"):
-        from_experts = combine(0, send_back(0))
-    for part in arrived:
-        from_experts = from_experts + part.astype(F32)
-    dot_sent = jnp.take(jnp.stack(slot_dots).reshape(device_count, capacity), found_at, axis=0)
-    dot_back = exchange(dot_sent[:, None, :], ALL_AXES).reshape(experts_all, capacity)
-
-    gate_grad = jnp.sum(jnp.where(slot_hot, dot_back[:, :, None], 0.0), axis=1).T
+        parts[0] = combine(0, send_back(0))
+    with jax.named_scope("partial_far"):
+        total = far_end(parts, part_found, far_count)
+    from_experts = total[:, :D]
+
+    lanes = jnp.arange(back_width - D, dtype=jnp.int32)
+    lanes = lanes // (2 * SLAB) * SLAB + lanes % SLAB
+    spread = (lanes[:, None] == expert_ids[None, :]).astype(BF)
+    gate_grad = mm(total[:, D:].astype(BF), spread)
     mean_term = jnp.sum(gate_probs * gate_grad, axis=1, keepdims=True)
     logit_grad = (gate_probs * (gate_grad - mean_term)).astype(BF)
     router_grad = mm_tn(ffn_in, logit_grad)
@@ -781,7 +773,9 @@
     qkv_found = far_begin(qkv_parts, far_count)
     out_share = far_end(out_sent, out_found, far_count)
     qkv_grad = far_end(qkv_parts, qkv_found, far_count)
-    normed_grad = quad_sum(normed_partial.reshape(4, TOK_DEV, D))
+    normed_found = quad_parts(normed_partial.reshape(4, TOK_DEV, D))
+    qkv_grad, *normed_found = tie(qkv_grad, *normed_found)
+    normed_grad = sum_parts(normed_found)
     normed_grad, out_sum = tie(normed_grad, out_sum)
     final_rows = (residual + out_sum).astype(BF)
     final_pair = jnp.concatenate(

time: 628 us -> 609 us (0.970)
    ppermute x24, waiting for transfers between devices: 91.9 us -> 113 us  [far_shift(): lax.ppermute(value, FAR_AXIS, [(i, (i + step) % count) for i in range(cou...]
    all_to_all x6 -> x5, waiting for transfers between devices: 20.5 us -> 1.91 us  [exchange(): return lax.all_to_all(value, axes, split_axis=0, concat_axis=0, tiled=True)]
    all_to_all x6 -> x5, starting transfers between devices: 27.6 us -> 20.8 us  [exchange(): return lax.all_to_all(value, axes, split_axis=0, concat_axis=0, tiled=True)]
    dot_general x29 -> x30, matrix products: 44.7 us -> 39.2 us  [dot(): lax.dot_general(left, right, (dims, ((), ())), preferred_element_type=F32)]
    unnamed x224 -> x128, local copies, waits for them, and re-layouts: 19.3 us -> 17.3 us
  transfers between devices with their start and end apart: 93 -> 92, of which waited for: 40 -> 37; matrix products, arithmetic and copies ran while one was open for 18% -> 17% of each run, Pallas kernels for 16% -> 16%
where the time goes in v8:
time: 609 us; the launch traced here: 601 us
  waiting for transfers between devices  235 us (39%)
  starting transfers between devices  125 us (21%)
  Pallas kernels  99.2 us (16%)
  local copies, waits for them, and re-layouts  50.8 us (8%)
  other arithmetic  46.7 us (8%)
  matrix products  41.6 us (7%)
    ppermute x24, waiting for transfers between devices, far_shift(): lax.ppermute(value, FAR_AXIS, [(i, (i + step) % count) for i in range(cou...  113 us
    ppermute x30, waiting for transfers between devices, quad_send(): return lax.ppermute(block, HEAD_AXES, [(i, i ^ step) for i in range(4)])  94.9 us
    ppermute x24, starting transfers between devices, far_shift(): lax.ppermute(value, FAR_AXIS, [(i, (i + step) % count) for i in range(cou...  40.8 us
    pallas_call x4, Pallas kernels, expert_chunk(): pl.pallas_call(expert_kernel, grid_spec=pltpu.PrefetchScalarGridSpec(num_...  40 us
    dot_general x30, matrix products, dot(): lax.dot_general(left, right, (dims, ((), ())), preferred_element_type=F32)  39.2 us
    ppermute x30, starting transfers between devices, quad_send(): return lax.ppermute(block, HEAD_AXES, [(i, i ^ step) for i in range(4)])  35.4 us
    pallas_call x1, Pallas kernels, attend_back(): pl.pallas_call(attend_back_kernel, grid=(rows // ROW, heads), in_specs=sp...  24.1 us
    all_to_all x5, starting transfers between devices, exchange(): return lax.all_to_all(value, axes, split_axis=0, concat_axis=0, tiled=True)  20.8 us
  transfers between devices with their start and end apart: 92, of which 37 were waited for; matrix products, arithmetic and copies ran while one was open for 17% of the time, Pallas kernels for 16%

profile of v8, /device:TPU:0, one launch (start us, length us, event | category | flops | bytes accessed | tf_op | source)
XLA Modules:
  0.0 601.4 jit_solution(13450079032143661390)
XLA Ops:
  1.3 3.0 collective-permute-start
  17.7 2.5 collective-permute-start.3
  25.3 3.0 all-to-all-start
  30.0 2.7 collective-permute-start.6
  43.0 11.1 %collective-permute-done.7 = bf16[256,1280]{1,0:T(8,128)(2,1)} collective-permute-done((bf16[256,1280]{1,0:T(8,128)(2,1)}, bf16[256,1280]{1,0:T(8,128)(2,1)}, u32[]{:S(2)}, u32[]{:S(2)}) %collective-permute-start.7) | collective-permute-done | bytes 655392 | tf_op jit(solution)/shard_map/ppermute | solution.py:188
  57.3 23.4 %collective-permute-done.8 = bf16[256,1280]{1,0:T(8,128)(2,1)S(1)} collective-permute-done((bf16[256,1280]{1,0:T(8,128)(2,1)}, bf16[256,1280]{1,0:T(8,128)(2,1)S(1)}, u32[]{:S(2)}, u32[]{:S(2)}) %collective-permute-start.8) | collective-permute-done | bytes 655392 | tf_op jit(solution)/shard_map/ppermute | solution.py:188
  87.5 5.7 collective-permute-done.4
  98.9 4.4 fusion.170.query_ref.key_ref.value_ref
  103.3 4.2 all-to-all-start.1
  113.1 2.7 dynamic-slice_bitcast_fusion.18
  115.8 2.4 collective-permute-start.17
  121.9 16.4 %attend.1 = bf16[512,1024]{1,0:T(8,128)(2,1)} custom-call(f32[512,1280]{1,0:T(8,128)} %fusion.170.query_ref.key_ref.value_ref, f32[512,1280]{1,0:T(8,128)} %fusion.170.query_ref.key_ref.value_ref, f32[512,1280]{1,0:T(8,128)} %fusion.170.query_ref.key_ref.value_ref, f32[512,128]{1,0:T(8,128)} %get-tuple-element.439.cos_ref, ...), custom_call_target="tpu_custom_call" | custom-call | flops 1048576 | bytes 1048576 | tf_op jit(solution)/shard_map/attend/pallas_call | solution.py:438
  138.4 4.2 collective-permute-done.17
  142.6 12.8 %collective-permute-done.16 = bf16[128,2048]{1,0:T(8,128)(2,1)} collective-permute-done((bf16[128,2048]{1,0:T(8,128)(2,1)}, bf16[128,2048]{1,0:T(8,128)(2,1)}, u32[]{:S(2)}, u32[]{:S(2)}) %collective-permute-start.16) | collective-permute-done | bytes 524320 | tf_op jit(solution)/shard_map/ppermute | solution.py:103
  155.4 2.4 collective-permute-done.15
  162.4 3.0 collective-permute-start.24
  168.2 5.4 all-to-all-start.2
  173.8 2.5 select_bitcast_fusion.3
  177.6 2.4 convolution_convert_fusion.2
  185.5 23.6 %collective-permute-done.19 = bf16[128,2048]{1,0:T(8,128)(2,1)} collective-permute-done((bf16[128,2048]{1,0:T(8,128)(2,1)S(1)}, bf16[128,2048]{1,0:T(8,128)(2,1)}, u32[]{:S(2)}, u32[]{:S(2)}) %collective-permute-start.19) | collective-permute-done | bytes 524320 | tf_op jit(solution)/shard_map/ppermute | solution.py:103
  209.1 13.3 %collective-permute-done.21 = bf16[128,2048]{1,0:T(8,128)(2,1)} collective-permute-done((bf16[128,2048]{1,0:T(8,128)(2,1)S(1)}, bf16[128,2048]{1,0:T(8,128)(2,1)}, u32[]{:S(2)}, u32[]{:S(2)}) %collective-permute-start.21) | collective-permute-done | bytes 524320 | tf_op jit(solution)/shard_map/ppermute | solution.py:103
  222.4 2.4 multiply_reduce_fusion.3
  225.0 2.5 collective-permute-start.29
  234.2 7.0 %collective-permute-done.26 = bf16[2,32,2048]{2,1,0:T(8,128)(2,1)S(1)} collective-permute-done((bf16[2,32,2048]{2,1,0:T(8,128)(2,1)S(1)}, bf16[2,32,2048]{2,1,0:T(8,128)(2,1)S(1)}, u32[]{:S(2)}, u32[]{:S(2)}) %collective-permute-start.26) | collective-permute-done | bytes 262176 | tf_op jit(solution)/shard_map/rows_out0/ppermute | solution.py:196
  249.8 10.0 %expert_chunk.4 = (bf16[256,768]{1,0:T(8,128)(2,1)S(1)}, bf16[256,768]{1,0:T(8,128)(2,1)S(1)}, bf16[256,768]{1,0:T(8,128)(2,1)S(1)}, bf16[256,2048]{1,0:T(8,128)...) custom-call(s32[2]{0:T(128)S(1)} %pad_add_fusion.2.here_ref, bf16[256,2048]{1,0:T(8,128)(2,1)S(1)} %bitcast.609, ...), custom_call_target="tpu_custom_call" | custom-call | flops 1048576 | bytes 1048576 | tf_op jit(solution)/shard_map/expert_chunk/pallas_call | solution.py:274
  260.2 3.2 collective-permute-done.34
  268.1 10.0 %expert_chunk.5 = (bf16[256,768]{1,0:T(8,128)(2,1)S(1)}, bf16[256,768]{1,0:T(8,128)(2,1)S(1)}, bf16[256,768]{1,0:T(8,128)(2,1)S(1)}, bf16[256,2048]{1,0:T(8,128)...) custom-call(s32[2]{0:T(128)S(1)} %pad_add_fusion.2.here_ref, bf16[256,2048]{1,0:T(8,128)(2,1)S(1)} %bitcast.611, ...), custom_call_target="tpu_custom_call" | custom-call | flops 1048576 | bytes 1048576 | tf_op jit(solution)/shard_map/expert_chunk/pallas_call | solution.py:274
  279.1 2.2 collective-permute-done.39
  285.6 10.0 %expert_chunk.6 = (bf16[256,768]{1,0:T(8,128)(2,1)S(1)}, bf16[256,768]{1,0:T(8,128)(2,1)S(1)}, bf16[256,768]{1,0:T(8,128)(2,1)S(1)}, bf16[256,2048]{1,0:T(8,128)...) custom-call(s32[2]{0:T(128)S(1)} %pad_add_fusion.2.here_ref, bf16[256,2048]{1,0:T(8,128)(2,1)S(1)} %bitcast.613, ...), custom_call_target="tpu_custom_call" | custom-call | flops 1048576 | bytes 1048576 | tf_op jit(solution)/shard_map/expert_chunk/pallas_call | solution.py:274
  300.7 10.1 %expert_chunk.7 = (bf16[256,768]{1,0:T(8,128)(2,1)S(1)}, bf16[256,768]{1,0:T(8,128)(2,1)S(1)}, bf16[256,768]{1,0:T(8,128)(2,1)S(1)}, bf16[256,2048]{1,0:T(8,128)...) custom-call(s32[2]{0:T(128)S(1)} %pad_add_fusion.2.here_ref, bf16[256,2048]{1,0:T(8,128)(2,1)S(1)} %bitcast.615, ...), custom_call_target="tpu_custom_call" | custom-call | flops 1048576 | bytes 1048576 | tf_op jit(solution)/shard_map/expert_chunk/pallas_call | solution.py:274
  315.8 6.6 %collective-permute-done.51 = bf16[2,32,2176]{2,1,0:T(8,128)(2,1)S(1)} collective-permute-done((bf16[2,32,2176]{2,1,0:T(8,128)(2,1)S(1)}, bf16[2,32,2176]{2,1,0:T(8,128)(2,1)S(1)}, u32[]{:S(2)}, u32[]{:S(2)}) %collective-permute-start.51) | collective-permute-done | bytes 278560 | tf_op jit(solution)/shard_map/rows_back2/ppermute | solution.py:103
  322.4 4.1 collective-permute-done.49
  327.6 3.3 collective-permute-start.61
  334.8 5.9 collective-permute-done.57
  340.7 5.4 collective-permute-done.58
  346.7 3.9 collective-permute-start.62
  354.6 5.4 collective-permute-done.53
  360.0 4.1 collective-permute-done.54
  364.2 7.3 %collective-permute-done.62 = bf16[128,2176]{1,0:T(8,128)(2,1)S(1)} collective-permute-done((bf16[128,2176]{1,0:T(8,128)(2,1)S(1)}, bf16[128,2176]{1,0:T(8,128)(2,1)S(1)}, u32[]{:S(2)}, u32[]{:S(2)}) %collective-permute-start.62) | collective-permute-done | bytes 557088 | tf_op jit(solution)/shard_map/partial_far/ppermute | solution.py:188
  377.3 18.7 %expert_grads.1 = f32[2048,2304]{1,0:T(8,128)} custom-call(bf16[256,2048]{1,0:T(8,128)(2,1)S(1)} %bitcast.610, bf16[256,2048]{1,0:T(8,128)(2,1)} %bitcast.612, bf16[256,2048]{1,0:T(8,128)(2,1)} %bitcast.614, bf16[256,2048]{1,0:T(8,128)(2,1)} %bitcast.616, bf16[256,2048]{1,0:T(8,128)(2,1)} %copy-done.3, bf16[256,2048]{1,0:T(8,128)(2,1)} %copy-done.4, ...), custom_call_target="tpu_custom_call" | custom-call | flops 1048576 | bytes 1048576 | tf_op jit(solution)/shard_map/expert_grads/pallas_call | solution.py:327
  399.5 2.4 convolution_convert_fusion.1
  404.1 3.3 convolution_convert_fusion.16.grad_ref
  417.4 24.1 %attend_back.1 = (bf16[512,1024]{1,0:T(8,128)(2,1)}, bf16[512,128]{1,0:T(8,128)(2,1)}, bf16[512,128]{1,0:T(8,128)(2,1)}, f32[1,128]{1,0:T(1,128)}, f32[1,128]{1,0:T(1,128)}) custom-call(f32[512,1280]{1,0:T(8,128)} %fusion.170.query_ref.key_ref.value_ref, f32[512,1280]{1,0:T(8,128)} %fusion.170.query_ref.key_ref.value_ref, ...), custom_call_target="tpu_custom_call" | custom-call | flops 1048576 | bytes 1048576 | tf_op jit(solution)/shard_map/attend_back/pallas_call | solution.py:453
  449.0 3.2 convolution_convert_fusion
  456.5 4.7 all-to-all-start.3
  462.8 3.8 collective-permute-start.71
  466.6 5.6 convolution_convert_fusion.3
  472.2 3.0 fusion
  475.2 4.1 collective-permute-done.72
  479.3 9.3 %collective-permute-done.71 = bf16[128,2048]{1,0:T(8,128)(2,1)S(1)} collective-permute-done((bf16[128,2048]{1,0:T(8,128)(2,1)S(1)}, bf16[128,2048]{1,0:T(8,128)(2,1)S(1)}, u32[]{:S(2)}, u32[]{:S(2)}) %collective-permute-start.71) | collective-permute-done | bytes 524320 | tf_op jit(solution)/shard_map/ppermute | solution.py:188
  494.5 2.5 collective-permute-start.78
  497.9 5.6 collective-permute-done.86
  506.5 10.6 %collective-permute-done.74 = bf16[256,1280]{1,0:T(8,128)(2,1)S(1)} collective-permute-done((bf16[256,1280]{1,0:T(8,128)(2,1)S(1)}, bf16[256,1280]{1,0:T(8,128)(2,1)S(1)}, u32[]{:S(2)}, u32[]{:S(2)}) %collective-permute-start.74) | collective-permute-done | bytes 655392 | tf_op jit(solution)/shard_map/ppermute | solution.py:188
  518.1 4.3 collective-permute-start.75
  522.4 2.7 fusion.161
  526.1 7.2 %collective-permute-done.73 = bf16[256,1280]{1,0:T(8,128)(2,1)} collective-permute-done((bf16[256,1280]{1,0:T(8,128)(2,1)}, bf16[256,1280]{1,0:T(8,128)(2,1)}, u32[]{:S(2)}, u32[]{:S(2)}) %collective-permute-start.73) | collective-permute-done | bytes 655392 | tf_op jit(solution)/shard_map/ppermute | solution.py:188
  535.5 10.8 %collective-permute-done.75 = bf16[256,1280]{1,0:T(8,128)(2,1)} collective-permute-done((bf16[256,1280]{1,0:T(8,128)(2,1)}, bf16[256,1280]{1,0:T(8,128)(2,1)}, u32[]{:S(2)}, u32[]{:S(2)}) %collective-permute-start.75) | collective-permute-done | bytes 655392 | tf_op jit(solution)/shard_map/ppermute | solution.py:188
  555.8 2.9 collective-permute-done.85
  560.9 3.3 collective-permute-start.81
  565.3 4.6 collective-permute-done.79
  569.9 10.1 %collective-permute-done.81 = bf16[128,2048]{1,0:T(8,128)(2,1)S(1)} collective-permute-done((bf16[128,2048]{1,0:T(8,128)(2,1)S(1)}, bf16[128,2048]{1,0:T(8,128)(2,1)S(1)}, u32[]{:S(2)}, u32[]{:S(2)}) %collective-permute-start.81) | collective-permute-done | bytes 524320 | tf_op jit(solution)/shard_map/ppermute | solution.py:188
  583.0 3.6 all-to-all-start.4
  586.6 2.5 fusion.11
  589.1 9.3 %collective-permute-done.82 = bf16[128,2048]{1,0:T(8,128)(2,1)S(1)} collective-permute-done((bf16[128,2048]{1,0:T(8,128)(2,1)S(1)}, bf16[128,2048]{1,0:T(8,128)(2,1)S(1)}, u32[]{:S(2)}, u32[]{:S(2)}) %collective-permute-start.82) | collective-permute-done | bytes 524320 | tf_op jit(solution)/shard_map/ppermute | solution.py:85
  (471 shorter events, 182.3 us)
Async XLA Ops:
  1.3 16.3 %collective-permute-start = (s32[1,384]{1,0:T(1,128)S(1)}, s32[1,384]{1,0:T(1,128)S(1)}, u32[]{:S(2)}, u32[]{:S(2)}) collective-permute-start(s32[1,384]{1,0:T(1,128)S(1)} %pad_add_fusion), channel_id=1, source_target_pairs={{0,4},{4,0},{1,5},{5,1},{2,6},{6,2},{3,7},{7,3},{8,12},{12,8},{9,1... | collective-permute-start | bytes 4616 | tf_op jit(solution)/shard_map/ppermute | solution.py:85
  4.3 35.6 %collective-permute-start.11 = (bf16[128,2048]{1,0:T(8,128)(2,1)}, bf16[128,2048]{1,0:T(8,128)(2,1)}, u32[]{:S(2)}, u32[]{:S(2)}) collective-permute-start(bf16[128,2048]{1,0:T(8,128)(2,1)} %param.12), channel_id=1, source_target_pairs={{0,1},{1,0},{2,3},{3,2},{4,5},{5,4},{6,7},{7,6},{8,9},{9,8},{10,11... | collective-permute-start | bytes 1572872 | tf_op jit(solution)/shard_map/ppermute | solution.py:85
  5.8 77.6 %collective-permute-start.12 = (bf16[128,2048]{1,0:T(8,128)(2,1)}, bf16[128,2048]{1,0:T(8,128)(2,1)}, u32[]{:S(2)}, u32[]{:S(2)}) collective-permute-start(bf16[128,2048]{1,0:T(8,128)(2,1)} %param.14), channel_id=1, source_target_pairs={{0,8},{8,16},{16,24},{24,0},{1,9},{9,17},{17,25},{25,1},{2,10},{10... | collective-permute-start | bytes 1572872 | tf_op jit(solution)/shard_map/ppermute | solution.py:188
  11.5 18.5 %collective-permute-start.1 = (bf16[64,1280]{1,0:T(8,128)(2,1)S(1)}, bf16[64,1280]{1,0:T(8,128)(2,1)S(1)}, u32[]{:S(2)}, u32[]{:S(2)}) collective-permute-start(bf16[64,1280]{1,0:T(8,128)(2,1)S(1)} %bitcast.714), channel_id=1, source_target_pairs={{0,1},{1,0},{4,5},{5,4},{2,3},{3,2},{6,7},{7,6},{8,9},{9,8},{12,13... | collective-permute-start | bytes 491528 | tf_op jit(solution)/shard_map/ppermute | solution.py:103
  12.1 17.8 %collective-permute-start.2 = (bf16[64,1280]{1,0:T(8,128)(2,1)S(1)}, bf16[64,1280]{1,0:T(8,128)(2,1)S(1)}, u32[]{:S(2)}, u32[]{:S(2)}) collective-permute-start(bf16[64,1280]{1,0:T(8,128)(2,1)S(1)} %bitcast.715), channel_id=1, source_target_pairs={{0,4},{1,5},{4,0},{5,1},{2,6},{3,7},{6,2},{7,3},{8,12},{9,13},{12,... | collective-permute-start | bytes 491528 | tf_op jit(solution)/shard_map/ppermute | solution.py:103
  25.3 13.7 %all-to-all-start = ((bf16[32,32,128]{2,1,0:T(8,128)(2,1)}), bf16[32,32,128]{2,1,0:T(8,128)(2,1)S(1)}, u32[]{:S(2)}, u32[]{:S(2)}) async-start(bf16[32,32,128]{2,1,0:T(8,128)(2,1)} %bitcast.290), calls=%async_computation | async-start | bytes 524288 | tf_op jit(solution)/shard_map/all_to_all | solution.py:94
  30.0 56.9 %collective-permute-start.6 = (bf16[128,2048]{1,0:T(8,128)(2,1)S(1)}, bf16[128,2048]{1,0:T(8,128)(2,1)}, u32[]{:S(2)}, u32[]{:S(2)}) collective-permute-start(bf16[128,2048]{1,0:T(8,128)(2,1)S(1)} %copy-done.12), channel_id=1, source_target_pairs={{0,5},{1,4},{4,1},{5,0},{2,7},{3,6},{6,3},{7,2},{8,13},{9,12},{12,... | collective-permute-start | bytes 1572872 | tf_op jit(solution)/shard_map/ppermute | solution.py:115
  32.7 54.8 %collective-permute-start.5 = (bf16[128,2048]{1,0:T(8,128)(2,1)S(1)}, bf16[128,2048]{1,0:T(8,128)(2,1)}, u32[]{:S(2)}, u32[]{:S(2)}) collective-permute-start(bf16[128,2048]{1,0:T(8,128)(2,1)S(1)} %copy-done.12), channel_id=1, source_target_pairs={{0,4},{1,5},{4,0},{5,1},{2,6},{3,7},{6,2},{7,3},{8,12},{9,13},{12,... | collective-permute-start | bytes 1572872 | tf_op jit(solution)/shard_map/ppermute | solution.py:115
  34.3 19.8 %collective-permute-start.7 = (bf16[256,1280]{1,0:T(8,128)(2,1)}, bf16[256,1280]{1,0:T(8,128)(2,1)}, u32[]{:S(2)}, u32[]{:S(2)}) collective-permute-start(bf16[256,1280]{1,0:T(8,128)(2,1)} %bitcast.18), channel_id=1, source_target_pairs={{0,8},{8,16},{16,24},{24,0},{1,9},{9,17},{17,25},{25,1},{2,10},{10... | collective-permute-start | bytes 1966088 | tf_op jit(solution)/shard_map/ppermute | solution.py:188
  39.9 41.2 %collective-permute-start.9 = (bf16[256,1280]{1,0:T(8,128)(2,1)}, bf16[256,1280]{1,0:T(8,128)(2,1)S(1)}, u32[]{:S(2)}, u32[]{:S(2)}) collective-permute-start(bf16[256,1280]{1,0:T(8,128)(2,1)} %bitcast.18), channel_id=1, source_target_pairs={{0,24},{8,0},{16,8},{24,16},{1,25},{9,1},{17,9},{25,17},{2,26},{10... | collective-permute-start | bytes 1966088 | tf_op jit(solution)/shard_map/ppermute | solution.py:188
  54.1 26.6 %collective-permute-start.8 = (bf16[256,1280]{1,0:T(8,128)(2,1)}, bf16[256,1280]{1,0:T(8,128)(2,1)S(1)}, u32[]{:S(2)}, u32[]{:S(2)}) collective-permute-start(bf16[256,1280]{1,0:T(8,128)(2,1)} %collective-permute-done.7), channel_id=1, source_target_pairs={{0,8},{8,16},{16,24},{24,0},{1,9},{9,17},{17,25},{25,1},{2,10},{10... | collective-permute-start | bytes 1966088 | tf_op jit(solution)/shard_map/ppermute | solution.py:188
  81.3 16.5 %collective-permute-start.10 = (bf16[8,128,1280]{2,1,0:T(8,128)(2,1)S(1)}, bf16[8,128,1280]{2,1,0:T(8,128)(2,1)S(1)}, u32[]{:S(2)}, u32[]{:S(2)}) collective-permute-start(bf16[8,128,1280]{2,1,0:T(8,128)(2,1)S(1)} %bitcast.648), channel_id=1, source_target_pairs={{0,2},{2,0},{1,3},{3,1},{4,6},{6,4},{5,7},{7,5},{8,10},{10,8},{9,1... | collective-permute-start | bytes 7864328 | tf_op jit(solution)/shard_map/ppermute | solution.py:85
  83.4 27.8 %collective-permute-start.14 = (bf16[128,2048]{1,0:T(8,128)(2,1)}, bf16[128,2048]{1,0:T(8,128)(2,1)}, u32[]{:S(2)}, u32[]{:S(2)}) collective-permute-start(bf16[128,2048]{1,0:T(8,128)(2,1)} %param.14), channel_id=1, source_target_pairs={{0,24},{8,0},{16,8},{24,16},{1,25},{9,1},{17,9},{25,17},{2,26},{10... | collective-permute-start | bytes 1572872 | tf_op jit(solution)/shard_map/ppermute | solution.py:188
  86.9 22.5 %collective-permute-start.13 = (bf16[128,2048]{1,0:T(8,128)(2,1)}, bf16[128,2048]{1,0:T(8,128)(2,1)}, u32[]{:S(2)}, u32[]{:S(2)}) collective-permute-start(bf16[128,2048]{1,0:T(8,128)(2,1)} %collective-permute-done.12), channel_id=1, source_target_pairs={{0,8},{8,16},{16,24},{24,0},{1,9},{9,17},{17,25},{25,1},{2,10},{10... | collective-permute-start | bytes 1572872 | tf_op jit(solution)/shard_map/ppermute | solution.py:188
  103.3 63.6 %all-to-all-start.1 = ((bf16[32,32,1024]{2,1,0:T(8,128)(2,1)}), bf16[32,32,1024]{2,1,0:T(8,128)(2,1)S(1)}, u32[]{:S(2)}, u32[]{:S(2)}) async-start(bf16[32,32,1024]{2,1,0:T(8,128)(2,1)} %bitcast.27), calls=%async_computation.1 | async-start | bytes 4194304 | tf_op jit(solution)/shard_map/all_to_all | solution.py:94
  115.8 26.8 %collective-permute-start.17 = (bf16[128,2048]{1,0:T(8,128)(2,1)}, bf16[128,2048]{1,0:T(8,128)(2,1)}, u32[]{:S(2)}, u32[]{:S(2)}) collective-permute-start(bf16[128,2048]{1,0:T(8,128)(2,1)} %get-tuple-element.292), channel_id=1, source_target_pairs={{0,5},{1,4},{4,1},{5,0},{2,7},{3,6},{6,3},{7,2},{8,13},{9,12},{12,... | collective-permute-start | bytes 1572872 | tf_op jit(solution)/shard_map/ppermute | solution.py:103
  118.2 37.2 %collective-permute-start.16 = (bf16[128,2048]{1,0:T(8,128)(2,1)}, bf16[128,2048]{1,0:T(8,128)(2,1)}, u32[]{:S(2)}, u32[]{:S(2)}) collective-permute-start(bf16[128,2048]{1,0:T(8,128)(2,1)} %get-tuple-element.293), channel_id=1, source_target_pairs={{0,4},{1,5},{4,0},{5,1},{2,6},{3,7},{6,2},{7,3},{8,12},{9,13},{12,... | collective-permute-start | bytes 1572872 | tf_op jit(solution)/shard_map/ppermute | solution.py:103
  118.8 39.0 %collective-permute-start.15 = (bf16[128,2048]{1,0:T(8,128)(2,1)}, bf16[128,2048]{1,0:T(8,128)(2,1)}, u32[]{:S(2)}, u32[]{:S(2)}) collective-permute-start(bf16[128,2048]{1,0:T(8,128)(2,1)} %get-tuple-element.294), channel_id=1, source_target_pairs={{0,1},{1,0},{4,5},{5,4},{2,3},{3,2},{6,7},{7,6},{8,9},{9,8},{12,13... | collective-permute-start | bytes 1572872 | tf_op jit(solution)/shard_map/ppermute | solution.py:103
  168.2 59.2 %all-to-all-start.2 = ((bf16[32,32,1024]{2,1,0:T(8,128)(2,1)}), bf16[32,32,1024]{2,1,0:T(8,128)(2,1)}, u32[]{:S(2)}, u32[]{:S(2)}) async-start(bf16[32,32,1024]{2,1,0:T(8,128)(2,1)} %bitcast.28), calls=%async_computation.2 | async-start | bytes 4194304 | tf_op jit(solution)/shard_map/all_to_all | solution.py:94
  180.1 29.0 %collective-permute-start.19 = (bf16[128,2048]{1,0:T(8,128)(2,1)S(1)}, bf16[128,2048]{1,0:T(8,128)(2,1)}, u32[]{:S(2)}, u32[]{:S(2)}) collective-permute-start(bf16[128,2048]{1,0:T(8,128)(2,1)S(1)} %get-tuple-element.285), channel_id=1, source_target_pairs={{0,1},{1,0},{4,5},{5,4},{2,3},{3,2},{6,7},{7,6},{8,9},{9,8},{12,13... | collective-permute-start | bytes 1572872 | tf_op jit(solution)/shard_map/ppermute | solution.py:103
  182.1 40.3 %collective-permute-start.21 = (bf16[128,2048]{1,0:T(8,128)(2,1)S(1)}, bf16[128,2048]{1,0:T(8,128)(2,1)}, u32[]{:S(2)}, u32[]{:S(2)}) collective-permute-start(bf16[128,2048]{1,0:T(8,128)(2,1)S(1)} %get-tuple-element.286), channel_id=1, source_target_pairs={{0,5},{1,4},{4,1},{5,0},{2,7},{3,6},{6,3},{7,2},{8,13},{9,12},{12,... | collective-permute-start | bytes 1572872 | tf_op jit(solution)/shard_map/ppermute | solution.py:103
  183.6 38.9 %collective-permute-start.20 = (bf16[128,2048]{1,0:T(8,128)(2,1)S(1)}, bf16[128,2048]{1,0:T(8,128)(2,1)}, u32[]{:S(2)}, u32[]{:S(2)}) collective-permute-start(bf16[128,2048]{1,0:T(8,128)(2,1)S(1)} %get-tuple-element.287), channel_id=1, source_target_pairs={{0,4},{1,5},{4,0},{5,1},{2,6},{3,7},{6,2},{7,3},{8,12},{9,13},{12,... | collective-permute-start | bytes 1572872 | tf_op jit(solution)/shard_map/ppermute | solution.py:103
  225.0 17.7 %collective-permute-start.29 = (bf16[128,2048]{1,0:T(8,128)(2,1)S(1)}, bf16[128,2048]{1,0:T(8,128)(2,1)}, u32[]{:S(2)}, u32[]{:S(2)}) collective-permute-start(bf16[128,2048]{1,0:T(8,128)(2,1)S(1)} %multiply_convert_fusion.1), channel_id=1, source_target_pairs={{0,8},{8,16},{16,24},{24,0},{1,9},{9,17},{17,25},{25,1},{2,10},{10... | collective-permute-start | bytes 1572872 | tf_op jit(solution)/shard_map/rows_far1/ppermute | solution.py:188
  244.3 15.4 %collective-permute-start.31 = (bf16[2,32,2048]{2,1,0:T(8,128)(2,1)S(1)}, bf16[2,32,2048]{2,1,0:T(8,128)(2,1)S(1)}, u32[]{:S(2)}, u32[]{:S(2)}) collective-permute-start(bf16[2,32,2048]{2,1,0:T(8,128)(2,1)S(1)} %bitcast.710), channel_id=1, source_target_pairs={{0,4},{1,5},{4,0},{5,1},{2,6},{3,7},{6,2},{7,3},{8,12},{9,13},{12,... | collective-permute-start | bytes 786440 | tf_op jit(solution)/shard_map/rows_out1/ppermute | solution.py:196
  245.0 14.7 %collective-permute-start.32 = (bf16[2,32,2048]{2,1,0:T(8,128)(2,1)S(1)}, bf16[2,32,2048]{2,1,0:T(8,128)(2,1)S(1)}, u32[]{:S(2)}, u32[]{:S(2)}) collective-permute-start(bf16[2,32,2048]{2,1,0:T(8,128)(2,1)S(1)} %bitcast.707), channel_id=1, source_target_pairs={{0,5},{1,4},{4,1},{5,0},{2,7},{3,6},{6,3},{7,2},{8,13},{9,12},{12,... | collective-permute-start | bytes 786440 | tf_op jit(solution)/shard_map/rows_out1/ppermute | solution.py:196
  247.8 15.5 %collective-permute-start.34 = (bf16[128,2048]{1,0:T(8,128)(2,1)}, bf16[128,2048]{1,0:T(8,128)(2,1)S(1)}, u32[]{:S(2)}, u32[]{:S(2)}) collective-permute-start(bf16[128,2048]{1,0:T(8,128)(2,1)} %collective-permute-done.29), channel_id=1, source_target_pairs={{0,8},{8,16},{16,24},{24,0},{1,9},{9,17},{17,25},{25,1},{2,10},{10... | collective-permute-start | bytes 1572872 | tf_op jit(solution)/shard_map/rows_far2/ppermute | solution.py:188
  263.9 14.2 %collective-permute-start.36 = (bf16[2,32,2048]{2,1,0:T(8,128)(2,1)S(1)}, bf16[2,32,2048]{2,1,0:T(8,128)(2,1)S(1)}, u32[]{:S(2)}, u32[]{:S(2)}) collective-permute-start(bf16[2,32,2048]{2,1,0:T(8,128)(2,1)S(1)} %bitcast.711), channel_id=1, source_target_pairs={{0,4},{1,5},{4,0},{5,1},{2,6},{3,7},{6,2},{7,3},{8,12},{9,13},{12,... | collective-permute-start | bytes 786440 | tf_op jit(solution)/shard_map/rows_out2/ppermute | solution.py:196
  264.6 13.5 %collective-permute-start.37 = (bf16[2,32,2048]{2,1,0:T(8,128)(2,1)S(1)}, bf16[2,32,2048]{2,1,0:T(8,128)(2,1)S(1)}, u32[]{:S(2)}, u32[]{:S(2)}) collective-permute-start(bf16[2,32,2048]{2,1,0:T(8,128)(2,1)S(1)} %bitcast.708), channel_id=1, source_target_pairs={{0,5},{1,4},{4,1},{5,0},{2,7},{3,6},{6,3},{7,2},{8,13},{9,12},{12,... | collective-permute-start | bytes 786440 | tf_op jit(solution)/shard_map/rows_out2/ppermute | solution.py:196
  267.4 13.9 %collective-permute-start.39 = (bf16[128,2048]{1,0:T(8,128)(2,1)S(1)}, bf16[128,2048]{1,0:T(8,128)(2,1)S(1)}, u32[]{:S(2)}, u32[]{:S(2)}) collective-permute-start(bf16[128,2048]{1,0:T(8,128)(2,1)S(1)} %collective-permute-done.34), channel_id=1, source_target_pairs={{0,8},{8,16},{16,24},{24,0},{1,9},{9,17},{17,25},{25,1},{2,10},{10... | collective-permute-start | bytes 1572872 | tf_op jit(solution)/shard_map/rows_far3/ppermute | solution.py:188
  279.0 17.7 %collective-permute-start.44 = (bf16[2,2,32,2176]{3,2,1,0:T(8,128)(2,1)S(1)}, bf16[2,2,32,2176]{3,2,1,0:T(8,128)(2,1)S(1)}, u32[]{:S(2)}, u32[]{:S(2)}) collective-permute-start(bf16[2,2,32,2176]{3,2,1,0:T(8,128)(2,1)S(1)} %get-tuple-element.336), channel_id=1, source_target_pairs={{0,2},{2,0},{1,3},{3,1},{4,6},{6,4},{5,7},{7,5},{8,10},{10,8},{9,1... | collective-permute-start | bytes 1671176 | tf_op jit(solution)/shard_map/rows_back1/ppermute | solution.py:85
  281.9 13.8 %collective-permute-start.41 = (bf16[2,32,2048]{2,1,0:T(8,128)(2,1)S(1)}, bf16[2,32,2048]{2,1,0:T(8,128)(2,1)S(1)}, u32[]{:S(2)}, u32[]{:S(2)}) collective-permute-start(bf16[2,32,2048]{2,1,0:T(8,128)(2,1)S(1)} %bitcast.713), channel_id=1, source_target_pairs={{0,4},{1,5},{4,0},{5,1},{2,6},{3,7},{6,2},{7,3},{8,12},{9,13},{12,... | collective-permute-start | bytes 786440 | tf_op jit(solution)/shard_map/rows_out3/ppermute | solution.py:196
  296.7 14.4 %collective-permute-start.48 = (bf16[2,2,32,2176]{3,2,1,0:T(8,128)(2,1)S(1)}, bf16[2,2,32,2176]{3,2,1,0:T(8,128)(2,1)S(1)}, u32[]{:S(2)}, u32[]{:S(2)}) collective-permute-start(bf16[2,2,32,2176]{3,2,1,0:T(8,128)(2,1)S(1)} %get-tuple-element.330), channel_id=1, source_target_pairs={{0,2},{2,0},{1,3},{3,1},{4,6},{6,4},{5,7},{7,5},{8,10},{10,8},{9,1... | collective-permute-start | bytes 1671176 | tf_op jit(solution)/shard_map/rows_back2/ppermute | solution.py:85
  296.9 15.9 %collective-permute-start.47 = (bf16[2,32,2176]{2,1,0:T(8,128)(2,1)S(1)}, bf16[2,32,2176]{2,1,0:T(8,128)(2,1)S(1)}, u32[]{:S(2)}, u32[]{:S(2)}) collective-permute-start(bf16[2,32,2176]{2,1,0:T(8,128)(2,1)S(1)} %get-tuple-element.332), channel_id=1, source_target_pairs={{0,5},{1,4},{4,1},{5,0},{2,7},{3,6},{6,3},{7,2},{8,13},{9,12},{12,... | collective-permute-start | bytes 835592 | tf_op jit(solution)/shard_map/rows_back1/ppermute | solution.py:103
  297.9 16.1 %collective-permute-start.45 = (bf16[2,32,2176]{2,1,0:T(8,128)(2,1)S(1)}, bf16[2,32,2176]{2,1,0:T(8,128)(2,1)S(1)}, u32[]{:S(2)}, u32[]{:S(2)}) collective-permute-start(bf16[2,32,2176]{2,1,0:T(8,128)(2,1)S(1)} %get-tuple-element.334), channel_id=1, source_target_pairs={{0,1},{1,0},{4,5},{5,4},{2,3},{3,2},{6,7},{7,6},{8,9},{9,8},{12,13... | collective-permute-start | bytes 835592 | tf_op jit(solution)/shard_map/rows_back1/ppermute | solution.py:103
  299.1 16.3 %collective-permute-start.46 = (bf16[2,32,2176]{2,1,0:T(8,128)(2,1)S(1)}, bf16[2,32,2176]{2,1,0:T(8,128)(2,1)S(1)}, u32[]{:S(2)}, u32[]{:S(2)}) collective-permute-start(bf16[2,32,2176]{2,1,0:T(8,128)(2,1)S(1)} %get-tuple-element.335), channel_id=1, source_target_pairs={{0,4},{1,5},{4,0},{5,1},{2,6},{3,7},{6,2},{7,3},{8,12},{9,13},{12,... | collective-permute-start | bytes 835592 | tf_op jit(solution)/shard_map/rows_back1/ppermute | solution.py:103
  311.0 19.9 %collective-permute-start.56 = (bf16[2,2,32,2176]{3,2,1,0:T(8,128)(2,1)S(1)}, bf16[2,2,32,2176]{3,2,1,0:T(8,128)(2,1)S(1)}, u32[]{:S(2)}, u32[]{:S(2)}) collective-permute-start(bf16[2,2,32,2176]{3,2,1,0:T(8,128)(2,1)S(1)} %get-tuple-element.318), channel_id=1, source_target_pairs={{0,2},{2,0},{1,3},{3,1},{4,6},{6,4},{5,7},{7,5},{8,10},{10,8},{9,1... | collective-permute-start | bytes 1671176 | tf_op jit(solution)/shard_map/rows_back3/ppermute | solution.py:85
  312.8 13.6 %collective-permute-start.49 = (bf16[2,32,2176]{2,1,0:T(8,128)(2,1)S(1)}, bf16[2,32,2176]{2,1,0:T(8,128)(2,1)S(1)}, u32[]{:S(2)}, u32[]{:S(2)}) collective-permute-start(bf16[2,32,2176]{2,1,0:T(8,128)(2,1)S(1)} %get-tuple-element.328), channel_id=1, source_target_pairs={{0,1},{1,0},{4,5},{5,4},{2,3},{3,2},{6,7},{7,6},{8,9},{9,8},{12,13... | collective-permute-start | bytes 835592 | tf_op jit(solution)/shard_map/rows_back2/ppermute | solution.py:103
  327.6 19.0 %collective-permute-start.61 = (bf16[128,2176]{1,0:T(8,128)(2,1)S(1)}, bf16[128,2176]{1,0:T(8,128)(2,1)S(1)}, u32[]{:S(2)}, u32[]{:S(2)}) collective-permute-start(bf16[128,2176]{1,0:T(8,128)(2,1)S(1)} %fusion.7), channel_id=1, source_target_pairs={{0,24},{8,0},{16,8},{24,16},{1,25},{9,1},{17,9},{25,17},{2,26},{10... | collective-permute-start | bytes 1671176 | tf_op jit(solution)/shard_map/partial_far/ppermute | solution.py:188
  332.1 14.0 %collective-permute-start.58 = (bf16[2,32,2176]{2,1,0:T(8,128)(2,1)S(1)}, bf16[2,32,2176]{2,1,0:T(8,128)(2,1)S(1)}, u32[]{:S(2)}, u32[]{:S(2)}) collective-permute-start(bf16[2,32,2176]{2,1,0:T(8,128)(2,1)S(1)} %get-tuple-element.316), channel_id=1, source_target_pairs={{0,4},{1,5},{4,0},{5,1},{2,6},{3,7},{6,2},{7,3},{8,12},{9,13},{12,... | collective-permute-start | bytes 835592 | tf_op jit(solution)/shard_map/rows_back3/ppermute | solution.py:103
  334.7 15.9 %collective-permute-start.52 = (bf16[2,2,32,2176]{3,2,1,0:T(8,128)(2,1)S(1)}, bf16[2,2,32,2176]{3,2,1,0:T(8,128)(2,1)S(1)}, u32[]{:S(2)}, u32[]{:S(2)}) collective-permute-start(bf16[2,2,32,2176]{3,2,1,0:T(8,128)(2,1)S(1)} %get-tuple-element.324), channel_id=1, source_target_pairs={{0,2},{2,0},{1,3},{3,1},{4,6},{6,4},{5,7},{7,5},{8,10},{10,8},{9,1... | collective-permute-start | bytes 1671176 | tf_op jit(solution)/shard_map/rows_back0/ppermute | solution.py:85
  346.5 17.7 %collective-permute-start.60 = (bf16[128,2176]{1,0:T(8,128)(2,1)S(1)}, bf16[128,2176]{1,0:T(8,128)(2,1)S(1)}, u32[]{:S(2)}, u32[]{:S(2)}) collective-permute-start(bf16[128,2176]{1,0:T(8,128)(2,1)S(1)} %fusion.8), channel_id=1, source_target_pairs={{0,8},{8,16},{16,24},{24,0},{1,9},{9,17},{17,25},{25,1},{2,10},{10... | collective-permute-start | bytes 1671176 | tf_op jit(solution)/shard_map/partial_far/ppermute | solution.py:188
  346.7 24.8 %collective-permute-start.62 = (bf16[128,2176]{1,0:T(8,128)(2,1)S(1)}, bf16[128,2176]{1,0:T(8,128)(2,1)S(1)}, u32[]{:S(2)}, u32[]{:S(2)}) collective-permute-start(bf16[128,2176]{1,0:T(8,128)(2,1)S(1)} %add_convert_fusion), channel_id=1, source_target_pairs={{0,24},{8,0},{16,8},{24,16},{1,25},{9,1},{17,9},{25,17},{2,26},{10... | collective-permute-start | bytes 1671176 | tf_op jit(solution)/shard_map/partial_far/ppermute | solution.py:188
  373.7 22.2 %collective-permute-start.65 = (bf16[128,2048]{1,0:T(8,128)(2,1)S(1)}, bf16[128,2048]{1,0:T(8,128)(2,1)S(1)}, u32[]{:S(2)}, u32[]{:S(2)}) collective-permute-start(bf16[128,2048]{1,0:T(8,128)(2,1)S(1)} %fusion.47), channel_id=1, source_target_pairs={{0,5},{1,4},{4,1},{5,0},{2,7},{3,6},{6,3},{7,2},{8,13},{9,12},{12,... | collective-permute-start | bytes 1572872 | tf_op jit(solution)/shard_map/ppermute | solution.py:115
  375.5 22.5 %collective-permute-start.64 = (bf16[128,2048]{1,0:T(8,128)(2,1)S(1)}, bf16[128,2048]{1,0:T(8,128)(2,1)S(1)}, u32[]{:S(2)}, u32[]{:S(2)}) collective-permute-start(bf16[128,2048]{1,0:T(8,128)(2,1)S(1)} %fusion.47), channel_id=1, source_target_pairs={{0,4},{1,5},{4,0},{5,1},{2,6},{3,7},{6,2},{7,3},{8,12},{9,13},{12,... | collective-permute-start | bytes 1572872 | tf_op jit(solution)/shard_map/ppermute | solution.py:115
  375.9 22.2 %collective-permute-start.63 = (bf16[128,2048]{1,0:T(8,128)(2,1)S(1)}, bf16[128,2048]{1,0:T(8,128)(2,1)S(1)}, u32[]{:S(2)}, u32[]{:S(2)}) collective-permute-start(bf16[128,2048]{1,0:T(8,128)(2,1)S(1)} %fusion.47), channel_id=1, source_target_pairs={{0,1},{1,0},{4,5},{5,4},{2,3},{3,2},{6,7},{7,6},{8,9},{9,8},{12,13... | collective-permute-start | bytes 1572872 | tf_op jit(solution)/shard_map/ppermute | solution.py:115
  409.9 31.6 %collective-permute-start.67 = (bf16[128,2048]{1,0:T(8,128)(2,1)}, bf16[128,2048]{1,0:T(8,128)(2,1)S(1)}, u32[]{:S(2)}, u32[]{:S(2)}) collective-permute-start(bf16[128,2048]{1,0:T(8,128)(2,1)} %get-tuple-element.278), channel_id=1, source_target_pairs={{0,1},{1,0},{4,5},{5,4},{2,3},{3,2},{6,7},{7,6},{8,9},{9,8},{12,13... | collective-permute-start | bytes 1572872 | tf_op jit(solution)/shard_map/ppermute | solution.py:103
  410.8 30.7 %collective-permute-start.69 = (bf16[128,2048]{1,0:T(8,128)(2,1)}, bf16[128,2048]{1,0:T(8,128)(2,1)S(1)}, u32[]{:S(2)}, u32[]{:S(2)}) collective-permute-start(bf16[128,2048]{1,0:T(8,128)(2,1)} %get-tuple-element.279), channel_id=1, source_target_pairs={{0,5},{1,4},{4,1},{5,0},{2,7},{3,6},{6,3},{7,2},{8,13},{9,12},{12,... | collective-permute-start | bytes 1572872 | tf_op jit(solution)/shard_map/ppermute | solution.py:103
  412.3 30.8 %collective-permute-start.68 = (bf16[128,2048]{1,0:T(8,128)(2,1)}, bf16[128,2048]{1,0:T(8,128)(2,1)}, u32[]{:S(2)}, u32[]{:S(2)}) collective-permute-start(bf16[128,2048]{1,0:T(8,128)(2,1)} %get-tuple-element.280), channel_id=1, source_target_pairs={{0,4},{1,5},{4,0},{5,1},{2,6},{3,7},{6,2},{7,3},{8,12},{9,13},{12,... | collective-permute-start | bytes 1572872 | tf_op jit(solution)/shard_map/ppermute | solution.py:103
  455.3 16.8 %collective-permute-start.70 = (bf16[8,128,1280]{2,1,0:T(8,128)(2,1)}, bf16[8,128,1280]{2,1,0:T(8,128)(2,1)}, u32[]{:S(2)}, u32[]{:S(2)}) collective-permute-start(bf16[8,128,1280]{2,1,0:T(8,128)(2,1)} %fusion.9), channel_id=1, source_target_pairs={{0,2},{2,0},{1,3},{3,1},{4,6},{6,4},{5,7},{7,5},{8,10},{10,8},{9,1... | collective-permute-start | bytes 7864328 | tf_op jit(solution)/shard_map/ppermute | solution.py:85
  456.5 65.9 %all-to-all-start.3 = ((bf16[8,4,32,2048]{3,2,1,0:T(8,128)(2,1)}), bf16[8,4,32,2048]{3,2,1,0:T(8,128)(2,1)}, u32[]{:S(2)}, u32[]{:S(2)}) async-start(bf16[8,4,32,2048]{3,2,1,0:T(8,128)(2,1)} %pad_maximum_fusion.3), calls=%async_computation.3 | async-start | bytes 8388608 | tf_op jit(solution)/shard_map/all_to_all | solution.py:94
  462.7 16.6 %collective-permute-start.72 = (bf16[128,2048]{1,0:T(8,128)(2,1)S(1)}, bf16[128,2048]{1,0:T(8,128)(2,1)S(1)}, u32[]{:S(2)}, u32[]{:S(2)}) collective-permute-start(bf16[128,2048]{1,0:T(8,128)(2,1)S(1)} %get-tuple-element.276), channel_id=1, source_target_pairs={{0,8},{8,16},{16,24},{24,0},{1,9},{9,17},{17,25},{25,1},{2,10},{10... | collective-permute-start | bytes 1572872 | tf_op jit(solution)/shard_map/ppermute | solution.py:188
  462.8 25.8 %collective-permute-start.71 = (bf16[128,2048]{1,0:T(8,128)(2,1)S(1)}, bf16[128,2048]{1,0:T(8,128)(2,1)S(1)}, u32[]{:S(2)}, u32[]{:S(2)}) collective-permute-start(bf16[128,2048]{1,0:T(8,128)(2,1)S(1)} %get-tuple-element.277), channel_id=1, source_target_pairs={{0,24},{8,0},{16,8},{24,16},{1,25},{9,1},{17,9},{25,17},{2,26},{10... | collective-permute-start | bytes 1572872 | tf_op jit(solution)/shard_map/ppermute | solution.py:188
  488.7 14.9 %collective-permute-start.86 = (bf16[128,2048]{1,0:T(8,128)(2,1)S(1)}, bf16[128,2048]{1,0:T(8,128)(2,1)S(1)}, u32[]{:S(2)}, u32[]{:S(2)}) collective-permute-start(bf16[128,2048]{1,0:T(8,128)(2,1)S(1)} %fusion.58), channel_id=1, source_target_pairs={{0,24},{8,0},{16,8},{24,16},{1,25},{9,1},{17,9},{25,17},{2,26},{10... | collective-permute-start | bytes 1572872 | tf_op jit(solution)/shard_map/ppermute | solution.py:188
  491.6 25.5 %collective-permute-start.74 = (bf16[256,1280]{1,0:T(8,128)(2,1)S(1)}, bf16[256,1280]{1,0:T(8,128)(2,1)S(1)}, u32[]{:S(2)}, u32[]{:S(2)}) collective-permute-start(bf16[256,1280]{1,0:T(8,128)(2,1)S(1)} %get-tuple-element.271), channel_id=1, source_target_pairs={{0,24},{8,0},{16,8},{24,16},{1,25},{9,1},{17,9},{25,17},{2,26},{10... | collective-permute-start | bytes 1966088 | tf_op jit(solution)/shard_map/ppermute | solution.py:188
  494.5 54.1 %collective-permute-start.78 = (bf16[128,2048]{1,0:T(8,128)(2,1)}, bf16[128,2048]{1,0:T(8,128)(2,1)}, u32[]{:S(2)}, u32[]{:S(2)}) collective-permute-start(bf16[128,2048]{1,0:T(8,128)(2,1)} %get-tuple-element.272), channel_id=1, source_target_pairs={{0,5},{1,4},{4,1},{5,0},{2,7},{3,6},{6,3},{7,2},{8,13},{9,12},{12,... | collective-permute-start | bytes 1572872 | tf_op jit(solution)/shard_map/ppermute | solution.py:103
  496.9 51.6 %collective-permute-start.77 = (bf16[128,2048]{1,0:T(8,128)(2,1)}, bf16[128,2048]{1,0:T(8,128)(2,1)}, u32[]{:S(2)}, u32[]{:S(2)}) collective-permute-start(bf16[128,2048]{1,0:T(8,128)(2,1)} %get-tuple-element.273), channel_id=1, source_target_pairs={{0,4},{1,5},{4,0},{5,1},{2,6},{3,7},{6,2},{7,3},{8,12},{9,13},{12,... | collective-permute-start | bytes 1572872 | tf_op jit(solution)/shard_map/ppermute | solution.py:103
  497.5 51.1 %collective-permute-start.76 = (bf16[128,2048]{1,0:T(8,128)(2,1)}, bf16[128,2048]{1,0:T(8,128)(2,1)}, u32[]{:S(2)}, u32[]{:S(2)}) collective-permute-start(bf16[128,2048]{1,0:T(8,128)(2,1)} %get-tuple-element.274), channel_id=1, source_target_pairs={{0,1},{1,0},{4,5},{5,4},{2,3},{3,2},{6,7},{7,6},{8,9},{9,8},{12,13... | collective-permute-start | bytes 1572872 | tf_op jit(solution)/shard_map/ppermute | solution.py:103
  503.6 29.8 %collective-permute-start.73 = (bf16[256,1280]{1,0:T(8,128)(2,1)}, bf16[256,1280]{1,0:T(8,128)(2,1)}, u32[]{:S(2)}, u32[]{:S(2)}) collective-permute-start(bf16[256,1280]{1,0:T(8,128)(2,1)} %get-tuple-element.270), channel_id=1, source_target_pairs={{0,8},{8,16},{16,24},{24,0},{1,9},{9,17},{17,25},{25,1},{2,10},{10... | collective-permute-start | bytes 1966088 | tf_op jit(solution)/shard_map/ppermute | solution.py:188
  518.1 28.2 %collective-permute-start.75 = (bf16[256,1280]{1,0:T(8,128)(2,1)}, bf16[256,1280]{1,0:T(8,128)(2,1)}, u32[]{:S(2)}, u32[]{:S(2)}) collective-permute-start(bf16[256,1280]{1,0:T(8,128)(2,1)} %fusion.15), channel_id=1, source_target_pairs={{0,24},{8,0},{16,8},{24,16},{1,25},{9,1},{17,9},{25,17},{2,26},{10... | collective-permute-start | bytes 1966088 | tf_op jit(solution)/shard_map/ppermute | solution.py:188
  533.4 27.2 %collective-permute-start.80 = (bf16[128,2048]{1,0:T(8,128)(2,1)S(1)}, bf16[128,2048]{1,0:T(8,128)(2,1)S(1)}, u32[]{:S(2)}, u32[]{:S(2)}) collective-permute-start(bf16[128,2048]{1,0:T(8,128)(2,1)S(1)} %convolution_convert_fusion.10), channel_id=1, source_target_pairs={{0,24},{8,0},{16,8},{24,16},{1,25},{9,1},{17,9},{25,17},{2,26},{10... | collective-permute-start | bytes 1572872 | tf_op jit(solution)/shard_map/ppermute | solution.py:188
  546.3 23.5 %collective-permute-start.79 = (bf16[128,2048]{1,0:T(8,128)(2,1)S(1)}, bf16[128,2048]{1,0:T(8,128)(2,1)S(1)}, u32[]{:S(2)}, u32[]{:S(2)}) collective-permute-start(bf16[128,2048]{1,0:T(8,128)(2,1)S(1)} %convolution_convert_fusion.12), channel_id=1, source_target_pairs={{0,8},{8,16},{16,24},{24,0},{1,9},{9,17},{17,25},{25,1},{2,10},{10... | collective-permute-start | bytes 1572872 | tf_op jit(solution)/shard_map/ppermute | solution.py:188
  560.9 19.0 %collective-permute-start.81 = (bf16[128,2048]{1,0:T(8,128)(2,1)S(1)}, bf16[128,2048]{1,0:T(8,128)(2,1)S(1)}, u32[]{:S(2)}, u32[]{:S(2)}) collective-permute-start(bf16[128,2048]{1,0:T(8,128)(2,1)S(1)} %add_convert_fusion.2), channel_id=1, source_target_pairs={{0,24},{8,0},{16,8},{24,16},{1,25},{9,1},{17,9},{25,17},{2,26},{10... | collective-permute-start | bytes 1572872 | tf_op jit(solution)/shard_map/ppermute | solution.py:188
  580.9 17.4 %collective-permute-start.82 = (bf16[128,2048]{1,0:T(8,128)(2,1)S(1)}, bf16[128,2048]{1,0:T(8,128)(2,1)S(1)}, u32[]{:S(2)}, u32[]{:S(2)}) collective-permute-start(bf16[128,2048]{1,0:T(8,128)(2,1)S(1)} %add_convert_fusion.1), channel_id=1, source_target_pairs={{0,1},{1,0},{2,3},{3,2},{4,5},{5,4},{6,7},{7,6},{8,9},{9,8},{10,11... | collective-permute-start | bytes 1572872 | tf_op jit(solution)/shard_map/ppermute | solution.py:85
  583.0 16.6 %all-to-all-start.4 = ((f32[32,24,128]{2,1,0:T(8,128)}), f32[32,24,128]{2,1,0:T(8,128)S(1)}, u32[]{:S(2)}, u32[]{:S(2)}) async-start(f32[32,24,128]{2,1,0:T(8,128)} %bitcast.298), calls=%async_computation.4 | async-start | bytes 786432 | tf_op jit(solution)/shard_map/all_to_all | solution.py:94
  (83 other events, 594.4 us)

commit v9 on v8

--- a/solution.py
+++ b/solution.py
@@ -22,6 +22,8 @@
 NEAR = 2
 CORES = 2
 SLAB = NEAR * CORES * 2
+COT_CUT = 1280
+HEADS_STEP = 4
 LANES = 128
 
 EPS = 1e-06
@@ -367,9 +369,11 @@
         key_low[...] = turned(head_normed(key_ref[...], kgain_ref)[2], cos_ref, sin_ref).astype(BF)
         value_low[...] = value_ref[...].astype(BF)
 
-    query = turned(head_normed(query_ref[...], qgain_ref)[2], cos_ref, sin_ref).astype(BF)
-    probs = head_probs(query, key_low[...], row_ref, start_ref, key_row_ref)
-    mixed_ref[...] = mm(probs.astype(BF), value_low[...]).astype(BF)
+    for part in range(HEADS_STEP):
+        lanes = pl.ds(part * HEAD_DIM, HEAD_DIM)
+        query = turned(head_normed(query_ref[:, lanes], qgain_ref)[2], cos_ref, sin_ref).astype(BF)
+        probs = head_probs(query, key_low[...], row_ref, start_ref, key_row_ref)
+        mixed_ref[:, lanes] = mm(probs.astype(BF), value_low[...]).astype(BF)
 
 
 def attend_back_kernel(
@@ -399,16 +403,20 @@
         grad = grad * gain_ref[...]
         return scale * (grad - normal * jnp.mean(normal * grad, axis=-1, keepdims=True))
 
-    normal, scale, gained = head_normed(query_ref[...], qgain_ref)
-    query = turned(gained, cos_ref, sin_ref).astype(BF)
-    probs = head_probs(query, key_low[...], row_ref, start_ref, key_row_ref)
-    grad = grad_ref[...]
-    value_total[...] += mm_tn(probs.astype(BF), grad)
-    prob_grad = mm_nt(grad, value_low[...])
-    score_grad = (probs * (prob_grad - jnp.sum(probs * prob_grad, axis=-1, keepdims=True))).astype(BF)
-    key_total[...] += mm_tn(score_grad, query) * score_scale
-    query_grad = mm(score_grad, key_low[...]) * score_scale
-    query_out[...] = raw_grad(query_grad, normal, scale, qgain_ref, qgain_out).astype(BF)
+    for part in range(HEADS_STEP):
+        lanes = pl.ds(part * HEAD_DIM, HEAD_DIM)
+        normal, scale, gained = head_normed(query_ref[:, lanes], qgain_ref)
+        query = turned(gained, cos_ref, sin_ref).astype(BF)
+        probs = head_probs(query, key_low[...], row_ref, start_ref, key_row_ref)
+        grad = grad_ref[:, lanes]
+        value_total[...] += mm_tn(probs.astype(BF), grad)
+        prob_grad = mm_nt(grad, value_low[...])
+        score_grad = (
+            probs * (prob_grad - jnp.sum(probs * prob_grad, axis=-1, keepdims=True))
+        ).astype(BF)
+        key_total[...] += mm_tn(score_grad, query) * score_scale
+        query_grad = mm(score_grad, key_low[...]) * score_scale
+        query_out[:, lanes] = raw_grad(query_grad, normal, scale, qgain_ref, qgain_out).astype(BF)
 
     @pl.when(head == pl.num_programs(1) - 1)
     def _():
@@ -418,7 +426,7 @@
 
 
 def attend_specs(heads):
-    head = pl.BlockSpec((ROW, HEAD_DIM), lambda b, h: (b, h))
+    head = pl.BlockSpec((ROW, HEADS_STEP * HEAD_DIM), lambda b, h: (b, h))
     whole = pl.BlockSpec((ROW, HEAD_DIM), lambda b, h: (b, 0))
     gain = pl.BlockSpec((1, HEAD_DIM), lambda b, h: (0, 0))
     column = pl.BlockSpec((1, ROW, 1), lambda b, h: (b, 0, 0))
@@ -437,7 +445,7 @@
     rows = projected.shape[0]
     return pl.pallas_call(
         attend_kernel,
-        grid=(rows // ROW, heads),
+        grid=(rows // ROW, heads // HEADS_STEP),
         in_specs=specs,
         out_specs=head,
         out_shape=jax.ShapeDtypeStruct((rows, heads * HEAD_DIM), BF),
@@ -452,7 +460,7 @@
     rows = projected.shape[0]
     return pl.pallas_call(
         attend_back_kernel,
-        grid=(rows // ROW, heads),
+        grid=(rows // ROW, heads // HEADS_STEP),
         in_specs=specs + [head],
         out_specs=[head, whole, whole, gain, gain],
         out_shape=[
@@ -589,8 +597,8 @@
     cot_low = mm(hot_half, cot_pair).astype(BF)
     cot_rows = cot_low.astype(F32)
     cot_sent = [
-        mm(slot_low, half).astype(BF).reshape(device_count, capacity, D // 2)
-        for half in (cot_low[:, : D // 2], cot_low[:, D // 2 :])
+        mm(slot_low, part).astype(BF).reshape(device_count, capacity, part.shape[1])
+        for part in (cot_low[:, :COT_CUT], cot_low[:, COT_CUT:])
     ]
     qkv_own = far_stack(qkv_far).reshape(far_count * NEAR, half_rows, width)
     qkv_mine = jnp.stack(pair_order(qkv_own, swap(qkv_own, CORE_AXIS), CORE_AXIS), axis=1).reshape(

time: 609 us -> 603 us (level)
  Pallas kernels: 99.2 us -> 86.4 us
  waiting for transfers between devices: 235 us -> 245 us
    pallas_call x2, Pallas kernels: 40.5 us -> 27.8 us  [the longest x1 16.9 us: attend_back(): pl.pallas_call(attend_back_kernel, grid=(rows // ROW, heads // HEADS_STEP...]
    ppermute x24, waiting for transfers between devices: 113 us -> 123 us  [far_shift(): lax.ppermute(value, FAR_AXIS, [(i, (i + step) % count) for i in range(cou...]
    unnamed x128 -> x138, local copies, waits for them, and re-layouts: 17.3 us -> 14.4 us
  transfers between devices with their start and end apart: 92 -> 92, of which waited for: 37 -> 39; matrix products, arithmetic and copies ran while one was open for 17% -> 17% of each run, Pallas kernels for 16% -> 15%
where the time goes in v9:
time: 603 us; the launch traced here: 595 us
  waiting for transfers between devices  245 us (41%)
  starting transfers between devices  127 us (21%)
  Pallas kernels  86.4 us (14%)
  local copies, waits for them, and re-layouts  47.8 us (8%)
  other arithmetic  44.7 us (7%)
  matrix products  41.3 us (7%)
    ppermute x24, waiting for transfers between devices, far_shift(): lax.ppermute(value, FAR_AXIS, [(i, (i + step) % count) for i in range(cou...  123 us
    ppermute x30, waiting for transfers between devices, quad_send(): return lax.ppermute(block, HEAD_AXES, [(i, i ^ step) for i in range(4)])  96.5 us
    ppermute x24, starting transfers between devices, far_shift(): lax.ppermute(value, FAR_AXIS, [(i, (i + step) % count) for i in range(cou...  41.2 us
    pallas_call x4, Pallas kernels, expert_chunk(): pl.pallas_call(expert_kernel, grid_spec=pltpu.PrefetchScalarGridSpec(num_...  40 us
    dot_general x30, matrix products, dot(): lax.dot_general(left, right, (dims, ((), ())), preferred_element_type=F32)  38.9 us
    ppermute x30, starting transfers between devices, quad_send(): return lax.ppermute(block, HEAD_AXES, [(i, i ^ step) for i in range(4)])  36.1 us
    all_to_all x5, starting transfers between devices, exchange(): return lax.all_to_all(value, axes, split_axis=0, concat_axis=0, tiled=True)  21.8 us
    pallas_call x1, Pallas kernels, expert_grads(): pl.pallas_call(functools.partial(expert_grad_kernel, count), grid=(D // t...  18.7 us
  transfers between devices with their start and end apart: 92, of which 39 were waited for; matrix products, arithmetic and copies ran while one was open for 17% of the time, Pallas kernels for 15%

profile of v9, /device:TPU:0, one launch (start us, length us, event | category | flops | bytes accessed | tf_op | source)
XLA Modules:
  0.0 595.2 jit_solution(6482961643356124711)
XLA Ops:
  1.3 3.0 collective-permute-start
  17.8 2.5 collective-permute-start.3
  25.3 2.9 all-to-all-start
  30.0 2.7 collective-permute-start.6
  40.4 13.6 %collective-permute-done.7 = bf16[256,1280]{1,0:T(8,128)(2,1)} collective-permute-done((bf16[256,1280]{1,0:T(8,128)(2,1)}, bf16[256,1280]{1,0:T(8,128)(2,1)}, u32[]{:S(2)}, u32[]{:S(2)}) %collective-permute-start.7) | collective-permute-done | bytes 655392 | tf_op jit(solution)/shard_map/ppermute | solution.py:190
  56.5 24.1 %collective-permute-done.8 = bf16[256,1280]{1,0:T(8,128)(2,1)S(1)} collective-permute-done((bf16[256,1280]{1,0:T(8,128)(2,1)}, bf16[256,1280]{1,0:T(8,128)(2,1)S(1)}, u32[]{:S(2)}, u32[]{:S(2)}) %collective-permute-start.8) | collective-permute-done | bytes 655392 | tf_op jit(solution)/shard_map/ppermute | solution.py:190
  84.3 2.3 convolution_convert_fusion.2
  88.9 4.3 collective-permute-done.4
  98.9 4.4 fusion.170.query_ref.key_ref.value_ref
  103.3 4.3 all-to-all-start.1
  109.4 3.5 collective-permute-done.13
  116.8 2.7 dynamic-slice_bitcast_fusion.18
  125.6 10.9 %attend.1 = bf16[512,1024]{1,0:T(8,128)(2,1)} custom-call(f32[512,1280]{1,0:T(8,128)} %fusion.170.query_ref.key_ref.value_ref, f32[512,1280]{1,0:T(8,128)} %fusion.170.query_ref.key_ref.value_ref, f32[512,1280]{1,0:T(8,128)} %fusion.170.query_ref.key_ref.value_ref, f32[512,128]{1,0:T(8,128)} %get-tuple-element.439.cos_ref, ...), custom_call_target="tpu_custom_call" | custom-call | flops 1048576 | bytes 1048576 | tf_op jit(solution)/shard_map/attend/pallas_call | solution.py:446
  136.5 13.1 %collective-permute-done.17 = bf16[128,2048]{1,0:T(8,128)(2,1)S(1)} collective-permute-done((bf16[128,2048]{1,0:T(8,128)(2,1)}, bf16[128,2048]{1,0:T(8,128)(2,1)S(1)}, u32[]{:S(2)}, u32[]{:S(2)}) %collective-permute-start.17) | collective-permute-done | bytes 524320 | tf_op jit(solution)/shard_map/ppermute | solution.py:105
  149.6 9.5 %collective-permute-done.16 = bf16[128,2048]{1,0:T(8,128)(2,1)S(1)} collective-permute-done((bf16[128,2048]{1,0:T(8,128)(2,1)}, bf16[128,2048]{1,0:T(8,128)(2,1)S(1)}, u32[]{:S(2)}, u32[]{:S(2)}) %collective-permute-start.16) | collective-permute-done | bytes 524320 | tf_op jit(solution)/shard_map/ppermute | solution.py:105
  162.3 3.0 collective-permute-start.22
  169.1 4.2 collective-permute-done.23
  173.5 6.3 %all-to-all-start.2 = ((bf16[32,32,768]{2,1,0:T(8,128)(2,1)}), bf16[32,32,768]{2,1,0:T(8,128)(2,1)}, u32[]{:S(2)}, u32[]{:S(2)}) async-start(bf16[32,32,768]{2,1,0:T(8,128)(2,1)} %bitcast.655), calls=%async_computation.2 | async-start | bytes 3145728 | tf_op jit(solution)/shard_map/all_to_all | solution.py:96
  182.9 2.4 convolution_convert_fusion.3
  192.1 17.6 %collective-permute-done.19 = bf16[128,2048]{1,0:T(8,128)(2,1)} collective-permute-done((bf16[128,2048]{1,0:T(8,128)(2,1)S(1)}, bf16[128,2048]{1,0:T(8,128)(2,1)}, u32[]{:S(2)}, u32[]{:S(2)}) %collective-permute-start.19) | collective-permute-done | bytes 524320 | tf_op jit(solution)/shard_map/ppermute | solution.py:105
  209.7 13.2 %collective-permute-done.21 = bf16[128,2048]{1,0:T(8,128)(2,1)} collective-permute-done((bf16[128,2048]{1,0:T(8,128)(2,1)S(1)}, bf16[128,2048]{1,0:T(8,128)(2,1)}, u32[]{:S(2)}, u32[]{:S(2)}) %collective-permute-start.21) | collective-permute-done | bytes 524320 | tf_op jit(solution)/shard_map/ppermute | solution.py:105
  222.9 2.4 multiply_reduce_fusion.3
  229.8 2.6 collective-permute-start.27
  232.5 2.7 pad_maximum_fusion.2
  235.6 6.6 %collective-permute-done.26 = bf16[2,32,2048]{2,1,0:T(8,128)(2,1)S(1)} collective-permute-done((bf16[2,32,2048]{2,1,0:T(8,128)(2,1)S(1)}, bf16[2,32,2048]{2,1,0:T(8,128)(2,1)S(1)}, u32[]{:S(2)}, u32[]{:S(2)}) %collective-permute-start.26) | collective-permute-done | bytes 262176 | tf_op jit(solution)/shard_map/rows_out0/ppermute | solution.py:198
  250.0 10.0 %expert_chunk.4 = (bf16[256,768]{1,0:T(8,128)(2,1)S(1)}, bf16[256,768]{1,0:T(8,128)(2,1)S(1)}, bf16[256,768]{1,0:T(8,128)(2,1)S(1)}, bf16[256,2048]{1,0:T(8,128)...) custom-call(s32[2]{0:T(128)S(1)} %pad_add_fusion.2.here_ref, bf16[256,2048]{1,0:T(8,128)(2,1)S(1)} %bitcast.609, ...), custom_call_target="tpu_custom_call" | custom-call | flops 1048576 | bytes 1048576 | tf_op jit(solution)/shard_map/expert_chunk/pallas_call | solution.py:276
  260.3 2.8 collective-permute-done.34
  268.0 10.0 %expert_chunk.5 = (bf16[256,768]{1,0:T(8,128)(2,1)S(1)}, bf16[256,768]{1,0:T(8,128)(2,1)S(1)}, bf16[256,768]{1,0:T(8,128)(2,1)S(1)}, bf16[256,2048]{1,0:T(8,128)...) custom-call(s32[2]{0:T(128)S(1)} %pad_add_fusion.2.here_ref, bf16[256,2048]{1,0:T(8,128)(2,1)S(1)} %bitcast.611, ...), custom_call_target="tpu_custom_call" | custom-call | flops 1048576 | bytes 1048576 | tf_op jit(solution)/shard_map/expert_chunk/pallas_call | solution.py:276
  285.4 10.0 %expert_chunk.6 = (bf16[256,768]{1,0:T(8,128)(2,1)S(1)}, bf16[256,768]{1,0:T(8,128)(2,1)S(1)}, bf16[256,768]{1,0:T(8,128)(2,1)S(1)}, bf16[256,2048]{1,0:T(8,128)...) custom-call(s32[2]{0:T(128)S(1)} %pad_add_fusion.2.here_ref, bf16[256,2048]{1,0:T(8,128)(2,1)S(1)} %bitcast.613, ...), custom_call_target="tpu_custom_call" | custom-call | flops 1048576 | bytes 1048576 | tf_op jit(solution)/shard_map/expert_chunk/pallas_call | solution.py:276
  300.5 10.1 %expert_chunk.7 = (bf16[256,768]{1,0:T(8,128)(2,1)S(1)}, bf16[256,768]{1,0:T(8,128)(2,1)S(1)}, bf16[256,768]{1,0:T(8,128)(2,1)S(1)}, bf16[256,2048]{1,0:T(8,128)...) custom-call(s32[2]{0:T(128)S(1)} %pad_add_fusion.2.here_ref, bf16[256,2048]{1,0:T(8,128)(2,1)S(1)} %bitcast.615, ...), custom_call_target="tpu_custom_call" | custom-call | flops 1048576 | bytes 1048576 | tf_op jit(solution)/shard_map/expert_chunk/pallas_call | solution.py:276
  315.6 6.5 %collective-permute-done.51 = bf16[2,32,2176]{2,1,0:T(8,128)(2,1)S(1)} collective-permute-done((bf16[2,32,2176]{2,1,0:T(8,128)(2,1)S(1)}, bf16[2,32,2176]{2,1,0:T(8,128)(2,1)S(1)}, u32[]{:S(2)}, u32[]{:S(2)}) %collective-permute-start.51) | collective-permute-done | bytes 278560 | tf_op jit(solution)/shard_map/rows_back2/ppermute | solution.py:105
  322.1 4.6 collective-permute-done.49
  327.4 3.3 collective-permute-start.61
  334.6 5.9 collective-permute-done.57
  340.5 5.5 collective-permute-done.58
  346.6 3.9 collective-permute-start.62
  354.5 5.7 collective-permute-done.53
  360.3 3.7 collective-permute-done.54
  364.0 7.8 %collective-permute-done.62 = bf16[128,2176]{1,0:T(8,128)(2,1)S(1)} collective-permute-done((bf16[128,2176]{1,0:T(8,128)(2,1)S(1)}, bf16[128,2176]{1,0:T(8,128)(2,1)S(1)}, u32[]{:S(2)}, u32[]{:S(2)}) %collective-permute-start.62) | collective-permute-done | bytes 557088 | tf_op jit(solution)/shard_map/partial_far/ppermute | solution.py:190
  377.6 18.7 %expert_grads.1 = f32[2048,2304]{1,0:T(8,128)} custom-call(bf16[256,2048]{1,0:T(8,128)(2,1)S(1)} %bitcast.610, bf16[256,2048]{1,0:T(8,128)(2,1)} %bitcast.612, bf16[256,2048]{1,0:T(8,128)(2,1)} %bitcast.614, bf16[256,2048]{1,0:T(8,128)(2,1)} %bitcast.616, bf16[256,2048]{1,0:T(8,128)(2,1)} %copy-done.3, bf16[256,2048]{1,0:T(8,128)(2,1)} %copy-done.4, ...), custom_call_target="tpu_custom_call" | custom-call | flops 1048576 | bytes 1048576 | tf_op jit(solution)/shard_map/expert_grads/pallas_call | solution.py:329
  399.8 2.4 convolution_convert_fusion.1
  404.4 3.3 convolution_convert_fusion.16.grad_ref
  417.8 16.9 %attend_back.1 = (bf16[512,1024]{1,0:T(8,128)(2,1)}, bf16[512,128]{1,0:T(8,128)(2,1)}, bf16[512,128]{1,0:T(8,128)(2,1)}, f32[1,128]{1,0:T(1,128)}, f32[1,128]{1,0:T(1,128)}) custom-call(f32[512,1280]{1,0:T(8,128)} %fusion.170.query_ref.key_ref.value_ref, f32[512,1280]{1,0:T(8,128)} %fusion.170.query_ref.key_ref.value_ref, ...), custom_call_target="tpu_custom_call" | custom-call | flops 1048576 | bytes 1048576 | tf_op jit(solution)/shard_map/attend_back/pallas_call | solution.py:461
  442.9 3.2 convolution_convert_fusion
  450.4 4.7 all-to-all-start.3
  456.6 3.8 collective-permute-start.71
  460.4 5.6 convolution_convert_fusion.4
  466.1 3.0 fusion
  469.0 4.1 collective-permute-done.72
  473.2 9.0 %collective-permute-done.71 = bf16[128,2048]{1,0:T(8,128)(2,1)S(1)} collective-permute-done((bf16[128,2048]{1,0:T(8,128)(2,1)S(1)}, bf16[128,2048]{1,0:T(8,128)(2,1)S(1)}, u32[]{:S(2)}, u32[]{:S(2)}) %collective-permute-start.71) | collective-permute-done | bytes 524320 | tf_op jit(solution)/shard_map/ppermute | solution.py:190
  488.3 2.5 collective-permute-start.78
  491.8 5.4 collective-permute-done.86
  499.9 11.0 %collective-permute-done.74 = bf16[256,1280]{1,0:T(8,128)(2,1)S(1)} collective-permute-done((bf16[256,1280]{1,0:T(8,128)(2,1)S(1)}, bf16[256,1280]{1,0:T(8,128)(2,1)S(1)}, u32[]{:S(2)}, u32[]{:S(2)}) %collective-permute-start.74) | collective-permute-done | bytes 655392 | tf_op jit(solution)/shard_map/ppermute | solution.py:190
  511.9 4.6 collective-permute-start.75
  516.5 2.8 fusion.161
  520.3 6.9 %collective-permute-done.73 = bf16[256,1280]{1,0:T(8,128)(2,1)} collective-permute-done((bf16[256,1280]{1,0:T(8,128)(2,1)}, bf16[256,1280]{1,0:T(8,128)(2,1)}, u32[]{:S(2)}, u32[]{:S(2)}) %collective-permute-start.73) | collective-permute-done | bytes 655392 | tf_op jit(solution)/shard_map/ppermute | solution.py:190
  529.4 10.7 %collective-permute-done.75 = bf16[256,1280]{1,0:T(8,128)(2,1)S(1)} collective-permute-done((bf16[256,1280]{1,0:T(8,128)(2,1)}, bf16[256,1280]{1,0:T(8,128)(2,1)S(1)}, u32[]{:S(2)}, u32[]{:S(2)}) %collective-permute-start.75) | collective-permute-done | bytes 655392 | tf_op jit(solution)/shard_map/ppermute | solution.py:190
  549.3 2.9 collective-permute-done.85
  554.4 2.5 collective-permute-start.81
  558.1 5.5 collective-permute-done.79
  563.7 10.0 %collective-permute-done.81 = bf16[128,2048]{1,0:T(8,128)(2,1)S(1)} collective-permute-done((bf16[128,2048]{1,0:T(8,128)(2,1)S(1)}, bf16[128,2048]{1,0:T(8,128)(2,1)S(1)}, u32[]{:S(2)}, u32[]{:S(2)}) %collective-permute-start.81) | collective-permute-done | bytes 524320 | tf_op jit(solution)/shard_map/ppermute | solution.py:190
  576.8 3.6 all-to-all-start.4
  580.5 2.5 fusion.11
  582.9 9.2 %collective-permute-done.82 = bf16[128,2048]{1,0:T(8,128)(2,1)S(1)} collective-permute-done((bf16[128,2048]{1,0:T(8,128)(2,1)S(1)}, bf16[128,2048]{1,0:T(8,128)(2,1)S(1)}, u32[]{:S(2)}, u32[]{:S(2)}) %collective-permute-start.82) | collective-permute-done | bytes 524320 | tf_op jit(solution)/shard_map/ppermute | solution.py:87
  (481 shorter events, 182.7 us)
Async XLA Ops:
  1.3 16.4 %collective-permute-start = (s32[1,384]{1,0:T(1,128)S(1)}, s32[1,384]{1,0:T(1,128)S(1)}, u32[]{:S(2)}, u32[]{:S(2)}) collective-permute-start(s32[1,384]{1,0:T(1,128)S(1)} %pad_add_fusion), channel_id=1, source_target_pairs={{0,4},{4,0},{1,5},{5,1},{2,6},{6,2},{3,7},{7,3},{8,12},{12,8},{9,1... | collective-permute-start | bytes 4616 | tf_op jit(solution)/shard_map/ppermute | solution.py:87
  4.3 35.6 %collective-permute-start.11 = (bf16[128,2048]{1,0:T(8,128)(2,1)}, bf16[128,2048]{1,0:T(8,128)(2,1)}, u32[]{:S(2)}, u32[]{:S(2)}) collective-permute-start(bf16[128,2048]{1,0:T(8,128)(2,1)} %param.12), channel_id=1, source_target_pairs={{0,1},{1,0},{2,3},{3,2},{4,5},{5,4},{6,7},{7,6},{8,9},{9,8},{10,11... | collective-permute-start | bytes 1572872 | tf_op jit(solution)/shard_map/ppermute | solution.py:87
  5.8 80.9 %collective-permute-start.12 = (bf16[128,2048]{1,0:T(8,128)(2,1)}, bf16[128,2048]{1,0:T(8,128)(2,1)}, u32[]{:S(2)}, u32[]{:S(2)}) collective-permute-start(bf16[128,2048]{1,0:T(8,128)(2,1)} %param.14), channel_id=1, source_target_pairs={{0,8},{8,16},{16,24},{24,0},{1,9},{9,17},{17,25},{25,1},{2,10},{10... | collective-permute-start | bytes 1572872 | tf_op jit(solution)/shard_map/ppermute | solution.py:190
  11.5 18.5 %collective-permute-start.1 = (bf16[64,1280]{1,0:T(8,128)(2,1)S(1)}, bf16[64,1280]{1,0:T(8,128)(2,1)S(1)}, u32[]{:S(2)}, u32[]{:S(2)}) collective-permute-start(bf16[64,1280]{1,0:T(8,128)(2,1)S(1)} %bitcast.717), channel_id=1, source_target_pairs={{0,1},{1,0},{4,5},{5,4},{2,3},{3,2},{6,7},{7,6},{8,9},{9,8},{12,13... | collective-permute-start | bytes 491528 | tf_op jit(solution)/shard_map/ppermute | solution.py:105
  12.1 17.8 %collective-permute-start.2 = (bf16[64,1280]{1,0:T(8,128)(2,1)S(1)}, bf16[64,1280]{1,0:T(8,128)(2,1)S(1)}, u32[]{:S(2)}, u32[]{:S(2)}) collective-permute-start(bf16[64,1280]{1,0:T(8,128)(2,1)S(1)} %bitcast.718), channel_id=1, source_target_pairs={{0,4},{1,5},{4,0},{5,1},{2,6},{3,7},{6,2},{7,3},{8,12},{9,13},{12,... | collective-permute-start | bytes 491528 | tf_op jit(solution)/shard_map/ppermute | solution.py:105
  25.3 13.7 %all-to-all-start = ((bf16[32,32,128]{2,1,0:T(8,128)(2,1)}), bf16[32,32,128]{2,1,0:T(8,128)(2,1)S(1)}, u32[]{:S(2)}, u32[]{:S(2)}) async-start(bf16[32,32,128]{2,1,0:T(8,128)(2,1)} %bitcast.290), calls=%async_computation | async-start | bytes 524288 | tf_op jit(solution)/shard_map/all_to_all | solution.py:96
  30.0 58.2 %collective-permute-start.6 = (bf16[128,2048]{1,0:T(8,128)(2,1)S(1)}, bf16[128,2048]{1,0:T(8,128)(2,1)}, u32[]{:S(2)}, u32[]{:S(2)}) collective-permute-start(bf16[128,2048]{1,0:T(8,128)(2,1)S(1)} %copy-done.12), channel_id=1, source_target_pairs={{0,5},{1,4},{4,1},{5,0},{2,7},{3,6},{6,3},{7,2},{8,13},{9,12},{12,... | collective-permute-start | bytes 1572872 | tf_op jit(solution)/shard_map/ppermute | solution.py:117
  32.7 56.1 %collective-permute-start.5 = (bf16[128,2048]{1,0:T(8,128)(2,1)S(1)}, bf16[128,2048]{1,0:T(8,128)(2,1)}, u32[]{:S(2)}, u32[]{:S(2)}) collective-permute-start(bf16[128,2048]{1,0:T(8,128)(2,1)S(1)} %copy-done.12), channel_id=1, source_target_pairs={{0,4},{1,5},{4,0},{5,1},{2,6},{3,7},{6,2},{7,3},{8,12},{9,13},{12,... | collective-permute-start | bytes 1572872 | tf_op jit(solution)/shard_map/ppermute | solution.py:117
  34.3 19.8 %collective-permute-start.7 = (bf16[256,1280]{1,0:T(8,128)(2,1)}, bf16[256,1280]{1,0:T(8,128)(2,1)}, u32[]{:S(2)}, u32[]{:S(2)}) collective-permute-start(bf16[256,1280]{1,0:T(8,128)(2,1)} %bitcast.18), channel_id=1, source_target_pairs={{0,8},{8,16},{16,24},{24,0},{1,9},{9,17},{17,25},{25,1},{2,10},{10... | collective-permute-start | bytes 1966088 | tf_op jit(solution)/shard_map/ppermute | solution.py:190
  39.9 41.2 %collective-permute-start.9 = (bf16[256,1280]{1,0:T(8,128)(2,1)}, bf16[256,1280]{1,0:T(8,128)(2,1)S(1)}, u32[]{:S(2)}, u32[]{:S(2)}) collective-permute-start(bf16[256,1280]{1,0:T(8,128)(2,1)} %bitcast.18), channel_id=1, source_target_pairs={{0,24},{8,0},{16,8},{24,16},{1,25},{9,1},{17,9},{25,17},{2,26},{10... | collective-permute-start | bytes 1966088 | tf_op jit(solution)/shard_map/ppermute | solution.py:190
  54.1 26.6 %collective-permute-start.8 = (bf16[256,1280]{1,0:T(8,128)(2,1)}, bf16[256,1280]{1,0:T(8,128)(2,1)S(1)}, u32[]{:S(2)}, u32[]{:S(2)}) collective-permute-start(bf16[256,1280]{1,0:T(8,128)(2,1)} %collective-permute-done.7), channel_id=1, source_target_pairs={{0,8},{8,16},{16,24},{24,0},{1,9},{9,17},{17,25},{25,1},{2,10},{10... | collective-permute-start | bytes 1966088 | tf_op jit(solution)/shard_map/ppermute | solution.py:190
  81.2 16.5 %collective-permute-start.10 = (bf16[8,128,1280]{2,1,0:T(8,128)(2,1)S(1)}, bf16[8,128,1280]{2,1,0:T(8,128)(2,1)S(1)}, u32[]{:S(2)}, u32[]{:S(2)}) collective-permute-start(bf16[8,128,1280]{2,1,0:T(8,128)(2,1)S(1)} %bitcast.648), channel_id=1, source_target_pairs={{0,2},{2,0},{1,3},{3,1},{4,6},{6,4},{5,7},{7,5},{8,10},{10,8},{9,1... | collective-permute-start | bytes 7864328 | tf_op jit(solution)/shard_map/ppermute | solution.py:87
  86.7 28.2 %collective-permute-start.14 = (bf16[128,2048]{1,0:T(8,128)(2,1)}, bf16[128,2048]{1,0:T(8,128)(2,1)}, u32[]{:S(2)}, u32[]{:S(2)}) collective-permute-start(bf16[128,2048]{1,0:T(8,128)(2,1)} %param.14), channel_id=1, source_target_pairs={{0,24},{8,0},{16,8},{24,16},{1,25},{9,1},{17,9},{25,17},{2,26},{10... | collective-permute-start | bytes 1572872 | tf_op jit(solution)/shard_map/ppermute | solution.py:190
  88.2 24.7 %collective-permute-start.13 = (bf16[128,2048]{1,0:T(8,128)(2,1)}, bf16[128,2048]{1,0:T(8,128)(2,1)}, u32[]{:S(2)}, u32[]{:S(2)}) collective-permute-start(bf16[128,2048]{1,0:T(8,128)(2,1)} %collective-permute-done.12), channel_id=1, source_target_pairs={{0,8},{8,16},{16,24},{24,0},{1,9},{9,17},{17,25},{25,1},{2,10},{10... | collective-permute-start | bytes 1572872 | tf_op jit(solution)/shard_map/ppermute | solution.py:190
  103.3 70.2 %all-to-all-start.1 = ((bf16[32,32,1280]{2,1,0:T(8,128)(2,1)}), bf16[32,32,1280]{2,1,0:T(8,128)(2,1)}, u32[]{:S(2)}, u32[]{:S(2)}) async-start(bf16[32,32,1280]{2,1,0:T(8,128)(2,1)} %bitcast.27), calls=%async_computation.1 | async-start | bytes 5242880 | tf_op jit(solution)/shard_map/all_to_all | solution.py:96
  119.5 30.1 %collective-permute-start.17 = (bf16[128,2048]{1,0:T(8,128)(2,1)}, bf16[128,2048]{1,0:T(8,128)(2,1)S(1)}, u32[]{:S(2)}, u32[]{:S(2)}) collective-permute-start(bf16[128,2048]{1,0:T(8,128)(2,1)} %get-tuple-element.292), channel_id=1, source_target_pairs={{0,5},{1,4},{4,1},{5,0},{2,7},{3,6},{6,3},{7,2},{8,13},{9,12},{12,... | collective-permute-start | bytes 1572872 | tf_op jit(solution)/shard_map/ppermute | solution.py:105
  121.8 37.4 %collective-permute-start.16 = (bf16[128,2048]{1,0:T(8,128)(2,1)}, bf16[128,2048]{1,0:T(8,128)(2,1)S(1)}, u32[]{:S(2)}, u32[]{:S(2)}) collective-permute-start(bf16[128,2048]{1,0:T(8,128)(2,1)} %get-tuple-element.293), channel_id=1, source_target_pairs={{0,4},{1,5},{4,0},{5,1},{2,6},{3,7},{6,2},{7,3},{8,12},{9,13},{12,... | collective-permute-start | bytes 1572872 | tf_op jit(solution)/shard_map/ppermute | solution.py:105
  122.2 38.9 %collective-permute-start.15 = (bf16[128,2048]{1,0:T(8,128)(2,1)S(1)}, bf16[128,2048]{1,0:T(8,128)(2,1)S(1)}, u32[]{:S(2)}, u32[]{:S(2)}) collective-permute-start(bf16[128,2048]{1,0:T(8,128)(2,1)S(1)} %get-tuple-element.294), channel_id=1, source_target_pairs={{0,1},{1,0},{4,5},{5,4},{2,3},{3,2},{6,7},{7,6},{8,9},{9,8},{12,13... | collective-permute-start | bytes 1572872 | tf_op jit(solution)/shard_map/ppermute | solution.py:105
  161.7 18.1 %collective-permute-start.18 = (bf16[2,256,2048]{2,1,0:T(8,128)(2,1)S(1)}, bf16[2,256,2048]{2,1,0:T(8,128)(2,1)}, u32[]{:S(2)}, u32[]{:S(2)}) collective-permute-start(bf16[2,256,2048]{2,1,0:T(8,128)(2,1)S(1)} %bitcast.653), channel_id=1, source_target_pairs={{0,2},{2,0},{1,3},{3,1},{4,6},{6,4},{5,7},{7,5},{8,10},{10,8},{9,1... | collective-permute-start | bytes 6291464 | tf_op jit(solution)/shard_map/ppermute | solution.py:87
  173.5 54.2 %all-to-all-start.2 = ((bf16[32,32,768]{2,1,0:T(8,128)(2,1)}), bf16[32,32,768]{2,1,0:T(8,128)(2,1)}, u32[]{:S(2)}, u32[]{:S(2)}) async-start(bf16[32,32,768]{2,1,0:T(8,128)(2,1)} %bitcast.655), calls=%async_computation.2 | async-start | bytes 3145728 | tf_op jit(solution)/shard_map/all_to_all | solution.py:96
  185.5 24.2 %collective-permute-start.19 = (bf16[128,2048]{1,0:T(8,128)(2,1)S(1)}, bf16[128,2048]{1,0:T(8,128)(2,1)}, u32[]{:S(2)}, u32[]{:S(2)}) collective-permute-start(bf16[128,2048]{1,0:T(8,128)(2,1)S(1)} %get-tuple-element.285), channel_id=1, source_target_pairs={{0,1},{1,0},{4,5},{5,4},{2,3},{3,2},{6,7},{7,6},{8,9},{9,8},{12,13... | collective-permute-start | bytes 1572872 | tf_op jit(solution)/shard_map/ppermute | solution.py:105
  187.4 35.4 %collective-permute-start.21 = (bf16[128,2048]{1,0:T(8,128)(2,1)S(1)}, bf16[128,2048]{1,0:T(8,128)(2,1)}, u32[]{:S(2)}, u32[]{:S(2)}) collective-permute-start(bf16[128,2048]{1,0:T(8,128)(2,1)S(1)} %get-tuple-element.286), channel_id=1, source_target_pairs={{0,5},{1,4},{4,1},{5,0},{2,7},{3,6},{6,3},{7,2},{8,13},{9,12},{12,... | collective-permute-start | bytes 1572872 | tf_op jit(solution)/shard_map/ppermute | solution.py:105
  189.7 33.2 %collective-permute-start.20 = (bf16[128,2048]{1,0:T(8,128)(2,1)S(1)}, bf16[128,2048]{1,0:T(8,128)(2,1)}, u32[]{:S(2)}, u32[]{:S(2)}) collective-permute-start(bf16[128,2048]{1,0:T(8,128)(2,1)S(1)} %get-tuple-element.287), channel_id=1, source_target_pairs={{0,4},{1,5},{4,0},{5,1},{2,6},{3,7},{6,2},{7,3},{8,12},{9,13},{12,... | collective-permute-start | bytes 1572872 | tf_op jit(solution)/shard_map/ppermute | solution.py:105
  225.9 17.8 %collective-permute-start.29 = (bf16[128,2048]{1,0:T(8,128)(2,1)S(1)}, bf16[128,2048]{1,0:T(8,128)(2,1)S(1)}, u32[]{:S(2)}, u32[]{:S(2)}) collective-permute-start(bf16[128,2048]{1,0:T(8,128)(2,1)S(1)} %multiply_convert_fusion.1), channel_id=1, source_target_pairs={{0,8},{8,16},{16,24},{24,0},{1,9},{9,17},{17,25},{25,1},{2,10},{10... | collective-permute-start | bytes 1572872 | tf_op jit(solution)/shard_map/rows_far1/ppermute | solution.py:190
  244.3 15.7 %collective-permute-start.31 = (bf16[2,32,2048]{2,1,0:T(8,128)(2,1)S(1)}, bf16[2,32,2048]{2,1,0:T(8,128)(2,1)S(1)}, u32[]{:S(2)}, u32[]{:S(2)}) collective-permute-start(bf16[2,32,2048]{2,1,0:T(8,128)(2,1)S(1)} %bitcast.713), channel_id=1, source_target_pairs={{0,4},{1,5},{4,0},{5,1},{2,6},{3,7},{6,2},{7,3},{8,12},{9,13},{12,... | collective-permute-start | bytes 786440 | tf_op jit(solution)/shard_map/rows_out1/ppermute | solution.py:198
  245.5 14.5 %collective-permute-start.32 = (bf16[2,32,2048]{2,1,0:T(8,128)(2,1)S(1)}, bf16[2,32,2048]{2,1,0:T(8,128)(2,1)S(1)}, u32[]{:S(2)}, u32[]{:S(2)}) collective-permute-start(bf16[2,32,2048]{2,1,0:T(8,128)(2,1)S(1)} %bitcast.710), channel_id=1, source_target_pairs={{0,5},{1,4},{4,1},{5,0},{2,7},{3,6},{6,3},{7,2},{8,13},{9,12},{12,... | collective-permute-start | bytes 786440 | tf_op jit(solution)/shard_map/rows_out1/ppermute | solution.py:198
  247.8 15.3 %collective-permute-start.34 = (bf16[128,2048]{1,0:T(8,128)(2,1)S(1)}, bf16[128,2048]{1,0:T(8,128)(2,1)S(1)}, u32[]{:S(2)}, u32[]{:S(2)}) collective-permute-start(bf16[128,2048]{1,0:T(8,128)(2,1)S(1)} %collective-permute-done.29), channel_id=1, source_target_pairs={{0,8},{8,16},{16,24},{24,0},{1,9},{9,17},{17,25},{25,1},{2,10},{10... | collective-permute-start | bytes 1572872 | tf_op jit(solution)/shard_map/rows_far2/ppermute | solution.py:190
  263.6 14.3 %collective-permute-start.36 = (bf16[2,32,2048]{2,1,0:T(8,128)(2,1)S(1)}, bf16[2,32,2048]{2,1,0:T(8,128)(2,1)S(1)}, u32[]{:S(2)}, u32[]{:S(2)}) collective-permute-start(bf16[2,32,2048]{2,1,0:T(8,128)(2,1)S(1)} %bitcast.714), channel_id=1, source_target_pairs={{0,4},{1,5},{4,0},{5,1},{2,6},{3,7},{6,2},{7,3},{8,12},{9,13},{12,... | collective-permute-start | bytes 786440 | tf_op jit(solution)/shard_map/rows_out2/ppermute | solution.py:198
  267.2 13.9 %collective-permute-start.39 = (bf16[128,2048]{1,0:T(8,128)(2,1)S(1)}, bf16[128,2048]{1,0:T(8,128)(2,1)S(1)}, u32[]{:S(2)}, u32[]{:S(2)}) collective-permute-start(bf16[128,2048]{1,0:T(8,128)(2,1)S(1)} %collective-permute-done.34), channel_id=1, source_target_pairs={{0,8},{8,16},{16,24},{24,0},{1,9},{9,17},{17,25},{25,1},{2,10},{10... | collective-permute-start | bytes 1572872 | tf_op jit(solution)/shard_map/rows_far3/ppermute | solution.py:190
  278.9 17.6 %collective-permute-start.44 = (bf16[2,2,32,2176]{3,2,1,0:T(8,128)(2,1)S(1)}, bf16[2,2,32,2176]{3,2,1,0:T(8,128)(2,1)S(1)}, u32[]{:S(2)}, u32[]{:S(2)}) collective-permute-start(bf16[2,2,32,2176]{3,2,1,0:T(8,128)(2,1)S(1)} %get-tuple-element.336), channel_id=1, source_target_pairs={{0,2},{2,0},{1,3},{3,1},{4,6},{6,4},{5,7},{7,5},{8,10},{10,8},{9,1... | collective-permute-start | bytes 1671176 | tf_op jit(solution)/shard_map/rows_back1/ppermute | solution.py:87
  281.7 13.8 %collective-permute-start.41 = (bf16[2,32,2048]{2,1,0:T(8,128)(2,1)S(1)}, bf16[2,32,2048]{2,1,0:T(8,128)(2,1)S(1)}, u32[]{:S(2)}, u32[]{:S(2)}) collective-permute-start(bf16[2,32,2048]{2,1,0:T(8,128)(2,1)S(1)} %bitcast.716), channel_id=1, source_target_pairs={{0,4},{1,5},{4,0},{5,1},{2,6},{3,7},{6,2},{7,3},{8,12},{9,13},{12,... | collective-permute-start | bytes 786440 | tf_op jit(solution)/shard_map/rows_out3/ppermute | solution.py:198
  296.4 14.4 %collective-permute-start.48 = (bf16[2,2,32,2176]{3,2,1,0:T(8,128)(2,1)S(1)}, bf16[2,2,32,2176]{3,2,1,0:T(8,128)(2,1)S(1)}, u32[]{:S(2)}, u32[]{:S(2)}) collective-permute-start(bf16[2,2,32,2176]{3,2,1,0:T(8,128)(2,1)S(1)} %get-tuple-element.330), channel_id=1, source_target_pairs={{0,2},{2,0},{1,3},{3,1},{4,6},{6,4},{5,7},{7,5},{8,10},{10,8},{9,1... | collective-permute-start | bytes 1671176 | tf_op jit(solution)/shard_map/rows_back2/ppermute | solution.py:87
  296.7 16.1 %collective-permute-start.47 = (bf16[2,32,2176]{2,1,0:T(8,128)(2,1)S(1)}, bf16[2,32,2176]{2,1,0:T(8,128)(2,1)S(1)}, u32[]{:S(2)}, u32[]{:S(2)}) collective-permute-start(bf16[2,32,2176]{2,1,0:T(8,128)(2,1)S(1)} %get-tuple-element.332), channel_id=1, source_target_pairs={{0,5},{1,4},{4,1},{5,0},{2,7},{3,6},{6,3},{7,2},{8,13},{9,12},{12,... | collective-permute-start | bytes 835592 | tf_op jit(solution)/shard_map/rows_back1/ppermute | solution.py:105
  297.8 16.5 %collective-permute-start.45 = (bf16[2,32,2176]{2,1,0:T(8,128)(2,1)S(1)}, bf16[2,32,2176]{2,1,0:T(8,128)(2,1)S(1)}, u32[]{:S(2)}, u32[]{:S(2)}) collective-permute-start(bf16[2,32,2176]{2,1,0:T(8,128)(2,1)S(1)} %get-tuple-element.334), channel_id=1, source_target_pairs={{0,1},{1,0},{4,5},{5,4},{2,3},{3,2},{6,7},{7,6},{8,9},{9,8},{12,13... | collective-permute-start | bytes 835592 | tf_op jit(solution)/shard_map/rows_back1/ppermute | solution.py:105
  299.4 15.8 %collective-permute-start.46 = (bf16[2,32,2176]{2,1,0:T(8,128)(2,1)S(1)}, bf16[2,32,2176]{2,1,0:T(8,128)(2,1)S(1)}, u32[]{:S(2)}, u32[]{:S(2)}) collective-permute-start(bf16[2,32,2176]{2,1,0:T(8,128)(2,1)S(1)} %get-tuple-element.335), channel_id=1, source_target_pairs={{0,4},{1,5},{4,0},{5,1},{2,6},{3,7},{6,2},{7,3},{8,12},{9,13},{12,... | collective-permute-start | bytes 835592 | tf_op jit(solution)/shard_map/rows_back1/ppermute | solution.py:105
  310.7 20.0 %collective-permute-start.56 = (bf16[2,2,32,2176]{3,2,1,0:T(8,128)(2,1)S(1)}, bf16[2,2,32,2176]{3,2,1,0:T(8,128)(2,1)S(1)}, u32[]{:S(2)}, u32[]{:S(2)}) collective-permute-start(bf16[2,2,32,2176]{3,2,1,0:T(8,128)(2,1)S(1)} %get-tuple-element.318), channel_id=1, source_target_pairs={{0,2},{2,0},{1,3},{3,1},{4,6},{6,4},{5,7},{7,5},{8,10},{10,8},{9,1... | collective-permute-start | bytes 1671176 | tf_op jit(solution)/shard_map/rows_back3/ppermute | solution.py:87
  312.8 14.0 %collective-permute-start.49 = (bf16[2,32,2176]{2,1,0:T(8,128)(2,1)S(1)}, bf16[2,32,2176]{2,1,0:T(8,128)(2,1)S(1)}, u32[]{:S(2)}, u32[]{:S(2)}) collective-permute-start(bf16[2,32,2176]{2,1,0:T(8,128)(2,1)S(1)} %get-tuple-element.328), channel_id=1, source_target_pairs={{0,1},{1,0},{4,5},{5,4},{2,3},{3,2},{6,7},{7,6},{8,9},{9,8},{12,13... | collective-permute-start | bytes 835592 | tf_op jit(solution)/shard_map/rows_back2/ppermute | solution.py:105
  327.4 19.1 %collective-permute-start.61 = (bf16[128,2176]{1,0:T(8,128)(2,1)S(1)}, bf16[128,2176]{1,0:T(8,128)(2,1)S(1)}, u32[]{:S(2)}, u32[]{:S(2)}) collective-permute-start(bf16[128,2176]{1,0:T(8,128)(2,1)S(1)} %fusion.7), channel_id=1, source_target_pairs={{0,24},{8,0},{16,8},{24,16},{1,25},{9,1},{17,9},{25,17},{2,26},{10... | collective-permute-start | bytes 1671176 | tf_op jit(solution)/shard_map/partial_far/ppermute | solution.py:190
  332.0 14.0 %collective-permute-start.58 = (bf16[2,32,2176]{2,1,0:T(8,128)(2,1)S(1)}, bf16[2,32,2176]{2,1,0:T(8,128)(2,1)S(1)}, u32[]{:S(2)}, u32[]{:S(2)}) collective-permute-start(bf16[2,32,2176]{2,1,0:T(8,128)(2,1)S(1)} %get-tuple-element.316), channel_id=1, source_target_pairs={{0,4},{1,5},{4,0},{5,1},{2,6},{3,7},{6,2},{7,3},{8,12},{9,13},{12,... | collective-permute-start | bytes 835592 | tf_op jit(solution)/shard_map/rows_back3/ppermute | solution.py:105
  334.5 16.0 %collective-permute-start.52 = (bf16[2,2,32,2176]{3,2,1,0:T(8,128)(2,1)S(1)}, bf16[2,2,32,2176]{3,2,1,0:T(8,128)(2,1)S(1)}, u32[]{:S(2)}, u32[]{:S(2)}) collective-permute-start(bf16[2,2,32,2176]{3,2,1,0:T(8,128)(2,1)S(1)} %get-tuple-element.324), channel_id=1, source_target_pairs={{0,2},{2,0},{1,3},{3,1},{4,6},{6,4},{5,7},{7,5},{8,10},{10,8},{9,1... | collective-permute-start | bytes 1671176 | tf_op jit(solution)/shard_map/rows_back0/ppermute | solution.py:87
  346.4 17.6 %collective-permute-start.60 = (bf16[128,2176]{1,0:T(8,128)(2,1)S(1)}, bf16[128,2176]{1,0:T(8,128)(2,1)S(1)}, u32[]{:S(2)}, u32[]{:S(2)}) collective-permute-start(bf16[128,2176]{1,0:T(8,128)(2,1)S(1)} %fusion.8), channel_id=1, source_target_pairs={{0,8},{8,16},{16,24},{24,0},{1,9},{9,17},{17,25},{25,1},{2,10},{10... | collective-permute-start | bytes 1671176 | tf_op jit(solution)/shard_map/partial_far/ppermute | solution.py:190
  346.6 25.2 %collective-permute-start.62 = (bf16[128,2176]{1,0:T(8,128)(2,1)S(1)}, bf16[128,2176]{1,0:T(8,128)(2,1)S(1)}, u32[]{:S(2)}, u32[]{:S(2)}) collective-permute-start(bf16[128,2176]{1,0:T(8,128)(2,1)S(1)} %add_convert_fusion), channel_id=1, source_target_pairs={{0,24},{8,0},{16,8},{24,16},{1,25},{9,1},{17,9},{25,17},{2,26},{10... | collective-permute-start | bytes 1671176 | tf_op jit(solution)/shard_map/partial_far/ppermute | solution.py:190
  374.0 22.2 %collective-permute-start.65 = (bf16[128,2048]{1,0:T(8,128)(2,1)S(1)}, bf16[128,2048]{1,0:T(8,128)(2,1)S(1)}, u32[]{:S(2)}, u32[]{:S(2)}) collective-permute-start(bf16[128,2048]{1,0:T(8,128)(2,1)S(1)} %fusion.47), channel_id=1, source_target_pairs={{0,5},{1,4},{4,1},{5,0},{2,7},{3,6},{6,3},{7,2},{8,13},{9,12},{12,... | collective-permute-start | bytes 1572872 | tf_op jit(solution)/shard_map/ppermute | solution.py:117
  375.5 22.9 %collective-permute-start.64 = (bf16[128,2048]{1,0:T(8,128)(2,1)S(1)}, bf16[128,2048]{1,0:T(8,128)(2,1)S(1)}, u32[]{:S(2)}, u32[]{:S(2)}) collective-permute-start(bf16[128,2048]{1,0:T(8,128)(2,1)S(1)} %fusion.47), channel_id=1, source_target_pairs={{0,4},{1,5},{4,0},{5,1},{2,6},{3,7},{6,2},{7,3},{8,12},{9,13},{12,... | collective-permute-start | bytes 1572872 | tf_op jit(solution)/shard_map/ppermute | solution.py:117
  376.0 22.3 %collective-permute-start.63 = (bf16[128,2048]{1,0:T(8,128)(2,1)S(1)}, bf16[128,2048]{1,0:T(8,128)(2,1)S(1)}, u32[]{:S(2)}, u32[]{:S(2)}) collective-permute-start(bf16[128,2048]{1,0:T(8,128)(2,1)S(1)} %fusion.47), channel_id=1, source_target_pairs={{0,1},{1,0},{4,5},{5,4},{2,3},{3,2},{6,7},{7,6},{8,9},{9,8},{12,13... | collective-permute-start | bytes 1572872 | tf_op jit(solution)/shard_map/ppermute | solution.py:117
  410.3 24.4 %collective-permute-start.67 = (bf16[128,2048]{1,0:T(8,128)(2,1)}, bf16[128,2048]{1,0:T(8,128)(2,1)S(1)}, u32[]{:S(2)}, u32[]{:S(2)}) collective-permute-start(bf16[128,2048]{1,0:T(8,128)(2,1)} %get-tuple-element.278), channel_id=1, source_target_pairs={{0,1},{1,0},{4,5},{5,4},{2,3},{3,2},{6,7},{7,6},{8,9},{9,8},{12,13... | collective-permute-start | bytes 1572872 | tf_op jit(solution)/shard_map/ppermute | solution.py:105
  410.8 25.0 %collective-permute-start.69 = (bf16[128,2048]{1,0:T(8,128)(2,1)}, bf16[128,2048]{1,0:T(8,128)(2,1)S(1)}, u32[]{:S(2)}, u32[]{:S(2)}) collective-permute-start(bf16[128,2048]{1,0:T(8,128)(2,1)} %get-tuple-element.279), channel_id=1, source_target_pairs={{0,5},{1,4},{4,1},{5,0},{2,7},{3,6},{6,3},{7,2},{8,13},{9,12},{12,... | collective-permute-start | bytes 1572872 | tf_op jit(solution)/shard_map/ppermute | solution.py:105
  412.5 24.8 %collective-permute-start.68 = (bf16[128,2048]{1,0:T(8,128)(2,1)}, bf16[128,2048]{1,0:T(8,128)(2,1)}, u32[]{:S(2)}, u32[]{:S(2)}) collective-permute-start(bf16[128,2048]{1,0:T(8,128)(2,1)} %get-tuple-element.280), channel_id=1, source_target_pairs={{0,4},{1,5},{4,0},{5,1},{2,6},{3,7},{6,2},{7,3},{8,12},{9,13},{12,... | collective-permute-start | bytes 1572872 | tf_op jit(solution)/shard_map/ppermute | solution.py:105
  449.2 16.8 %collective-permute-start.70 = (bf16[8,128,1280]{2,1,0:T(8,128)(2,1)}, bf16[8,128,1280]{2,1,0:T(8,128)(2,1)}, u32[]{:S(2)}, u32[]{:S(2)}) collective-permute-start(bf16[8,128,1280]{2,1,0:T(8,128)(2,1)} %fusion.9), channel_id=1, source_target_pairs={{0,2},{2,0},{1,3},{3,1},{4,6},{6,4},{5,7},{7,5},{8,10},{10,8},{9,1... | collective-permute-start | bytes 7864328 | tf_op jit(solution)/shard_map/ppermute | solution.py:87
  450.4 66.1 %all-to-all-start.3 = ((bf16[8,4,32,2048]{3,2,1,0:T(8,128)(2,1)}), bf16[8,4,32,2048]{3,2,1,0:T(8,128)(2,1)}, u32[]{:S(2)}, u32[]{:S(2)}) async-start(bf16[8,4,32,2048]{3,2,1,0:T(8,128)(2,1)} %pad_maximum_fusion.3), calls=%async_computation.3 | async-start | bytes 8388608 | tf_op jit(solution)/shard_map/all_to_all | solution.py:96
  456.5 16.6 %collective-permute-start.72 = (bf16[128,2048]{1,0:T(8,128)(2,1)S(1)}, bf16[128,2048]{1,0:T(8,128)(2,1)S(1)}, u32[]{:S(2)}, u32[]{:S(2)}) collective-permute-start(bf16[128,2048]{1,0:T(8,128)(2,1)S(1)} %get-tuple-element.276), channel_id=1, source_target_pairs={{0,8},{8,16},{16,24},{24,0},{1,9},{9,17},{17,25},{25,1},{2,10},{10... | collective-permute-start | bytes 1572872 | tf_op jit(solution)/shard_map/ppermute | solution.py:190
  456.6 25.6 %collective-permute-start.71 = (bf16[128,2048]{1,0:T(8,128)(2,1)S(1)}, bf16[128,2048]{1,0:T(8,128)(2,1)S(1)}, u32[]{:S(2)}, u32[]{:S(2)}) collective-permute-start(bf16[128,2048]{1,0:T(8,128)(2,1)S(1)} %get-tuple-element.277), channel_id=1, source_target_pairs={{0,24},{8,0},{16,8},{24,16},{1,25},{9,1},{17,9},{25,17},{2,26},{10... | collective-permute-start | bytes 1572872 | tf_op jit(solution)/shard_map/ppermute | solution.py:190
  482.3 14.9 %collective-permute-start.86 = (bf16[128,2048]{1,0:T(8,128)(2,1)S(1)}, bf16[128,2048]{1,0:T(8,128)(2,1)S(1)}, u32[]{:S(2)}, u32[]{:S(2)}) collective-permute-start(bf16[128,2048]{1,0:T(8,128)(2,1)S(1)} %fusion.58), channel_id=1, source_target_pairs={{0,24},{8,0},{16,8},{24,16},{1,25},{9,1},{17,9},{25,17},{2,26},{10... | collective-permute-start | bytes 1572872 | tf_op jit(solution)/shard_map/ppermute | solution.py:190
  485.4 25.5 %collective-permute-start.74 = (bf16[256,1280]{1,0:T(8,128)(2,1)S(1)}, bf16[256,1280]{1,0:T(8,128)(2,1)S(1)}, u32[]{:S(2)}, u32[]{:S(2)}) collective-permute-start(bf16[256,1280]{1,0:T(8,128)(2,1)S(1)} %get-tuple-element.271), channel_id=1, source_target_pairs={{0,24},{8,0},{16,8},{24,16},{1,25},{9,1},{17,9},{25,17},{2,26},{10... | collective-permute-start | bytes 1966088 | tf_op jit(solution)/shard_map/ppermute | solution.py:190
  488.3 53.8 %collective-permute-start.78 = (bf16[128,2048]{1,0:T(8,128)(2,1)}, bf16[128,2048]{1,0:T(8,128)(2,1)}, u32[]{:S(2)}, u32[]{:S(2)}) collective-permute-start(bf16[128,2048]{1,0:T(8,128)(2,1)} %get-tuple-element.272), channel_id=1, source_target_pairs={{0,5},{1,4},{4,1},{5,0},{2,7},{3,6},{6,3},{7,2},{8,13},{9,12},{12,... | collective-permute-start | bytes 1572872 | tf_op jit(solution)/shard_map/ppermute | solution.py:105
  490.8 51.3 %collective-permute-start.77 = (bf16[128,2048]{1,0:T(8,128)(2,1)}, bf16[128,2048]{1,0:T(8,128)(2,1)}, u32[]{:S(2)}, u32[]{:S(2)}) collective-permute-start(bf16[128,2048]{1,0:T(8,128)(2,1)} %get-tuple-element.273), channel_id=1, source_target_pairs={{0,4},{1,5},{4,0},{5,1},{2,6},{3,7},{6,2},{7,3},{8,12},{9,13},{12,... | collective-permute-start | bytes 1572872 | tf_op jit(solution)/shard_map/ppermute | solution.py:105
  491.3 50.8 %collective-permute-start.76 = (bf16[128,2048]{1,0:T(8,128)(2,1)}, bf16[128,2048]{1,0:T(8,128)(2,1)}, u32[]{:S(2)}, u32[]{:S(2)}) collective-permute-start(bf16[128,2048]{1,0:T(8,128)(2,1)} %get-tuple-element.274), channel_id=1, source_target_pairs={{0,1},{1,0},{4,5},{5,4},{2,3},{3,2},{6,7},{7,6},{8,9},{9,8},{12,13... | collective-permute-start | bytes 1572872 | tf_op jit(solution)/shard_map/ppermute | solution.py:105
  497.2 30.0 %collective-permute-start.73 = (bf16[256,1280]{1,0:T(8,128)(2,1)}, bf16[256,1280]{1,0:T(8,128)(2,1)}, u32[]{:S(2)}, u32[]{:S(2)}) collective-permute-start(bf16[256,1280]{1,0:T(8,128)(2,1)} %get-tuple-element.270), channel_id=1, source_target_pairs={{0,8},{8,16},{16,24},{24,0},{1,9},{9,17},{17,25},{25,1},{2,10},{10... | collective-permute-start | bytes 1966088 | tf_op jit(solution)/shard_map/ppermute | solution.py:190
  511.9 28.1 %collective-permute-start.75 = (bf16[256,1280]{1,0:T(8,128)(2,1)}, bf16[256,1280]{1,0:T(8,128)(2,1)S(1)}, u32[]{:S(2)}, u32[]{:S(2)}) collective-permute-start(bf16[256,1280]{1,0:T(8,128)(2,1)} %fusion.15), channel_id=1, source_target_pairs={{0,24},{8,0},{16,8},{24,16},{1,25},{9,1},{17,9},{25,17},{2,26},{10... | collective-permute-start | bytes 1966088 | tf_op jit(solution)/shard_map/ppermute | solution.py:190
  527.2 26.9 %collective-permute-start.80 = (bf16[128,2048]{1,0:T(8,128)(2,1)S(1)}, bf16[128,2048]{1,0:T(8,128)(2,1)S(1)}, u32[]{:S(2)}, u32[]{:S(2)}) collective-permute-start(bf16[128,2048]{1,0:T(8,128)(2,1)S(1)} %convolution_convert_fusion.11), channel_id=1, source_target_pairs={{0,24},{8,0},{16,8},{24,16},{1,25},{9,1},{17,9},{25,17},{2,26},{10... | collective-permute-start | bytes 1572872 | tf_op jit(solution)/shard_map/ppermute | solution.py:190
  540.0 23.6 %collective-permute-start.79 = (bf16[128,2048]{1,0:T(8,128)(2,1)S(1)}, bf16[128,2048]{1,0:T(8,128)(2,1)S(1)}, u32[]{:S(2)}, u32[]{:S(2)}) collective-permute-start(bf16[128,2048]{1,0:T(8,128)(2,1)S(1)} %convolution_convert_fusion.13), channel_id=1, source_target_pairs={{0,8},{8,16},{16,24},{24,0},{1,9},{9,17},{17,25},{25,1},{2,10},{10... | collective-permute-start | bytes 1572872 | tf_op jit(solution)/shard_map/ppermute | solution.py:190
  554.4 19.3 %collective-permute-start.81 = (bf16[128,2048]{1,0:T(8,128)(2,1)S(1)}, bf16[128,2048]{1,0:T(8,128)(2,1)S(1)}, u32[]{:S(2)}, u32[]{:S(2)}) collective-permute-start(bf16[128,2048]{1,0:T(8,128)(2,1)S(1)} %add_convert_fusion.2), channel_id=1, source_target_pairs={{0,24},{8,0},{16,8},{24,16},{1,25},{9,1},{17,9},{25,17},{2,26},{10... | collective-permute-start | bytes 1572872 | tf_op jit(solution)/shard_map/ppermute | solution.py:190
  574.7 17.4 %collective-permute-start.82 = (bf16[128,2048]{1,0:T(8,128)(2,1)S(1)}, bf16[128,2048]{1,0:T(8,128)(2,1)S(1)}, u32[]{:S(2)}, u32[]{:S(2)}) collective-permute-start(bf16[128,2048]{1,0:T(8,128)(2,1)S(1)} %add_convert_fusion.1), channel_id=1, source_target_pairs={{0,1},{1,0},{2,3},{3,2},{4,5},{5,4},{6,7},{7,6},{8,9},{9,8},{10,11... | collective-permute-start | bytes 1572872 | tf_op jit(solution)/shard_map/ppermute | solution.py:87
  576.8 16.5 %all-to-all-start.4 = ((f32[32,24,128]{2,1,0:T(8,128)}), f32[32,24,128]{2,1,0:T(8,128)S(1)}, u32[]{:S(2)}, u32[]{:S(2)}) async-start(f32[32,24,128]{2,1,0:T(8,128)} %bitcast.298), calls=%async_computation.4 | async-start | bytes 786432 | tf_op jit(solution)/shard_map/all_to_all | solution.py:96
  (88 other events, 569.7 us)

commit v10 on v9

--- a/solution.py
+++ b/solution.py
@@ -724,7 +724,6 @@
     gate_grad = mm(total[:, D:].astype(BF), spread)
     mean_term = jnp.sum(gate_probs * gate_grad, axis=1, keepdims=True)
     logit_grad = (gate_probs * (gate_grad - mean_term)).astype(BF)
-    router_grad = mm_tn(ffn_in, logit_grad)
     ffn_in_grad = from_experts + mm_nt(logit_grad, router_full)
     resid_part, gain_ffn_grad = ffn_back(ffn_in_grad)
     resid_low = (cot_rows + resid_part).astype(BF)
@@ -783,7 +782,8 @@
     qkv_grad = far_end(qkv_parts, qkv_found, far_count)
     normed_found = quad_parts(normed_partial.reshape(4, TOK_DEV, D))
     qkv_grad, *normed_found = tie(qkv_grad, *normed_found)
-    normed_grad = sum_parts(normed_found)
+    normed_grad, logit_late = tie(sum_parts(normed_found), logit_grad)
+    router_grad = mm_tn(ffn_in, logit_late)
     normed_grad, out_sum = tie(normed_grad, out_sum)
     final_rows = (residual + out_sum).astype(BF)
     final_pair = jnp.concatenate(

time: 603 us -> 602 us (level)
  waiting for transfers between devices: 245 us -> 235 us
    ppermute x24, waiting for transfers between devices: 123 us -> 115 us  [far_shift(): lax.ppermute(value, FAR_AXIS, [(i, (i + step) % count) for i in range(cou...]
    unnamed x138 -> x146, local copies, waits for them, and re-layouts: 14.4 us -> 15.1 us
  transfers between devices with their start and end apart: 92 -> 92, of which waited for: 39 -> 39; matrix products, arithmetic and copies ran while one was open for 17% -> 18% of each run, Pallas kernels for 15% -> 15%
where the time goes in v10:
time: 602 us; the launch traced here: 594 us
  waiting for transfers between devices  235 us (39%)
  starting transfers between devices  127 us (21%)
  Pallas kernels  86.5 us (14%)
  local copies, waits for them, and re-layouts  50.9 us (8%)
  other arithmetic  46.5 us (8%)
  matrix products  44.9 us (7%)
    ppermute x24, waiting for transfers between devices, far_shift(): lax.ppermute(value, FAR_AXIS, [(i, (i + step) % count) for i in range(cou...  115 us
    ppermute x30, waiting for transfers between devices, quad_send(): return lax.ppermute(block, HEAD_AXES, [(i, i ^ step) for i in range(4)])  94.6 us
    dot_general x30, matrix products, dot(): lax.dot_general(left, right, (dims, ((), ())), preferred_element_type=F32)  43.5 us
    ppermute x24, starting transfers between devices, far_shift(): lax.ppermute(value, FAR_AXIS, [(i, (i + step) % count) for i in range(cou...  41.2 us
    pallas_call x4, Pallas kernels, expert_chunk(): pl.pallas_call(expert_kernel, grid_spec=pltpu.PrefetchScalarGridSpec(num_...  40 us
    ppermute x30, starting transfers between devices, quad_send(): return lax.ppermute(block, HEAD_AXES, [(i, i ^ step) for i in range(4)])  36 us
    all_to_all x5, starting transfers between devices, exchange(): return lax.all_to_all(value, axes, split_axis=0, concat_axis=0, tiled=True)  21.8 us
    pallas_call x1, Pallas kernels, expert_grads(): pl.pallas_call(functools.partial(expert_grad_kernel, count), grid=(D // t...  18.7 us
  transfers between devices with their start and end apart: 92, of which 39 were waited for; matrix products, arithmetic and copies ran while one was open for 18% of the time, Pallas kernels for 15%

profile of v10, /device:TPU:0, one launch (start us, length us, event | category | flops | bytes accessed | tf_op | source)
XLA Modules:
  0.0 593.8 jit_solution(3268518982058167941)
XLA Ops:
  1.3 3.0 collective-permute-start
  17.7 2.5 collective-permute-start.3
  24.8 2.9 all-to-all-start
  29.5 2.7 collective-permute-start.6
  39.9 13.6 %collective-permute-done.7 = bf16[256,1280]{1,0:T(8,128)(2,1)} collective-permute-done((bf16[256,1280]{1,0:T(8,128)(2,1)}, bf16[256,1280]{1,0:T(8,128)(2,1)}, u32[]{:S(2)}, u32[]{:S(2)}) %collective-permute-start.7) | collective-permute-done | bytes 655392 | tf_op jit(solution)/shard_map/ppermute | solution.py:190
  56.0 24.1 %collective-permute-done.8 = bf16[256,1280]{1,0:T(8,128)(2,1)S(1)} collective-permute-done((bf16[256,1280]{1,0:T(8,128)(2,1)}, bf16[256,1280]{1,0:T(8,128)(2,1)S(1)}, u32[]{:S(2)}, u32[]{:S(2)}) %collective-permute-start.8) | collective-permute-done | bytes 655392 | tf_op jit(solution)/shard_map/ppermute | solution.py:190
  83.8 2.3 convolution_convert_fusion.2
  88.3 4.3 collective-permute-done.4
  98.3 4.3 fusion.170.query_ref.key_ref.value_ref
  102.7 4.3 all-to-all-start.1
  108.9 3.5 collective-permute-done.13
  116.2 2.7 dynamic-slice_bitcast_fusion.18
  118.9 2.3 collective-permute-start.17
  125.0 10.9 %attend.1 = bf16[512,1024]{1,0:T(8,128)(2,1)} custom-call(f32[512,1280]{1,0:T(8,128)} %fusion.170.query_ref.key_ref.value_ref, f32[512,1280]{1,0:T(8,128)} %fusion.170.query_ref.key_ref.value_ref, f32[512,1280]{1,0:T(8,128)} %fusion.170.query_ref.key_ref.value_ref, f32[512,128]{1,0:T(8,128)} %get-tuple-element.443.cos_ref, ...), custom_call_target="tpu_custom_call" | custom-call | flops 1048576 | bytes 1048576 | tf_op jit(solution)/shard_map/attend/pallas_call | solution.py:446
  135.9 13.1 %collective-permute-done.17 = bf16[128,2048]{1,0:T(8,128)(2,1)S(1)} collective-permute-done((bf16[128,2048]{1,0:T(8,128)(2,1)}, bf16[128,2048]{1,0:T(8,128)(2,1)S(1)}, u32[]{:S(2)}, u32[]{:S(2)}) %collective-permute-start.17) | collective-permute-done | bytes 524320 | tf_op jit(solution)/shard_map/ppermute | solution.py:105
  149.0 9.5 %collective-permute-done.16 = bf16[128,2048]{1,0:T(8,128)(2,1)S(1)} collective-permute-done((bf16[128,2048]{1,0:T(8,128)(2,1)}, bf16[128,2048]{1,0:T(8,128)(2,1)S(1)}, u32[]{:S(2)}, u32[]{:S(2)}) %collective-permute-start.16) | collective-permute-done | bytes 524320 | tf_op jit(solution)/shard_map/ppermute | solution.py:105
  161.8 3.0 collective-permute-start.22
  168.5 4.3 collective-permute-done.23
  172.9 6.3 %all-to-all-start.2 = ((bf16[32,32,768]{2,1,0:T(8,128)(2,1)}), bf16[32,32,768]{2,1,0:T(8,128)(2,1)}, u32[]{:S(2)}, u32[]{:S(2)}) async-start(bf16[32,32,768]{2,1,0:T(8,128)(2,1)} %bitcast.655), calls=%async_computation.2 | async-start | bytes 3145728 | tf_op jit(solution)/shard_map/all_to_all | solution.py:96
  182.3 2.4 convolution_convert_fusion.3
  191.6 17.5 %collective-permute-done.19 = bf16[128,2048]{1,0:T(8,128)(2,1)} collective-permute-done((bf16[128,2048]{1,0:T(8,128)(2,1)S(1)}, bf16[128,2048]{1,0:T(8,128)(2,1)}, u32[]{:S(2)}, u32[]{:S(2)}) %collective-permute-start.19) | collective-permute-done | bytes 524320 | tf_op jit(solution)/shard_map/ppermute | solution.py:105
  209.1 13.2 %collective-permute-done.21 = bf16[128,2048]{1,0:T(8,128)(2,1)} collective-permute-done((bf16[128,2048]{1,0:T(8,128)(2,1)S(1)}, bf16[128,2048]{1,0:T(8,128)(2,1)}, u32[]{:S(2)}, u32[]{:S(2)}) %collective-permute-start.21) | collective-permute-done | bytes 524320 | tf_op jit(solution)/shard_map/ppermute | solution.py:105
  222.3 2.4 multiply_reduce_fusion.3
  229.3 2.6 collective-permute-start.27
  231.9 2.7 pad_maximum_fusion.2
  235.0 6.7 %collective-permute-done.26 = bf16[2,32,2048]{2,1,0:T(8,128)(2,1)S(1)} collective-permute-done((bf16[2,32,2048]{2,1,0:T(8,128)(2,1)S(1)}, bf16[2,32,2048]{2,1,0:T(8,128)(2,1)S(1)}, u32[]{:S(2)}, u32[]{:S(2)}) %collective-permute-start.26) | collective-permute-done | bytes 262176 | tf_op jit(solution)/shard_map/rows_out0/ppermute | solution.py:198
  249.4 10.0 %expert_chunk.4 = (bf16[256,768]{1,0:T(8,128)(2,1)S(1)}, bf16[256,768]{1,0:T(8,128)(2,1)S(1)}, bf16[256,768]{1,0:T(8,128)(2,1)S(1)}, bf16[256,2048]{1,0:T(8,128)...) custom-call(s32[2]{0:T(128)S(1)} %pad_add_fusion.2.here_ref, bf16[256,2048]{1,0:T(8,128)(2,1)S(1)} %bitcast.609, ...), custom_call_target="tpu_custom_call" | custom-call | flops 1048576 | bytes 1048576 | tf_op jit(solution)/shard_map/expert_chunk/pallas_call | solution.py:276
  259.7 2.8 collective-permute-done.34
  267.4 10.0 %expert_chunk.5 = (bf16[256,768]{1,0:T(8,128)(2,1)S(1)}, bf16[256,768]{1,0:T(8,128)(2,1)S(1)}, bf16[256,768]{1,0:T(8,128)(2,1)S(1)}, bf16[256,2048]{1,0:T(8,128)...) custom-call(s32[2]{0:T(128)S(1)} %pad_add_fusion.2.here_ref, bf16[256,2048]{1,0:T(8,128)(2,1)S(1)} %bitcast.611, ...), custom_call_target="tpu_custom_call" | custom-call | flops 1048576 | bytes 1048576 | tf_op jit(solution)/shard_map/expert_chunk/pallas_call | solution.py:276
  284.9 10.0 %expert_chunk.6 = (bf16[256,768]{1,0:T(8,128)(2,1)S(1)}, bf16[256,768]{1,0:T(8,128)(2,1)S(1)}, bf16[256,768]{1,0:T(8,128)(2,1)S(1)}, bf16[256,2048]{1,0:T(8,128)...) custom-call(s32[2]{0:T(128)S(1)} %pad_add_fusion.2.here_ref, bf16[256,2048]{1,0:T(8,128)(2,1)S(1)} %bitcast.613, ...), custom_call_target="tpu_custom_call" | custom-call | flops 1048576 | bytes 1048576 | tf_op jit(solution)/shard_map/expert_chunk/pallas_call | solution.py:276
  299.9 10.1 %expert_chunk.7 = (bf16[256,768]{1,0:T(8,128)(2,1)S(1)}, bf16[256,768]{1,0:T(8,128)(2,1)S(1)}, bf16[256,768]{1,0:T(8,128)(2,1)S(1)}, bf16[256,2048]{1,0:T(8,128)...) custom-call(s32[2]{0:T(128)S(1)} %pad_add_fusion.2.here_ref, bf16[256,2048]{1,0:T(8,128)(2,1)S(1)} %bitcast.615, ...), custom_call_target="tpu_custom_call" | custom-call | flops 1048576 | bytes 1048576 | tf_op jit(solution)/shard_map/expert_chunk/pallas_call | solution.py:276
  315.0 6.6 %collective-permute-done.51 = bf16[2,32,2176]{2,1,0:T(8,128)(2,1)S(1)} collective-permute-done((bf16[2,32,2176]{2,1,0:T(8,128)(2,1)S(1)}, bf16[2,32,2176]{2,1,0:T(8,128)(2,1)S(1)}, u32[]{:S(2)}, u32[]{:S(2)}) %collective-permute-start.51) | collective-permute-done | bytes 278560 | tf_op jit(solution)/shard_map/rows_back2/ppermute | solution.py:105
  321.6 4.6 collective-permute-done.49
  326.8 3.3 collective-permute-start.61
  334.0 5.9 collective-permute-done.57
  339.9 5.5 collective-permute-done.58
  346.1 3.9 collective-permute-start.62
  354.0 5.7 collective-permute-done.53
  359.7 3.7 collective-permute-done.54
  363.4 7.8 %collective-permute-done.62 = bf16[128,2176]{1,0:T(8,128)(2,1)S(1)} collective-permute-done((bf16[128,2176]{1,0:T(8,128)(2,1)S(1)}, bf16[128,2176]{1,0:T(8,128)(2,1)S(1)}, u32[]{:S(2)}, u32[]{:S(2)}) %collective-permute-start.62) | collective-permute-done | bytes 557088 | tf_op jit(solution)/shard_map/partial_far/ppermute | solution.py:190
  377.0 18.7 %expert_grads.1 = f32[2048,2304]{1,0:T(8,128)} custom-call(bf16[256,2048]{1,0:T(8,128)(2,1)S(1)} %bitcast.610, bf16[256,2048]{1,0:T(8,128)(2,1)} %bitcast.612, bf16[256,2048]{1,0:T(8,128)(2,1)} %bitcast.614, bf16[256,2048]{1,0:T(8,128)(2,1)} %bitcast.616, bf16[256,2048]{1,0:T(8,128)(2,1)} %copy-done.3, bf16[256,2048]{1,0:T(8,128)(2,1)} %copy-done.4, ...), custom_call_target="tpu_custom_call" | custom-call | flops 1048576 | bytes 1048576 | tf_op jit(solution)/shard_map/expert_grads/pallas_call | solution.py:329
  399.3 2.4 convolution_convert_fusion.1
  403.9 3.3 convolution_convert_fusion.16.grad_ref
  417.2 16.9 %attend_back.1 = (bf16[512,1024]{1,0:T(8,128)(2,1)}, bf16[512,128]{1,0:T(8,128)(2,1)}, bf16[512,128]{1,0:T(8,128)(2,1)}, f32[1,128]{1,0:T(1,128)}, f32[1,128]{1,0:T(1,128)}) custom-call(f32[512,1280]{1,0:T(8,128)} %fusion.170.query_ref.key_ref.value_ref, f32[512,1280]{1,0:T(8,128)} %fusion.170.query_ref.key_ref.value_ref, ...), custom_call_target="tpu_custom_call" | custom-call | flops 1048576 | bytes 1048576 | tf_op jit(solution)/shard_map/attend_back/pallas_call | solution.py:461
  441.4 3.2 convolution_convert_fusion
  448.1 4.6 all-to-all-start.3
  454.2 3.8 collective-permute-start.71
  458.0 5.6 convolution_convert_fusion.4
  463.7 3.0 fusion
  466.7 4.1 collective-permute-done.72
  470.8 9.0 %collective-permute-done.71 = bf16[128,2048]{1,0:T(8,128)(2,1)S(1)} collective-permute-done((bf16[128,2048]{1,0:T(8,128)(2,1)S(1)}, bf16[128,2048]{1,0:T(8,128)(2,1)S(1)}, u32[]{:S(2)}, u32[]{:S(2)}) %collective-permute-start.71) | collective-permute-done | bytes 524320 | tf_op jit(solution)/shard_map/ppermute | solution.py:190
  485.3 2.5 collective-permute-start.78
  488.8 6.0 %collective-permute-done.86 = bf16[128,2048]{1,0:T(8,128)(2,1)S(1)} collective-permute-done((bf16[128,2048]{1,0:T(8,128)(2,1)S(1)}, bf16[128,2048]{1,0:T(8,128)(2,1)S(1)}, u32[]{:S(2)}, u32[]{:S(2)}) %collective-permute-start.86) | collective-permute-done | bytes 524320 | tf_op jit(solution)/shard_map/ppermute | solution.py:190
  497.5 11.0 %collective-permute-done.74 = bf16[256,1280]{1,0:T(8,128)(2,1)S(1)} collective-permute-done((bf16[256,1280]{1,0:T(8,128)(2,1)S(1)}, bf16[256,1280]{1,0:T(8,128)(2,1)S(1)}, u32[]{:S(2)}, u32[]{:S(2)}) %collective-permute-start.74) | collective-permute-done | bytes 655392 | tf_op jit(solution)/shard_map/ppermute | solution.py:190
  508.7 4.3 collective-permute-start.75
  513.0 3.7 fusion.161
  520.4 4.4 collective-permute-done.73
  527.0 10.8 %collective-permute-done.75 = bf16[256,1280]{1,0:T(8,128)(2,1)} collective-permute-done((bf16[256,1280]{1,0:T(8,128)(2,1)S(1)}, bf16[256,1280]{1,0:T(8,128)(2,1)}, u32[]{:S(2)}, u32[]{:S(2)}) %collective-permute-start.75) | collective-permute-done | bytes 655392 | tf_op jit(solution)/shard_map/ppermute | solution.py:190
  550.1 2.5 collective-permute-done.85
  558.1 2.4 collective-permute-start.81
  561.7 9.9 %collective-permute-done.81 = bf16[128,2048]{1,0:T(8,128)(2,1)S(1)} collective-permute-done((bf16[128,2048]{1,0:T(8,128)(2,1)S(1)}, bf16[128,2048]{1,0:T(8,128)(2,1)S(1)}, u32[]{:S(2)}, u32[]{:S(2)}) %collective-permute-start.81) | collective-permute-done | bytes 524320 | tf_op jit(solution)/shard_map/ppermute | solution.py:190
  575.4 3.7 all-to-all-start.4
  579.2 2.5 fusion.11
  581.6 7.7 %collective-permute-done.82 = bf16[128,2048]{1,0:T(8,128)(2,1)S(1)} collective-permute-done((bf16[128,2048]{1,0:T(8,128)(2,1)S(1)}, bf16[128,2048]{1,0:T(8,128)(2,1)S(1)}, u32[]{:S(2)}, u32[]{:S(2)}) %collective-permute-start.82) | collective-permute-done | bytes 524320 | tf_op jit(solution)/shard_map/ppermute | solution.py:87
  (489 shorter events, 187.8 us)
Async XLA Ops:
  1.3 16.4 %collective-permute-start = (s32[1,384]{1,0:T(1,128)S(1)}, s32[1,384]{1,0:T(1,128)S(1)}, u32[]{:S(2)}, u32[]{:S(2)}) collective-permute-start(s32[1,384]{1,0:T(1,128)S(1)} %pad_add_fusion), channel_id=1, source_target_pairs={{0,4},{4,0},{1,5},{5,1},{2,6},{6,2},{3,7},{7,3},{8,12},{12,8},{9,1... | collective-permute-start | bytes 4616 | tf_op jit(solution)/shard_map/ppermute | solution.py:87
  4.3 35.1 %collective-permute-start.11 = (bf16[128,2048]{1,0:T(8,128)(2,1)}, bf16[128,2048]{1,0:T(8,128)(2,1)}, u32[]{:S(2)}, u32[]{:S(2)}) collective-permute-start(bf16[128,2048]{1,0:T(8,128)(2,1)} %param.12), channel_id=1, source_target_pairs={{0,1},{1,0},{2,3},{3,2},{4,5},{5,4},{6,7},{7,6},{8,9},{9,8},{10,11... | collective-permute-start | bytes 1572872 | tf_op jit(solution)/shard_map/ppermute | solution.py:87
  5.8 80.3 %collective-permute-start.12 = (bf16[128,2048]{1,0:T(8,128)(2,1)}, bf16[128,2048]{1,0:T(8,128)(2,1)}, u32[]{:S(2)}, u32[]{:S(2)}) collective-permute-start(bf16[128,2048]{1,0:T(8,128)(2,1)} %param.14), channel_id=1, source_target_pairs={{0,8},{8,16},{16,24},{24,0},{1,9},{9,17},{17,25},{25,1},{2,10},{10... | collective-permute-start | bytes 1572872 | tf_op jit(solution)/shard_map/ppermute | solution.py:190
  11.5 17.9 %collective-permute-start.1 = (bf16[64,1280]{1,0:T(8,128)(2,1)S(1)}, bf16[64,1280]{1,0:T(8,128)(2,1)S(1)}, u32[]{:S(2)}, u32[]{:S(2)}) collective-permute-start(bf16[64,1280]{1,0:T(8,128)(2,1)S(1)} %bitcast.717), channel_id=1, source_target_pairs={{0,1},{1,0},{4,5},{5,4},{2,3},{3,2},{6,7},{7,6},{8,9},{9,8},{12,13... | collective-permute-start | bytes 491528 | tf_op jit(solution)/shard_map/ppermute | solution.py:105
  12.1 17.3 %collective-permute-start.2 = (bf16[64,1280]{1,0:T(8,128)(2,1)S(1)}, bf16[64,1280]{1,0:T(8,128)(2,1)S(1)}, u32[]{:S(2)}, u32[]{:S(2)}) collective-permute-start(bf16[64,1280]{1,0:T(8,128)(2,1)S(1)} %bitcast.718), channel_id=1, source_target_pairs={{0,4},{1,5},{4,0},{5,1},{2,6},{3,7},{6,2},{7,3},{8,12},{9,13},{12,... | collective-permute-start | bytes 491528 | tf_op jit(solution)/shard_map/ppermute | solution.py:105
  24.8 13.7 %all-to-all-start = ((bf16[32,32,128]{2,1,0:T(8,128)(2,1)}), bf16[32,32,128]{2,1,0:T(8,128)(2,1)S(1)}, u32[]{:S(2)}, u32[]{:S(2)}) async-start(bf16[32,32,128]{2,1,0:T(8,128)(2,1)} %bitcast.290), calls=%async_computation | async-start | bytes 524288 | tf_op jit(solution)/shard_map/all_to_all | solution.py:96
  29.5 58.2 %collective-permute-start.6 = (bf16[128,2048]{1,0:T(8,128)(2,1)S(1)}, bf16[128,2048]{1,0:T(8,128)(2,1)}, u32[]{:S(2)}, u32[]{:S(2)}) collective-permute-start(bf16[128,2048]{1,0:T(8,128)(2,1)S(1)} %copy-done.12), channel_id=1, source_target_pairs={{0,5},{1,4},{4,1},{5,0},{2,7},{3,6},{6,3},{7,2},{8,13},{9,12},{12,... | collective-permute-start | bytes 1572872 | tf_op jit(solution)/shard_map/ppermute | solution.py:117
  32.2 56.1 %collective-permute-start.5 = (bf16[128,2048]{1,0:T(8,128)(2,1)S(1)}, bf16[128,2048]{1,0:T(8,128)(2,1)}, u32[]{:S(2)}, u32[]{:S(2)}) collective-permute-start(bf16[128,2048]{1,0:T(8,128)(2,1)S(1)} %copy-done.12), channel_id=1, source_target_pairs={{0,4},{1,5},{4,0},{5,1},{2,6},{3,7},{6,2},{7,3},{8,12},{9,13},{12,... | collective-permute-start | bytes 1572872 | tf_op jit(solution)/shard_map/ppermute | solution.py:117
  33.7 19.8 %collective-permute-start.7 = (bf16[256,1280]{1,0:T(8,128)(2,1)}, bf16[256,1280]{1,0:T(8,128)(2,1)}, u32[]{:S(2)}, u32[]{:S(2)}) collective-permute-start(bf16[256,1280]{1,0:T(8,128)(2,1)} %bitcast.18), channel_id=1, source_target_pairs={{0,8},{8,16},{16,24},{24,0},{1,9},{9,17},{17,25},{25,1},{2,10},{10... | collective-permute-start | bytes 1966088 | tf_op jit(solution)/shard_map/ppermute | solution.py:190
  39.4 41.2 %collective-permute-start.9 = (bf16[256,1280]{1,0:T(8,128)(2,1)}, bf16[256,1280]{1,0:T(8,128)(2,1)S(1)}, u32[]{:S(2)}, u32[]{:S(2)}) collective-permute-start(bf16[256,1280]{1,0:T(8,128)(2,1)} %bitcast.18), channel_id=1, source_target_pairs={{0,24},{8,0},{16,8},{24,16},{1,25},{9,1},{17,9},{25,17},{2,26},{10... | collective-permute-start | bytes 1966088 | tf_op jit(solution)/shard_map/ppermute | solution.py:190
  53.5 26.6 %collective-permute-start.8 = (bf16[256,1280]{1,0:T(8,128)(2,1)}, bf16[256,1280]{1,0:T(8,128)(2,1)S(1)}, u32[]{:S(2)}, u32[]{:S(2)}) collective-permute-start(bf16[256,1280]{1,0:T(8,128)(2,1)} %collective-permute-done.7), channel_id=1, source_target_pairs={{0,8},{8,16},{16,24},{24,0},{1,9},{9,17},{17,25},{25,1},{2,10},{10... | collective-permute-start | bytes 1966088 | tf_op jit(solution)/shard_map/ppermute | solution.py:190
  80.7 16.5 %collective-permute-start.10 = (bf16[8,128,1280]{2,1,0:T(8,128)(2,1)S(1)}, bf16[8,128,1280]{2,1,0:T(8,128)(2,1)S(1)}, u32[]{:S(2)}, u32[]{:S(2)}) collective-permute-start(bf16[8,128,1280]{2,1,0:T(8,128)(2,1)S(1)} %bitcast.648), channel_id=1, source_target_pairs={{0,2},{2,0},{1,3},{3,1},{4,6},{6,4},{5,7},{7,5},{8,10},{10,8},{9,1... | collective-permute-start | bytes 7864328 | tf_op jit(solution)/shard_map/ppermute | solution.py:87
  86.1 28.2 %collective-permute-start.14 = (bf16[128,2048]{1,0:T(8,128)(2,1)}, bf16[128,2048]{1,0:T(8,128)(2,1)}, u32[]{:S(2)}, u32[]{:S(2)}) collective-permute-start(bf16[128,2048]{1,0:T(8,128)(2,1)} %param.14), channel_id=1, source_target_pairs={{0,24},{8,0},{16,8},{24,16},{1,25},{9,1},{17,9},{25,17},{2,26},{10... | collective-permute-start | bytes 1572872 | tf_op jit(solution)/shard_map/ppermute | solution.py:190
  87.7 24.7 %collective-permute-start.13 = (bf16[128,2048]{1,0:T(8,128)(2,1)}, bf16[128,2048]{1,0:T(8,128)(2,1)}, u32[]{:S(2)}, u32[]{:S(2)}) collective-permute-start(bf16[128,2048]{1,0:T(8,128)(2,1)} %collective-permute-done.12), channel_id=1, source_target_pairs={{0,8},{8,16},{16,24},{24,0},{1,9},{9,17},{17,25},{25,1},{2,10},{10... | collective-permute-start | bytes 1572872 | tf_op jit(solution)/shard_map/ppermute | solution.py:190
  102.7 70.3 %all-to-all-start.1 = ((bf16[32,32,1280]{2,1,0:T(8,128)(2,1)}), bf16[32,32,1280]{2,1,0:T(8,128)(2,1)}, u32[]{:S(2)}, u32[]{:S(2)}) async-start(bf16[32,32,1280]{2,1,0:T(8,128)(2,1)} %bitcast.27), calls=%async_computation.1 | async-start | bytes 5242880 | tf_op jit(solution)/shard_map/all_to_all | solution.py:96
  118.9 30.1 %collective-permute-start.17 = (bf16[128,2048]{1,0:T(8,128)(2,1)}, bf16[128,2048]{1,0:T(8,128)(2,1)S(1)}, u32[]{:S(2)}, u32[]{:S(2)}) collective-permute-start(bf16[128,2048]{1,0:T(8,128)(2,1)} %get-tuple-element.296), channel_id=1, source_target_pairs={{0,5},{1,4},{4,1},{5,0},{2,7},{3,6},{6,3},{7,2},{8,13},{9,12},{12,... | collective-permute-start | bytes 1572872 | tf_op jit(solution)/shard_map/ppermute | solution.py:105
  121.2 37.3 %collective-permute-start.16 = (bf16[128,2048]{1,0:T(8,128)(2,1)}, bf16[128,2048]{1,0:T(8,128)(2,1)S(1)}, u32[]{:S(2)}, u32[]{:S(2)}) collective-permute-start(bf16[128,2048]{1,0:T(8,128)(2,1)} %get-tuple-element.297), channel_id=1, source_target_pairs={{0,4},{1,5},{4,0},{5,1},{2,6},{3,7},{6,2},{7,3},{8,12},{9,13},{12,... | collective-permute-start | bytes 1572872 | tf_op jit(solution)/shard_map/ppermute | solution.py:105
  121.7 38.9 %collective-permute-start.15 = (bf16[128,2048]{1,0:T(8,128)(2,1)S(1)}, bf16[128,2048]{1,0:T(8,128)(2,1)S(1)}, u32[]{:S(2)}, u32[]{:S(2)}) collective-permute-start(bf16[128,2048]{1,0:T(8,128)(2,1)S(1)} %get-tuple-element.298), channel_id=1, source_target_pairs={{0,1},{1,0},{4,5},{5,4},{2,3},{3,2},{6,7},{7,6},{8,9},{9,8},{12,13... | collective-permute-start | bytes 1572872 | tf_op jit(solution)/shard_map/ppermute | solution.py:105
  161.1 18.1 %collective-permute-start.18 = (bf16[2,256,2048]{2,1,0:T(8,128)(2,1)S(1)}, bf16[2,256,2048]{2,1,0:T(8,128)(2,1)}, u32[]{:S(2)}, u32[]{:S(2)}) collective-permute-start(bf16[2,256,2048]{2,1,0:T(8,128)(2,1)S(1)} %bitcast.653), channel_id=1, source_target_pairs={{0,2},{2,0},{1,3},{3,1},{4,6},{6,4},{5,7},{7,5},{8,10},{10,8},{9,1... | collective-permute-start | bytes 6291464 | tf_op jit(solution)/shard_map/ppermute | solution.py:87
  172.9 54.2 %all-to-all-start.2 = ((bf16[32,32,768]{2,1,0:T(8,128)(2,1)}), bf16[32,32,768]{2,1,0:T(8,128)(2,1)}, u32[]{:S(2)}, u32[]{:S(2)}) async-start(bf16[32,32,768]{2,1,0:T(8,128)(2,1)} %bitcast.655), calls=%async_computation.2 | async-start | bytes 3145728 | tf_op jit(solution)/shard_map/all_to_all | solution.py:96
  184.9 24.2 %collective-permute-start.19 = (bf16[128,2048]{1,0:T(8,128)(2,1)S(1)}, bf16[128,2048]{1,0:T(8,128)(2,1)}, u32[]{:S(2)}, u32[]{:S(2)}) collective-permute-start(bf16[128,2048]{1,0:T(8,128)(2,1)S(1)} %get-tuple-element.289), channel_id=1, source_target_pairs={{0,1},{1,0},{4,5},{5,4},{2,3},{3,2},{6,7},{7,6},{8,9},{9,8},{12,13... | collective-permute-start | bytes 1572872 | tf_op jit(solution)/shard_map/ppermute | solution.py:105
  186.9 35.4 %collective-permute-start.21 = (bf16[128,2048]{1,0:T(8,128)(2,1)S(1)}, bf16[128,2048]{1,0:T(8,128)(2,1)}, u32[]{:S(2)}, u32[]{:S(2)}) collective-permute-start(bf16[128,2048]{1,0:T(8,128)(2,1)S(1)} %get-tuple-element.290), channel_id=1, source_target_pairs={{0,5},{1,4},{4,1},{5,0},{2,7},{3,6},{6,3},{7,2},{8,13},{9,12},{12,... | collective-permute-start | bytes 1572872 | tf_op jit(solution)/shard_map/ppermute | solution.py:105
  189.2 33.1 %collective-permute-start.20 = (bf16[128,2048]{1,0:T(8,128)(2,1)S(1)}, bf16[128,2048]{1,0:T(8,128)(2,1)}, u32[]{:S(2)}, u32[]{:S(2)}) collective-permute-start(bf16[128,2048]{1,0:T(8,128)(2,1)S(1)} %get-tuple-element.291), channel_id=1, source_target_pairs={{0,4},{1,5},{4,0},{5,1},{2,6},{3,7},{6,2},{7,3},{8,12},{9,13},{12,... | collective-permute-start | bytes 1572872 | tf_op jit(solution)/shard_map/ppermute | solution.py:105
  225.4 17.8 %collective-permute-start.29 = (bf16[128,2048]{1,0:T(8,128)(2,1)S(1)}, bf16[128,2048]{1,0:T(8,128)(2,1)S(1)}, u32[]{:S(2)}, u32[]{:S(2)}) collective-permute-start(bf16[128,2048]{1,0:T(8,128)(2,1)S(1)} %multiply_convert_fusion.1), channel_id=1, source_target_pairs={{0,8},{8,16},{16,24},{24,0},{1,9},{9,17},{17,25},{25,1},{2,10},{10... | collective-permute-start | bytes 1572872 | tf_op jit(solution)/shard_map/rows_far1/ppermute | solution.py:190
  243.7 15.7 %collective-permute-start.31 = (bf16[2,32,2048]{2,1,0:T(8,128)(2,1)S(1)}, bf16[2,32,2048]{2,1,0:T(8,128)(2,1)S(1)}, u32[]{:S(2)}, u32[]{:S(2)}) collective-permute-start(bf16[2,32,2048]{2,1,0:T(8,128)(2,1)S(1)} %bitcast.713), channel_id=1, source_target_pairs={{0,4},{1,5},{4,0},{5,1},{2,6},{3,7},{6,2},{7,3},{8,12},{9,13},{12,... | collective-permute-start | bytes 786440 | tf_op jit(solution)/shard_map/rows_out1/ppermute | solution.py:198
  244.9 14.5 %collective-permute-start.32 = (bf16[2,32,2048]{2,1,0:T(8,128)(2,1)S(1)}, bf16[2,32,2048]{2,1,0:T(8,128)(2,1)S(1)}, u32[]{:S(2)}, u32[]{:S(2)}) collective-permute-start(bf16[2,32,2048]{2,1,0:T(8,128)(2,1)S(1)} %bitcast.710), channel_id=1, source_target_pairs={{0,5},{1,4},{4,1},{5,0},{2,7},{3,6},{6,3},{7,2},{8,13},{9,12},{12,... | collective-permute-start | bytes 786440 | tf_op jit(solution)/shard_map/rows_out1/ppermute | solution.py:198
  247.2 15.3 %collective-permute-start.34 = (bf16[128,2048]{1,0:T(8,128)(2,1)S(1)}, bf16[128,2048]{1,0:T(8,128)(2,1)S(1)}, u32[]{:S(2)}, u32[]{:S(2)}) collective-permute-start(bf16[128,2048]{1,0:T(8,128)(2,1)S(1)} %collective-permute-done.29), channel_id=1, source_target_pairs={{0,8},{8,16},{16,24},{24,0},{1,9},{9,17},{17,25},{25,1},{2,10},{10... | collective-permute-start | bytes 1572872 | tf_op jit(solution)/shard_map/rows_far2/ppermute | solution.py:190
  263.1 14.3 %collective-permute-start.36 = (bf16[2,32,2048]{2,1,0:T(8,128)(2,1)S(1)}, bf16[2,32,2048]{2,1,0:T(8,128)(2,1)S(1)}, u32[]{:S(2)}, u32[]{:S(2)}) collective-permute-start(bf16[2,32,2048]{2,1,0:T(8,128)(2,1)S(1)} %bitcast.714), channel_id=1, source_target_pairs={{0,4},{1,5},{4,0},{5,1},{2,6},{3,7},{6,2},{7,3},{8,12},{9,13},{12,... | collective-permute-start | bytes 786440 | tf_op jit(solution)/shard_map/rows_out2/ppermute | solution.py:198
  266.6 13.9 %collective-permute-start.39 = (bf16[128,2048]{1,0:T(8,128)(2,1)S(1)}, bf16[128,2048]{1,0:T(8,128)(2,1)S(1)}, u32[]{:S(2)}, u32[]{:S(2)}) collective-permute-start(bf16[128,2048]{1,0:T(8,128)(2,1)S(1)} %collective-permute-done.34), channel_id=1, source_target_pairs={{0,8},{8,16},{16,24},{24,0},{1,9},{9,17},{17,25},{25,1},{2,10},{10... | collective-permute-start | bytes 1572872 | tf_op jit(solution)/shard_map/rows_far3/ppermute | solution.py:190
  278.3 17.6 %collective-permute-start.44 = (bf16[2,2,32,2176]{3,2,1,0:T(8,128)(2,1)S(1)}, bf16[2,2,32,2176]{3,2,1,0:T(8,128)(2,1)S(1)}, u32[]{:S(2)}, u32[]{:S(2)}) collective-permute-start(bf16[2,2,32,2176]{3,2,1,0:T(8,128)(2,1)S(1)} %get-tuple-element.340), channel_id=1, source_target_pairs={{0,2},{2,0},{1,3},{3,1},{4,6},{6,4},{5,7},{7,5},{8,10},{10,8},{9,1... | collective-permute-start | bytes 1671176 | tf_op jit(solution)/shard_map/rows_back1/ppermute | solution.py:87
  281.1 13.8 %collective-permute-start.41 = (bf16[2,32,2048]{2,1,0:T(8,128)(2,1)S(1)}, bf16[2,32,2048]{2,1,0:T(8,128)(2,1)S(1)}, u32[]{:S(2)}, u32[]{:S(2)}) collective-permute-start(bf16[2,32,2048]{2,1,0:T(8,128)(2,1)S(1)} %bitcast.716), channel_id=1, source_target_pairs={{0,4},{1,5},{4,0},{5,1},{2,6},{3,7},{6,2},{7,3},{8,12},{9,13},{12,... | collective-permute-start | bytes 786440 | tf_op jit(solution)/shard_map/rows_out3/ppermute | solution.py:198
  295.9 14.4 %collective-permute-start.48 = (bf16[2,2,32,2176]{3,2,1,0:T(8,128)(2,1)S(1)}, bf16[2,2,32,2176]{3,2,1,0:T(8,128)(2,1)S(1)}, u32[]{:S(2)}, u32[]{:S(2)}) collective-permute-start(bf16[2,2,32,2176]{3,2,1,0:T(8,128)(2,1)S(1)} %get-tuple-element.334), channel_id=1, source_target_pairs={{0,2},{2,0},{1,3},{3,1},{4,6},{6,4},{5,7},{7,5},{8,10},{10,8},{9,1... | collective-permute-start | bytes 1671176 | tf_op jit(solution)/shard_map/rows_back2/ppermute | solution.py:87
  296.1 16.1 %collective-permute-start.47 = (bf16[2,32,2176]{2,1,0:T(8,128)(2,1)S(1)}, bf16[2,32,2176]{2,1,0:T(8,128)(2,1)S(1)}, u32[]{:S(2)}, u32[]{:S(2)}) collective-permute-start(bf16[2,32,2176]{2,1,0:T(8,128)(2,1)S(1)} %get-tuple-element.336), channel_id=1, source_target_pairs={{0,5},{1,4},{4,1},{5,0},{2,7},{3,6},{6,3},{7,2},{8,13},{9,12},{12,... | collective-permute-start | bytes 835592 | tf_op jit(solution)/shard_map/rows_back1/ppermute | solution.py:105
  297.3 16.5 %collective-permute-start.45 = (bf16[2,32,2176]{2,1,0:T(8,128)(2,1)S(1)}, bf16[2,32,2176]{2,1,0:T(8,128)(2,1)S(1)}, u32[]{:S(2)}, u32[]{:S(2)}) collective-permute-start(bf16[2,32,2176]{2,1,0:T(8,128)(2,1)S(1)} %get-tuple-element.338), channel_id=1, source_target_pairs={{0,1},{1,0},{4,5},{5,4},{2,3},{3,2},{6,7},{7,6},{8,9},{9,8},{12,13... | collective-permute-start | bytes 835592 | tf_op jit(solution)/shard_map/rows_back1/ppermute | solution.py:105
  298.8 15.8 %collective-permute-start.46 = (bf16[2,32,2176]{2,1,0:T(8,128)(2,1)S(1)}, bf16[2,32,2176]{2,1,0:T(8,128)(2,1)S(1)}, u32[]{:S(2)}, u32[]{:S(2)}) collective-permute-start(bf16[2,32,2176]{2,1,0:T(8,128)(2,1)S(1)} %get-tuple-element.339), channel_id=1, source_target_pairs={{0,4},{1,5},{4,0},{5,1},{2,6},{3,7},{6,2},{7,3},{8,12},{9,13},{12,... | collective-permute-start | bytes 835592 | tf_op jit(solution)/shard_map/rows_back1/ppermute | solution.py:105
  310.2 19.9 %collective-permute-start.56 = (bf16[2,2,32,2176]{3,2,1,0:T(8,128)(2,1)S(1)}, bf16[2,2,32,2176]{3,2,1,0:T(8,128)(2,1)S(1)}, u32[]{:S(2)}, u32[]{:S(2)}) collective-permute-start(bf16[2,2,32,2176]{3,2,1,0:T(8,128)(2,1)S(1)} %get-tuple-element.322), channel_id=1, source_target_pairs={{0,2},{2,0},{1,3},{3,1},{4,6},{6,4},{5,7},{7,5},{8,10},{10,8},{9,1... | collective-permute-start | bytes 1671176 | tf_op jit(solution)/shard_map/rows_back3/ppermute | solution.py:87
  312.2 13.9 %collective-permute-start.49 = (bf16[2,32,2176]{2,1,0:T(8,128)(2,1)S(1)}, bf16[2,32,2176]{2,1,0:T(8,128)(2,1)S(1)}, u32[]{:S(2)}, u32[]{:S(2)}) collective-permute-start(bf16[2,32,2176]{2,1,0:T(8,128)(2,1)S(1)} %get-tuple-element.332), channel_id=1, source_target_pairs={{0,1},{1,0},{4,5},{5,4},{2,3},{3,2},{6,7},{7,6},{8,9},{9,8},{12,13... | collective-permute-start | bytes 835592 | tf_op jit(solution)/shard_map/rows_back2/ppermute | solution.py:105
  326.8 19.1 %collective-permute-start.61 = (bf16[128,2176]{1,0:T(8,128)(2,1)S(1)}, bf16[128,2176]{1,0:T(8,128)(2,1)S(1)}, u32[]{:S(2)}, u32[]{:S(2)}) collective-permute-start(bf16[128,2176]{1,0:T(8,128)(2,1)S(1)} %fusion.7), channel_id=1, source_target_pairs={{0,24},{8,0},{16,8},{24,16},{1,25},{9,1},{17,9},{25,17},{2,26},{10... | collective-permute-start | bytes 1671176 | tf_op jit(solution)/shard_map/partial_far/ppermute | solution.py:190
  331.4 14.0 %collective-permute-start.58 = (bf16[2,32,2176]{2,1,0:T(8,128)(2,1)S(1)}, bf16[2,32,2176]{2,1,0:T(8,128)(2,1)S(1)}, u32[]{:S(2)}, u32[]{:S(2)}) collective-permute-start(bf16[2,32,2176]{2,1,0:T(8,128)(2,1)S(1)} %get-tuple-element.320), channel_id=1, source_target_pairs={{0,4},{1,5},{4,0},{5,1},{2,6},{3,7},{6,2},{7,3},{8,12},{9,13},{12,... | collective-permute-start | bytes 835592 | tf_op jit(solution)/shard_map/rows_back3/ppermute | solution.py:105
  333.9 16.0 %collective-permute-start.52 = (bf16[2,2,32,2176]{3,2,1,0:T(8,128)(2,1)S(1)}, bf16[2,2,32,2176]{3,2,1,0:T(8,128)(2,1)S(1)}, u32[]{:S(2)}, u32[]{:S(2)}) collective-permute-start(bf16[2,2,32,2176]{3,2,1,0:T(8,128)(2,1)S(1)} %get-tuple-element.328), channel_id=1, source_target_pairs={{0,2},{2,0},{1,3},{3,1},{4,6},{6,4},{5,7},{7,5},{8,10},{10,8},{9,1... | collective-permute-start | bytes 1671176 | tf_op jit(solution)/shard_map/rows_back0/ppermute | solution.py:87
  345.8 17.6 %collective-permute-start.60 = (bf16[128,2176]{1,0:T(8,128)(2,1)S(1)}, bf16[128,2176]{1,0:T(8,128)(2,1)S(1)}, u32[]{:S(2)}, u32[]{:S(2)}) collective-permute-start(bf16[128,2176]{1,0:T(8,128)(2,1)S(1)} %fusion.8), channel_id=1, source_target_pairs={{0,8},{8,16},{16,24},{24,0},{1,9},{9,17},{17,25},{25,1},{2,10},{10... | collective-permute-start | bytes 1671176 | tf_op jit(solution)/shard_map/partial_far/ppermute | solution.py:190
  346.1 25.2 %collective-permute-start.62 = (bf16[128,2176]{1,0:T(8,128)(2,1)S(1)}, bf16[128,2176]{1,0:T(8,128)(2,1)S(1)}, u32[]{:S(2)}, u32[]{:S(2)}) collective-permute-start(bf16[128,2176]{1,0:T(8,128)(2,1)S(1)} %add_convert_fusion), channel_id=1, source_target_pairs={{0,24},{8,0},{16,8},{24,16},{1,25},{9,1},{17,9},{25,17},{2,26},{10... | collective-permute-start | bytes 1671176 | tf_op jit(solution)/shard_map/partial_far/ppermute | solution.py:190
  373.5 22.2 %collective-permute-start.65 = (bf16[128,2048]{1,0:T(8,128)(2,1)S(1)}, bf16[128,2048]{1,0:T(8,128)(2,1)S(1)}, u32[]{:S(2)}, u32[]{:S(2)}) collective-permute-start(bf16[128,2048]{1,0:T(8,128)(2,1)S(1)} %fusion.47), channel_id=1, source_target_pairs={{0,5},{1,4},{4,1},{5,0},{2,7},{3,6},{6,3},{7,2},{8,13},{9,12},{12,... | collective-permute-start | bytes 1572872 | tf_op jit(solution)/shard_map/ppermute | solution.py:117
  375.0 22.9 %collective-permute-start.64 = (bf16[128,2048]{1,0:T(8,128)(2,1)S(1)}, bf16[128,2048]{1,0:T(8,128)(2,1)S(1)}, u32[]{:S(2)}, u32[]{:S(2)}) collective-permute-start(bf16[128,2048]{1,0:T(8,128)(2,1)S(1)} %fusion.47), channel_id=1, source_target_pairs={{0,4},{1,5},{4,0},{5,1},{2,6},{3,7},{6,2},{7,3},{8,12},{9,13},{12,... | collective-permute-start | bytes 1572872 | tf_op jit(solution)/shard_map/ppermute | solution.py:117
  375.5 22.4 %collective-permute-start.63 = (bf16[128,2048]{1,0:T(8,128)(2,1)S(1)}, bf16[128,2048]{1,0:T(8,128)(2,1)S(1)}, u32[]{:S(2)}, u32[]{:S(2)}) collective-permute-start(bf16[128,2048]{1,0:T(8,128)(2,1)S(1)} %fusion.47), channel_id=1, source_target_pairs={{0,1},{1,0},{4,5},{5,4},{2,3},{3,2},{6,7},{7,6},{8,9},{9,8},{12,13... | collective-permute-start | bytes 1572872 | tf_op jit(solution)/shard_map/ppermute | solution.py:117
  409.7 24.3 %collective-permute-start.67 = (bf16[128,2048]{1,0:T(8,128)(2,1)}, bf16[128,2048]{1,0:T(8,128)(2,1)S(1)}, u32[]{:S(2)}, u32[]{:S(2)}) collective-permute-start(bf16[128,2048]{1,0:T(8,128)(2,1)} %get-tuple-element.282), channel_id=1, source_target_pairs={{0,1},{1,0},{4,5},{5,4},{2,3},{3,2},{6,7},{7,6},{8,9},{9,8},{12,13... | collective-permute-start | bytes 1572872 | tf_op jit(solution)/shard_map/ppermute | solution.py:105
  410.3 24.9 %collective-permute-start.69 = (bf16[128,2048]{1,0:T(8,128)(2,1)}, bf16[128,2048]{1,0:T(8,128)(2,1)S(1)}, u32[]{:S(2)}, u32[]{:S(2)}) collective-permute-start(bf16[128,2048]{1,0:T(8,128)(2,1)} %get-tuple-element.283), channel_id=1, source_target_pairs={{0,5},{1,4},{4,1},{5,0},{2,7},{3,6},{6,3},{7,2},{8,13},{9,12},{12,... | collective-permute-start | bytes 1572872 | tf_op jit(solution)/shard_map/ppermute | solution.py:105
  411.9 24.7 %collective-permute-start.68 = (bf16[128,2048]{1,0:T(8,128)(2,1)}, bf16[128,2048]{1,0:T(8,128)(2,1)}, u32[]{:S(2)}, u32[]{:S(2)}) collective-permute-start(bf16[128,2048]{1,0:T(8,128)(2,1)} %get-tuple-element.284), channel_id=1, source_target_pairs={{0,4},{1,5},{4,0},{5,1},{2,6},{3,7},{6,2},{7,3},{8,12},{9,13},{12,... | collective-permute-start | bytes 1572872 | tf_op jit(solution)/shard_map/ppermute | solution.py:105
  447.8 15.9 %collective-permute-start.70 = (bf16[8,128,1280]{2,1,0:T(8,128)(2,1)}, bf16[8,128,1280]{2,1,0:T(8,128)(2,1)}, u32[]{:S(2)}, u32[]{:S(2)}) collective-permute-start(bf16[8,128,1280]{2,1,0:T(8,128)(2,1)} %fusion.9), channel_id=1, source_target_pairs={{0,2},{2,0},{1,3},{3,1},{4,6},{6,4},{5,7},{7,5},{8,10},{10,8},{9,1... | collective-permute-start | bytes 7864328 | tf_op jit(solution)/shard_map/ppermute | solution.py:87
  448.1 64.9 %all-to-all-start.3 = ((bf16[8,4,32,2048]{3,2,1,0:T(8,128)(2,1)}), bf16[8,4,32,2048]{3,2,1,0:T(8,128)(2,1)}, u32[]{:S(2)}, u32[]{:S(2)}) async-start(bf16[8,4,32,2048]{3,2,1,0:T(8,128)(2,1)} %pad_maximum_fusion.3), calls=%async_computation.3 | async-start | bytes 8388608 | tf_op jit(solution)/shard_map/all_to_all | solution.py:96
  454.1 16.6 %collective-permute-start.72 = (bf16[128,2048]{1,0:T(8,128)(2,1)S(1)}, bf16[128,2048]{1,0:T(8,128)(2,1)S(1)}, u32[]{:S(2)}, u32[]{:S(2)}) collective-permute-start(bf16[128,2048]{1,0:T(8,128)(2,1)S(1)} %get-tuple-element.280), channel_id=1, source_target_pairs={{0,8},{8,16},{16,24},{24,0},{1,9},{9,17},{17,25},{25,1},{2,10},{10... | collective-permute-start | bytes 1572872 | tf_op jit(solution)/shard_map/ppermute | solution.py:190
  454.2 25.6 %collective-permute-start.71 = (bf16[128,2048]{1,0:T(8,128)(2,1)S(1)}, bf16[128,2048]{1,0:T(8,128)(2,1)S(1)}, u32[]{:S(2)}, u32[]{:S(2)}) collective-permute-start(bf16[128,2048]{1,0:T(8,128)(2,1)S(1)} %get-tuple-element.281), channel_id=1, source_target_pairs={{0,24},{8,0},{16,8},{24,16},{1,25},{9,1},{17,9},{25,17},{2,26},{10... | collective-permute-start | bytes 1572872 | tf_op jit(solution)/shard_map/ppermute | solution.py:190
  479.9 14.9 %collective-permute-start.86 = (bf16[128,2048]{1,0:T(8,128)(2,1)S(1)}, bf16[128,2048]{1,0:T(8,128)(2,1)S(1)}, u32[]{:S(2)}, u32[]{:S(2)}) collective-permute-start(bf16[128,2048]{1,0:T(8,128)(2,1)S(1)} %fusion.58), channel_id=1, source_target_pairs={{0,24},{8,0},{16,8},{24,16},{1,25},{9,1},{17,9},{25,17},{2,26},{10... | collective-permute-start | bytes 1572872 | tf_op jit(solution)/shard_map/ppermute | solution.py:190
  482.2 26.3 %collective-permute-start.74 = (bf16[256,1280]{1,0:T(8,128)(2,1)S(1)}, bf16[256,1280]{1,0:T(8,128)(2,1)S(1)}, u32[]{:S(2)}, u32[]{:S(2)}) collective-permute-start(bf16[256,1280]{1,0:T(8,128)(2,1)S(1)} %get-tuple-element.275), channel_id=1, source_target_pairs={{0,24},{8,0},{16,8},{24,16},{1,25},{9,1},{17,9},{25,17},{2,26},{10... | collective-permute-start | bytes 1966088 | tf_op jit(solution)/shard_map/ppermute | solution.py:190
  485.3 55.0 %collective-permute-start.78 = (bf16[128,2048]{1,0:T(8,128)(2,1)}, bf16[128,2048]{1,0:T(8,128)(2,1)}, u32[]{:S(2)}, u32[]{:S(2)}) collective-permute-start(bf16[128,2048]{1,0:T(8,128)(2,1)} %get-tuple-element.276), channel_id=1, source_target_pairs={{0,5},{1,4},{4,1},{5,0},{2,7},{3,6},{6,3},{7,2},{8,13},{9,12},{12,... | collective-permute-start | bytes 1572872 | tf_op jit(solution)/shard_map/ppermute | solution.py:105
  487.8 52.5 %collective-permute-start.77 = (bf16[128,2048]{1,0:T(8,128)(2,1)}, bf16[128,2048]{1,0:T(8,128)(2,1)}, u32[]{:S(2)}, u32[]{:S(2)}) collective-permute-start(bf16[128,2048]{1,0:T(8,128)(2,1)} %get-tuple-element.277), channel_id=1, source_target_pairs={{0,4},{1,5},{4,0},{5,1},{2,6},{3,7},{6,2},{7,3},{8,12},{9,13},{12,... | collective-permute-start | bytes 1572872 | tf_op jit(solution)/shard_map/ppermute | solution.py:105
  488.4 51.9 %collective-permute-start.76 = (bf16[128,2048]{1,0:T(8,128)(2,1)}, bf16[128,2048]{1,0:T(8,128)(2,1)}, u32[]{:S(2)}, u32[]{:S(2)}) collective-permute-start(bf16[128,2048]{1,0:T(8,128)(2,1)} %get-tuple-element.278), channel_id=1, source_target_pairs={{0,1},{1,0},{4,5},{5,4},{2,3},{3,2},{6,7},{7,6},{8,9},{9,8},{12,13... | collective-permute-start | bytes 1572872 | tf_op jit(solution)/shard_map/ppermute | solution.py:105
  494.8 30.0 %collective-permute-start.73 = (bf16[256,1280]{1,0:T(8,128)(2,1)S(1)}, bf16[256,1280]{1,0:T(8,128)(2,1)}, u32[]{:S(2)}, u32[]{:S(2)}) collective-permute-start(bf16[256,1280]{1,0:T(8,128)(2,1)S(1)} %get-tuple-element.274), channel_id=1, source_target_pairs={{0,8},{8,16},{16,24},{24,0},{1,9},{9,17},{17,25},{25,1},{2,10},{10... | collective-permute-start | bytes 1966088 | tf_op jit(solution)/shard_map/ppermute | solution.py:190
  508.7 29.1 %collective-permute-start.75 = (bf16[256,1280]{1,0:T(8,128)(2,1)S(1)}, bf16[256,1280]{1,0:T(8,128)(2,1)}, u32[]{:S(2)}, u32[]{:S(2)}) collective-permute-start(bf16[256,1280]{1,0:T(8,128)(2,1)S(1)} %fusion.15), channel_id=1, source_target_pairs={{0,24},{8,0},{16,8},{24,16},{1,25},{9,1},{17,9},{25,17},{2,26},{10... | collective-permute-start | bytes 1966088 | tf_op jit(solution)/shard_map/ppermute | solution.py:190
  524.8 30.8 %collective-permute-start.80 = (bf16[128,2048]{1,0:T(8,128)(2,1)}, bf16[128,2048]{1,0:T(8,128)(2,1)}, u32[]{:S(2)}, u32[]{:S(2)}) collective-permute-start(bf16[128,2048]{1,0:T(8,128)(2,1)} %convolution_convert_fusion.11), channel_id=1, source_target_pairs={{0,24},{8,0},{16,8},{24,16},{1,25},{9,1},{17,9},{25,17},{2,26},{10... | collective-permute-start | bytes 1572872 | tf_op jit(solution)/shard_map/ppermute | solution.py:190
  537.8 23.9 %collective-permute-start.79 = (bf16[128,2048]{1,0:T(8,128)(2,1)}, bf16[128,2048]{1,0:T(8,128)(2,1)}, u32[]{:S(2)}, u32[]{:S(2)}) collective-permute-start(bf16[128,2048]{1,0:T(8,128)(2,1)} %convolution_convert_fusion.13), channel_id=1, source_target_pairs={{0,8},{8,16},{16,24},{24,0},{1,9},{9,17},{17,25},{25,1},{2,10},{10... | collective-permute-start | bytes 1572872 | tf_op jit(solution)/shard_map/ppermute | solution.py:190
  558.1 13.5 %collective-permute-start.81 = (bf16[128,2048]{1,0:T(8,128)(2,1)S(1)}, bf16[128,2048]{1,0:T(8,128)(2,1)S(1)}, u32[]{:S(2)}, u32[]{:S(2)}) collective-permute-start(bf16[128,2048]{1,0:T(8,128)(2,1)S(1)} %add_convert_fusion.2), channel_id=1, source_target_pairs={{0,24},{8,0},{16,8},{24,16},{1,25},{9,1},{17,9},{25,17},{2,26},{10... | collective-permute-start | bytes 1572872 | tf_op jit(solution)/shard_map/ppermute | solution.py:190
  573.6 15.7 %collective-permute-start.82 = (bf16[128,2048]{1,0:T(8,128)(2,1)S(1)}, bf16[128,2048]{1,0:T(8,128)(2,1)S(1)}, u32[]{:S(2)}, u32[]{:S(2)}) collective-permute-start(bf16[128,2048]{1,0:T(8,128)(2,1)S(1)} %add_convert_fusion.1), channel_id=1, source_target_pairs={{0,1},{1,0},{2,3},{3,2},{4,5},{5,4},{6,7},{7,6},{8,9},{9,8},{10,11... | collective-permute-start | bytes 1572872 | tf_op jit(solution)/shard_map/ppermute | solution.py:87
  575.4 16.5 %all-to-all-start.4 = ((f32[32,24,128]{2,1,0:T(8,128)}), f32[32,24,128]{2,1,0:T(8,128)S(1)}, u32[]{:S(2)}, u32[]{:S(2)}) async-start(f32[32,24,128]{2,1,0:T(8,128)} %bitcast.298), calls=%async_computation.4 | async-start | bytes 786432 | tf_op jit(solution)/shard_map/all_to_all | solution.py:96
  (92 other events, 597.1 us)

commit v11 on v10

--- a/solution.py
+++ b/solution.py
@@ -22,7 +22,7 @@
 NEAR = 2
 CORES = 2
 SLAB = NEAR * CORES * 2
-COT_CUT = 1280
+COT_CUT = 1152
 HEADS_STEP = 4
 LANES = 128
 
@@ -749,12 +749,20 @@
         .transpose(1, 0, 2, 3)
         .reshape(NEAR * 2, far_part * out_rows, D)
     )
-    out_grad = quad_swap(out_grad).reshape(far_count, out_rows, D)
+    out_quad = quad_parts(out_grad)
     query_grad, key_grad, value_grad, query_gain_grad, key_gain_grad = attend_back(
         projected, shared, mixed_grad, per_group
     )
-    query_grad, out_grad = tie(query_grad, out_grad)
-    out_sent = far_parts(out_grad, far_count)
+    query_grad, *out_quad = tie(query_grad, *out_quad)
+    if far_part == 1:
+        out_sent = []
+        for step in range(far_count):
+            at = lax.bitwise_xor(lax.rem(far_index + far_count - step, far_count), quad_index())
+            low = jnp.where(at == 0, out_quad[0], out_quad[1])
+            high = jnp.where(at == 2, out_quad[2], out_quad[3])
+            out_sent.append(jnp.where(at < 2, low, high))
+    else:
+        out_sent = far_parts(quad_order(out_quad).reshape(far_count, out_rows, D), far_count)
     out_found = far_begin(out_sent, far_count)
     gated, query_grad = tie(jnp.stack(gated_outs, axis=1), query_grad)
     gated = exchange(gated, SLAB_AXES)

time: 602 us -> 601 us (level)
    ppermute x24, waiting for transfers between devices: 115 us -> 108 us  [far_shift(): lax.ppermute(value, FAR_AXIS, [(i, (i + step) % count) for i in range(cou...]
    unnamed x146 -> x142, local copies, waits for them, and re-layouts: 15.1 us -> 15.4 us
  transfers between devices with their start and end apart: 92 -> 92, of which waited for: 39 -> 42; matrix products, arithmetic and copies ran while one was open for 18% -> 19% of each run, Pallas kernels for 15% -> 15%
where the time goes in v11:
time: 601 us; the launch traced here: 593 us
  waiting for transfers between devices  232 us (39%)
  starting transfers between devices  125 us (21%)
  Pallas kernels  86.6 us (14%)
  local copies, waits for them, and re-layouts  51.8 us (9%)
  other arithmetic  48.3 us (8%)
  matrix products  46.2 us (8%)
    ppermute x24, waiting for transfers between devices, far_shift(): lax.ppermute(value, FAR_AXIS, [(i, (i + step) % count) for i in range(cou...  108 us
    ppermute x30, waiting for transfers between devices, quad_send(): return lax.ppermute(block, HEAD_AXES, [(i, i ^ step) for i in range(4)])  97.3 us
    dot_general x30, matrix products, dot(): lax.dot_general(left, right, (dims, ((), ())), preferred_element_type=F32)  43.8 us
    ppermute x24, starting transfers between devices, far_shift(): lax.ppermute(value, FAR_AXIS, [(i, (i + step) % count) for i in range(cou...  41.7 us
    pallas_call x4, Pallas kernels, expert_chunk(): pl.pallas_call(expert_kernel, grid_spec=pltpu.PrefetchScalarGridSpec(num_...  40.1 us
    ppermute x30, starting transfers between devices, quad_send(): return lax.ppermute(block, HEAD_AXES, [(i, i ^ step) for i in range(4)])  35.3 us
    all_to_all x5, starting transfers between devices, exchange(): return lax.all_to_all(value, axes, split_axis=0, concat_axis=0, tiled=True)  19.8 us
    pallas_call x1, Pallas kernels, expert_grads(): pl.pallas_call(functools.partial(expert_grad_kernel, count), grid=(D // t...  18.8 us
  transfers between devices with their start and end apart: 92, of which 42 were waited for; matrix products, arithmetic and copies ran while one was open for 19% of the time, Pallas kernels for 15%

profile of v11, /device:TPU:0, one launch (start us, length us, event | category | flops | bytes accessed | tf_op | source)
XLA Modules:
  0.0 592.6 jit_solution(10308336983980137096)
XLA Ops:
  1.3 3.0 collective-permute-start
  17.8 2.5 collective-permute-start.3
  24.2 2.9 all-to-all-start
  28.9 2.7 collective-permute-start.6
  41.9 11.1 %collective-permute-done.7 = bf16[256,1280]{1,0:T(8,128)(2,1)} collective-permute-done((bf16[256,1280]{1,0:T(8,128)(2,1)}, bf16[256,1280]{1,0:T(8,128)(2,1)}, u32[]{:S(2)}, u32[]{:S(2)}) %collective-permute-start.7) | collective-permute-done | bytes 655392 | tf_op jit(solution)/shard_map/ppermute | solution.py:190
  56.3 23.2 %collective-permute-done.8 = bf16[256,1280]{1,0:T(8,128)(2,1)S(1)} collective-permute-done((bf16[256,1280]{1,0:T(8,128)(2,1)}, bf16[256,1280]{1,0:T(8,128)(2,1)S(1)}, u32[]{:S(2)}, u32[]{:S(2)}) %collective-permute-start.8) | collective-permute-done | bytes 655392 | tf_op jit(solution)/shard_map/ppermute | solution.py:190
  86.2 5.8 collective-permute-done.4
  97.8 4.4 fusion.168.query_ref.key_ref.value_ref
  102.1 4.3 all-to-all-start.1
  111.9 2.7 dynamic-slice_bitcast_fusion.17
  114.6 2.4 collective-permute-start.17
  120.6 10.9 %attend.1 = bf16[512,1024]{1,0:T(8,128)(2,1)} custom-call(f32[512,1280]{1,0:T(8,128)} %fusion.168.query_ref.key_ref.value_ref, f32[512,1280]{1,0:T(8,128)} %fusion.168.query_ref.key_ref.value_ref, f32[512,1280]{1,0:T(8,128)} %fusion.168.query_ref.key_ref.value_ref, f32[512,128]{1,0:T(8,128)} %get-tuple-element.446.cos_ref, ...), custom_call_target="tpu_custom_call" | custom-call | flops 1048576 | bytes 1048576 | tf_op jit(solution)/shard_map/attend/pallas_call | solution.py:446
  131.5 12.5 %collective-permute-done.17 = bf16[128,2048]{1,0:T(8,128)(2,1)S(1)} collective-permute-done((bf16[128,2048]{1,0:T(8,128)(2,1)}, bf16[128,2048]{1,0:T(8,128)(2,1)S(1)}, u32[]{:S(2)}, u32[]{:S(2)}) %collective-permute-start.17) | collective-permute-done | bytes 524320 | tf_op jit(solution)/shard_map/ppermute | solution.py:105
  144.0 12.2 %collective-permute-done.16 = bf16[128,2048]{1,0:T(8,128)(2,1)S(1)} collective-permute-done((bf16[128,2048]{1,0:T(8,128)(2,1)}, bf16[128,2048]{1,0:T(8,128)(2,1)S(1)}, u32[]{:S(2)}, u32[]{:S(2)}) %collective-permute-start.16) | collective-permute-done | bytes 524320 | tf_op jit(solution)/shard_map/ppermute | solution.py:105
  162.7 2.8 collective-permute-start.24
  167.0 5.4 collective-permute-done.23
  172.4 3.9 all-to-all-start.2
  177.8 2.5 select_bitcast_fusion.3
  190.9 18.2 %collective-permute-done.19 = bf16[128,2048]{1,0:T(8,128)(2,1)} collective-permute-done((bf16[128,2048]{1,0:T(8,128)(2,1)}, bf16[128,2048]{1,0:T(8,128)(2,1)}, u32[]{:S(2)}, u32[]{:S(2)}) %collective-permute-start.19) | collective-permute-done | bytes 524320 | tf_op jit(solution)/shard_map/ppermute | solution.py:105
  209.1 13.2 %collective-permute-done.21 = bf16[128,2048]{1,0:T(8,128)(2,1)} collective-permute-done((bf16[128,2048]{1,0:T(8,128)(2,1)}, bf16[128,2048]{1,0:T(8,128)(2,1)}, u32[]{:S(2)}, u32[]{:S(2)}) %collective-permute-start.21) | collective-permute-done | bytes 524320 | tf_op jit(solution)/shard_map/ppermute | solution.py:105
  225.3 2.6 collective-permute-start.29
  229.3 3.7 collective-permute-start.27
  233.0 2.9 pad_maximum_fusion.2
  236.4 6.1 %collective-permute-done.26 = bf16[2,32,2048]{2,1,0:T(8,128)(2,1)S(1)} collective-permute-done((bf16[2,32,2048]{2,1,0:T(8,128)(2,1)S(1)}, bf16[2,32,2048]{2,1,0:T(8,128)(2,1)S(1)}, u32[]{:S(2)}, u32[]{:S(2)}) %collective-permute-start.26) | collective-permute-done | bytes 262176 | tf_op jit(solution)/shard_map/rows_out0/ppermute | solution.py:198
  245.0 2.5 collective-permute-start.32
  248.2 2.4 collective-permute-start.34
  250.8 10.0 %expert_chunk.4 = (bf16[256,768]{1,0:T(8,128)(2,1)S(1)}, bf16[256,768]{1,0:T(8,128)(2,1)S(1)}, bf16[256,768]{1,0:T(8,128)(2,1)S(1)}, bf16[256,2048]{1,0:T(8,128)...) custom-call(s32[2]{0:T(128)S(1)} %pad_add_fusion.2.here_ref, bf16[256,2048]{1,0:T(8,128)(2,1)S(1)} %bitcast.582, ...), custom_call_target="tpu_custom_call" | custom-call | flops 1048576 | bytes 1048576 | tf_op jit(solution)/shard_map/expert_chunk/pallas_call | solution.py:276
  268.8 10.0 %expert_chunk.5 = (bf16[256,768]{1,0:T(8,128)(2,1)S(1)}, bf16[256,768]{1,0:T(8,128)(2,1)S(1)}, bf16[256,768]{1,0:T(8,128)(2,1)S(1)}, bf16[256,2048]{1,0:T(8,128)...) custom-call(s32[2]{0:T(128)S(1)} %pad_add_fusion.2.here_ref, bf16[256,2048]{1,0:T(8,128)(2,1)S(1)} %bitcast.584, ...), custom_call_target="tpu_custom_call" | custom-call | flops 1048576 | bytes 1048576 | tf_op jit(solution)/shard_map/expert_chunk/pallas_call | solution.py:276
  285.6 10.0 %expert_chunk.6 = (bf16[256,768]{1,0:T(8,128)(2,1)S(1)}, bf16[256,768]{1,0:T(8,128)(2,1)S(1)}, bf16[256,768]{1,0:T(8,128)(2,1)S(1)}, bf16[256,2048]{1,0:T(8,128)...) custom-call(s32[2]{0:T(128)S(1)} %pad_add_fusion.2.here_ref, bf16[256,2048]{1,0:T(8,128)(2,1)S(1)} %bitcast.586, ...), custom_call_target="tpu_custom_call" | custom-call | flops 1048576 | bytes 1048576 | tf_op jit(solution)/shard_map/expert_chunk/pallas_call | solution.py:276
  300.9 10.2 %expert_chunk.7 = (bf16[256,768]{1,0:T(8,128)(2,1)S(1)}, bf16[256,768]{1,0:T(8,128)(2,1)S(1)}, bf16[256,768]{1,0:T(8,128)(2,1)S(1)}, bf16[256,2048]{1,0:T(8,128)...) custom-call(s32[2]{0:T(128)S(1)} %pad_add_fusion.2.here_ref, bf16[256,2048]{1,0:T(8,128)(2,1)S(1)} %bitcast.588, ...), custom_call_target="tpu_custom_call" | custom-call | flops 1048576 | bytes 1048576 | tf_op jit(solution)/shard_map/expert_chunk/pallas_call | solution.py:276
  316.1 6.6 %collective-permute-done.51 = bf16[2,32,2176]{2,1,0:T(8,128)(2,1)S(1)} collective-permute-done((bf16[2,32,2176]{2,1,0:T(8,128)(2,1)S(1)}, bf16[2,32,2176]{2,1,0:T(8,128)(2,1)S(1)}, u32[]{:S(2)}, u32[]{:S(2)}) %collective-permute-start.51) | collective-permute-done | bytes 278560 | tf_op jit(solution)/shard_map/rows_back2/ppermute | solution.py:105
  322.6 4.0 collective-permute-done.49
  327.9 3.0 collective-permute-start.61
  334.7 5.9 collective-permute-done.57
  340.6 5.9 collective-permute-done.58
  347.1 3.9 collective-permute-start.62
  355.0 4.8 collective-permute-done.53
  359.9 4.4 collective-permute-done.54
  364.3 7.0 %collective-permute-done.62 = bf16[128,2176]{1,0:T(8,128)(2,1)S(1)} collective-permute-done((bf16[128,2176]{1,0:T(8,128)(2,1)S(1)}, bf16[128,2176]{1,0:T(8,128)(2,1)S(1)}, u32[]{:S(2)}, u32[]{:S(2)}) %collective-permute-start.62) | collective-permute-done | bytes 557088 | tf_op jit(solution)/shard_map/partial_far/ppermute | solution.py:190
  373.6 2.4 collective-permute-start.65
  377.2 18.8 %expert_grads.1 = f32[2048,2304]{1,0:T(8,128)} custom-call(bf16[256,2048]{1,0:T(8,128)(2,1)S(1)} %bitcast.583, bf16[256,2048]{1,0:T(8,128)(2,1)} %bitcast.585, bf16[256,2048]{1,0:T(8,128)(2,1)} %bitcast.587, bf16[256,2048]{1,0:T(8,128)(2,1)} %bitcast.589, bf16[256,2048]{1,0:T(8,128)(2,1)} %copy-done.3, bf16[256,2048]{1,0:T(8,128)(2,1)} %copy-done.4, ...), custom_call_target="tpu_custom_call" | custom-call | flops 1048576 | bytes 1048576 | tf_op jit(solution)/shard_map/expert_grads/pallas_call | solution.py:329
  399.5 2.4 convolution_convert_fusion.1
  404.1 3.4 convolution_convert_fusion.16.grad_ref
  417.4 16.8 %attend_back.1 = (bf16[512,1024]{1,0:T(8,128)(2,1)}, bf16[512,128]{1,0:T(8,128)(2,1)}, bf16[512,128]{1,0:T(8,128)(2,1)}, f32[1,128]{1,0:T(1,128)}, f32[1,128]{1,0:T(1,128)}) custom-call(f32[512,1280]{1,0:T(8,128)} %fusion.168.query_ref.key_ref.value_ref, f32[512,1280]{1,0:T(8,128)} %fusion.168.query_ref.key_ref.value_ref, ...), custom_call_target="tpu_custom_call" | custom-call | flops 1048576 | bytes 1048576 | tf_op jit(solution)/shard_map/attend_back/pallas_call | solution.py:461
  439.2 3.2 convolution_convert_fusion
  445.9 4.6 all-to-all-start.3
  452.0 3.8 collective-permute-start.71
  455.8 5.8 convolution_convert_fusion.4
  461.7 2.8 fusion
  464.5 4.1 collective-permute-done.72
  468.6 9.0 %collective-permute-done.71 = bf16[128,2048]{1,0:T(8,128)(2,1)S(1)} collective-permute-done((bf16[128,2048]{1,0:T(8,128)(2,1)S(1)}, bf16[128,2048]{1,0:T(8,128)(2,1)S(1)}, u32[]{:S(2)}, u32[]{:S(2)}) %collective-permute-start.71) | collective-permute-done | bytes 524320 | tf_op jit(solution)/shard_map/ppermute | solution.py:190
  485.3 2.6 collective-permute-start.78
  488.8 5.2 collective-permute-done.86
  496.2 11.6 %collective-permute-done.74 = bf16[256,1280]{1,0:T(8,128)(2,1)S(1)} collective-permute-done((bf16[256,1280]{1,0:T(8,128)(2,1)S(1)}, bf16[256,1280]{1,0:T(8,128)(2,1)S(1)}, u32[]{:S(2)}, u32[]{:S(2)}) %collective-permute-start.74) | collective-permute-done | bytes 655392 | tf_op jit(solution)/shard_map/ppermute | solution.py:190
  508.0 4.5 collective-permute-start.75
  512.6 3.7 fusion.159
  519.9 4.0 collective-permute-done.73
  526.3 10.6 %collective-permute-done.75 = bf16[256,1280]{1,0:T(8,128)(2,1)S(1)} collective-permute-done((bf16[256,1280]{1,0:T(8,128)(2,1)S(1)}, bf16[256,1280]{1,0:T(8,128)(2,1)S(1)}, u32[]{:S(2)}, u32[]{:S(2)}) %collective-permute-start.75) | collective-permute-done | bytes 655392 | tf_op jit(solution)/shard_map/ppermute | solution.py:190
  542.0 2.4 collective-permute-start.85
  556.7 2.6 collective-permute-start.81
  560.5 10.0 %collective-permute-done.81 = bf16[128,2048]{1,0:T(8,128)(2,1)S(1)} collective-permute-done((bf16[128,2048]{1,0:T(8,128)(2,1)S(1)}, bf16[128,2048]{1,0:T(8,128)(2,1)S(1)}, u32[]{:S(2)}, u32[]{:S(2)}) %collective-permute-start.81) | collective-permute-done | bytes 524320 | tf_op jit(solution)/shard_map/ppermute | solution.py:190
  574.1 4.1 all-to-all-start.4
  578.3 2.5 fusion.11
  580.8 7.8 %collective-permute-done.82 = bf16[128,2048]{1,0:T(8,128)(2,1)S(1)} collective-permute-done((bf16[128,2048]{1,0:T(8,128)(2,1)S(1)}, bf16[128,2048]{1,0:T(8,128)(2,1)S(1)}, u32[]{:S(2)}, u32[]{:S(2)}) %collective-permute-start.82) | collective-permute-done | bytes 524320 | tf_op jit(solution)/shard_map/ppermute | solution.py:87
  (483 shorter events, 188.8 us)
Async XLA Ops:
  1.3 16.4 %collective-permute-start = (s32[1,384]{1,0:T(1,128)S(1)}, s32[1,384]{1,0:T(1,128)S(1)}, u32[]{:S(2)}, u32[]{:S(2)}) collective-permute-start(s32[1,384]{1,0:T(1,128)S(1)} %pad_add_fusion), channel_id=1, source_target_pairs={{0,4},{4,0},{1,5},{5,1},{2,6},{6,2},{3,7},{7,3},{8,12},{12,8},{9,1... | collective-permute-start | bytes 4616 | tf_op jit(solution)/shard_map/ppermute | solution.py:87
  4.3 34.5 %collective-permute-start.11 = (bf16[128,2048]{1,0:T(8,128)(2,1)}, bf16[128,2048]{1,0:T(8,128)(2,1)}, u32[]{:S(2)}, u32[]{:S(2)}) collective-permute-start(bf16[128,2048]{1,0:T(8,128)(2,1)} %param.12), channel_id=1, source_target_pairs={{0,1},{1,0},{2,3},{3,2},{4,5},{5,4},{6,7},{7,6},{8,9},{9,8},{10,11... | collective-permute-start | bytes 1572872 | tf_op jit(solution)/shard_map/ppermute | solution.py:87
  5.8 76.3 %collective-permute-start.12 = (bf16[128,2048]{1,0:T(8,128)(2,1)}, bf16[128,2048]{1,0:T(8,128)(2,1)}, u32[]{:S(2)}, u32[]{:S(2)}) collective-permute-start(bf16[128,2048]{1,0:T(8,128)(2,1)} %param.14), channel_id=1, source_target_pairs={{0,8},{8,16},{16,24},{24,0},{1,9},{9,17},{17,25},{25,1},{2,10},{10... | collective-permute-start | bytes 1572872 | tf_op jit(solution)/shard_map/ppermute | solution.py:190
  11.5 17.3 %collective-permute-start.1 = (bf16[64,1280]{1,0:T(8,128)(2,1)S(1)}, bf16[64,1280]{1,0:T(8,128)(2,1)S(1)}, u32[]{:S(2)}, u32[]{:S(2)}) collective-permute-start(bf16[64,1280]{1,0:T(8,128)(2,1)S(1)} %bitcast.686), channel_id=1, source_target_pairs={{0,1},{1,0},{4,5},{5,4},{2,3},{3,2},{6,7},{7,6},{8,9},{9,8},{12,13... | collective-permute-start | bytes 491528 | tf_op jit(solution)/shard_map/ppermute | solution.py:105
  12.1 16.7 %collective-permute-start.2 = (bf16[64,1280]{1,0:T(8,128)(2,1)S(1)}, bf16[64,1280]{1,0:T(8,128)(2,1)S(1)}, u32[]{:S(2)}, u32[]{:S(2)}) collective-permute-start(bf16[64,1280]{1,0:T(8,128)(2,1)S(1)} %bitcast.687), channel_id=1, source_target_pairs={{0,4},{1,5},{4,0},{5,1},{2,6},{3,7},{6,2},{7,3},{8,12},{9,13},{12,... | collective-permute-start | bytes 491528 | tf_op jit(solution)/shard_map/ppermute | solution.py:105
  24.2 13.7 %all-to-all-start = ((bf16[32,32,128]{2,1,0:T(8,128)(2,1)}), bf16[32,32,128]{2,1,0:T(8,128)(2,1)S(1)}, u32[]{:S(2)}, u32[]{:S(2)}) async-start(bf16[32,32,128]{2,1,0:T(8,128)(2,1)} %bitcast.280), calls=%async_computation | async-start | bytes 524288 | tf_op jit(solution)/shard_map/all_to_all | solution.py:96
  28.9 56.7 %collective-permute-start.6 = (bf16[128,2048]{1,0:T(8,128)(2,1)S(1)}, bf16[128,2048]{1,0:T(8,128)(2,1)}, u32[]{:S(2)}, u32[]{:S(2)}) collective-permute-start(bf16[128,2048]{1,0:T(8,128)(2,1)S(1)} %copy-done.11), channel_id=1, source_target_pairs={{0,5},{1,4},{4,1},{5,0},{2,7},{3,6},{6,3},{7,2},{8,13},{9,12},{12,... | collective-permute-start | bytes 1572872 | tf_op jit(solution)/shard_map/ppermute | solution.py:117
  31.6 54.6 %collective-permute-start.5 = (bf16[128,2048]{1,0:T(8,128)(2,1)S(1)}, bf16[128,2048]{1,0:T(8,128)(2,1)}, u32[]{:S(2)}, u32[]{:S(2)}) collective-permute-start(bf16[128,2048]{1,0:T(8,128)(2,1)S(1)} %copy-done.11), channel_id=1, source_target_pairs={{0,4},{1,5},{4,0},{5,1},{2,6},{3,7},{6,2},{7,3},{8,12},{9,13},{12,... | collective-permute-start | bytes 1572872 | tf_op jit(solution)/shard_map/ppermute | solution.py:117
  33.1 19.8 %collective-permute-start.7 = (bf16[256,1280]{1,0:T(8,128)(2,1)}, bf16[256,1280]{1,0:T(8,128)(2,1)}, u32[]{:S(2)}, u32[]{:S(2)}) collective-permute-start(bf16[256,1280]{1,0:T(8,128)(2,1)} %bitcast.18), channel_id=1, source_target_pairs={{0,8},{8,16},{16,24},{24,0},{1,9},{9,17},{17,25},{25,1},{2,10},{10... | collective-permute-start | bytes 1966088 | tf_op jit(solution)/shard_map/ppermute | solution.py:190
  38.8 41.3 %collective-permute-start.9 = (bf16[256,1280]{1,0:T(8,128)(2,1)}, bf16[256,1280]{1,0:T(8,128)(2,1)S(1)}, u32[]{:S(2)}, u32[]{:S(2)}) collective-permute-start(bf16[256,1280]{1,0:T(8,128)(2,1)} %bitcast.18), channel_id=1, source_target_pairs={{0,24},{8,0},{16,8},{24,16},{1,25},{9,1},{17,9},{25,17},{2,26},{10... | collective-permute-start | bytes 1966088 | tf_op jit(solution)/shard_map/ppermute | solution.py:190
  53.0 26.6 %collective-permute-start.8 = (bf16[256,1280]{1,0:T(8,128)(2,1)}, bf16[256,1280]{1,0:T(8,128)(2,1)S(1)}, u32[]{:S(2)}, u32[]{:S(2)}) collective-permute-start(bf16[256,1280]{1,0:T(8,128)(2,1)} %collective-permute-done.7), channel_id=1, source_target_pairs={{0,8},{8,16},{16,24},{24,0},{1,9},{9,17},{17,25},{25,1},{2,10},{10... | collective-permute-start | bytes 1966088 | tf_op jit(solution)/shard_map/ppermute | solution.py:190
  80.1 16.5 %collective-permute-start.10 = (bf16[8,128,1280]{2,1,0:T(8,128)(2,1)S(1)}, bf16[8,128,1280]{2,1,0:T(8,128)(2,1)S(1)}, u32[]{:S(2)}, u32[]{:S(2)}) collective-permute-start(bf16[8,128,1280]{2,1,0:T(8,128)(2,1)S(1)} %bitcast.621), channel_id=1, source_target_pairs={{0,2},{2,0},{1,3},{3,1},{4,6},{6,4},{5,7},{7,5},{8,10},{10,8},{9,1... | collective-permute-start | bytes 7864328 | tf_op jit(solution)/shard_map/ppermute | solution.py:87
  82.1 27.8 %collective-permute-start.14 = (bf16[128,2048]{1,0:T(8,128)(2,1)}, bf16[128,2048]{1,0:T(8,128)(2,1)}, u32[]{:S(2)}, u32[]{:S(2)}) collective-permute-start(bf16[128,2048]{1,0:T(8,128)(2,1)} %param.14), channel_id=1, source_target_pairs={{0,24},{8,0},{16,8},{24,16},{1,25},{9,1},{17,9},{25,17},{2,26},{10... | collective-permute-start | bytes 1572872 | tf_op jit(solution)/shard_map/ppermute | solution.py:190
  85.5 22.5 %collective-permute-start.13 = (bf16[128,2048]{1,0:T(8,128)(2,1)}, bf16[128,2048]{1,0:T(8,128)(2,1)}, u32[]{:S(2)}, u32[]{:S(2)}) collective-permute-start(bf16[128,2048]{1,0:T(8,128)(2,1)} %collective-permute-done.12), channel_id=1, source_target_pairs={{0,8},{8,16},{16,24},{24,0},{1,9},{9,17},{17,25},{25,1},{2,10},{10... | collective-permute-start | bytes 1572872 | tf_op jit(solution)/shard_map/ppermute | solution.py:190
  102.1 70.3 %all-to-all-start.1 = ((bf16[32,32,1152]{2,1,0:T(8,128)(2,1)}), bf16[32,32,1152]{2,1,0:T(8,128)(2,1)}, u32[]{:S(2)}, u32[]{:S(2)}) async-start(bf16[32,32,1152]{2,1,0:T(8,128)(2,1)} %bitcast.27), calls=%async_computation.1 | async-start | bytes 4718592 | tf_op jit(solution)/shard_map/all_to_all | solution.py:96
  114.6 29.4 %collective-permute-start.17 = (bf16[128,2048]{1,0:T(8,128)(2,1)}, bf16[128,2048]{1,0:T(8,128)(2,1)S(1)}, u32[]{:S(2)}, u32[]{:S(2)}) collective-permute-start(bf16[128,2048]{1,0:T(8,128)(2,1)} %get-tuple-element.299), channel_id=1, source_target_pairs={{0,5},{1,4},{4,1},{5,0},{2,7},{3,6},{6,3},{7,2},{8,13},{9,12},{12,... | collective-permute-start | bytes 1572872 | tf_op jit(solution)/shard_map/ppermute | solution.py:105
  117.0 39.2 %collective-permute-start.16 = (bf16[128,2048]{1,0:T(8,128)(2,1)}, bf16[128,2048]{1,0:T(8,128)(2,1)S(1)}, u32[]{:S(2)}, u32[]{:S(2)}) collective-permute-start(bf16[128,2048]{1,0:T(8,128)(2,1)} %get-tuple-element.300), channel_id=1, source_target_pairs={{0,4},{1,5},{4,0},{5,1},{2,6},{3,7},{6,2},{7,3},{8,12},{9,13},{12,... | collective-permute-start | bytes 1572872 | tf_op jit(solution)/shard_map/ppermute | solution.py:105
  117.5 41.0 %collective-permute-start.15 = (bf16[128,2048]{1,0:T(8,128)(2,1)S(1)}, bf16[128,2048]{1,0:T(8,128)(2,1)S(1)}, u32[]{:S(2)}, u32[]{:S(2)}) collective-permute-start(bf16[128,2048]{1,0:T(8,128)(2,1)S(1)} %get-tuple-element.301), channel_id=1, source_target_pairs={{0,1},{1,0},{4,5},{5,4},{2,3},{3,2},{6,7},{7,6},{8,9},{9,8},{12,13... | collective-permute-start | bytes 1572872 | tf_op jit(solution)/shard_map/ppermute | solution.py:105
  160.4 16.1 %collective-permute-start.18 = (bf16[2,256,2048]{2,1,0:T(8,128)(2,1)}, bf16[2,256,2048]{2,1,0:T(8,128)(2,1)S(1)}, u32[]{:S(2)}, u32[]{:S(2)}) collective-permute-start(bf16[2,256,2048]{2,1,0:T(8,128)(2,1)} %bitcast.45), channel_id=1, source_target_pairs={{0,2},{2,0},{1,3},{3,1},{4,6},{6,4},{5,7},{7,5},{8,10},{10,8},{9,1... | collective-permute-start | bytes 6291464 | tf_op jit(solution)/shard_map/ppermute | solution.py:87
  172.4 55.5 %all-to-all-start.2 = ((bf16[32,32,896]{2,1,0:T(8,128)(2,1)}), bf16[32,32,896]{2,1,0:T(8,128)(2,1)}, u32[]{:S(2)}, u32[]{:S(2)}) async-start(bf16[32,32,896]{2,1,0:T(8,128)(2,1)} %bitcast.28), calls=%async_computation.2 | async-start | bytes 3670016 | tf_op jit(solution)/shard_map/all_to_all | solution.py:96
  185.0 24.1 %collective-permute-start.19 = (bf16[128,2048]{1,0:T(8,128)(2,1)}, bf16[128,2048]{1,0:T(8,128)(2,1)}, u32[]{:S(2)}, u32[]{:S(2)}) collective-permute-start(bf16[128,2048]{1,0:T(8,128)(2,1)} %get-tuple-element.292), channel_id=1, source_target_pairs={{0,1},{1,0},{4,5},{5,4},{2,3},{3,2},{6,7},{7,6},{8,9},{9,8},{12,13... | collective-permute-start | bytes 1572872 | tf_op jit(solution)/shard_map/ppermute | solution.py:105
  186.7 35.5 %collective-permute-start.21 = (bf16[128,2048]{1,0:T(8,128)(2,1)}, bf16[128,2048]{1,0:T(8,128)(2,1)}, u32[]{:S(2)}, u32[]{:S(2)}) collective-permute-start(bf16[128,2048]{1,0:T(8,128)(2,1)} %get-tuple-element.293), channel_id=1, source_target_pairs={{0,5},{1,4},{4,1},{5,0},{2,7},{3,6},{6,3},{7,2},{8,13},{9,12},{12,... | collective-permute-start | bytes 1572872 | tf_op jit(solution)/shard_map/ppermute | solution.py:105
  188.2 34.1 %collective-permute-start.20 = (bf16[128,2048]{1,0:T(8,128)(2,1)S(1)}, bf16[128,2048]{1,0:T(8,128)(2,1)}, u32[]{:S(2)}, u32[]{:S(2)}) collective-permute-start(bf16[128,2048]{1,0:T(8,128)(2,1)S(1)} %get-tuple-element.294), channel_id=1, source_target_pairs={{0,4},{1,5},{4,0},{5,1},{2,6},{3,7},{6,2},{7,3},{8,12},{9,13},{12,... | collective-permute-start | bytes 1572872 | tf_op jit(solution)/shard_map/ppermute | solution.py:105
  225.3 18.7 %collective-permute-start.29 = (bf16[128,2048]{1,0:T(8,128)(2,1)S(1)}, bf16[128,2048]{1,0:T(8,128)(2,1)S(1)}, u32[]{:S(2)}, u32[]{:S(2)}) collective-permute-start(bf16[128,2048]{1,0:T(8,128)(2,1)S(1)} %multiply_convert_fusion.1), channel_id=1, source_target_pairs={{0,8},{8,16},{16,24},{24,0},{1,9},{9,17},{17,25},{25,1},{2,10},{10... | collective-permute-start | bytes 1572872 | tf_op jit(solution)/shard_map/rows_far1/ppermute | solution.py:190
  244.6 16.2 %collective-permute-start.31 = (bf16[2,32,2048]{2,1,0:T(8,128)(2,1)S(1)}, bf16[2,32,2048]{2,1,0:T(8,128)(2,1)S(1)}, u32[]{:S(2)}, u32[]{:S(2)}) collective-permute-start(bf16[2,32,2048]{2,1,0:T(8,128)(2,1)S(1)} %bitcast.682), channel_id=1, source_target_pairs={{0,4},{1,5},{4,0},{5,1},{2,6},{3,7},{6,2},{7,3},{8,12},{9,13},{12,... | collective-permute-start | bytes 786440 | tf_op jit(solution)/shard_map/rows_out1/ppermute | solution.py:198
  245.0 15.7 %collective-permute-start.32 = (bf16[2,32,2048]{2,1,0:T(8,128)(2,1)S(1)}, bf16[2,32,2048]{2,1,0:T(8,128)(2,1)S(1)}, u32[]{:S(2)}, u32[]{:S(2)}) collective-permute-start(bf16[2,32,2048]{2,1,0:T(8,128)(2,1)S(1)} %bitcast.679), channel_id=1, source_target_pairs={{0,5},{1,4},{4,1},{5,0},{2,7},{3,6},{6,3},{7,2},{8,13},{9,12},{12,... | collective-permute-start | bytes 786440 | tf_op jit(solution)/shard_map/rows_out1/ppermute | solution.py:198
  248.2 15.3 %collective-permute-start.34 = (bf16[128,2048]{1,0:T(8,128)(2,1)S(1)}, bf16[128,2048]{1,0:T(8,128)(2,1)S(1)}, u32[]{:S(2)}, u32[]{:S(2)}) collective-permute-start(bf16[128,2048]{1,0:T(8,128)(2,1)S(1)} %collective-permute-done.29), channel_id=1, source_target_pairs={{0,8},{8,16},{16,24},{24,0},{1,9},{9,17},{17,25},{25,1},{2,10},{10... | collective-permute-start | bytes 1572872 | tf_op jit(solution)/shard_map/rows_far2/ppermute | solution.py:190
  264.0 14.8 %collective-permute-start.36 = (bf16[2,32,2048]{2,1,0:T(8,128)(2,1)S(1)}, bf16[2,32,2048]{2,1,0:T(8,128)(2,1)S(1)}, u32[]{:S(2)}, u32[]{:S(2)}) collective-permute-start(bf16[2,32,2048]{2,1,0:T(8,128)(2,1)S(1)} %bitcast.683), channel_id=1, source_target_pairs={{0,4},{1,5},{4,0},{5,1},{2,6},{3,7},{6,2},{7,3},{8,12},{9,13},{12,... | collective-permute-start | bytes 786440 | tf_op jit(solution)/shard_map/rows_out2/ppermute | solution.py:198
  264.6 14.2 %collective-permute-start.37 = (bf16[2,32,2048]{2,1,0:T(8,128)(2,1)S(1)}, bf16[2,32,2048]{2,1,0:T(8,128)(2,1)S(1)}, u32[]{:S(2)}, u32[]{:S(2)}) collective-permute-start(bf16[2,32,2048]{2,1,0:T(8,128)(2,1)S(1)} %bitcast.680), channel_id=1, source_target_pairs={{0,5},{1,4},{4,1},{5,0},{2,7},{3,6},{6,3},{7,2},{8,13},{9,12},{12,... | collective-permute-start | bytes 786440 | tf_op jit(solution)/shard_map/rows_out2/ppermute | solution.py:198
  267.6 13.7 %collective-permute-start.39 = (bf16[128,2048]{1,0:T(8,128)(2,1)S(1)}, bf16[128,2048]{1,0:T(8,128)(2,1)S(1)}, u32[]{:S(2)}, u32[]{:S(2)}) collective-permute-start(bf16[128,2048]{1,0:T(8,128)(2,1)S(1)} %collective-permute-done.34), channel_id=1, source_target_pairs={{0,8},{8,16},{16,24},{24,0},{1,9},{9,17},{17,25},{25,1},{2,10},{10... | collective-permute-start | bytes 1572872 | tf_op jit(solution)/shard_map/rows_far3/ppermute | solution.py:190
  279.8 17.2 %collective-permute-start.44 = (bf16[2,2,32,2176]{3,2,1,0:T(8,128)(2,1)S(1)}, bf16[2,2,32,2176]{3,2,1,0:T(8,128)(2,1)S(1)}, u32[]{:S(2)}, u32[]{:S(2)}) collective-permute-start(bf16[2,2,32,2176]{3,2,1,0:T(8,128)(2,1)S(1)} %get-tuple-element.343), channel_id=1, source_target_pairs={{0,2},{2,0},{1,3},{3,1},{4,6},{6,4},{5,7},{7,5},{8,10},{10,8},{9,1... | collective-permute-start | bytes 1671176 | tf_op jit(solution)/shard_map/rows_back1/ppermute | solution.py:87
  281.8 13.8 %collective-permute-start.41 = (bf16[2,32,2048]{2,1,0:T(8,128)(2,1)S(1)}, bf16[2,32,2048]{2,1,0:T(8,128)(2,1)S(1)}, u32[]{:S(2)}, u32[]{:S(2)}) collective-permute-start(bf16[2,32,2048]{2,1,0:T(8,128)(2,1)S(1)} %bitcast.685), channel_id=1, source_target_pairs={{0,4},{1,5},{4,0},{5,1},{2,6},{3,7},{6,2},{7,3},{8,12},{9,13},{12,... | collective-permute-start | bytes 786440 | tf_op jit(solution)/shard_map/rows_out3/ppermute | solution.py:198
  296.6 14.8 %collective-permute-start.48 = (bf16[2,2,32,2176]{3,2,1,0:T(8,128)(2,1)S(1)}, bf16[2,2,32,2176]{3,2,1,0:T(8,128)(2,1)S(1)}, u32[]{:S(2)}, u32[]{:S(2)}) collective-permute-start(bf16[2,2,32,2176]{3,2,1,0:T(8,128)(2,1)S(1)} %get-tuple-element.337), channel_id=1, source_target_pairs={{0,2},{2,0},{1,3},{3,1},{4,6},{6,4},{5,7},{7,5},{8,10},{10,8},{9,1... | collective-permute-start | bytes 1671176 | tf_op jit(solution)/shard_map/rows_back2/ppermute | solution.py:87
  297.1 16.6 %collective-permute-start.47 = (bf16[2,32,2176]{2,1,0:T(8,128)(2,1)S(1)}, bf16[2,32,2176]{2,1,0:T(8,128)(2,1)S(1)}, u32[]{:S(2)}, u32[]{:S(2)}) collective-permute-start(bf16[2,32,2176]{2,1,0:T(8,128)(2,1)S(1)} %get-tuple-element.339), channel_id=1, source_target_pairs={{0,5},{1,4},{4,1},{5,0},{2,7},{3,6},{6,3},{7,2},{8,13},{9,12},{12,... | collective-permute-start | bytes 835592 | tf_op jit(solution)/shard_map/rows_back1/ppermute | solution.py:105
  298.7 15.4 %collective-permute-start.45 = (bf16[2,32,2176]{2,1,0:T(8,128)(2,1)S(1)}, bf16[2,32,2176]{2,1,0:T(8,128)(2,1)S(1)}, u32[]{:S(2)}, u32[]{:S(2)}) collective-permute-start(bf16[2,32,2176]{2,1,0:T(8,128)(2,1)S(1)} %get-tuple-element.341), channel_id=1, source_target_pairs={{0,1},{1,0},{4,5},{5,4},{2,3},{3,2},{6,7},{7,6},{8,9},{9,8},{12,13... | collective-permute-start | bytes 835592 | tf_op jit(solution)/shard_map/rows_back1/ppermute | solution.py:105
  299.2 16.4 %collective-permute-start.46 = (bf16[2,32,2176]{2,1,0:T(8,128)(2,1)S(1)}, bf16[2,32,2176]{2,1,0:T(8,128)(2,1)S(1)}, u32[]{:S(2)}, u32[]{:S(2)}) collective-permute-start(bf16[2,32,2176]{2,1,0:T(8,128)(2,1)S(1)} %get-tuple-element.342), channel_id=1, source_target_pairs={{0,4},{1,5},{4,0},{5,1},{2,6},{3,7},{6,2},{7,3},{8,12},{9,13},{12,... | collective-permute-start | bytes 835592 | tf_op jit(solution)/shard_map/rows_back1/ppermute | solution.py:105
  311.2 19.6 %collective-permute-start.56 = (bf16[2,2,32,2176]{3,2,1,0:T(8,128)(2,1)S(1)}, bf16[2,2,32,2176]{3,2,1,0:T(8,128)(2,1)S(1)}, u32[]{:S(2)}, u32[]{:S(2)}) collective-permute-start(bf16[2,2,32,2176]{3,2,1,0:T(8,128)(2,1)S(1)} %get-tuple-element.325), channel_id=1, source_target_pairs={{0,2},{2,0},{1,3},{3,1},{4,6},{6,4},{5,7},{7,5},{8,10},{10,8},{9,1... | collective-permute-start | bytes 1671176 | tf_op jit(solution)/shard_map/rows_back3/ppermute | solution.py:87
  327.9 19.1 %collective-permute-start.61 = (bf16[128,2176]{1,0:T(8,128)(2,1)S(1)}, bf16[128,2176]{1,0:T(8,128)(2,1)S(1)}, u32[]{:S(2)}, u32[]{:S(2)}) collective-permute-start(bf16[128,2176]{1,0:T(8,128)(2,1)S(1)} %fusion.7), channel_id=1, source_target_pairs={{0,24},{8,0},{16,8},{24,16},{1,25},{9,1},{17,9},{25,17},{2,26},{10... | collective-permute-start | bytes 1671176 | tf_op jit(solution)/shard_map/partial_far/ppermute | solution.py:190
  332.5 14.0 %collective-permute-start.58 = (bf16[2,32,2176]{2,1,0:T(8,128)(2,1)S(1)}, bf16[2,32,2176]{2,1,0:T(8,128)(2,1)S(1)}, u32[]{:S(2)}, u32[]{:S(2)}) collective-permute-start(bf16[2,32,2176]{2,1,0:T(8,128)(2,1)S(1)} %get-tuple-element.323), channel_id=1, source_target_pairs={{0,4},{1,5},{4,0},{5,1},{2,6},{3,7},{6,2},{7,3},{8,12},{9,13},{12,... | collective-permute-start | bytes 835592 | tf_op jit(solution)/shard_map/rows_back3/ppermute | solution.py:105
  334.7 16.3 %collective-permute-start.52 = (bf16[2,2,32,2176]{3,2,1,0:T(8,128)(2,1)S(1)}, bf16[2,2,32,2176]{3,2,1,0:T(8,128)(2,1)S(1)}, u32[]{:S(2)}, u32[]{:S(2)}) collective-permute-start(bf16[2,2,32,2176]{3,2,1,0:T(8,128)(2,1)S(1)} %get-tuple-element.331), channel_id=1, source_target_pairs={{0,2},{2,0},{1,3},{3,1},{4,6},{6,4},{5,7},{7,5},{8,10},{10,8},{9,1... | collective-permute-start | bytes 1671176 | tf_op jit(solution)/shard_map/rows_back0/ppermute | solution.py:87
  346.9 17.4 %collective-permute-start.60 = (bf16[128,2176]{1,0:T(8,128)(2,1)S(1)}, bf16[128,2176]{1,0:T(8,128)(2,1)S(1)}, u32[]{:S(2)}, u32[]{:S(2)}) collective-permute-start(bf16[128,2176]{1,0:T(8,128)(2,1)S(1)} %fusion.8), channel_id=1, source_target_pairs={{0,8},{8,16},{16,24},{24,0},{1,9},{9,17},{17,25},{25,1},{2,10},{10... | collective-permute-start | bytes 1671176 | tf_op jit(solution)/shard_map/partial_far/ppermute | solution.py:190
  347.1 24.2 %collective-permute-start.62 = (bf16[128,2176]{1,0:T(8,128)(2,1)S(1)}, bf16[128,2176]{1,0:T(8,128)(2,1)S(1)}, u32[]{:S(2)}, u32[]{:S(2)}) collective-permute-start(bf16[128,2176]{1,0:T(8,128)(2,1)S(1)} %add_convert_fusion), channel_id=1, source_target_pairs={{0,24},{8,0},{16,8},{24,16},{1,25},{9,1},{17,9},{25,17},{2,26},{10... | collective-permute-start | bytes 1671176 | tf_op jit(solution)/shard_map/partial_far/ppermute | solution.py:190
  373.6 22.4 %collective-permute-start.65 = (bf16[128,2048]{1,0:T(8,128)(2,1)S(1)}, bf16[128,2048]{1,0:T(8,128)(2,1)S(1)}, u32[]{:S(2)}, u32[]{:S(2)}) collective-permute-start(bf16[128,2048]{1,0:T(8,128)(2,1)S(1)} %fusion.47), channel_id=1, source_target_pairs={{0,5},{1,4},{4,1},{5,0},{2,7},{3,6},{6,3},{7,2},{8,13},{9,12},{12,... | collective-permute-start | bytes 1572872 | tf_op jit(solution)/shard_map/ppermute | solution.py:117
  376.0 22.0 %collective-permute-start.64 = (bf16[128,2048]{1,0:T(8,128)(2,1)S(1)}, bf16[128,2048]{1,0:T(8,128)(2,1)S(1)}, u32[]{:S(2)}, u32[]{:S(2)}) collective-permute-start(bf16[128,2048]{1,0:T(8,128)(2,1)S(1)} %fusion.47), channel_id=1, source_target_pairs={{0,4},{1,5},{4,0},{5,1},{2,6},{3,7},{6,2},{7,3},{8,12},{9,13},{12,... | collective-permute-start | bytes 1572872 | tf_op jit(solution)/shard_map/ppermute | solution.py:117
  376.9 21.2 %collective-permute-start.63 = (bf16[128,2048]{1,0:T(8,128)(2,1)S(1)}, bf16[128,2048]{1,0:T(8,128)(2,1)S(1)}, u32[]{:S(2)}, u32[]{:S(2)}) collective-permute-start(bf16[128,2048]{1,0:T(8,128)(2,1)S(1)} %fusion.47), channel_id=1, source_target_pairs={{0,1},{1,0},{4,5},{5,4},{2,3},{3,2},{6,7},{7,6},{8,9},{9,8},{12,13... | collective-permute-start | bytes 1572872 | tf_op jit(solution)/shard_map/ppermute | solution.py:117
  409.9 24.3 %collective-permute-start.69 = (bf16[128,2048]{1,0:T(8,128)(2,1)}, bf16[128,2048]{1,0:T(8,128)(2,1)S(1)}, u32[]{:S(2)}, u32[]{:S(2)}) collective-permute-start(bf16[128,2048]{1,0:T(8,128)(2,1)} %get-tuple-element.284), channel_id=1, source_target_pairs={{0,5},{1,4},{4,1},{5,0},{2,7},{3,6},{6,3},{7,2},{8,13},{9,12},{12,... | collective-permute-start | bytes 1572872 | tf_op jit(solution)/shard_map/ppermute | solution.py:105
  411.7 24.5 %collective-permute-start.68 = (bf16[128,2048]{1,0:T(8,128)(2,1)}, bf16[128,2048]{1,0:T(8,128)(2,1)}, u32[]{:S(2)}, u32[]{:S(2)}) collective-permute-start(bf16[128,2048]{1,0:T(8,128)(2,1)} %get-tuple-element.285), channel_id=1, source_target_pairs={{0,4},{1,5},{4,0},{5,1},{2,6},{3,7},{6,2},{7,3},{8,12},{9,13},{12,... | collective-permute-start | bytes 1572872 | tf_op jit(solution)/shard_map/ppermute | solution.py:105
  413.1 23.2 %collective-permute-start.67 = (bf16[128,2048]{1,0:T(8,128)(2,1)}, bf16[128,2048]{1,0:T(8,128)(2,1)}, u32[]{:S(2)}, u32[]{:S(2)}) collective-permute-start(bf16[128,2048]{1,0:T(8,128)(2,1)} %get-tuple-element.286), channel_id=1, source_target_pairs={{0,1},{1,0},{4,5},{5,4},{2,3},{3,2},{6,7},{7,6},{8,9},{9,8},{12,13... | collective-permute-start | bytes 1572872 | tf_op jit(solution)/shard_map/ppermute | solution.py:105
  445.6 16.1 %collective-permute-start.70 = (bf16[8,128,1280]{2,1,0:T(8,128)(2,1)}, bf16[8,128,1280]{2,1,0:T(8,128)(2,1)}, u32[]{:S(2)}, u32[]{:S(2)}) collective-permute-start(bf16[8,128,1280]{2,1,0:T(8,128)(2,1)} %fusion.9), channel_id=1, source_target_pairs={{0,2},{2,0},{1,3},{3,1},{4,6},{6,4},{5,7},{7,5},{8,10},{10,8},{9,1... | collective-permute-start | bytes 7864328 | tf_op jit(solution)/shard_map/ppermute | solution.py:87
  445.9 66.7 %all-to-all-start.3 = ((bf16[8,4,32,2048]{3,2,1,0:T(8,128)(2,1)}), bf16[8,4,32,2048]{3,2,1,0:T(8,128)(2,1)}, u32[]{:S(2)}, u32[]{:S(2)}) async-start(bf16[8,4,32,2048]{3,2,1,0:T(8,128)(2,1)} %pad_maximum_fusion.3), calls=%async_computation.3 | async-start | bytes 8388608 | tf_op jit(solution)/shard_map/all_to_all | solution.py:96
  451.9 16.6 %collective-permute-start.72 = (bf16[128,2048]{1,0:T(8,128)(2,1)S(1)}, bf16[128,2048]{1,0:T(8,128)(2,1)S(1)}, u32[]{:S(2)}, u32[]{:S(2)}) collective-permute-start(bf16[128,2048]{1,0:T(8,128)(2,1)S(1)} %get-tuple-element.282), channel_id=1, source_target_pairs={{0,8},{8,16},{16,24},{24,0},{1,9},{9,17},{17,25},{25,1},{2,10},{10... | collective-permute-start | bytes 1572872 | tf_op jit(solution)/shard_map/ppermute | solution.py:190
  452.0 25.6 %collective-permute-start.71 = (bf16[128,2048]{1,0:T(8,128)(2,1)S(1)}, bf16[128,2048]{1,0:T(8,128)(2,1)S(1)}, u32[]{:S(2)}, u32[]{:S(2)}) collective-permute-start(bf16[128,2048]{1,0:T(8,128)(2,1)S(1)} %get-tuple-element.283), channel_id=1, source_target_pairs={{0,24},{8,0},{16,8},{24,16},{1,25},{9,1},{17,9},{25,17},{2,26},{10... | collective-permute-start | bytes 1572872 | tf_op jit(solution)/shard_map/ppermute | solution.py:190
  479.1 14.9 %collective-permute-start.86 = (bf16[128,2048]{1,0:T(8,128)(2,1)S(1)}, bf16[128,2048]{1,0:T(8,128)(2,1)S(1)}, u32[]{:S(2)}, u32[]{:S(2)}) collective-permute-start(bf16[128,2048]{1,0:T(8,128)(2,1)S(1)} %add_convert_fusion.1), channel_id=1, source_target_pairs={{0,24},{8,0},{16,8},{24,16},{1,25},{9,1},{17,9},{25,17},{2,26},{10... | collective-permute-start | bytes 1572872 | tf_op jit(solution)/shard_map/ppermute | solution.py:190
  482.3 25.5 %collective-permute-start.74 = (bf16[256,1280]{1,0:T(8,128)(2,1)S(1)}, bf16[256,1280]{1,0:T(8,128)(2,1)S(1)}, u32[]{:S(2)}, u32[]{:S(2)}) collective-permute-start(bf16[256,1280]{1,0:T(8,128)(2,1)S(1)} %get-tuple-element.277), channel_id=1, source_target_pairs={{0,24},{8,0},{16,8},{24,16},{1,25},{9,1},{17,9},{25,17},{2,26},{10... | collective-permute-start | bytes 1966088 | tf_op jit(solution)/shard_map/ppermute | solution.py:190
  485.3 53.5 %collective-permute-start.78 = (bf16[128,2048]{1,0:T(8,128)(2,1)}, bf16[128,2048]{1,0:T(8,128)(2,1)}, u32[]{:S(2)}, u32[]{:S(2)}) collective-permute-start(bf16[128,2048]{1,0:T(8,128)(2,1)} %get-tuple-element.278), channel_id=1, source_target_pairs={{0,5},{1,4},{4,1},{5,0},{2,7},{3,6},{6,3},{7,2},{8,13},{9,12},{12,... | collective-permute-start | bytes 1572872 | tf_op jit(solution)/shard_map/ppermute | solution.py:105
  487.9 50.9 %collective-permute-start.77 = (bf16[128,2048]{1,0:T(8,128)(2,1)}, bf16[128,2048]{1,0:T(8,128)(2,1)}, u32[]{:S(2)}, u32[]{:S(2)}) collective-permute-start(bf16[128,2048]{1,0:T(8,128)(2,1)} %get-tuple-element.279), channel_id=1, source_target_pairs={{0,4},{1,5},{4,0},{5,1},{2,6},{3,7},{6,2},{7,3},{8,12},{9,13},{12,... | collective-permute-start | bytes 1572872 | tf_op jit(solution)/shard_map/ppermute | solution.py:105
  487.9 50.9 %collective-permute-start.76 = (bf16[128,2048]{1,0:T(8,128)(2,1)}, bf16[128,2048]{1,0:T(8,128)(2,1)}, u32[]{:S(2)}, u32[]{:S(2)}) collective-permute-start(bf16[128,2048]{1,0:T(8,128)(2,1)} %get-tuple-element.280), channel_id=1, source_target_pairs={{0,1},{1,0},{4,5},{5,4},{2,3},{3,2},{6,7},{7,6},{8,9},{9,8},{12,13... | collective-permute-start | bytes 1572872 | tf_op jit(solution)/shard_map/ppermute | solution.py:105
  493.9 30.0 %collective-permute-start.73 = (bf16[256,1280]{1,0:T(8,128)(2,1)}, bf16[256,1280]{1,0:T(8,128)(2,1)}, u32[]{:S(2)}, u32[]{:S(2)}) collective-permute-start(bf16[256,1280]{1,0:T(8,128)(2,1)} %get-tuple-element.276), channel_id=1, source_target_pairs={{0,8},{8,16},{16,24},{24,0},{1,9},{9,17},{17,25},{25,1},{2,10},{10... | collective-permute-start | bytes 1966088 | tf_op jit(solution)/shard_map/ppermute | solution.py:190
  508.0 28.8 %collective-permute-start.75 = (bf16[256,1280]{1,0:T(8,128)(2,1)S(1)}, bf16[256,1280]{1,0:T(8,128)(2,1)S(1)}, u32[]{:S(2)}, u32[]{:S(2)}) collective-permute-start(bf16[256,1280]{1,0:T(8,128)(2,1)S(1)} %fusion.15), channel_id=1, source_target_pairs={{0,24},{8,0},{16,8},{24,16},{1,25},{9,1},{17,9},{25,17},{2,26},{10... | collective-permute-start | bytes 1966088 | tf_op jit(solution)/shard_map/ppermute | solution.py:190
  523.9 30.2 %collective-permute-start.80 = (bf16[128,2048]{1,0:T(8,128)(2,1)}, bf16[128,2048]{1,0:T(8,128)(2,1)}, u32[]{:S(2)}, u32[]{:S(2)}) collective-permute-start(bf16[128,2048]{1,0:T(8,128)(2,1)} %convolution_convert_fusion.11), channel_id=1, source_target_pairs={{0,24},{8,0},{16,8},{24,16},{1,25},{9,1},{17,9},{25,17},{2,26},{10... | collective-permute-start | bytes 1572872 | tf_op jit(solution)/shard_map/ppermute | solution.py:190
  536.8 23.7 %collective-permute-start.79 = (bf16[128,2048]{1,0:T(8,128)(2,1)}, bf16[128,2048]{1,0:T(8,128)(2,1)}, u32[]{:S(2)}, u32[]{:S(2)}) collective-permute-start(bf16[128,2048]{1,0:T(8,128)(2,1)} %convolution_convert_fusion.13), channel_id=1, source_target_pairs={{0,8},{8,16},{16,24},{24,0},{1,9},{9,17},{17,25},{25,1},{2,10},{10... | collective-permute-start | bytes 1572872 | tf_op jit(solution)/shard_map/ppermute | solution.py:190
  556.7 13.8 %collective-permute-start.81 = (bf16[128,2048]{1,0:T(8,128)(2,1)S(1)}, bf16[128,2048]{1,0:T(8,128)(2,1)S(1)}, u32[]{:S(2)}, u32[]{:S(2)}) collective-permute-start(bf16[128,2048]{1,0:T(8,128)(2,1)S(1)} %add_convert_fusion.3), channel_id=1, source_target_pairs={{0,24},{8,0},{16,8},{24,16},{1,25},{9,1},{17,9},{25,17},{2,26},{10... | collective-permute-start | bytes 1572872 | tf_op jit(solution)/shard_map/ppermute | solution.py:190
  572.6 16.0 %collective-permute-start.82 = (bf16[128,2048]{1,0:T(8,128)(2,1)S(1)}, bf16[128,2048]{1,0:T(8,128)(2,1)S(1)}, u32[]{:S(2)}, u32[]{:S(2)}) collective-permute-start(bf16[128,2048]{1,0:T(8,128)(2,1)S(1)} %add_convert_fusion.2), channel_id=1, source_target_pairs={{0,1},{1,0},{2,3},{3,2},{4,5},{5,4},{6,7},{7,6},{8,9},{9,8},{10,11... | collective-permute-start | bytes 1572872 | tf_op jit(solution)/shard_map/ppermute | solution.py:87
  574.1 16.9 %all-to-all-start.4 = ((f32[32,24,128]{2,1,0:T(8,128)}), f32[32,24,128]{2,1,0:T(8,128)S(1)}, u32[]{:S(2)}, u32[]{:S(2)}) async-start(f32[32,24,128]{2,1,0:T(8,128)} %bitcast.288), calls=%async_computation.4 | async-start | bytes 786432 | tf_op jit(solution)/shard_map/all_to_all | solution.py:96
  (90 other events, 629.4 us)

commit v12 on v11

--- a/solution.py
+++ b/solution.py
@@ -357,7 +357,7 @@
     allowed = (key_row_ref[0] <= row_ref[0]) & (key_row_ref[0] >= start_ref[0])
     scores = jnp.where(allowed, scores, -1e30)
     exped = jnp.exp(scores - jnp.max(scores, axis=-1, keepdims=True))
-    return exped / jnp.sum(exped, axis=-1, keepdims=True)
+    return exped * (1.0 / jnp.sum(exped, axis=-1, keepdims=True))
 
 
 def attend_kernel(
@@ -414,14 +414,14 @@
         score_grad = (
             probs * (prob_grad - jnp.sum(probs * prob_grad, axis=-1, keepdims=True))
         ).astype(BF)
-        key_total[...] += mm_tn(score_grad, query) * score_scale
+        key_total[...] += mm_tn(score_grad, query)
         query_grad = mm(score_grad, key_low[...]) * score_scale
         query_out[:, lanes] = raw_grad(query_grad, normal, scale, qgain_ref, qgain_out).astype(BF)
 
     @pl.when(head == pl.num_programs(1) - 1)
     def _():
         key_normal, key_scale, _ = head_normed(key_ref[...], kgain_ref)
-        key_out[...] = raw_grad(key_total[...], key_normal, key_scale, kgain_ref, kgain_out).astype(BF)
+        key_out[...] = raw_grad(key_total[...] * score_scale, key_normal, key_scale, kgain_ref, kgain_out).astype(BF)
         value_out[...] = value_total[...].astype(BF)
 
 

time: 601 us -> 601 us (level)
  no operation moved by 1% of the time
where the time goes in v12:
time: 601 us; the launch traced here: 593 us
  waiting for transfers between devices  232 us (39%)
  starting transfers between devices  125 us (21%)
  Pallas kernels  86.6 us (14%)
  local copies, waits for them, and re-layouts  51.8 us (9%)
  other arithmetic  48.3 us (8%)
  matrix products  46.2 us (8%)
    ppermute x24, waiting for transfers between devices, far_shift(): lax.ppermute(value, FAR_AXIS, [(i, (i + step) % count) for i in range(cou...  108 us
    ppermute x30, waiting for transfers between devices, quad_send(): return lax.ppermute(block, HEAD_AXES, [(i, i ^ step) for i in range(4)])  97.3 us
    dot_general x30, matrix products, dot(): lax.dot_general(left, right, (dims, ((), ())), preferred_element_type=F32)  43.8 us
    ppermute x24, starting transfers between devices, far_shift(): lax.ppermute(value, FAR_AXIS, [(i, (i + step) % count) for i in range(cou...  41.7 us
    pallas_call x4, Pallas kernels, expert_chunk(): pl.pallas_call(expert_kernel, grid_spec=pltpu.PrefetchScalarGridSpec(num_...  40.1 us
    ppermute x30, starting transfers between devices, quad_send(): return lax.ppermute(block, HEAD_AXES, [(i, i ^ step) for i in range(4)])  35.3 us
    all_to_all x5, starting transfers between devices, exchange(): return lax.all_to_all(value, axes, split_axis=0, concat_axis=0, tiled=True)  19.8 us
    pallas_call x1, Pallas kernels, expert_grads(): pl.pallas_call(functools.partial(expert_grad_kernel, count), grid=(D // t...  18.8 us
  transfers between devices with their start and end apart: 92, of which 42 were waited for; matrix products, arithmetic and copies ran while one was open for 19% of the time, Pallas kernels for 15%

profile of v12, /device:TPU:0, one launch (start us, length us, event | category | flops | bytes accessed | tf_op | source)
XLA Modules:
  0.0 592.6 jit_solution(17025216424950794293)
XLA Ops:
  1.3 3.0 collective-permute-start
  17.8 2.5 collective-permute-start.3
  24.2 2.9 all-to-all-start
  28.9 2.7 collective-permute-start.6
  41.9 11.1 %collective-permute-done.7 = bf16[256,1280]{1,0:T(8,128)(2,1)} collective-permute-done((bf16[256,1280]{1,0:T(8,128)(2,1)}, bf16[256,1280]{1,0:T(8,128)(2,1)}, u32[]{:S(2)}, u32[]{:S(2)}) %collective-permute-start.7) | collective-permute-done | bytes 655392 | tf_op jit(solution)/shard_map/ppermute | solution.py:190
  56.3 23.2 %collective-permute-done.8 = bf16[256,1280]{1,0:T(8,128)(2,1)S(1)} collective-permute-done((bf16[256,1280]{1,0:T(8,128)(2,1)}, bf16[256,1280]{1,0:T(8,128)(2,1)S(1)}, u32[]{:S(2)}, u32[]{:S(2)}) %collective-permute-start.8) | collective-permute-done | bytes 655392 | tf_op jit(solution)/shard_map/ppermute | solution.py:190
  86.2 5.8 collective-permute-done.4
  97.8 4.4 fusion.168.query_ref.key_ref.value_ref
  102.1 4.3 all-to-all-start.1
  111.9 2.7 dynamic-slice_bitcast_fusion.17
  114.6 2.4 collective-permute-start.17
  120.6 10.9 %attend.1 = bf16[512,1024]{1,0:T(8,128)(2,1)} custom-call(f32[512,1280]{1,0:T(8,128)} %fusion.168.query_ref.key_ref.value_ref, f32[512,1280]{1,0:T(8,128)} %fusion.168.query_ref.key_ref.value_ref, f32[512,1280]{1,0:T(8,128)} %fusion.168.query_ref.key_ref.value_ref, f32[512,128]{1,0:T(8,128)} %get-tuple-element.446.cos_ref, ...), custom_call_target="tpu_custom_call" | custom-call | flops 1048576 | bytes 1048576 | tf_op jit(solution)/shard_map/attend/pallas_call | solution.py:446
  131.5 12.5 %collective-permute-done.17 = bf16[128,2048]{1,0:T(8,128)(2,1)S(1)} collective-permute-done((bf16[128,2048]{1,0:T(8,128)(2,1)}, bf16[128,2048]{1,0:T(8,128)(2,1)S(1)}, u32[]{:S(2)}, u32[]{:S(2)}) %collective-permute-start.17) | collective-permute-done | bytes 524320 | tf_op jit(solution)/shard_map/ppermute | solution.py:105
  144.0 12.2 %collective-permute-done.16 = bf16[128,2048]{1,0:T(8,128)(2,1)S(1)} collective-permute-done((bf16[128,2048]{1,0:T(8,128)(2,1)}, bf16[128,2048]{1,0:T(8,128)(2,1)S(1)}, u32[]{:S(2)}, u32[]{:S(2)}) %collective-permute-start.16) | collective-permute-done | bytes 524320 | tf_op jit(solution)/shard_map/ppermute | solution.py:105
  162.7 2.8 collective-permute-start.24
  167.0 5.4 collective-permute-done.23
  172.4 3.9 all-to-all-start.2
  177.8 2.5 select_bitcast_fusion.3
  190.9 18.2 %collective-permute-done.19 = bf16[128,2048]{1,0:T(8,128)(2,1)} collective-permute-done((bf16[128,2048]{1,0:T(8,128)(2,1)}, bf16[128,2048]{1,0:T(8,128)(2,1)}, u32[]{:S(2)}, u32[]{:S(2)}) %collective-permute-start.19) | collective-permute-done | bytes 524320 | tf_op jit(solution)/shard_map/ppermute | solution.py:105
  209.1 13.2 %collective-permute-done.21 = bf16[128,2048]{1,0:T(8,128)(2,1)} collective-permute-done((bf16[128,2048]{1,0:T(8,128)(2,1)}, bf16[128,2048]{1,0:T(8,128)(2,1)}, u32[]{:S(2)}, u32[]{:S(2)}) %collective-permute-start.21) | collective-permute-done | bytes 524320 | tf_op jit(solution)/shard_map/ppermute | solution.py:105
  225.3 2.6 collective-permute-start.29
  229.3 3.7 collective-permute-start.27
  233.0 2.9 pad_maximum_fusion.2
  236.4 6.1 %collective-permute-done.26 = bf16[2,32,2048]{2,1,0:T(8,128)(2,1)S(1)} collective-permute-done((bf16[2,32,2048]{2,1,0:T(8,128)(2,1)S(1)}, bf16[2,32,2048]{2,1,0:T(8,128)(2,1)S(1)}, u32[]{:S(2)}, u32[]{:S(2)}) %collective-permute-start.26) | collective-permute-done | bytes 262176 | tf_op jit(solution)/shard_map/rows_out0/ppermute | solution.py:198
  245.0 2.5 collective-permute-start.32
  248.2 2.4 collective-permute-start.34
  250.8 10.0 %expert_chunk.4 = (bf16[256,768]{1,0:T(8,128)(2,1)S(1)}, bf16[256,768]{1,0:T(8,128)(2,1)S(1)}, bf16[256,768]{1,0:T(8,128)(2,1)S(1)}, bf16[256,2048]{1,0:T(8,128)...) custom-call(s32[2]{0:T(128)S(1)} %pad_add_fusion.2.here_ref, bf16[256,2048]{1,0:T(8,128)(2,1)S(1)} %bitcast.582, ...), custom_call_target="tpu_custom_call" | custom-call | flops 1048576 | bytes 1048576 | tf_op jit(solution)/shard_map/expert_chunk/pallas_call | solution.py:276
  268.8 10.0 %expert_chunk.5 = (bf16[256,768]{1,0:T(8,128)(2,1)S(1)}, bf16[256,768]{1,0:T(8,128)(2,1)S(1)}, bf16[256,768]{1,0:T(8,128)(2,1)S(1)}, bf16[256,2048]{1,0:T(8,128)...) custom-call(s32[2]{0:T(128)S(1)} %pad_add_fusion.2.here_ref, bf16[256,2048]{1,0:T(8,128)(2,1)S(1)} %bitcast.584, ...), custom_call_target="tpu_custom_call" | custom-call | flops 1048576 | bytes 1048576 | tf_op jit(solution)/shard_map/expert_chunk/pallas_call | solution.py:276
  285.6 10.0 %expert_chunk.6 = (bf16[256,768]{1,0:T(8,128)(2,1)S(1)}, bf16[256,768]{1,0:T(8,128)(2,1)S(1)}, bf16[256,768]{1,0:T(8,128)(2,1)S(1)}, bf16[256,2048]{1,0:T(8,128)...) custom-call(s32[2]{0:T(128)S(1)} %pad_add_fusion.2.here_ref, bf16[256,2048]{1,0:T(8,128)(2,1)S(1)} %bitcast.586, ...), custom_call_target="tpu_custom_call" | custom-call | flops 1048576 | bytes 1048576 | tf_op jit(solution)/shard_map/expert_chunk/pallas_call | solution.py:276
  300.9 10.2 %expert_chunk.7 = (bf16[256,768]{1,0:T(8,128)(2,1)S(1)}, bf16[256,768]{1,0:T(8,128)(2,1)S(1)}, bf16[256,768]{1,0:T(8,128)(2,1)S(1)}, bf16[256,2048]{1,0:T(8,128)...) custom-call(s32[2]{0:T(128)S(1)} %pad_add_fusion.2.here_ref, bf16[256,2048]{1,0:T(8,128)(2,1)S(1)} %bitcast.588, ...), custom_call_target="tpu_custom_call" | custom-call | flops 1048576 | bytes 1048576 | tf_op jit(solution)/shard_map/expert_chunk/pallas_call | solution.py:276
  316.1 6.6 %collective-permute-done.51 = bf16[2,32,2176]{2,1,0:T(8,128)(2,1)S(1)} collective-permute-done((bf16[2,32,2176]{2,1,0:T(8,128)(2,1)S(1)}, bf16[2,32,2176]{2,1,0:T(8,128)(2,1)S(1)}, u32[]{:S(2)}, u32[]{:S(2)}) %collective-permute-start.51) | collective-permute-done | bytes 278560 | tf_op jit(solution)/shard_map/rows_back2/ppermute | solution.py:105
  322.6 4.0 collective-permute-done.49
  327.9 3.0 collective-permute-start.61
  334.7 5.9 collective-permute-done.57
  340.6 5.9 collective-permute-done.58
  347.1 3.9 collective-permute-start.62
  355.0 4.8 collective-permute-done.53
  359.9 4.4 collective-permute-done.54
  364.3 7.0 %collective-permute-done.62 = bf16[128,2176]{1,0:T(8,128)(2,1)S(1)} collective-permute-done((bf16[128,2176]{1,0:T(8,128)(2,1)S(1)}, bf16[128,2176]{1,0:T(8,128)(2,1)S(1)}, u32[]{:S(2)}, u32[]{:S(2)}) %collective-permute-start.62) | collective-permute-done | bytes 557088 | tf_op jit(solution)/shard_map/partial_far/ppermute | solution.py:190
  373.6 2.4 collective-permute-start.65
  377.2 18.8 %expert_grads.1 = f32[2048,2304]{1,0:T(8,128)} custom-call(bf16[256,2048]{1,0:T(8,128)(2,1)S(1)} %bitcast.583, bf16[256,2048]{1,0:T(8,128)(2,1)} %bitcast.585, bf16[256,2048]{1,0:T(8,128)(2,1)} %bitcast.587, bf16[256,2048]{1,0:T(8,128)(2,1)} %bitcast.589, bf16[256,2048]{1,0:T(8,128)(2,1)} %copy-done.3, bf16[256,2048]{1,0:T(8,128)(2,1)} %copy-done.4, ...), custom_call_target="tpu_custom_call" | custom-call | flops 1048576 | bytes 1048576 | tf_op jit(solution)/shard_map/expert_grads/pallas_call | solution.py:329
  399.5 2.4 convolution_convert_fusion.1
  404.1 3.4 convolution_convert_fusion.16.grad_ref
  417.4 16.8 %attend_back.1 = (bf16[512,1024]{1,0:T(8,128)(2,1)}, bf16[512,128]{1,0:T(8,128)(2,1)}, bf16[512,128]{1,0:T(8,128)(2,1)}, f32[1,128]{1,0:T(1,128)}, f32[1,128]{1,0:T(1,128)}) custom-call(f32[512,1280]{1,0:T(8,128)} %fusion.168.query_ref.key_ref.value_ref, f32[512,1280]{1,0:T(8,128)} %fusion.168.query_ref.key_ref.value_ref, ...), custom_call_target="tpu_custom_call" | custom-call | flops 1048576 | bytes 1048576 | tf_op jit(solution)/shard_map/attend_back/pallas_call | solution.py:461
  439.2 3.2 convolution_convert_fusion
  445.9 4.6 all-to-all-start.3
  452.0 3.8 collective-permute-start.71
  455.8 5.8 convolution_convert_fusion.4
  461.7 2.8 fusion
  464.5 4.1 collective-permute-done.72
  468.6 9.0 %collective-permute-done.71 = bf16[128,2048]{1,0:T(8,128)(2,1)S(1)} collective-permute-done((bf16[128,2048]{1,0:T(8,128)(2,1)S(1)}, bf16[128,2048]{1,0:T(8,128)(2,1)S(1)}, u32[]{:S(2)}, u32[]{:S(2)}) %collective-permute-start.71) | collective-permute-done | bytes 524320 | tf_op jit(solution)/shard_map/ppermute | solution.py:190
  485.3 2.6 collective-permute-start.78
  488.8 5.2 collective-permute-done.86
  496.2 11.6 %collective-permute-done.74 = bf16[256,1280]{1,0:T(8,128)(2,1)S(1)} collective-permute-done((bf16[256,1280]{1,0:T(8,128)(2,1)S(1)}, bf16[256,1280]{1,0:T(8,128)(2,1)S(1)}, u32[]{:S(2)}, u32[]{:S(2)}) %collective-permute-start.74) | collective-permute-done | bytes 655392 | tf_op jit(solution)/shard_map/ppermute | solution.py:190
  508.0 4.5 collective-permute-start.75
  512.6 3.7 fusion.159
  519.9 4.0 collective-permute-done.73
  526.3 10.6 %collective-permute-done.75 = bf16[256,1280]{1,0:T(8,128)(2,1)S(1)} collective-permute-done((bf16[256,1280]{1,0:T(8,128)(2,1)S(1)}, bf16[256,1280]{1,0:T(8,128)(2,1)S(1)}, u32[]{:S(2)}, u32[]{:S(2)}) %collective-permute-start.75) | collective-permute-done | bytes 655392 | tf_op jit(solution)/shard_map/ppermute | solution.py:190
  542.0 2.4 collective-permute-start.85
  556.7 2.6 collective-permute-start.81
  560.5 10.0 %collective-permute-done.81 = bf16[128,2048]{1,0:T(8,128)(2,1)S(1)} collective-permute-done((bf16[128,2048]{1,0:T(8,128)(2,1)S(1)}, bf16[128,2048]{1,0:T(8,128)(2,1)S(1)}, u32[]{:S(2)}, u32[]{:S(2)}) %collective-permute-start.81) | collective-permute-done | bytes 524320 | tf_op jit(solution)/shard_map/ppermute | solution.py:190
  574.1 4.1 all-to-all-start.4
  578.3 2.5 fusion.11
  580.8 7.8 %collective-permute-done.82 = bf16[128,2048]{1,0:T(8,128)(2,1)S(1)} collective-permute-done((bf16[128,2048]{1,0:T(8,128)(2,1)S(1)}, bf16[128,2048]{1,0:T(8,128)(2,1)S(1)}, u32[]{:S(2)}, u32[]{:S(2)}) %collective-permute-start.82) | collective-permute-done | bytes 524320 | tf_op jit(solution)/shard_map/ppermute | solution.py:87
  (483 shorter events, 188.8 us)
Async XLA Ops:
  1.3 16.4 %collective-permute-start = (s32[1,384]{1,0:T(1,128)S(1)}, s32[1,384]{1,0:T(1,128)S(1)}, u32[]{:S(2)}, u32[]{:S(2)}) collective-permute-start(s32[1,384]{1,0:T(1,128)S(1)} %pad_add_fusion), channel_id=1, source_target_pairs={{0,4},{4,0},{1,5},{5,1},{2,6},{6,2},{3,7},{7,3},{8,12},{12,8},{9,1... | collective-permute-start | bytes 4616 | tf_op jit(solution)/shard_map/ppermute | solution.py:87
  4.3 34.5 %collective-permute-start.11 = (bf16[128,2048]{1,0:T(8,128)(2,1)}, bf16[128,2048]{1,0:T(8,128)(2,1)}, u32[]{:S(2)}, u32[]{:S(2)}) collective-permute-start(bf16[128,2048]{1,0:T(8,128)(2,1)} %param.12), channel_id=1, source_target_pairs={{0,1},{1,0},{2,3},{3,2},{4,5},{5,4},{6,7},{7,6},{8,9},{9,8},{10,11... | collective-permute-start | bytes 1572872 | tf_op jit(solution)/shard_map/ppermute | solution.py:87
  5.8 76.3 %collective-permute-start.12 = (bf16[128,2048]{1,0:T(8,128)(2,1)}, bf16[128,2048]{1,0:T(8,128)(2,1)}, u32[]{:S(2)}, u32[]{:S(2)}) collective-permute-start(bf16[128,2048]{1,0:T(8,128)(2,1)} %param.14), channel_id=1, source_target_pairs={{0,8},{8,16},{16,24},{24,0},{1,9},{9,17},{17,25},{25,1},{2,10},{10... | collective-permute-start | bytes 1572872 | tf_op jit(solution)/shard_map/ppermute | solution.py:190
  11.5 17.3 %collective-permute-start.1 = (bf16[64,1280]{1,0:T(8,128)(2,1)S(1)}, bf16[64,1280]{1,0:T(8,128)(2,1)S(1)}, u32[]{:S(2)}, u32[]{:S(2)}) collective-permute-start(bf16[64,1280]{1,0:T(8,128)(2,1)S(1)} %bitcast.686), channel_id=1, source_target_pairs={{0,1},{1,0},{4,5},{5,4},{2,3},{3,2},{6,7},{7,6},{8,9},{9,8},{12,13... | collective-permute-start | bytes 491528 | tf_op jit(solution)/shard_map/ppermute | solution.py:105
  12.1 16.7 %collective-permute-start.2 = (bf16[64,1280]{1,0:T(8,128)(2,1)S(1)}, bf16[64,1280]{1,0:T(8,128)(2,1)S(1)}, u32[]{:S(2)}, u32[]{:S(2)}) collective-permute-start(bf16[64,1280]{1,0:T(8,128)(2,1)S(1)} %bitcast.687), channel_id=1, source_target_pairs={{0,4},{1,5},{4,0},{5,1},{2,6},{3,7},{6,2},{7,3},{8,12},{9,13},{12,... | collective-permute-start | bytes 491528 | tf_op jit(solution)/shard_map/ppermute | solution.py:105
  24.2 13.7 %all-to-all-start = ((bf16[32,32,128]{2,1,0:T(8,128)(2,1)}), bf16[32,32,128]{2,1,0:T(8,128)(2,1)S(1)}, u32[]{:S(2)}, u32[]{:S(2)}) async-start(bf16[32,32,128]{2,1,0:T(8,128)(2,1)} %bitcast.280), calls=%async_computation | async-start | bytes 524288 | tf_op jit(solution)/shard_map/all_to_all | solution.py:96
  28.9 56.7 %collective-permute-start.6 = (bf16[128,2048]{1,0:T(8,128)(2,1)S(1)}, bf16[128,2048]{1,0:T(8,128)(2,1)}, u32[]{:S(2)}, u32[]{:S(2)}) collective-permute-start(bf16[128,2048]{1,0:T(8,128)(2,1)S(1)} %copy-done.11), channel_id=1, source_target_pairs={{0,5},{1,4},{4,1},{5,0},{2,7},{3,6},{6,3},{7,2},{8,13},{9,12},{12,... | collective-permute-start | bytes 1572872 | tf_op jit(solution)/shard_map/ppermute | solution.py:117
  31.6 54.6 %collective-permute-start.5 = (bf16[128,2048]{1,0:T(8,128)(2,1)S(1)}, bf16[128,2048]{1,0:T(8,128)(2,1)}, u32[]{:S(2)}, u32[]{:S(2)}) collective-permute-start(bf16[128,2048]{1,0:T(8,128)(2,1)S(1)} %copy-done.11), channel_id=1, source_target_pairs={{0,4},{1,5},{4,0},{5,1},{2,6},{3,7},{6,2},{7,3},{8,12},{9,13},{12,... | collective-permute-start | bytes 1572872 | tf_op jit(solution)/shard_map/ppermute | solution.py:117
  33.1 19.8 %collective-permute-start.7 = (bf16[256,1280]{1,0:T(8,128)(2,1)}, bf16[256,1280]{1,0:T(8,128)(2,1)}, u32[]{:S(2)}, u32[]{:S(2)}) collective-permute-start(bf16[256,1280]{1,0:T(8,128)(2,1)} %bitcast.18), channel_id=1, source_target_pairs={{0,8},{8,16},{16,24},{24,0},{1,9},{9,17},{17,25},{25,1},{2,10},{10... | collective-permute-start | bytes 1966088 | tf_op jit(solution)/shard_map/ppermute | solution.py:190
  38.8 41.3 %collective-permute-start.9 = (bf16[256,1280]{1,0:T(8,128)(2,1)}, bf16[256,1280]{1,0:T(8,128)(2,1)S(1)}, u32[]{:S(2)}, u32[]{:S(2)}) collective-permute-start(bf16[256,1280]{1,0:T(8,128)(2,1)} %bitcast.18), channel_id=1, source_target_pairs={{0,24},{8,0},{16,8},{24,16},{1,25},{9,1},{17,9},{25,17},{2,26},{10... | collective-permute-start | bytes 1966088 | tf_op jit(solution)/shard_map/ppermute | solution.py:190
  53.0 26.6 %collective-permute-start.8 = (bf16[256,1280]{1,0:T(8,128)(2,1)}, bf16[256,1280]{1,0:T(8,128)(2,1)S(1)}, u32[]{:S(2)}, u32[]{:S(2)}) collective-permute-start(bf16[256,1280]{1,0:T(8,128)(2,1)} %collective-permute-done.7), channel_id=1, source_target_pairs={{0,8},{8,16},{16,24},{24,0},{1,9},{9,17},{17,25},{25,1},{2,10},{10... | collective-permute-start | bytes 1966088 | tf_op jit(solution)/shard_map/ppermute | solution.py:190
  80.1 16.5 %collective-permute-start.10 = (bf16[8,128,1280]{2,1,0:T(8,128)(2,1)S(1)}, bf16[8,128,1280]{2,1,0:T(8,128)(2,1)S(1)}, u32[]{:S(2)}, u32[]{:S(2)}) collective-permute-start(bf16[8,128,1280]{2,1,0:T(8,128)(2,1)S(1)} %bitcast.621), channel_id=1, source_target_pairs={{0,2},{2,0},{1,3},{3,1},{4,6},{6,4},{5,7},{7,5},{8,10},{10,8},{9,1... | collective-permute-start | bytes 7864328 | tf_op jit(solution)/shard_map/ppermute | solution.py:87
  82.1 27.8 %collective-permute-start.14 = (bf16[128,2048]{1,0:T(8,128)(2,1)}, bf16[128,2048]{1,0:T(8,128)(2,1)}, u32[]{:S(2)}, u32[]{:S(2)}) collective-permute-start(bf16[128,2048]{1,0:T(8,128)(2,1)} %param.14), channel_id=1, source_target_pairs={{0,24},{8,0},{16,8},{24,16},{1,25},{9,1},{17,9},{25,17},{2,26},{10... | collective-permute-start | bytes 1572872 | tf_op jit(solution)/shard_map/ppermute | solution.py:190
  85.5 22.5 %collective-permute-start.13 = (bf16[128,2048]{1,0:T(8,128)(2,1)}, bf16[128,2048]{1,0:T(8,128)(2,1)}, u32[]{:S(2)}, u32[]{:S(2)}) collective-permute-start(bf16[128,2048]{1,0:T(8,128)(2,1)} %collective-permute-done.12), channel_id=1, source_target_pairs={{0,8},{8,16},{16,24},{24,0},{1,9},{9,17},{17,25},{25,1},{2,10},{10... | collective-permute-start | bytes 1572872 | tf_op jit(solution)/shard_map/ppermute | solution.py:190
  102.1 70.3 %all-to-all-start.1 = ((bf16[32,32,1152]{2,1,0:T(8,128)(2,1)}), bf16[32,32,1152]{2,1,0:T(8,128)(2,1)}, u32[]{:S(2)}, u32[]{:S(2)}) async-start(bf16[32,32,1152]{2,1,0:T(8,128)(2,1)} %bitcast.27), calls=%async_computation.1 | async-start | bytes 4718592 | tf_op jit(solution)/shard_map/all_to_all | solution.py:96
  114.6 29.4 %collective-permute-start.17 = (bf16[128,2048]{1,0:T(8,128)(2,1)}, bf16[128,2048]{1,0:T(8,128)(2,1)S(1)}, u32[]{:S(2)}, u32[]{:S(2)}) collective-permute-start(bf16[128,2048]{1,0:T(8,128)(2,1)} %get-tuple-element.299), channel_id=1, source_target_pairs={{0,5},{1,4},{4,1},{5,0},{2,7},{3,6},{6,3},{7,2},{8,13},{9,12},{12,... | collective-permute-start | bytes 1572872 | tf_op jit(solution)/shard_map/ppermute | solution.py:105
  117.0 39.2 %collective-permute-start.16 = (bf16[128,2048]{1,0:T(8,128)(2,1)}, bf16[128,2048]{1,0:T(8,128)(2,1)S(1)}, u32[]{:S(2)}, u32[]{:S(2)}) collective-permute-start(bf16[128,2048]{1,0:T(8,128)(2,1)} %get-tuple-element.300), channel_id=1, source_target_pairs={{0,4},{1,5},{4,0},{5,1},{2,6},{3,7},{6,2},{7,3},{8,12},{9,13},{12,... | collective-permute-start | bytes 1572872 | tf_op jit(solution)/shard_map/ppermute | solution.py:105
  117.5 41.0 %collective-permute-start.15 = (bf16[128,2048]{1,0:T(8,128)(2,1)S(1)}, bf16[128,2048]{1,0:T(8,128)(2,1)S(1)}, u32[]{:S(2)}, u32[]{:S(2)}) collective-permute-start(bf16[128,2048]{1,0:T(8,128)(2,1)S(1)} %get-tuple-element.301), channel_id=1, source_target_pairs={{0,1},{1,0},{4,5},{5,4},{2,3},{3,2},{6,7},{7,6},{8,9},{9,8},{12,13... | collective-permute-start | bytes 1572872 | tf_op jit(solution)/shard_map/ppermute | solution.py:105
  160.4 16.1 %collective-permute-start.18 = (bf16[2,256,2048]{2,1,0:T(8,128)(2,1)}, bf16[2,256,2048]{2,1,0:T(8,128)(2,1)S(1)}, u32[]{:S(2)}, u32[]{:S(2)}) collective-permute-start(bf16[2,256,2048]{2,1,0:T(8,128)(2,1)} %bitcast.45), channel_id=1, source_target_pairs={{0,2},{2,0},{1,3},{3,1},{4,6},{6,4},{5,7},{7,5},{8,10},{10,8},{9,1... | collective-permute-start | bytes 6291464 | tf_op jit(solution)/shard_map/ppermute | solution.py:87
  172.4 55.5 %all-to-all-start.2 = ((bf16[32,32,896]{2,1,0:T(8,128)(2,1)}), bf16[32,32,896]{2,1,0:T(8,128)(2,1)}, u32[]{:S(2)}, u32[]{:S(2)}) async-start(bf16[32,32,896]{2,1,0:T(8,128)(2,1)} %bitcast.28), calls=%async_computation.2 | async-start | bytes 3670016 | tf_op jit(solution)/shard_map/all_to_all | solution.py:96
  185.0 24.1 %collective-permute-start.19 = (bf16[128,2048]{1,0:T(8,128)(2,1)}, bf16[128,2048]{1,0:T(8,128)(2,1)}, u32[]{:S(2)}, u32[]{:S(2)}) collective-permute-start(bf16[128,2048]{1,0:T(8,128)(2,1)} %get-tuple-element.292), channel_id=1, source_target_pairs={{0,1},{1,0},{4,5},{5,4},{2,3},{3,2},{6,7},{7,6},{8,9},{9,8},{12,13... | collective-permute-start | bytes 1572872 | tf_op jit(solution)/shard_map/ppermute | solution.py:105
  186.7 35.5 %collective-permute-start.21 = (bf16[128,2048]{1,0:T(8,128)(2,1)}, bf16[128,2048]{1,0:T(8,128)(2,1)}, u32[]{:S(2)}, u32[]{:S(2)}) collective-permute-start(bf16[128,2048]{1,0:T(8,128)(2,1)} %get-tuple-element.293), channel_id=1, source_target_pairs={{0,5},{1,4},{4,1},{5,0},{2,7},{3,6},{6,3},{7,2},{8,13},{9,12},{12,... | collective-permute-start | bytes 1572872 | tf_op jit(solution)/shard_map/ppermute | solution.py:105
  188.2 34.1 %collective-permute-start.20 = (bf16[128,2048]{1,0:T(8,128)(2,1)S(1)}, bf16[128,2048]{1,0:T(8,128)(2,1)}, u32[]{:S(2)}, u32[]{:S(2)}) collective-permute-start(bf16[128,2048]{1,0:T(8,128)(2,1)S(1)} %get-tuple-element.294), channel_id=1, source_target_pairs={{0,4},{1,5},{4,0},{5,1},{2,6},{3,7},{6,2},{7,3},{8,12},{9,13},{12,... | collective-permute-start | bytes 1572872 | tf_op jit(solution)/shard_map/ppermute | solution.py:105
  225.3 18.7 %collective-permute-start.29 = (bf16[128,2048]{1,0:T(8,128)(2,1)S(1)}, bf16[128,2048]{1,0:T(8,128)(2,1)S(1)}, u32[]{:S(2)}, u32[]{:S(2)}) collective-permute-start(bf16[128,2048]{1,0:T(8,128)(2,1)S(1)} %multiply_convert_fusion.1), channel_id=1, source_target_pairs={{0,8},{8,16},{16,24},{24,0},{1,9},{9,17},{17,25},{25,1},{2,10},{10... | collective-permute-start | bytes 1572872 | tf_op jit(solution)/shard_map/rows_far1/ppermute | solution.py:190
  244.6 16.2 %collective-permute-start.31 = (bf16[2,32,2048]{2,1,0:T(8,128)(2,1)S(1)}, bf16[2,32,2048]{2,1,0:T(8,128)(2,1)S(1)}, u32[]{:S(2)}, u32[]{:S(2)}) collective-permute-start(bf16[2,32,2048]{2,1,0:T(8,128)(2,1)S(1)} %bitcast.682), channel_id=1, source_target_pairs={{0,4},{1,5},{4,0},{5,1},{2,6},{3,7},{6,2},{7,3},{8,12},{9,13},{12,... | collective-permute-start | bytes 786440 | tf_op jit(solution)/shard_map/rows_out1/ppermute | solution.py:198
  245.0 15.7 %collective-permute-start.32 = (bf16[2,32,2048]{2,1,0:T(8,128)(2,1)S(1)}, bf16[2,32,2048]{2,1,0:T(8,128)(2,1)S(1)}, u32[]{:S(2)}, u32[]{:S(2)}) collective-permute-start(bf16[2,32,2048]{2,1,0:T(8,128)(2,1)S(1)} %bitcast.679), channel_id=1, source_target_pairs={{0,5},{1,4},{4,1},{5,0},{2,7},{3,6},{6,3},{7,2},{8,13},{9,12},{12,... | collective-permute-start | bytes 786440 | tf_op jit(solution)/shard_map/rows_out1/ppermute | solution.py:198
  248.2 15.3 %collective-permute-start.34 = (bf16[128,2048]{1,0:T(8,128)(2,1)S(1)}, bf16[128,2048]{1,0:T(8,128)(2,1)S(1)}, u32[]{:S(2)}, u32[]{:S(2)}) collective-permute-start(bf16[128,2048]{1,0:T(8,128)(2,1)S(1)} %collective-permute-done.29), channel_id=1, source_target_pairs={{0,8},{8,16},{16,24},{24,0},{1,9},{9,17},{17,25},{25,1},{2,10},{10... | collective-permute-start | bytes 1572872 | tf_op jit(solution)/shard_map/rows_far2/ppermute | solution.py:190
  264.0 14.8 %collective-permute-start.36 = (bf16[2,32,2048]{2,1,0:T(8,128)(2,1)S(1)}, bf16[2,32,2048]{2,1,0:T(8,128)(2,1)S(1)}, u32[]{:S(2)}, u32[]{:S(2)}) collective-permute-start(bf16[2,32,2048]{2,1,0:T(8,128)(2,1)S(1)} %bitcast.683), channel_id=1, source_target_pairs={{0,4},{1,5},{4,0},{5,1},{2,6},{3,7},{6,2},{7,3},{8,12},{9,13},{12,... | collective-permute-start | bytes 786440 | tf_op jit(solution)/shard_map/rows_out2/ppermute | solution.py:198
  264.6 14.2 %collective-permute-start.37 = (bf16[2,32,2048]{2,1,0:T(8,128)(2,1)S(1)}, bf16[2,32,2048]{2,1,0:T(8,128)(2,1)S(1)}, u32[]{:S(2)}, u32[]{:S(2)}) collective-permute-start(bf16[2,32,2048]{2,1,0:T(8,128)(2,1)S(1)} %bitcast.680), channel_id=1, source_target_pairs={{0,5},{1,4},{4,1},{5,0},{2,7},{3,6},{6,3},{7,2},{8,13},{9,12},{12,... | collective-permute-start | bytes 786440 | tf_op jit(solution)/shard_map/rows_out2/ppermute | solution.py:198
  267.6 13.7 %collective-permute-start.39 = (bf16[128,2048]{1,0:T(8,128)(2,1)S(1)}, bf16[128,2048]{1,0:T(8,128)(2,1)S(1)}, u32[]{:S(2)}, u32[]{:S(2)}) collective-permute-start(bf16[128,2048]{1,0:T(8,128)(2,1)S(1)} %collective-permute-done.34), channel_id=1, source_target_pairs={{0,8},{8,16},{16,24},{24,0},{1,9},{9,17},{17,25},{25,1},{2,10},{10... | collective-permute-start | bytes 1572872 | tf_op jit(solution)/shard_map/rows_far3/ppermute | solution.py:190
  279.8 17.2 %collective-permute-start.44 = (bf16[2,2,32,2176]{3,2,1,0:T(8,128)(2,1)S(1)}, bf16[2,2,32,2176]{3,2,1,0:T(8,128)(2,1)S(1)}, u32[]{:S(2)}, u32[]{:S(2)}) collective-permute-start(bf16[2,2,32,2176]{3,2,1,0:T(8,128)(2,1)S(1)} %get-tuple-element.343), channel_id=1, source_target_pairs={{0,2},{2,0},{1,3},{3,1},{4,6},{6,4},{5,7},{7,5},{8,10},{10,8},{9,1... | collective-permute-start | bytes 1671176 | tf_op jit(solution)/shard_map/rows_back1/ppermute | solution.py:87
  281.8 13.8 %collective-permute-start.41 = (bf16[2,32,2048]{2,1,0:T(8,128)(2,1)S(1)}, bf16[2,32,2048]{2,1,0:T(8,128)(2,1)S(1)}, u32[]{:S(2)}, u32[]{:S(2)}) collective-permute-start(bf16[2,32,2048]{2,1,0:T(8,128)(2,1)S(1)} %bitcast.685), channel_id=1, source_target_pairs={{0,4},{1,5},{4,0},{5,1},{2,6},{3,7},{6,2},{7,3},{8,12},{9,13},{12,... | collective-permute-start | bytes 786440 | tf_op jit(solution)/shard_map/rows_out3/ppermute | solution.py:198
  296.6 14.8 %collective-permute-start.48 = (bf16[2,2,32,2176]{3,2,1,0:T(8,128)(2,1)S(1)}, bf16[2,2,32,2176]{3,2,1,0:T(8,128)(2,1)S(1)}, u32[]{:S(2)}, u32[]{:S(2)}) collective-permute-start(bf16[2,2,32,2176]{3,2,1,0:T(8,128)(2,1)S(1)} %get-tuple-element.337), channel_id=1, source_target_pairs={{0,2},{2,0},{1,3},{3,1},{4,6},{6,4},{5,7},{7,5},{8,10},{10,8},{9,1... | collective-permute-start | bytes 1671176 | tf_op jit(solution)/shard_map/rows_back2/ppermute | solution.py:87
  297.1 16.6 %collective-permute-start.47 = (bf16[2,32,2176]{2,1,0:T(8,128)(2,1)S(1)}, bf16[2,32,2176]{2,1,0:T(8,128)(2,1)S(1)}, u32[]{:S(2)}, u32[]{:S(2)}) collective-permute-start(bf16[2,32,2176]{2,1,0:T(8,128)(2,1)S(1)} %get-tuple-element.339), channel_id=1, source_target_pairs={{0,5},{1,4},{4,1},{5,0},{2,7},{3,6},{6,3},{7,2},{8,13},{9,12},{12,... | collective-permute-start | bytes 835592 | tf_op jit(solution)/shard_map/rows_back1/ppermute | solution.py:105
  298.7 15.4 %collective-permute-start.45 = (bf16[2,32,2176]{2,1,0:T(8,128)(2,1)S(1)}, bf16[2,32,2176]{2,1,0:T(8,128)(2,1)S(1)}, u32[]{:S(2)}, u32[]{:S(2)}) collective-permute-start(bf16[2,32,2176]{2,1,0:T(8,128)(2,1)S(1)} %get-tuple-element.341), channel_id=1, source_target_pairs={{0,1},{1,0},{4,5},{5,4},{2,3},{3,2},{6,7},{7,6},{8,9},{9,8},{12,13... | collective-permute-start | bytes 835592 | tf_op jit(solution)/shard_map/rows_back1/ppermute | solution.py:105
  299.2 16.4 %collective-permute-start.46 = (bf16[2,32,2176]{2,1,0:T(8,128)(2,1)S(1)}, bf16[2,32,2176]{2,1,0:T(8,128)(2,1)S(1)}, u32[]{:S(2)}, u32[]{:S(2)}) collective-permute-start(bf16[2,32,2176]{2,1,0:T(8,128)(2,1)S(1)} %get-tuple-element.342), channel_id=1, source_target_pairs={{0,4},{1,5},{4,0},{5,1},{2,6},{3,7},{6,2},{7,3},{8,12},{9,13},{12,... | collective-permute-start | bytes 835592 | tf_op jit(solution)/shard_map/rows_back1/ppermute | solution.py:105
  311.2 19.6 %collective-permute-start.56 = (bf16[2,2,32,2176]{3,2,1,0:T(8,128)(2,1)S(1)}, bf16[2,2,32,2176]{3,2,1,0:T(8,128)(2,1)S(1)}, u32[]{:S(2)}, u32[]{:S(2)}) collective-permute-start(bf16[2,2,32,2176]{3,2,1,0:T(8,128)(2,1)S(1)} %get-tuple-element.325), channel_id=1, source_target_pairs={{0,2},{2,0},{1,3},{3,1},{4,6},{6,4},{5,7},{7,5},{8,10},{10,8},{9,1... | collective-permute-start | bytes 1671176 | tf_op jit(solution)/shard_map/rows_back3/ppermute | solution.py:87
  327.9 19.1 %collective-permute-start.61 = (bf16[128,2176]{1,0:T(8,128)(2,1)S(1)}, bf16[128,2176]{1,0:T(8,128)(2,1)S(1)}, u32[]{:S(2)}, u32[]{:S(2)}) collective-permute-start(bf16[128,2176]{1,0:T(8,128)(2,1)S(1)} %fusion.7), channel_id=1, source_target_pairs={{0,24},{8,0},{16,8},{24,16},{1,25},{9,1},{17,9},{25,17},{2,26},{10... | collective-permute-start | bytes 1671176 | tf_op jit(solution)/shard_map/partial_far/ppermute | solution.py:190
  332.5 14.0 %collective-permute-start.58 = (bf16[2,32,2176]{2,1,0:T(8,128)(2,1)S(1)}, bf16[2,32,2176]{2,1,0:T(8,128)(2,1)S(1)}, u32[]{:S(2)}, u32[]{:S(2)}) collective-permute-start(bf16[2,32,2176]{2,1,0:T(8,128)(2,1)S(1)} %get-tuple-element.323), channel_id=1, source_target_pairs={{0,4},{1,5},{4,0},{5,1},{2,6},{3,7},{6,2},{7,3},{8,12},{9,13},{12,... | collective-permute-start | bytes 835592 | tf_op jit(solution)/shard_map/rows_back3/ppermute | solution.py:105
  334.7 16.3 %collective-permute-start.52 = (bf16[2,2,32,2176]{3,2,1,0:T(8,128)(2,1)S(1)}, bf16[2,2,32,2176]{3,2,1,0:T(8,128)(2,1)S(1)}, u32[]{:S(2)}, u32[]{:S(2)}) collective-permute-start(bf16[2,2,32,2176]{3,2,1,0:T(8,128)(2,1)S(1)} %get-tuple-element.331), channel_id=1, source_target_pairs={{0,2},{2,0},{1,3},{3,1},{4,6},{6,4},{5,7},{7,5},{8,10},{10,8},{9,1... | collective-permute-start | bytes 1671176 | tf_op jit(solution)/shard_map/rows_back0/ppermute | solution.py:87
  346.9 17.4 %collective-permute-start.60 = (bf16[128,2176]{1,0:T(8,128)(2,1)S(1)}, bf16[128,2176]{1,0:T(8,128)(2,1)S(1)}, u32[]{:S(2)}, u32[]{:S(2)}) collective-permute-start(bf16[128,2176]{1,0:T(8,128)(2,1)S(1)} %fusion.8), channel_id=1, source_target_pairs={{0,8},{8,16},{16,24},{24,0},{1,9},{9,17},{17,25},{25,1},{2,10},{10... | collective-permute-start | bytes 1671176 | tf_op jit(solution)/shard_map/partial_far/ppermute | solution.py:190
  347.1 24.2 %collective-permute-start.62 = (bf16[128,2176]{1,0:T(8,128)(2,1)S(1)}, bf16[128,2176]{1,0:T(8,128)(2,1)S(1)}, u32[]{:S(2)}, u32[]{:S(2)}) collective-permute-start(bf16[128,2176]{1,0:T(8,128)(2,1)S(1)} %add_convert_fusion), channel_id=1, source_target_pairs={{0,24},{8,0},{16,8},{24,16},{1,25},{9,1},{17,9},{25,17},{2,26},{10... | collective-permute-start | bytes 1671176 | tf_op jit(solution)/shard_map/partial_far/ppermute | solution.py:190
  373.6 22.4 %collective-permute-start.65 = (bf16[128,2048]{1,0:T(8,128)(2,1)S(1)}, bf16[128,2048]{1,0:T(8,128)(2,1)S(1)}, u32[]{:S(2)}, u32[]{:S(2)}) collective-permute-start(bf16[128,2048]{1,0:T(8,128)(2,1)S(1)} %fusion.47), channel_id=1, source_target_pairs={{0,5},{1,4},{4,1},{5,0},{2,7},{3,6},{6,3},{7,2},{8,13},{9,12},{12,... | collective-permute-start | bytes 1572872 | tf_op jit(solution)/shard_map/ppermute | solution.py:117
  376.0 22.0 %collective-permute-start.64 = (bf16[128,2048]{1,0:T(8,128)(2,1)S(1)}, bf16[128,2048]{1,0:T(8,128)(2,1)S(1)}, u32[]{:S(2)}, u32[]{:S(2)}) collective-permute-start(bf16[128,2048]{1,0:T(8,128)(2,1)S(1)} %fusion.47), channel_id=1, source_target_pairs={{0,4},{1,5},{4,0},{5,1},{2,6},{3,7},{6,2},{7,3},{8,12},{9,13},{12,... | collective-permute-start | bytes 1572872 | tf_op jit(solution)/shard_map/ppermute | solution.py:117
  376.9 21.2 %collective-permute-start.63 = (bf16[128,2048]{1,0:T(8,128)(2,1)S(1)}, bf16[128,2048]{1,0:T(8,128)(2,1)S(1)}, u32[]{:S(2)}, u32[]{:S(2)}) collective-permute-start(bf16[128,2048]{1,0:T(8,128)(2,1)S(1)} %fusion.47), channel_id=1, source_target_pairs={{0,1},{1,0},{4,5},{5,4},{2,3},{3,2},{6,7},{7,6},{8,9},{9,8},{12,13... | collective-permute-start | bytes 1572872 | tf_op jit(solution)/shard_map/ppermute | solution.py:117
  409.9 24.3 %collective-permute-start.69 = (bf16[128,2048]{1,0:T(8,128)(2,1)}, bf16[128,2048]{1,0:T(8,128)(2,1)S(1)}, u32[]{:S(2)}, u32[]{:S(2)}) collective-permute-start(bf16[128,2048]{1,0:T(8,128)(2,1)} %get-tuple-element.284), channel_id=1, source_target_pairs={{0,5},{1,4},{4,1},{5,0},{2,7},{3,6},{6,3},{7,2},{8,13},{9,12},{12,... | collective-permute-start | bytes 1572872 | tf_op jit(solution)/shard_map/ppermute | solution.py:105
  411.7 24.5 %collective-permute-start.68 = (bf16[128,2048]{1,0:T(8,128)(2,1)}, bf16[128,2048]{1,0:T(8,128)(2,1)}, u32[]{:S(2)}, u32[]{:S(2)}) collective-permute-start(bf16[128,2048]{1,0:T(8,128)(2,1)} %get-tuple-element.285), channel_id=1, source_target_pairs={{0,4},{1,5},{4,0},{5,1},{2,6},{3,7},{6,2},{7,3},{8,12},{9,13},{12,... | collective-permute-start | bytes 1572872 | tf_op jit(solution)/shard_map/ppermute | solution.py:105
  413.1 23.2 %collective-permute-start.67 = (bf16[128,2048]{1,0:T(8,128)(2,1)}, bf16[128,2048]{1,0:T(8,128)(2,1)}, u32[]{:S(2)}, u32[]{:S(2)}) collective-permute-start(bf16[128,2048]{1,0:T(8,128)(2,1)} %get-tuple-element.286), channel_id=1, source_target_pairs={{0,1},{1,0},{4,5},{5,4},{2,3},{3,2},{6,7},{7,6},{8,9},{9,8},{12,13... | collective-permute-start | bytes 1572872 | tf_op jit(solution)/shard_map/ppermute | solution.py:105
  445.6 16.1 %collective-permute-start.70 = (bf16[8,128,1280]{2,1,0:T(8,128)(2,1)}, bf16[8,128,1280]{2,1,0:T(8,128)(2,1)}, u32[]{:S(2)}, u32[]{:S(2)}) collective-permute-start(bf16[8,128,1280]{2,1,0:T(8,128)(2,1)} %fusion.9), channel_id=1, source_target_pairs={{0,2},{2,0},{1,3},{3,1},{4,6},{6,4},{5,7},{7,5},{8,10},{10,8},{9,1... | collective-permute-start | bytes 7864328 | tf_op jit(solution)/shard_map/ppermute | solution.py:87
  445.9 66.7 %all-to-all-start.3 = ((bf16[8,4,32,2048]{3,2,1,0:T(8,128)(2,1)}), bf16[8,4,32,2048]{3,2,1,0:T(8,128)(2,1)}, u32[]{:S(2)}, u32[]{:S(2)}) async-start(bf16[8,4,32,2048]{3,2,1,0:T(8,128)(2,1)} %pad_maximum_fusion.3), calls=%async_computation.3 | async-start | bytes 8388608 | tf_op jit(solution)/shard_map/all_to_all | solution.py:96
  451.9 16.6 %collective-permute-start.72 = (bf16[128,2048]{1,0:T(8,128)(2,1)S(1)}, bf16[128,2048]{1,0:T(8,128)(2,1)S(1)}, u32[]{:S(2)}, u32[]{:S(2)}) collective-permute-start(bf16[128,2048]{1,0:T(8,128)(2,1)S(1)} %get-tuple-element.282), channel_id=1, source_target_pairs={{0,8},{8,16},{16,24},{24,0},{1,9},{9,17},{17,25},{25,1},{2,10},{10... | collective-permute-start | bytes 1572872 | tf_op jit(solution)/shard_map/ppermute | solution.py:190
  452.0 25.6 %collective-permute-start.71 = (bf16[128,2048]{1,0:T(8,128)(2,1)S(1)}, bf16[128,2048]{1,0:T(8,128)(2,1)S(1)}, u32[]{:S(2)}, u32[]{:S(2)}) collective-permute-start(bf16[128,2048]{1,0:T(8,128)(2,1)S(1)} %get-tuple-element.283), channel_id=1, source_target_pairs={{0,24},{8,0},{16,8},{24,16},{1,25},{9,1},{17,9},{25,17},{2,26},{10... | collective-permute-start | bytes 1572872 | tf_op jit(solution)/shard_map/ppermute | solution.py:190
  479.1 14.9 %collective-permute-start.86 = (bf16[128,2048]{1,0:T(8,128)(2,1)S(1)}, bf16[128,2048]{1,0:T(8,128)(2,1)S(1)}, u32[]{:S(2)}, u32[]{:S(2)}) collective-permute-start(bf16[128,2048]{1,0:T(8,128)(2,1)S(1)} %add_convert_fusion.1), channel_id=1, source_target_pairs={{0,24},{8,0},{16,8},{24,16},{1,25},{9,1},{17,9},{25,17},{2,26},{10... | collective-permute-start | bytes 1572872 | tf_op jit(solution)/shard_map/ppermute | solution.py:190
  482.3 25.5 %collective-permute-start.74 = (bf16[256,1280]{1,0:T(8,128)(2,1)S(1)}, bf16[256,1280]{1,0:T(8,128)(2,1)S(1)}, u32[]{:S(2)}, u32[]{:S(2)}) collective-permute-start(bf16[256,1280]{1,0:T(8,128)(2,1)S(1)} %get-tuple-element.277), channel_id=1, source_target_pairs={{0,24},{8,0},{16,8},{24,16},{1,25},{9,1},{17,9},{25,17},{2,26},{10... | collective-permute-start | bytes 1966088 | tf_op jit(solution)/shard_map/ppermute | solution.py:190
  485.3 53.5 %collective-permute-start.78 = (bf16[128,2048]{1,0:T(8,128)(2,1)}, bf16[128,2048]{1,0:T(8,128)(2,1)}, u32[]{:S(2)}, u32[]{:S(2)}) collective-permute-start(bf16[128,2048]{1,0:T(8,128)(2,1)} %get-tuple-element.278), channel_id=1, source_target_pairs={{0,5},{1,4},{4,1},{5,0},{2,7},{3,6},{6,3},{7,2},{8,13},{9,12},{12,... | collective-permute-start | bytes 1572872 | tf_op jit(solution)/shard_map/ppermute | solution.py:105
  487.9 50.9 %collective-permute-start.77 = (bf16[128,2048]{1,0:T(8,128)(2,1)}, bf16[128,2048]{1,0:T(8,128)(2,1)}, u32[]{:S(2)}, u32[]{:S(2)}) collective-permute-start(bf16[128,2048]{1,0:T(8,128)(2,1)} %get-tuple-element.279), channel_id=1, source_target_pairs={{0,4},{1,5},{4,0},{5,1},{2,6},{3,7},{6,2},{7,3},{8,12},{9,13},{12,... | collective-permute-start | bytes 1572872 | tf_op jit(solution)/shard_map/ppermute | solution.py:105
  487.9 50.9 %collective-permute-start.76 = (bf16[128,2048]{1,0:T(8,128)(2,1)}, bf16[128,2048]{1,0:T(8,128)(2,1)}, u32[]{:S(2)}, u32[]{:S(2)}) collective-permute-start(bf16[128,2048]{1,0:T(8,128)(2,1)} %get-tuple-element.280), channel_id=1, source_target_pairs={{0,1},{1,0},{4,5},{5,4},{2,3},{3,2},{6,7},{7,6},{8,9},{9,8},{12,13... | collective-permute-start | bytes 1572872 | tf_op jit(solution)/shard_map/ppermute | solution.py:105
  493.9 30.0 %collective-permute-start.73 = (bf16[256,1280]{1,0:T(8,128)(2,1)}, bf16[256,1280]{1,0:T(8,128)(2,1)}, u32[]{:S(2)}, u32[]{:S(2)}) collective-permute-start(bf16[256,1280]{1,0:T(8,128)(2,1)} %get-tuple-element.276), channel_id=1, source_target_pairs={{0,8},{8,16},{16,24},{24,0},{1,9},{9,17},{17,25},{25,1},{2,10},{10... | collective-permute-start | bytes 1966088 | tf_op jit(solution)/shard_map/ppermute | solution.py:190
  508.0 28.8 %collective-permute-start.75 = (bf16[256,1280]{1,0:T(8,128)(2,1)S(1)}, bf16[256,1280]{1,0:T(8,128)(2,1)S(1)}, u32[]{:S(2)}, u32[]{:S(2)}) collective-permute-start(bf16[256,1280]{1,0:T(8,128)(2,1)S(1)} %fusion.15), channel_id=1, source_target_pairs={{0,24},{8,0},{16,8},{24,16},{1,25},{9,1},{17,9},{25,17},{2,26},{10... | collective-permute-start | bytes 1966088 | tf_op jit(solution)/shard_map/ppermute | solution.py:190
  523.9 30.2 %collective-permute-start.80 = (bf16[128,2048]{1,0:T(8,128)(2,1)}, bf16[128,2048]{1,0:T(8,128)(2,1)}, u32[]{:S(2)}, u32[]{:S(2)}) collective-permute-start(bf16[128,2048]{1,0:T(8,128)(2,1)} %convolution_convert_fusion.11), channel_id=1, source_target_pairs={{0,24},{8,0},{16,8},{24,16},{1,25},{9,1},{17,9},{25,17},{2,26},{10... | collective-permute-start | bytes 1572872 | tf_op jit(solution)/shard_map/ppermute | solution.py:190
  536.8 23.7 %collective-permute-start.79 = (bf16[128,2048]{1,0:T(8,128)(2,1)}, bf16[128,2048]{1,0:T(8,128)(2,1)}, u32[]{:S(2)}, u32[]{:S(2)}) collective-permute-start(bf16[128,2048]{1,0:T(8,128)(2,1)} %convolution_convert_fusion.13), channel_id=1, source_target_pairs={{0,8},{8,16},{16,24},{24,0},{1,9},{9,17},{17,25},{25,1},{2,10},{10... | collective-permute-start | bytes 1572872 | tf_op jit(solution)/shard_map/ppermute | solution.py:190
  556.7 13.8 %collective-permute-start.81 = (bf16[128,2048]{1,0:T(8,128)(2,1)S(1)}, bf16[128,2048]{1,0:T(8,128)(2,1)S(1)}, u32[]{:S(2)}, u32[]{:S(2)}) collective-permute-start(bf16[128,2048]{1,0:T(8,128)(2,1)S(1)} %add_convert_fusion.3), channel_id=1, source_target_pairs={{0,24},{8,0},{16,8},{24,16},{1,25},{9,1},{17,9},{25,17},{2,26},{10... | collective-permute-start | bytes 1572872 | tf_op jit(solution)/shard_map/ppermute | solution.py:190
  572.6 16.0 %collective-permute-start.82 = (bf16[128,2048]{1,0:T(8,128)(2,1)S(1)}, bf16[128,2048]{1,0:T(8,128)(2,1)S(1)}, u32[]{:S(2)}, u32[]{:S(2)}) collective-permute-start(bf16[128,2048]{1,0:T(8,128)(2,1)S(1)} %add_convert_fusion.2), channel_id=1, source_target_pairs={{0,1},{1,0},{2,3},{3,2},{4,5},{5,4},{6,7},{7,6},{8,9},{9,8},{10,11... | collective-permute-start | bytes 1572872 | tf_op jit(solution)/shard_map/ppermute | solution.py:87
  574.1 16.9 %all-to-all-start.4 = ((f32[32,24,128]{2,1,0:T(8,128)}), f32[32,24,128]{2,1,0:T(8,128)S(1)}, u32[]{:S(2)}, u32[]{:S(2)}) async-start(f32[32,24,128]{2,1,0:T(8,128)} %bitcast.288), calls=%async_computation.4 | async-start | bytes 786432 | tf_op jit(solution)/shard_map/all_to_all | solution.py:96
  (90 other events, 629.4 us)
